TPU v7x, 32 devices: a whole 2x2x4 slice. The times are simulated.
32 devices in a mesh: wide: 16 (over z, x, core), seq: 2 (over y).
Axes of the slice: x: 2, y: 2, z: 4, core: 2. Of those that a mesh axis runs over, the one named last changes fastest.
Arguments:
- tokens: bfloat16 [32, 1024, 768], P('wide', 'seq'), may hold values from -6 to 6
- time_embed: float32 [32, 768], P('wide'), may hold values from -6 to 6
- segment_ids: int32 [32, 1024], P('wide', 'seq'), may hold values from 0 to 4, as said below
- pad_mask: int32 [32, 1024], P('wide', 'seq'), may hold values 0 or 1
- out_grad: bfloat16 [32, 1024, 768], P('wide', 'seq'), may hold values from -6 to 6
- qkv_weight: bfloat16 [2, 768, 2304], P(None, 'wide'), may hold values from -0.21875 to 0.21875
- out_weight: bfloat16 [2, 768, 768], P(None, 'wide'), may hold values from -1.25 to 1.25
- up_weight: bfloat16 [2, 768, 3072], P(None, 'wide'), may hold values from -0.21875 to 0.21875
- down_weight: bfloat16 [2, 3072, 768], P(None, 'wide'), may hold values from -0.109375 to 0.109375
- norm_gains: bfloat16 [2, 2, 768], P(None, None, 'wide'), may hold values from 0.5 to 1.5
- bias_rows: bfloat16 [2, 6, 768], P(None, None, 'wide'), may hold values from -1.75 to 1.75
- up_bias: bfloat16 [2, 3072], P(None, 'wide'), may hold values from -1.75 to 1.75
Outputs:
- output: float32 [32, 1024, 768], P('wide', 'seq')
- input_gradient: float32 [32, 1024, 768], P('wide', 'seq')
- qkv_weight_gradient: float32 [2, 768, 2304], P(None, 'wide')
- out_weight_gradient: float32 [2, 768, 768], P(None, 'wide')
- up_weight_gradient: float32 [2, 768, 3072], P(None, 'wide')
- down_weight_gradient: float32 [2, 3072, 768], P(None, 'wide')
- norm_gains_gradient: float32 [2, 2, 768], P(None, None, 'wide')
- bias_rows_gradient: float32 [2, 6, 768], P(None, None, 'wide')
- up_bias_gradient: float32 [2, 3072], P(None, 'wide')
Inputs may be any that keep to these rules, and one draw needn't show every extreme that they name: `segment_ids`: in each sequence the ids never fall along positions, are 0 at the first token and 4 at the last; one document of every sequence covers positions 384 to 639.
All inputs are finite; a program needn't handle non-finite values. No bound on the sum of `pad_mask` on one device may be relied on, other than what follows from the above.
Results may differ from a plain program's by a relative error of at most 0.011.
Values may be sent and summed in bfloat16 or wider, within the bound.
No kernel may reach another device: no remote copies, remote signals or barrier semaphores. Data moves between devices by JAX's collectives and lax.ppermute only.
A program may use at most 320 MiB of HBM per device.

v0:
```python
import jax
import jax.numpy as jnp
from jax import lax
from jax.sharding import PartitionSpec as P

HEAD_SIZE = 64


epsilon = 1e-05
negative_fill = -1000000000.0


def layer_norm(hidden, scale_gain, offset):
    center = hidden - jnp.mean(hidden, axis=-1, keepdims=True)
    spread = jnp.mean(center * center, axis=-1, keepdims=True)
    return center * lax.rsqrt(spread + epsilon) * scale_gain + offset


def product(left, right):
    return jnp.dot(left, right, preferred_element_type=jnp.float32)


def left_product(left, right):
    return lax.dot_general(
        left, right, (((0,), (0,)), ((), ())), preferred_element_type=jnp.float32
    )


def times_transposed(left, right):
    return lax.dot_general(
        left, right, (((1,), (1,)), ((), ())), preferred_element_type=jnp.float32
    )


def split_heads(packed):
    return packed.reshape(packed.shape[0], 3, -1, HEAD_SIZE).transpose(2, 1, 0, 3)


def masked_scores(query_rows, key_portion, allowed):
    return jnp.where(
        allowed, times_transposed(query_rows, key_portion) * HEAD_SIZE ** (-0.5), negative_fill
    )


def attend_forward(packed, allowed):
    length = packed.shape[0]

    def one_head(head_parts):
        attention_scores = masked_scores(head_parts[0], head_parts[1], allowed)
        row_max = jnp.max(attention_scores, axis=-1, keepdims=True)
        weights_exp = jnp.exp(attention_scores - row_max)
        row_sum = jnp.sum(weights_exp, axis=-1, keepdims=True)
        attention_probs = (weights_exp / row_sum).astype(jnp.bfloat16)
        attended = product(attention_probs, head_parts[2]).astype(jnp.bfloat16)
        return (attended, (row_max + jnp.log(row_sum))[:, 0])

    head_outputs, log_total = lax.map(one_head, split_heads(packed))
    return (head_outputs.transpose(1, 0, 2).reshape(length, -1), log_total)


def attend_backward(packed, log_total, upstream, allowed):
    length = packed.shape[0]
    upstream_heads = upstream.reshape(length, -1, HEAD_SIZE).transpose(1, 0, 2)

    def one_head(head_parts):
        pieces, head_total, head_upstream = head_parts
        attention_scores = masked_scores(pieces[0], pieces[1], allowed)
        attention_probs = jnp.exp(attention_scores - head_total[:, None])
        grad_probability = times_transposed(head_upstream, pieces[2])
        inner_sum = jnp.sum(attention_probs * grad_probability, axis=-1, keepdims=True)
        grad_scores = (attention_probs * (grad_probability - inner_sum)).astype(jnp.bfloat16)
        grad_queries = product(grad_scores, pieces[1]) * HEAD_SIZE ** (-0.5)
        grad_keys = left_product(grad_scores, pieces[0]) * HEAD_SIZE ** (-0.5)
        grad_values = left_product(attention_probs.astype(jnp.bfloat16), head_upstream)
        return jnp.stack([grad_queries, grad_keys, grad_values]).astype(jnp.bfloat16)

    head_grads = lax.map(one_head, (split_heads(packed), log_total, upstream_heads))
    return head_grads.transpose(2, 1, 0, 3).reshape(length, 3, -1)


def layer_params(weights, layer_index):
    qkv_weight, out_weight, up_weight, down_weight, norm_gains, bias_rows, up_bias = weights
    return (
        qkv_weight[layer_index],
        out_weight[layer_index],
        up_weight[layer_index],
        down_weight[layer_index],
        norm_gains[layer_index].astype(jnp.float32),
        bias_rows[layer_index].astype(jnp.float32),
        up_bias[layer_index].astype(jnp.float32),
    )


def layer_forward(hidden, params, allowed):
    qkv_weight, out_weight, up_weight, down_weight, norm_gains, bias_rows, up_bias = params
    features = hidden.shape[1]
    normed = layer_norm(hidden, norm_gains[0], bias_rows[0]).astype(jnp.bfloat16)
    offsets = jnp.concatenate([bias_rows[1], jnp.zeros_like(bias_rows[1]), bias_rows[2]])
    projected = (
        (product(normed, qkv_weight) + offsets).astype(jnp.bfloat16).reshape(-1, 3, features)
    )
    packed = lax.all_to_all(projected, "seq", split_axis=2, concat_axis=0, tiled=True)
    attended, log_total = attend_forward(packed, allowed)
    returned = lax.all_to_all(attended, "seq", split_axis=0, concat_axis=1, tiled=True)
    middle = hidden + (product(returned, out_weight) + bias_rows[3])
    second_normed = layer_norm(middle, norm_gains[1], bias_rows[4]).astype(jnp.bfloat16)
    pre_activation = product(second_normed, up_weight) + up_bias
    activated = jax.nn.gelu(pre_activation, approximate=True).astype(jnp.bfloat16)
    result = middle + (product(activated, down_weight) + bias_rows[5])
    return (
        result,
        (
            hidden,
            normed,
            packed,
            log_total,
            returned,
            middle,
            second_normed,
            pre_activation,
            activated,
        ),
    )


def layer_backward(gradient, stored, params, allowed):
    qkv_weight, out_weight, up_weight, down_weight, norm_gains, bias_rows, up_bias = params
    (
        hidden,
        normed,
        packed,
        log_total,
        returned,
        middle,
        second_normed,
        pre_activation,
        activated,
    ) = stored
    features = hidden.shape[1]
    branch_grad = gradient.astype(jnp.bfloat16)
    down_grad = left_product(activated, branch_grad)
    down_bias_grad = jnp.sum(branch_grad, axis=0, dtype=jnp.float32)
    activated_grad = times_transposed(branch_grad, down_weight)
    gelu_pull = jax.vjp(
        lambda inner_value: jax.nn.gelu(inner_value, approximate=True), pre_activation
    )[1]
    upper_grad = gelu_pull(activated_grad)[0].astype(jnp.bfloat16)
    up_grad = left_product(second_normed, upper_grad)
    up_bias_grad = jnp.sum(upper_grad, axis=0, dtype=jnp.float32)
    second_grad = times_transposed(upper_grad, up_weight)
    second_pull = jax.vjp(layer_norm, middle, norm_gains[1], bias_rows[4])[1]
    middle_part, second_gain_grad, second_offset_grad = second_pull(second_grad)
    middle_grad = gradient + middle_part
    attention_grad = middle_grad.astype(jnp.bfloat16)
    out_weight_grad = left_product(returned, attention_grad)
    out_bias_grad = jnp.sum(attention_grad, axis=0, dtype=jnp.float32)
    returned_grad = times_transposed(attention_grad, out_weight).astype(jnp.bfloat16)
    upstream = lax.all_to_all(returned_grad, "seq", split_axis=1, concat_axis=0, tiled=True)
    packed_grad = attend_backward(packed, log_total, upstream, allowed)
    projected_grad = lax.all_to_all(
        packed_grad, "seq", split_axis=0, concat_axis=2, tiled=True
    ).reshape(hidden.shape[0], 3 * features)
    qkv_grad = left_product(normed, projected_grad)
    column_sums = jnp.sum(projected_grad, axis=0, dtype=jnp.float32)
    normed_grad = times_transposed(projected_grad, qkv_weight)
    first_pull = jax.vjp(layer_norm, hidden, norm_gains[0], bias_rows[0])[1]
    hidden_part, first_gain_grad, first_offset_grad = first_pull(normed_grad)
    gain_grads = jnp.stack([first_gain_grad, second_gain_grad])
    offset_grads = jnp.stack(
        [
            first_offset_grad,
            column_sums[0:features],
            column_sums[2 * features : 3 * features],
            out_bias_grad,
            second_offset_grad,
            down_bias_grad,
        ]
    )
    return (
        middle_grad + hidden_part,
        (qkv_grad, out_weight_grad, up_grad, down_grad, gain_grads, offset_grads, up_bias_grad),
    )


def per_device(
    tokens,
    time_embed,
    segment_ids,
    pad_mask,
    out_grad,
    qkv_weight,
    out_weight,
    up_weight,
    down_weight,
    norm_gains,
    bias_rows,
    up_bias,
):
    layers = qkv_weight.shape[0]
    doc_full, padding_full = (
        lax.all_gather(segment_ids, "seq", axis=1, tiled=True),
        lax.all_gather(pad_mask, "seq", axis=1, tiled=True),
    )
    token_rows, grad_rows, time_rows, doc_rows, padding_rows = (
        tokens,
        out_grad,
        time_embed,
        doc_full,
        padding_full,
    )
    length = doc_rows.shape[1]
    positions = jnp.arange(length)
    diagonal = positions[:, None] == positions[None, :]
    totals = [None] * layers
    outputs = []
    input_grads = []
    for micro_index in range(token_rows.shape[0]):
        forward_weights = (
            lax.all_gather(qkv_weight, "wide", axis=1, tiled=True),
            lax.all_gather(out_weight, "wide", axis=1, tiled=True),
            lax.all_gather(up_weight, "wide", axis=1, tiled=True),
            lax.all_gather(down_weight, "wide", axis=1, tiled=True),
            lax.all_gather(norm_gains, "wide", axis=2, tiled=True),
            lax.all_gather(bias_rows, "wide", axis=2, tiled=True),
            lax.all_gather(up_bias, "wide", axis=1, tiled=True),
        )
        doc_row = doc_rows[micro_index]
        allowed = (doc_row[:, None] == doc_row[None, :]) & (
            (padding_rows[micro_index][None, :] == 1) | diagonal
        )
        hidden = token_rows[micro_index].astype(jnp.float32) + time_rows[micro_index][None, :]
        stored_list = []
        for layer_index in range(layers):
            hidden, stored = layer_forward(
                hidden, layer_params(forward_weights, layer_index), allowed
            )
            stored_list.append(stored)
        outputs.append(hidden)
        backward_weights = (
            lax.all_gather(qkv_weight, "wide", axis=1, tiled=True),
            lax.all_gather(out_weight, "wide", axis=1, tiled=True),
            lax.all_gather(up_weight, "wide", axis=1, tiled=True),
            lax.all_gather(down_weight, "wide", axis=1, tiled=True),
            lax.all_gather(norm_gains, "wide", axis=2, tiled=True),
            lax.all_gather(bias_rows, "wide", axis=2, tiled=True),
            lax.all_gather(up_bias, "wide", axis=1, tiled=True),
        )
        gradient = grad_rows[micro_index].astype(jnp.float32)
        for layer_index in range(layers - 1, -1, -1):
            gradient, layer_grads = layer_backward(
                gradient,
                stored_list[layer_index],
                layer_params(backward_weights, layer_index),
                allowed,
            )
            if totals[layer_index] is None:
                totals[layer_index] = layer_grads
            else:
                totals[layer_index] = tuple(
                    (earlier + later for earlier, later in zip(totals[layer_index], layer_grads))
                )
        input_grads.append(gradient)
    stacked = [
        jnp.stack([totals[layer_index][part_index] for layer_index in range(layers)])
        for part_index in range(7)
    ]
    shares = (
        lax.psum_scatter(stacked[0], "wide", scatter_dimension=1, tiled=True),
        lax.psum_scatter(stacked[1], "wide", scatter_dimension=1, tiled=True),
        lax.psum_scatter(stacked[2], "wide", scatter_dimension=1, tiled=True),
        lax.psum_scatter(stacked[3], "wide", scatter_dimension=1, tiled=True),
        lax.psum_scatter(stacked[4], "wide", scatter_dimension=2, tiled=True),
        lax.psum_scatter(stacked[5], "wide", scatter_dimension=2, tiled=True),
        lax.psum_scatter(stacked[6], "wide", scatter_dimension=1, tiled=True),
    )
    halves = (
        lax.psum_scatter(
            shares[0].astype(jnp.bfloat16), "seq", scatter_dimension=1, tiled=True
        ).astype(jnp.float32),
        lax.psum_scatter(
            shares[1].astype(jnp.bfloat16), "seq", scatter_dimension=1, tiled=True
        ).astype(jnp.float32),
        lax.psum_scatter(
            shares[2].astype(jnp.bfloat16), "seq", scatter_dimension=1, tiled=True
        ).astype(jnp.float32),
        lax.psum_scatter(
            shares[3].astype(jnp.bfloat16), "seq", scatter_dimension=1, tiled=True
        ).astype(jnp.float32),
        lax.psum_scatter(
            shares[4].astype(jnp.bfloat16), "seq", scatter_dimension=2, tiled=True
        ).astype(jnp.float32),
        lax.psum_scatter(
            shares[5].astype(jnp.bfloat16), "seq", scatter_dimension=2, tiled=True
        ).astype(jnp.float32),
        lax.psum_scatter(
            shares[6].astype(jnp.bfloat16), "seq", scatter_dimension=1, tiled=True
        ).astype(jnp.float32),
    )
    summed = (
        lax.all_gather(halves[0].astype(jnp.bfloat16), "seq", axis=1, tiled=True).astype(
            jnp.float32
        ),
        lax.all_gather(halves[1].astype(jnp.bfloat16), "seq", axis=1, tiled=True).astype(
            jnp.float32
        ),
        lax.all_gather(halves[2].astype(jnp.bfloat16), "seq", axis=1, tiled=True).astype(
            jnp.float32
        ),
        lax.all_gather(halves[3].astype(jnp.bfloat16), "seq", axis=1, tiled=True).astype(
            jnp.float32
        ),
        lax.all_gather(halves[4].astype(jnp.bfloat16), "seq", axis=2, tiled=True).astype(
            jnp.float32
        ),
        lax.all_gather(halves[5].astype(jnp.bfloat16), "seq", axis=2, tiled=True).astype(
            jnp.float32
        ),
        lax.all_gather(halves[6].astype(jnp.bfloat16), "seq", axis=1, tiled=True).astype(
            jnp.float32
        ),
    )
    final_outputs = jnp.stack(outputs)
    final_grads = jnp.stack(input_grads)
    return (
        final_outputs,
        final_grads,
        summed[0],
        summed[1],
        summed[2],
        summed[3],
        summed[4],
        summed[5],
        summed[6],
    )


def solution(mesh):
    return jax.shard_map(
        per_device,
        mesh=mesh,
        in_specs=(
            P("wide", "seq", None),
            P("wide", None),
            P("wide", "seq"),
            P("wide", "seq"),
            P("wide", "seq", None),
            P(None, "wide", None),
            P(None, "wide", None),
            P(None, "wide", None),
            P(None, "wide", None),
            P(None, None, "wide"),
            P(None, None, "wide"),
            P(None, "wide"),
        ),
        out_specs=(
            P("wide", "seq", None),
            P("wide", "seq", None),
            P(None, "wide", None),
            P(None, "wide", None),
            P(None, "wide", None),
            P(None, "wide", None),
            P(None, None, "wide"),
            P(None, None, "wide"),
            P(None, "wide"),
        ),
        check_vma=False,
    )
```

profile of v0, /device:TPU:0, one launch (start us, length us, event | category | flops | bytes accessed | tf_op | source)
XLA Modules:
  0.0 2007.0 jit_solution(4837119748774001693)
XLA Ops:
  12.1 25.5 %all_gather.66 = bf16[2,6,768]{1,0,2:T(2,128)(2,1)S(1)} all-gather(bf16[2,6,48]{1,0,2:T(2,128)(2,1)S(1)} %copy.149), channel_id=1, replica_groups=mesh['wide'=16,'seq'=2] {'wide'}, dimensions={2}, use_global_device_ids=true | all-gather | bytes 19584 | tf_op jit(solution)/shard_map/all_gather | solution.py:224
  38.3 19.5 all_gather.32
  67.3 19.3 all-gather
  86.7 31.3 %slice_reduce_fusion.1 = (f32[768]{0:T(1024)}, f32[768]{0:T(1024)}, f32[768]{0:T(1024)}, f32[768]{0:T(1024)S(1)}, f32[768]{0:T(1024)S(1)}, /*index=5*/f32[768]{0...) fusion(f32[1,6,768]{1,0,2:T(1,128)S(1)} %get-tuple-element.839,, ...), kind=kLoop, calls=%fused_computation.412 | loop fusion | bytes 73728 | tf_op jit(solution)/shard_map/slice | solution.py:106
  118.0 9.5 slice_reduce_fusion.2
  164.6 21.1 %all-to-all-done = bf16[512,3,768]{0,1,2:T(4,128)(2,1)} async-done(((bf16[512,3,768]{0,1,2:T(4,128)(2,1)}), bf16[512,3,768]{0,1,2:T(4,128)(2,1)}, u32[]{:S(2)}, u32[]{:S(2)}) %all-to-all-start) | async-done | bytes 2359328 | tf_op jit(solution)/shard_map/all_to_all | solution.py:102
  197.6 6.6 reshape.1391
  210.2 53.8 %while.96 = (s32[]{:T(128)}, bf16[6,1024,64]{1,2,0:T(8,128)(2,1)S(1)}, f32[6,1024]{1,0:T(8,128)S(1)}, bf16[6,3,1024,64]{3,2,1,0:T(8,128)(2,1)}, s32[1024]{0:T(10...) while((s32[]{:T(128)}, bf16[6,1024,64]{1,2,0:T(8,128)(2,1)S(1)}, ...), condition=%wide.region_5.6_spmd.clone, body=%wide.region_2.5_spmd.clone.sunk | while | flops 281082880 | bytes 30330020 | solution.py:57
  277.0 6.6 reshape.1395
  289.6 53.1 %while.98 = (s32[]{:T(128)}, bf16[6,1024,64]{1,2,0:T(8,128)(2,1)S(1)}, f32[6,1024]{1,0:T(8,128)S(1)}, bf16[6,3,1024,64]{3,2,1,0:T(8,128)(2,1)}, s32[1024]{0:T(10...) while((s32[]{:T(128)}, bf16[6,1024,64]{1,2,0:T(8,128)(2,1)S(1)}, ...), condition=%wide.region_21.22_spmd.clone, body=%wide.region_18.21_spmd.clone.sunk | while | flops 281082880 | bytes 30330020 | solution.py:57
  352.6 6.9 all-to-all-done.5
  363.2 8.3 fusion.187
  371.5 8.2 fusion.301
  406.6 8.7 fusion.298
  429.0 8.0 all-to-all-done.2
  448.8 6.6 reshape.1393
  461.4 53.6 %while.97 = (s32[]{:T(128)}, bf16[6,1024,64]{1,2,0:T(8,128)(2,1)S(1)}, f32[6,1024]{1,0:T(8,128)S(1)}, bf16[6,3,1024,64]{3,2,1,0:T(8,128)(2,1)}, s32[1024]{0:T(10...) while((s32[]{:T(128)}, bf16[6,1024,64]{1,2,0:T(8,128)(2,1)S(1)}, ...), condition=%wide.region_13.14_spmd.clone, body=%wide.region_10.13_spmd.clone.sunk | while | flops 281082880 | bytes 30330020 | solution.py:57
  528.0 6.6 reshape.1397
  540.7 53.4 %while.99 = (s32[]{:T(128)}, bf16[6,1024,64]{1,2,0:T(8,128)(2,1)S(1)}, f32[6,1024]{1,0:T(8,128)S(1)}, bf16[6,3,1024,64]{3,2,1,0:T(8,128)(2,1)}, s32[1024]{0:T(10...) while((s32[]{:T(128)}, bf16[6,1024,64]{1,2,0:T(8,128)(2,1)S(1)}, ...), condition=%wide.region_29.30_spmd.clone, body=%wide.region_26.29_spmd.clone.sunk | while | flops 281082880 | bytes 30330020 | solution.py:57
  617.6 10.5 convert_reduce_fusion.1
  635.7 8.1 convert_reduce_fusion
  672.1 78.9 %while.102 = (s32[]{:T(128)}, bf16[6,3,1024,64]{2,3,0,1:T(8,128)(2,1)S(1)}, bf16[6,3,1024,64]{3,2,1,0:T(8,128)(2,1)}, f32[6,1024]{1,0:T(8,128)S(1)}, bf16[6,1024...) while((s32[]{:T(128)}, ...), condition=%wide.region_50.51_spmd.clone, body=%wide.region_48.50_spmd.clone.sunk | while | flops 686226432 | bytes 51019960 | solution.py:77
  766.6 93.5 %while.100 = (s32[]{:T(128)}, bf16[6,3,1024,64]{2,3,0,1:T(8,128)(2,1)}, bf16[6,3,1024,64]{3,2,1,0:T(8,128)(2,1)}, f32[6,1024]{1,0:T(8,128)}, bf16[6,1024,64]{1,2...) while((s32[]{:T(128)}, ...), condition=%wide.region_36.37_spmd.clone, body=%wide.region_34.36_spmd.clone.sunk | while | flops 686226432 | bytes 51020976 | solution.py:77
  882.4 21.3 %all-to-all-done.9 = bf16[1024,3,384]{2,1,0:T(4,128)(2,1)} async-done(((bf16[1024,3,384]{2,1,0:T(4,128)(2,1)}), bf16[1024,3,384]{2,1,0:T(4,128)(2,1)}, u32[]{:S(2)}, u32[]{:S(2)}) %all-to-all-start.9) | async-done | bytes 2359328 | tf_op jit(solution)/shard_map/all_to_all | solution.py:160
  927.3 7.5 convert_reduce_fusion.2
  934.9 7.7 convert_reduce_fusion.3
  988.4 83.9 %while.101 = (s32[]{:T(128)}, bf16[6,3,1024,64]{2,3,0,1:T(8,128)(2,1)S(1)}, bf16[6,3,1024,64]{3,2,1,0:T(8,128)(2,1)}, f32[6,1024]{1,0:T(8,128)}, bf16[6,1024,64]...) while((s32[]{:T(128)}, ...), condition=%wide.region_43.44_spmd.clone, body=%wide.region_41.43_spmd.clone.sunk | while | flops 686226432 | bytes 51019960 | solution.py:77
  1087.9 93.1 %while.103 = (s32[]{:T(128)}, bf16[6,3,1024,64]{2,3,0,1:T(8,128)(2,1)}, bf16[6,3,1024,64]{3,2,1,0:T(8,128)(2,1)}, f32[6,1024]{1,0:T(8,128)}, bf16[6,1024,64]{1,2...) while((s32[]{:T(128)}, ...), condition=%wide.region_57.58_spmd.clone, body=%wide.region_55.57_spmd.clone.sunk | while | flops 686226432 | bytes 51020976 | solution.py:77
  1206.9 18.6 all-to-all-done.15
  1243.3 11.0 pad_maximum_fusion.2
  1255.7 12.0 fusion.244
  1267.7 11.8 add_bitcast_fusion
  1279.6 6.7 fusion.265
  1286.3 10.6 add_bitcast_fusion.1
  1296.9 6.7 pad_maximum_fusion.1
  1326.5 12.9 pad_maximum_fusion
  1365.4 32.7 %reduce-scatter.29.cloned.1.call-done = f32[2,48,2304]{2,1,0:T(8,128)} async-done(((f32[2,768,2304]{2,1,0:T(8,128)}), f32[2,48,2304]{2,1,0:T(8,128)}) %reduce-scatter.29.cloned.1.call-update) | async-done | bytes 884752 | tf_op jit(solution)/shard_map/reduce_scatter | solution.py:268
  1400.5 9.7 add_bitcast_fusion.11
  1410.3 185.9 %reduce-scatter.35.cloned.1.call-done = f32[2,192,768]{2,1,0:T(8,128)} async-done(((f32[2,3072,768]{2,1,0:T(8,128)}), f32[2,192,768]{2,1,0:T(8,128)}) %reduce-scatter.35.cloned.1.call-update) | async-done | bytes 1179664 | tf_op jit(solution)/shard_map/reduce_scatter | solution.py:271
  1598.4 8.2 add_bitcast_fusion.10
  1618.2 188.6 %reduce-scatter.33.cloned.1.call-done = f32[2,48,3072]{2,1,0:T(8,128)} async-done(((f32[2,768,3072]{2,1,0:T(8,128)}), f32[2,48,3072]{2,1,0:T(8,128)}) %reduce-scatter.33.cloned.1.call-update) | async-done | bytes 1179664 | tf_op jit(solution)/shard_map/reduce_scatter | solution.py:270
  1814.4 50.7 %reduce-scatter.45.cloned.1.call-done = f32[48,4]{1,0:T(8,128)} async-done(((f32[768,4]{1,0:T(8,128)}), f32[48,4]{1,0:T(8,128)}) %reduce-scatter.45.cloned.1.call-update) | async-done | bytes 784
  1866.0 57.5 %reduce-scatter.47.cloned.1.call-done = f32[48,12]{1,0:T(8,128)} async-done(((f32[768,12]{1,0:T(8,128)}), f32[48,12]{1,0:T(8,128)}) %reduce-scatter.47.cloned.1.call-update) | async-done | bytes 2320
  1953.2 7.9 all_gather.74
  1962.0 8.3 reduce-scatter.37.cloned.1.call-done
  1970.3 9.6 all_gather.77
  1981.0 7.3 reduce-scatter.43.cloned.1.call-done
  1989.5 9.4 all_gather.76
  (1152 shorter events, 1072.4 us)
Async XLA Ops:
  7.2 120.3 %all-gather.7.cloned.1.call-start = ((), (), s32[]{:S(2)}) async-start(), calls=%async_computation.28 | async-start | bytes 7520256 | tf_op jit(solution)/shard_map/all_gather | solution.py:219
  7.9 340.7 %all-gather.9.cloned.1.call-start = ((), (), s32[]{:S(2)}) async-start(), calls=%async_computation.29 | async-start | bytes 2506752 | tf_op jit(solution)/shard_map/all_gather | solution.py:220
  8.7 354.5 %all-gather.11.cloned.1.call-start = ((), (), s32[]{:S(2)}) async-start(), calls=%async_computation.30 | async-start | bytes 10027008 | tf_op jit(solution)/shard_map/all_gather | solution.py:221
  9.4 362.1 %all-gather.13.cloned.1.call-start = ((), (), s32[]{:S(2)}) async-start(), calls=%async_computation.31 | async-start | bytes 10027008 | tf_op jit(solution)/shard_map/all_gather | solution.py:222
  10.8 337.9 %copy-start.72 = (f32[768]{0:T(1024)}, f32[768]{0:T(1024)S(1)}, u32[]{:S(2)}) copy-start(f32[768]{0:T(1024)S(1)} %get-tuple-element.675) | copy-start | bytes 9220
  10.8 349.6 %copy-start.70 = (f32[768]{0:T(1024)}, f32[768]{0:T(1024)S(1)}, u32[]{:S(2)}) copy-start(f32[768]{0:T(1024)S(1)} %get-tuple-element.676) | copy-start | bytes 9220
  11.2 137.9 %copy-start.95 = (f32[512]{0:T(512)}, f32[512]{0:T(512)S(1)}, u32[]{:S(2)}) copy-start(f32[512]{0:T(512)S(1)} %broadcast_multiply_fusion.3) | copy-start | bytes 6148
  11.2 116.3 %copy-start.97 = (f32[512]{0:T(512)}, f32[512]{0:T(512)S(1)}, u32[]{:S(2)}) copy-start(f32[512]{0:T(512)S(1)} %broadcast_multiply_fusion.7) | copy-start | bytes 6148
  11.9 55.3 %copy-start.112 = (f32[512]{0:T(512)}, f32[512]{0:T(512)S(1)}, u32[]{:S(2)}) copy-start(f32[512]{0:T(512)S(1)} %get-tuple-element.653) | copy-start | bytes 6148
  11.9 74.8 %copy-start.114 = (f32[512]{0:T(512)}, f32[512]{0:T(512)S(1)}, u32[]{:S(2)}) copy-start(f32[512]{0:T(512)S(1)} %get-tuple-element.654) | copy-start | bytes 6148
  12.0 115.6 %copy-start.124 = (f32[512]{0:T(512)}, f32[512]{0:T(512)S(1)}, u32[]{:S(2)}) copy-start(f32[512]{0:T(512)S(1)} %fusion.255) | copy-start | bytes 6148
  86.7 62.5 %copy-start.126 = (f32[512]{0:T(512)}, f32[512]{0:T(512)S(1)}, u32[]{:S(2)}) copy-start(f32[512]{0:T(512)S(1)} %fusion.259) | copy-start | bytes 6148
  118.0 283.7 %copy-start.66 = (f32[768]{0:T(1024)}, f32[768]{0:T(1024)S(1)}, u32[]{:S(2)}) copy-start(f32[768]{0:T(1024)S(1)} %get-tuple-element.899) | copy-start | bytes 9220
  118.0 297.8 %copy-start.132 = (f32[768]{0:T(1024)}, f32[768]{0:T(1024)S(1)}, u32[]{:S(2)}) copy-start(f32[768]{0:T(1024)S(1)} %get-tuple-element.664) | copy-start | bytes 9220
  127.5 274.3 %copy-start.61 = (f32[768]{0:T(1024)}, f32[768]{0:T(1024)S(1)}, u32[]{:S(2)}) copy-start(f32[768]{0:T(1024)S(1)} %get-tuple-element.901) | copy-start | bytes 9220
  127.5 288.3 %copy-start.84 = (f32[768]{0:T(1024)}, f32[768]{0:T(1024)S(1)}, u32[]{:S(2)}) copy-start(f32[768]{0:T(1024)S(1)} %get-tuple-element.658) | copy-start | bytes 9220
  142.9 42.8 %all-to-all-start = ((bf16[512,3,768]{0,1,2:T(4,128)(2,1)}), bf16[512,3,768]{0,1,2:T(4,128)(2,1)}, u32[]{:S(2)}, u32[]{:S(2)}) async-start(bf16[512,3,768]{0,1,2:T(4,128)(2,1)} %copy.151), calls=%async_computation | async-start | bytes 6291456 | tf_op jit(solution)/shard_map/all_to_all | solution.py:102
  149.2 257.4 %copy-start.144 = (f32[1,3072]{1,0:T(1,128)}, f32[1,3072]{1,0:T(1,128)S(1)}, u32[]{:S(2)}) copy-start(f32[1,3072]{1,0:T(1,128)S(1)} %get-tuple-element.842) | copy-start | bytes 36868
  185.7 80.4 %all-to-all-start.4 = ((bf16[512,3,768]{0,1,2:T(4,128)(2,1)}), bf16[512,3,768]{0,1,2:T(4,128)(2,1)}, u32[]{:S(2)}, u32[]{:S(2)}) async-start(bf16[512,3,768]{0,1,2:T(4,128)(2,1)} %copy.164), calls=%async_computation.4 | async-start | bytes 6291456 | tf_op jit(solution)/shard_map/all_to_all | solution.py:102
  266.1 78.7 %all-to-all-start.1 = ((bf16[2,512,384]{1,2,0:T(8,128)(2,1)}), bf16[2,512,384]{1,2,0:T(8,128)(2,1)}, u32[]{:S(2)}, u32[]{:S(2)}) async-start(bf16[2,512,384]{1,2,0:T(8,128)(2,1)} %copy.155), calls=%async_computation.1 | async-start | bytes 1572864 | tf_op jit(solution)/shard_map/all_to_all | solution.py:104
  344.9 14.6 all-to-all-start.5
  396.5 40.6 %all-to-all-start.2 = ((bf16[512,3,768]{0,1,2:T(4,128)(2,1)}), bf16[512,3,768]{0,1,2:T(4,128)(2,1)}, u32[]{:S(2)}, u32[]{:S(2)}) async-start(bf16[512,3,768]{0,1,2:T(4,128)(2,1)} %copy.158), calls=%async_computation.2 | async-start | bytes 6291456 | tf_op jit(solution)/shard_map/all_to_all | solution.py:102
  415.4 193.8 %copy-start.15 = (f32[512,768]{1,0:T(8,128)}, f32[512,768]{1,0:T(8,128)S(1)}, u32[]{:S(2)}) copy-start(f32[512,768]{1,0:T(8,128)S(1)} %get-tuple-element.873) | copy-start | bytes 4718596
  437.1 80.1 %all-to-all-start.6 = ((bf16[512,3,768]{0,1,2:T(4,128)(2,1)}), bf16[512,3,768]{0,1,2:T(4,128)(2,1)}, u32[]{:S(2)}, u32[]{:S(2)}) async-start(bf16[512,3,768]{0,1,2:T(4,128)(2,1)} %copy.170), calls=%async_computation.6 | async-start | bytes 6291456 | tf_op jit(solution)/shard_map/all_to_all | solution.py:102
  517.1 78.6 %all-to-all-start.3 = ((bf16[2,512,384]{1,2,0:T(8,128)(2,1)}), bf16[2,512,384]{1,2,0:T(8,128)(2,1)}, u32[]{:S(2)}, u32[]{:S(2)}) async-start(bf16[2,512,384]{1,2,0:T(8,128)(2,1)} %copy.162), calls=%async_computation.3 | async-start | bytes 1572864 | tf_op jit(solution)/shard_map/all_to_all | solution.py:104
  595.7 13.5 all-to-all-start.7
  654.4 11.7 all-to-all-start.12
  666.0 88.6 %all-to-all-start.8 = ((bf16[512,2,384]{0,2,1:T(8,128)(2,1)}), bf16[512,2,384]{0,2,1:T(8,128)(2,1)}, u32[]{:S(2)}, u32[]{:S(2)}) async-start(bf16[512,2,384]{0,2,1:T(8,128)(2,1)} %bitcast.50), calls=%async_computation.8 | async-start | bytes 1572864 | tf_op jit(solution)/shard_map/all_to_all | solution.py:158
  754.6 111.1 %all-to-all-start.13 = ((bf16[1024,3,384]{2,1,0:T(4,128)(2,1)}), bf16[1024,3,384]{2,1,0:T(4,128)(2,1)S(1)}, u32[]{:S(2)}, u32[]{:S(2)}) async-start(bf16[1024,3,384]{2,1,0:T(4,128)(2,1)} %copy.196), calls=%async_computation.13 | async-start | bytes 6291456 | tf_op jit(solution)/shard_map/all_to_all | solution.py:160
  865.7 38.0 %all-to-all-start.9 = ((bf16[1024,3,384]{2,1,0:T(4,128)(2,1)}), bf16[1024,3,384]{2,1,0:T(4,128)(2,1)}, u32[]{:S(2)}, u32[]{:S(2)}) async-start(bf16[1024,3,384]{2,1,0:T(4,128)(2,1)} %copy.180), calls=%async_computation.9 | async-start | bytes 6291456 | tf_op jit(solution)/shard_map/all_to_all | solution.py:160
  871.1 453.6 %reduce-scatter.49.cloned.1.call-start = ((), (), s32[]{:S(2)}) async-start(), calls=%async_computation.42 | async-start | bytes 1671168
  968.0 13.2 all-to-all-start.10
  972.3 389.9 %reduce-scatter.31.cloned.1.call-start = ((), (), s32[]{:S(2)}) async-start(), calls=%async_computation.33 | async-start | bytes 5013504 | tf_op jit(solution)/shard_map/reduce_scatter | solution.py:269
  981.2 94.9 %all-to-all-start.14 = ((bf16[512,2,384]{0,2,1:T(8,128)(2,1)}), bf16[512,2,384]{0,2,1:T(8,128)(2,1)}, u32[]{:S(2)}, u32[]{:S(2)}) async-start(bf16[512,2,384]{0,2,1:T(8,128)(2,1)} %bitcast.76), calls=%async_computation.14 | async-start | bytes 1572864 | tf_op jit(solution)/shard_map/all_to_all | solution.py:158
  1076.1 110.7 %all-to-all-start.11 = ((bf16[1024,3,384]{2,1,0:T(4,128)(2,1)}), bf16[1024,3,384]{2,1,0:T(4,128)(2,1)S(1)}, u32[]{:S(2)}, u32[]{:S(2)}) async-start(bf16[1024,3,384]{2,1,0:T(4,128)(2,1)} %copy.188), calls=%async_computation.11 | async-start | bytes 6291456 | tf_op jit(solution)/shard_map/all_to_all | solution.py:160
  1188.5 37.1 %all-to-all-start.15 = ((bf16[1024,3,384]{2,1,0:T(4,128)(2,1)}), bf16[1024,3,384]{2,1,0:T(4,128)(2,1)}, u32[]{:S(2)}, u32[]{:S(2)}) async-start(bf16[1024,3,384]{2,1,0:T(4,128)(2,1)} %copy.204), calls=%async_computation.15 | async-start | bytes 6291456 | tf_op jit(solution)/shard_map/all_to_all | solution.py:160
  1193.8 204.3 %reduce-scatter.29.cloned.1.call-start = ((), (), s32[]{:S(2)}) async-start(), calls=%async_computation.32 | async-start | bytes 15040512 | tf_op jit(solution)/shard_map/reduce_scatter | solution.py:268
  1254.3 341.9 %reduce-scatter.35.cloned.1.call-start = ((), (), s32[]{:S(2)}) async-start(), calls=%async_computation.35 | async-start | bytes 20054016 | tf_op jit(solution)/shard_map/reduce_scatter | solution.py:271
  1303.7 304.9 %reduce-scatter.51.cloned.1.call-start = ((), (), s32[]{:S(2)}) async-start(), calls=%async_computation.43 | async-start | bytes 73728
  1326.5 480.4 %reduce-scatter.33.cloned.1.call-start = ((), (), s32[]{:S(2)}) async-start(), calls=%async_computation.34 | async-start | bytes 20054016 | tf_op jit(solution)/shard_map/reduce_scatter | solution.py:270
  1339.6 525.5 %reduce-scatter.45.cloned.1.call-start = ((), (), s32[]{:S(2)}) async-start(), calls=%async_computation.40 | async-start | bytes 417792
  1357.0 566.5 %reduce-scatter.47.cloned.1.call-start = ((), (), s32[]{:S(2)}) async-start(), calls=%async_computation.41 | async-start | bytes 417792
  1362.2 577.9 %reduce-scatter.41.cloned.1.call-start = ((), (), s32[]{:S(2)}) async-start(), calls=%async_computation.38 | async-start | bytes 221184
  1364.1 588.1 %reduce-scatter.39.cloned.1.call-start = ((), (), s32[]{:S(2)}) async-start(), calls=%async_computation.37 | async-start | bytes 663552
  1400.5 569.8 %reduce-scatter.37.cloned.1.call-start = ((), (), s32[]{:S(2)}) async-start(), calls=%async_computation.36 | async-start | bytes 884736 | tf_op jit(solution)/shard_map/reduce_scatter | solution.py:286
  1598.4 389.9 %reduce-scatter.43.cloned.1.call-start = ((), (), s32[]{:S(2)}) async-start(), calls=%async_computation.39 | async-start | bytes 884736
  1618.2 191.6 %copy-start.20 = (f32[512,768]{1,0:T(8,128)S(1)}, f32[512,768]{1,0:T(8,128)}, u32[]{:S(2)}) copy-start(f32[512,768]{1,0:T(8,128)} %copy-done.18) | copy-start | bytes 4718596
  1618.2 191.6 %copy-start.129 = (f32[512]{0:T(512)S(1)}, f32[512]{0:T(512)}, u32[]{:S(2)}) copy-start(f32[512]{0:T(512)} %copy-done.128) | copy-start | bytes 6148
  (234 other events, 1715.0 us)
Sparse Core Ops, SparseCore 0:
  10.3 71.6 all-gather.6
  84.2 41.9 all-gather.8
  128.5 80.2 all-gather.10
  211.0 79.5 all-gather.12
  944.5 57.1 reduce-scatter.48
  1005.8 74.5 reduce-scatter.30
  1254.4 143.6 reduce-scatter.28
  1402.2 193.9 reduce-scatter.34
  1599.0 8.9 reduce-scatter.50
  1611.9 194.8 reduce-scatter.32
  1810.4 54.6 reduce-scatter.44
  1868.8 54.6 reduce-scatter.46
  1926.3 9.7 reduce-scatter.40
  1938.8 13.3 reduce-scatter.38
  1955.0 15.2 reduce-scatter.36
  1973.0 15.2 reduce-scatter.42
where the time goes:
time: 2020 us; the launch traced here: 2010 us
  matrix products  703 us (35%)
  waiting for transfers between devices  626 us (31%)
  local copies, waits for them, and re-layouts  327 us (16%)
  other arithmetic  133 us (7%)
  blocking collectives  124 us (6%)
  starting transfers between devices  74.7 us (4%)
    dot_general x88, matrix products, times_transposed(): lax.dot_general(left, right, (((1,), (1,)), ((), ())), preferred_element_...  343 us
    dot_general x64, matrix products, product(): return jnp.dot(left, right, preferred_element_type=jnp.float32)  199 us
    reduce_scatter x1, waiting for transfers between devices, per_device(): lax.psum_scatter(stacked[2], 'wide', scatter_dimension=1, tiled=True)  189 us
    reduce_scatter x1, waiting for transfers between devices, per_device(): lax.psum_scatter(stacked[3], 'wide', scatter_dimension=1, tiled=True)  186 us
    dot_general x64, matrix products, left_product(): lax.dot_general(left, right, (((0,), (0,)), ((), ())), preferred_element_...  161 us
    unnamed x23, waiting for transfers between devices  123 us
    unnamed x460, local copies, waits for them, and re-layouts  62.7 us
    while x96, local copies, waits for them, and re-layouts  48 us
  transfers between devices with their start and end apart: 32, of which 15 were waited for; matrix products, arithmetic and copies ran while one was open for 49% of the time, Pallas kernels for 0%

commit v1 on v0

v1 whole, which is shorter than its diff:
```python
import functools

import jax
import jax.numpy as jnp
from jax import lax
from jax.experimental import pallas as pl
from jax.experimental.pallas import tpu as pltpu
from jax.sharding import PartitionSpec as P

HEAD_SIZE = 64
PAIR = 2 * HEAD_SIZE
FORWARD_ROWS = 512
BACKWARD_ROWS = 256

epsilon = 1e-05
masked_bias = -1e30
half = jnp.bfloat16
single = jnp.float32


def contract(left, right, left_dim, right_dim):
    return lax.dot_general(
        left, right, (((left_dim,), (right_dim,)), ((), ())), preferred_element_type=jnp.float32
    )


def first_head_lanes():
    return lax.broadcasted_iota(jnp.int32, (1, PAIR), 1) < HEAD_SIZE


def one_head_of(pair, head):
    lanes = first_head_lanes()
    keep = lanes if head == 0 else jnp.logical_not(lanes)
    return jnp.where(keep, pair, jnp.zeros_like(pair))


def attend_kernel(query_ref, key_ref, value_ref, bias_ref, out_ref, total_ref, *, rows):
    keys = key_ref[...]
    values = value_ref[...]
    scale = jnp.asarray(HEAD_SIZE ** (-0.5), half)
    for start in range(0, keys.shape[0], rows):
        window = pl.ds(start, rows)
        queries = query_ref[window, :] * scale
        bias = bias_ref[:, window]
        attended = []
        for head in range(2):
            scores = contract(keys, one_head_of(queries, head), 1, 1) + bias
            top = jnp.max(scores, axis=0, keepdims=True)
            weights = jnp.exp(scores - top)
            total = jnp.sum(weights, axis=0, keepdims=True)
            mixed = contract(values, weights.astype(half), 0, 0) * (1.0 / total)
            attended.append(mixed[HEAD_SIZE * head : HEAD_SIZE * (head + 1)])
            total_ref[head : head + 1, window] = top + jnp.log(total)
        out_ref[window, :] = jnp.concatenate(attended, 0).T.astype(half)


def attend_forward(packed, bias):
    length = packed.shape[0]
    features = packed.shape[1] // 3
    pairs = features // PAIR
    columns = lambda part: pl.BlockSpec((length, PAIR), lambda i: (0, part * pairs + i))
    return pl.pallas_call(
        functools.partial(attend_kernel, rows=FORWARD_ROWS),
        grid=(pairs,),
        in_specs=[
            columns(0),
            columns(1),
            columns(2),
            pl.BlockSpec((length, length), lambda i: (0, 0)),
        ],
        out_specs=[columns(0), pl.BlockSpec((None, 2, length), lambda i: (i, 0, 0))],
        out_shape=[
            jax.ShapeDtypeStruct((length, features), half),
            jax.ShapeDtypeStruct((pairs, 2, length), single),
        ],
        compiler_params=pltpu.CompilerParams(vmem_limit_bytes=56 << 20),
        cost_estimate=pl.CostEstimate(
            flops=4 * length * length * features * 4,
            bytes_accessed=8 * length * features,
            transcendentals=length * length * features // HEAD_SIZE,
        ),
        name="attend_forward",
    )(packed, packed, packed, bias)


def attend_grad_kernel(
    query_ref,
    key_ref,
    value_ref,
    bias_ref,
    upstream_ref,
    total_ref,
    attended_ref,
    out_ref,
    key_sum,
    value_sum,
    *,
    rows,
):
    pair = pl.program_id(0)
    features = out_ref.shape[1] // 3
    keys = key_ref[...]
    values = value_ref[...]
    scale = HEAD_SIZE ** (-0.5)
    for start in range(0, keys.shape[0], rows):
        window = pl.ds(start, rows)
        queries = query_ref[window, :] * jnp.asarray(scale, half)
        upstream = upstream_ref[window, :]
        product = (upstream.astype(single) * attended_ref[window, :].astype(single)).T
        bias = bias_ref[:, window]
        query_grads, key_grad, value_grad = [], 0.0, 0.0
        for head in range(2):
            head_queries = one_head_of(queries, head)
            head_upstream = one_head_of(upstream, head)
            inner = jnp.sum(
                product[HEAD_SIZE * head : HEAD_SIZE * (head + 1)], axis=0, keepdims=True
            )
            scores = contract(keys, head_queries, 1, 1) + bias
            weights = jnp.exp(scores - total_ref[head : head + 1, window])
            weight_grads = contract(values, head_upstream, 1, 1)
            score_grads = (weights * (weight_grads - inner)).astype(half)
            value_grad = value_grad + contract(weights.astype(half), head_upstream, 1, 0)
            key_grad = key_grad + contract(score_grads, head_queries, 1, 0)
            query_grads.append(
                contract(keys, score_grads, 0, 0)[HEAD_SIZE * head : HEAD_SIZE * (head + 1)]
            )
        out_ref[window, pl.ds(pl.multiple_of(pair * PAIR, PAIR), PAIR)] = (
            jnp.concatenate(query_grads, 0).T * scale
        ).astype(half)
        if start == 0:
            key_sum[...] = key_grad
            value_sum[...] = value_grad
        else:
            key_sum[...] += key_grad
            value_sum[...] += value_grad
    out_ref[:, pl.ds(pl.multiple_of(features + pair * PAIR, PAIR), PAIR)] = key_sum[...].astype(
        half
    )
    out_ref[:, pl.ds(pl.multiple_of(2 * features + pair * PAIR, PAIR), PAIR)] = value_sum[
        ...
    ].astype(half)


def attend_backward(packed, bias, upstream, totals, attended):
    length = packed.shape[0]
    features = packed.shape[1] // 3
    pairs = features // PAIR
    columns = lambda part: pl.BlockSpec((length, PAIR), lambda i: (0, part * pairs + i))
    return pl.pallas_call(
        functools.partial(attend_grad_kernel, rows=BACKWARD_ROWS),
        grid=(pairs,),
        in_specs=[
            columns(0),
            columns(1),
            columns(2),
            pl.BlockSpec((length, length), lambda i: (0, 0)),
            columns(0),
            pl.BlockSpec((None, 2, length), lambda i: (i, 0, 0)),
            columns(0),
        ],
        out_specs=pl.BlockSpec((length, 3 * features), lambda i: (0, 0)),
        out_shape=jax.ShapeDtypeStruct((length, 3 * features), half),
        scratch_shapes=[pltpu.VMEM((length, PAIR), single)] * 2,
        compiler_params=pltpu.CompilerParams(vmem_limit_bytes=56 << 20),
        cost_estimate=pl.CostEstimate(
            flops=10 * length * length * features * 4,
            bytes_accessed=16 * length * features,
            transcendentals=length * length * features // HEAD_SIZE,
        ),
        name="attend_backward",
    )(packed, packed, packed, bias, upstream, totals, attended)


def layer_norm(hidden, scale_gain, offset):
    center = hidden - jnp.mean(hidden, axis=-1, keepdims=True)
    spread = jnp.mean(center * center, axis=-1, keepdims=True)
    return center * lax.rsqrt(spread + epsilon) * scale_gain + offset


def layer_norm_grad(hidden, scale_gain, upstream):
    center = hidden - jnp.mean(hidden, axis=-1, keepdims=True)
    inverse = lax.rsqrt(jnp.mean(center * center, axis=-1, keepdims=True) + epsilon)
    normal = center * inverse
    scaled = upstream * scale_gain
    slope = jnp.mean(scaled, axis=-1, keepdims=True)
    tilt = jnp.mean(scaled * normal, axis=-1, keepdims=True)
    return (
        inverse * (scaled - slope - normal * tilt),
        jnp.sum(upstream * normal, axis=0),
        jnp.sum(upstream, axis=0),
    )


def layer_forward(hidden, matrices, rows, bias):
    qkv_weight, out_weight, up_weight, down_weight = matrices
    gains, offsets, up_bias = rows
    normed = layer_norm(hidden, gains[0], offsets[0]).astype(half)
    shift = jnp.concatenate([offsets[1], jnp.zeros_like(offsets[1]), offsets[2]])
    packed = (contract(normed, qkv_weight, 1, 0) + shift).astype(half)
    attended, totals = attend_forward(packed, bias)
    middle = hidden + (contract(attended, out_weight, 1, 0) + offsets[3])
    second = layer_norm(middle, gains[1], offsets[4]).astype(half)
    pre_activation = contract(second, up_weight, 1, 0) + up_bias
    activated = jax.nn.gelu(pre_activation, approximate=True).astype(half)
    result = middle + (contract(activated, down_weight, 1, 0) + offsets[5])
    return (
        result,
        (hidden, normed, packed, totals, attended, middle, second, pre_activation, activated),
    )


def per_device(
    tokens,
    time_embed,
    segment_ids,
    pad_mask,
    out_grad,
    qkv_weight,
    out_weight,
    up_weight,
    down_weight,
    norm_gains,
    bias_rows,
    up_bias,
):
    layers = qkv_weight.shape[0]
    features = tokens.shape[2]
    groups = lax.axis_size("wide")
    swap = [(0, 1), (1, 0)]

    def whole_sequence(part):
        return lax.all_to_all(part, "seq", split_axis=0, concat_axis=1, tiled=True)[0]

    marks = whole_sequence(jnp.stack([segment_ids, pad_mask], axis=2))
    my_tokens = whole_sequence(tokens)
    my_upstream = whole_sequence(out_grad)
    my_time = lax.dynamic_index_in_dim(time_embed, lax.axis_index("seq"), 0, keepdims=True)

    sources = (qkv_weight, out_weight, up_weight, down_weight)
    small = jnp.concatenate(
        [norm_gains.reshape(-1), bias_rows.reshape(-1), up_bias.reshape(-1)]
    )
    matrices = [[None] * 4 for _ in range(layers)]
    matrices[0][0] = lax.all_gather(qkv_weight[0], "wide", axis=0, tiled=True)
    small_whole = lax.all_gather(small, "wide", axis=0, tiled=False)
    for layer in range(layers):
        for index, source in enumerate(sources):
            if matrices[layer][index] is None:
                matrices[layer][index] = lax.all_gather(
                    source[layer], "wide", axis=0, tiled=True
                )
    cut_gains = norm_gains.size
    cut_rows = cut_gains + bias_rows.size

    def whole_rows(part, count):
        parts = part.reshape(groups, layers, count, -1)
        return parts.transpose(1, 2, 0, 3).reshape(layers, count, -1).astype(single)

    all_gains = whole_rows(small_whole[:, :cut_gains], norm_gains.shape[1])
    all_offsets = whole_rows(small_whole[:, cut_gains:cut_rows], bias_rows.shape[1])
    all_up_bias = whole_rows(small_whole[:, cut_rows:], 1)[:, 0]

    doc, pad = marks[:, 0], marks[:, 1]
    positions = jnp.arange(doc.shape[0])
    allowed = (doc[:, None] == doc[None, :]) & (
        (pad[:, None] == 1) | (positions[:, None] == positions[None, :])
    )
    bias = jnp.where(allowed, 0.0, masked_bias)

    hidden = my_tokens.astype(single) + my_time
    saved = []
    for layer in range(layers):
        rows = (all_gains[layer], all_offsets[layer], all_up_bias[layer])
        hidden, kept = layer_forward(hidden, matrices[layer], rows, bias)
        saved.append(kept)

    def split_back(result):
        parts = result.reshape(2, -1, features).astype(half)
        return lax.all_to_all(parts, "seq", split_axis=0, concat_axis=0, tiled=True)

    output = split_back(hidden).astype(single)

    def scatter(term):
        share = lax.psum_scatter(term.astype(half), "wide", scatter_dimension=0, tiled=True)
        other = lax.ppermute(share, "seq", swap)
        return share.astype(single) + other.astype(single)

    gradient = my_upstream.astype(single)
    weight_grads = [None] * layers
    small_grads = [None] * layers
    for layer in range(layers - 1, -1, -1):
        qkv_full, out_full, up_full, down_full = matrices[layer]
        gains = all_gains[layer]
        (hidden, normed, packed, totals, attended, middle, second, pre_activation, activated) = (
            saved[layer]
        )
        branch = gradient.astype(half)
        down_share = scatter(contract(activated, branch, 0, 0))
        down_bias_grad = jnp.sum(branch, axis=0, dtype=single)
        activated_grad = contract(branch, down_full, 1, 1)
        pull = jax.vjp(lambda value: jax.nn.gelu(value, approximate=True), pre_activation)[1]
        upper = pull(activated_grad)[0].astype(half)
        up_share = scatter(contract(second, upper, 0, 0))
        up_bias_grad = jnp.sum(upper, axis=0, dtype=single)
        second_grad = contract(upper, up_full, 1, 1)
        middle_part, second_gain, second_offset = layer_norm_grad(middle, gains[1], second_grad)
        middle_grad = gradient + middle_part
        attention_grad = middle_grad.astype(half)
        out_share = scatter(contract(attended, attention_grad, 0, 0))
        out_bias_grad = jnp.sum(attention_grad, axis=0, dtype=single)
        upstream = contract(attention_grad, out_full, 1, 1).astype(half)
        packed_grad = attend_backward(packed, bias, upstream, totals, attended)
        qkv_share = scatter(contract(normed, packed_grad, 0, 0))
        column_sums = jnp.sum(packed_grad, axis=0, dtype=single)
        normed_grad = contract(packed_grad, qkv_full, 1, 1)
        hidden_part, first_gain, first_offset = layer_norm_grad(hidden, gains[0], normed_grad)
        gradient = middle_grad + hidden_part
        weight_grads[layer] = (qkv_share, out_share, up_share, down_share)
        small_grads[layer] = (
            jnp.stack([first_gain, second_gain]),
            jnp.stack(
                [
                    first_offset,
                    column_sums[:features],
                    column_sums[2 * features :],
                    out_bias_grad,
                    second_offset,
                    down_bias_grad,
                ]
            ),
            up_bias_grad,
        )
    input_grad = split_back(gradient).astype(single)

    def by_owner(parts):
        stacked = jnp.stack(parts)
        stacked = stacked.reshape(layers, -1, groups, stacked.shape[-1] // groups)
        return stacked.transpose(2, 0, 1, 3).reshape(groups, -1)

    owned = jnp.concatenate(
        [by_owner([small_grads[layer][part] for layer in range(layers)]) for part in range(3)],
        axis=1,
    )
    owned = lax.psum_scatter(owned, "wide", scatter_dimension=0, tiled=True)[0]
    owned = owned + lax.ppermute(owned, "seq", swap)
    stacked = [
        jnp.stack([weight_grads[layer][part] for layer in range(layers)]) for part in range(4)
    ]
    return (
        output,
        input_grad,
        *stacked,
        owned[:cut_gains].reshape(norm_gains.shape),
        owned[cut_gains:cut_rows].reshape(bias_rows.shape),
        owned[cut_rows:].reshape(up_bias.shape),
    )


def solution(mesh):
    tokens_spec = P("wide", "seq", None)
    matrix_spec = P(None, "wide", None)
    rows_spec = P(None, None, "wide")
    return jax.shard_map(
        per_device,
        mesh=mesh,
        in_specs=(
            tokens_spec,
            P("wide", None),
            P("wide", "seq"),
            P("wide", "seq"),
            tokens_spec,
            matrix_spec,
            matrix_spec,
            matrix_spec,
            matrix_spec,
            rows_spec,
            rows_spec,
            P(None, "wide"),
        ),
        out_specs=(
            tokens_spec,
            tokens_spec,
            matrix_spec,
            matrix_spec,
            matrix_spec,
            matrix_spec,
            rows_spec,
            rows_spec,
            P(None, "wide"),
        ),
        check_vma=False,
    )
```

time: 2020 us -> 1200 us (0.59)
  matrix products: 703 us -> 216 us
  local copies, waits for them, and re-layouts: 327 us -> 27 us
  Pallas kernels: 0 us -> 125 us
  blocking collectives: 124 us -> 22.4 us
  other arithmetic: 133 us -> 38.1 us
  waiting for transfers between devices: 626 us -> 717 us
  starting transfers between devices: 74.7 us -> 32 us
    dot_general x216 -> x24, matrix products: 703 us -> 216 us  [contract(): lax.dot_general(left, right, (((left_dim,), (right_dim,)), ((), ())), pre...]
    all_gather x4 -> x8, waiting for transfers between devices: 0.06 us -> 195 us  [the longest x7 195 us: per_device(): lax.all_gather(source[layer], 'wide', axis=0, tiled=True)]
    pallas_call x0 -> x4, Pallas kernels: none -> 125 us  [the longest x2 74.6 us: attend_backward(): pl.pallas_call(functools.partial(attend_grad_kernel, rows=BACKWARD_ROWS),...]
    unnamed x23 -> x18, waiting for transfers between devices: 123 us -> 2.69 us
    all_gather x12 -> x1, blocking collectives: 119 us -> 22.4 us  [per_device(): small_whole = lax.all_gather(small, 'wide', axis=0, tiled=False)]
    reshape x16 -> x7, local copies, waits for them, and re-layouts: 74.5 us -> 0.61 us  [the longest x3 0.28 us: by_owner(): return stacked.transpose(2, 0, 1, 3).reshape(groups, -1)]
    all_to_all x28 -> x0, local copies, waits for them, and re-layouts: 60.4 us -> none  [the longest x8 25.6 us: layer_forward(): lax.all_to_all(projected, 'seq', split_axis=2, concat_axis=0, tiled=True)]
    all_to_all x16 -> x5, starting transfers between devices: 73.7 us -> 18.9 us  [the longest x3 11.6 us: whole_sequence(): lax.all_to_all(part, 'seq', split_axis=0, concat_axis=1, tiled=True)[0]]
  transfers between devices with their start and end apart: 32 -> 31, of which waited for: 15 -> 19; matrix products, arithmetic and copies ran while one was open for 49% -> 17% of each run, Pallas kernels for 0% -> 7%
where the time goes in v1:
time: 1200 us; the launch traced here: 1190 us
  waiting for transfers between devices  717 us (60%)
  matrix products  216 us (18%)
  Pallas kernels  125 us (10%)
  other arithmetic  38.1 us (3%)
  starting transfers between devices  32 us (3%)
  local copies, waits for them, and re-layouts  27 us (2%)
  blocking collectives  22.4 us (2%)
  between operations  15.4 us (1%)
    reduce_scatter x8, waiting for transfers between devices, scatter(): lax.psum_scatter(term.astype(half), 'wide', scatter_dimension=0, tiled=True)  446 us
    dot_general x24, matrix products, contract(): lax.dot_general(left, right, (((left_dim,), (right_dim,)), ((), ())), pre...  216 us
    all_gather x7, waiting for transfers between devices, per_device(): lax.all_gather(source[layer], 'wide', axis=0, tiled=True)  195 us
    pallas_call x2, Pallas kernels, attend_backward(): pl.pallas_call(functools.partial(attend_grad_kernel, rows=BACKWARD_ROWS),...  74.6 us
    pallas_call x2, Pallas kernels, attend_forward(): pl.pallas_call(functools.partial(attend_kernel, rows=FORWARD_ROWS), grid=...  50.6 us
    all_to_all x3, waiting for transfers between devices, whole_sequence(): lax.all_to_all(part, 'seq', split_axis=0, concat_axis=1, tiled=True)[0]  34.9 us
  transfers between devices with their start and end apart: 31, of which 19 were waited for; matrix products, arithmetic and copies ran while one was open for 17% of the time, Pallas kernels for 7%

profile of v1, /device:TPU:0, one launch (start us, length us, event | category | flops | bytes accessed | tf_op | source)
XLA Modules:
  0.0 1193.5 jit_solution(12314121060530069320)
XLA Ops:
  16.4 4.2 all-to-all-start.1
  21.7 22.4 %all-gather.9 = bf16[16,1,1152]{2,1,0:T(2,128)(2,1)S(1)} all-gather(bf16[1,1,1152]{2,1,0:T(2,128)(2,1)S(1)} %reshape.354), channel_id=2, replica_groups=mesh['wide'=16,'seq'=2] {'wide'}, dimensions={0}, use_global_device_ids=true | all-gather | bytes 39168 | tf_op jit(solution)/shard_map/all_gather | solution.py:245
  45.0 3.7 all-to-all-start
  52.3 16.6 %all-to-all-done = bf16[2,512,768]{2,1,0:T(8,128)(2,1)S(1)} async-done(((bf16[2,512,768]{2,1,0:T(8,128)(2,1)}), bf16[2,512,768]{2,1,0:T(8,128)(2,1)S(1)}, u32[]{:S(2)}, u32[]{:S(2)}) %all-to-all-start) | async-done | bytes 1572896 | tf_op jit(solution)/shard_map/all_to_all | solution.py:232
  73.8 18.3 %all-to-all-done.3 = bf16[2,512,768]{2,1,0:T(8,128)(2,1)S(1)} async-done(((bf16[2,512,768]{2,1,0:T(8,128)(2,1)}), bf16[2,512,768]{2,1,0:T(8,128)(2,1)S(1)}, u32[]{:S(2)}, u32[]{:S(2)}) %all-to-all-start.3) | async-done | bytes 1572896 | tf_op jit(solution)/shard_map/all_to_all | solution.py:232
  95.1 8.4 add_convert_fusion.1.query_ref.key_ref.value_ref
  103.5 25.4 %attend_forward.2 = (bf16[1024,768]{1,0:T(8,128)(2,1)}, f32[6,2,1024]{2,1,0:T(2,128)}) custom-call(bf16[1024,2304]{1,0:T(8,128)(2,1)} %add_convert_fusion.1.query_ref.key_ref.value_ref, bf16[1024,2304]{1,0:T(8,128)(2,1)} %add_convert_fusion.1.query_ref.key_ref.value_ref, bf16[1024,2304]{1,0:T(8,128)(2,1)} %add_convert_fusion.1.query_ref.key_ref.value_ref, ...), custom_call_target="tpu_custom_call" | custom-call | flops 12884901888 | bytes 6291456 | tf_op jit(solution)/shard_map/attend_forward/pallas_call | solution.py:62
  129.0 3.9 fusion.67
  135.1 21.0 %all-gather.23.cloned.1.call-done = bf16[1,768,3072]{2,1,0:T(8,128)(2,1)} async-done(((bf16[1,48,3072]{2,1,0:T(8,128)(2,1)}), bf16[1,768,3072]{2,1,0:T(8,128)(2,1)}) %all-gather.23.cloned.1.call-update) | async-done | bytes 4718608 | tf_op jit(solution)/shard_map/all_gather | solution.py:249
  156.0 11.0 fusion.28
  167.1 43.5 %all-gather.25.cloned.1.call-done = bf16[1,3072,768]{2,1,0:T(8,128)(2,1)} async-done(((bf16[1,192,768]{2,1,0:T(8,128)(2,1)}), bf16[1,3072,768]{2,1,0:T(8,128)(2,1)}) %all-gather.25.cloned.1.call-update) | async-done | bytes 4718608 | tf_op jit(solution)/shard_map/all_gather | solution.py:249
  210.6 13.1 %fusion.68 = (f32[1024]{0:T(1024)S(1)}, f32[1024,768]{1,0:T(8,128)S(1)}) fusion(f32[1024,768]{1,0:T(8,128)} %copy-done.6, f32[768]{0:T(1024)S(1)} %get-tuple-element.66, bf16[1,3072,768]{2,1,0:T(8,128)(2,1)} %all-gather.25.cloned.1.call-done, f32[1024,3072]{1,0:T(8,128)} %fusion.28, f32[3072]{0:T(1024)S(1)} %add.281), kind=kOutput, calls=%fused_computation.181 | convolution fusion | flops 4865653760 | bytes 23612416 | tf_op jit(solution)/shard_map/dot_general | solution.py:22
  225.9 32.6 %all-gather.27.cloned.1.call-done = bf16[1,768,2304]{2,1,0:T(8,128)(2,1)} async-done(((bf16[1,48,2304]{2,1,0:T(8,128)(2,1)}), bf16[1,768,2304]{2,1,0:T(8,128)(2,1)}) %all-gather.27.cloned.1.call-update) | async-done | bytes 3538960 | tf_op jit(solution)/shard_map/all_gather | solution.py:249
  258.5 9.3 add_convert_fusion.query_ref.key_ref.value_ref
  267.7 25.2 %attend_forward.3 = (bf16[1024,768]{1,0:T(8,128)(2,1)}, f32[6,2,1024]{2,1,0:T(2,128)}) custom-call(bf16[1024,2304]{1,0:T(8,128)(2,1)} %add_convert_fusion.query_ref.key_ref.value_ref, bf16[1024,2304]{1,0:T(8,128)(2,1)} %add_convert_fusion.query_ref.key_ref.value_ref, bf16[1024,2304]{1,0:T(8,128)(2,1)} %add_convert_fusion.query_ref.key_ref.value_ref, ...), custom_call_target="tpu_custom_call" | custom-call | flops 12884901888 | bytes 6291456 | tf_op jit(solution)/shard_map/attend_forward/pallas_call | solution.py:62
  292.9 5.1 all-gather.29.cloned.1.call-done
  298.1 4.2 fusion.69
  304.6 48.6 %all-gather.31.cloned.1.call-done = bf16[1,768,3072]{2,1,0:T(8,128)(2,1)} async-done(((bf16[1,48,3072]{2,1,0:T(8,128)(2,1)}), bf16[1,768,3072]{2,1,0:T(8,128)(2,1)}) %all-gather.31.cloned.1.call-update) | async-done | bytes 4718608 | tf_op jit(solution)/shard_map/all_gather | solution.py:249
  353.1 11.0 fusion.20
  364.1 43.8 %all-gather.33.cloned.1.call-done = bf16[1,3072,768]{2,1,0:T(8,128)(2,1)} async-done(((bf16[1,192,768]{2,1,0:T(8,128)(2,1)}), bf16[1,3072,768]{2,1,0:T(8,128)(2,1)}) %all-gather.33.cloned.1.call-update) | async-done | bytes 4718608 | tf_op jit(solution)/shard_map/all_gather | solution.py:249
  408.0 16.0 %convert_reduce_fusion = (f32[3072]{0:T(1024)}, bf16[1024,3072]{1,0:T(8,128)(2,1)S(1)}) fusion(f32[1024,3072]{1,0:T(8,128)} %fusion.20, f32[3072]{0:T(1024)S(1)} %add.304, bf16[1024,768]{1,0:T(8,128)(2,1)S(1)} %bitcast.148, bf16[1,3072,768]{2,1,0:T(8,128)(2,1)} %all-gather.33.cloned.1.call-done), kind=kOutput, calls=%fused_computation.18 | convolution fusion | flops 4904186880 | bytes 25190400 | tf_op jit(solution)/shard_map/dot_general | solution.py:22
  424.0 5.7 multiply_reduce_fusion
  435.4 4.5 convolution_convert_fusion.7.upstream_ref
  439.9 37.3 %attend_backward.2 = bf16[1024,2304]{1,0:T(8,128)(2,1)} custom-call(bf16[1024,2304]{1,0:T(8,128)(2,1)} %add_convert_fusion.query_ref.key_ref.value_ref, bf16[1024,2304]{1,0:T(8,128)(2,1)} %add_convert_fusion.query_ref.key_ref.value_ref, bf16[1024,2304]{1,0:T(8,128)(2,1)} %add_convert_fusion.query_ref.key_ref.value_ref, f32[1024,1024]{1,0:T(8,128)} %fusion.32.bias_ref, ...), custom_call_target="tpu_custom_call" | custom-call | flops 32212254720 | bytes 12582912 | tf_op jit(solution)/shard_map/attend_backward/pallas_call | solution.py:149
  477.2 6.7 multiply_reduce_fusion.1
  485.3 17.0 %convert_reduce_fusion.1 = (f32[3072]{0:T(1024)S(1)}, bf16[1024,3072]{1,0:T(8,128)(2,1)}) fusion(f32[1024,3072]{1,0:T(8,128)} %fusion.28, f32[3072]{0:T(1024)S(1)} %add.281, bf16[1,3072,768]{2,1,0:T(8,128)(2,1)} %all-gather.25.cloned.1.call-done, f32[1024,768]{1,0:T(8,128)S(1)} %get-tuple-element.79), kind=kOutput, calls=%fused_computation.19 | convolution fusion | flops 4904973312 | bytes 26763264 | tf_op jit(solution)/shard_map/dot_general | solution.py:22
  502.4 9.4 multiply_reduce_fusion.2
  518.1 37.3 %attend_backward.3 = bf16[1024,2304]{1,0:T(8,128)(2,1)} custom-call(bf16[1024,2304]{1,0:T(8,128)(2,1)} %add_convert_fusion.1.query_ref.key_ref.value_ref, bf16[1024,2304]{1,0:T(8,128)(2,1)} %add_convert_fusion.1.query_ref.key_ref.value_ref, bf16[1024,2304]{1,0:T(8,128)(2,1)} %add_convert_fusion.1.query_ref.key_ref.value_ref, f32[1024,1024]{1,0:T(8,128)} %fusion.32.bias_ref, ...), custom_call_target="tpu_custom_call" | custom-call | flops 32212254720 | bytes 12582912 | tf_op jit(solution)/shard_map/attend_backward/pallas_call | solution.py:149
  555.5 8.5 multiply_reduce_fusion.3
  573.0 4.8 convolution_convert_fusion.9
  577.9 9.4 convolution_convert_fusion.4
  588.7 7.9 convolution_convert_fusion.5
  597.3 10.5 convolution_convert_fusion.2
  608.4 10.4 convolution_convert_fusion.3
  620.3 12.3 %convolution_convert_fusion = bf16[3072,768]{1,0:T(8,128)(2,1)} fusion(bf16[1024,768]{1,0:T(8,128)(2,1)S(1)} %bitcast.149, f32[1024,3072]{1,0:T(8,128)} %fusion.20, f32[3072]{0:T(1024)S(1)} %copy-done.43), kind=kOutput, calls=%fused_computation.26 | convolution fusion | flops 4865654784 | bytes 18886656 | tf_op jit(solution)/shard_map/dot_general | solution.py:22
  632.6 13.3 %convolution_convert_fusion.1 = bf16[3072,768]{1,0:T(8,128)(2,1)} fusion(f32[1024,768]{1,0:T(8,128)} %copy-done.13, f32[1024,3072]{1,0:T(8,128)} %fusion.28, f32[3072]{0:T(1024)S(1)} %add.281), kind=kOutput, calls=%fused_computation.27 | convolution fusion | flops 4866441216 | bytes 20459520 | tf_op jit(solution)/shard_map/dot_general | solution.py:22
  646.6 13.4 %add_convert_fusion.3 = bf16[1024,768]{1,0:T(8,128)(2,1)} fusion(f32[1024,768]{1,0:T(8,128)} %copy-done.8, bf16[1,3072,768]{2,1,0:T(8,128)(2,1)} %all-gather.33.cloned.1.call-done, f32[768]{0:T(1024)S(1)} %copy-done.47, f32[1024,3072]{1,0:T(8,128)} %fusion.20, f32[3072]{0:T(1024)S(1)} %copy-done.43), kind=kOutput, calls=%fused_computation.75 | convolution fusion | flops 4865654784 | bytes 22035456 | tf_op jit(solution)/shard_map/dot_general | solution.py:22
  663.7 4.4 add_convert_fusion.2
  668.2 15.4 %all-to-all-done.2 = bf16[2,512,768]{2,1,0:T(8,128)(2,1)S(1)} async-done(((bf16[2,512,768]{2,1,0:T(8,128)(2,1)}), bf16[2,512,768]{2,1,0:T(8,128)(2,1)S(1)}, u32[]{:S(2)}, u32[]{:S(2)}) %all-to-all-start.2) | async-done | bytes 1572896 | tf_op jit(solution)/shard_map/all_to_all | solution.py:279
  691.5 16.6 %collective-permute-done.8 = f32[1152]{0:T(1024)S(1)} collective-permute-done((f32[1152]{0:T(1024)S(1)}, f32[1152]{0:T(1024)S(1)}, u32[]{:S(2)}, u32[]{:S(2)}) %collective-permute-start.8) | collective-permute-done | bytes 4640 | tf_op jit(solution)/shard_map/ppermute | solution.py:345
  714.0 6.4 reduce-scatter.13.cloned.1.call-done
  721.9 69.8 %reduce-scatter.11.cloned.1.call-done = bf16[48,2304]{1,0:T(8,128)(2,1)} async-done(((bf16[768,2304]{1,0:T(8,128)(2,1)}), bf16[48,2304]{1,0:T(8,128)(2,1)}) %reduce-scatter.11.cloned.1.call-update) | async-done | bytes 221200 | tf_op jit(solution)/shard_map/reduce_scatter | solution.py:284
  794.8 68.3 %reduce-scatter.9.cloned.1.call-done = bf16[48,2304]{1,0:T(8,128)(2,1)} async-done(((bf16[768,2304]{1,0:T(8,128)(2,1)}), bf16[48,2304]{1,0:T(8,128)(2,1)}) %reduce-scatter.9.cloned.1.call-update) | async-done | bytes 221200 | tf_op jit(solution)/shard_map/reduce_scatter | solution.py:284
  865.6 3.7 collective-permute-done
  870.3 71.6 %reduce-scatter.19.cloned.1.call-done = bf16[48,3072]{1,0:T(8,128)(2,1)} async-done(((bf16[768,3072]{1,0:T(8,128)(2,1)}), bf16[48,3072]{1,0:T(8,128)(2,1)}) %reduce-scatter.19.cloned.1.call-update) | async-done | bytes 294928 | tf_op jit(solution)/shard_map/reduce_scatter | solution.py:284
  944.3 75.9 %reduce-scatter.17.cloned.1.call-done = bf16[48,3072]{1,0:T(8,128)(2,1)} async-done(((bf16[768,3072]{1,0:T(8,128)(2,1)}), bf16[48,3072]{1,0:T(8,128)(2,1)}) %reduce-scatter.17.cloned.1.call-update) | async-done | bytes 294928 | tf_op jit(solution)/shard_map/reduce_scatter | solution.py:284
  1021.7 77.4 %reduce-scatter.23.cloned.1.call-done = bf16[192,768]{1,0:T(8,128)(2,1)} async-done(((bf16[3072,768]{1,0:T(8,128)(2,1)}), bf16[192,768]{1,0:T(8,128)(2,1)}) %reduce-scatter.23.cloned.1.call-update) | async-done | bytes 294928 | tf_op jit(solution)/shard_map/reduce_scatter | solution.py:284
  1100.5 76.9 %reduce-scatter.21.cloned.1.call-done = bf16[192,768]{1,0:T(8,128)(2,1)} async-done(((bf16[3072,768]{1,0:T(8,128)(2,1)}), bf16[192,768]{1,0:T(8,128)(2,1)}) %reduce-scatter.21.cloned.1.call-update) | async-done | bytes 294928 | tf_op jit(solution)/shard_map/reduce_scatter | solution.py:284
  (313 shorter events, 95.9 us)
Async XLA Ops:
  7.2 37.8 %copy-start = (f32[2,768]{1,0:T(2,128)S(1)}, f32[2,768]{1,0:T(2,128)}, u32[]{:S(2)}) copy-start(f32[2,768]{1,0:T(2,128)} %param.13) | copy-start | bytes 18436
  7.3 87.8 %all-gather.19.cloned.1.call-start = ((), (), s32[]{:S(2)}) async-start(), calls=%async_computation.21 | async-start | bytes 3760128 | tf_op jit(solution)/shard_map/all_gather | solution.py:244
  9.2 119.8 %all-gather.21.cloned.1.call-start = ((), (), s32[]{:S(2)}) async-start(), calls=%async_computation.22 | async-start | bytes 1253376 | tf_op jit(solution)/shard_map/all_gather | solution.py:249
  10.9 145.2 %all-gather.23.cloned.1.call-start = ((), (), s32[]{:S(2)}) async-start(), calls=%async_computation.23 | async-start | bytes 5013504 | tf_op jit(solution)/shard_map/all_gather | solution.py:249
  12.9 197.7 %all-gather.25.cloned.1.call-start = ((), (), s32[]{:S(2)}) async-start(), calls=%async_computation.24 | async-start | bytes 5013504 | tf_op jit(solution)/shard_map/all_gather | solution.py:249
  13.8 244.7 %all-gather.27.cloned.1.call-start = ((), (), s32[]{:S(2)}) async-start(), calls=%async_computation.25 | async-start | bytes 3760128 | tf_op jit(solution)/shard_map/all_gather | solution.py:249
  14.4 283.7 %all-gather.29.cloned.1.call-start = ((), (), s32[]{:S(2)}) async-start(), calls=%async_computation.26 | async-start | bytes 1253376 | tf_op jit(solution)/shard_map/all_gather | solution.py:249
  15.0 338.2 %all-gather.31.cloned.1.call-start = ((), (), s32[]{:S(2)}) async-start(), calls=%async_computation.27 | async-start | bytes 5013504 | tf_op jit(solution)/shard_map/all_gather | solution.py:249
  16.4 28.7 %all-to-all-start.1 = ((s32[2,512,2]{1,2,0:T(2,128)}), s32[2,512,2]{1,2,0:T(2,128)S(1)}, u32[]{:S(2)}, u32[]{:S(2)}) async-start(s32[2,512,2]{1,2,0:T(2,128)} %pad_add_fusion), calls=%async_computation.1 | async-start | bytes 16384 | tf_op jit(solution)/shard_map/all_to_all | solution.py:232
  20.6 387.4 %all-gather.33.cloned.1.call-start = ((), (), s32[]{:S(2)}) async-start(), calls=%async_computation.28 | async-start | bytes 5013504 | tf_op jit(solution)/shard_map/all_gather | solution.py:249
  45.0 363.0 %copy-start.42 = (f32[3072]{0:T(1024)}, f32[3072]{0:T(1024)S(1)}, u32[]{:S(2)}) copy-start(f32[3072]{0:T(1024)S(1)} %add.304) | copy-start | bytes 36868
  45.0 84.0 %copy-start.20 = (f32[768]{0:T(1024)}, f32[768]{0:T(1024)S(1)}, u32[]{:S(2)}) copy-start(f32[768]{0:T(1024)S(1)} %dynamic-slice_reduce_fusion.1) | copy-start | bytes 9220
  45.0 23.9 %all-to-all-start = ((bf16[2,512,768]{2,1,0:T(8,128)(2,1)}), bf16[2,512,768]{2,1,0:T(8,128)(2,1)S(1)}, u32[]{:S(2)}, u32[]{:S(2)}) async-start(bf16[2,512,768]{2,1,0:T(8,128)(2,1)} %param.12), calls=%async_computation | async-start | bytes 3145728 | tf_op jit(solution)/shard_map/all_to_all | solution.py:232
  49.4 106.7 %copy-start.48 = (f32[768]{0:T(1024)}, f32[768]{0:T(1024)S(1)}, u32[]{:S(2)}) copy-start(f32[768]{0:T(1024)S(1)} %get-tuple-element.67) | copy-start | bytes 9220
  49.4 209.1 %copy-start.52 = (f32[768]{0:T(1024)}, f32[768]{0:T(1024)S(1)}, u32[]{:S(2)}) copy-start(f32[768]{0:T(1024)S(1)} %get-tuple-element.65) | copy-start | bytes 9220
  49.4 303.8 %copy-start.50 = (f32[768]{0:T(1024)}, f32[768]{0:T(1024)S(1)}, u32[]{:S(2)}) copy-start(f32[768]{0:T(1024)S(1)} %get-tuple-element.60) | copy-start | bytes 9220
  49.4 43.8 %copy-start.23 = (f32[768]{0:T(1024)}, f32[768]{0:T(1024)S(1)}, u32[]{:S(2)}) copy-start(f32[768]{0:T(1024)S(1)} %get-tuple-element.77) | copy-start | bytes 9220
  49.4 106.6 %copy-start.34 = (f32[768]{0:T(1024)}, f32[768]{0:T(1024)S(1)}, u32[]{:S(2)}) copy-start(f32[768]{0:T(1024)S(1)} %get-tuple-element.76) | copy-start | bytes 9220
  49.4 380.3 %copy-start.36 = (f32[768]{0:T(1024)}, f32[768]{0:T(1024)S(1)}, u32[]{:S(2)}) copy-start(f32[768]{0:T(1024)S(1)} %get-tuple-element.74) | copy-start | bytes 9220
  68.9 60.0 %copy-start.2 = (bf16[2,512,768]{2,1,0:T(8,128)(2,1)}, bf16[2,512,768]{2,1,0:T(8,128)(2,1)S(1)}, u32[]{:S(2)}) copy-start(bf16[2,512,768]{2,1,0:T(8,128)(2,1)S(1)} %all-to-all-done) | copy-start | bytes 4718596
  68.9 23.2 %all-to-all-start.3 = ((bf16[2,512,768]{2,1,0:T(8,128)(2,1)}), bf16[2,512,768]{2,1,0:T(8,128)(2,1)S(1)}, u32[]{:S(2)}, u32[]{:S(2)}) async-start(bf16[2,512,768]{2,1,0:T(8,128)(2,1)} %param.16), calls=%async_computation.3 | async-start | bytes 3145728 | tf_op jit(solution)/shard_map/all_to_all | solution.py:232
  72.6 614.7 %reduce-scatter.15.cloned.1.call-start = ((), (), s32[]{:S(2)}) async-start(), calls=%async_computation.16 | async-start | bytes 1253376 | tf_op jit(solution)/shard_map/reduce_scatter | solution.py:284
  92.1 337.6 %copy-start.4 = (bf16[2,512,768]{2,1,0:T(8,128)(2,1)}, bf16[2,512,768]{2,1,0:T(8,128)(2,1)S(1)}, u32[]{:S(2)}) copy-start(bf16[2,512,768]{2,1,0:T(8,128)(2,1)S(1)} %all-to-all-done.3) | copy-start | bytes 4718596
  302.3 127.4 %copy-start.31 = (f32[1024]{0:T(1024)}, f32[1024]{0:T(1024)S(1)}, u32[]{:S(2)}) copy-start(f32[1024]{0:T(1024)S(1)} %broadcast_multiply_fusion.8) | copy-start | bytes 12292
  304.5 125.2 %copy-start.40 = (f32[1024]{0:T(1024)}, f32[1024]{0:T(1024)S(1)}, u32[]{:S(2)}) copy-start(f32[1024]{0:T(1024)S(1)} %add_rsqrt_fusion) | copy-start | bytes 12292
  511.8 178.1 %all-reduce.3.cloned.1.call-start = ((), (), s32[]{:S(2)}) async-start(), calls=%async_computation.29 | async-start | bytes 147456
  518.1 37.4 %copy-start.26 = (f32[1,4,2,128]{3,1,2,0:T(4,128)S(1)}, f32[1,4,2,128]{3,1,2,0:T(4,128)}, u32[]{:S(2)}) copy-start(f32[1,4,2,128]{3,1,2,0:T(4,128)} %copy-done.25) | copy-start | bytes 12292
  518.1 37.4 %copy-start.28 = (f32[1,4,2,128]{3,1,2,0:T(4,128)S(1)}, f32[1,4,2,128]{3,1,2,0:T(4,128)}, u32[]{:S(2)}) copy-start(f32[1,4,2,128]{3,1,2,0:T(4,128)} %copy-done.27) | copy-start | bytes 12292
  518.1 37.4 %copy-start.57 = (bf16[1,768,2304]{2,1,0:T(8,128)(2,1)S(1)}, bf16[1,768,2304]{2,1,0:T(8,128)(2,1)}, u32[]{:S(2)}) copy-start(bf16[1,768,2304]{2,1,0:T(8,128)(2,1)} %all-gather.19.cloned.1.call-done) | copy-start | bytes 10616836
  572.9 147.5 %reduce-scatter.13.cloned.1.call-start = ((), (), s32[]{:S(2)}) async-start(), calls=%async_computation.15 | async-start | bytes 1253376 | tf_op jit(solution)/shard_map/reduce_scatter | solution.py:284
  577.8 213.9 %reduce-scatter.11.cloned.1.call-start = ((), (), s32[]{:S(2)}) async-start(), calls=%async_computation.14 | async-start | bytes 3760128 | tf_op jit(solution)/shard_map/reduce_scatter | solution.py:284
  587.3 275.8 %reduce-scatter.9.cloned.1.call-start = ((), (), s32[]{:S(2)}) async-start(), calls=%async_computation.13 | async-start | bytes 3760128 | tf_op jit(solution)/shard_map/reduce_scatter | solution.py:284
  596.6 345.2 %reduce-scatter.19.cloned.1.call-start = ((), (), s32[]{:S(2)}) async-start(), calls=%async_computation.18 | async-start | bytes 5013504 | tf_op jit(solution)/shard_map/reduce_scatter | solution.py:284
  607.8 412.4 %reduce-scatter.17.cloned.1.call-start = ((), (), s32[]{:S(2)}) async-start(), calls=%async_computation.17 | async-start | bytes 5013504 | tf_op jit(solution)/shard_map/reduce_scatter | solution.py:284
  618.9 480.2 %reduce-scatter.23.cloned.1.call-start = ((), (), s32[]{:S(2)}) async-start(), calls=%async_computation.20 | async-start | bytes 5013504 | tf_op jit(solution)/shard_map/reduce_scatter | solution.py:284
  632.6 544.8 %reduce-scatter.21.cloned.1.call-start = ((), (), s32[]{:S(2)}) async-start(), calls=%async_computation.19 | async-start | bytes 5013504 | tf_op jit(solution)/shard_map/reduce_scatter | solution.py:284
  660.0 23.6 %all-to-all-start.2 = ((bf16[2,512,768]{2,1,0:T(8,128)(2,1)}), bf16[2,512,768]{2,1,0:T(8,128)(2,1)S(1)}, u32[]{:S(2)}, u32[]{:S(2)}) async-start(bf16[2,512,768]{2,1,0:T(8,128)(2,1)} %bitcast.151), calls=%async_computation.2 | async-start | bytes 3145728 | tf_op jit(solution)/shard_map/all_to_all | solution.py:279
  683.6 28.5 %all-to-all-start.4 = ((bf16[2,512,768]{2,1,0:T(8,128)(2,1)}), bf16[2,512,768]{2,1,0:T(8,128)(2,1)S(1)}, u32[]{:S(2)}, u32[]{:S(2)}) async-start(bf16[2,512,768]{2,1,0:T(8,128)(2,1)} %bitcast.150), calls=%async_computation.4 | async-start | bytes 3145728 | tf_op jit(solution)/shard_map/all_to_all | solution.py:279
  687.3 34.6 %collective-permute-start.3 = (bf16[48,768]{1,0:T(8,128)(2,1)}, bf16[48,768]{1,0:T(8,128)(2,1)S(1)}, u32[]{:S(2)}, u32[]{:S(2)}) collective-permute-start(bf16[48,768]{1,0:T(8,128)(2,1)} %reduce-scatter.15.cloned.1.call-done), channel_id=1, source_target_pairs={{0,1},{1,0},{2,3},{3,2},{4,5},{5,4},{6,7},{7,6},{8,9},{9,8},{10,11... | collective-permute-start | bytes 221192 | tf_op jit(solution)/shard_map/ppermute | solution.py:285
  691.3 16.8 %collective-permute-start.8 = (f32[1152]{0:T(1024)S(1)}, f32[1152]{0:T(1024)S(1)}, u32[]{:S(2)}, u32[]{:S(2)}) collective-permute-start(f32[1152]{0:T(1024)S(1)} %dynamic-slice_reduce_fusion), channel_id=1, source_target_pairs={{0,1},{1,0},{2,3},{3,2},{4,5},{5,4},{6,7},{7,6},{8,9},{9,8},{10,11... | collective-permute-start | bytes 13832 | tf_op jit(solution)/shard_map/ppermute | solution.py:345
  720.4 72.8 %collective-permute-start.2 = (bf16[48,768]{1,0:T(8,128)(2,1)}, bf16[48,768]{1,0:T(8,128)(2,1)S(1)}, u32[]{:S(2)}, u32[]{:S(2)}) collective-permute-start(bf16[48,768]{1,0:T(8,128)(2,1)} %reduce-scatter.13.cloned.1.call-done), channel_id=1, source_target_pairs={{0,1},{1,0},{2,3},{3,2},{4,5},{5,4},{6,7},{7,6},{8,9},{9,8},{10,11... | collective-permute-start | bytes 221192 | tf_op jit(solution)/shard_map/ppermute | solution.py:285
  791.7 72.9 %collective-permute-start.1 = (bf16[48,2304]{1,0:T(8,128)(2,1)}, bf16[48,2304]{1,0:T(8,128)(2,1)S(1)}, u32[]{:S(2)}, u32[]{:S(2)}) collective-permute-start(bf16[48,2304]{1,0:T(8,128)(2,1)} %reduce-scatter.11.cloned.1.call-done), channel_id=1, source_target_pairs={{0,1},{1,0},{2,3},{3,2},{4,5},{5,4},{6,7},{7,6},{8,9},{9,8},{10,11... | collective-permute-start | bytes 663560 | tf_op jit(solution)/shard_map/ppermute | solution.py:285
  863.1 6.1 collective-permute-start
  941.9 237.0 %collective-permute-start.5 = (bf16[48,3072]{1,0:T(8,128)(2,1)}, bf16[48,3072]{1,0:T(8,128)(2,1)S(1)}, u32[]{:S(2)}, u32[]{:S(2)}) collective-permute-start(bf16[48,3072]{1,0:T(8,128)(2,1)} %reduce-scatter.19.cloned.1.call-done), channel_id=1, source_target_pairs={{0,1},{1,0},{2,3},{3,2},{4,5},{5,4},{6,7},{7,6},{8,9},{9,8},{10,11... | collective-permute-start | bytes 884744 | tf_op jit(solution)/shard_map/ppermute | solution.py:285
  1020.2 159.7 %collective-permute-start.4 = (bf16[48,3072]{1,0:T(8,128)(2,1)}, bf16[48,3072]{1,0:T(8,128)(2,1)S(1)}, u32[]{:S(2)}, u32[]{:S(2)}) collective-permute-start(bf16[48,3072]{1,0:T(8,128)(2,1)} %reduce-scatter.17.cloned.1.call-done), channel_id=1, source_target_pairs={{0,1},{1,0},{2,3},{3,2},{4,5},{5,4},{6,7},{7,6},{8,9},{9,8},{10,11... | collective-permute-start | bytes 884744 | tf_op jit(solution)/shard_map/ppermute | solution.py:285
  1099.1 83.0 %copy-start.18 = (bf16[192,768]{1,0:T(8,128)(2,1)S(1)}, bf16[192,768]{1,0:T(8,128)(2,1)}, u32[]{:S(2)}) copy-start(bf16[192,768]{1,0:T(8,128)(2,1)} %reduce-scatter.23.cloned.1.call-done) | copy-start | bytes 884740
  1099.1 83.0 %collective-permute-start.7 = (bf16[192,768]{1,0:T(8,128)(2,1)}, bf16[192,768]{1,0:T(8,128)(2,1)S(1)}, u32[]{:S(2)}, u32[]{:S(2)}) collective-permute-start(bf16[192,768]{1,0:T(8,128)(2,1)} %reduce-scatter.23.cloned.1.call-done), channel_id=1, source_target_pairs={{0,1},{1,0},{2,3},{3,2},{4,5},{5,4},{6,7},{7,6},{8,9},{9,8},{10,11... | collective-permute-start | bytes 884744 | tf_op jit(solution)/shard_map/ppermute | solution.py:285
  1177.4 7.9 collective-permute-start.6
  (50 other events, 628.7 us)
Sparse Core Ops, SparseCore 0:
  10.9 49.6 all-gather.18
  63.5 37.2 all-gather.20
  103.7 52.2 all-gather.22
  158.8 51.7 all-gather.24
  212.7 45.7 all-gather.26
  260.6 37.4 all-gather.28
  300.9 52.1 all-gather.30
  356.0 51.9 all-gather.32
  511.9 56.6 reduce-scatter.14
  573.0 83.7 all-reduce.2
  661.5 58.8 reduce-scatter.12
  724.6 67.0 reduce-scatter.10
  796.1 66.9 reduce-scatter.8
  867.3 74.5 reduce-scatter.18
  945.6 74.5 reduce-scatter.16
  1024.4 74.6 reduce-scatter.22
  1102.8 74.5 reduce-scatter.20

commit v2 on v1

--- a/solution.py
+++ b/solution.py
@@ -241,8 +241,14 @@
         [norm_gains.reshape(-1), bias_rows.reshape(-1), up_bias.reshape(-1)]
     )
     matrices = [[None] * 4 for _ in range(layers)]
-    matrices[0][0] = lax.all_gather(qkv_weight[0], "wide", axis=0, tiled=True)
-    small_whole = lax.all_gather(small, "wide", axis=0, tiled=False)
+    side = small.reshape(qkv_weight.shape[1], -1)
+    side_width = side.shape[1]
+    side = jnp.pad(side, ((0, 0), (0, -side_width % PAIR)))
+    first_whole = lax.all_gather(
+        jnp.concatenate([qkv_weight[0], side], axis=1), "wide", axis=0, tiled=True
+    )
+    matrices[0][0] = first_whole[:, : qkv_weight.shape[2]]
+    small_whole = first_whole[:, qkv_weight.shape[2] :][:, :side_width].reshape(groups, -1)
     for layer in range(layers):
         for index, source in enumerate(sources):
             if matrices[layer][index] is None:
@@ -278,15 +284,91 @@
         parts = result.reshape(2, -1, features).astype(half)
         return lax.all_to_all(parts, "seq", split_axis=0, concat_axis=0, tiled=True)
 
-    output = split_back(hidden).astype(single)
-
-    def scatter(term):
-        share = lax.psum_scatter(term.astype(half), "wide", scatter_dimension=0, tiled=True)
-        other = lax.ppermute(share, "seq", swap)
-        return share.astype(single) + other.astype(single)
+    output = split_back(hidden)
+
+    core = lax.axis_index("wide") & 1
+    row_unit = qkv_weight.shape[1]
+    pair_up = lambda bit: [(index, index ^ bit) for index in range(groups)]
+
+    def column_half(array, which):
+        count = array.shape[1] // 2
+        return lax.dynamic_slice_in_dim(array, which * count, count, axis=1)
+
+    def core_terms(left, right):
+        return contract(left, column_half(right, 1 - core), 0, 0).astype(half)
+
+    def merge_cores(left, right, received):
+        kept = contract(left, column_half(right, core), 0, 0) + received.astype(single)
+        kept = kept.astype(half)
+        pieces = kept.shape[0] // (groups * row_unit)
+        kept = kept.reshape(groups // 2, 2, pieces, row_unit, kept.shape[1])
+        return [kept[:, :, piece] for piece in range(pieces)]
+
+    def side_of(array, which, axis):
+        return lax.dynamic_index_in_dim(array, which, axis, keepdims=False)
+
+    def reduce_group(terms):
+        place = lax.axis_index("seq")
+        pieces, counts = [], []
+        arrived = yield [lax.ppermute(core_terms(*term), "wide", pair_up(1)) for term in terms]
+        for (left, right), received in zip(terms, arrived):
+            merged = merge_cores(left, right, received)
+            counts.append((len(merged), merged[0].shape[-1]))
+            pieces += merged
+        sent = jnp.concatenate([side_of(piece, 1 - place, 1) for piece in pieces], axis=-1)
+        kept = jnp.concatenate([side_of(piece, place, 1) for piece in pieces], axis=-1)
+        (received,) = yield [lax.ppermute(sent, "seq", swap)]
+        current = (kept.astype(single) + received.astype(single)).astype(half)
+        bit = 2
+        while bit < groups:
+            current = current.reshape(-1, 2, row_unit, current.shape[-1])
+            mine = (lax.axis_index("wide") >> (bit.bit_length() - 1)) & 1
+            sent = side_of(current, 1 - mine, 1)
+            (received,) = yield [lax.ppermute(sent, "wide", pair_up(bit))]
+            kept = side_of(current, mine, 1)
+            current = (kept.astype(single) + received.astype(single)).astype(half)
+            bit *= 2
+        current = current.reshape(row_unit, -1)
+        (other,) = yield [lax.ppermute(current, "seq", swap)]
+        same = place == core
+        owned = jnp.where(same, current, other)
+        passed = jnp.where(same, other, current)
+        (received,) = yield [lax.ppermute(passed, "wide", pair_up(1))]
+        low = jnp.where(core == 0, owned, received)
+        high = jnp.where(core == 0, received, owned)
+        shares, start = [], 0
+        for count, width in counts:
+            rows = []
+            for _ in range(count):
+                window = slice(start, start + width)
+                rows.append(jnp.concatenate([low[:, window], high[:, window]], axis=1))
+                start += width
+            shares.append(jnp.concatenate(rows, axis=0).astype(single))
+        return shares
+
+    weight_grads = [[None] * 4 for _ in range(layers)]
+    running = []
+
+    def begin(layer, parts, terms):
+        steps = reduce_group(terms)
+        running.append([layer, parts, steps, next(steps)])
+
+    def advance(main):
+        if not running:
+            return main
+        flying = [entry[3] for entry in running]
+        main, flying = lax.optimization_barrier((main, flying))
+        for entry, arrived in zip(list(running), flying):
+            layer, parts, steps, _ = entry
+            try:
+                entry[3] = steps.send(arrived)
+            except StopIteration as stop:
+                for part, share in zip(parts, stop.value):
+                    weight_grads[layer][part] = share
+                running.remove(entry)
+        return main
 
     gradient = my_upstream.astype(single)
-    weight_grads = [None] * layers
     small_grads = [None] * layers
     for layer in range(layers - 1, -1, -1):
         qkv_full, out_full, up_full, down_full = matrices[layer]
@@ -295,27 +377,39 @@
             saved[layer]
         )
         branch = gradient.astype(half)
-        down_share = scatter(contract(activated, branch, 0, 0))
         down_bias_grad = jnp.sum(branch, axis=0, dtype=single)
         activated_grad = contract(branch, down_full, 1, 1)
         pull = jax.vjp(lambda value: jax.nn.gelu(value, approximate=True), pre_activation)[1]
         upper = pull(activated_grad)[0].astype(half)
-        up_share = scatter(contract(second, upper, 0, 0))
+        upper = advance(upper)
+        first_batch = ((3, 2), ((activated, branch), (second, upper)))
+        if layer:
+            begin(layer, *first_batch)
         up_bias_grad = jnp.sum(upper, axis=0, dtype=single)
         second_grad = contract(upper, up_full, 1, 1)
         middle_part, second_gain, second_offset = layer_norm_grad(middle, gains[1], second_grad)
         middle_grad = gradient + middle_part
         attention_grad = middle_grad.astype(half)
-        out_share = scatter(contract(attended, attention_grad, 0, 0))
         out_bias_grad = jnp.sum(attention_grad, axis=0, dtype=single)
+        attention_grad = advance(attention_grad)
+        if not layer:
+            begin(layer, (3, 2, 1), first_batch[1] + ((attended, attention_grad),))
         upstream = contract(attention_grad, out_full, 1, 1).astype(half)
+        if not layer:
+            upstream = advance(upstream)
+        if layer == layers - 1:
+            upstream, output = lax.optimization_barrier((upstream, output))
+            output = output.astype(single)
         packed_grad = attend_backward(packed, bias, upstream, totals, attended)
-        qkv_share = scatter(contract(normed, packed_grad, 0, 0))
+        packed_grad = advance(packed_grad)
+        if layer:
+            begin(layer, (0, 1), ((normed, packed_grad), (attended, attention_grad)))
+        else:
+            begin(layer, (0,), ((normed, packed_grad),))
         column_sums = jnp.sum(packed_grad, axis=0, dtype=single)
         normed_grad = contract(packed_grad, qkv_full, 1, 1)
         hidden_part, first_gain, first_offset = layer_norm_grad(hidden, gains[0], normed_grad)
-        gradient = middle_grad + hidden_part
-        weight_grads[layer] = (qkv_share, out_share, up_share, down_share)
+        gradient = advance(middle_grad + hidden_part)
         small_grads[layer] = (
             jnp.stack([first_gain, second_gain]),
             jnp.stack(
@@ -330,7 +424,10 @@
             ),
             up_bias_grad,
         )
-    input_grad = split_back(gradient).astype(single)
+    input_grad = split_back(gradient)
+    while running:
+        input_grad = advance(input_grad)
+    input_grad = input_grad.astype(single)
 
     def by_owner(parts):
         stacked = jnp.stack(parts)

time: 1200 us -> 893 us (0.74)
  waiting for transfers between devices: 717 us -> 376 us
  other arithmetic: 38.1 us -> 69.6 us
  local copies, waits for them, and re-layouts: 27 us -> 49.1 us
  matrix products: 216 us -> 195 us
  starting transfers between devices: 32 us -> 48.8 us
  blocking collectives: 22.4 us -> 7.85 us
    reduce_scatter x8 -> x0, waiting for transfers between devices: 446 us -> none  [scatter(): lax.psum_scatter(term.astype(half), 'wide', scatter_dimension=0, tiled=True)]
    ppermute x8 -> x32, waiting for transfers between devices: 6.85 us -> 91.6 us  [the longest x12 63.5 us: reduce_group(): received, = (yield [lax.ppermute(sent, 'wide', pair_up(bit))])]
    unnamed x18 -> x10, waiting for transfers between devices: 2.69 us -> 38.7 us
    all_gather x1 -> x0, blocking collectives: 22.4 us -> none  [per_device(): small_whole = lax.all_gather(small, 'wide', axis=0, tiled=False)]
    convert_element_type x3 -> x18, other arithmetic: 8.22 us -> 30.2 us  [the longest x12 16.2 us: reduce_group(): current = (kept.astype(single) + received.astype(single)).astype(half)]
    dot_general x24 -> x32, matrix products: 216 us -> 195 us  [contract(): lax.dot_general(left, right, (((left_dim,), (right_dim,)), ((), ())), pre...]
    all_gather x7, waiting for transfers between devices: 195 us -> 215 us  [per_device(): lax.all_gather(source[layer], 'wide', axis=0, tiled=True)]
    ppermute x8 -> x32, starting transfers between devices: 12.2 us -> 31.1 us  [the longest x12 16.3 us: reduce_group(): received, = (yield [lax.ppermute(sent, 'wide', pair_up(bit))])]
  transfers between devices with their start and end apart: 31 -> 46, of which waited for: 19 -> 23; matrix products, arithmetic and copies ran while one was open for 17% -> 27% of each run, Pallas kernels for 7% -> 14%
where the time goes in v2:
time: 893 us; the launch traced here: 887 us
  waiting for transfers between devices  376 us (42%)
  matrix products  195 us (22%)
  Pallas kernels  125 us (14%)
  other arithmetic  69.6 us (8%)
  local copies, waits for them, and re-layouts  49.1 us (5%)
  starting transfers between devices  48.8 us (5%)
  between operations  16.3 us (2%)
    all_gather x7, waiting for transfers between devices, per_device(): lax.all_gather(source[layer], 'wide', axis=0, tiled=True)  215 us
    dot_general x32, matrix products, contract(): lax.dot_general(left, right, (((left_dim,), (right_dim,)), ((), ())), pre...  195 us
    pallas_call x2, Pallas kernels, attend_backward(): pl.pallas_call(functools.partial(attend_grad_kernel, rows=BACKWARD_ROWS),...  74.5 us
    ppermute x12, waiting for transfers between devices, reduce_group(): received, = (yield [lax.ppermute(sent, 'wide', pair_up(bit))])  63.5 us
    pallas_call x2, Pallas kernels, attend_forward(): pl.pallas_call(functools.partial(attend_kernel, rows=FORWARD_ROWS), grid=...  50.4 us
    unnamed x10, waiting for transfers between devices  38.7 us
    all_to_all x2, waiting for transfers between devices, whole_sequence(): lax.all_to_all(part, 'seq', split_axis=0, concat_axis=1, tiled=True)[0]  29.8 us
    ppermute x4, waiting for transfers between devices, reduce_group(): received, = (yield [lax.ppermute(sent, 'seq', swap)])  25.2 us
  transfers between devices with their start and end apart: 46, of which 23 were waited for; matrix products, arithmetic and copies ran while one was open for 27% of the time, Pallas kernels for 14%

profile of v2, /device:TPU:0, one launch (start us, length us, event | category | flops | bytes accessed | tf_op | source)
XLA Modules:
  0.0 887.3 jit_solution(4300211142788249209)
XLA Ops:
  18.9 7.8 all_to_all.37
  26.7 3.7 all-to-all-start.1
  34.7 13.8 %all-to-all-done.1 = bf16[2,512,768]{2,1,0:T(8,128)(2,1)S(1)} async-done(((bf16[2,512,768]{2,1,0:T(8,128)(2,1)}), bf16[2,512,768]{2,1,0:T(8,128)(2,1)S(1)}, u32[]{:S(2)}, u32[]{:S(2)}) %all-to-all-start.1) | async-done | bytes 1572896 | tf_op jit(solution)/shard_map/all_to_all | solution.py:232
  53.2 16.1 %all-to-all-done = bf16[2,512,768]{2,1,0:T(8,128)(2,1)S(1)} async-done(((bf16[2,512,768]{2,1,0:T(8,128)(2,1)}), bf16[2,512,768]{2,1,0:T(8,128)(2,1)S(1)}, u32[]{:S(2)}, u32[]{:S(2)}) %all-to-all-start) | async-done | bytes 1572896 | tf_op jit(solution)/shard_map/all_to_all | solution.py:232
  74.3 7.9 add_convert_fusion.1.query_ref.key_ref.value_ref
  82.2 25.2 %attend_forward.2 = (bf16[1024,768]{1,0:T(8,128)(2,1)}, f32[6,2,1024]{2,1,0:T(2,128)}) custom-call(bf16[1024,2304]{1,0:T(8,128)(2,1)} %add_convert_fusion.1.query_ref.key_ref.value_ref, bf16[1024,2304]{1,0:T(8,128)(2,1)} %add_convert_fusion.1.query_ref.key_ref.value_ref, bf16[1024,2304]{1,0:T(8,128)(2,1)} %add_convert_fusion.1.query_ref.key_ref.value_ref, ...), custom_call_target="tpu_custom_call" | custom-call | flops 12884901888 | bytes 6291456 | tf_op jit(solution)/shard_map/attend_forward/pallas_call | solution.py:62
  115.8 42.0 %all-gather.20.cloned.1.call-done = bf16[1,768,3072]{2,1,0:T(8,128)(2,1)} async-done(((bf16[1,48,3072]{2,1,0:T(8,128)(2,1)}), bf16[1,768,3072]{2,1,0:T(8,128)(2,1)}) %all-gather.20.cloned.1.call-update) | async-done | bytes 4718608 | tf_op jit(solution)/shard_map/all_gather | solution.py:255
  157.8 14.1 %multiply_convert_fusion.1 = (bf16[1024,3072]{1,0:T(8,128)(2,1)}, f32[1024,3072]{1,0:T(8,128)}) fusion(f32[3072]{0:T(1024)S(1)} %add.428, bf16[1024,768]{1,0:T(8,128)(2,1)S(1)} %add_convert_fusion.11, bf16[1,768,3072]{2,1,0:T(8,128)(2,1)} %all-gather.20.cloned.1.call-done), kind=kOutput, calls=%fused_computation.21 | convolution fusion | flops 4863295488 | bytes 25178112 | tf_op jit(solution)/shard_map/dot_general | solution.py:22
  171.8 40.4 %all-gather.22.cloned.1.call-done = bf16[1,3072,768]{2,1,0:T(8,128)(2,1)} async-done(((bf16[1,192,768]{2,1,0:T(8,128)(2,1)}), bf16[1,3072,768]{2,1,0:T(8,128)(2,1)}) %all-gather.22.cloned.1.call-update) | async-done | bytes 4718608 | tf_op jit(solution)/shard_map/all_gather | solution.py:255
  212.3 9.3 %fusion.125 = (f32[1024]{0:T(1024)S(1)}, f32[1024,768]{1,0:T(8,128)S(1)}) fusion(f32[1024,768]{1,0:T(8,128)} %copy-done.7, f32[768]{0:T(1024)S(1)} %get-tuple-element.171, bf16[1024,3072]{1,0:T(8,128)(2,1)} %get-tuple-element.269, bf16[1,3072,768]{2,1,0:T(8,128)(2,1)} %all-gather.22.cloned.1.call-done), kind=kOutput, calls=%fused_computation.327 | convolution fusion | flops 4834196480 | bytes 17308672 | tf_op jit(solution)/shard_map/dot_general | solution.py:22
  223.9 36.9 %all-gather.24.cloned.1.call-done = bf16[1,768,2304]{2,1,0:T(8,128)(2,1)} async-done(((bf16[1,48,2304]{2,1,0:T(8,128)(2,1)}), bf16[1,768,2304]{2,1,0:T(8,128)(2,1)}) %all-gather.24.cloned.1.call-update) | async-done | bytes 3538960 | tf_op jit(solution)/shard_map/all_gather | solution.py:255
  260.8 8.5 add_convert_fusion.query_ref.key_ref.value_ref
  269.3 25.2 %attend_forward.3 = (bf16[1024,768]{1,0:T(8,128)(2,1)}, f32[6,2,1024]{2,1,0:T(2,128)}) custom-call(bf16[1024,2304]{1,0:T(8,128)(2,1)} %add_convert_fusion.query_ref.key_ref.value_ref, bf16[1024,2304]{1,0:T(8,128)(2,1)} %add_convert_fusion.query_ref.key_ref.value_ref, bf16[1024,2304]{1,0:T(8,128)(2,1)} %add_convert_fusion.query_ref.key_ref.value_ref, ...), custom_call_target="tpu_custom_call" | custom-call | flops 12884901888 | bytes 6291456 | tf_op jit(solution)/shard_map/attend_forward/pallas_call | solution.py:62
  294.6 5.7 all-gather.26.cloned.1.call-done
  307.0 48.4 %all-gather.30.cloned.1.call-done = bf16[1,768,3072]{2,1,0:T(8,128)(2,1)} async-done(((bf16[1,48,3072]{2,1,0:T(8,128)(2,1)}), bf16[1,768,3072]{2,1,0:T(8,128)(2,1)}) %all-gather.30.cloned.1.call-update) | async-done | bytes 4718608 | tf_op jit(solution)/shard_map/all_gather | solution.py:255
  355.4 13.4 %multiply_convert_fusion = (bf16[1024,3072]{1,0:T(8,128)(2,1)}, f32[1024,3072]{1,0:T(8,128)}) fusion(f32[3072]{0:T(1024)S(1)} %add.451, bf16[1024,768]{1,0:T(8,128)(2,1)} %add_convert_fusion.9, bf16[1,768,3072]{2,1,0:T(8,128)(2,1)} %all-gather.30.cloned.1.call-done), kind=kOutput, calls=%fused_computation.20 | convolution fusion | flops 4863295488 | bytes 25178112 | tf_op jit(solution)/shard_map/dot_general | solution.py:22
  368.7 41.3 %all-gather.28.cloned.1.call-done = bf16[1,3072,768]{2,1,0:T(8,128)(2,1)} async-done(((bf16[1,192,768]{2,1,0:T(8,128)(2,1)}), bf16[1,3072,768]{2,1,0:T(8,128)(2,1)}) %all-gather.28.cloned.1.call-update) | async-done | bytes 4718608 | tf_op jit(solution)/shard_map/all_gather | solution.py:255
  410.0 16.3 %convert_reduce_fusion = (f32[3072]{0:T(1024)S(1)}, bf16[1024,3072]{1,0:T(8,128)(2,1)S(1)}) fusion(f32[1024,3072]{1,0:T(8,128)} %get-tuple-element.277, f32[3072]{0:T(1024)S(1)} %add.451, bf16[1024,768]{1,0:T(8,128)(2,1)} %bitcast.311, bf16[1,3072,768]{2,1,0:T(8,128)(2,1)} %all-gather.28.cloned.1.call-done), kind=kOutput, calls=%fused_computation.18 | convolution fusion | flops 4904186880 | bytes 25190400 | tf_op jit(solution)/shard_map/dot_general | solution.py:22
  426.4 4.0 convolution_convert_fusion.3
  432.7 4.8 convolution_convert_fusion.1
  437.8 6.3 add_convert_fusion.8
  444.2 4.6 all-to-all-start.3
  448.9 9.9 %multiply_reduce_fusion = (f32[768]{0:T(1024)S(1)}, f32[1024]{0:T(1024)S(1)}, f32[1024]{0:T(1024)S(1)}, f32[768]{0:T(1024)S(1)}, f32[1024,768]{1,0:T(8,128)S(1)}) fusion(f32[1024,768]{1,0:T(8,128)} %copy-done.4, f32[1024]{0:T(1024)S(1)} %add_rsqrt_fusion, f32[1024]{0:T(1024)S(1)} %broadcast_multiply_fusion.8, f32[768]{0:T(1024)S(1)} %get-tuple-element.179, ...), kind=kOutput, calls=%fused_computation.70 | convolution fusion | flops 4838912000 | bytes 17327104 | tf_op jit(solution)/shard_map/dot_general | solution.py:22
  463.3 5.1 fusion.44
  468.4 5.6 fusion.81
  494.8 37.4 %attend_backward.2 = bf16[1024,2304]{1,0:T(8,128)(2,1)} custom-call(bf16[1024,2304]{1,0:T(8,128)(2,1)} %add_convert_fusion.query_ref.key_ref.value_ref, bf16[1024,2304]{1,0:T(8,128)(2,1)} %add_convert_fusion.query_ref.key_ref.value_ref, bf16[1024,2304]{1,0:T(8,128)(2,1)} %add_convert_fusion.query_ref.key_ref.value_ref, f32[1024,1024]{1,0:T(8,128)} %fusion.32.bias_ref, ...), custom_call_target="tpu_custom_call" | custom-call | flops 32212254720 | bytes 12582912 | tf_op jit(solution)/shard_map/attend_backward/pallas_call | solution.py:149
  532.1 6.7 collective-permute-done.2
  538.8 5.3 convolution_convert_fusion.5
  550.0 6.0 multiply_reduce_fusion.1
  562.0 16.2 %collective-permute-done.3 = bf16[4,48,3072]{2,1,0:T(8,128)(2,1)} collective-permute-done((bf16[4,48,3072]{2,1,0:T(8,128)(2,1)}, bf16[4,48,3072]{2,1,0:T(8,128)(2,1)}, u32[]{:S(2)}, u32[]{:S(2)}) %collective-permute-start.3) | collective-permute-done | bytes 1179680 | tf_op jit(solution)/shard_map/ppermute | solution.py:327
  578.1 4.4 fusion.40
  594.0 5.0 convolution_convert_fusion
  599.1 15.6 %fusion.6 = bf16[1024,3072]{1,0:T(8,128)(2,1)} fusion(f32[1024,3072]{1,0:T(8,128)} %get-tuple-element.270, f32[3072]{0:T(1024)S(1)} %copy-done.88, bf16[1024,768]{1,0:T(8,128)(2,1)S(1)} %get-tuple-element.184, bf16[1,3072,768]{2,1,0:T(8,128)(2,1)S(1)} %bitcast.362), kind=kOutput, calls=%fused_computation.10 | convolution fusion | flops 4897898496 | bytes 25178112 | tf_op jit(solution)/shard_map/dot_general | solution.py:22
  622.4 5.7 convolution_convert_fusion.2
  628.2 5.8 multiply_reduce_fusion.2
  656.6 4.6 add_convert_fusion.3
  661.2 5.0 add_convert_fusion.4
  671.0 37.1 %attend_backward.3 = bf16[1024,2304]{1,0:T(8,128)(2,1)} custom-call(bf16[1024,2304]{1,0:T(8,128)(2,1)} %add_convert_fusion.1.query_ref.key_ref.value_ref, bf16[1024,2304]{1,0:T(8,128)(2,1)} %add_convert_fusion.1.query_ref.key_ref.value_ref, bf16[1024,2304]{1,0:T(8,128)(2,1)} %add_convert_fusion.1.query_ref.key_ref.value_ref, f32[1024,1024]{1,0:T(8,128)} %fusion.32.bias_ref, ...), custom_call_target="tpu_custom_call" | custom-call | flops 32212254720 | bytes 12582912 | tf_op jit(solution)/shard_map/attend_backward/pallas_call | solution.py:149
  708.2 17.5 %collective-permute-done.17 = bf16[8,48,3456]{2,1,0:T(8,128)(2,1)S(1)} collective-permute-done((bf16[8,48,3456]{2,1,0:T(8,128)(2,1)S(1)}, bf16[8,48,3456]{2,1,0:T(8,128)(2,1)S(1)}, u32[]{:S(2)}, u32[]{:S(2)}) %collective-permute-start.17) | collective-permute-done | bytes 2654240 | tf_op jit(solution)/shard_map/ppermute | solution.py:320
  725.7 4.0 convert_reduce_fusion.3
  733.4 6.7 multiply_reduce_fusion.3
  754.8 19.7 %collective-permute-done.19 = bf16[4,48,3456]{2,1,0:T(8,128)(2,1)S(1)} collective-permute-done((bf16[4,48,3456]{2,1,0:T(8,128)(2,1)S(1)}, bf16[4,48,3456]{2,1,0:T(8,128)(2,1)S(1)}, u32[]{:S(2)}, u32[]{:S(2)}) %collective-permute-start.19) | collective-permute-done | bytes 1327136 | tf_op jit(solution)/shard_map/ppermute | solution.py:327
  780.9 3.9 all-to-all-start.4
  791.0 36.2 %all-reduce.4.cloned.1.call-done = f32[16,1152]{1,0:T(8,128)} async-done(((f32[16,1152]{1,0:T(8,128)}), f32[16,1152]{1,0:T(8,128)}) %all-reduce.4.cloned.1.call-update) | async-done | bytes 73744
  838.3 3.8 collective-permute-start.24
  843.1 10.8 %collective-permute-done.24 = bf16[1,48,3456]{2,1,0:T(8,128)(2,1)S(1)} collective-permute-done((bf16[1,48,3456]{2,1,0:T(8,128)(2,1)S(1)}, bf16[1,48,3456]{2,1,0:T(8,128)(2,1)S(1)}, u32[]{:S(2)}, u32[]{:S(2)}) %collective-permute-start.24) | collective-permute-done | bytes 331808 | tf_op jit(solution)/shard_map/ppermute | solution.py:327
  855.7 5.9 collective-permute-done.27
  863.9 7.3 collective-permute-done.29
  (528 shorter events, 183.9 us)
Async XLA Ops:
  7.2 63.2 %all-gather.16.cloned.1.call-start = ((), (), s32[]{:S(2)}) async-start(), calls=%async_computation.5 | async-start | bytes 3969024 | tf_op jit(solution)/shard_map/all_gather | solution.py:247
  12.3 95.1 %all-gather.18.cloned.1.call-start = ((), (), s32[]{:S(2)}) async-start(), calls=%async_computation.6 | async-start | bytes 1253376 | tf_op jit(solution)/shard_map/all_gather | solution.py:255
  14.0 143.8 %all-gather.20.cloned.1.call-start = ((), (), s32[]{:S(2)}) async-start(), calls=%async_computation.7 | async-start | bytes 5013504 | tf_op jit(solution)/shard_map/all_gather | solution.py:255
  15.9 196.3 %all-gather.22.cloned.1.call-start = ((), (), s32[]{:S(2)}) async-start(), calls=%async_computation.8 | async-start | bytes 5013504 | tf_op jit(solution)/shard_map/all_gather | solution.py:255
  16.9 243.9 %all-gather.24.cloned.1.call-start = ((), (), s32[]{:S(2)}) async-start(), calls=%async_computation.9 | async-start | bytes 3760128 | tf_op jit(solution)/shard_map/all_gather | solution.py:255
  17.5 282.8 %all-gather.26.cloned.1.call-start = ((), (), s32[]{:S(2)}) async-start(), calls=%async_computation.10 | async-start | bytes 1253376 | tf_op jit(solution)/shard_map/all_gather | solution.py:255
  18.0 337.3 %all-gather.30.cloned.1.call-start = ((), (), s32[]{:S(2)}) async-start(), calls=%async_computation.12 | async-start | bytes 5013504 | tf_op jit(solution)/shard_map/all_gather | solution.py:255
  26.7 21.7 %all-to-all-start.1 = ((bf16[2,512,768]{2,1,0:T(8,128)(2,1)}), bf16[2,512,768]{2,1,0:T(8,128)(2,1)S(1)}, u32[]{:S(2)}, u32[]{:S(2)}) async-start(bf16[2,512,768]{2,1,0:T(8,128)(2,1)} %param.12), calls=%async_computation.1 | async-start | bytes 3145728 | tf_op jit(solution)/shard_map/all_to_all | solution.py:232
  30.4 379.7 %all-gather.28.cloned.1.call-start = ((), (), s32[]{:S(2)}) async-start(), calls=%async_computation.11 | async-start | bytes 5013504 | tf_op jit(solution)/shard_map/all_gather | solution.py:255
  31.8 75.6 %copy-start.59 = (f32[768]{0:T(1024)}, f32[768]{0:T(1024)S(1)}, u32[]{:S(2)}) copy-start(f32[768]{0:T(1024)S(1)} %fusion.110) | copy-start | bytes 9220
  48.4 20.9 %all-to-all-start = ((bf16[2,512,768]{2,1,0:T(8,128)(2,1)}), bf16[2,512,768]{2,1,0:T(8,128)(2,1)S(1)}, u32[]{:S(2)}, u32[]{:S(2)}) async-start(bf16[2,512,768]{2,1,0:T(8,128)(2,1)} %param.16), calls=%async_computation | async-start | bytes 3145728 | tf_op jit(solution)/shard_map/all_to_all | solution.py:232
  72.3 149.9 %copy-start.69 = (f32[768]{0:T(1024)}, f32[768]{0:T(1024)S(1)}, u32[]{:S(2)}) copy-start(f32[768]{0:T(1024)S(1)} %get-tuple-element.180) | copy-start | bytes 9220
  430.7 43.3 %collective-permute-start.1 = (bf16[768,1536]{1,0:T(8,128)(2,1)}, bf16[768,1536]{1,0:T(8,128)(2,1)}, u32[]{:S(2)}, u32[]{:S(2)}) collective-permute-start(bf16[768,1536]{1,0:T(8,128)(2,1)} %convolution_convert_fusion.3), channel_id=1, source_target_pairs={{0,2},{2,0},{4,6},{6,4},{8,10},{10,8},{12,14},{14,12},{16,18},{18,... | collective-permute-start | bytes 7077896 | tf_op jit(solution)/shard_map/ppermute | solution.py:313
  437.6 36.5 %collective-permute-start = (bf16[3072,384]{1,0:T(8,128)(2,1)}, bf16[3072,384]{1,0:T(8,128)(2,1)}, u32[]{:S(2)}, u32[]{:S(2)}) collective-permute-start(bf16[3072,384]{1,0:T(8,128)(2,1)} %convolution_convert_fusion.1), channel_id=1, source_target_pairs={{0,2},{2,0},{4,6},{6,4},{8,10},{10,8},{12,14},{14,12},{16,18},{18,... | collective-permute-start | bytes 7077896 | tf_op jit(solution)/shard_map/ppermute | solution.py:313
  444.2 47.3 %all-to-all-start.3 = ((bf16[2,512,768]{2,1,0:T(8,128)(2,1)}), bf16[2,512,768]{2,1,0:T(8,128)(2,1)}, u32[]{:S(2)}, u32[]{:S(2)}) async-start(bf16[2,512,768]{2,1,0:T(8,128)(2,1)} %bitcast.344), calls=%async_computation.3 | async-start | bytes 3145728 | tf_op jit(solution)/shard_map/all_to_all | solution.py:285
  448.8 378.4 %all-reduce.4.cloned.1.call-start = ((), (), s32[]{:S(2)}) async-start(), calls=%async_computation.13 | async-start | bytes 147456
  485.1 53.7 %collective-permute-start.2 = (bf16[8,48,3072]{2,1,0:T(8,128)(2,1)}, bf16[8,48,3072]{2,1,0:T(8,128)(2,1)}, u32[]{:S(2)}, u32[]{:S(2)}) collective-permute-start(bf16[8,48,3072]{2,1,0:T(8,128)(2,1)} %get-tuple-element.198), channel_id=1, source_target_pairs={{0,1},{1,0},{2,3},{3,2},{4,5},{5,4},{6,7},{7,6},{8,9},{9,8},{10,11... | collective-permute-start | bytes 7077896 | tf_op jit(solution)/shard_map/ppermute | solution.py:320
  491.4 70.5 %collective-permute-start.5 = (bf16[768,384]{1,0:T(8,128)(2,1)}, bf16[768,384]{1,0:T(8,128)(2,1)}, u32[]{:S(2)}, u32[]{:S(2)}) collective-permute-start(bf16[768,384]{1,0:T(8,128)(2,1)} %convolution_convert_fusion.9), channel_id=1, source_target_pairs={{0,2},{2,0},{4,6},{6,4},{8,10},{10,8},{12,14},{14,12},{16,18},{18,... | collective-permute-start | bytes 1769480 | tf_op jit(solution)/shard_map/ppermute | solution.py:313
  544.1 34.0 %collective-permute-start.4 = (bf16[768,1152]{1,0:T(8,128)(2,1)}, bf16[768,1152]{1,0:T(8,128)(2,1)}, u32[]{:S(2)}, u32[]{:S(2)}) collective-permute-start(bf16[768,1152]{1,0:T(8,128)(2,1)} %convolution_convert_fusion.5), channel_id=1, source_target_pairs={{0,2},{2,0},{4,6},{6,4},{8,10},{10,8},{12,14},{14,12},{16,18},{18,... | collective-permute-start | bytes 5308424 | tf_op jit(solution)/shard_map/ppermute | solution.py:313
  549.5 28.7 %collective-permute-start.3 = (bf16[4,48,3072]{2,1,0:T(8,128)(2,1)}, bf16[4,48,3072]{2,1,0:T(8,128)(2,1)}, u32[]{:S(2)}, u32[]{:S(2)}) collective-permute-start(bf16[4,48,3072]{2,1,0:T(8,128)(2,1)} %dynamic-slice_bitcast_fusion.1), channel_id=1, source_target_pairs={{0,4},{2,6},{4,0},{6,2},{8,12},{10,14},{12,8},{14,10},{16,20},{18,... | collective-permute-start | bytes 3538952 | tf_op jit(solution)/shard_map/ppermute | solution.py:327
  587.9 27.8 %collective-permute-start.7 = (bf16[8,48,1536]{2,1,0:T(8,128)(2,1)}, bf16[8,48,1536]{2,1,0:T(8,128)(2,1)S(1)}, u32[]{:S(2)}, u32[]{:S(2)}) collective-permute-start(bf16[8,48,1536]{2,1,0:T(8,128)(2,1)} %pad_maximum_fusion), channel_id=1, source_target_pairs={{0,1},{1,0},{2,3},{3,2},{4,5},{5,4},{6,7},{7,6},{8,9},{9,8},{10,11... | collective-permute-start | bytes 3538952 | tf_op jit(solution)/shard_map/ppermute | solution.py:320
  592.1 22.7 %collective-permute-start.6 = (bf16[2,48,3072]{2,1,0:T(8,128)(2,1)}, bf16[2,48,3072]{2,1,0:T(8,128)(2,1)}, u32[]{:S(2)}, u32[]{:S(2)}) collective-permute-start(bf16[2,48,3072]{2,1,0:T(8,128)(2,1)} %dynamic-slice_bitcast_fusion.7), channel_id=1, source_target_pairs={{0,8},{2,10},{4,12},{6,14},{8,0},{10,2},{12,4},{14,6},{16,24},{18,... | collective-permute-start | bytes 1769480 | tf_op jit(solution)/shard_map/ppermute | solution.py:327
  599.0 56.5 %collective-permute-start.12 = (bf16[3072,384]{1,0:T(8,128)(2,1)}, bf16[3072,384]{1,0:T(8,128)(2,1)}, u32[]{:S(2)}, u32[]{:S(2)}) collective-permute-start(bf16[3072,384]{1,0:T(8,128)(2,1)} %convolution_convert_fusion), channel_id=1, source_target_pairs={{0,2},{2,0},{4,6},{6,4},{8,10},{10,8},{12,14},{14,12},{16,18},{18,... | collective-permute-start | bytes 7077896 | tf_op jit(solution)/shard_map/ppermute | solution.py:313
  618.5 22.6 %collective-permute-start.9 = (bf16[4,48,1536]{2,1,0:T(8,128)(2,1)S(1)}, bf16[4,48,1536]{2,1,0:T(8,128)(2,1)}, u32[]{:S(2)}, u32[]{:S(2)}) collective-permute-start(bf16[4,48,1536]{2,1,0:T(8,128)(2,1)S(1)} %dynamic-slice_bitcast_fusion.6), channel_id=1, source_target_pairs={{0,4},{2,6},{4,0},{6,2},{8,12},{10,14},{12,8},{14,10},{16,20},{18,... | collective-permute-start | bytes 1769480 | tf_op jit(solution)/shard_map/ppermute | solution.py:327
  620.5 20.6 %collective-permute-start.8 = (bf16[1,48,3072]{2,1,0:T(8,128)(2,1)S(1)}, bf16[1,48,3072]{2,1,0:T(8,128)(2,1)S(1)}, u32[]{:S(2)}, u32[]{:S(2)}) collective-permute-start(bf16[1,48,3072]{2,1,0:T(8,128)(2,1)S(1)} %constant_dynamic-slice_fusion.3), channel_id=1, source_target_pairs={{0,16},{2,18},{4,20},{6,22},{8,24},{10,26},{12,28},{14,30},{16,0},... | collective-permute-start | bytes 884744 | tf_op jit(solution)/shard_map/ppermute | solution.py:327
  634.0 21.5 %collective-permute-start.13 = (bf16[768,1536]{1,0:T(8,128)(2,1)}, bf16[768,1536]{1,0:T(8,128)(2,1)}, u32[]{:S(2)}, u32[]{:S(2)}) collective-permute-start(bf16[768,1536]{1,0:T(8,128)(2,1)} %convolution_convert_fusion.2), channel_id=1, source_target_pairs={{0,2},{2,0},{4,6},{6,4},{8,10},{10,8},{12,14},{14,12},{16,18},{18,... | collective-permute-start | bytes 7077896 | tf_op jit(solution)/shard_map/ppermute | solution.py:313
  643.9 11.5 %collective-permute-start.14 = (bf16[768,384]{1,0:T(8,128)(2,1)S(1)}, bf16[768,384]{1,0:T(8,128)(2,1)S(1)}, u32[]{:S(2)}, u32[]{:S(2)}) collective-permute-start(bf16[768,384]{1,0:T(8,128)(2,1)S(1)} %convolution_convert_fusion.8), channel_id=1, source_target_pairs={{0,2},{2,0},{4,6},{6,4},{8,10},{10,8},{12,14},{14,12},{16,18},{18,... | collective-permute-start | bytes 1769480 | tf_op jit(solution)/shard_map/ppermute | solution.py:313
  645.7 9.0 %collective-permute-start.11 = (bf16[2,48,1536]{2,1,0:T(8,128)(2,1)S(1)}, bf16[2,48,1536]{2,1,0:T(8,128)(2,1)S(1)}, u32[]{:S(2)}, u32[]{:S(2)}) collective-permute-start(bf16[2,48,1536]{2,1,0:T(8,128)(2,1)S(1)} %dynamic-slice_bitcast_fusion.9), channel_id=1, source_target_pairs={{0,8},{2,10},{4,12},{6,14},{8,0},{10,2},{12,4},{14,6},{16,24},{18,... | collective-permute-start | bytes 884744 | tf_op jit(solution)/shard_map/ppermute | solution.py:327
  646.7 8.7 collective-permute-start.10
  667.3 58.4 %collective-permute-start.17 = (bf16[8,48,3456]{2,1,0:T(8,128)(2,1)S(1)}, bf16[8,48,3456]{2,1,0:T(8,128)(2,1)S(1)}, u32[]{:S(2)}, u32[]{:S(2)}) collective-permute-start(bf16[8,48,3456]{2,1,0:T(8,128)(2,1)S(1)} %get-tuple-element.210), channel_id=1, source_target_pairs={{0,1},{1,0},{2,3},{3,2},{4,5},{5,4},{6,7},{7,6},{8,9},{9,8},{10,11... | collective-permute-start | bytes 7962632 | tf_op jit(solution)/shard_map/ppermute | solution.py:320
  669.2 39.0 %collective-permute-start.16 = (bf16[1,48,1536]{2,1,0:T(8,128)(2,1)S(1)}, bf16[1,48,1536]{2,1,0:T(8,128)(2,1)S(1)}, u32[]{:S(2)}, u32[]{:S(2)}) collective-permute-start(bf16[1,48,1536]{2,1,0:T(8,128)(2,1)S(1)} %constant_dynamic-slice_fusion.2), channel_id=1, source_target_pairs={{0,16},{2,18},{4,20},{6,22},{8,24},{10,26},{12,28},{14,30},{16,0},... | collective-permute-start | bytes 442376 | tf_op jit(solution)/shard_map/ppermute | solution.py:327
  670.9 37.3 %collective-permute-start.15 = (bf16[48,3072]{1,0:T(8,128)(2,1)S(1)}, bf16[48,3072]{1,0:T(8,128)(2,1)S(1)}, u32[]{:S(2)}, u32[]{:S(2)}) collective-permute-start(bf16[48,3072]{1,0:T(8,128)(2,1)S(1)} %broadcast_select_fusion.7), channel_id=1, source_target_pairs={{0,2},{2,0},{4,6},{6,4},{8,10},{10,8},{12,14},{14,12},{16,18},{18,... | collective-permute-start | bytes 884744 | tf_op jit(solution)/shard_map/ppermute | solution.py:336
  745.1 29.3 %collective-permute-start.19 = (bf16[4,48,3456]{2,1,0:T(8,128)(2,1)S(1)}, bf16[4,48,3456]{2,1,0:T(8,128)(2,1)S(1)}, u32[]{:S(2)}, u32[]{:S(2)}) collective-permute-start(bf16[4,48,3456]{2,1,0:T(8,128)(2,1)S(1)} %dynamic-slice_bitcast_fusion), channel_id=1, source_target_pairs={{0,4},{2,6},{4,0},{6,2},{8,12},{10,14},{12,8},{14,10},{16,20},{18,... | collective-permute-start | bytes 3981320 | tf_op jit(solution)/shard_map/ppermute | solution.py:327
  746.7 27.8 %collective-permute-start.20 = (bf16[768,1152]{1,0:T(8,128)(2,1)S(1)}, bf16[768,1152]{1,0:T(8,128)(2,1)S(1)}, u32[]{:S(2)}, u32[]{:S(2)}) collective-permute-start(bf16[768,1152]{1,0:T(8,128)(2,1)S(1)} %copy-done.94), channel_id=1, source_target_pairs={{0,2},{2,0},{4,6},{6,4},{8,10},{10,8},{12,14},{14,12},{16,18},{18,... | collective-permute-start | bytes 5308424 | tf_op jit(solution)/shard_map/ppermute | solution.py:313
  746.8 8.0 collective-permute-start.18
  777.8 56.6 %collective-permute-start.23 = (bf16[8,48,1152]{2,1,0:T(8,128)(2,1)}, bf16[8,48,1152]{2,1,0:T(8,128)(2,1)}, u32[]{:S(2)}, u32[]{:S(2)}) collective-permute-start(bf16[8,48,1152]{2,1,0:T(8,128)(2,1)} %dynamic-slice_bitcast_fusion.2), channel_id=1, source_target_pairs={{0,1},{1,0},{2,3},{3,2},{4,5},{5,4},{6,7},{7,6},{8,9},{9,8},{10,11... | collective-permute-start | bytes 2654216 | tf_op jit(solution)/shard_map/ppermute | solution.py:320
  780.9 53.5 %all-to-all-start.4 = ((bf16[2,512,768]{2,1,0:T(8,128)(2,1)}), bf16[2,512,768]{2,1,0:T(8,128)(2,1)S(1)}, u32[]{:S(2)}, u32[]{:S(2)}) async-start(bf16[2,512,768]{2,1,0:T(8,128)(2,1)} %bitcast.329), calls=%async_computation.4 | async-start | bytes 3145728 | tf_op jit(solution)/shard_map/all_to_all | solution.py:285
  786.8 47.6 %collective-permute-start.22 = (bf16[2,48,3456]{2,1,0:T(8,128)(2,1)}, bf16[2,48,3456]{2,1,0:T(8,128)(2,1)}, u32[]{:S(2)}, u32[]{:S(2)}) collective-permute-start(bf16[2,48,3456]{2,1,0:T(8,128)(2,1)} %dynamic-slice_bitcast_fusion.5), channel_id=1, source_target_pairs={{0,8},{2,10},{4,12},{6,14},{8,0},{10,2},{12,4},{14,6},{16,24},{18,... | collective-permute-start | bytes 1990664 | tf_op jit(solution)/shard_map/ppermute | solution.py:327
  789.6 44.8 %collective-permute-start.21 = (bf16[48,1536]{1,0:T(8,128)(2,1)}, bf16[48,1536]{1,0:T(8,128)(2,1)}, u32[]{:S(2)}, u32[]{:S(2)}) collective-permute-start(bf16[48,1536]{1,0:T(8,128)(2,1)} %broadcast_select_fusion.11), channel_id=1, source_target_pairs={{0,2},{2,0},{4,6},{6,4},{8,10},{10,8},{12,14},{14,12},{16,18},{18,... | collective-permute-start | bytes 442376 | tf_op jit(solution)/shard_map/ppermute | solution.py:336
  828.6 3.7 collective-permute-start.32
  836.0 17.9 %collective-permute-start.25 = (bf16[4,48,1152]{2,1,0:T(8,128)(2,1)S(1)}, bf16[4,48,1152]{2,1,0:T(8,128)(2,1)S(1)}, u32[]{:S(2)}, u32[]{:S(2)}) collective-permute-start(bf16[4,48,1152]{2,1,0:T(8,128)(2,1)S(1)} %dynamic-slice_bitcast_fusion.8), channel_id=1, source_target_pairs={{0,4},{2,6},{4,0},{6,2},{8,12},{10,14},{12,8},{14,10},{16,20},{18,... | collective-permute-start | bytes 1327112 | tf_op jit(solution)/shard_map/ppermute | solution.py:327
  838.3 15.6 %collective-permute-start.24 = (bf16[1,48,3456]{2,1,0:T(8,128)(2,1)S(1)}, bf16[1,48,3456]{2,1,0:T(8,128)(2,1)S(1)}, u32[]{:S(2)}, u32[]{:S(2)}) collective-permute-start(bf16[1,48,3456]{2,1,0:T(8,128)(2,1)S(1)} %constant_dynamic-slice_fusion.1), channel_id=1, source_target_pairs={{0,16},{2,18},{4,20},{6,22},{8,24},{10,26},{12,28},{14,30},{16,0},... | collective-permute-start | bytes 995336 | tf_op jit(solution)/shard_map/ppermute | solution.py:327
  854.1 8.0 collective-permute-start.26
  855.6 6.0 collective-permute-start.27
  862.3 8.9 %collective-permute-start.28 = (bf16[48,3456]{1,0:T(8,128)(2,1)S(1)}, bf16[48,3456]{1,0:T(8,128)(2,1)S(1)}, u32[]{:S(2)}, u32[]{:S(2)}) collective-permute-start(bf16[48,3456]{1,0:T(8,128)(2,1)S(1)} %broadcast_select_fusion.3), channel_id=1, source_target_pairs={{0,2},{2,0},{4,6},{6,4},{8,10},{10,8},{12,14},{14,12},{16,18},{18,... | collective-permute-start | bytes 995336 | tf_op jit(solution)/shard_map/ppermute | solution.py:336
  862.4 8.8 collective-permute-start.29
  871.4 4.8 collective-permute-start.30
  876.3 1.4 collective-permute-start.31
  (117 other events, 1350.0 us)
Sparse Core Ops, SparseCore 0:
  12.4 50.5 all-gather.15
  65.3 37.3 all-gather.17
  105.5 52.1 all-gather.19
  160.5 51.7 all-gather.21
  215.0 45.7 all-gather.23
  262.9 37.3 all-gather.25
  303.1 52.1 all-gather.29
  358.2 51.7 all-gather.27
  741.7 85.3 all-reduce.3

commit v3 on v1

--- a/solution.py
+++ b/solution.py
@@ -171,6 +171,35 @@
     )(packed, packed, packed, bias, upstream, totals, attended)
 
 
+def place_pieces(pieces, out_shape, targets, indices):
+    def kernel(index_ref, *refs):
+        sources, out_ref, semaphores = refs[: len(pieces)], refs[-2], refs[-1]
+        copies = [
+            pltpu.make_async_copy(
+                source, out_ref.at[target(index_ref)], semaphores.at[number]
+            )
+            for number, (source, target) in enumerate(zip(sources, targets))
+        ]
+        for copy in copies:
+            copy.start()
+        for copy in copies:
+            copy.wait()
+
+    size = 2 * 2
+    for extent in out_shape:
+        size *= extent
+    anywhere = pl.BlockSpec(memory_space=pl.ANY)
+    return pl.pallas_call(
+        kernel,
+        in_specs=[pl.BlockSpec(memory_space=pltpu.SMEM)] + [anywhere] * len(pieces),
+        out_specs=anywhere,
+        out_shape=jax.ShapeDtypeStruct(out_shape, pieces[0].dtype),
+        scratch_shapes=[pltpu.SemaphoreType.DMA((len(pieces),))],
+        cost_estimate=pl.CostEstimate(flops=0, bytes_accessed=size, transcendentals=0),
+        name="place_pieces",
+    )(indices, *pieces)
+
+
 def layer_norm(hidden, scale_gain, offset):
     center = hidden - jnp.mean(hidden, axis=-1, keepdims=True)
     spread = jnp.mean(center * center, axis=-1, keepdims=True)
@@ -188,24 +217,6 @@
         inverse * (scaled - slope - normal * tilt),
         jnp.sum(upstream * normal, axis=0),
         jnp.sum(upstream, axis=0),
-    )
-
-
-def layer_forward(hidden, matrices, rows, bias):
-    qkv_weight, out_weight, up_weight, down_weight = matrices
-    gains, offsets, up_bias = rows
-    normed = layer_norm(hidden, gains[0], offsets[0]).astype(half)
-    shift = jnp.concatenate([offsets[1], jnp.zeros_like(offsets[1]), offsets[2]])
-    packed = (contract(normed, qkv_weight, 1, 0) + shift).astype(half)
-    attended, totals = attend_forward(packed, bias)
-    middle = hidden + (contract(attended, out_weight, 1, 0) + offsets[3])
-    second = layer_norm(middle, gains[1], offsets[4]).astype(half)
-    pre_activation = contract(second, up_weight, 1, 0) + up_bias
-    activated = jax.nn.gelu(pre_activation, approximate=True).astype(half)
-    result = middle + (contract(activated, down_weight, 1, 0) + offsets[5])
-    return (
-        result,
-        (hidden, normed, packed, totals, attended, middle, second, pre_activation, activated),
     )
 
 
@@ -231,24 +242,101 @@
     def whole_sequence(part):
         return lax.all_to_all(part, "seq", split_axis=0, concat_axis=1, tiled=True)[0]
 
+    core = lax.axis_index("wide") & 1
+    place = lax.axis_index("seq")
+    indices = jnp.stack([core, place]).astype(jnp.int32)
+    row_unit = qkv_weight.shape[1]
+    pair_up = lambda bit: [(index, index ^ bit) for index in range(groups)]
+    bit_of = lambda bit: (lax.axis_index("wide") >> (bit.bit_length() - 1)) & 1
+    running = []
+
+    def begin(steps, finish):
+        running.append([steps, finish, next(steps)])
+
+    def advance(main):
+        if not running:
+            return main
+        main, flying = lax.optimization_barrier((main, [entry[2] for entry in running]))
+        for entry, arrived in zip(list(running), flying):
+            try:
+                entry[2] = entry[0].send(arrived)
+            except StopIteration as stop:
+                entry[1](stop.value)
+                running.remove(entry)
+        return main
+
+    def side_of(array, which, axis):
+        return lax.dynamic_index_in_dim(array, which, axis, keepdims=False)
+
+    def gather_steps(shard, split_rows):
+        rows, columns = shard.shape
+        if split_rows:
+            rows //= 2
+            mine = side_of(shard.reshape(2, rows, columns), place, 0)
+        else:
+            columns //= 2
+            mine = lax.dynamic_slice_in_dim(shard, place * columns, columns, axis=1)
+        current = mine[None]
+        bit = groups // 2
+        while bit > 1:
+            (received,) = yield [lax.ppermute(current, "wide", pair_up(bit))]
+            count = current.shape[0]
+            current = place_pieces(
+                [current, received],
+                (count, 2, rows, columns),
+                [lambda ref: (slice(None), ref[0]), lambda ref: (slice(None), 1 - ref[0])],
+                bit_of(bit).reshape(1).astype(jnp.int32),
+            ).reshape(2 * count, rows, columns)
+            bit //= 2
+        (beside,) = yield [lax.ppermute(current, "seq", swap)]
+        passed = yield [lax.ppermute(part, "wide", pair_up(1)) for part in (current, beside)]
+        count = current.shape[0]
+
+        def target(own_core, own_place):
+            def where(ref):
+                which_core = ref[0] if own_core else 1 - ref[0]
+                which_place = ref[1] if own_place else 1 - ref[1]
+                if split_rows:
+                    return (slice(None), which_core, which_place)
+                start = pl.multiple_of(which_place * columns, columns)
+                return (slice(None), which_core, slice(None), pl.ds(start, columns))
+
+            return where
+
+        whole = place_pieces(
+            [current, beside, *passed],
+            (count, 2, 2, rows, columns) if split_rows else (count, 2, rows, 2 * columns),
+            [target(True, True), target(True, False), target(False, True), target(False, False)],
+            indices,
+        )
+        return whole.reshape(-1, shard.shape[1])
+
+    my_tokens = whole_sequence(tokens)
     marks = whole_sequence(jnp.stack([segment_ids, pad_mask], axis=2))
-    my_tokens = whole_sequence(tokens)
-    my_upstream = whole_sequence(out_grad)
-    my_time = lax.dynamic_index_in_dim(time_embed, lax.axis_index("seq"), 0, keepdims=True)
-
-    sources = (qkv_weight, out_weight, up_weight, down_weight)
+    my_time = lax.dynamic_index_in_dim(time_embed, place, 0, keepdims=True)
+
     small = jnp.concatenate(
         [norm_gains.reshape(-1), bias_rows.reshape(-1), up_bias.reshape(-1)]
     )
-    matrices = [[None] * 4 for _ in range(layers)]
-    matrices[0][0] = lax.all_gather(qkv_weight[0], "wide", axis=0, tiled=True)
-    small_whole = lax.all_gather(small, "wide", axis=0, tiled=False)
-    for layer in range(layers):
-        for index, source in enumerate(sources):
-            if matrices[layer][index] is None:
-                matrices[layer][index] = lax.all_gather(
-                    source[layer], "wide", axis=0, tiled=True
-                )
+    side = small.reshape(row_unit, -1)
+    side_width = side.shape[1]
+    side = jnp.pad(side, ((0, 0), (0, -side_width % PAIR)))
+    cuts = [0]
+    for source in (qkv_weight, out_weight, up_weight):
+        cuts.append(cuts[-1] + source.shape[2])
+
+    def beside_each_other(layer, *more):
+        parts = [qkv_weight[layer], out_weight[layer], up_weight[layer], *more]
+        return jnp.concatenate(parts, axis=1)
+
+    def split_matrices(joined):
+        return [joined[:, low:high] for low, high in zip(cuts, cuts[1:])]
+
+    first_whole = lax.all_gather(beside_each_other(0, side), "wide", axis=0, tiled=True)
+    first_down = lax.all_gather(down_weight[0], "wide", axis=0, tiled=True)
+    matrices = [None] * layers
+    matrices[0] = split_matrices(first_whole) + [first_down]
+    small_whole = first_whole[:, cuts[-1] :][:, :side_width].reshape(groups, -1)
     cut_gains = norm_gains.size
     cut_rows = cut_gains + bias_rows.size
 
@@ -267,26 +355,142 @@
     )
     bias = jnp.where(allowed, 0.0, masked_bias)
 
+    joined = {}
+    downs = {}
+    for layer in range(1, layers):
+        begin(
+            gather_steps(beside_each_other(layer), False),
+            functools.partial(joined.__setitem__, layer),
+        )
+    bit = groups // 2
+    while bit > 1:
+        my_tokens = advance(my_tokens)
+        bit //= 2
     hidden = my_tokens.astype(single) + my_time
     saved = []
     for layer in range(layers):
-        rows = (all_gains[layer], all_offsets[layer], all_up_bias[layer])
-        hidden, kept = layer_forward(hidden, matrices[layer], rows, bias)
-        saved.append(kept)
+        if layer:
+            matrices[layer] = split_matrices(joined[layer]) + [None]
+        qkv_full, out_full, up_full, down_full = matrices[layer]
+        gains, offsets = all_gains[layer], all_offsets[layer]
+        before = hidden
+        normed = layer_norm(hidden, gains[0], offsets[0]).astype(half)
+        shift = jnp.concatenate([offsets[1], jnp.zeros_like(offsets[1]), offsets[2]])
+        packed = (contract(normed, qkv_full, 1, 0) + shift).astype(half)
+        if layer:
+            packed = advance(packed)
+        attended, totals = attend_forward(packed, bias)
+        attended = advance(attended)
+        if layer == 0:
+            for later in range(1, layers):
+                begin(
+                    gather_steps(down_weight[later], True),
+                    functools.partial(downs.__setitem__, later),
+                )
+            attended, out_grad = lax.optimization_barrier((attended, out_grad))
+            my_upstream = whole_sequence(out_grad)
+        middle = hidden + (contract(attended, out_full, 1, 0) + offsets[3])
+        second = layer_norm(middle, gains[1], offsets[4]).astype(half)
+        if layer:
+            second = advance(second)
+        pre_activation = contract(second, up_full, 1, 0) + all_up_bias[layer]
+        activated = jax.nn.gelu(pre_activation, approximate=True).astype(half)
+        activated = advance(activated)
+        if layer:
+            while layer not in downs:
+                activated = advance(activated)
+            matrices[layer][3] = down_full = downs[layer]
+        hidden = middle + (contract(activated, down_full, 1, 0) + offsets[5])
+        if layer < layers - 1:
+            while layer + 1 not in joined:
+                hidden = advance(hidden)
+            hidden = advance(hidden)
+        saved.append(
+            (before, normed, packed, totals, attended, middle, second, pre_activation, activated)
+        )
 
     def split_back(result):
         parts = result.reshape(2, -1, features).astype(half)
         return lax.all_to_all(parts, "seq", split_axis=0, concat_axis=0, tiled=True)
 
-    output = split_back(hidden).astype(single)
-
-    def scatter(term):
-        share = lax.psum_scatter(term.astype(half), "wide", scatter_dimension=0, tiled=True)
-        other = lax.ppermute(share, "seq", swap)
-        return share.astype(single) + other.astype(single)
+    output = split_back(hidden)
+
+    def column_half(array, which):
+        count = array.shape[1] // 2
+        return lax.dynamic_slice_in_dim(array, which * count, count, axis=1)
+
+    def total_of(addends):
+        return functools.reduce(jnp.add, [addend.astype(single) for addend in addends])
+
+    def owner_blocks(array):
+        pieces = array.shape[0] // (groups * row_unit)
+        array = array.reshape(groups // 2, 2, pieces, row_unit, array.shape[1])
+        return [array[:, :, piece] for piece in range(pieces)]
+
+    def reduce_group(terms):
+        sent = [contract(left, column_half(right, 1 - core), 0, 0).astype(half) for left, right in terms]
+        sent = [lax.ppermute(part, "wide", pair_up(1)) for part in sent]
+        kept = [contract(left, column_half(right, core), 0, 0).astype(half) for left, right in terms]
+        arrived = yield sent
+        counts, blocks = [], ([], [])
+        for own, other in zip(kept, arrived):
+            own_blocks, other_blocks = owner_blocks(own), owner_blocks(other)
+            counts.append((len(own_blocks), own.shape[1]))
+            for pair in zip(own_blocks, other_blocks):
+                for side in range(2):
+                    which = place if side == 0 else 1 - place
+                    chosen = [side_of(part, which, 1) for part in pair]
+                    blocks[side].append(total_of(chosen).astype(half))
+        (received,) = yield [lax.ppermute(jnp.concatenate(blocks[1], axis=-1), "seq", swap)]
+        addends = [jnp.concatenate(blocks[0], axis=-1), received]
+        width = received.shape[-1]
+        bit = 2
+        while bit < groups:
+            views = [addend.reshape(-1, 2, row_unit, width) for addend in addends]
+            mine = bit_of(bit)
+            sent = total_of([side_of(view, 1 - mine, 1) for view in views]).astype(half)
+            (received,) = yield [lax.ppermute(sent, "wide", pair_up(bit))]
+            addends = [side_of(view, mine, 1) for view in views] + [received]
+            bit *= 2
+        current = total_of(addends).astype(half).reshape(row_unit, width)
+        (other,) = yield [lax.ppermute(current, "seq", swap)]
+        same = place == core
+        owned = jnp.where(same, current, other)
+        (received,) = yield [lax.ppermute(jnp.where(same, other, current), "wide", pair_up(1))]
+        low = jnp.where(core == 0, owned, received)
+        high = jnp.where(core == 0, received, owned)
+        shares, start = [], 0
+        for count, each in counts:
+            rows = []
+            for _ in range(count):
+                window = slice(start, start + each)
+                rows.append(jnp.concatenate([low[:, window], high[:, window]], axis=1))
+                start += each
+            shares.append(jnp.concatenate(rows, axis=0).astype(single))
+        return shares
+
+    def reduce_small(array):
+        bit = 1
+        while bit < groups:
+            view = array.reshape(-1, 2, array.shape[-1])
+            mine = bit_of(bit)
+            sent = side_of(view, 1 - mine, 1)
+            (received,) = yield [lax.ppermute(sent, "wide", pair_up(bit))]
+            array = side_of(view, mine, 1) + received
+            bit *= 2
+        (received,) = yield [lax.ppermute(array, "seq", swap)]
+        return (array + received)[0]
+
+    weight_grads = [[None] * 4 for _ in range(layers)]
+
+    def begin_group(layer, parts, terms):
+        def finish(shares):
+            for part, share in zip(parts, shares):
+                weight_grads[layer][part] = share
+
+        begin(reduce_group(terms), finish)
 
     gradient = my_upstream.astype(single)
-    weight_grads = [None] * layers
     small_grads = [None] * layers
     for layer in range(layers - 1, -1, -1):
         qkv_full, out_full, up_full, down_full = matrices[layer]
@@ -295,27 +499,39 @@
             saved[layer]
         )
         branch = gradient.astype(half)
-        down_share = scatter(contract(activated, branch, 0, 0))
         down_bias_grad = jnp.sum(branch, axis=0, dtype=single)
         activated_grad = contract(branch, down_full, 1, 1)
         pull = jax.vjp(lambda value: jax.nn.gelu(value, approximate=True), pre_activation)[1]
         upper = pull(activated_grad)[0].astype(half)
-        up_share = scatter(contract(second, upper, 0, 0))
+        upper = advance(upper)
+        first_batch = ((3, 2), ((activated, branch), (second, upper)))
+        if layer:
+            begin_group(layer, *first_batch)
         up_bias_grad = jnp.sum(upper, axis=0, dtype=single)
         second_grad = contract(upper, up_full, 1, 1)
         middle_part, second_gain, second_offset = layer_norm_grad(middle, gains[1], second_grad)
         middle_grad = gradient + middle_part
         attention_grad = middle_grad.astype(half)
-        out_share = scatter(contract(attended, attention_grad, 0, 0))
         out_bias_grad = jnp.sum(attention_grad, axis=0, dtype=single)
+        attention_grad = advance(attention_grad)
+        if not layer:
+            begin_group(layer, (3, 2, 1), first_batch[1] + ((attended, attention_grad),))
         upstream = contract(attention_grad, out_full, 1, 1).astype(half)
+        if not layer:
+            upstream = advance(upstream)
+        if layer == layers - 1:
+            upstream, output = lax.optimization_barrier((upstream, output))
+            output = output.astype(single)
         packed_grad = attend_backward(packed, bias, upstream, totals, attended)
-        qkv_share = scatter(contract(normed, packed_grad, 0, 0))
+        packed_grad = advance(packed_grad)
+        if layer:
+            begin_group(layer, (0, 1), ((normed, packed_grad), (attended, attention_grad)))
+        else:
+            begin_group(layer, (0,), ((normed, packed_grad),))
         column_sums = jnp.sum(packed_grad, axis=0, dtype=single)
         normed_grad = contract(packed_grad, qkv_full, 1, 1)
         hidden_part, first_gain, first_offset = layer_norm_grad(hidden, gains[0], normed_grad)
-        gradient = middle_grad + hidden_part
-        weight_grads[layer] = (qkv_share, out_share, up_share, down_share)
+        gradient = advance(middle_grad + hidden_part)
         small_grads[layer] = (
             jnp.stack([first_gain, second_gain]),
             jnp.stack(
@@ -330,8 +546,6 @@
             ),
             up_bias_grad,
         )
-    input_grad = split_back(gradient).astype(single)
-
     def by_owner(parts):
         stacked = jnp.stack(parts)
         stacked = stacked.reshape(layers, -1, groups, stacked.shape[-1] // groups)
@@ -341,8 +555,13 @@
         [by_owner([small_grads[layer][part] for layer in range(layers)]) for part in range(3)],
         axis=1,
     )
-    owned = lax.psum_scatter(owned, "wide", scatter_dimension=0, tiled=True)[0]
-    owned = owned + lax.ppermute(owned, "seq", swap)
+    small_result = []
+    begin(reduce_small(owned), small_result.append)
+    input_grad = split_back(gradient)
+    while running:
+        input_grad = advance(input_grad)
+    input_grad = input_grad.astype(single)
+    owned = small_result[0]
     stacked = [
         jnp.stack([weight_grads[layer][part] for layer in range(layers)]) for part in range(4)
     ]

time: 1200 us -> 1450 us (1.21)
  Pallas kernels: 125 us -> 752 us
  waiting for transfers between devices: 717 us -> 201 us
  other arithmetic: 38.1 us -> 110 us
  local copies, waits for them, and re-layouts: 27 us -> 79.2 us
  starting transfers between devices: 32 us -> 67.4 us
  blocking collectives: 22.4 us -> 0 us
    pallas_call x0 -> x8, Pallas kernels: none -> 627 us  [place_pieces(): pl.pallas_call(kernel, in_specs=[pl.BlockSpec(memory_space=pltpu.SMEM)] +...]
    reduce_scatter x8 -> x0, waiting for transfers between devices: 446 us -> none  [scatter(): lax.psum_scatter(term.astype(half), 'wide', scatter_dimension=0, tiled=True)]
    all_gather x8 -> x2, waiting for transfers between devices: 195 us -> 0.04 us  [the longest x1 0.02 us: per_device(): lax.all_gather(beside_each_other(0, side), 'wide', axis=0, tiled=True)]
    ppermute x9 -> x49, waiting for transfers between devices: 23.5 us -> 171 us  [the longest x6 76.8 us: gather_steps(): received, = (yield [lax.ppermute(current, 'wide', pair_up(bit))])]
    ppermute x9 -> x49, starting transfers between devices: 12.4 us -> 47.5 us  [the longest x12 16.9 us: reduce_group(): received, = (yield [lax.ppermute(sent, 'wide', pair_up(bit))])]
    convert_element_type x4 -> x30, other arithmetic: 10.1 us -> 37.3 us  [the longest x12 18.1 us: reduce_group(): sent = total_of([side_of(view, 1 - mine, 1) for view in views]).astype(half)]
    all_gather x1 -> x0, blocking collectives: 22.4 us -> none  [per_device(): small_whole = lax.all_gather(small, 'wide', axis=0, tiled=False)]
    all_to_all x3, waiting for transfers between devices: 34.9 us -> 16.3 us  [whole_sequence(): lax.all_to_all(part, 'seq', split_axis=0, concat_axis=1, tiled=True)[0]]
  transfers between devices with their start and end apart: 31 -> 56, of which waited for: 19 -> 22; matrix products, arithmetic and copies ran while one was open for 17% -> 19% of each run, Pallas kernels for 7% -> 38%
where the time goes in v3:
time: 1450 us; the launch traced here: 1440 us
  Pallas kernels  752 us (52%)
  matrix products  213 us (15%)
  waiting for transfers between devices  201 us (14%)
  other arithmetic  110 us (8%)
  local copies, waits for them, and re-layouts  79.2 us (5%)
  starting transfers between devices  67.4 us (5%)
  between operations  16.7 us (1%)
    pallas_call x8, Pallas kernels, place_pieces(): pl.pallas_call(kernel, in_specs=[pl.BlockSpec(memory_space=pltpu.SMEM)] +...  627 us
    dot_general x32, matrix products, contract(): lax.dot_general(left, right, (((left_dim,), (right_dim,)), ((), ())), pre...  213 us
    ppermute x6, waiting for transfers between devices, gather_steps(): received, = (yield [lax.ppermute(current, 'wide', pair_up(bit))])  76.8 us
    pallas_call x2, Pallas kernels, attend_backward(): pl.pallas_call(functools.partial(attend_grad_kernel, rows=BACKWARD_ROWS),...  74.2 us
    ppermute x12, waiting for transfers between devices, reduce_group(): received, = (yield [lax.ppermute(sent, 'wide', pair_up(bit))])  57.3 us
    pallas_call x2, Pallas kernels, attend_forward(): pl.pallas_call(functools.partial(attend_kernel, rows=FORWARD_ROWS), grid=...  50.8 us
  transfers between devices with their start and end apart: 56, of which 22 were waited for; matrix products, arithmetic and copies ran while one was open for 19% of the time, Pallas kernels for 38%

profile of v3, /device:TPU:0, one launch (start us, length us, event | category | flops | bytes accessed | tf_op | source)
XLA Modules:
  0.0 1438.9 jit_solution(6318859471804920290)
XLA Ops:
  13.7 4.2 all-to-all-start
  21.8 16.3 %all-to-all-done = bf16[2,512,768]{2,1,0:T(8,128)(2,1)S(1)} async-done(((bf16[2,512,768]{2,1,0:T(8,128)(2,1)}), bf16[2,512,768]{2,1,0:T(8,128)(2,1)S(1)}, u32[]{:S(2)}, u32[]{:S(2)}) %all-to-all-start) | async-done | bytes 1572896 | tf_op jit(solution)/shard_map/all_to_all | solution.py:243
  38.9 9.7 collective-permute-done.refs_1_
  48.6 19.0 %place_pieces.8 = bf16[1,2,48,3072]{3,2,1,0:T(8,128)(2,1)} custom-call(s32[1]{0:T(128)} %bitcast.5.index_ref, bf16[1,48,3072]{2,1,0:T(8,128)(2,1)} %copy-done.50, bf16[1,48,3072]{2,1,0:T(8,128)(2,1)} %collective-permute-done.refs_1_), custom_call_target="tpu_custom_call" | custom-call | bytes 1179648 | tf_op jit(solution)/shard_map/place_pieces/pallas_call | solution.py:192
  69.9 42.6 %collective-permute-done.1.refs_1_ = bf16[2,48,3072]{2,1,0:T(8,128)(2,1)S(1)} collective-permute-done((bf16[2,48,3072]{2,1,0:T(8,128)(2,1)}, bf16[2,48,3072]{2,1,0:T(8,128)(2,1)S(1)}, u32[]{:S(2)}, u32[]{:S(2)}) %collective-permute-start.1) | collective-permute-done | bytes 589856 | tf_op jit(solution)/shard_map/ppermute | solution.py:282
  113.4 36.9 %place_pieces.9 = bf16[2,2,48,3072]{3,2,1,0:T(8,128)(2,1)} custom-call(s32[1]{0:T(128)} %bitcast.7.index_ref, bf16[2,48,3072]{2,1,0:T(8,128)(2,1)} %bitcast.415, bf16[2,48,3072]{2,1,0:T(8,128)(2,1)} %copy-done.52), custom_call_target="tpu_custom_call" | custom-call | bytes 2359296 | tf_op jit(solution)/shard_map/place_pieces/pallas_call | solution.py:192
  162.4 19.2 %collective-permute-done.2.refs_1_ = bf16[4,48,3072]{2,1,0:T(8,128)(2,1)S(1)} collective-permute-done((bf16[4,48,3072]{2,1,0:T(8,128)(2,1)}, bf16[4,48,3072]{2,1,0:T(8,128)(2,1)S(1)}, u32[]{:S(2)}, u32[]{:S(2)}) %collective-permute-start.2) | collective-permute-done | bytes 1179680 | tf_op jit(solution)/shard_map/ppermute | solution.py:282
  182.6 72.6 %place_pieces.10 = bf16[4,2,48,3072]{3,2,1,0:T(8,128)(2,1)} custom-call(s32[1]{0:T(128)} %bitcast.16.index_ref, bf16[4,48,3072]{2,1,0:T(8,128)(2,1)} %bitcast.393, bf16[4,48,3072]{2,1,0:T(8,128)(2,1)} %copy-done.46), custom_call_target="tpu_custom_call" | custom-call | bytes 4718592 | tf_op jit(solution)/shard_map/place_pieces/pallas_call | solution.py:192
  260.3 7.9 add_convert_fusion.1.query_ref.key_ref.value_ref
  268.3 25.2 %attend_forward.2 = (bf16[1024,768]{1,0:T(8,128)(2,1)}, f32[6,2,1024]{2,1,0:T(2,128)}) custom-call(bf16[1024,2304]{1,0:T(8,128)(2,1)} %add_convert_fusion.1.query_ref.key_ref.value_ref, bf16[1024,2304]{1,0:T(8,128)(2,1)} %add_convert_fusion.1.query_ref.key_ref.value_ref, bf16[1024,2304]{1,0:T(8,128)(2,1)} %add_convert_fusion.1.query_ref.key_ref.value_ref, ...), custom_call_target="tpu_custom_call" | custom-call | flops 12884901888 | bytes 6291456 | tf_op jit(solution)/shard_map/attend_forward/pallas_call | solution.py:62
  293.5 14.5 %collective-permute-done.3.refs_1_ = bf16[8,48,3072]{2,1,0:T(8,128)(2,1)} collective-permute-done((bf16[8,48,3072]{2,1,0:T(8,128)(2,1)}, bf16[8,48,3072]{2,1,0:T(8,128)(2,1)}, u32[]{:S(2)}, u32[]{:S(2)}) %collective-permute-start.3) | collective-permute-done | bytes 2359328 | tf_op jit(solution)/shard_map/ppermute | solution.py:291
  317.9 15.3 %multiply_convert_fusion.1 = (bf16[1024,3072]{1,0:T(8,128)(2,1)}, f32[1024,3072]{1,0:T(8,128)}) fusion(f32[3072]{0:T(1024)S(1)} %add.985, bf16[1024,768]{0,1:T(8,128)(2,1)S(1)} %add_convert_fusion.5, bf16[768,6272]{1,0:T(8,128)(2,1)} %all-gather.4.cloned.1.call-done), kind=kOutput, calls=%fused_computation.21 | convolution fusion | flops 4863295488 | bytes 25178112 | tf_op jit(solution)/shard_map/dot_general | solution.py:22
  336.6 10.1 place_pieces.11
  346.8 9.1 add_add_fusion.1
  355.9 287.7 %place_pieces.12 = bf16[8,2,48,6144]{3,2,1,0:T(8,128)(2,1)} custom-call(s32[2]{0:T(128)} %pad_add_fusion.1.index_ref, bf16[8,48,3072]{2,1,0:T(8,128)(2,1)} %bitcast.376, bf16[8,48,3072]{2,1,0:T(8,128)(2,1)} %collective-permute-done.3.refs_1_, bf16[8,48,3072]{2,1,0:T(8,128)(2,1)} %collective-permute-done.4.refs_2_, ...), custom_call_target="tpu_custom_call" | custom-call | bytes 18874368 | tf_op jit(solution)/shard_map/place_pieces/pallas_call | solution.py:192
  644.3 19.0 %place_pieces.13 = bf16[2,2,96,768]{3,2,1,0:T(8,128)(2,1)} custom-call(s32[1]{0:T(128)} %bitcast.7.index_ref, bf16[2,96,768]{2,1,0:T(8,128)(2,1)} %bitcast.452, bf16[2,96,768]{2,1,0:T(8,128)(2,1)} %copy-done.71), custom_call_target="tpu_custom_call" | custom-call | bytes 1179648 | tf_op jit(solution)/shard_map/place_pieces/pallas_call | solution.py:192
  666.0 8.1 add_convert_fusion.query_ref.key_ref.value_ref
  674.1 5.3 collective-permute-done.8.refs_1_
  679.4 36.9 %place_pieces.14 = bf16[4,2,96,768]{3,2,1,0:T(8,128)(2,1)} custom-call(s32[1]{0:T(128)} %bitcast.16.index_ref, bf16[4,96,768]{2,1,0:T(8,128)(2,1)} %bitcast.413, bf16[4,96,768]{2,1,0:T(8,128)(2,1)} %collective-permute-done.8.refs_1_), custom_call_target="tpu_custom_call" | custom-call | bytes 2359296 | tf_op jit(solution)/shard_map/place_pieces/pallas_call | solution.py:192
  718.1 25.6 %attend_forward.3 = (bf16[1024,768]{1,0:T(8,128)(2,1)}, f32[6,2,1024]{2,1,0:T(2,128)}) custom-call(bf16[1024,2304]{1,0:T(8,128)(2,1)} %add_convert_fusion.query_ref.key_ref.value_ref, bf16[1024,2304]{1,0:T(8,128)(2,1)} %add_convert_fusion.query_ref.key_ref.value_ref, bf16[1024,2304]{1,0:T(8,128)(2,1)} %add_convert_fusion.query_ref.key_ref.value_ref, ...), custom_call_target="tpu_custom_call" | custom-call | flops 12884901888 | bytes 6291456 | tf_op jit(solution)/shard_map/attend_forward/pallas_call | solution.py:62
  750.7 144.7 %place_pieces.15 = bf16[8,2,2,96,768]{4,3,2,1,0:T(8,128)(2,1)} custom-call(s32[2]{0:T(128)} %pad_add_fusion.1.index_ref, bf16[8,96,768]{2,1,0:T(8,128)(2,1)} %bitcast.391, bf16[8,96,768]{2,1,0:T(8,128)(2,1)} %copy-done.44, bf16[8,96,768]{2,1,0:T(8,128)(2,1)} %copy-done.45, bf16[8,96,768]{2,1,0:T(8,128)(2,1)} %collective-permute-done.11.refs_3_), custom_call_target="tpu_custom_call" | custom-call | bytes 9437184 | tf_op jit(solution)/shard_map/place_pieces/pallas_call | solution.py:192
  895.5 14.8 %multiply_convert_fusion = (bf16[1024,3072]{1,0:T(8,128)(2,1)}, f32[1024,3072]{1,0:T(8,128)}) fusion(f32[3072]{0:T(1024)S(1)} %add.1008, bf16[1024,768]{0,1:T(8,128)(2,1)S(1)} %add_convert_fusion.3, bf16[768,6144]{1,0:T(8,128)(2,1)} %bitcast.368), kind=kOutput, calls=%fused_computation.20 | convolution fusion | flops 4863295488 | bytes 25178112 | tf_op jit(solution)/shard_map/dot_general | solution.py:22
  910.3 16.5 %convert_reduce_fusion = (f32[3072]{0:T(1024)S(1)}, bf16[1024,3072]{1,0:T(8,128)(2,1)}) fusion(f32[1024,3072]{1,0:T(8,128)} %get-tuple-element.315, f32[3072]{0:T(1024)S(1)} %add.1008, bf16[1024,768]{1,0:T(8,128)(2,1)S(1)} %bitcast.365, bf16[3072,768]{1,0:T(8,128)(2,1)S(1)} %bitcast.401), kind=kOutput, calls=%fused_computation.18 | convolution fusion | flops 4904186880 | bytes 25190400 | tf_op jit(solution)/shard_map/dot_general | solution.py:22
  926.8 9.0 fusion.153
  939.8 4.8 convolution_convert_fusion.3
  951.8 9.7 add_convert_fusion.2
  964.1 4.7 all-to-all-start.3
  969.4 4.9 convert_reduce_fusion.5
  976.3 6.4 convolution_convert_fusion.2
  984.2 5.1 convolution_convert_fusion.6
  1017.5 37.0 %attend_backward.2 = bf16[1024,2304]{1,0:T(8,128)(2,1)} custom-call(bf16[1024,2304]{1,0:T(8,128)(2,1)} %add_convert_fusion.query_ref.key_ref.value_ref, bf16[1024,2304]{1,0:T(8,128)(2,1)} %add_convert_fusion.query_ref.key_ref.value_ref, bf16[1024,2304]{1,0:T(8,128)(2,1)} %add_convert_fusion.query_ref.key_ref.value_ref, f32[1024,1024]{1,0:T(8,128)} %fusion.20.bias_ref, ...), custom_call_target="tpu_custom_call" | custom-call | flops 32212254720 | bytes 12582912 | tf_op jit(solution)/shard_map/attend_backward/pallas_call | solution.py:149
  1054.6 10.4 fusion.152
  1079.4 5.5 multiply_add_fusion.2
  1089.0 4.0 convolution_convert_fusion.10
  1093.0 5.6 collective-permute-done.15
  1101.0 8.0 convolution_convert_fusion
  1109.1 4.9 convolution_convert_fusion.1
  1122.4 17.3 %fusion.6 = bf16[1024,3072]{1,0:T(8,128)(2,1)} fusion(f32[1024,3072]{1,0:T(8,128)} %get-tuple-element.311, f32[3072]{0:T(1024)S(1)} %copy-done.110, bf16[1024,768]{0,1:T(8,128)(2,1)S(1)} %get-tuple-element.236, bf16[1,3072,768]{2,1,0:T(8,128)(2,1)S(1)} %bitcast.472), kind=kOutput, calls=%fused_computation.10 | convolution fusion | flops 4897898496 | bytes 25178112 | tf_op jit(solution)/shard_map/dot_general | solution.py:22
  1145.1 5.4 convolution_convert_fusion.5
  1162.9 9.1 fusion.155
  1216.4 37.2 %attend_backward.3 = bf16[1024,2304]{1,0:T(8,128)(2,1)} custom-call(bf16[1024,2304]{1,0:T(8,128)(2,1)} %add_convert_fusion.1.query_ref.key_ref.value_ref, bf16[1024,2304]{1,0:T(8,128)(2,1)} %add_convert_fusion.1.query_ref.key_ref.value_ref, bf16[1024,2304]{1,0:T(8,128)(2,1)} %add_convert_fusion.1.query_ref.key_ref.value_ref, f32[1024,1024]{1,0:T(8,128)} %fusion.20.bias_ref, ...), custom_call_target="tpu_custom_call" | custom-call | flops 32212254720 | bytes 12582912 | tf_op jit(solution)/shard_map/attend_backward/pallas_call | solution.py:149
  1254.9 17.1 %collective-permute-done.29 = bf16[8,48,3456]{2,1,0:T(8,128)(2,1)} collective-permute-done((bf16[8,48,3456]{2,1,0:T(8,128)(2,1)}, bf16[8,48,3456]{2,1,0:T(8,128)(2,1)}, u32[]{:S(2)}, u32[]{:S(2)}) %collective-permute-start.29) | collective-permute-done | bytes 2654240 | tf_op jit(solution)/shard_map/ppermute | solution.py:444
  1284.1 7.5 fusion.154
  1317.2 17.6 %collective-permute-done.31 = bf16[4,48,3456]{2,1,0:T(8,128)(2,1)S(1)} collective-permute-done((bf16[4,48,3456]{2,1,0:T(8,128)(2,1)}, bf16[4,48,3456]{2,1,0:T(8,128)(2,1)S(1)}, u32[]{:S(2)}, u32[]{:S(2)}) %collective-permute-start.31) | collective-permute-done | bytes 1327136 | tf_op jit(solution)/shard_map/ppermute | solution.py:452
  1348.9 12.0 collective-permute-done.34
  1360.8 13.4 all-to-all-done.4
  1384.9 11.9 collective-permute-done.37
  1413.1 6.1 collective-permute-done.44
  (617 shorter events, 286.5 us)
Async XLA Ops:
  7.2 250.7 %all-gather.4.cloned.1.call-start = ((), (), s32[]{:S(2)}) async-start(), calls=%async_computation.5 | async-start | bytes 10235904 | tf_op jit(solution)/shard_map/all_gather | solution.py:335
  13.7 24.4 %all-to-all-start = ((bf16[2,512,768]{2,1,0:T(8,128)(2,1)}), bf16[2,512,768]{2,1,0:T(8,128)(2,1)S(1)}, u32[]{:S(2)}, u32[]{:S(2)}) async-start(bf16[2,512,768]{2,1,0:T(8,128)(2,1)} %param.12), calls=%async_computation | async-start | bytes 3145728 | tf_op jit(solution)/shard_map/all_to_all | solution.py:243
  18.2 30.3 %collective-permute-start = (bf16[1,48,3072]{2,1,0:T(8,128)(2,1)S(1)}, bf16[1,48,3072]{2,1,0:T(8,128)(2,1)}, u32[]{:S(2)}, u32[]{:S(2)}) collective-permute-start(bf16[1,48,3072]{2,1,0:T(8,128)(2,1)S(1)} %fusion.107.refs_0_), channel_id=1, source_target_pairs={{0,16},{2,18},{4,20},{6,22},{8,24},{10,26},{12,28},{14,30},{16,0},... | collective-permute-start | bytes 884744 | tf_op jit(solution)/shard_map/ppermute | solution.py:282
  67.6 45.0 %collective-permute-start.1 = (bf16[2,48,3072]{2,1,0:T(8,128)(2,1)}, bf16[2,48,3072]{2,1,0:T(8,128)(2,1)S(1)}, u32[]{:S(2)}, u32[]{:S(2)}) collective-permute-start(bf16[2,48,3072]{2,1,0:T(8,128)(2,1)} %bitcast.414), channel_id=1, source_target_pairs={{0,8},{2,10},{4,12},{6,14},{8,0},{10,2},{12,4},{14,6},{16,24},{18,... | collective-permute-start | bytes 1769480 | tf_op jit(solution)/shard_map/ppermute | solution.py:282
  150.2 31.3 %collective-permute-start.2 = (bf16[4,48,3072]{2,1,0:T(8,128)(2,1)}, bf16[4,48,3072]{2,1,0:T(8,128)(2,1)S(1)}, u32[]{:S(2)}, u32[]{:S(2)}) collective-permute-start(bf16[4,48,3072]{2,1,0:T(8,128)(2,1)} %bitcast.392), channel_id=1, source_target_pairs={{0,4},{2,6},{4,0},{6,2},{8,12},{10,14},{12,8},{14,10},{16,20},{18,... | collective-permute-start | bytes 3538952 | tf_op jit(solution)/shard_map/ppermute | solution.py:282
  152.4 7.2 all-to-all-start.1
  155.6 191.1 %all-gather.6.cloned.1.call-start = ((), (), s32[]{:S(2)}) async-start(), calls=%async_computation.6 | async-start | bytes 5013504 | tf_op jit(solution)/shard_map/all_gather | solution.py:336
  157.5 178.4 %collective-permute-start.6 = (bf16[1,96,768]{2,1,0:T(8,128)(2,1)S(1)}, bf16[1,96,768]{2,1,0:T(8,128)(2,1)S(1)}, u32[]{:S(2)}, u32[]{:S(2)}) collective-permute-start(bf16[1,96,768]{2,1,0:T(8,128)(2,1)S(1)} %constant_dynamic-slice_fusion.15.refs_0_), channel_id=1, source_target_pairs={{0,16},{2,18},{4,20},{6,22},{8,24},{10,26},{12,28},{14,30},{16,0},... | collective-permute-start | bytes 442376 | tf_op jit(solution)/shard_map/ppermute | solution.py:282
  255.2 52.8 %collective-permute-start.3 = (bf16[8,48,3072]{2,1,0:T(8,128)(2,1)}, bf16[8,48,3072]{2,1,0:T(8,128)(2,1)}, u32[]{:S(2)}, u32[]{:S(2)}) collective-permute-start(bf16[8,48,3072]{2,1,0:T(8,128)(2,1)} %bitcast.374), channel_id=1, source_target_pairs={{0,1},{1,0},{2,3},{3,2},{4,5},{5,4},{6,7},{7,6},{8,9},{9,8},{10,11... | collective-permute-start | bytes 7077896 | tf_op jit(solution)/shard_map/ppermute | solution.py:291
  256.9 79.1 %collective-permute-start.4 = (bf16[8,48,3072]{2,1,0:T(8,128)(2,1)}, bf16[8,48,3072]{2,1,0:T(8,128)(2,1)}, u32[]{:S(2)}, u32[]{:S(2)}) collective-permute-start(bf16[8,48,3072]{2,1,0:T(8,128)(2,1)} %bitcast.375), channel_id=1, source_target_pairs={{0,2},{2,0},{4,6},{6,4},{8,10},{10,8},{12,14},{14,12},{16,18},{18,... | collective-permute-start | bytes 7077896 | tf_op jit(solution)/shard_map/ppermute | solution.py:292
  308.3 27.7 %collective-permute-start.5 = (bf16[8,48,3072]{2,1,0:T(8,128)(2,1)}, bf16[8,48,3072]{2,1,0:T(8,128)(2,1)}, u32[]{:S(2)}, u32[]{:S(2)}) collective-permute-start(bf16[8,48,3072]{2,1,0:T(8,128)(2,1)} %collective-permute-done.3.refs_1_), channel_id=1, source_target_pairs={{0,2},{2,0},{4,6},{6,4},{8,10},{10,8},{12,14},{14,12},{16,18},{18,... | collective-permute-start | bytes 7077896 | tf_op jit(solution)/shard_map/ppermute | solution.py:292
  308.3 25.0 %all-to-all-start.2 = ((bf16[2,512,768]{2,1,0:T(8,128)(2,1)}), bf16[2,512,768]{2,1,0:T(8,128)(2,1)S(1)}, u32[]{:S(2)}, u32[]{:S(2)}) async-start(bf16[2,512,768]{2,1,0:T(8,128)(2,1)} %param.16), calls=%async_computation.2 | async-start | bytes 3145728 | tf_op jit(solution)/shard_map/all_to_all | solution.py:243
  346.7 296.9 %collective-permute-start.7 = (bf16[2,96,768]{2,1,0:T(8,128)(2,1)}, bf16[2,96,768]{2,1,0:T(8,128)(2,1)S(1)}, u32[]{:S(2)}, u32[]{:S(2)}) collective-permute-start(bf16[2,96,768]{2,1,0:T(8,128)(2,1)} %bitcast.451), channel_id=1, source_target_pairs={{0,8},{2,10},{4,12},{6,14},{8,0},{10,2},{12,4},{14,6},{16,24},{18,... | collective-permute-start | bytes 884744 | tf_op jit(solution)/shard_map/ppermute | solution.py:282
  663.3 16.1 %collective-permute-start.8 = (bf16[4,96,768]{2,1,0:T(8,128)(2,1)}, bf16[4,96,768]{2,1,0:T(8,128)(2,1)}, u32[]{:S(2)}, u32[]{:S(2)}) collective-permute-start(bf16[4,96,768]{2,1,0:T(8,128)(2,1)} %bitcast.412), channel_id=1, source_target_pairs={{0,4},{2,6},{4,0},{6,2},{8,12},{10,14},{12,8},{14,10},{16,20},{18,... | collective-permute-start | bytes 1769480 | tf_op jit(solution)/shard_map/ppermute | solution.py:282
  716.3 27.9 %collective-permute-start.9 = (bf16[8,96,768]{2,1,0:T(8,128)(2,1)}, bf16[8,96,768]{2,1,0:T(8,128)(2,1)S(1)}, u32[]{:S(2)}, u32[]{:S(2)}) collective-permute-start(bf16[8,96,768]{2,1,0:T(8,128)(2,1)} %bitcast.389), channel_id=1, source_target_pairs={{0,1},{1,0},{2,3},{3,2},{4,5},{5,4},{6,7},{7,6},{8,9},{9,8},{10,11... | collective-permute-start | bytes 3538952 | tf_op jit(solution)/shard_map/ppermute | solution.py:291
  718.1 31.6 %collective-permute-start.10 = (bf16[8,96,768]{2,1,0:T(8,128)(2,1)}, bf16[8,96,768]{2,1,0:T(8,128)(2,1)S(1)}, u32[]{:S(2)}, u32[]{:S(2)}) collective-permute-start(bf16[8,96,768]{2,1,0:T(8,128)(2,1)} %bitcast.390), channel_id=1, source_target_pairs={{0,2},{2,0},{4,6},{6,4},{8,10},{10,8},{12,14},{14,12},{16,18},{18,... | collective-permute-start | bytes 3538952 | tf_op jit(solution)/shard_map/ppermute | solution.py:292
  939.7 49.6 %collective-permute-start.13 = (bf16[768,1536]{1,0:T(8,128)(2,1)}, bf16[768,1536]{1,0:T(8,128)(2,1)}, u32[]{:S(2)}, u32[]{:S(2)}) collective-permute-start(bf16[768,1536]{1,0:T(8,128)(2,1)} %convolution_convert_fusion.7), channel_id=1, source_target_pairs={{0,2},{2,0},{4,6},{6,4},{8,10},{10,8},{12,14},{14,12},{16,18},{18,... | collective-permute-start | bytes 7077896 | tf_op jit(solution)/shard_map/ppermute | solution.py:432
  944.6 44.7 %collective-permute-start.12 = (bf16[3072,384]{1,0:T(8,128)(2,1)}, bf16[3072,384]{1,0:T(8,128)(2,1)}, u32[]{:S(2)}, u32[]{:S(2)}) collective-permute-start(bf16[3072,384]{1,0:T(8,128)(2,1)} %convolution_convert_fusion.3), channel_id=1, source_target_pairs={{0,2},{2,0},{4,6},{6,4},{8,10},{10,8},{12,14},{14,12},{16,18},{18,... | collective-permute-start | bytes 7077896 | tf_op jit(solution)/shard_map/ppermute | solution.py:432
  964.1 47.5 %all-to-all-start.3 = ((bf16[2,512,768]{2,1,0:T(8,128)(2,1)}), bf16[2,512,768]{2,1,0:T(8,128)(2,1)}, u32[]{:S(2)}, u32[]{:S(2)}) async-start(bf16[2,512,768]{2,1,0:T(8,128)(2,1)} %bitcast.379), calls=%async_computation.3 | async-start | bytes 3145728 | tf_op jit(solution)/shard_map/all_to_all | solution.py:414
  1000.4 54.2 %collective-permute-start.14 = (bf16[8,48,3072]{2,1,0:T(8,128)(2,1)}, bf16[8,48,3072]{2,1,0:T(8,128)(2,1)S(1)}, u32[]{:S(2)}, u32[]{:S(2)}) collective-permute-start(bf16[8,48,3072]{2,1,0:T(8,128)(2,1)} %fusion.51), channel_id=1, source_target_pairs={{0,1},{1,0},{2,3},{3,2},{4,5},{5,4},{6,7},{7,6},{8,9},{9,8},{10,11... | collective-permute-start | bytes 7077896 | tf_op jit(solution)/shard_map/ppermute | solution.py:444
  1011.6 81.4 %collective-permute-start.17 = (bf16[768,384]{1,0:T(8,128)(2,1)}, bf16[768,384]{1,0:T(8,128)(2,1)}, u32[]{:S(2)}, u32[]{:S(2)}) collective-permute-start(bf16[768,384]{1,0:T(8,128)(2,1)} %convolution_convert_fusion.17), channel_id=1, source_target_pairs={{0,2},{2,0},{4,6},{6,4},{8,10},{10,8},{12,14},{14,12},{16,18},{18,... | collective-permute-start | bytes 1769480 | tf_op jit(solution)/shard_map/ppermute | solution.py:432
  1068.5 30.1 %collective-permute-start.16 = (bf16[768,1152]{1,0:T(8,128)(2,1)}, bf16[768,1152]{1,0:T(8,128)(2,1)}, u32[]{:S(2)}, u32[]{:S(2)}) collective-permute-start(bf16[768,1152]{1,0:T(8,128)(2,1)} %convolution_convert_fusion.11), channel_id=1, source_target_pairs={{0,2},{2,0},{4,6},{6,4},{8,10},{10,8},{12,14},{14,12},{16,18},{18,... | collective-permute-start | bytes 5308424 | tf_op jit(solution)/shard_map/ppermute | solution.py:432
  1070.4 28.2 %collective-permute-start.15 = (bf16[4,48,3072]{2,1,0:T(8,128)(2,1)}, bf16[4,48,3072]{2,1,0:T(8,128)(2,1)}, u32[]{:S(2)}, u32[]{:S(2)}) collective-permute-start(bf16[4,48,3072]{2,1,0:T(8,128)(2,1)} %fusion.52), channel_id=1, source_target_pairs={{0,4},{2,6},{4,0},{6,2},{8,12},{10,14},{12,8},{14,10},{16,20},{18,... | collective-permute-start | bytes 3538952 | tf_op jit(solution)/shard_map/ppermute | solution.py:452
  1117.1 28.0 %collective-permute-start.19 = (bf16[8,48,1536]{2,1,0:T(8,128)(2,1)}, bf16[8,48,1536]{2,1,0:T(8,128)(2,1)}, u32[]{:S(2)}, u32[]{:S(2)}) collective-permute-start(bf16[8,48,1536]{2,1,0:T(8,128)(2,1)} %pad_maximum_fusion), channel_id=1, source_target_pairs={{0,1},{1,0},{2,3},{3,2},{4,5},{5,4},{6,7},{7,6},{8,9},{9,8},{10,11... | collective-permute-start | bytes 3538952 | tf_op jit(solution)/shard_map/ppermute | solution.py:444
  1120.7 24.3 %collective-permute-start.18 = (bf16[2,48,3072]{2,1,0:T(8,128)(2,1)}, bf16[2,48,3072]{2,1,0:T(8,128)(2,1)}, u32[]{:S(2)}, u32[]{:S(2)}) collective-permute-start(bf16[2,48,3072]{2,1,0:T(8,128)(2,1)} %fusion.74), channel_id=1, source_target_pairs={{0,8},{2,10},{4,12},{6,14},{8,0},{10,2},{12,4},{14,6},{16,24},{18,... | collective-permute-start | bytes 1769480 | tf_op jit(solution)/shard_map/ppermute | solution.py:452
  1122.4 79.7 %collective-permute-start.24 = (bf16[3072,384]{1,0:T(8,128)(2,1)}, bf16[3072,384]{1,0:T(8,128)(2,1)}, u32[]{:S(2)}, u32[]{:S(2)}) collective-permute-start(bf16[3072,384]{1,0:T(8,128)(2,1)} %convolution_convert_fusion.1), channel_id=1, source_target_pairs={{0,2},{2,0},{4,6},{6,4},{8,10},{10,8},{12,14},{14,12},{16,18},{18,... | collective-permute-start | bytes 7077896 | tf_op jit(solution)/shard_map/ppermute | solution.py:432
  1156.4 30.5 %collective-permute-start.21 = (bf16[4,48,1536]{2,1,0:T(8,128)(2,1)}, bf16[4,48,1536]{2,1,0:T(8,128)(2,1)}, u32[]{:S(2)}, u32[]{:S(2)}) collective-permute-start(bf16[4,48,1536]{2,1,0:T(8,128)(2,1)} %fusion.75), channel_id=1, source_target_pairs={{0,4},{2,6},{4,0},{6,2},{8,12},{10,14},{12,8},{14,10},{16,20},{18,... | collective-permute-start | bytes 1769480 | tf_op jit(solution)/shard_map/ppermute | solution.py:452
  1159.9 27.0 %collective-permute-start.20 = (bf16[1,48,3072]{2,1,0:T(8,128)(2,1)}, bf16[1,48,3072]{2,1,0:T(8,128)(2,1)S(1)}, u32[]{:S(2)}, u32[]{:S(2)}) collective-permute-start(bf16[1,48,3072]{2,1,0:T(8,128)(2,1)} %fusion.81), channel_id=1, source_target_pairs={{0,16},{2,18},{4,20},{6,22},{8,24},{10,26},{12,28},{14,30},{16,0},... | collective-permute-start | bytes 884744 | tf_op jit(solution)/shard_map/ppermute | solution.py:452
  1179.1 23.1 %collective-permute-start.25 = (bf16[768,1536]{1,0:T(8,128)(2,1)}, bf16[768,1536]{1,0:T(8,128)(2,1)}, u32[]{:S(2)}, u32[]{:S(2)}) collective-permute-start(bf16[768,1536]{1,0:T(8,128)(2,1)} %convolution_convert_fusion.5), channel_id=1, source_target_pairs={{0,2},{2,0},{4,6},{6,4},{8,10},{10,8},{12,14},{14,12},{16,18},{18,... | collective-permute-start | bytes 7077896 | tf_op jit(solution)/shard_map/ppermute | solution.py:432
  1189.4 12.7 collective-permute-start.26
  1190.6 9.5 collective-permute-start.23
  1192.9 9.2 collective-permute-start.22
  1212.8 59.2 %collective-permute-start.29 = (bf16[8,48,3456]{2,1,0:T(8,128)(2,1)}, bf16[8,48,3456]{2,1,0:T(8,128)(2,1)}, u32[]{:S(2)}, u32[]{:S(2)}) collective-permute-start(bf16[8,48,3456]{2,1,0:T(8,128)(2,1)} %fusion.103), channel_id=1, source_target_pairs={{0,1},{1,0},{2,3},{3,2},{4,5},{5,4},{6,7},{7,6},{8,9},{9,8},{10,11... | collective-permute-start | bytes 7962632 | tf_op jit(solution)/shard_map/ppermute | solution.py:444
  1215.1 39.7 %collective-permute-start.28 = (bf16[1,48,1536]{2,1,0:T(8,128)(2,1)S(1)}, bf16[1,48,1536]{2,1,0:T(8,128)(2,1)S(1)}, u32[]{:S(2)}, u32[]{:S(2)}) collective-permute-start(bf16[1,48,1536]{2,1,0:T(8,128)(2,1)S(1)} %fusion.110), channel_id=1, source_target_pairs={{0,16},{2,18},{4,20},{6,22},{8,24},{10,26},{12,28},{14,30},{16,0},... | collective-permute-start | bytes 442376 | tf_op jit(solution)/shard_map/ppermute | solution.py:452
  1216.0 38.8 %collective-permute-start.27 = (bf16[48,3072]{1,0:T(8,128)(2,1)S(1)}, bf16[48,3072]{1,0:T(8,128)(2,1)S(1)}, u32[]{:S(2)}, u32[]{:S(2)}) collective-permute-start(bf16[48,3072]{1,0:T(8,128)(2,1)S(1)} %broadcast_select_fusion.7), channel_id=1, source_target_pairs={{0,2},{2,0},{4,6},{6,4},{8,10},{10,8},{12,14},{14,12},{16,18},{18,... | collective-permute-start | bytes 884744 | tf_op jit(solution)/shard_map/ppermute | solution.py:459
  1303.0 44.9 %collective-permute-start.36 = (f32[8,1152]{1,0:T(8,128)}, f32[8,1152]{1,0:T(8,128)S(1)}, u32[]{:S(2)}, u32[]{:S(2)}) collective-permute-start(f32[8,1152]{1,0:T(8,128)} %bitcast.357), channel_id=1, source_target_pairs={{0,2},{2,0},{4,6},{6,4},{8,10},{10,8},{12,14},{14,12},{16,18},{18,... | collective-permute-start | bytes 110600 | tf_op jit(solution)/shard_map/ppermute | solution.py:478
  1303.0 31.8 %collective-permute-start.32 = (bf16[768,1152]{1,0:T(8,128)(2,1)}, bf16[768,1152]{1,0:T(8,128)(2,1)S(1)}, u32[]{:S(2)}, u32[]{:S(2)}) collective-permute-start(bf16[768,1152]{1,0:T(8,128)(2,1)} %convolution_convert_fusion.9), channel_id=1, source_target_pairs={{0,2},{2,0},{4,6},{6,4},{8,10},{10,8},{12,14},{14,12},{16,18},{18,... | collective-permute-start | bytes 5308424 | tf_op jit(solution)/shard_map/ppermute | solution.py:432
  1303.6 31.2 %collective-permute-start.31 = (bf16[4,48,3456]{2,1,0:T(8,128)(2,1)}, bf16[4,48,3456]{2,1,0:T(8,128)(2,1)S(1)}, u32[]{:S(2)}, u32[]{:S(2)}) collective-permute-start(bf16[4,48,3456]{2,1,0:T(8,128)(2,1)} %fusion.48), channel_id=1, source_target_pairs={{0,4},{2,6},{4,0},{6,2},{8,12},{10,14},{12,8},{14,10},{16,20},{18,... | collective-permute-start | bytes 3981320 | tf_op jit(solution)/shard_map/ppermute | solution.py:452
  1305.0 12.2 collective-permute-start.30
  1336.5 37.8 %collective-permute-start.35 = (bf16[8,48,1152]{2,1,0:T(8,128)(2,1)}, bf16[8,48,1152]{2,1,0:T(8,128)(2,1)}, u32[]{:S(2)}, u32[]{:S(2)}) collective-permute-start(bf16[8,48,1152]{2,1,0:T(8,128)(2,1)} %get-tuple-element.243), channel_id=1, source_target_pairs={{0,1},{1,0},{2,3},{3,2},{4,5},{5,4},{6,7},{7,6},{8,9},{9,8},{10,11... | collective-permute-start | bytes 2654216 | tf_op jit(solution)/shard_map/ppermute | solution.py:444
  1339.3 34.9 %all-to-all-start.4 = ((bf16[2,512,768]{2,1,0:T(8,128)(2,1)}), bf16[2,512,768]{2,1,0:T(8,128)(2,1)S(1)}, u32[]{:S(2)}, u32[]{:S(2)}) async-start(bf16[2,512,768]{2,1,0:T(8,128)(2,1)} %bitcast.90), calls=%async_computation.4 | async-start | bytes 3145728 | tf_op jit(solution)/shard_map/all_to_all | solution.py:414
  1345.0 15.9 %collective-permute-start.34 = (bf16[2,48,3456]{2,1,0:T(8,128)(2,1)S(1)}, bf16[2,48,3456]{2,1,0:T(8,128)(2,1)}, u32[]{:S(2)}, u32[]{:S(2)}) collective-permute-start(bf16[2,48,3456]{2,1,0:T(8,128)(2,1)S(1)} %fusion.69), channel_id=1, source_target_pairs={{0,8},{2,10},{4,12},{6,14},{8,0},{10,2},{12,4},{14,6},{16,24},{18,... | collective-permute-start | bytes 1990664 | tf_op jit(solution)/shard_map/ppermute | solution.py:452
  1376.6 8.3 collective-permute-start.39
  1378.2 18.6 %collective-permute-start.38 = (bf16[4,48,1152]{2,1,0:T(8,128)(2,1)S(1)}, bf16[4,48,1152]{2,1,0:T(8,128)(2,1)S(1)}, u32[]{:S(2)}, u32[]{:S(2)}) collective-permute-start(bf16[4,48,1152]{2,1,0:T(8,128)(2,1)S(1)} %fusion.82), channel_id=1, source_target_pairs={{0,4},{2,6},{4,0},{6,2},{8,12},{10,14},{12,8},{14,10},{16,20},{18,... | collective-permute-start | bytes 1327112 | tf_op jit(solution)/shard_map/ppermute | solution.py:452
  1381.3 15.4 %collective-permute-start.37 = (bf16[1,48,3456]{2,1,0:T(8,128)(2,1)S(1)}, bf16[1,48,3456]{2,1,0:T(8,128)(2,1)S(1)}, u32[]{:S(2)}, u32[]{:S(2)}) collective-permute-start(bf16[1,48,3456]{2,1,0:T(8,128)(2,1)S(1)} %fusion.72), channel_id=1, source_target_pairs={{0,16},{2,18},{4,20},{6,22},{8,24},{10,26},{12,28},{14,30},{16,0},... | collective-permute-start | bytes 995336 | tf_op jit(solution)/shard_map/ppermute | solution.py:452
  1399.4 9.1 collective-permute-start.40
  1410.4 8.8 collective-permute-start.43
  1410.6 8.6 collective-permute-start.44
  (143 other events, 3117.1 us)
Sparse Core Ops, SparseCore 0:
  13.8 103.2 all-gather.3
  159.3 56.3 all-gather.5

commit v4 on v3

--- a/solution.py
+++ b/solution.py
@@ -192,9 +192,10 @@
     return pl.pallas_call(
         kernel,
         in_specs=[pl.BlockSpec(memory_space=pltpu.SMEM)] + [anywhere] * len(pieces),
-        out_specs=anywhere,
+        out_specs=pl.BlockSpec(memory_space=pltpu.VMEM),
         out_shape=jax.ShapeDtypeStruct(out_shape, pieces[0].dtype),
         scratch_shapes=[pltpu.SemaphoreType.DMA((len(pieces),))],
+        compiler_params=pltpu.CompilerParams(vmem_limit_bytes=32 << 20),
         cost_estimate=pl.CostEstimate(flops=0, bytes_accessed=size, transcendentals=0),
         name="place_pieces",
     )(indices, *pieces)

time: 1450 us -> 829 us (0.57)
  Pallas kernels: 752 us -> 132 us
  waiting for transfers between devices: 201 us -> 176 us
    pallas_call x8, Pallas kernels: 627 us -> 6.64 us  [place_pieces(): pl.pallas_call(kernel, in_specs=[pl.BlockSpec(memory_space=pltpu.SMEM)] +...]
    ppermute x6, waiting for transfers between devices: 76.8 us -> 54.6 us  [gather_steps(): received, = (yield [lax.ppermute(current, 'wide', pair_up(bit))])]
  transfers between devices with their start and end apart: 56 -> 56, of which waited for: 22 -> 23; matrix products, arithmetic and copies ran while one was open for 19% -> 35% of each run, Pallas kernels for 38% -> 16%
where the time goes in v4:
time: 829 us; the launch traced here: 813 us
  matrix products  213 us (26%)
  waiting for transfers between devices  176 us (21%)
  Pallas kernels  132 us (16%)
  other arithmetic  115 us (14%)
  local copies, waits for them, and re-layouts  84.7 us (10%)
  starting transfers between devices  76.5 us (9%)
  between operations  16.4 us (2%)
    dot_general x32, matrix products, contract(): lax.dot_general(left, right, (((left_dim,), (right_dim,)), ((), ())), pre...  213 us
    pallas_call x2, Pallas kernels, attend_backward(): pl.pallas_call(functools.partial(attend_grad_kernel, rows=BACKWARD_ROWS),...  74.4 us
    ppermute x12, waiting for transfers between devices, reduce_group(): received, = (yield [lax.ppermute(sent, 'wide', pair_up(bit))])  58.1 us
    ppermute x6, waiting for transfers between devices, gather_steps(): received, = (yield [lax.ppermute(current, 'wide', pair_up(bit))])  54.6 us
    pallas_call x2, Pallas kernels, attend_forward(): pl.pallas_call(functools.partial(attend_kernel, rows=FORWARD_ROWS), grid=...  50.7 us
    ppermute x4, waiting for transfers between devices, reduce_group(): lax.ppermute(jnp.concatenate(blocks[1], axis=-1), 'seq', swap)  18.7 us
    convert_element_type x12, other arithmetic, reduce_group(): sent = total_of([side_of(view, 1 - mine, 1) for view in views]).astype(half)  18.1 us
    unnamed x284, local copies, waits for them, and re-layouts  17.2 us
  transfers between devices with their start and end apart: 56, of which 23 were waited for; matrix products, arithmetic and copies ran while one was open for 35% of the time, Pallas kernels for 16%

profile of v4, /device:TPU:0, one launch (start us, length us, event | category | flops | bytes accessed | tf_op | source)
XLA Modules:
  0.0 813.1 jit_solution(2431497735245605969)
XLA Ops:
  13.7 4.2 all-to-all-start
  21.8 16.3 %all-to-all-done = bf16[2,512,768]{2,1,0:T(8,128)(2,1)S(1)} async-done(((bf16[2,512,768]{2,1,0:T(8,128)(2,1)}), bf16[2,512,768]{2,1,0:T(8,128)(2,1)S(1)}, u32[]{:S(2)}, u32[]{:S(2)}) %all-to-all-start) | async-done | bytes 1572896 | tf_op jit(solution)/shard_map/all_to_all | solution.py:244
  39.8 8.7 %collective-permute-done.refs_1_ = bf16[1,48,3072]{2,1,0:T(8,128)(2,1)S(1)} collective-permute-done((bf16[1,48,3072]{2,1,0:T(8,128)(2,1)S(1)}, bf16[1,48,3072]{2,1,0:T(8,128)(2,1)S(1)}, u32[]{:S(2)}, u32[]{:S(2)}) %collective-permute-start) | collective-permute-done | bytes 294944 | tf_op jit(solution)/shard_map/ppermute | solution.py:283
  51.0 22.2 %collective-permute-done.1.refs_1_ = bf16[2,48,3072]{2,1,0:T(8,128)(2,1)S(1)} collective-permute-done((bf16[2,48,3072]{2,1,0:T(8,128)(2,1)S(1)}, bf16[2,48,3072]{2,1,0:T(8,128)(2,1)S(1)}, u32[]{:S(2)}, u32[]{:S(2)}) %collective-permute-start.1) | collective-permute-done | bytes 589856 | tf_op jit(solution)/shard_map/ppermute | solution.py:283
  76.1 5.2 all-to-all-start.1
  82.8 7.1 collective-permute-start.6
  92.9 22.1 %collective-permute-done.2.refs_1_ = bf16[4,48,3072]{2,1,0:T(8,128)(2,1)S(1)} collective-permute-done((bf16[4,48,3072]{2,1,0:T(8,128)(2,1)S(1)}, bf16[4,48,3072]{2,1,0:T(8,128)(2,1)S(1)}, u32[]{:S(2)}, u32[]{:S(2)}) %collective-permute-start.2) | collective-permute-done | bytes 1179680 | tf_op jit(solution)/shard_map/ppermute | solution.py:283
  126.3 8.8 %add_convert_fusion.1.query_ref.key_ref.value_ref = bf16[1024,2304]{1,0:T(8,128)(2,1)} fusion(f32[2304]{0:T(1024)S(1)} %get-tuple-element.307, bf16[768,6272]{1,0:T(8,128)(2,1)} %all-gather.4.cloned.1.call-done, bf16[1024,768]{0,1:T(8,128)(2,1)} %copy.250, f32[768]{0:T(1024)S(1)} %get-tuple-element.228, f32[768]{0:T(1024)S(1)} %get-tuple-element.234, ...), kind=kOutput, calls=%fused_computation.25 | convolution fusion | flops 3634102272 | bytes 9857024 | tf_op jit(solution)/shard_map/dot_general | solution.py:22
  135.1 25.3 %attend_forward.2 = (bf16[1024,768]{1,0:T(8,128)(2,1)}, f32[6,2,1024]{2,1,0:T(2,128)}) custom-call(bf16[1024,2304]{1,0:T(8,128)(2,1)} %add_convert_fusion.1.query_ref.key_ref.value_ref, bf16[1024,2304]{1,0:T(8,128)(2,1)} %add_convert_fusion.1.query_ref.key_ref.value_ref, bf16[1024,2304]{1,0:T(8,128)(2,1)} %add_convert_fusion.1.query_ref.key_ref.value_ref, ...), custom_call_target="tpu_custom_call" | custom-call | flops 12884901888 | bytes 6291456 | tf_op jit(solution)/shard_map/attend_forward/pallas_call | solution.py:62
  160.4 8.2 %collective-permute-done.3.refs_1_ = bf16[8,48,3072]{2,1,0:T(8,128)(2,1)} collective-permute-done((bf16[8,48,3072]{2,1,0:T(8,128)(2,1)S(1)}, bf16[8,48,3072]{2,1,0:T(8,128)(2,1)}, u32[]{:S(2)}, u32[]{:S(2)}) %collective-permute-start.3) | collective-permute-done | bytes 2359328 | tf_op jit(solution)/shard_map/ppermute | solution.py:292
  168.9 4.8 all-to-all-start.2
  173.8 4.0 fusion.150
  180.0 15.3 %multiply_convert_fusion.1 = (bf16[1024,3072]{1,0:T(8,128)(2,1)}, f32[1024,3072]{1,0:T(8,128)}) fusion(f32[3072]{0:T(1024)S(1)} %add.985, bf16[1024,768]{0,1:T(8,128)(2,1)S(1)} %add_convert_fusion.5, bf16[768,6272]{1,0:T(8,128)(2,1)} %all-gather.4.cloned.1.call-done), kind=kOutput, calls=%fused_computation.21 | convolution fusion | flops 4863295488 | bytes 25178112 | tf_op jit(solution)/shard_map/dot_general | solution.py:22
  203.5 10.3 %add_add_fusion.1 = f32[1024,768]{0,1:T(8,128)} fusion(f32[1024,768]{0,1:T(8,128)} %copy-done.11, bf16[1024,3072]{1,0:T(8,128)(2,1)} %get-tuple-element.100, bf16[1,3072,768]{2,1,0:T(8,128)(2,1)} %all-gather.6.cloned.1.call-done, f32[768]{0:T(1024)S(1)} %get-tuple-element.223), kind=kOutput, calls=%fused_computation.80 | convolution fusion | flops 4833411072 | bytes 17304576 | tf_op jit(solution)/shard_map/dot_general | solution.py:22
  213.8 3.9 place_pieces.12
  227.0 8.1 add_convert_fusion.query_ref.key_ref.value_ref
  238.8 25.4 %attend_forward.3 = (bf16[1024,768]{1,0:T(8,128)(2,1)}, f32[6,2,1024]{2,1,0:T(2,128)}) custom-call(bf16[1024,2304]{1,0:T(8,128)(2,1)} %add_convert_fusion.query_ref.key_ref.value_ref, bf16[1024,2304]{1,0:T(8,128)(2,1)} %add_convert_fusion.query_ref.key_ref.value_ref, bf16[1024,2304]{1,0:T(8,128)(2,1)} %add_convert_fusion.query_ref.key_ref.value_ref, ...), custom_call_target="tpu_custom_call" | custom-call | flops 12884901888 | bytes 6291456 | tf_op jit(solution)/shard_map/attend_forward/pallas_call | solution.py:62
  271.7 12.3 %multiply_convert_fusion = (bf16[1024,3072]{1,0:T(8,128)(2,1)}, f32[1024,3072]{1,0:T(8,128)}) fusion(f32[3072]{0:T(1024)S(1)} %copy-done.108, bf16[1024,768]{0,1:T(8,128)(2,1)S(1)} %add_convert_fusion.3, bf16[768,6144]{1,0:T(8,128)(2,1)S(1)} %bitcast.370), kind=kOutput, calls=%fused_computation.20 | convolution fusion | flops 4863295488 | bytes 25178112 | tf_op jit(solution)/shard_map/dot_general | solution.py:22
  284.0 17.1 %convert_reduce_fusion = (f32[3072]{0:T(1024)S(1)}, bf16[1024,3072]{1,0:T(8,128)(2,1)}) fusion(f32[1024,3072]{1,0:T(8,128)} %get-tuple-element.315, f32[3072]{0:T(1024)S(1)} %copy-done.108, bf16[1024,768]{1,0:T(8,128)(2,1)} %bitcast.18, bf16[3072,768]{1,0:T(8,128)(2,1)S(1)} %bitcast.380), kind=kOutput, calls=%fused_computation.18 | convolution fusion | flops 4904186880 | bytes 25190400 | tf_op jit(solution)/shard_map/dot_general | solution.py:22
  301.1 8.5 %fusion.153 = (f32[768]{0:T(1024)S(1)}, f32[1024,768]{1,0:T(8,128)}) fusion(bf16[1024,3072]{1,0:T(8,128)(2,1)} %get-tuple-element.325, bf16[768,6144]{1,0:T(8,128)(2,1)S(1)} %bitcast.371), kind=kOutput, calls=%fused_computation.397 | convolution fusion | flops 4832623616 | bytes 14158848 | tf_op jit(solution)/shard_map/dot_general | solution.py:22
  309.6 4.0 convolution_convert_fusion.7
  313.7 4.8 convolution_convert_fusion.3
  325.7 9.7 %add_convert_fusion.2 = bf16[1024,768]{0,1:T(8,128)(2,1)} fusion(f32[1024,768]{0,1:T(8,128)S(1)} %copy-done.9, bf16[1024,3072]{1,0:T(8,128)(2,1)} %get-tuple-element.314, bf16[3072,768]{1,0:T(8,128)(2,1)} %bitcast.381, f32[768]{0:T(1024)S(1)} %copy-done.116), kind=kOutput, calls=%fused_computation.71 | convolution fusion | flops 4834197504 | bytes 15731712 | tf_op jit(solution)/shard_map/dot_general | solution.py:22
  337.9 4.7 all-to-all-start.3
  343.3 4.9 convert_reduce_fusion.5
  350.2 6.4 convolution_convert_fusion.2
  358.0 4.9 convolution_convert_fusion.6
  391.2 37.3 %attend_backward.2 = bf16[1024,2304]{1,0:T(8,128)(2,1)} custom-call(bf16[1024,2304]{1,0:T(8,128)(2,1)} %add_convert_fusion.query_ref.key_ref.value_ref, bf16[1024,2304]{1,0:T(8,128)(2,1)} %add_convert_fusion.query_ref.key_ref.value_ref, bf16[1024,2304]{1,0:T(8,128)(2,1)} %add_convert_fusion.query_ref.key_ref.value_ref, f32[1024,1024]{1,0:T(8,128)} %fusion.20.bias_ref, ...), custom_call_target="tpu_custom_call" | custom-call | flops 32212254720 | bytes 12582912 | tf_op jit(solution)/shard_map/attend_backward/pallas_call | solution.py:149
  428.5 10.4 %fusion.152 = (f32[768]{0:T(1024)}, f32[1024,768]{1,0:T(8,128)}) fusion(bf16[1024,2304]{1,0:T(8,128)(2,1)} %attend_backward.2, bf16[768,6144]{1,0:T(8,128)(2,1)} %bitcast.367), kind=kOutput, calls=%fused_computation.396 | convolution fusion | flops 3624664320 | bytes 11406336 | tf_op jit(solution)/shard_map/dot_general | solution.py:22
  452.3 5.5 multiply_add_fusion.2
  461.7 4.0 convolution_convert_fusion.10
  465.8 6.8 collective-permute-done.15
  475.0 8.0 convolution_convert_fusion
  483.0 4.9 convolution_convert_fusion.1
  494.9 17.1 %fusion.6 = bf16[1024,3072]{1,0:T(8,128)(2,1)} fusion(f32[1024,3072]{1,0:T(8,128)} %get-tuple-element.311, f32[3072]{0:T(1024)S(1)} %copy-done.107, bf16[1024,768]{0,1:T(8,128)(2,1)S(1)} %get-tuple-element.236, bf16[1,3072,768]{2,1,0:T(8,128)(2,1)S(1)} %bitcast.470), kind=kOutput, calls=%fused_computation.10 | convolution fusion | flops 4897898496 | bytes 25178112 | tf_op jit(solution)/shard_map/dot_general | solution.py:22
  518.4 5.3 convolution_convert_fusion.5
  523.7 3.9 convolution_convert_fusion.4
  532.2 4.6 collective-permute-start.20
  536.8 9.1 %fusion.155 = (f32[768]{0:T(1024)S(1)}, f32[1024,768]{1,0:T(8,128)}) fusion(bf16[1024,3072]{1,0:T(8,128)(2,1)S(1)} %copy-done.21, bf16[768,6272]{1,0:T(8,128)(2,1)} %all-gather.4.cloned.1.call-done), kind=kOutput, calls=%fused_computation.399 | convolution fusion | flops 4832623616 | bytes 14158848 | tf_op jit(solution)/shard_map/dot_general | solution.py:22
  545.9 4.1 copy.221
  589.9 37.1 %attend_backward.3 = bf16[1024,2304]{1,0:T(8,128)(2,1)} custom-call(bf16[1024,2304]{1,0:T(8,128)(2,1)} %add_convert_fusion.1.query_ref.key_ref.value_ref, bf16[1024,2304]{1,0:T(8,128)(2,1)} %add_convert_fusion.1.query_ref.key_ref.value_ref, bf16[1024,2304]{1,0:T(8,128)(2,1)} %add_convert_fusion.1.query_ref.key_ref.value_ref, f32[1024,1024]{1,0:T(8,128)} %fusion.20.bias_ref, ...), custom_call_target="tpu_custom_call" | custom-call | flops 32212254720 | bytes 12582912 | tf_op jit(solution)/shard_map/attend_backward/pallas_call | solution.py:149
  628.3 17.6 %collective-permute-done.29 = bf16[8,48,3456]{2,1,0:T(8,128)(2,1)} collective-permute-done((bf16[8,48,3456]{2,1,0:T(8,128)(2,1)}, bf16[8,48,3456]{2,1,0:T(8,128)(2,1)}, u32[]{:S(2)}, u32[]{:S(2)}) %collective-permute-start.29) | collective-permute-done | bytes 2654240 | tf_op jit(solution)/shard_map/ppermute | solution.py:445
  658.0 7.5 fusion.154
  692.4 16.3 %collective-permute-done.31 = bf16[4,48,3456]{2,1,0:T(8,128)(2,1)S(1)} collective-permute-done((bf16[4,48,3456]{2,1,0:T(8,128)(2,1)}, bf16[4,48,3456]{2,1,0:T(8,128)(2,1)S(1)}, u32[]{:S(2)}, u32[]{:S(2)}) %collective-permute-start.31) | collective-permute-done | bytes 1327136 | tf_op jit(solution)/shard_map/ppermute | solution.py:453
  722.9 12.1 %collective-permute-done.34 = bf16[2,48,3456]{2,1,0:T(8,128)(2,1)} collective-permute-done((bf16[2,48,3456]{2,1,0:T(8,128)(2,1)S(1)}, bf16[2,48,3456]{2,1,0:T(8,128)(2,1)}, u32[]{:S(2)}, u32[]{:S(2)}) %collective-permute-start.34) | collective-permute-done | bytes 663584 | tf_op jit(solution)/shard_map/ppermute | solution.py:453
  735.1 13.1 %all-to-all-done.4 = bf16[2,512,768]{2,1,0:T(8,128)(2,1)S(1)} async-done(((bf16[2,512,768]{2,1,0:T(8,128)(2,1)}), bf16[2,512,768]{2,1,0:T(8,128)(2,1)S(1)}, u32[]{:S(2)}, u32[]{:S(2)}) %all-to-all-start.4) | async-done | bytes 1572896 | tf_op jit(solution)/shard_map/all_to_all | solution.py:415
  758.5 12.2 %collective-permute-done.37 = bf16[1,48,3456]{2,1,0:T(8,128)(2,1)S(1)} collective-permute-done((bf16[1,48,3456]{2,1,0:T(8,128)(2,1)S(1)}, bf16[1,48,3456]{2,1,0:T(8,128)(2,1)S(1)}, u32[]{:S(2)}, u32[]{:S(2)}) %collective-permute-start.37) | collective-permute-done | bytes 331808 | tf_op jit(solution)/shard_map/ppermute | solution.py:453
  786.8 6.8 collective-permute-done.44
  (617 shorter events, 276.0 us)
Async XLA Ops:
  7.2 115.5 %all-gather.4.cloned.1.call-start = ((), (), s32[]{:S(2)}) async-start(), calls=%async_computation.5 | async-start | bytes 10235904 | tf_op jit(solution)/shard_map/all_gather | solution.py:336
  13.7 24.4 %all-to-all-start = ((bf16[2,512,768]{2,1,0:T(8,128)(2,1)}), bf16[2,512,768]{2,1,0:T(8,128)(2,1)S(1)}, u32[]{:S(2)}, u32[]{:S(2)}) async-start(bf16[2,512,768]{2,1,0:T(8,128)(2,1)} %param.12), calls=%async_computation | async-start | bytes 3145728 | tf_op jit(solution)/shard_map/all_to_all | solution.py:244
  18.2 30.2 %collective-permute-start = (bf16[1,48,3072]{2,1,0:T(8,128)(2,1)S(1)}, bf16[1,48,3072]{2,1,0:T(8,128)(2,1)S(1)}, u32[]{:S(2)}, u32[]{:S(2)}) collective-permute-start(bf16[1,48,3072]{2,1,0:T(8,128)(2,1)S(1)} %fusion.107.refs_0_), channel_id=1, source_target_pairs={{0,16},{2,18},{4,20},{6,22},{8,24},{10,26},{12,28},{14,30},{16,0},... | collective-permute-start | bytes 884744 | tf_op jit(solution)/shard_map/ppermute | solution.py:283
  48.6 24.6 %collective-permute-start.1 = (bf16[2,48,3072]{2,1,0:T(8,128)(2,1)S(1)}, bf16[2,48,3072]{2,1,0:T(8,128)(2,1)S(1)}, u32[]{:S(2)}, u32[]{:S(2)}) collective-permute-start(bf16[2,48,3072]{2,1,0:T(8,128)(2,1)S(1)} %bitcast.384), channel_id=1, source_target_pairs={{0,8},{2,10},{4,12},{6,14},{8,0},{10,2},{12,4},{14,6},{16,24},{18,... | collective-permute-start | bytes 1769480 | tf_op jit(solution)/shard_map/ppermute | solution.py:283
  73.4 41.6 %collective-permute-start.2 = (bf16[4,48,3072]{2,1,0:T(8,128)(2,1)S(1)}, bf16[4,48,3072]{2,1,0:T(8,128)(2,1)S(1)}, u32[]{:S(2)}, u32[]{:S(2)}) collective-permute-start(bf16[4,48,3072]{2,1,0:T(8,128)(2,1)S(1)} %bitcast.378), channel_id=1, source_target_pairs={{0,4},{2,6},{4,0},{6,2},{8,12},{10,14},{12,8},{14,10},{16,20},{18,... | collective-permute-start | bytes 3538952 | tf_op jit(solution)/shard_map/ppermute | solution.py:283
  76.1 13.9 %all-to-all-start.1 = ((s32[2,512,2]{1,2,0:T(2,128)}), s32[2,512,2]{1,2,0:T(2,128)S(1)}, u32[]{:S(2)}, u32[]{:S(2)}) async-start(s32[2,512,2]{1,2,0:T(2,128)} %pad_add_fusion), calls=%async_computation.1 | async-start | bytes 16384 | tf_op jit(solution)/shard_map/all_to_all | solution.py:244
  81.4 122.1 %all-gather.6.cloned.1.call-start = ((), (), s32[]{:S(2)}) async-start(), calls=%async_computation.6 | async-start | bytes 5013504 | tf_op jit(solution)/shard_map/all_gather | solution.py:337
  82.8 118.1 %collective-permute-start.6 = (bf16[1,96,768]{2,1,0:T(8,128)(2,1)}, bf16[1,96,768]{2,1,0:T(8,128)(2,1)}, u32[]{:S(2)}, u32[]{:S(2)}) collective-permute-start(bf16[1,96,768]{2,1,0:T(8,128)(2,1)} %constant_dynamic-slice_fusion.15.refs_0_), channel_id=1, source_target_pairs={{0,16},{2,18},{4,20},{6,22},{8,24},{10,26},{12,28},{14,30},{16,0},... | collective-permute-start | bytes 442376 | tf_op jit(solution)/shard_map/ppermute | solution.py:283
  117.5 51.1 %collective-permute-start.3 = (bf16[8,48,3072]{2,1,0:T(8,128)(2,1)S(1)}, bf16[8,48,3072]{2,1,0:T(8,128)(2,1)}, u32[]{:S(2)}, u32[]{:S(2)}) collective-permute-start(bf16[8,48,3072]{2,1,0:T(8,128)(2,1)S(1)} %bitcast.372), channel_id=1, source_target_pairs={{0,1},{1,0},{2,3},{3,2},{4,5},{5,4},{6,7},{7,6},{8,9},{9,8},{10,11... | collective-permute-start | bytes 7077896 | tf_op jit(solution)/shard_map/ppermute | solution.py:292
  119.2 81.7 %collective-permute-start.4 = (bf16[8,48,3072]{2,1,0:T(8,128)(2,1)S(1)}, bf16[8,48,3072]{2,1,0:T(8,128)(2,1)}, u32[]{:S(2)}, u32[]{:S(2)}) collective-permute-start(bf16[8,48,3072]{2,1,0:T(8,128)(2,1)S(1)} %bitcast.373), channel_id=1, source_target_pairs={{0,2},{2,0},{4,6},{6,4},{8,10},{10,8},{12,14},{14,12},{16,18},{18,... | collective-permute-start | bytes 7077896 | tf_op jit(solution)/shard_map/ppermute | solution.py:293
  168.9 32.0 %collective-permute-start.5 = (bf16[8,48,3072]{2,1,0:T(8,128)(2,1)}, bf16[8,48,3072]{2,1,0:T(8,128)(2,1)}, u32[]{:S(2)}, u32[]{:S(2)}) collective-permute-start(bf16[8,48,3072]{2,1,0:T(8,128)(2,1)} %collective-permute-done.3.refs_1_), channel_id=1, source_target_pairs={{0,2},{2,0},{4,6},{6,4},{8,10},{10,8},{12,14},{14,12},{16,18},{18,... | collective-permute-start | bytes 7077896 | tf_op jit(solution)/shard_map/ppermute | solution.py:293
  168.9 27.0 %all-to-all-start.2 = ((bf16[2,512,768]{2,1,0:T(8,128)(2,1)}), bf16[2,512,768]{2,1,0:T(8,128)(2,1)}, u32[]{:S(2)}, u32[]{:S(2)}) async-start(bf16[2,512,768]{2,1,0:T(8,128)(2,1)} %param.16), calls=%async_computation.2 | async-start | bytes 3145728 | tf_op jit(solution)/shard_map/all_to_all | solution.py:244
  201.9 19.3 %collective-permute-start.7 = (bf16[2,96,768]{2,1,0:T(8,128)(2,1)S(1)}, bf16[2,96,768]{2,1,0:T(8,128)(2,1)S(1)}, u32[]{:S(2)}, u32[]{:S(2)}) collective-permute-start(bf16[2,96,768]{2,1,0:T(8,128)(2,1)S(1)} %bitcast.386), channel_id=1, source_target_pairs={{0,8},{2,10},{4,12},{6,14},{8,0},{10,2},{12,4},{14,6},{16,24},{18,... | collective-permute-start | bytes 884744 | tf_op jit(solution)/shard_map/ppermute | solution.py:283
  221.3 15.5 %collective-permute-start.8 = (bf16[4,96,768]{2,1,0:T(8,128)(2,1)S(1)}, bf16[4,96,768]{2,1,0:T(8,128)(2,1)S(1)}, u32[]{:S(2)}, u32[]{:S(2)}) collective-permute-start(bf16[4,96,768]{2,1,0:T(8,128)(2,1)S(1)} %bitcast.382), channel_id=1, source_target_pairs={{0,4},{2,6},{4,0},{6,2},{8,12},{10,14},{12,8},{14,10},{16,20},{18,... | collective-permute-start | bytes 1769480 | tf_op jit(solution)/shard_map/ppermute | solution.py:283
  237.0 27.3 %collective-permute-start.9 = (bf16[8,96,768]{2,1,0:T(8,128)(2,1)S(1)}, bf16[8,96,768]{2,1,0:T(8,128)(2,1)S(1)}, u32[]{:S(2)}, u32[]{:S(2)}) collective-permute-start(bf16[8,96,768]{2,1,0:T(8,128)(2,1)S(1)} %bitcast.375), channel_id=1, source_target_pairs={{0,1},{1,0},{2,3},{3,2},{4,5},{5,4},{6,7},{7,6},{8,9},{9,8},{10,11... | collective-permute-start | bytes 3538952 | tf_op jit(solution)/shard_map/ppermute | solution.py:292
  238.8 31.2 %collective-permute-start.10 = (bf16[8,96,768]{2,1,0:T(8,128)(2,1)S(1)}, bf16[8,96,768]{2,1,0:T(8,128)(2,1)S(1)}, u32[]{:S(2)}, u32[]{:S(2)}) collective-permute-start(bf16[8,96,768]{2,1,0:T(8,128)(2,1)S(1)} %bitcast.376), channel_id=1, source_target_pairs={{0,2},{2,0},{4,6},{6,4},{8,10},{10,8},{12,14},{14,12},{16,18},{18,... | collective-permute-start | bytes 3538952 | tf_op jit(solution)/shard_map/ppermute | solution.py:293
  313.6 49.3 %collective-permute-start.13 = (bf16[768,1536]{1,0:T(8,128)(2,1)}, bf16[768,1536]{1,0:T(8,128)(2,1)}, u32[]{:S(2)}, u32[]{:S(2)}) collective-permute-start(bf16[768,1536]{1,0:T(8,128)(2,1)} %convolution_convert_fusion.7), channel_id=1, source_target_pairs={{0,2},{2,0},{4,6},{6,4},{8,10},{10,8},{12,14},{14,12},{16,18},{18,... | collective-permute-start | bytes 7077896 | tf_op jit(solution)/shard_map/ppermute | solution.py:433
  318.5 44.5 %collective-permute-start.12 = (bf16[3072,384]{1,0:T(8,128)(2,1)}, bf16[3072,384]{1,0:T(8,128)(2,1)}, u32[]{:S(2)}, u32[]{:S(2)}) collective-permute-start(bf16[3072,384]{1,0:T(8,128)(2,1)} %convolution_convert_fusion.3), channel_id=1, source_target_pairs={{0,2},{2,0},{4,6},{6,4},{8,10},{10,8},{12,14},{14,12},{16,18},{18,... | collective-permute-start | bytes 7077896 | tf_op jit(solution)/shard_map/ppermute | solution.py:433
  337.9 47.3 %all-to-all-start.3 = ((bf16[2,512,768]{2,1,0:T(8,128)(2,1)}), bf16[2,512,768]{2,1,0:T(8,128)(2,1)}, u32[]{:S(2)}, u32[]{:S(2)}) async-start(bf16[2,512,768]{2,1,0:T(8,128)(2,1)} %bitcast.390), calls=%async_computation.3 | async-start | bytes 3145728 | tf_op jit(solution)/shard_map/all_to_all | solution.py:415
  374.1 54.4 %collective-permute-start.14 = (bf16[8,48,3072]{2,1,0:T(8,128)(2,1)}, bf16[8,48,3072]{2,1,0:T(8,128)(2,1)S(1)}, u32[]{:S(2)}, u32[]{:S(2)}) collective-permute-start(bf16[8,48,3072]{2,1,0:T(8,128)(2,1)} %fusion.51), channel_id=1, source_target_pairs={{0,1},{1,0},{2,3},{3,2},{4,5},{5,4},{6,7},{7,6},{8,9},{9,8},{10,11... | collective-permute-start | bytes 7077896 | tf_op jit(solution)/shard_map/ppermute | solution.py:445
  385.2 80.5 %collective-permute-start.17 = (bf16[768,384]{1,0:T(8,128)(2,1)}, bf16[768,384]{1,0:T(8,128)(2,1)}, u32[]{:S(2)}, u32[]{:S(2)}) collective-permute-start(bf16[768,384]{1,0:T(8,128)(2,1)} %convolution_convert_fusion.17), channel_id=1, source_target_pairs={{0,2},{2,0},{4,6},{6,4},{8,10},{10,8},{12,14},{14,12},{16,18},{18,... | collective-permute-start | bytes 1769480 | tf_op jit(solution)/shard_map/ppermute | solution.py:433
  442.4 30.1 %collective-permute-start.16 = (bf16[768,1152]{1,0:T(8,128)(2,1)}, bf16[768,1152]{1,0:T(8,128)(2,1)}, u32[]{:S(2)}, u32[]{:S(2)}) collective-permute-start(bf16[768,1152]{1,0:T(8,128)(2,1)} %convolution_convert_fusion.11), channel_id=1, source_target_pairs={{0,2},{2,0},{4,6},{6,4},{8,10},{10,8},{12,14},{14,12},{16,18},{18,... | collective-permute-start | bytes 5308424 | tf_op jit(solution)/shard_map/ppermute | solution.py:433
  444.3 28.2 %collective-permute-start.15 = (bf16[4,48,3072]{2,1,0:T(8,128)(2,1)}, bf16[4,48,3072]{2,1,0:T(8,128)(2,1)}, u32[]{:S(2)}, u32[]{:S(2)}) collective-permute-start(bf16[4,48,3072]{2,1,0:T(8,128)(2,1)} %fusion.52), channel_id=1, source_target_pairs={{0,4},{2,6},{4,0},{6,2},{8,12},{10,14},{12,8},{14,10},{16,20},{18,... | collective-permute-start | bytes 3538952 | tf_op jit(solution)/shard_map/ppermute | solution.py:453
  491.0 27.4 %collective-permute-start.19 = (bf16[8,48,1536]{2,1,0:T(8,128)(2,1)}, bf16[8,48,1536]{2,1,0:T(8,128)(2,1)}, u32[]{:S(2)}, u32[]{:S(2)}) collective-permute-start(bf16[8,48,1536]{2,1,0:T(8,128)(2,1)} %pad_maximum_fusion), channel_id=1, source_target_pairs={{0,1},{1,0},{2,3},{3,2},{4,5},{5,4},{6,7},{7,6},{8,9},{9,8},{10,11... | collective-permute-start | bytes 3538952 | tf_op jit(solution)/shard_map/ppermute | solution.py:445
  494.2 23.1 %collective-permute-start.18 = (bf16[2,48,3072]{2,1,0:T(8,128)(2,1)}, bf16[2,48,3072]{2,1,0:T(8,128)(2,1)}, u32[]{:S(2)}, u32[]{:S(2)}) collective-permute-start(bf16[2,48,3072]{2,1,0:T(8,128)(2,1)} %fusion.74), channel_id=1, source_target_pairs={{0,8},{2,10},{4,12},{6,14},{8,0},{10,2},{12,4},{14,6},{16,24},{18,... | collective-permute-start | bytes 1769480 | tf_op jit(solution)/shard_map/ppermute | solution.py:453
  494.8 81.2 %collective-permute-start.24 = (bf16[3072,384]{1,0:T(8,128)(2,1)}, bf16[3072,384]{1,0:T(8,128)(2,1)}, u32[]{:S(2)}, u32[]{:S(2)}) collective-permute-start(bf16[3072,384]{1,0:T(8,128)(2,1)} %convolution_convert_fusion.1), channel_id=1, source_target_pairs={{0,2},{2,0},{4,6},{6,4},{8,10},{10,8},{12,14},{14,12},{16,18},{18,... | collective-permute-start | bytes 7077896 | tf_op jit(solution)/shard_map/ppermute | solution.py:433
  529.6 31.5 %collective-permute-start.21 = (bf16[4,48,1536]{2,1,0:T(8,128)(2,1)}, bf16[4,48,1536]{2,1,0:T(8,128)(2,1)}, u32[]{:S(2)}, u32[]{:S(2)}) collective-permute-start(bf16[4,48,1536]{2,1,0:T(8,128)(2,1)} %fusion.75), channel_id=1, source_target_pairs={{0,4},{2,6},{4,0},{6,2},{8,12},{10,14},{12,8},{14,10},{16,20},{18,... | collective-permute-start | bytes 1769480 | tf_op jit(solution)/shard_map/ppermute | solution.py:453
  532.2 28.8 %collective-permute-start.20 = (bf16[1,48,3072]{2,1,0:T(8,128)(2,1)}, bf16[1,48,3072]{2,1,0:T(8,128)(2,1)S(1)}, u32[]{:S(2)}, u32[]{:S(2)}) collective-permute-start(bf16[1,48,3072]{2,1,0:T(8,128)(2,1)} %fusion.81), channel_id=1, source_target_pairs={{0,16},{2,18},{4,20},{6,22},{8,24},{10,26},{12,28},{14,30},{16,0},... | collective-permute-start | bytes 884744 | tf_op jit(solution)/shard_map/ppermute | solution.py:453
  553.2 22.9 %collective-permute-start.25 = (bf16[768,1536]{1,0:T(8,128)(2,1)}, bf16[768,1536]{1,0:T(8,128)(2,1)}, u32[]{:S(2)}, u32[]{:S(2)}) collective-permute-start(bf16[768,1536]{1,0:T(8,128)(2,1)} %convolution_convert_fusion.5), channel_id=1, source_target_pairs={{0,2},{2,0},{4,6},{6,4},{8,10},{10,8},{12,14},{14,12},{16,18},{18,... | collective-permute-start | bytes 7077896 | tf_op jit(solution)/shard_map/ppermute | solution.py:433
  563.5 12.5 %collective-permute-start.26 = (bf16[768,384]{1,0:T(8,128)(2,1)S(1)}, bf16[768,384]{1,0:T(8,128)(2,1)S(1)}, u32[]{:S(2)}, u32[]{:S(2)}) collective-permute-start(bf16[768,384]{1,0:T(8,128)(2,1)S(1)} %convolution_convert_fusion.15), channel_id=1, source_target_pairs={{0,2},{2,0},{4,6},{6,4},{8,10},{10,8},{12,14},{14,12},{16,18},{18,... | collective-permute-start | bytes 1769480 | tf_op jit(solution)/shard_map/ppermute | solution.py:433
  564.7 9.5 %collective-permute-start.23 = (bf16[2,48,1536]{2,1,0:T(8,128)(2,1)S(1)}, bf16[2,48,1536]{2,1,0:T(8,128)(2,1)S(1)}, u32[]{:S(2)}, u32[]{:S(2)}) collective-permute-start(bf16[2,48,1536]{2,1,0:T(8,128)(2,1)S(1)} %fusion.93), channel_id=1, source_target_pairs={{0,8},{2,10},{4,12},{6,14},{8,0},{10,2},{12,4},{14,6},{16,24},{18,... | collective-permute-start | bytes 884744 | tf_op jit(solution)/shard_map/ppermute | solution.py:453
  566.9 9.2 %collective-permute-start.22 = (bf16[48,3072]{1,0:T(8,128)(2,1)S(1)}, bf16[48,3072]{1,0:T(8,128)(2,1)S(1)}, u32[]{:S(2)}, u32[]{:S(2)}) collective-permute-start(bf16[48,3072]{1,0:T(8,128)(2,1)S(1)} %fusion.104), channel_id=1, source_target_pairs={{0,1},{1,0},{2,3},{3,2},{4,5},{5,4},{6,7},{7,6},{8,9},{9,8},{10,11... | collective-permute-start | bytes 884744 | tf_op jit(solution)/shard_map/ppermute | solution.py:457
  586.8 59.2 %collective-permute-start.29 = (bf16[8,48,3456]{2,1,0:T(8,128)(2,1)}, bf16[8,48,3456]{2,1,0:T(8,128)(2,1)}, u32[]{:S(2)}, u32[]{:S(2)}) collective-permute-start(bf16[8,48,3456]{2,1,0:T(8,128)(2,1)} %fusion.103), channel_id=1, source_target_pairs={{0,1},{1,0},{2,3},{3,2},{4,5},{5,4},{6,7},{7,6},{8,9},{9,8},{10,11... | collective-permute-start | bytes 7962632 | tf_op jit(solution)/shard_map/ppermute | solution.py:445
  589.4 38.9 %collective-permute-start.28 = (bf16[1,48,1536]{2,1,0:T(8,128)(2,1)S(1)}, bf16[1,48,1536]{2,1,0:T(8,128)(2,1)S(1)}, u32[]{:S(2)}, u32[]{:S(2)}) collective-permute-start(bf16[1,48,1536]{2,1,0:T(8,128)(2,1)S(1)} %fusion.110), channel_id=1, source_target_pairs={{0,16},{2,18},{4,20},{6,22},{8,24},{10,26},{12,28},{14,30},{16,0},... | collective-permute-start | bytes 442376 | tf_op jit(solution)/shard_map/ppermute | solution.py:453
  589.5 38.8 %collective-permute-start.27 = (bf16[48,3072]{1,0:T(8,128)(2,1)S(1)}, bf16[48,3072]{1,0:T(8,128)(2,1)S(1)}, u32[]{:S(2)}, u32[]{:S(2)}) collective-permute-start(bf16[48,3072]{1,0:T(8,128)(2,1)S(1)} %broadcast_select_fusion.7), channel_id=1, source_target_pairs={{0,2},{2,0},{4,6},{6,4},{8,10},{10,8},{12,14},{14,12},{16,18},{18,... | collective-permute-start | bytes 884744 | tf_op jit(solution)/shard_map/ppermute | solution.py:460
  676.9 45.0 %collective-permute-start.36 = (f32[8,1152]{1,0:T(8,128)}, f32[8,1152]{1,0:T(8,128)S(1)}, u32[]{:S(2)}, u32[]{:S(2)}) collective-permute-start(f32[8,1152]{1,0:T(8,128)} %bitcast.357), channel_id=1, source_target_pairs={{0,2},{2,0},{4,6},{6,4},{8,10},{10,8},{12,14},{14,12},{16,18},{18,... | collective-permute-start | bytes 110600 | tf_op jit(solution)/shard_map/ppermute | solution.py:479
  676.9 31.8 %collective-permute-start.32 = (bf16[768,1152]{1,0:T(8,128)(2,1)}, bf16[768,1152]{1,0:T(8,128)(2,1)S(1)}, u32[]{:S(2)}, u32[]{:S(2)}) collective-permute-start(bf16[768,1152]{1,0:T(8,128)(2,1)} %convolution_convert_fusion.9), channel_id=1, source_target_pairs={{0,2},{2,0},{4,6},{6,4},{8,10},{10,8},{12,14},{14,12},{16,18},{18,... | collective-permute-start | bytes 5308424 | tf_op jit(solution)/shard_map/ppermute | solution.py:433
  677.4 31.2 %collective-permute-start.31 = (bf16[4,48,3456]{2,1,0:T(8,128)(2,1)}, bf16[4,48,3456]{2,1,0:T(8,128)(2,1)S(1)}, u32[]{:S(2)}, u32[]{:S(2)}) collective-permute-start(bf16[4,48,3456]{2,1,0:T(8,128)(2,1)} %fusion.48), channel_id=1, source_target_pairs={{0,4},{2,6},{4,0},{6,2},{8,12},{10,14},{12,8},{14,10},{16,20},{18,... | collective-permute-start | bytes 3981320 | tf_op jit(solution)/shard_map/ppermute | solution.py:453
  679.9 12.5 %collective-permute-start.30 = (bf16[48,1536]{1,0:T(8,128)(2,1)S(1)}, bf16[48,1536]{1,0:T(8,128)(2,1)S(1)}, u32[]{:S(2)}, u32[]{:S(2)}) collective-permute-start(bf16[48,1536]{1,0:T(8,128)(2,1)S(1)} %fusion.115), channel_id=1, source_target_pairs={{0,1},{1,0},{2,3},{3,2},{4,5},{5,4},{6,7},{7,6},{8,9},{9,8},{10,11... | collective-permute-start | bytes 442376 | tf_op jit(solution)/shard_map/ppermute | solution.py:457
  710.4 37.8 %collective-permute-start.35 = (bf16[8,48,1152]{2,1,0:T(8,128)(2,1)}, bf16[8,48,1152]{2,1,0:T(8,128)(2,1)}, u32[]{:S(2)}, u32[]{:S(2)}) collective-permute-start(bf16[8,48,1152]{2,1,0:T(8,128)(2,1)} %get-tuple-element.243), channel_id=1, source_target_pairs={{0,1},{1,0},{2,3},{3,2},{4,5},{5,4},{6,7},{7,6},{8,9},{9,8},{10,11... | collective-permute-start | bytes 2654216 | tf_op jit(solution)/shard_map/ppermute | solution.py:445
  713.5 34.6 %all-to-all-start.4 = ((bf16[2,512,768]{2,1,0:T(8,128)(2,1)}), bf16[2,512,768]{2,1,0:T(8,128)(2,1)S(1)}, u32[]{:S(2)}, u32[]{:S(2)}) async-start(bf16[2,512,768]{2,1,0:T(8,128)(2,1)} %bitcast.90), calls=%async_computation.4 | async-start | bytes 3145728 | tf_op jit(solution)/shard_map/all_to_all | solution.py:415
  719.2 15.9 %collective-permute-start.34 = (bf16[2,48,3456]{2,1,0:T(8,128)(2,1)S(1)}, bf16[2,48,3456]{2,1,0:T(8,128)(2,1)}, u32[]{:S(2)}, u32[]{:S(2)}) collective-permute-start(bf16[2,48,3456]{2,1,0:T(8,128)(2,1)S(1)} %fusion.69), channel_id=1, source_target_pairs={{0,8},{2,10},{4,12},{6,14},{8,0},{10,2},{12,4},{14,6},{16,24},{18,... | collective-permute-start | bytes 1990664 | tf_op jit(solution)/shard_map/ppermute | solution.py:453
  750.5 8.0 collective-permute-start.39
  753.1 17.6 %collective-permute-start.38 = (bf16[4,48,1152]{2,1,0:T(8,128)(2,1)S(1)}, bf16[4,48,1152]{2,1,0:T(8,128)(2,1)S(1)}, u32[]{:S(2)}, u32[]{:S(2)}) collective-permute-start(bf16[4,48,1152]{2,1,0:T(8,128)(2,1)S(1)} %fusion.82), channel_id=1, source_target_pairs={{0,4},{2,6},{4,0},{6,2},{8,12},{10,14},{12,8},{14,10},{16,20},{18,... | collective-permute-start | bytes 1327112 | tf_op jit(solution)/shard_map/ppermute | solution.py:453
  755.2 15.4 %collective-permute-start.37 = (bf16[1,48,3456]{2,1,0:T(8,128)(2,1)S(1)}, bf16[1,48,3456]{2,1,0:T(8,128)(2,1)S(1)}, u32[]{:S(2)}, u32[]{:S(2)}) collective-permute-start(bf16[1,48,3456]{2,1,0:T(8,128)(2,1)S(1)} %fusion.72), channel_id=1, source_target_pairs={{0,16},{2,18},{4,20},{6,22},{8,24},{10,26},{12,28},{14,30},{16,0},... | collective-permute-start | bytes 995336 | tf_op jit(solution)/shard_map/ppermute | solution.py:453
  773.3 8.9 %collective-permute-start.40 = (bf16[48,3456]{1,0:T(8,128)(2,1)S(1)}, bf16[48,3456]{1,0:T(8,128)(2,1)S(1)}, u32[]{:S(2)}, u32[]{:S(2)}) collective-permute-start(bf16[48,3456]{1,0:T(8,128)(2,1)S(1)} %fusion.83), channel_id=1, source_target_pairs={{0,1},{1,0},{2,3},{3,2},{4,5},{5,4},{6,7},{7,6},{8,9},{9,8},{10,11... | collective-permute-start | bytes 995336 | tf_op jit(solution)/shard_map/ppermute | solution.py:457
  784.8 8.8 %collective-permute-start.43 = (bf16[48,3456]{1,0:T(8,128)(2,1)S(1)}, bf16[48,3456]{1,0:T(8,128)(2,1)S(1)}, u32[]{:S(2)}, u32[]{:S(2)}) collective-permute-start(bf16[48,3456]{1,0:T(8,128)(2,1)S(1)} %broadcast_select_fusion.3), channel_id=1, source_target_pairs={{0,2},{2,0},{4,6},{6,4},{8,10},{10,8},{12,14},{14,12},{16,18},{18,... | collective-permute-start | bytes 995336 | tf_op jit(solution)/shard_map/ppermute | solution.py:460
  785.0 8.6 %collective-permute-start.44 = (bf16[1,48,1152]{2,1,0:T(8,128)(2,1)S(1)}, bf16[1,48,1152]{2,1,0:T(8,128)(2,1)S(1)}, u32[]{:S(2)}, u32[]{:S(2)}) collective-permute-start(bf16[1,48,1152]{2,1,0:T(8,128)(2,1)S(1)} %fusion.114), channel_id=1, source_target_pairs={{0,16},{2,18},{4,20},{6,22},{8,24},{10,26},{12,28},{14,30},{16,0},... | collective-permute-start | bytes 331784 | tf_op jit(solution)/shard_map/ppermute | solution.py:453
  (143 other events, 1488.0 us)
Sparse Core Ops, SparseCore 0:
  13.8 108.8 all-gather.3
  125.6 54.9 all-gather.5

commit v5 on v4

--- a/solution.py
+++ b/solution.py
@@ -11,11 +11,17 @@
 PAIR = 2 * HEAD_SIZE
 FORWARD_ROWS = 512
 BACKWARD_ROWS = 256
+ROW_TILE = 256
+FF_CHUNK = 1024
 
 epsilon = 1e-05
 masked_bias = -1e30
 half = jnp.bfloat16
 single = jnp.float32
+
+
+def estimate(flops, size):
+    return pl.CostEstimate(flops=flops // 16, bytes_accessed=size // 16, transcendentals=0)
 
 
 def contract(left, right, left_dim, right_dim):
@@ -74,11 +80,7 @@
             jax.ShapeDtypeStruct((pairs, 2, length), single),
         ],
         compiler_params=pltpu.CompilerParams(vmem_limit_bytes=56 << 20),
-        cost_estimate=pl.CostEstimate(
-            flops=4 * length * length * features * 4,
-            bytes_accessed=8 * length * features,
-            transcendentals=length * length * features // HEAD_SIZE,
-        ),
+        cost_estimate=estimate(16 * length * length * features, 8 * length * features),
         name="attend_forward",
     )(packed, packed, packed, bias)
 
@@ -162,11 +164,7 @@
         out_shape=jax.ShapeDtypeStruct((length, 3 * features), half),
         scratch_shapes=[pltpu.VMEM((length, PAIR), single)] * 2,
         compiler_params=pltpu.CompilerParams(vmem_limit_bytes=56 << 20),
-        cost_estimate=pl.CostEstimate(
-            flops=10 * length * length * features * 4,
-            bytes_accessed=16 * length * features,
-            transcendentals=length * length * features // HEAD_SIZE,
-        ),
+        cost_estimate=estimate(40 * length * length * features, 16 * length * features),
         name="attend_backward",
     )(packed, packed, packed, bias, upstream, totals, attended)
 
@@ -196,29 +194,356 @@
         out_shape=jax.ShapeDtypeStruct(out_shape, pieces[0].dtype),
         scratch_shapes=[pltpu.SemaphoreType.DMA((len(pieces),))],
         compiler_params=pltpu.CompilerParams(vmem_limit_bytes=32 << 20),
-        cost_estimate=pl.CostEstimate(flops=0, bytes_accessed=size, transcendentals=0),
+        cost_estimate=estimate(0, size),
         name="place_pieces",
     )(indices, *pieces)
 
 
-def layer_norm(hidden, scale_gain, offset):
-    center = hidden - jnp.mean(hidden, axis=-1, keepdims=True)
-    spread = jnp.mean(center * center, axis=-1, keepdims=True)
-    return center * lax.rsqrt(spread + epsilon) * scale_gain + offset
-
-
-def layer_norm_grad(hidden, scale_gain, upstream):
+def normal_of(hidden):
     center = hidden - jnp.mean(hidden, axis=-1, keepdims=True)
     inverse = lax.rsqrt(jnp.mean(center * center, axis=-1, keepdims=True) + epsilon)
-    normal = center * inverse
-    scaled = upstream * scale_gain
+    return center * inverse, inverse
+
+
+def norm_pull(normal, inverse, gain, upstream):
+    scaled = upstream * gain
     slope = jnp.mean(scaled, axis=-1, keepdims=True)
     tilt = jnp.mean(scaled * normal, axis=-1, keepdims=True)
-    return (
-        inverse * (scaled - slope - normal * tilt),
-        jnp.sum(upstream * normal, axis=0),
-        jnp.sum(upstream, axis=0),
-    )
+    return inverse * (scaled - slope - normal * tilt)
+
+
+def column_sum(array):
+    return jnp.sum(array, axis=0, keepdims=True)
+
+
+def tile_of(columns):
+    return pl.BlockSpec((ROW_TILE, columns), lambda i: (i, 0))
+
+
+def resident(shape, *index):
+    place = index or (0,) * len(shape)
+    return pl.BlockSpec(shape, lambda i: place, pipeline_mode=pl.Buffered(1))
+
+
+def row_tiled(kernel, name, length, in_specs, out_specs, out_shape, operands, flops):
+    size = sum(operand.size * operand.dtype.itemsize for operand in operands)
+    size += sum(shape.size * jnp.dtype(shape.dtype).itemsize for shape in out_shape)
+    return pl.pallas_call(
+        kernel,
+        grid=(length // ROW_TILE,),
+        in_specs=in_specs,
+        out_specs=out_specs,
+        out_shape=out_shape,
+        compiler_params=pltpu.CompilerParams(vmem_limit_bytes=56 << 20),
+        cost_estimate=estimate(flops, size),
+        name=name,
+    )(*operands)
+
+
+def project_kernel(hidden_ref, gains_ref, offsets_ref, weight_ref, normed_ref, packed_ref):
+    features = hidden_ref.shape[1]
+    normal, _ = normal_of(hidden_ref[...])
+    normed = (normal * gains_ref[0:1] + offsets_ref[0:1]).astype(half)
+    normed_ref[...] = normed
+    for part in range(3):
+        window = slice(part * features, (part + 1) * features)
+        product = contract(normed, weight_ref[:, window], 1, 0)
+        if part != 1:
+            row = 1 if part == 0 else 2
+            product = product + offsets_ref[row : row + 1]
+        packed_ref[:, window] = product.astype(half)
+
+
+def project(hidden, gains, offsets, joined):
+    length, features = hidden.shape
+    return row_tiled(
+        project_kernel,
+        "project",
+        length,
+        [
+            tile_of(features),
+            resident(gains.shape),
+            resident(offsets.shape),
+            resident((features, 3 * features)),
+        ],
+        [tile_of(features), tile_of(3 * features)],
+        [
+            jax.ShapeDtypeStruct((length, features), half),
+            jax.ShapeDtypeStruct((length, 3 * features), half),
+        ],
+        (hidden, gains, offsets, joined),
+        6 * length * features * features,
+    )
+
+
+def feed_kernel(
+    attended_ref,
+    hidden_ref,
+    gains_ref,
+    offsets_ref,
+    up_bias_ref,
+    out_weight_ref,
+    up_ref,
+    down_ref,
+    middle_ref,
+    second_ref,
+    activated_ref,
+    slope_ref,
+    result_ref,
+):
+    hidden_units = up_ref.shape[1]
+    middle = hidden_ref[...] + (
+        contract(attended_ref[...], out_weight_ref[...], 1, 0) + offsets_ref[3:4]
+    )
+    middle_ref[...] = middle
+    normal, _ = normal_of(middle)
+    second = (normal * gains_ref[1:2] + offsets_ref[4:5]).astype(half)
+    second_ref[...] = second
+    result = middle + offsets_ref[5:6]
+    rate = 0.7978845608028654
+    for start in range(0, hidden_units, FF_CHUNK):
+        window = slice(start, start + FF_CHUNK)
+        value = contract(second, up_ref[:, window], 1, 0) + up_bias_ref[:, window]
+        square = value * value
+        bent = jnp.tanh(value * (rate + (rate * 0.044715) * square))
+        opened = 0.5 + 0.5 * bent
+        activated = (value * opened).astype(half)
+        activated_ref[:, window] = activated
+        curve = (value * (0.5 * rate + (1.5 * rate * 0.044715) * square)) * (1.0 - bent * bent)
+        slope_ref[:, window] = (opened + curve).astype(half)
+        result = result + contract(activated, down_ref[window, :], 1, 0)
+    result_ref[...] = result.astype(result_ref.dtype)
+
+
+def feed(attended, hidden, gains, offsets, up_bias, joined, down, result_type):
+    length, features = hidden.shape
+    units = down.shape[0]
+    out_place = 3
+    up_place = 4 * features // units
+    shape = jax.ShapeDtypeStruct
+    return row_tiled(
+        feed_kernel,
+        "feed",
+        length,
+        [
+            tile_of(features),
+            tile_of(features),
+            resident(gains.shape),
+            resident(offsets.shape),
+            resident(up_bias.shape),
+            resident((features, features), 0, out_place),
+            resident((features, units), 0, up_place),
+            resident(down.shape),
+        ],
+        [tile_of(features), tile_of(features), tile_of(units), tile_of(units), tile_of(features)],
+        [
+            shape((length, features), single),
+            shape((length, features), half),
+            shape((length, units), half),
+            shape((length, units), half),
+            shape((length, features), result_type),
+        ],
+        (attended, hidden, gains, offsets, up_bias, joined, joined, down),
+        2 * length * features * (features + 2 * units),
+    )
+
+
+def feed_grad_kernel(
+    gradient_ref,
+    slope_ref,
+    middle_ref,
+    gains_ref,
+    out_weight_ref,
+    up_ref,
+    down_ref,
+    branch_ref,
+    upper_ref,
+    middle_grad_ref,
+    attention_grad_ref,
+    upstream_ref,
+    sums_ref,
+    unit_sums_ref,
+):
+    units = up_ref.shape[1]
+
+    @pl.when(pl.program_id(0) == 0)
+    def _():
+        sums_ref[...] = jnp.zeros_like(sums_ref)
+        unit_sums_ref[...] = jnp.zeros_like(unit_sums_ref)
+
+    gradient = gradient_ref[...].astype(single)
+    branch = gradient.astype(half)
+    branch_ref[...] = branch
+    sums_ref[0:1] += column_sum(branch.astype(single))
+    second_grad = jnp.zeros(gradient.shape, single)
+    for start in range(0, units, FF_CHUNK):
+        window = slice(start, start + FF_CHUNK)
+        pulled = contract(branch, down_ref[window, :], 1, 1) * slope_ref[:, window].astype(single)
+        upper = pulled.astype(half)
+        upper_ref[:, window] = upper
+        unit_sums_ref[:, window] += column_sum(upper.astype(single))
+        second_grad = second_grad + contract(upper, up_ref[:, window], 1, 1)
+    normal, inverse = normal_of(middle_ref[...])
+    middle_grad = gradient + norm_pull(normal, inverse, gains_ref[1:2], second_grad)
+    sums_ref[1:2] += column_sum(second_grad * normal)
+    sums_ref[2:3] += column_sum(second_grad)
+    middle_grad_ref[...] = middle_grad
+    attention_grad = middle_grad.astype(half)
+    attention_grad_ref[...] = attention_grad
+    sums_ref[3:4] += column_sum(attention_grad.astype(single))
+    upstream_ref[...] = contract(attention_grad, out_weight_ref[...], 1, 1).astype(half)
+
+
+def feed_grad(gradient, slope, middle, gains, joined, down):
+    length, features = middle.shape
+    units = down.shape[0]
+    shape = jax.ShapeDtypeStruct
+    return row_tiled(
+        feed_grad_kernel,
+        "feed_grad",
+        length,
+        [
+            tile_of(features),
+            tile_of(units),
+            tile_of(features),
+            resident(gains.shape),
+            resident((features, features), 0, 3),
+            resident((features, units), 0, 4 * features // units),
+            resident(down.shape),
+        ],
+        [
+            tile_of(features),
+            tile_of(units),
+            tile_of(features),
+            tile_of(features),
+            tile_of(features),
+            resident((8, features)),
+            resident((1, units)),
+        ],
+        [
+            shape((length, features), half),
+            shape((length, units), half),
+            shape((length, features), single),
+            shape((length, features), half),
+            shape((length, features), half),
+            shape((8, features), single),
+            shape((1, units), single),
+        ],
+        (gradient, slope, middle, gains, joined, joined, down),
+        2 * length * features * (features + 2 * units),
+    )
+
+
+def project_grad_kernel(
+    packed_grad_ref, hidden_ref, middle_grad_ref, gains_ref, weight_ref, result_ref, sums_ref
+):
+    features = hidden_ref.shape[1]
+
+    @pl.when(pl.program_id(0) == 0)
+    def _():
+        sums_ref[...] = jnp.zeros_like(sums_ref)
+
+    packed_grad = packed_grad_ref[...]
+    normed_grad = contract(packed_grad, weight_ref[...], 1, 1)
+    normal, inverse = normal_of(hidden_ref[...])
+    result = middle_grad_ref[...] + norm_pull(normal, inverse, gains_ref[0:1], normed_grad)
+    result_ref[...] = result.astype(result_ref.dtype)
+    sums_ref[0:1] += column_sum(normed_grad * normal)
+    sums_ref[1:2] += column_sum(normed_grad)
+    sums_ref[2:3] += column_sum(packed_grad[:, :features].astype(single))
+    sums_ref[3:4] += column_sum(packed_grad[:, 2 * features :].astype(single))
+
+
+def project_grad(packed_grad, hidden, middle_grad, gains, joined, result_type):
+    length, features = hidden.shape
+    shape = jax.ShapeDtypeStruct
+    return row_tiled(
+        project_grad_kernel,
+        "project_grad",
+        length,
+        [
+            tile_of(3 * features),
+            tile_of(features),
+            tile_of(features),
+            resident(gains.shape),
+            resident((features, 3 * features)),
+        ],
+        [tile_of(features), resident((8, features))],
+        [shape((length, features), result_type), shape((8, features), single)],
+        (packed_grad, hidden, middle_grad, gains, joined),
+        6 * length * features * features,
+    )
+
+
+def term_blocks(terms, core, groups, row_unit):
+    pieces = [left.shape[1] // (groups * row_unit) for left, _ in terms]
+    widths = [right.shape[1] // 2 for _, right in terms]
+    total = sum(count * width for count, width in zip(pieces, widths))
+    chips = groups // 2
+    out_shape = (chips, 2, row_unit, total)
+    if row_unit % 16:
+        columns = []
+        for (left, right), count, width in zip(terms, pieces, widths):
+            part = contract(left, right, 0, 0).astype(half)
+            part = part.reshape(chips, 2, count, row_unit, 2, width).transpose(2, 1, 0, 4, 3, 5)
+            columns += [part[piece] for piece in range(count)]
+        whole = jnp.concatenate(columns, axis=-1)
+        return [
+            lax.dynamic_index_in_dim(whole, which, 0, keepdims=False) for which in (1 - core, core)
+        ]
+    number = len(terms)
+
+    def kernel(core_ref, *refs):
+        sources = refs[: 2 * number]
+        other_ref, own_ref = refs[2 * number : 2 * number + 2]
+        buffers = refs[2 * number + 2 : 4 * number + 2]
+        semaphores = refs[4 * number + 2]
+        first_core = core_ref[0] == 0
+        copies = [
+            pltpu.make_async_copy(source, buffer, semaphores.at[index])
+            for index, (source, buffer) in enumerate(zip(sources, buffers))
+        ]
+        for copy in copies:
+            copy.start()
+        start = 0
+        for index, (count, width) in enumerate(zip(pieces, widths)):
+            copies[2 * index].wait()
+            copies[2 * index + 1].wait()
+            left, right = buffers[2 * index], buffers[2 * index + 1]
+            rows = groups * row_unit
+            step = max(size for size in (768, 640, 512, 384, 256, 128) if width % size == 0)
+            held = chips // count
+            for turn in range(count):
+                turned = left[:, turn * rows : (turn + 1) * rows].T
+                some = slice(turn * held, (turn + 1) * held)
+                for low in range(0, 2 * width, step):
+                    product = contract(turned, right[:, low : low + step], 1, 0).astype(half)
+                    product = product.reshape(held, 2, count, row_unit, step)
+                    side, inside = divmod(low, width)
+                    for piece in range(count):
+                        lanes = start + piece * width + inside
+                        lanes = slice(lanes, lanes + step)
+                        even, odd = product[:, 0, piece], product[:, 1, piece]
+                        other_ref[some, side, :, lanes] = jnp.where(first_core, odd, even)
+                        own_ref[some, side, :, lanes] = jnp.where(first_core, even, odd)
+            start += count * width
+
+    anywhere = pl.BlockSpec(memory_space=pl.ANY)
+    operands = [operand for term in terms for operand in term]
+    size = sum(operand.size for operand in operands) * 2
+    flops = sum(2 * left.size * right.shape[1] for left, right in terms)
+    shape = jax.ShapeDtypeStruct(out_shape, half)
+    return pl.pallas_call(
+        kernel,
+        in_specs=[pl.BlockSpec(memory_space=pltpu.SMEM)] + [anywhere] * len(operands),
+        out_specs=[pl.BlockSpec(memory_space=pltpu.VMEM)] * 2,
+        out_shape=[shape, shape],
+        scratch_shapes=[pltpu.VMEM(operand.shape, half) for operand in operands]
+        + [pltpu.SemaphoreType.DMA((len(operands),))],
+        compiler_params=pltpu.CompilerParams(vmem_limit_bytes=60 << 20),
+        cost_estimate=estimate(flops, size + 4 * shape.size),
+        name="term_blocks",
+    )(core.reshape(1).astype(jnp.int32), *operands)
 
 
 def per_device(
@@ -252,19 +577,36 @@
     running = []
 
     def begin(steps, finish):
-        running.append([steps, finish, next(steps)])
-
-    def advance(main):
-        if not running:
+        entry = [steps, finish, next(steps), None]
+        running.append(entry)
+        return entry
+
+    def launch(main, entries):
+        fresh = [entry for entry in entries if entry in running and entry[3] is None]
+        if fresh:
+            sends = [[sent for sent, _, _ in entry[2]] for entry in fresh]
+            main, sends = lax.optimization_barrier((main, sends))
+            for entry, sent in zip(fresh, sends):
+                entry[3] = [
+                    lax.ppermute(part, axis, pairs)
+                    for part, (_, axis, pairs) in zip(sent, entry[2])
+                ]
+        return main
+
+    def advance(main, *only):
+        chosen = [entry for entry in only or list(running) if entry in running]
+        main = launch(main, chosen)
+        if not chosen:
             return main
-        main, flying = lax.optimization_barrier((main, [entry[2] for entry in running]))
-        for entry, arrived in zip(list(running), flying):
+        main, flying = lax.optimization_barrier((main, [entry[3] for entry in chosen]))
+        for entry, arrived in zip(chosen, flying):
+            entry[3] = None
             try:
                 entry[2] = entry[0].send(arrived)
             except StopIteration as stop:
                 entry[1](stop.value)
                 running.remove(entry)
-        return main
+        return launch(main, chosen)
 
     def side_of(array, which, axis):
         return lax.dynamic_index_in_dim(array, which, axis, keepdims=False)
@@ -280,7 +622,7 @@
         current = mine[None]
         bit = groups // 2
         while bit > 1:
-            (received,) = yield [lax.ppermute(current, "wide", pair_up(bit))]
+            (received,) = yield [(current, "wide", pair_up(bit))]
             count = current.shape[0]
             current = place_pieces(
                 [current, received],
@@ -289,8 +631,8 @@
                 bit_of(bit).reshape(1).astype(jnp.int32),
             ).reshape(2 * count, rows, columns)
             bit //= 2
-        (beside,) = yield [lax.ppermute(current, "seq", swap)]
-        passed = yield [lax.ppermute(part, "wide", pair_up(1)) for part in (current, beside)]
+        (beside,) = yield [(current, "seq", swap)]
+        passed = yield [(part, "wide", pair_up(1)) for part in (current, beside)]
         count = current.shape[0]
 
         def target(own_core, own_place):
@@ -330,13 +672,10 @@
         parts = [qkv_weight[layer], out_weight[layer], up_weight[layer], *more]
         return jnp.concatenate(parts, axis=1)
 
-    def split_matrices(joined):
-        return [joined[:, low:high] for low, high in zip(cuts, cuts[1:])]
-
     first_whole = lax.all_gather(beside_each_other(0, side), "wide", axis=0, tiled=True)
     first_down = lax.all_gather(down_weight[0], "wide", axis=0, tiled=True)
     matrices = [None] * layers
-    matrices[0] = split_matrices(first_whole) + [first_down]
+    matrices[0] = (first_whole, first_down)
     small_whole = first_whole[:, cuts[-1] :][:, :side_width].reshape(groups, -1)
     cut_gains = norm_gains.size
     cut_rows = cut_gains + bias_rows.size
@@ -370,14 +709,10 @@
     hidden = my_tokens.astype(single) + my_time
     saved = []
     for layer in range(layers):
-        if layer:
-            matrices[layer] = split_matrices(joined[layer]) + [None]
-        qkv_full, out_full, up_full, down_full = matrices[layer]
+        whole = joined[layer] if layer else first_whole
         gains, offsets = all_gains[layer], all_offsets[layer]
         before = hidden
-        normed = layer_norm(hidden, gains[0], offsets[0]).astype(half)
-        shift = jnp.concatenate([offsets[1], jnp.zeros_like(offsets[1]), offsets[2]])
-        packed = (contract(normed, qkv_full, 1, 0) + shift).astype(half)
+        normed, packed = project(hidden, gains, offsets, whole)
         if layer:
             packed = advance(packed)
         attended, totals = attend_forward(packed, bias)
@@ -388,27 +723,29 @@
                     gather_steps(down_weight[later], True),
                     functools.partial(downs.__setitem__, later),
                 )
+            attended = launch(attended, list(running))
             attended, out_grad = lax.optimization_barrier((attended, out_grad))
             my_upstream = whole_sequence(out_grad)
-        middle = hidden + (contract(attended, out_full, 1, 0) + offsets[3])
-        second = layer_norm(middle, gains[1], offsets[4]).astype(half)
-        if layer:
-            second = advance(second)
-        pre_activation = contract(second, up_full, 1, 0) + all_up_bias[layer]
-        activated = jax.nn.gelu(pre_activation, approximate=True).astype(half)
-        activated = advance(activated)
-        if layer:
+        else:
             while layer not in downs:
-                activated = advance(activated)
-            matrices[layer][3] = down_full = downs[layer]
-        hidden = middle + (contract(activated, down_full, 1, 0) + offsets[5])
+                attended = advance(attended)
+        down = downs[layer] if layer else first_down
+        matrices[layer] = (whole, down)
+        middle, second, activated, slope, hidden = feed(
+            attended,
+            hidden,
+            gains,
+            offsets,
+            all_up_bias[layer][None],
+            whole,
+            down,
+            single if layer < layers - 1 else half,
+        )
         if layer < layers - 1:
             while layer + 1 not in joined:
                 hidden = advance(hidden)
             hidden = advance(hidden)
-        saved.append(
-            (before, normed, packed, totals, attended, middle, second, pre_activation, activated)
-        )
+        saved.append((before, normed, packed, totals, attended, middle, second, activated, slope))
 
     def split_back(result):
         parts = result.reshape(2, -1, features).astype(half)
@@ -416,50 +753,35 @@
 
     output = split_back(hidden)
 
-    def column_half(array, which):
-        count = array.shape[1] // 2
-        return lax.dynamic_slice_in_dim(array, which * count, count, axis=1)
-
     def total_of(addends):
         return functools.reduce(jnp.add, [addend.astype(single) for addend in addends])
 
-    def owner_blocks(array):
-        pieces = array.shape[0] // (groups * row_unit)
-        array = array.reshape(groups // 2, 2, pieces, row_unit, array.shape[1])
-        return [array[:, :, piece] for piece in range(pieces)]
-
-    def reduce_group(terms):
-        sent = [contract(left, column_half(right, 1 - core), 0, 0).astype(half) for left, right in terms]
-        sent = [lax.ppermute(part, "wide", pair_up(1)) for part in sent]
-        kept = [contract(left, column_half(right, core), 0, 0).astype(half) for left, right in terms]
-        arrived = yield sent
-        counts, blocks = [], ([], [])
-        for own, other in zip(kept, arrived):
-            own_blocks, other_blocks = owner_blocks(own), owner_blocks(other)
-            counts.append((len(own_blocks), own.shape[1]))
-            for pair in zip(own_blocks, other_blocks):
-                for side in range(2):
-                    which = place if side == 0 else 1 - place
-                    chosen = [side_of(part, which, 1) for part in pair]
-                    blocks[side].append(total_of(chosen).astype(half))
-        (received,) = yield [lax.ppermute(jnp.concatenate(blocks[1], axis=-1), "seq", swap)]
-        addends = [jnp.concatenate(blocks[0], axis=-1), received]
-        width = received.shape[-1]
-        bit = 2
-        while bit < groups:
-            views = [addend.reshape(-1, 2, row_unit, width) for addend in addends]
-            mine = bit_of(bit)
-            sent = total_of([side_of(view, 1 - mine, 1) for view in views]).astype(half)
-            (received,) = yield [lax.ppermute(sent, "wide", pair_up(bit))]
-            addends = [side_of(view, mine, 1) for view in views] + [received]
-            bit *= 2
-        current = total_of(addends).astype(half).reshape(row_unit, width)
-        (other,) = yield [lax.ppermute(current, "seq", swap)]
-        same = place == core
-        owned = jnp.where(same, current, other)
-        (received,) = yield [lax.ppermute(jnp.where(same, other, current), "wide", pair_up(1))]
-        low = jnp.where(core == 0, owned, received)
-        high = jnp.where(core == 0, received, owned)
+    chip_bits = [1 << number for number in range(groups.bit_length() - 2, 0, -1)]
+
+    def reduce_group(terms, spread):
+        other, own = term_blocks(terms, core, groups, row_unit)
+        counts = [(left.shape[1] // (groups * row_unit), right.shape[1] // 2) for left, right in terms]
+        (received,) = yield [(other, "wide", pair_up(1))]
+        width = own.shape[-1]
+        axes = chip_bits + ["seq"]
+        addends = [part.reshape((2,) * len(axes) + (row_unit, width)) for part in (own, received)]
+        for stage in (["seq"] if spread else []) + chip_bits[::-1]:
+            axis = axes.index(stage)
+            mine = place if stage == "seq" else bit_of(stage)
+            sent = total_of([side_of(part, 1 - mine, axis) for part in addends]).astype(half)
+            if stage == "seq":
+                (received,) = yield [(sent, "seq", swap)]
+            else:
+                (received,) = yield [(sent, "wide", pair_up(stage))]
+            addends = [side_of(part, mine, axis) for part in addends] + [received]
+            axes.remove(stage)
+        current = total_of(addends).astype(half)
+        (received,) = yield [(current, "seq", swap)]
+        if spread:
+            low = jnp.where(place == 0, current, received).astype(single)
+            high = jnp.where(place == 0, received, current).astype(single)
+        else:
+            low, high = current.astype(single) + received.astype(single)
         shares, start = [], 0
         for count, each in counts:
             rows = []
@@ -467,7 +789,7 @@
                 window = slice(start, start + each)
                 rows.append(jnp.concatenate([low[:, window], high[:, window]], axis=1))
                 start += each
-            shares.append(jnp.concatenate(rows, axis=0).astype(single))
+            shares.append(jnp.concatenate(rows, axis=0))
         return shares
 
     def reduce_small(array):
@@ -476,77 +798,65 @@
             view = array.reshape(-1, 2, array.shape[-1])
             mine = bit_of(bit)
             sent = side_of(view, 1 - mine, 1)
-            (received,) = yield [lax.ppermute(sent, "wide", pair_up(bit))]
+            (received,) = yield [(sent, "wide", pair_up(bit))]
             array = side_of(view, mine, 1) + received
             bit *= 2
-        (received,) = yield [lax.ppermute(array, "seq", swap)]
+        (received,) = yield [(array, "seq", swap)]
         return (array + received)[0]
 
     weight_grads = [[None] * 4 for _ in range(layers)]
 
-    def begin_group(layer, parts, terms):
+    def begin_group(spread, *named):
         def finish(shares):
-            for part, share in zip(parts, shares):
+            for (layer, part, _), share in zip(named, shares):
                 weight_grads[layer][part] = share
 
-        begin(reduce_group(terms), finish)
-
-    gradient = my_upstream.astype(single)
+        return begin(reduce_group([term for _, _, term in named], spread), finish)
+
+    gradient = my_upstream
     small_grads = [None] * layers
+    waiting = []
     for layer in range(layers - 1, -1, -1):
-        qkv_full, out_full, up_full, down_full = matrices[layer]
+        whole, down = matrices[layer]
         gains = all_gains[layer]
-        (hidden, normed, packed, totals, attended, middle, second, pre_activation, activated) = (
-            saved[layer]
+        hidden, normed, packed, totals, attended, middle, second, activated, slope = saved[layer]
+        early = None
+        if layer < layers - 1:
+            branch = gradient.astype(half)
+            early = begin_group(True, *waiting, (layer, 3, (activated, branch)))
+            gradient = launch(gradient, [early])
+            waiting = []
+        branch, upper, middle_grad, attention_grad, upstream, sums, unit_sums = feed_grad(
+            gradient, slope, middle, gains, whole, down
         )
-        branch = gradient.astype(half)
-        down_bias_grad = jnp.sum(branch, axis=0, dtype=single)
-        activated_grad = contract(branch, down_full, 1, 1)
-        pull = jax.vjp(lambda value: jax.nn.gelu(value, approximate=True), pre_activation)[1]
-        upper = pull(activated_grad)[0].astype(half)
-        upper = advance(upper)
-        first_batch = ((3, 2), ((activated, branch), (second, upper)))
+        upstream = advance(upstream)
+        named = [(layer, 2, (second, upper)), (layer, 1, (attended, attention_grad))]
+        if early is None:
+            named = [(layer, 3, (activated, branch))] + named
+        entry = begin_group(False, *named)
+        upstream = launch(upstream, [entry])
+        if layer == 0:
+            upstream = advance(upstream, entry)
+        packed_grad = attend_backward(packed, bias, upstream, totals, attended)
+        if layer == layers - 1:
+            packed_grad, output = lax.optimization_barrier((packed_grad, output))
+            output = output.astype(single)
+        packed_grad = advance(packed_grad)
+        last = (layer, 0, (normed, packed_grad))
         if layer:
-            begin_group(layer, *first_batch)
-        up_bias_grad = jnp.sum(upper, axis=0, dtype=single)
-        second_grad = contract(upper, up_full, 1, 1)
-        middle_part, second_gain, second_offset = layer_norm_grad(middle, gains[1], second_grad)
-        middle_grad = gradient + middle_part
-        attention_grad = middle_grad.astype(half)
-        out_bias_grad = jnp.sum(attention_grad, axis=0, dtype=single)
-        attention_grad = advance(attention_grad)
-        if not layer:
-            begin_group(layer, (3, 2, 1), first_batch[1] + ((attended, attention_grad),))
-        upstream = contract(attention_grad, out_full, 1, 1).astype(half)
-        if not layer:
-            upstream = advance(upstream)
-        if layer == layers - 1:
-            upstream, output = lax.optimization_barrier((upstream, output))
-            output = output.astype(single)
-        packed_grad = attend_backward(packed, bias, upstream, totals, attended)
-        packed_grad = advance(packed_grad)
-        if layer:
-            begin_group(layer, (0, 1), ((normed, packed_grad), (attended, attention_grad)))
+            waiting = [last]
         else:
-            begin_group(layer, (0,), ((normed, packed_grad),))
-        column_sums = jnp.sum(packed_grad, axis=0, dtype=single)
-        normed_grad = contract(packed_grad, qkv_full, 1, 1)
-        hidden_part, first_gain, first_offset = layer_norm_grad(hidden, gains[0], normed_grad)
-        gradient = advance(middle_grad + hidden_part)
+            entry = begin_group(False, last)
+            packed_grad = advance(packed_grad, entry)
+        gradient, more_sums = project_grad(
+            packed_grad, hidden, middle_grad, gains, whole, single if layer else half
+        )
         small_grads[layer] = (
-            jnp.stack([first_gain, second_gain]),
-            jnp.stack(
-                [
-                    first_offset,
-                    column_sums[:features],
-                    column_sums[2 * features :],
-                    out_bias_grad,
-                    second_offset,
-                    down_bias_grad,
-                ]
-            ),
-            up_bias_grad,
+            jnp.stack([more_sums[0], sums[1]]),
+            jnp.stack([more_sums[1], more_sums[2], more_sums[3], sums[3], sums[2], sums[0]]),
+            unit_sums[0],
         )
+
     def by_owner(parts):
         stacked = jnp.stack(parts)
         stacked = stacked.reshape(layers, -1, groups, stacked.shape[-1] // groups)

time: 829 us -> 775 us (0.935)
  matrix products: 213 us -> 0 us
  Pallas kernels: 132 us -> 323 us
  waiting for transfers between devices: 176 us -> 276 us
  local copies, waits for them, and re-layouts: 84.7 us -> 28.6 us
  other arithmetic: 115 us -> 64.4 us
  starting transfers between devices: 76.5 us -> 56.2 us
    dot_general x32 -> x0, matrix products: 213 us -> none  [contract(): lax.dot_general(left, right, (((left_dim,), (right_dim,)), ((), ())), pre...]
    pallas_call x0 -> x12, Pallas kernels: none -> 190 us  [the longest x8 129 us: row_tiled(): pl.pallas_call(kernel, grid=(length // ROW_TILE,), in_specs=in_specs, out...]
    all_to_all x3, waiting for transfers between devices: 16.3 us -> 66.5 us  [whole_sequence(): lax.all_to_all(part, 'seq', split_axis=0, concat_axis=1, tiled=True)[0]]
    ppermute x49 -> x38, waiting for transfers between devices: 144 us -> 194 us  [launch(): lax.ppermute(part, axis, pairs)]
    reduce_sum x17 -> x0, other arithmetic: 34.3 us -> none  [the longest x4 13.2 us: layer_norm_grad(): jnp.sum(upstream * normal, axis=0)]
    ppermute x49 -> x38, starting transfers between devices: 53.7 us -> 36.4 us  [launch(): lax.ppermute(part, axis, pairs)]
    convert_element_type x28 -> x19, other arithmetic: 32.1 us -> 47.5 us  [the longest x13 36.4 us: reduce_group(): total_of([side_of(part, 1 - mine, axis) for part in addends]).astype(half)]
    dot_general x4 -> x0, local copies, waits for them, and re-layouts: 15.2 us -> none  [contract(): lax.dot_general(left, right, (((left_dim,), (right_dim,)), ((), ())), pre...]
  transfers between devices with their start and end apart: 56 -> 45, of which waited for: 23 -> 20; matrix products, arithmetic and copies ran while one was open for 35% -> 4% of each run, Pallas kernels for 16% -> 32%
where the time goes in v5:
time: 775 us; the launch traced here: 764 us
  Pallas kernels  323 us (42%)
  waiting for transfers between devices  276 us (36%)
  other arithmetic  64.4 us (8%)
  starting transfers between devices  56.2 us (7%)
  local copies, waits for them, and re-layouts  28.6 us (4%)
  between operations  15.5 us (2%)
    ppermute x38, waiting for transfers between devices, launch(): lax.ppermute(part, axis, pairs)  194 us
    pallas_call x8, Pallas kernels, row_tiled(): pl.pallas_call(kernel, grid=(length // ROW_TILE,), in_specs=in_specs, out...  129 us
    pallas_call x2, Pallas kernels, attend_backward(): pl.pallas_call(functools.partial(attend_grad_kernel, rows=BACKWARD_ROWS),...  74.3 us
    all_to_all x3, waiting for transfers between devices, whole_sequence(): lax.all_to_all(part, 'seq', split_axis=0, concat_axis=1, tiled=True)[0]  66.5 us
    pallas_call x4, Pallas kernels, term_blocks(): pl.pallas_call(kernel, in_specs=[pl.BlockSpec(memory_space=pltpu.SMEM)] +...  61.2 us
    pallas_call x2, Pallas kernels, attend_forward(): pl.pallas_call(functools.partial(attend_kernel, rows=FORWARD_ROWS), grid=...  50.4 us
    ppermute x38, starting transfers between devices, launch(): lax.ppermute(part, axis, pairs)  36.4 us
    convert_element_type x13, other arithmetic, reduce_group(): total_of([side_of(part, 1 - mine, axis) for part in addends]).astype(half)  36.4 us
  transfers between devices with their start and end apart: 45, of which 20 were waited for; matrix products, arithmetic and copies ran while one was open for 4% of the time, Pallas kernels for 32%

profile of v5, /device:TPU:0, one launch (start us, length us, event | category | flops | bytes accessed | tf_op | source)
XLA Modules:
  0.0 763.6 jit_solution(14327001413509140495)
XLA Ops:
  11.9 4.2 all-to-all-start
  16.4 19.9 %all-to-all-done = bf16[2,512,768]{2,1,0:T(8,128)(2,1)S(1)} async-done(((bf16[2,512,768]{2,1,0:T(8,128)(2,1)}), bf16[2,512,768]{2,1,0:T(8,128)(2,1)S(1)}, u32[]{:S(2)}, u32[]{:S(2)}) %all-to-all-start) | async-done | bytes 1572896 | tf_op jit(solution)/shard_map/all_to_all | solution.py:569
  40.2 17.8 %collective-permute-done.refs_1_ = bf16[1,48,3072]{2,1,0:T(8,128)(2,1)S(1)} collective-permute-done((bf16[1,48,3072]{2,1,0:T(8,128)(2,1)S(1)}, bf16[1,48,3072]{2,1,0:T(8,128)(2,1)S(1)}, u32[]{:S(2)}, u32[]{:S(2)}) %collective-permute-start) | collective-permute-done | bytes 294944 | tf_op jit(solution)/shard_map/ppermute | solution.py:591
  58.3 47.3 %collective-permute-done.1.refs_1_ = bf16[2,48,3072]{2,1,0:T(8,128)(2,1)S(1)} collective-permute-done((bf16[2,48,3072]{2,1,0:T(8,128)(2,1)S(1)}, bf16[2,48,3072]{2,1,0:T(8,128)(2,1)S(1)}, u32[]{:S(2)}, u32[]{:S(2)}) %collective-permute-start.1) | collective-permute-done | bytes 589856 | tf_op jit(solution)/shard_map/ppermute | solution.py:591
  107.3 29.1 %collective-permute-done.2.refs_1_ = bf16[4,48,3072]{2,1,0:T(8,128)(2,1)S(1)} collective-permute-done((bf16[4,48,3072]{2,1,0:T(8,128)(2,1)S(1)}, bf16[4,48,3072]{2,1,0:T(8,128)(2,1)S(1)}, u32[]{:S(2)}, u32[]{:S(2)}) %collective-permute-start.2) | collective-permute-done | bytes 1179680 | tf_op jit(solution)/shard_map/ppermute | solution.py:591
  141.2 3.2 all-to-all-start.1
  144.5 46.6 %all-to-all-done.1 = s32[2,512,2]{1,2,0:T(2,128)S(1)} async-done(((s32[2,512,2]{1,2,0:T(2,128)}), s32[2,512,2]{1,2,0:T(2,128)S(1)}, u32[]{:S(2)}, u32[]{:S(2)}) %all-to-all-start.1) | async-done | bytes 8224 | tf_op jit(solution)/shard_map/all_to_all | solution.py:569
  199.9 8.9 %project.2 = (bf16[1024,768]{1,0:T(8,128)(2,1)}, bf16[1024,2304]{1,0:T(8,128)(2,1)}) custom-call(f32[1024,768]{1,0:T(8,128)} %convert_add_fusion.hidden_ref, f32[2,768]{1,0:T(2,128)} %squeeze.178.gains_ref, f32[6,768]{1,0:T(8,128)} %squeeze.179.offsets_ref, bf16[768,6272]{1,0:T(8,128)(2,1)} %all-gather.4.cloned.1.call-done.weight_ref.out_weight_ref.up_ref), custom_call_target="tpu_custom_call" | custom-call | flops 226492416 | bytes 1193472 | tf_op jit(solution)/shard_map/project/pallas_call | solution.py:231
  208.8 25.2 %attend_forward.2 = (bf16[1024,768]{1,0:T(8,128)(2,1)}, f32[6,2,1024]{2,1,0:T(2,128)}) custom-call(bf16[1024,2304]{1,0:T(8,128)(2,1)} %get-tuple-element.188.query_ref.key_ref.value_ref, bf16[1024,2304]{1,0:T(8,128)(2,1)} %get-tuple-element.188.query_ref.key_ref.value_ref, bf16[1024,2304]{1,0:T(8,128)(2,1)} %get-tuple-element.188.query_ref.key_ref.value_ref, ...), custom_call_target="tpu_custom_call" | custom-call | flops 805306368 | bytes 393216 | tf_op jit(solution)/shard_map/attend_forward/pallas_call | solution.py:68
  236.1 24.1 %feed.2 = (f32[1024,768]{1,0:T(8,128)}, bf16[1024,768]{1,0:T(8,128)(2,1)}, bf16[1024,3072]{1,0:T(8,128)(2,1)}, bf16[1024,3072]{1,0:T(8,128)(2,1)}, f32[1024,768]{1,0:T(8,128)}) custom-call(bf16[1024,768]{1,0:T(8,128)(2,1)} %get-tuple-element.195.attended_ref.refs_2_, f32[1024,768]{1,0:T(8,128)} %convert_add_fusion.hidden_ref, f32[2,768]{1,0:T(2,128)} %squeeze.178.gains_ref, ...), custom_call_target="tpu_custom_call" | custom-call | flops 679477248 | bytes 3074304 | tf_op jit(solution)/shard_map/feed/pallas_call | solution.py:231
  260.7 9.0 %collective-permute-done.7.refs_1_ = bf16[2,96,768]{2,1,0:T(8,128)(2,1)S(1)} collective-permute-done((bf16[2,96,768]{2,1,0:T(8,128)(2,1)S(1)}, bf16[2,96,768]{2,1,0:T(8,128)(2,1)S(1)}, u32[]{:S(2)}, u32[]{:S(2)}) %collective-permute-start.7) | collective-permute-done | bytes 294944 | tf_op jit(solution)/shard_map/ppermute | solution.py:591
  275.8 3.9 place_pieces.13
  279.7 3.5 copy-done.2
  283.2 9.0 %project.3 = (bf16[1024,768]{1,0:T(8,128)(2,1)}, bf16[1024,2304]{1,0:T(8,128)(2,1)}) custom-call(f32[1024,768]{1,0:T(8,128)} %get-tuple-element.206.hidden_ref, f32[2,768]{1,0:T(2,128)} %squeeze.182.gains_ref, f32[6,768]{1,0:T(8,128)} %squeeze.183.offsets_ref, bf16[768,6144]{1,0:T(8,128)(2,1)} %bitcast.220), custom_call_target="tpu_custom_call" | custom-call | flops 226492416 | bytes 1181184 | tf_op jit(solution)/shard_map/project/pallas_call | solution.py:231
  294.4 25.2 %attend_forward.3 = (bf16[1024,768]{1,0:T(8,128)(2,1)}, f32[6,2,1024]{2,1,0:T(2,128)}) custom-call(bf16[1024,2304]{1,0:T(8,128)(2,1)} %get-tuple-element.213.query_ref.key_ref.value_ref, bf16[1024,2304]{1,0:T(8,128)(2,1)} %get-tuple-element.213.query_ref.key_ref.value_ref, bf16[1024,2304]{1,0:T(8,128)(2,1)} %get-tuple-element.213.query_ref.key_ref.value_ref, ...), custom_call_target="tpu_custom_call" | custom-call | flops 805306368 | bytes 393216 | tf_op jit(solution)/shard_map/attend_forward/pallas_call | solution.py:68
  320.2 4.7 all-to-all-start.2
  330.6 23.9 %feed.3 = (f32[1024,768]{1,0:T(8,128)}, bf16[1024,768]{1,0:T(8,128)(2,1)}, bf16[1024,3072]{1,0:T(8,128)(2,1)}, bf16[1024,3072]{1,0:T(8,128)(2,1)}, bf16[1024,768]{1,0:T(8,128)(2,1)}) custom-call(bf16[1024,768]{1,0:T(8,128)(2,1)} %get-tuple-element.222.attended_ref.refs_4_, f32[1024,768]{1,0:T(8,128)} %get-tuple-element.206.hidden_ref, ...), custom_call_target="tpu_custom_call" | custom-call | flops 679477248 | bytes 2951424 | tf_op jit(solution)/shard_map/feed/pallas_call | solution.py:231
  354.5 21.1 %feed_grad.2 = (bf16[1024,768]{1,0:T(8,128)(2,1)}, bf16[1024,3072]{1,0:T(8,128)(2,1)}, f32[1024,768]{1,0:T(8,128)}, bf16[1024,768]{1,0:T(8,128)(2,1)}, bf16[1024...) custom-call(bf16[1024,768]{1,0:T(8,128)(2,1)} %bitcast.27.gradient_ref, ...), custom_call_target="tpu_custom_call" | custom-call | flops 679477248 | bytes 3050112 | tf_op jit(solution)/shard_map/feed_grad/pallas_call | solution.py:231
  375.6 21.0 %term_blocks.4 = (bf16[8,2,48,3456]{3,2,1,0:T(8,128)(2,1)}, bf16[8,2,48,3456]{3,2,1,0:T(8,128)(2,1)}) custom-call(s32[1]{0:T(128)} %bitcast.23.core_ref, bf16[1024,3072]{1,0:T(8,128)(2,1)} %get-tuple-element.228.refs_0_, bf16[1024,768]{1,0:T(8,128)(2,1)} %get-tuple-element.229.refs_1_, bf16[1024,768]{1,0:T(8,128)(2,1)} %get-tuple-element.230.refs_2_, ...), custom_call_target="tpu_custom_call" | custom-call | flops 679477248 | bytes 1843200 | tf_op jit(solution)/shard_map/term_blocks/pallas_call | solution.py:536
  396.6 3.7 all-to-all-start.3
  400.3 37.2 %attend_backward.2.packed_grad_ref.refs_1_ = bf16[1024,2304]{1,0:T(8,128)(2,1)} custom-call(bf16[1024,2304]{1,0:T(8,128)(2,1)} %get-tuple-element.213.query_ref.key_ref.value_ref, bf16[1024,2304]{1,0:T(8,128)(2,1)} %get-tuple-element.213.query_ref.key_ref.value_ref, bf16[1024,2304]{1,0:T(8,128)(2,1)} %get-tuple-element.213.query_ref.key_ref.value_ref, ...), custom_call_target="tpu_custom_call" | custom-call | flops 2013265920 | bytes 786432 | tf_op jit(solution)/shard_map/attend_backward/pallas_call | solution.py:151
  437.5 4.7 fusion.3
  442.1 10.7 %project_grad.2 = (f32[1024,768]{1,0:T(8,128)}, f32[8,768]{1,0:T(8,128)}) custom-call(bf16[1024,2304]{1,0:T(8,128)(2,1)} %attend_backward.2.packed_grad_ref.refs_1_, f32[1024,768]{1,0:T(8,128)} %get-tuple-element.206.hidden_ref, f32[1024,768]{1,0:T(8,128)} %get-tuple-element.244.middle_grad_ref, f32[2,768]{1,0:T(2,128)} %squeeze.182.gains_ref, ...), custom_call_target="tpu_custom_call" | custom-call | flops 226492416 | bytes 1476480 | tf_op jit(solution)/shard_map/project_grad/pallas_call | solution.py:231
  452.8 3.2 convert_element_type.446.refs_3_
  456.1 17.8 %term_blocks.5 = (bf16[8,2,48,2688]{3,2,1,0:T(8,128)(2,1)}, bf16[8,2,48,2688]{3,2,1,0:T(8,128)(2,1)}) custom-call(s32[1]{0:T(128)} %bitcast.23.core_ref, bf16[1024,768]{1,0:T(8,128)(2,1)} %get-tuple-element.246.refs_0_, bf16[1024,2304]{1,0:T(8,128)(2,1)} %attend_backward.2.packed_grad_ref.refs_1_, bf16[1024,3072]{1,0:T(8,128)(2,1)} %get-tuple-element.247.refs_2_, ...), custom_call_target="tpu_custom_call" | custom-call | flops 528482304 | bytes 1400832 | tf_op jit(solution)/shard_map/term_blocks/pallas_call | solution.py:536
  474.9 21.2 %feed_grad.3 = (bf16[1024,768]{1,0:T(8,128)(2,1)}, bf16[1024,3072]{1,0:T(8,128)(2,1)}, f32[1024,768]{1,0:T(8,128)}, bf16[1024,768]{1,0:T(8,128)(2,1)}, bf16[1024...) custom-call(f32[1024,768]{1,0:T(8,128)} %get-tuple-element.249.gradient_ref, ...), custom_call_target="tpu_custom_call" | custom-call | flops 679477248 | bytes 3172992 | tf_op jit(solution)/shard_map/feed_grad/pallas_call | solution.py:231
  496.2 12.7 %term_blocks.6 = (bf16[8,2,48,1920]{3,2,1,0:T(8,128)(2,1)}, bf16[8,2,48,1920]{3,2,1,0:T(8,128)(2,1)}) custom-call(s32[1]{0:T(128)} %bitcast.23.core_ref, bf16[1024,768]{1,0:T(8,128)(2,1)} %get-tuple-element.260.refs_0_, bf16[1024,3072]{1,0:T(8,128)(2,1)} %get-tuple-element.261.refs_1_, bf16[1024,768]{1,0:T(8,128)(2,1)} %get-tuple-element.195.attended_ref.refs_2_, ...), custom_call_target="tpu_custom_call" | custom-call | flops 377487360 | bytes 1056768 | tf_op jit(solution)/shard_map/term_blocks/pallas_call | solution.py:536
  508.9 25.4 %collective-permute-done.13 = bf16[2,2,2,48,3456]{4,3,2,1,0:T(8,128)(2,1)} collective-permute-done((bf16[2,2,2,48,3456]{4,3,2,1,0:T(8,128)(2,1)}, bf16[2,2,2,48,3456]{4,3,2,1,0:T(8,128)(2,1)}, u32[]{:S(2)}, u32[]{:S(2)}) %collective-permute-start.13) | collective-permute-done | bytes 2654240 | tf_op jit(solution)/shard_map/ppermute | solution.py:591
  534.3 4.2 fusion.5
  538.5 3.8 fusion.4
  544.3 3.4 collective-permute-done.15
  551.0 37.1 %attend_backward.3.refs_1_.packed_grad_ref = bf16[1024,2304]{1,0:T(8,128)(2,1)} custom-call(bf16[1024,2304]{1,0:T(8,128)(2,1)} %get-tuple-element.188.query_ref.key_ref.value_ref, bf16[1024,2304]{1,0:T(8,128)(2,1)} %get-tuple-element.188.query_ref.key_ref.value_ref, bf16[1024,2304]{1,0:T(8,128)(2,1)} %get-tuple-element.188.query_ref.key_ref.value_ref, ...), custom_call_target="tpu_custom_call" | custom-call | flops 2013265920 | bytes 786432 | tf_op jit(solution)/shard_map/attend_backward/pallas_call | solution.py:151
  590.3 3.0 fusion.8
  593.3 3.2 fusion.6
  596.4 2.9 fusion.11
  599.3 9.8 %term_blocks.7 = (bf16[8,2,48,1152]{3,2,1,0:T(8,128)(2,1)}, bf16[8,2,48,1152]{3,2,1,0:T(8,128)(2,1)}) custom-call(s32[1]{0:T(128)} %bitcast.23.core_ref, bf16[1024,768]{1,0:T(8,128)(2,1)} %get-tuple-element.279.refs_0_, bf16[1024,2304]{1,0:T(8,128)(2,1)} %attend_backward.3.refs_1_.packed_grad_ref), custom_call_target="tpu_custom_call" | custom-call | flops 226492416 | bytes 614400 | tf_op jit(solution)/shard_map/term_blocks/pallas_call | solution.py:536
  609.9 3.1 collective-permute-done.19
  613.1 2.9 fusion.14
  617.3 10.0 %project_grad.3 = (bf16[1024,768]{1,0:T(8,128)(2,1)}, f32[8,768]{1,0:T(8,128)}) custom-call(bf16[1024,2304]{1,0:T(8,128)(2,1)} %attend_backward.3.refs_1_.packed_grad_ref, f32[1024,768]{1,0:T(8,128)} %convert_add_fusion.hidden_ref, f32[1024,768]{1,0:T(8,128)} %get-tuple-element.287.middle_grad_ref, f32[2,768]{1,0:T(2,128)} %squeeze.178.gains_ref, ...), custom_call_target="tpu_custom_call" | custom-call | flops 226492416 | bytes 1390464 | tf_op jit(solution)/shard_map/project_grad/pallas_call | solution.py:231
  627.3 3.9 all-to-all-start.4
  634.9 15.6 %all-to-all-done.4 = bf16[2,512,768]{2,1,0:T(8,128)(2,1)S(1)} async-done(((bf16[2,512,768]{2,1,0:T(8,128)(2,1)}), bf16[2,512,768]{2,1,0:T(8,128)(2,1)S(1)}, u32[]{:S(2)}, u32[]{:S(2)}) %all-to-all-start.4) | async-done | bytes 1572896 | tf_op jit(solution)/shard_map/all_to_all | solution.py:752
  650.5 13.1 %collective-permute-done.20 = bf16[2,48,3456]{2,1,0:T(8,128)(2,1)} collective-permute-done((bf16[2,48,3456]{2,1,0:T(8,128)(2,1)}, bf16[2,48,3456]{2,1,0:T(8,128)(2,1)}, u32[]{:S(2)}, u32[]{:S(2)}) %collective-permute-start.20) | collective-permute-done | bytes 663584 | tf_op jit(solution)/shard_map/ppermute | solution.py:591
  671.3 3.1 fusion.10
  684.2 21.1 %collective-permute-done.27 = bf16[2,48,1920]{2,1,0:T(8,128)(2,1)S(1)} collective-permute-done((bf16[2,48,1920]{2,1,0:T(8,128)(2,1)}, bf16[2,48,1920]{2,1,0:T(8,128)(2,1)S(1)}, u32[]{:S(2)}, u32[]{:S(2)}) %collective-permute-start.27) | collective-permute-done | bytes 368672 | tf_op jit(solution)/shard_map/ppermute | solution.py:591
  714.8 3.1 collective-permute-start.33
  719.7 4.0 collective-permute-done.33
  723.7 10.8 %collective-permute-done.32 = bf16[2,48,1152]{2,1,0:T(8,128)(2,1)S(1)} collective-permute-done((bf16[2,48,1152]{2,1,0:T(8,128)(2,1)S(1)}, bf16[2,48,1152]{2,1,0:T(8,128)(2,1)S(1)}, u32[]{:S(2)}, u32[]{:S(2)}) %collective-permute-start.32) | collective-permute-done | bytes 221216 | tf_op jit(solution)/shard_map/ppermute | solution.py:591
  744.1 3.9 collective-permute-done.35
  (260 shorter events, 101.9 us)
Async XLA Ops:
  7.2 137.2 %copy-start = (f32[2,768]{1,0:T(2,128)S(1)}, f32[2,768]{1,0:T(2,128)}, u32[]{:S(2)}) copy-start(f32[2,768]{1,0:T(2,128)} %param.13) | copy-start | bytes 18436
  7.2 188.5 %all-gather.4.cloned.1.call-start = ((), (), s32[]{:S(2)}) async-start(), calls=%async_computation.5 | async-start | bytes 10235904 | tf_op jit(solution)/shard_map/all_gather | solution.py:675
  11.0 225.1 %all-gather.6.cloned.1.call-start = ((), (), s32[]{:S(2)}) async-start(), calls=%async_computation.6 | async-start | bytes 5013504 | tf_op jit(solution)/shard_map/all_gather | solution.py:676
  11.9 24.4 %all-to-all-start = ((bf16[2,512,768]{2,1,0:T(8,128)(2,1)}), bf16[2,512,768]{2,1,0:T(8,128)(2,1)S(1)}, u32[]{:S(2)}, u32[]{:S(2)}) async-start(bf16[2,512,768]{2,1,0:T(8,128)(2,1)} %param.12), calls=%async_computation | async-start | bytes 3145728 | tf_op jit(solution)/shard_map/all_to_all | solution.py:569
  37.4 20.6 %collective-permute-start = (bf16[1,48,3072]{2,1,0:T(8,128)(2,1)S(1)}, bf16[1,48,3072]{2,1,0:T(8,128)(2,1)S(1)}, u32[]{:S(2)}, u32[]{:S(2)}) collective-permute-start(bf16[1,48,3072]{2,1,0:T(8,128)(2,1)S(1)} %fusion.28.refs_0_), channel_id=1, source_target_pairs={{0,16},{2,18},{4,20},{6,22},{8,24},{10,26},{12,28},{14,30},{16,0},... | collective-permute-start | bytes 884744 | tf_op jit(solution)/shard_map/ppermute | solution.py:591
  58.2 47.4 %collective-permute-start.1 = (bf16[2,48,3072]{2,1,0:T(8,128)(2,1)S(1)}, bf16[2,48,3072]{2,1,0:T(8,128)(2,1)S(1)}, u32[]{:S(2)}, u32[]{:S(2)}) collective-permute-start(bf16[2,48,3072]{2,1,0:T(8,128)(2,1)S(1)} %bitcast.238), channel_id=1, source_target_pairs={{0,8},{2,10},{4,12},{6,14},{8,0},{10,2},{12,4},{14,6},{16,24},{18,... | collective-permute-start | bytes 1769480 | tf_op jit(solution)/shard_map/ppermute | solution.py:591
  105.8 30.6 %collective-permute-start.2 = (bf16[4,48,3072]{2,1,0:T(8,128)(2,1)S(1)}, bf16[4,48,3072]{2,1,0:T(8,128)(2,1)S(1)}, u32[]{:S(2)}, u32[]{:S(2)}) collective-permute-start(bf16[4,48,3072]{2,1,0:T(8,128)(2,1)S(1)} %bitcast.234), channel_id=1, source_target_pairs={{0,4},{2,6},{4,0},{6,2},{8,12},{10,14},{12,8},{14,10},{16,20},{18,... | collective-permute-start | bytes 3538952 | tf_op jit(solution)/shard_map/ppermute | solution.py:591
  139.0 95.0 %collective-permute-start.3 = (bf16[8,48,3072]{2,1,0:T(8,128)(2,1)S(1)}, bf16[8,48,3072]{2,1,0:T(8,128)(2,1)}, u32[]{:S(2)}, u32[]{:S(2)}) collective-permute-start(bf16[8,48,3072]{2,1,0:T(8,128)(2,1)S(1)} %bitcast.228), channel_id=1, source_target_pairs={{0,1},{1,0},{2,3},{3,2},{4,5},{5,4},{6,7},{7,6},{8,9},{9,8},{10,11... | collective-permute-start | bytes 7077896 | tf_op jit(solution)/shard_map/ppermute | solution.py:591
  141.2 49.9 %all-to-all-start.1 = ((s32[2,512,2]{1,2,0:T(2,128)}), s32[2,512,2]{1,2,0:T(2,128)S(1)}, u32[]{:S(2)}, u32[]{:S(2)}) async-start(s32[2,512,2]{1,2,0:T(2,128)} %pad_add_fusion), calls=%async_computation.1 | async-start | bytes 16384 | tf_op jit(solution)/shard_map/all_to_all | solution.py:569
  208.8 25.8 %copy-start.12 = (bf16[1,192,768]{2,1,0:T(8,128)(2,1)S(1)}, bf16[1,192,768]{2,1,0:T(8,128)(2,1)}, u32[]{:S(2)}) copy-start(bf16[1,192,768]{2,1,0:T(8,128)(2,1)} %get-tuple-element.392) | copy-start | bytes 884740
  234.0 26.2 %collective-permute-start.4 = (bf16[8,48,3072]{2,1,0:T(8,128)(2,1)S(1)}, bf16[8,48,3072]{2,1,0:T(8,128)(2,1)}, u32[]{:S(2)}, u32[]{:S(2)}) collective-permute-start(bf16[8,48,3072]{2,1,0:T(8,128)(2,1)S(1)} %bitcast.229), channel_id=1, source_target_pairs={{0,2},{2,0},{4,6},{6,4},{8,10},{10,8},{12,14},{14,12},{16,18},{18,... | collective-permute-start | bytes 7077896 | tf_op jit(solution)/shard_map/ppermute | solution.py:591
  234.1 26.1 %collective-permute-start.5 = (bf16[8,48,3072]{2,1,0:T(8,128)(2,1)}, bf16[8,48,3072]{2,1,0:T(8,128)(2,1)}, u32[]{:S(2)}, u32[]{:S(2)}) collective-permute-start(bf16[8,48,3072]{2,1,0:T(8,128)(2,1)} %collective-permute-done.3.refs_1_), channel_id=1, source_target_pairs={{0,2},{2,0},{4,6},{6,4},{8,10},{10,8},{12,14},{14,12},{16,18},{18,... | collective-permute-start | bytes 7077896 | tf_op jit(solution)/shard_map/ppermute | solution.py:591
  234.7 25.5 %collective-permute-start.6 = (bf16[1,96,768]{2,1,0:T(8,128)(2,1)S(1)}, bf16[1,96,768]{2,1,0:T(8,128)(2,1)S(1)}, u32[]{:S(2)}, u32[]{:S(2)}) collective-permute-start(bf16[1,96,768]{2,1,0:T(8,128)(2,1)S(1)} %constant_dynamic-slice_fusion.8.refs_0_), channel_id=1, source_target_pairs={{0,16},{2,18},{4,20},{6,22},{8,24},{10,26},{12,28},{14,30},{16,0},... | collective-permute-start | bytes 442376 | tf_op jit(solution)/shard_map/ppermute | solution.py:591
  260.6 9.1 %collective-permute-start.7 = (bf16[2,96,768]{2,1,0:T(8,128)(2,1)S(1)}, bf16[2,96,768]{2,1,0:T(8,128)(2,1)S(1)}, u32[]{:S(2)}, u32[]{:S(2)}) collective-permute-start(bf16[2,96,768]{2,1,0:T(8,128)(2,1)S(1)} %bitcast.240), channel_id=1, source_target_pairs={{0,8},{2,10},{4,12},{6,14},{8,0},{10,2},{12,4},{14,6},{16,24},{18,... | collective-permute-start | bytes 884744 | tf_op jit(solution)/shard_map/ppermute | solution.py:591
  269.8 22.4 %collective-permute-start.8 = (bf16[4,96,768]{2,1,0:T(8,128)(2,1)S(1)}, bf16[4,96,768]{2,1,0:T(8,128)(2,1)S(1)}, u32[]{:S(2)}, u32[]{:S(2)}) collective-permute-start(bf16[4,96,768]{2,1,0:T(8,128)(2,1)S(1)} %bitcast.236), channel_id=1, source_target_pairs={{0,4},{2,6},{4,0},{6,2},{8,12},{10,14},{12,8},{14,10},{16,20},{18,... | collective-permute-start | bytes 1769480 | tf_op jit(solution)/shard_map/ppermute | solution.py:591
  292.8 26.9 %collective-permute-start.9 = (bf16[8,96,768]{2,1,0:T(8,128)(2,1)S(1)}, bf16[8,96,768]{2,1,0:T(8,128)(2,1)S(1)}, u32[]{:S(2)}, u32[]{:S(2)}) collective-permute-start(bf16[8,96,768]{2,1,0:T(8,128)(2,1)S(1)} %bitcast.231), channel_id=1, source_target_pairs={{0,1},{1,0},{2,3},{3,2},{4,5},{5,4},{6,7},{7,6},{8,9},{9,8},{10,11... | collective-permute-start | bytes 3538952 | tf_op jit(solution)/shard_map/ppermute | solution.py:591
  319.7 6.6 collective-permute-start.10
  319.7 6.6 collective-permute-start.11
  320.2 34.2 %all-to-all-start.2 = ((bf16[2,512,768]{2,1,0:T(8,128)(2,1)}), bf16[2,512,768]{2,1,0:T(8,128)(2,1)}, u32[]{:S(2)}, u32[]{:S(2)}) async-start(bf16[2,512,768]{2,1,0:T(8,128)(2,1)} %param.16), calls=%async_computation.2 | async-start | bytes 3145728 | tf_op jit(solution)/shard_map/all_to_all | solution.py:569
  396.5 40.9 %collective-permute-start.12 = (bf16[8,2,48,3456]{3,2,1,0:T(8,128)(2,1)}, bf16[8,2,48,3456]{3,2,1,0:T(8,128)(2,1)}, u32[]{:S(2)}, u32[]{:S(2)}) collective-permute-start(bf16[8,2,48,3456]{3,2,1,0:T(8,128)(2,1)} %get-tuple-element.239), channel_id=1, source_target_pairs={{0,2},{2,0},{4,6},{6,4},{8,10},{10,8},{12,14},{14,12},{16,18},{18,... | collective-permute-start | bytes 15925256 | tf_op jit(solution)/shard_map/ppermute | solution.py:591
  396.6 40.9 %all-to-all-start.3 = ((bf16[2,512,768]{2,1,0:T(8,128)(2,1)}), bf16[2,512,768]{2,1,0:T(8,128)(2,1)S(1)}, u32[]{:S(2)}, u32[]{:S(2)}) async-start(bf16[2,512,768]{2,1,0:T(8,128)(2,1)} %bitcast.29), calls=%async_computation.3 | async-start | bytes 3145728 | tf_op jit(solution)/shard_map/all_to_all | solution.py:752
  473.8 60.4 %collective-permute-start.14 = (bf16[8,2,48,2688]{3,2,1,0:T(8,128)(2,1)}, bf16[8,2,48,2688]{3,2,1,0:T(8,128)(2,1)}, u32[]{:S(2)}, u32[]{:S(2)}) collective-permute-start(bf16[8,2,48,2688]{3,2,1,0:T(8,128)(2,1)} %get-tuple-element.254), channel_id=1, source_target_pairs={{0,2},{2,0},{4,6},{6,4},{8,10},{10,8},{12,14},{14,12},{16,18},{18,... | collective-permute-start | bytes 12386312 | tf_op jit(solution)/shard_map/ppermute | solution.py:591
  474.4 59.9 %collective-permute-start.13 = (bf16[2,2,2,48,3456]{4,3,2,1,0:T(8,128)(2,1)}, bf16[2,2,2,48,3456]{4,3,2,1,0:T(8,128)(2,1)}, u32[]{:S(2)}, u32[]{:S(2)}) collective-permute-start(bf16[2,2,2,48,3456]{4,3,2,1,0:T(8,128)(2,1)} %fusion.3), channel_id=1, source_target_pairs={{0,4},{2,6},{4,0},{6,2},{8,12},{10,14},{12,8},{14,10},{16,20},{18,... | collective-permute-start | bytes 7962632 | tf_op jit(solution)/shard_map/ppermute | solution.py:591
  542.3 5.4 collective-permute-start.15
  542.3 47.9 %collective-permute-start.17 = (bf16[2,2,2,48,2688]{4,3,2,1,0:T(8,128)(2,1)}, bf16[2,2,2,48,2688]{4,3,2,1,0:T(8,128)(2,1)}, u32[]{:S(2)}, u32[]{:S(2)}) collective-permute-start(bf16[2,2,2,48,2688]{4,3,2,1,0:T(8,128)(2,1)} %fusion.5), channel_id=1, source_target_pairs={{0,1},{1,0},{2,3},{3,2},{4,5},{5,4},{6,7},{7,6},{8,9},{9,8},{10,11... | collective-permute-start | bytes 6193160 | tf_op jit(solution)/shard_map/ppermute | solution.py:591
  549.8 40.5 %collective-permute-start.18 = (bf16[2,2,2,48,1920]{4,3,2,1,0:T(8,128)(2,1)}, bf16[2,2,2,48,1920]{4,3,2,1,0:T(8,128)(2,1)S(1)}, u32[]{:S(2)}, u32[]{:S(2)}) collective-permute-start(bf16[2,2,2,48,1920]{4,3,2,1,0:T(8,128)(2,1)} %fusion.7), channel_id=1, source_target_pairs={{0,4},{2,6},{4,0},{6,2},{8,12},{10,14},{12,8},{14,10},{16,20},{18,... | collective-permute-start | bytes 4423688 | tf_op jit(solution)/shard_map/ppermute | solution.py:591
  550.3 37.7 %collective-permute-start.16 = (bf16[2,2,48,3456]{3,2,1,0:T(8,128)(2,1)}, bf16[2,2,48,3456]{3,2,1,0:T(8,128)(2,1)}, u32[]{:S(2)}, u32[]{:S(2)}) collective-permute-start(bf16[2,2,48,3456]{3,2,1,0:T(8,128)(2,1)} %fusion.4), channel_id=1, source_target_pairs={{0,8},{2,10},{4,12},{6,14},{8,0},{10,2},{12,4},{14,6},{16,24},{18,... | collective-permute-start | bytes 3981320 | tf_op jit(solution)/shard_map/ppermute | solution.py:591
  609.1 4.0 collective-permute-start.19
  609.3 54.3 %collective-permute-start.21 = (bf16[2,2,48,2688]{3,2,1,0:T(8,128)(2,1)}, bf16[2,2,48,2688]{3,2,1,0:T(8,128)(2,1)}, u32[]{:S(2)}, u32[]{:S(2)}) collective-permute-start(bf16[2,2,48,2688]{3,2,1,0:T(8,128)(2,1)} %fusion.6), channel_id=1, source_target_pairs={{0,4},{2,6},{4,0},{6,2},{8,12},{10,14},{12,8},{14,10},{16,20},{18,... | collective-permute-start | bytes 3096584 | tf_op jit(solution)/shard_map/ppermute | solution.py:591
  613.1 14.2 %copy-start.10 = (bf16[8,2,48,1152]{3,2,1,0:T(8,128)(2,1)}, bf16[8,2,48,1152]{3,2,1,0:T(8,128)(2,1)S(1)}, u32[]{:S(2)}) copy-start(bf16[8,2,48,1152]{3,2,1,0:T(8,128)(2,1)S(1)} %collective-permute-done.19) | copy-start | bytes 5308420
  616.0 47.6 %collective-permute-start.23 = (bf16[2,2,2,48,1152]{4,3,2,1,0:T(8,128)(2,1)}, bf16[2,2,2,48,1152]{4,3,2,1,0:T(8,128)(2,1)}, u32[]{:S(2)}, u32[]{:S(2)}) collective-permute-start(bf16[2,2,2,48,1152]{4,3,2,1,0:T(8,128)(2,1)} %fusion.14), channel_id=1, source_target_pairs={{0,4},{2,6},{4,0},{6,2},{8,12},{10,14},{12,8},{14,10},{16,20},{18,... | collective-permute-start | bytes 2654216 | tf_op jit(solution)/shard_map/ppermute | solution.py:591
  616.6 47.0 %collective-permute-start.22 = (bf16[2,2,48,1920]{3,2,1,0:T(8,128)(2,1)}, bf16[2,2,48,1920]{3,2,1,0:T(8,128)(2,1)}, u32[]{:S(2)}, u32[]{:S(2)}) collective-permute-start(bf16[2,2,48,1920]{3,2,1,0:T(8,128)(2,1)} %fusion.8), channel_id=1, source_target_pairs={{0,8},{2,10},{4,12},{6,14},{8,0},{10,2},{12,4},{14,6},{16,24},{18,... | collective-permute-start | bytes 2211848 | tf_op jit(solution)/shard_map/ppermute | solution.py:591
  627.3 23.2 %all-to-all-start.4 = ((bf16[2,512,768]{2,1,0:T(8,128)(2,1)}), bf16[2,512,768]{2,1,0:T(8,128)(2,1)S(1)}, u32[]{:S(2)}, u32[]{:S(2)}) async-start(bf16[2,512,768]{2,1,0:T(8,128)(2,1)} %bitcast.270), calls=%async_computation.4 | async-start | bytes 3145728 | tf_op jit(solution)/shard_map/all_to_all | solution.py:752
  631.7 31.9 %collective-permute-start.20 = (bf16[2,48,3456]{2,1,0:T(8,128)(2,1)}, bf16[2,48,3456]{2,1,0:T(8,128)(2,1)}, u32[]{:S(2)}, u32[]{:S(2)}) collective-permute-start(bf16[2,48,3456]{2,1,0:T(8,128)(2,1)} %fusion.11), channel_id=1, source_target_pairs={{0,16},{2,18},{4,20},{6,22},{8,24},{10,26},{12,28},{14,30},{16,0},... | collective-permute-start | bytes 1990664 | tf_op jit(solution)/shard_map/ppermute | solution.py:591
  650.5 13.2 %collective-permute-start.24 = (f32[8,1152]{1,0:T(8,128)S(1)}, f32[8,1152]{1,0:T(8,128)S(1)}, u32[]{:S(2)}, u32[]{:S(2)}) collective-permute-start(f32[8,1152]{1,0:T(8,128)S(1)} %bitcast.277), channel_id=1, source_target_pairs={{0,2},{2,0},{4,6},{6,4},{8,10},{10,8},{12,14},{14,12},{16,18},{18,... | collective-permute-start | bytes 110600 | tf_op jit(solution)/shard_map/ppermute | solution.py:591
  674.5 31.6 %collective-permute-start.25 = (bf16[2,48,3456]{2,1,0:T(8,128)(2,1)}, bf16[2,48,3456]{2,1,0:T(8,128)(2,1)}, u32[]{:S(2)}, u32[]{:S(2)}) collective-permute-start(bf16[2,48,3456]{2,1,0:T(8,128)(2,1)} %fusion.10), channel_id=1, source_target_pairs={{0,1},{1,0},{2,3},{3,2},{4,5},{5,4},{6,7},{7,6},{8,9},{9,8},{10,11... | collective-permute-start | bytes 1990664 | tf_op jit(solution)/shard_map/ppermute | solution.py:591
  676.2 29.8 %collective-permute-start.26 = (bf16[2,48,2688]{2,1,0:T(8,128)(2,1)}, bf16[2,48,2688]{2,1,0:T(8,128)(2,1)}, u32[]{:S(2)}, u32[]{:S(2)}) collective-permute-start(bf16[2,48,2688]{2,1,0:T(8,128)(2,1)} %fusion.13), channel_id=1, source_target_pairs={{0,8},{2,10},{4,12},{6,14},{8,0},{10,2},{12,4},{14,6},{16,24},{18,... | collective-permute-start | bytes 1548296 | tf_op jit(solution)/shard_map/ppermute | solution.py:591
  676.7 29.4 %collective-permute-start.28 = (bf16[2,2,48,1152]{3,2,1,0:T(8,128)(2,1)}, bf16[2,2,48,1152]{3,2,1,0:T(8,128)(2,1)}, u32[]{:S(2)}, u32[]{:S(2)}) collective-permute-start(bf16[2,2,48,1152]{3,2,1,0:T(8,128)(2,1)} %fusion.15), channel_id=1, source_target_pairs={{0,8},{2,10},{4,12},{6,14},{8,0},{10,2},{12,4},{14,6},{16,24},{18,... | collective-permute-start | bytes 1327112 | tf_op jit(solution)/shard_map/ppermute | solution.py:591
  678.3 27.0 %collective-permute-start.27 = (bf16[2,48,1920]{2,1,0:T(8,128)(2,1)}, bf16[2,48,1920]{2,1,0:T(8,128)(2,1)S(1)}, u32[]{:S(2)}, u32[]{:S(2)}) collective-permute-start(bf16[2,48,1920]{2,1,0:T(8,128)(2,1)} %fusion.18), channel_id=1, source_target_pairs={{0,16},{2,18},{4,20},{6,22},{8,24},{10,26},{12,28},{14,30},{16,0},... | collective-permute-start | bytes 1105928 | tf_op jit(solution)/shard_map/ppermute | solution.py:591
  680.1 4.1 collective-permute-start.29
  711.4 23.0 %collective-permute-start.31 = (bf16[2,48,1920]{2,1,0:T(8,128)(2,1)S(1)}, bf16[2,48,1920]{2,1,0:T(8,128)(2,1)S(1)}, u32[]{:S(2)}, u32[]{:S(2)}) collective-permute-start(bf16[2,48,1920]{2,1,0:T(8,128)(2,1)S(1)} %fusion.17), channel_id=1, source_target_pairs={{0,1},{1,0},{2,3},{3,2},{4,5},{5,4},{6,7},{7,6},{8,9},{9,8},{10,11... | collective-permute-start | bytes 1105928 | tf_op jit(solution)/shard_map/ppermute | solution.py:591
  711.9 22.5 %collective-permute-start.30 = (bf16[48,2688]{1,0:T(8,128)(2,1)S(1)}, bf16[48,2688]{1,0:T(8,128)(2,1)S(1)}, u32[]{:S(2)}, u32[]{:S(2)}) collective-permute-start(bf16[48,2688]{1,0:T(8,128)(2,1)S(1)} %fusion.22), channel_id=1, source_target_pairs={{0,16},{2,18},{4,20},{6,22},{8,24},{10,26},{12,28},{14,30},{16,0},... | collective-permute-start | bytes 774152 | tf_op jit(solution)/shard_map/ppermute | solution.py:591
  714.4 20.0 %collective-permute-start.32 = (bf16[2,48,1152]{2,1,0:T(8,128)(2,1)S(1)}, bf16[2,48,1152]{2,1,0:T(8,128)(2,1)S(1)}, u32[]{:S(2)}, u32[]{:S(2)}) collective-permute-start(bf16[2,48,1152]{2,1,0:T(8,128)(2,1)S(1)} %fusion.25), channel_id=1, source_target_pairs={{0,16},{2,18},{4,20},{6,22},{8,24},{10,26},{12,28},{14,30},{16,0},... | collective-permute-start | bytes 663560 | tf_op jit(solution)/shard_map/ppermute | solution.py:591
  714.8 8.8 %collective-permute-start.33 = (f32[2,1152]{1,0:T(2,128)S(1)}, f32[2,1152]{1,0:T(2,128)S(1)}, u32[]{:S(2)}, u32[]{:S(2)}) collective-permute-start(f32[2,1152]{1,0:T(2,128)S(1)} %bitcast.280), channel_id=1, source_target_pairs={{0,8},{2,10},{4,12},{6,14},{8,0},{10,2},{12,4},{14,6},{16,24},{18,... | collective-permute-start | bytes 27656 | tf_op jit(solution)/shard_map/ppermute | solution.py:591
  737.5 10.5 %collective-permute-start.34 = (bf16[48,2688]{1,0:T(8,128)(2,1)S(1)}, bf16[48,2688]{1,0:T(8,128)(2,1)S(1)}, u32[]{:S(2)}, u32[]{:S(2)}) collective-permute-start(bf16[48,2688]{1,0:T(8,128)(2,1)S(1)} %fusion.21), channel_id=1, source_target_pairs={{0,1},{1,0},{2,3},{3,2},{4,5},{5,4},{6,7},{7,6},{8,9},{9,8},{10,11... | collective-permute-start | bytes 774152 | tf_op jit(solution)/shard_map/ppermute | solution.py:591
  739.2 8.8 %collective-permute-start.35 = (bf16[2,48,1152]{2,1,0:T(8,128)(2,1)S(1)}, bf16[2,48,1152]{2,1,0:T(8,128)(2,1)S(1)}, u32[]{:S(2)}, u32[]{:S(2)}) collective-permute-start(bf16[2,48,1152]{2,1,0:T(8,128)(2,1)S(1)} %fusion.24), channel_id=1, source_target_pairs={{0,1},{1,0},{2,3},{3,2},{4,5},{5,4},{6,7},{7,6},{8,9},{9,8},{10,11... | collective-permute-start | bytes 663560 | tf_op jit(solution)/shard_map/ppermute | solution.py:591
  739.6 4.5 collective-permute-start.36
  748.3 4.1 collective-permute-start.37
  (24 other events, 113.9 us)
Sparse Core Ops, SparseCore 0:
  11.1 102.9 all-gather.3
  116.9 53.7 all-gather.5

commit v6 on v5

--- a/solution.py
+++ b/solution.py
@@ -315,11 +315,10 @@
     result_ref[...] = result.astype(result_ref.dtype)
 
 
-def feed(attended, hidden, gains, offsets, up_bias, joined, down, result_type):
+def feed(attended, hidden, gains, offsets, up_bias, joined, up, down, result_type):
     length, features = hidden.shape
     units = down.shape[0]
-    out_place = 3
-    up_place = 4 * features // units
+    up_array, up_place = up
     shape = jax.ShapeDtypeStruct
     return row_tiled(
         feed_kernel,
@@ -331,7 +330,7 @@
             resident(gains.shape),
             resident(offsets.shape),
             resident(up_bias.shape),
-            resident((features, features), 0, out_place),
+            resident((features, features), 0, 3),
             resident((features, units), 0, up_place),
             resident(down.shape),
         ],
@@ -343,7 +342,7 @@
             shape((length, units), half),
             shape((length, features), result_type),
         ],
-        (attended, hidden, gains, offsets, up_bias, joined, joined, down),
+        (attended, hidden, gains, offsets, up_bias, joined, up_array, down),
         2 * length * features * (features + 2 * units),
     )
 
@@ -394,7 +393,8 @@
     upstream_ref[...] = contract(attention_grad, out_weight_ref[...], 1, 1).astype(half)
 
 
-def feed_grad(gradient, slope, middle, gains, joined, down):
+def feed_grad(gradient, slope, middle, gains, joined, up, down):
+    up_array, up_place = up
     length, features = middle.shape
     units = down.shape[0]
     shape = jax.ShapeDtypeStruct
@@ -408,7 +408,7 @@
             tile_of(features),
             resident(gains.shape),
             resident((features, features), 0, 3),
-            resident((features, units), 0, 4 * features // units),
+            resident((features, units), 0, up_place),
             resident(down.shape),
         ],
         [
@@ -429,7 +429,7 @@
             shape((8, features), single),
             shape((1, units), single),
         ],
-        (gradient, slope, middle, gains, joined, joined, down),
+        (gradient, slope, middle, gains, joined, up_array, down),
         2 * length * features * (features + 2 * units),
     )
 
@@ -475,19 +475,22 @@
     )
 
 
-def term_blocks(terms, core, groups, row_unit):
+def term_blocks(terms, core, groups, row_unit, by_core):
     pieces = [left.shape[1] // (groups * row_unit) for left, _ in terms]
-    widths = [right.shape[1] // 2 for _, right in terms]
+    widths = [right.shape[1] // (2 if by_core else 1) for _, right in terms]
     total = sum(count * width for count, width in zip(pieces, widths))
     chips = groups // 2
-    out_shape = (chips, 2, row_unit, total)
+    out_shape = (chips, 2, row_unit, total) if by_core else (groups, row_unit, total)
+    outputs = 2 if by_core else 1
     if row_unit % 16:
         columns = []
         for (left, right), count, width in zip(terms, pieces, widths):
             part = contract(left, right, 0, 0).astype(half)
-            part = part.reshape(chips, 2, count, row_unit, 2, width).transpose(2, 1, 0, 4, 3, 5)
+            part = part.reshape(chips, 2, count, row_unit, -1, width).transpose(2, 1, 0, 4, 3, 5)
             columns += [part[piece] for piece in range(count)]
         whole = jnp.concatenate(columns, axis=-1)
+        if not by_core:
+            return [whole[:, :, 0].swapaxes(0, 1).reshape(out_shape)]
         return [
             lax.dynamic_index_in_dim(whole, which, 0, keepdims=False) for which in (1 - core, core)
         ]
@@ -495,9 +498,9 @@
 
     def kernel(core_ref, *refs):
         sources = refs[: 2 * number]
-        other_ref, own_ref = refs[2 * number : 2 * number + 2]
-        buffers = refs[2 * number + 2 : 4 * number + 2]
-        semaphores = refs[4 * number + 2]
+        outs = refs[2 * number : 2 * number + outputs]
+        buffers = refs[2 * number + outputs : 4 * number + outputs]
+        semaphores = refs[4 * number + outputs]
         first_core = core_ref[0] == 0
         copies = [
             pltpu.make_async_copy(source, buffer, semaphores.at[index])
@@ -516,7 +519,7 @@
             for turn in range(count):
                 turned = left[:, turn * rows : (turn + 1) * rows].T
                 some = slice(turn * held, (turn + 1) * held)
-                for low in range(0, 2 * width, step):
+                for low in range(0, right.shape[1], step):
                     product = contract(turned, right[:, low : low + step], 1, 0).astype(half)
                     product = product.reshape(held, 2, count, row_unit, step)
                     side, inside = divmod(low, width)
@@ -524,8 +527,14 @@
                         lanes = start + piece * width + inside
                         lanes = slice(lanes, lanes + step)
                         even, odd = product[:, 0, piece], product[:, 1, piece]
-                        other_ref[some, side, :, lanes] = jnp.where(first_core, odd, even)
-                        own_ref[some, side, :, lanes] = jnp.where(first_core, even, odd)
+                        if by_core:
+                            outs[0][some, side, :, lanes] = jnp.where(first_core, odd, even)
+                            outs[1][some, side, :, lanes] = jnp.where(first_core, even, odd)
+                        else:
+                            for chip in range(held):
+                                owner = 2 * (turn * held + chip)
+                                outs[0][owner, :, lanes] = even[chip]
+                                outs[0][owner + 1, :, lanes] = odd[chip]
             start += count * width
 
     anywhere = pl.BlockSpec(memory_space=pl.ANY)
@@ -536,12 +545,12 @@
     return pl.pallas_call(
         kernel,
         in_specs=[pl.BlockSpec(memory_space=pltpu.SMEM)] + [anywhere] * len(operands),
-        out_specs=[pl.BlockSpec(memory_space=pltpu.VMEM)] * 2,
-        out_shape=[shape, shape],
+        out_specs=[pl.BlockSpec(memory_space=pltpu.VMEM)] * outputs,
+        out_shape=[shape] * outputs,
         scratch_shapes=[pltpu.VMEM(operand.shape, half) for operand in operands]
         + [pltpu.SemaphoreType.DMA((len(operands),))],
         compiler_params=pltpu.CompilerParams(vmem_limit_bytes=60 << 20),
-        cost_estimate=estimate(flops, size + 4 * shape.size),
+        cost_estimate=estimate(flops, size + 2 * outputs * shape.size),
         name="term_blocks",
     )(core.reshape(1).astype(jnp.int32), *operands)
 
@@ -572,7 +581,17 @@
     place = lax.axis_index("seq")
     indices = jnp.stack([core, place]).astype(jnp.int32)
     row_unit = qkv_weight.shape[1]
-    pair_up = lambda bit: [(index, index ^ bit) for index in range(groups)]
+
+    def across(bit):
+        pairs = [(index, index ^ bit) for index in range(groups)]
+        return lambda part: lax.ppermute(part, "wide", pairs)
+
+    def beside_seq(part):
+        return lax.ppermute(part, "seq", swap)
+
+    def to_owners(part):
+        return lax.psum_scatter(part, "wide", scatter_dimension=0, tiled=True)
+
     bit_of = lambda bit: (lax.axis_index("wide") >> (bit.bit_length() - 1)) & 1
     running = []
 
@@ -584,13 +603,10 @@
     def launch(main, entries):
         fresh = [entry for entry in entries if entry in running and entry[3] is None]
         if fresh:
-            sends = [[sent for sent, _, _ in entry[2]] for entry in fresh]
+            sends = [[sent for sent, _ in entry[2]] for entry in fresh]
             main, sends = lax.optimization_barrier((main, sends))
             for entry, sent in zip(fresh, sends):
-                entry[3] = [
-                    lax.ppermute(part, axis, pairs)
-                    for part, (_, axis, pairs) in zip(sent, entry[2])
-                ]
+                entry[3] = [pass_on(part) for part, (_, pass_on) in zip(sent, entry[2])]
         return main
 
     def advance(main, *only):
@@ -611,52 +627,59 @@
     def side_of(array, which, axis):
         return lax.dynamic_index_in_dim(array, which, axis, keepdims=False)
 
-    def gather_steps(shard, split_rows):
-        rows, columns = shard.shape
-        if split_rows:
-            rows //= 2
-            mine = side_of(shard.reshape(2, rows, columns), place, 0)
-        else:
-            columns //= 2
-            mine = lax.dynamic_slice_in_dim(shard, place * columns, columns, axis=1)
-        current = mine[None]
-        bit = groups // 2
-        while bit > 1:
-            (received,) = yield [(current, "wide", pair_up(bit))]
-            count = current.shape[0]
-            current = place_pieces(
-                [current, received],
-                (count, 2, rows, columns),
-                [lambda ref: (slice(None), ref[0]), lambda ref: (slice(None), 1 - ref[0])],
-                bit_of(bit).reshape(1).astype(jnp.int32),
-            ).reshape(2 * count, rows, columns)
-            bit //= 2
-        (beside,) = yield [(current, "seq", swap)]
-        passed = yield [(part, "wide", pair_up(1)) for part in (current, beside)]
-        count = current.shape[0]
+    chip_bits = [1 << number for number in range(groups.bit_length() - 2, 0, -1)]
+
+    def join(current, received, which):
+        lead = current.shape[0]
+        joined = place_pieces(
+            [current, received],
+            (lead, 2) + current.shape[1:],
+            [lambda ref: (slice(None), ref[0]), lambda ref: (slice(None), 1 - ref[0])],
+            which.reshape(1).astype(jnp.int32),
+        )
+        return joined.reshape((2 * lead,) + current.shape[1:])
+
+    def gather_columns(shard):
+        rows, columns = shard.shape[0], shard.shape[1] // 2
+        current = lax.dynamic_slice_in_dim(shard, place * columns, columns, axis=1)[None]
+        for bit in chip_bits:
+            (received,) = yield [(current, across(bit))]
+            current = join(current, received, bit_of(bit))
+        (aside,) = yield [(current, beside_seq)]
+        passed = yield [(part, across(1)) for part in (current, aside)]
 
         def target(own_core, own_place):
             def where(ref):
                 which_core = ref[0] if own_core else 1 - ref[0]
                 which_place = ref[1] if own_place else 1 - ref[1]
-                if split_rows:
-                    return (slice(None), which_core, which_place)
                 start = pl.multiple_of(which_place * columns, columns)
                 return (slice(None), which_core, slice(None), pl.ds(start, columns))
 
             return where
 
-        whole = place_pieces(
-            [current, beside, *passed],
-            (count, 2, 2, rows, columns) if split_rows else (count, 2, rows, 2 * columns),
+        return place_pieces(
+            [current, aside, *passed],
+            (current.shape[0], 2, rows, 2 * columns),
             [target(True, True), target(True, False), target(False, True), target(False, False)],
             indices,
-        )
-        return whole.reshape(-1, shard.shape[1])
-
+        ).reshape(-1, 2 * columns)
+
+    def gather_rows(shard):
+        rows, columns = shard.shape[0] // 2, shard.shape[1]
+        current = side_of(shard.reshape(2, rows, columns), place, 0)[None]
+        for bit in chip_bits[:-1]:
+            (received,) = yield [(current, across(bit))]
+            current = join(current, received, bit_of(bit))
+        (received,) = yield [(current, beside_seq)]
+        current = join(current, received, place).reshape(-1, 2 * rows, columns)
+        for bit in chip_bits[-1:] + [1]:
+            (received,) = yield [(current, across(bit))]
+            current = join(current, received, bit_of(bit))
+        return current.reshape(-1, columns)
+
+    marks = whole_sequence(jnp.stack([segment_ids, pad_mask], axis=2))
+    tokens, marks = lax.optimization_barrier((tokens, marks))
     my_tokens = whole_sequence(tokens)
-    marks = whole_sequence(jnp.stack([segment_ids, pad_mask], axis=2))
-    my_time = lax.dynamic_index_in_dim(time_embed, place, 0, keepdims=True)
 
     small = jnp.concatenate(
         [norm_gains.reshape(-1), bias_rows.reshape(-1), up_bias.reshape(-1)]
@@ -664,19 +687,12 @@
     side = small.reshape(row_unit, -1)
     side_width = side.shape[1]
     side = jnp.pad(side, ((0, 0), (0, -side_width % PAIR)))
-    cuts = [0]
-    for source in (qkv_weight, out_weight, up_weight):
-        cuts.append(cuts[-1] + source.shape[2])
-
-    def beside_each_other(layer, *more):
-        parts = [qkv_weight[layer], out_weight[layer], up_weight[layer], *more]
-        return jnp.concatenate(parts, axis=1)
-
-    first_whole = lax.all_gather(beside_each_other(0, side), "wide", axis=0, tiled=True)
-    first_down = lax.all_gather(down_weight[0], "wide", axis=0, tiled=True)
-    matrices = [None] * layers
-    matrices[0] = (first_whole, first_down)
-    small_whole = first_whole[:, cuts[-1] :][:, :side_width].reshape(groups, -1)
+    joined_parts = [jnp.concatenate([qkv_weight[0], out_weight[0], side], axis=1)]
+    for layer in range(1, layers):
+        parts = [qkv_weight[layer], out_weight[layer], up_weight[layer]]
+        joined_parts.append(jnp.concatenate(parts, axis=1))
+    joined = [lax.all_gather(part, "wide", axis=0, tiled=True) for part in joined_parts]
+    small_whole = joined[0][:, -side.shape[1] :][:, :side_width].reshape(groups, -1)
     cut_gains = norm_gains.size
     cut_rows = cut_gains + bias_rows.size
 
@@ -695,42 +711,41 @@
     )
     bias = jnp.where(allowed, 0.0, masked_bias)
 
-    joined = {}
-    downs = {}
-    for layer in range(1, layers):
-        begin(
-            gather_steps(beside_each_other(layer), False),
-            functools.partial(joined.__setitem__, layer),
-        )
-    bit = groups // 2
-    while bit > 1:
-        my_tokens = advance(my_tokens)
-        bit //= 2
+    matrices = [None] * layers
+    ups, downs = {}, {}
+    fetches = [
+        begin(gather_columns(up_weight[0]), functools.partial(ups.__setitem__, 0)),
+        begin(gather_rows(down_weight[0]), functools.partial(downs.__setitem__, 0)),
+    ]
+    for _ in chip_bits:
+        time_embed = advance(time_embed, *fetches)
+    my_time = lax.dynamic_index_in_dim(time_embed, place, 0, keepdims=True)
     hidden = my_tokens.astype(single) + my_time
     saved = []
     for layer in range(layers):
-        whole = joined[layer] if layer else first_whole
+        whole = joined[layer]
         gains, offsets = all_gains[layer], all_offsets[layer]
         before = hidden
         normed, packed = project(hidden, gains, offsets, whole)
-        if layer:
-            packed = advance(packed)
+        if layer == layers - 1:
+            packed, out_grad = lax.optimization_barrier((packed, out_grad))
+            my_upstream = whole_sequence(out_grad)
+        packed = advance(packed, *fetches)
         attended, totals = attend_forward(packed, bias)
-        attended = advance(attended)
-        if layer == 0:
-            for later in range(1, layers):
+        attended = advance(attended, *fetches)
+        while running:
+            attended = advance(attended, *fetches)
+        up = (whole, 4 * features // up_bias.shape[1] // groups) if layer else (ups[0], 0)
+        matrices[layer] = (whole, up, downs[layer])
+        fetches = []
+        if layer < layers - 1:
+            fetches = [
                 begin(
-                    gather_steps(down_weight[later], True),
-                    functools.partial(downs.__setitem__, later),
+                    gather_rows(down_weight[layer + 1]),
+                    functools.partial(downs.__setitem__, layer + 1),
                 )
-            attended = launch(attended, list(running))
-            attended, out_grad = lax.optimization_barrier((attended, out_grad))
-            my_upstream = whole_sequence(out_grad)
-        else:
-            while layer not in downs:
-                attended = advance(attended)
-        down = downs[layer] if layer else first_down
-        matrices[layer] = (whole, down)
+            ]
+            attended = launch(attended, fetches)
         middle, second, activated, slope, hidden = feed(
             attended,
             hidden,
@@ -738,13 +753,12 @@
             offsets,
             all_up_bias[layer][None],
             whole,
-            down,
+            up,
+            downs[layer],
             single if layer < layers - 1 else half,
         )
-        if layer < layers - 1:
-            while layer + 1 not in joined:
-                hidden = advance(hidden)
-            hidden = advance(hidden)
+        for _ in chip_bits:
+            hidden = advance(hidden, *fetches)
         saved.append((before, normed, packed, totals, attended, middle, second, activated, slope))
 
     def split_back(result):
@@ -756,41 +770,45 @@
     def total_of(addends):
         return functools.reduce(jnp.add, [addend.astype(single) for addend in addends])
 
-    chip_bits = [1 << number for number in range(groups.bit_length() - 2, 0, -1)]
-
-    def reduce_group(terms, spread):
-        other, own = term_blocks(terms, core, groups, row_unit)
-        counts = [(left.shape[1] // (groups * row_unit), right.shape[1] // 2) for left, right in terms]
-        (received,) = yield [(other, "wide", pair_up(1))]
-        width = own.shape[-1]
-        axes = chip_bits + ["seq"]
-        addends = [part.reshape((2,) * len(axes) + (row_unit, width)) for part in (own, received)]
-        for stage in (["seq"] if spread else []) + chip_bits[::-1]:
-            axis = axes.index(stage)
-            mine = place if stage == "seq" else bit_of(stage)
-            sent = total_of([side_of(part, 1 - mine, axis) for part in addends]).astype(half)
-            if stage == "seq":
-                (received,) = yield [(sent, "seq", swap)]
-            else:
-                (received,) = yield [(sent, "wide", pair_up(stage))]
-            addends = [side_of(part, mine, axis) for part in addends] + [received]
-            axes.remove(stage)
-        current = total_of(addends).astype(half)
-        (received,) = yield [(current, "seq", swap)]
-        if spread:
-            low = jnp.where(place == 0, current, received).astype(single)
-            high = jnp.where(place == 0, received, current).astype(single)
-        else:
-            low, high = current.astype(single) + received.astype(single)
+    def shares_of(terms, low, high):
         shares, start = [], 0
-        for count, each in counts:
-            rows = []
-            for _ in range(count):
+        for left, right in terms:
+            rows, each = [], right.shape[1] // 2
+            if high is None:
+                each *= 2
+            for _ in range(left.shape[1] // (groups * row_unit)):
                 window = slice(start, start + each)
-                rows.append(jnp.concatenate([low[:, window], high[:, window]], axis=1))
+                if high is None:
+                    rows.append(low[:, window])
+                else:
+                    rows.append(jnp.concatenate([low[:, window], high[:, window]], axis=1))
                 start += each
             shares.append(jnp.concatenate(rows, axis=0))
         return shares
+
+    def scatter_group(terms):
+        (whole,) = term_blocks(terms, core, groups, row_unit, False)
+        whole = whole.reshape(groups * row_unit, -1)
+        (share,) = yield [(whole, to_owners)]
+        (received,) = yield [(share, beside_seq)]
+        return shares_of(terms, share.astype(single) + received.astype(single), None)
+
+    def reduce_group(terms):
+        other, own = term_blocks(terms, core, groups, row_unit, True)
+        (received,) = yield [(other, across(1))]
+        shape = (2,) * len(chip_bits) + (2, row_unit, own.shape[-1])
+        addends = [part.reshape(shape) for part in (own, received)]
+        axis = len(chip_bits) - 1
+        for bit in chip_bits[::-1]:
+            mine = bit_of(bit)
+            sent = total_of([side_of(part, 1 - mine, axis) for part in addends]).astype(half)
+            (received,) = yield [(sent, across(bit))]
+            addends = [side_of(part, mine, axis) for part in addends] + [received]
+            axis -= 1
+        current = total_of(addends).astype(half)
+        (received,) = yield [(current, beside_seq)]
+        low, high = current.astype(single) + received.astype(single)
+        return shares_of(terms, low, high)
 
     def reduce_small(array):
         bit = 1
@@ -798,59 +816,63 @@
             view = array.reshape(-1, 2, array.shape[-1])
             mine = bit_of(bit)
             sent = side_of(view, 1 - mine, 1)
-            (received,) = yield [(sent, "wide", pair_up(bit))]
+            (received,) = yield [(sent, across(bit))]
             array = side_of(view, mine, 1) + received
             bit *= 2
-        (received,) = yield [(array, "seq", swap)]
+        (received,) = yield [(array, beside_seq)]
         return (array + received)[0]
 
     weight_grads = [[None] * 4 for _ in range(layers)]
 
-    def begin_group(spread, *named):
+    def begin_group(steps, layer, named):
         def finish(shares):
-            for (layer, part, _), share in zip(named, shares):
+            for (part, _), share in zip(named, shares):
                 weight_grads[layer][part] = share
 
-        return begin(reduce_group([term for _, _, term in named], spread), finish)
+        return begin(steps([term for _, term in named]), finish)
 
     gradient = my_upstream
     small_grads = [None] * layers
-    waiting = []
+    held = []
     for layer in range(layers - 1, -1, -1):
-        whole, down = matrices[layer]
+        whole, up, down = matrices[layer]
         gains = all_gains[layer]
         hidden, normed, packed, totals, attended, middle, second, activated, slope = saved[layer]
-        early = None
-        if layer < layers - 1:
-            branch = gradient.astype(half)
-            early = begin_group(True, *waiting, (layer, 3, (activated, branch)))
-            gradient = launch(gradient, [early])
-            waiting = []
+        steps = scatter_group if layer else reduce_group
+        if not layer:
+            first = begin_group(steps, layer, [(3, (activated, gradient.astype(half)))])
+            gradient = launch(gradient, [first])
         branch, upper, middle_grad, attention_grad, upstream, sums, unit_sums = feed_grad(
-            gradient, slope, middle, gains, whole, down
+            gradient, slope, middle, gains, whole, up, down
         )
-        upstream = advance(upstream)
-        named = [(layer, 2, (second, upper)), (layer, 1, (attended, attention_grad))]
-        if early is None:
-            named = [(layer, 3, (activated, branch))] + named
-        entry = begin_group(False, *named)
-        upstream = launch(upstream, [entry])
-        if layer == 0:
-            upstream = advance(upstream, entry)
+        named = [(2, (second, upper)), (1, (attended, attention_grad))]
+        if layer:
+            held.append(begin_group(steps, layer, [(3, (activated, branch))] + named))
+            upstream = launch(upstream, held[-1:])
+        else:
+            second_group = begin_group(steps, layer, named)
+            upstream = launch(upstream, [second_group])
+            upstream = advance(upstream, first)
+            upstream = advance(upstream, second_group)
         packed_grad = attend_backward(packed, bias, upstream, totals, attended)
         if layer == layers - 1:
             packed_grad, output = lax.optimization_barrier((packed_grad, output))
             output = output.astype(single)
-        packed_grad = advance(packed_grad)
-        last = (layer, 0, (normed, packed_grad))
+        named = [(0, (normed, packed_grad))]
         if layer:
-            waiting = [last]
+            held.append(begin_group(steps, layer, named))
+            packed_grad = launch(packed_grad, held[-1:])
         else:
-            entry = begin_group(False, last)
-            packed_grad = advance(packed_grad, entry)
+            packed_grad = advance(packed_grad, first, second_group, *held[:1])
+            last_group = begin_group(steps, layer, named)
+            packed_grad = launch(packed_grad, [last_group])
+            packed_grad = advance(packed_grad, first)
+            packed_grad = advance(packed_grad, last_group)
         gradient, more_sums = project_grad(
             packed_grad, hidden, middle_grad, gains, whole, single if layer else half
         )
+        if not layer:
+            gradient = advance(gradient, first, second_group, last_group, *held[:1])
         small_grads[layer] = (
             jnp.stack([more_sums[0], sums[1]]),
             jnp.stack([more_sums[1], more_sums[2], more_sums[3], sums[3], sums[2], sums[0]]),

time: 775 us -> 690 us (0.89)
  waiting for transfers between devices: 276 us -> 172 us
  starting transfers between devices: 56.2 us -> 71 us
  other arithmetic: 64.4 us -> 51.6 us
    all_to_all x3 -> x2, waiting for transfers between devices: 66.5 us -> 0.01 us  [whole_sequence(): lax.all_to_all(part, 'seq', split_axis=0, concat_axis=1, tiled=True)[0]]
    ppermute x38, waiting for transfers between devices: 194 us -> 160 us  [the longest x29 131 us: across(): return lambda part: lax.ppermute(part, 'wide', pairs)]
    ppermute x38, starting transfers between devices: 36.4 us -> 54 us  [the longest x29 39.1 us: across(): return lambda part: lax.ppermute(part, 'wide', pairs)]
    convert_element_type x13 -> x9, other arithmetic: 36.4 us -> 21.7 us  [reduce_group(): total_of([side_of(part, 1 - mine, axis) for part in addends]).astype(half)]
    pallas_call x4 -> x5, Pallas kernels: 61.2 us -> 62.8 us  [term_blocks(): pl.pallas_call(kernel, in_specs=[pl.BlockSpec(memory_space=pltpu.SMEM)] +...]
  transfers between devices with their start and end apart: 45 -> 46, of which waited for: 20 -> 24; matrix products, arithmetic and copies ran while one was open for 4% -> 8% of each run, Pallas kernels for 32% -> 42%
where the time goes in v6:
time: 690 us; the launch traced here: 679 us
  Pallas kernels  328 us (48%)
  waiting for transfers between devices  172 us (25%)
  starting transfers between devices  71 us (10%)
  other arithmetic  51.6 us (7%)
  local copies, waits for them, and re-layouts  34.8 us (5%)
  between operations  14.9 us (2%)
    ppermute x29, waiting for transfers between devices, across(): return lambda part: lax.ppermute(part, 'wide', pairs)  131 us
    pallas_call x8, Pallas kernels, row_tiled(): pl.pallas_call(kernel, grid=(length // ROW_TILE,), in_specs=in_specs, out...  130 us
    pallas_call x2, Pallas kernels, attend_backward(): pl.pallas_call(functools.partial(attend_grad_kernel, rows=BACKWARD_ROWS),...  74.7 us
    pallas_call x5, Pallas kernels, term_blocks(): pl.pallas_call(kernel, in_specs=[pl.BlockSpec(memory_space=pltpu.SMEM)] +...  62.8 us
    pallas_call x2, Pallas kernels, attend_forward(): pl.pallas_call(functools.partial(attend_kernel, rows=FORWARD_ROWS), grid=...  50.4 us
    ppermute x29, starting transfers between devices, across(): return lambda part: lax.ppermute(part, 'wide', pairs)  39.1 us
    ppermute x9, waiting for transfers between devices, beside_seq(): return lax.ppermute(part, 'seq', swap)  29.1 us
    convert_element_type x9, other arithmetic, reduce_group(): total_of([side_of(part, 1 - mine, axis) for part in addends]).astype(half)  21.7 us
  transfers between devices with their start and end apart: 46, of which 24 were waited for; matrix products, arithmetic and copies ran while one was open for 8% of the time, Pallas kernels for 42%

profile of v6, /device:TPU:0, one launch (start us, length us, event | category | flops | bytes accessed | tf_op | source)
XLA Modules:
  0.0 678.9 jit_solution(9275054480130891968)
XLA Ops:
  14.4 4.1 collective-permute-start
  18.6 15.5 %collective-permute-done.refs_1_ = bf16[1,48,1536]{2,1,0:T(8,128)(2,1)S(1)} collective-permute-done((bf16[1,48,1536]{2,1,0:T(8,128)(2,1)S(1)}, bf16[1,48,1536]{2,1,0:T(8,128)(2,1)S(1)}, u32[]{:S(2)}, u32[]{:S(2)}) %collective-permute-start) | collective-permute-done | bytes 147488 | tf_op jit(solution)/shard_map/ppermute | solution.py:587
  34.1 7.6 %collective-permute-done.1.refs_1_ = bf16[1,96,768]{2,1,0:T(8,128)(2,1)S(1)} collective-permute-done((bf16[1,96,768]{2,1,0:T(8,128)(2,1)S(1)}, bf16[1,96,768]{2,1,0:T(8,128)(2,1)S(1)}, u32[]{:S(2)}, u32[]{:S(2)}) %collective-permute-start.1) | collective-permute-done | bytes 147488 | tf_op jit(solution)/shard_map/ppermute | solution.py:587
  44.6 6.5 all_to_all.37
  51.1 4.6 all-to-all-start.1
  55.7 3.9 collective-permute-done.2.refs_1_
  59.7 13.5 %collective-permute-done.3.refs_1_ = bf16[2,96,768]{2,1,0:T(8,128)(2,1)S(1)} collective-permute-done((bf16[2,96,768]{2,1,0:T(8,128)(2,1)S(1)}, bf16[2,96,768]{2,1,0:T(8,128)(2,1)S(1)}, u32[]{:S(2)}, u32[]{:S(2)}) %collective-permute-start.3) | collective-permute-done | bytes 294944 | tf_op jit(solution)/shard_map/ppermute | solution.py:587
  77.3 6.0 collective-permute-done.4.refs_1_
  84.1 4.5 collective-permute-done.5.refs_1_
  92.5 3.3 convert_add_fusion.hidden_ref
  99.9 9.0 %project.2 = (bf16[1024,768]{1,0:T(8,128)(2,1)}, bf16[1024,2304]{1,0:T(8,128)(2,1)}) custom-call(f32[1024,768]{1,0:T(8,128)} %convert_add_fusion.hidden_ref, f32[2,768]{1,0:T(2,128)} %squeeze.136.gains_ref, f32[6,768]{1,0:T(8,128)} %squeeze.137.offsets_ref, bf16[768,3200]{1,0:T(8,128)(2,1)} %all-gather.3.cloned.1.call-done.weight_ref.out_weight_ref), custom_call_target="tpu_custom_call" | custom-call | flops 226492416 | bytes 898560 | tf_op jit(solution)/shard_map/project/pallas_call | solution.py:231
  111.0 4.1 collective-permute-done.7.refs_1_
  117.2 2.8 fusion.2.bias_ref
  123.6 25.2 %attend_forward.2 = (bf16[1024,768]{1,0:T(8,128)(2,1)}, f32[6,2,1024]{2,1,0:T(2,128)}) custom-call(bf16[1024,2304]{1,0:T(8,128)(2,1)} %get-tuple-element.209.query_ref.key_ref.value_ref, bf16[1024,2304]{1,0:T(8,128)(2,1)} %get-tuple-element.209.query_ref.key_ref.value_ref, bf16[1024,2304]{1,0:T(8,128)(2,1)} %get-tuple-element.209.query_ref.key_ref.value_ref, ...), custom_call_target="tpu_custom_call" | custom-call | flops 805306368 | bytes 393216 | tf_op jit(solution)/shard_map/attend_forward/pallas_call | solution.py:68
  148.8 13.7 %collective-permute-start.11 = (bf16[1,96,768]{2,1,0:T(8,128)(2,1)}, bf16[1,96,768]{2,1,0:T(8,128)(2,1)}, u32[]{:S(2)}, u32[]{:S(2)}) collective-permute-start(bf16[1,96,768]{2,1,0:T(8,128)(2,1)} %get-tuple-element.221.refs_0_), channel_id=1, source_target_pairs={{0,16},{2,18},{4,20},{6,22},{8,24},{10,26},{12,28},{14,30},{16,0},... | collective-permute-start | bytes 442376 | tf_op jit(solution)/shard_map/ppermute | solution.py:587
  173.4 24.1 %feed.2 = (f32[1024,768]{1,0:T(8,128)}, bf16[1024,768]{1,0:T(8,128)(2,1)}, bf16[1024,3072]{1,0:T(8,128)(2,1)}, bf16[1024,3072]{1,0:T(8,128)(2,1)}, f32[1024,768]{1,0:T(8,128)}) custom-call(bf16[1024,768]{1,0:T(8,128)(2,1)} %get-tuple-element.216.attended_ref.refs_2_, f32[1024,768]{1,0:T(8,128)} %convert_add_fusion.hidden_ref, f32[2,768]{1,0:T(2,128)} %squeeze.136.gains_ref, ...), custom_call_target="tpu_custom_call" | custom-call | flops 679477248 | bytes 2472192 | tf_op jit(solution)/shard_map/feed/pallas_call | solution.py:231
  198.6 3.0 collective-permute-start.12
  201.5 7.2 %collective-permute-done.12.refs_1_ = bf16[2,96,768]{2,1,0:T(8,128)(2,1)S(1)} collective-permute-done((bf16[2,96,768]{2,1,0:T(8,128)(2,1)S(1)}, bf16[2,96,768]{2,1,0:T(8,128)(2,1)S(1)}, u32[]{:S(2)}, u32[]{:S(2)}) %collective-permute-start.12) | collective-permute-done | bytes 294944 | tf_op jit(solution)/shard_map/ppermute | solution.py:587
  210.4 13.2 %collective-permute-done.13.refs_1_ = bf16[4,96,768]{2,1,0:T(8,128)(2,1)S(1)} collective-permute-done((bf16[4,96,768]{2,1,0:T(8,128)(2,1)S(1)}, bf16[4,96,768]{2,1,0:T(8,128)(2,1)S(1)}, u32[]{:S(2)}, u32[]{:S(2)}) %collective-permute-start.13) | collective-permute-done | bytes 589856 | tf_op jit(solution)/shard_map/ppermute | solution.py:590
  225.8 9.1 %project.3 = (bf16[1024,768]{1,0:T(8,128)(2,1)}, bf16[1024,2304]{1,0:T(8,128)(2,1)}) custom-call(f32[1024,768]{1,0:T(8,128)} %get-tuple-element.232.hidden_ref, f32[2,768]{1,0:T(2,128)} %squeeze.138.gains_ref, f32[6,768]{1,0:T(8,128)} %squeeze.139.offsets_ref, bf16[768,6144]{1,0:T(8,128)(2,1)} %all-gather.5.cloned.1.call-done.weight_ref.out_weight_ref.up_ref), custom_call_target="tpu_custom_call" | custom-call | flops 226492416 | bytes 1181184 | tf_op jit(solution)/shard_map/project/pallas_call | solution.py:231
  234.9 15.3 %collective-permute-done.14.refs_1_ = bf16[4,192,768]{2,1,0:T(8,128)(2,1)S(1)} collective-permute-done((bf16[4,192,768]{2,1,0:T(8,128)(2,1)S(1)}, bf16[4,192,768]{2,1,0:T(8,128)(2,1)S(1)}, u32[]{:S(2)}, u32[]{:S(2)}) %collective-permute-start.14) | collective-permute-done | bytes 1179680 | tf_op jit(solution)/shard_map/ppermute | solution.py:587
  252.8 4.7 all-to-all-start.2
  258.3 25.2 %attend_forward.3 = (bf16[1024,768]{1,0:T(8,128)(2,1)}, f32[6,2,1024]{2,1,0:T(2,128)}) custom-call(bf16[1024,2304]{1,0:T(8,128)(2,1)} %get-tuple-element.238.query_ref.key_ref.value_ref, bf16[1024,2304]{1,0:T(8,128)(2,1)} %get-tuple-element.238.query_ref.key_ref.value_ref, bf16[1024,2304]{1,0:T(8,128)(2,1)} %get-tuple-element.238.query_ref.key_ref.value_ref, ...), custom_call_target="tpu_custom_call" | custom-call | flops 805306368 | bytes 393216 | tf_op jit(solution)/shard_map/attend_forward/pallas_call | solution.py:68
  287.5 23.9 %feed.3 = (f32[1024,768]{1,0:T(8,128)}, bf16[1024,768]{1,0:T(8,128)(2,1)}, bf16[1024,3072]{1,0:T(8,128)(2,1)}, bf16[1024,3072]{1,0:T(8,128)(2,1)}, bf16[1024,768]{1,0:T(8,128)(2,1)}) custom-call(bf16[1024,768]{1,0:T(8,128)(2,1)} %get-tuple-element.242.attended_ref.refs_4_, f32[1024,768]{1,0:T(8,128)} %get-tuple-element.232.hidden_ref, ...), custom_call_target="tpu_custom_call" | custom-call | flops 679477248 | bytes 2951424 | tf_op jit(solution)/shard_map/feed/pallas_call | solution.py:231
  311.4 21.4 %feed_grad.2 = (bf16[1024,768]{1,0:T(8,128)(2,1)}, bf16[1024,3072]{1,0:T(8,128)(2,1)}, f32[1024,768]{1,0:T(8,128)}, bf16[1024,768]{1,0:T(8,128)(2,1)}, bf16[1024...) custom-call(bf16[1024,768]{1,0:T(8,128)(2,1)} %bitcast.32.gradient_ref, ...), custom_call_target="tpu_custom_call" | custom-call | flops 679477248 | bytes 3050112 | tf_op jit(solution)/shard_map/feed_grad/pallas_call | solution.py:231
  332.8 19.6 %term_blocks.5 = bf16[16,48,6912]{2,1,0:T(8,128)(2,1)} custom-call(s32[1]{0:T(128)} %bitcast.21.core_ref, bf16[1024,3072]{1,0:T(8,128)(2,1)} %get-tuple-element.247.refs_0_, bf16[1024,768]{1,0:T(8,128)(2,1)} %get-tuple-element.248.refs_1_, bf16[1024,768]{1,0:T(8,128)(2,1)} %get-tuple-element.249.refs_2_, bf16[1024,3072]{1,0:T(8,128)(2,1)} %get-tuple-element.250.refs_3_, ...), custom_call_target="tpu_custom_call" | custom-call | flops 679477248 | bytes 1843200 | tf_op jit(solution)/shard_map/term_blocks/pallas_call | solution.py:545
  352.4 3.7 all-to-all-start.3
  356.2 37.7 %attend_backward.2.refs_1_.packed_grad_ref = bf16[1024,2304]{1,0:T(8,128)(2,1)} custom-call(bf16[1024,2304]{1,0:T(8,128)(2,1)} %get-tuple-element.238.query_ref.key_ref.value_ref, bf16[1024,2304]{1,0:T(8,128)(2,1)} %get-tuple-element.238.query_ref.key_ref.value_ref, bf16[1024,2304]{1,0:T(8,128)(2,1)} %get-tuple-element.238.query_ref.key_ref.value_ref, ...), custom_call_target="tpu_custom_call" | custom-call | flops 2013265920 | bytes 786432 | tf_op jit(solution)/shard_map/attend_backward/pallas_call | solution.py:151
  393.8 8.5 %term_blocks.6 = bf16[16,48,2304]{2,1,0:T(8,128)(2,1)} custom-call(s32[1]{0:T(128)} %bitcast.21.core_ref, bf16[1024,768]{1,0:T(8,128)(2,1)} %get-tuple-element.257.refs_0_, bf16[1024,2304]{1,0:T(8,128)(2,1)} %attend_backward.2.refs_1_.packed_grad_ref), custom_call_target="tpu_custom_call" | custom-call | flops 226492416 | bytes 614400 | tf_op jit(solution)/shard_map/term_blocks/pallas_call | solution.py:545
  402.4 10.5 %project_grad.2 = (f32[1024,768]{1,0:T(8,128)}, f32[8,768]{1,0:T(8,128)}) custom-call(bf16[1024,2304]{1,0:T(8,128)(2,1)} %attend_backward.2.refs_1_.packed_grad_ref, f32[1024,768]{1,0:T(8,128)} %get-tuple-element.232.hidden_ref, f32[1024,768]{1,0:T(8,128)} %get-tuple-element.259.middle_grad_ref, f32[2,768]{1,0:T(2,128)} %squeeze.138.gains_ref, ...), custom_call_target="tpu_custom_call" | custom-call | flops 226492416 | bytes 1476480 | tf_op jit(solution)/shard_map/project_grad/pallas_call | solution.py:231
  412.9 3.2 convert_element_type.337.refs_1_
  416.2 12.1 %term_blocks.7 = (bf16[8,2,48,1536]{3,2,1,0:T(8,128)(2,1)}, bf16[8,2,48,1536]{3,2,1,0:T(8,128)(2,1)}) custom-call(s32[1]{0:T(128)} %bitcast.21.core_ref, bf16[1024,3072]{1,0:T(8,128)(2,1)} %get-tuple-element.261.refs_0_, bf16[1024,768]{1,0:T(8,128)(2,1)} %convert_element_type.337.refs_1_), custom_call_target="tpu_custom_call" | custom-call | flops 301989888 | bytes 786432 | tf_op jit(solution)/shard_map/term_blocks/pallas_call | solution.py:545
  428.3 21.6 %feed_grad.3 = (bf16[1024,768]{1,0:T(8,128)(2,1)}, bf16[1024,3072]{1,0:T(8,128)(2,1)}, f32[1024,768]{1,0:T(8,128)}, bf16[1024,768]{1,0:T(8,128)(2,1)}, bf16[1024...) custom-call(f32[1024,768]{1,0:T(8,128)} %get-tuple-element.263.gradient_ref, ...), custom_call_target="tpu_custom_call" | custom-call | flops 679477248 | bytes 2570880 | tf_op jit(solution)/shard_map/feed_grad/pallas_call | solution.py:231
  449.9 12.8 %term_blocks.8 = (bf16[8,2,48,1920]{3,2,1,0:T(8,128)(2,1)}, bf16[8,2,48,1920]{3,2,1,0:T(8,128)(2,1)}) custom-call(s32[1]{0:T(128)} %bitcast.21.core_ref, bf16[1024,768]{1,0:T(8,128)(2,1)} %get-tuple-element.267.refs_0_, bf16[1024,3072]{1,0:T(8,128)(2,1)} %get-tuple-element.268.refs_1_, bf16[1024,768]{1,0:T(8,128)(2,1)} %get-tuple-element.216.attended_ref.refs_2_, ...), custom_call_target="tpu_custom_call" | custom-call | flops 377487360 | bytes 1056768 | tf_op jit(solution)/shard_map/term_blocks/pallas_call | solution.py:545
  463.4 8.6 %collective-permute-done.16 = bf16[8,2,48,1536]{3,2,1,0:T(8,128)(2,1)} collective-permute-done((bf16[8,2,48,1536]{3,2,1,0:T(8,128)(2,1)}, bf16[8,2,48,1536]{3,2,1,0:T(8,128)(2,1)}, u32[]{:S(2)}, u32[]{:S(2)}) %collective-permute-start.16) | collective-permute-done | bytes 2359328 | tf_op jit(solution)/shard_map/ppermute | solution.py:587
  472.1 3.1 fusion.5
  475.2 2.9 fusion.3
  480.1 37.0 %attend_backward.3.refs_1_.packed_grad_ref = bf16[1024,2304]{1,0:T(8,128)(2,1)} custom-call(bf16[1024,2304]{1,0:T(8,128)(2,1)} %get-tuple-element.209.query_ref.key_ref.value_ref, bf16[1024,2304]{1,0:T(8,128)(2,1)} %get-tuple-element.209.query_ref.key_ref.value_ref, bf16[1024,2304]{1,0:T(8,128)(2,1)} %get-tuple-element.209.query_ref.key_ref.value_ref, ...), custom_call_target="tpu_custom_call" | custom-call | flops 2013265920 | bytes 786432 | tf_op jit(solution)/shard_map/attend_backward/pallas_call | solution.py:151
  517.1 9.8 %term_blocks.9 = (bf16[8,2,48,1152]{3,2,1,0:T(8,128)(2,1)}, bf16[8,2,48,1152]{3,2,1,0:T(8,128)(2,1)}) custom-call(s32[1]{0:T(128)} %bitcast.21.core_ref, bf16[1024,768]{1,0:T(8,128)(2,1)} %get-tuple-element.291.refs_0_, bf16[1024,2304]{1,0:T(8,128)(2,1)} %attend_backward.3.refs_1_.packed_grad_ref), custom_call_target="tpu_custom_call" | custom-call | flops 226492416 | bytes 614400 | tf_op jit(solution)/shard_map/term_blocks/pallas_call | solution.py:545
  526.9 11.3 %collective-permute-done.18 = bf16[2,2,2,48,1536]{4,3,2,1,0:T(8,128)(2,1)} collective-permute-done((bf16[2,2,2,48,1536]{4,3,2,1,0:T(8,128)(2,1)}, bf16[2,2,2,48,1536]{4,3,2,1,0:T(8,128)(2,1)}, u32[]{:S(2)}, u32[]{:S(2)}) %collective-permute-start.18) | collective-permute-done | bytes 1179680 | tf_op jit(solution)/shard_map/ppermute | solution.py:587
  538.2 3.0 fusion.4
  545.4 14.4 %collective-permute-done.20 = bf16[2,2,48,1536]{3,2,1,0:T(8,128)(2,1)} collective-permute-done((bf16[2,2,48,1536]{3,2,1,0:T(8,128)(2,1)}, bf16[2,2,48,1536]{3,2,1,0:T(8,128)(2,1)}, u32[]{:S(2)}, u32[]{:S(2)}) %collective-permute-start.20) | collective-permute-done | bytes 589856 | tf_op jit(solution)/shard_map/ppermute | solution.py:587
  571.3 10.3 %project_grad.3 = (bf16[1024,768]{1,0:T(8,128)(2,1)}, f32[8,768]{1,0:T(8,128)}) custom-call(bf16[1024,2304]{1,0:T(8,128)(2,1)} %attend_backward.3.refs_1_.packed_grad_ref, f32[1024,768]{1,0:T(8,128)} %convert_add_fusion.hidden_ref, f32[1024,768]{1,0:T(8,128)} %get-tuple-element.303.middle_grad_ref, f32[2,768]{1,0:T(2,128)} %squeeze.136.gains_ref, ...), custom_call_target="tpu_custom_call" | custom-call | flops 226492416 | bytes 1095552 | tf_op jit(solution)/shard_map/project_grad/pallas_call | solution.py:231
  584.5 17.4 %collective-permute-done.23 = bf16[2,2,48,1920]{3,2,1,0:T(8,128)(2,1)} collective-permute-done((bf16[2,2,48,1920]{3,2,1,0:T(8,128)(2,1)}, bf16[2,2,48,1920]{3,2,1,0:T(8,128)(2,1)}, u32[]{:S(2)}, u32[]{:S(2)}) %collective-permute-start.23) | collective-permute-done | bytes 737312 | tf_op jit(solution)/shard_map/ppermute | solution.py:587
  608.4 3.8 all-to-all-start.4
  618.0 11.2 %all-to-all-done.4 = bf16[2,512,768]{2,1,0:T(8,128)(2,1)S(1)} async-done(((bf16[2,512,768]{2,1,0:T(8,128)(2,1)}), bf16[2,512,768]{2,1,0:T(8,128)(2,1)S(1)}, u32[]{:S(2)}, u32[]{:S(2)}) %all-to-all-start.4) | async-done | bytes 1572896 | tf_op jit(solution)/shard_map/all_to_all | solution.py:766
  645.9 5.7 collective-permute-done.30
  661.0 3.4 collective-permute-done.36
  (282 shorter events, 120.9 us)
Async XLA Ops:
  7.2 85.3 %copy-start = (f32[2,768]{1,0:T(2,128)S(1)}, f32[2,768]{1,0:T(2,128)}, u32[]{:S(2)}) copy-start(f32[2,768]{1,0:T(2,128)} %param.13) | copy-start | bytes 18436
  7.2 88.6 %all-gather.3.cloned.1.call-start = ((), (), s32[]{:S(2)}) async-start(), calls=%async_computation.7 | async-start | bytes 5222400 | tf_op jit(solution)/shard_map/all_gather | solution.py:694
  12.6 213.2 %all-gather.5.cloned.1.call-start = ((), (), s32[]{:S(2)}) async-start(), calls=%async_computation.8 | async-start | bytes 10027008 | tf_op jit(solution)/shard_map/all_gather | solution.py:694
  14.4 19.7 %collective-permute-start = (bf16[1,48,1536]{2,1,0:T(8,128)(2,1)S(1)}, bf16[1,48,1536]{2,1,0:T(8,128)(2,1)S(1)}, u32[]{:S(2)}, u32[]{:S(2)}) collective-permute-start(bf16[1,48,1536]{2,1,0:T(8,128)(2,1)S(1)} %constant_dynamic-slice_fusion.11.refs_0_), channel_id=1, source_target_pairs={{0,16},{2,18},{4,20},{6,22},{8,24},{10,26},{12,28},{14,30},{16,0},... | collective-permute-start | bytes 442376 | tf_op jit(solution)/shard_map/ppermute | solution.py:587
  18.5 23.2 %collective-permute-start.1 = (bf16[1,96,768]{2,1,0:T(8,128)(2,1)S(1)}, bf16[1,96,768]{2,1,0:T(8,128)(2,1)S(1)}, u32[]{:S(2)}, u32[]{:S(2)}) collective-permute-start(bf16[1,96,768]{2,1,0:T(8,128)(2,1)S(1)} %get-tuple-element.186.refs_0_), channel_id=1, source_target_pairs={{0,16},{2,18},{4,20},{6,22},{8,24},{10,26},{12,28},{14,30},{16,0},... | collective-permute-start | bytes 442376 | tf_op jit(solution)/shard_map/ppermute | solution.py:587
  42.5 17.1 %collective-permute-start.2 = (bf16[2,48,1536]{2,1,0:T(8,128)(2,1)S(1)}, bf16[2,48,1536]{2,1,0:T(8,128)(2,1)S(1)}, u32[]{:S(2)}, u32[]{:S(2)}) collective-permute-start(bf16[2,48,1536]{2,1,0:T(8,128)(2,1)S(1)} %bitcast.211), channel_id=1, source_target_pairs={{0,8},{2,10},{4,12},{6,14},{8,0},{10,2},{12,4},{14,6},{16,24},{18,... | collective-permute-start | bytes 884744 | tf_op jit(solution)/shard_map/ppermute | solution.py:587
  43.3 29.9 %collective-permute-start.3 = (bf16[2,96,768]{2,1,0:T(8,128)(2,1)S(1)}, bf16[2,96,768]{2,1,0:T(8,128)(2,1)S(1)}, u32[]{:S(2)}, u32[]{:S(2)}) collective-permute-start(bf16[2,96,768]{2,1,0:T(8,128)(2,1)S(1)} %bitcast.213), channel_id=1, source_target_pairs={{0,8},{2,10},{4,12},{6,14},{8,0},{10,2},{12,4},{14,6},{16,24},{18,... | collective-permute-start | bytes 884744 | tf_op jit(solution)/shard_map/ppermute | solution.py:587
  51.1 41.4 %all-to-all-start.1 = ((bf16[2,512,768]{2,1,0:T(8,128)(2,1)}), bf16[2,512,768]{2,1,0:T(8,128)(2,1)}, u32[]{:S(2)}, u32[]{:S(2)}) async-start(bf16[2,512,768]{2,1,0:T(8,128)(2,1)} %param.12), calls=%async_computation.1 | async-start | bytes 3145728 | tf_op jit(solution)/shard_map/all_to_all | solution.py:578
  73.3 9.9 %collective-permute-start.4 = (bf16[4,48,1536]{2,1,0:T(8,128)(2,1)S(1)}, bf16[4,48,1536]{2,1,0:T(8,128)(2,1)S(1)}, u32[]{:S(2)}, u32[]{:S(2)}) collective-permute-start(bf16[4,48,1536]{2,1,0:T(8,128)(2,1)S(1)} %bitcast.207), channel_id=1, source_target_pairs={{0,4},{2,6},{4,0},{6,2},{8,12},{10,14},{12,8},{14,10},{16,20},{18,... | collective-permute-start | bytes 1769480 | tf_op jit(solution)/shard_map/ppermute | solution.py:587
  75.7 12.8 %collective-permute-start.5 = (bf16[4,96,768]{2,1,0:T(8,128)(2,1)S(1)}, bf16[4,96,768]{2,1,0:T(8,128)(2,1)S(1)}, u32[]{:S(2)}, u32[]{:S(2)}) collective-permute-start(bf16[4,96,768]{2,1,0:T(8,128)(2,1)S(1)} %bitcast.205), channel_id=1, source_target_pairs={{0,1},{1,0},{2,3},{3,2},{4,5},{5,4},{6,7},{7,6},{8,9},{9,8},{10,11... | collective-permute-start | bytes 1769480 | tf_op jit(solution)/shard_map/ppermute | solution.py:590
  89.9 21.1 %collective-permute-start.6 = (bf16[8,48,1536]{2,1,0:T(8,128)(2,1)S(1)}, bf16[8,48,1536]{2,1,0:T(8,128)(2,1)}, u32[]{:S(2)}, u32[]{:S(2)}) collective-permute-start(bf16[8,48,1536]{2,1,0:T(8,128)(2,1)S(1)} %bitcast.198), channel_id=1, source_target_pairs={{0,1},{1,0},{2,3},{3,2},{4,5},{5,4},{6,7},{7,6},{8,9},{9,8},{10,11... | collective-permute-start | bytes 3538952 | tf_op jit(solution)/shard_map/ppermute | solution.py:590
  92.5 22.6 %collective-permute-start.7 = (bf16[4,192,768]{2,1,0:T(8,128)(2,1)S(1)}, bf16[4,192,768]{2,1,0:T(8,128)(2,1)}, u32[]{:S(2)}, u32[]{:S(2)}) collective-permute-start(bf16[4,192,768]{2,1,0:T(8,128)(2,1)S(1)} %bitcast.201), channel_id=1, source_target_pairs={{0,4},{2,6},{4,0},{6,2},{8,12},{10,14},{12,8},{14,10},{16,20},{18,... | collective-permute-start | bytes 3538952 | tf_op jit(solution)/shard_map/ppermute | solution.py:587
  116.5 32.3 %collective-permute-start.10 = (bf16[8,192,768]{2,1,0:T(8,128)(2,1)S(1)}, bf16[8,192,768]{2,1,0:T(8,128)(2,1)}, u32[]{:S(2)}, u32[]{:S(2)}) collective-permute-start(bf16[8,192,768]{2,1,0:T(8,128)(2,1)S(1)} %bitcast.194), channel_id=1, source_target_pairs={{0,2},{2,0},{4,6},{6,4},{8,10},{10,8},{12,14},{14,12},{16,18},{18,... | collective-permute-start | bytes 7077896 | tf_op jit(solution)/shard_map/ppermute | solution.py:587
  116.6 32.2 %collective-permute-start.8 = (bf16[8,48,1536]{2,1,0:T(8,128)(2,1)S(1)}, bf16[8,48,1536]{2,1,0:T(8,128)(2,1)}, u32[]{:S(2)}, u32[]{:S(2)}) collective-permute-start(bf16[8,48,1536]{2,1,0:T(8,128)(2,1)S(1)} %bitcast.199), channel_id=1, source_target_pairs={{0,2},{2,0},{4,6},{6,4},{8,10},{10,8},{12,14},{14,12},{16,18},{18,... | collective-permute-start | bytes 3538952 | tf_op jit(solution)/shard_map/ppermute | solution.py:587
  117.1 31.7 %collective-permute-start.9 = (bf16[8,48,1536]{2,1,0:T(8,128)(2,1)}, bf16[8,48,1536]{2,1,0:T(8,128)(2,1)}, u32[]{:S(2)}, u32[]{:S(2)}) collective-permute-start(bf16[8,48,1536]{2,1,0:T(8,128)(2,1)} %collective-permute-done.6.refs_1_), channel_id=1, source_target_pairs={{0,2},{2,0},{4,6},{6,4},{8,10},{10,8},{12,14},{14,12},{16,18},{18,... | collective-permute-start | bytes 3538952 | tf_op jit(solution)/shard_map/ppermute | solution.py:587
  148.8 48.7 %collective-permute-start.11 = (bf16[1,96,768]{2,1,0:T(8,128)(2,1)}, bf16[1,96,768]{2,1,0:T(8,128)(2,1)}, u32[]{:S(2)}, u32[]{:S(2)}) collective-permute-start(bf16[1,96,768]{2,1,0:T(8,128)(2,1)} %get-tuple-element.221.refs_0_), channel_id=1, source_target_pairs={{0,16},{2,18},{4,20},{6,22},{8,24},{10,26},{12,28},{14,30},{16,0},... | collective-permute-start | bytes 442376 | tf_op jit(solution)/shard_map/ppermute | solution.py:587
  198.5 26.5 %copy-start.22 = (f32[1,6,16,48]{3,1,0,2:T(8,128)S(1)}, f32[1,6,16,48]{3,1,0,2:T(8,128)}, u32[]{:S(2)}) copy-start(f32[1,6,16,48]{3,1,0,2:T(8,128)} %get-tuple-element.420) | copy-start | bytes 55300
  198.6 10.2 %collective-permute-start.12 = (bf16[2,96,768]{2,1,0:T(8,128)(2,1)S(1)}, bf16[2,96,768]{2,1,0:T(8,128)(2,1)S(1)}, u32[]{:S(2)}, u32[]{:S(2)}) collective-permute-start(bf16[2,96,768]{2,1,0:T(8,128)(2,1)S(1)} %bitcast.215), channel_id=1, source_target_pairs={{0,8},{2,10},{4,12},{6,14},{8,0},{10,2},{12,4},{14,6},{16,24},{18,... | collective-permute-start | bytes 884744 | tf_op jit(solution)/shard_map/ppermute | solution.py:587
  208.8 14.8 %collective-permute-start.13 = (bf16[4,96,768]{2,1,0:T(8,128)(2,1)S(1)}, bf16[4,96,768]{2,1,0:T(8,128)(2,1)S(1)}, u32[]{:S(2)}, u32[]{:S(2)}) collective-permute-start(bf16[4,96,768]{2,1,0:T(8,128)(2,1)S(1)} %bitcast.209), channel_id=1, source_target_pairs={{0,1},{1,0},{2,3},{3,2},{4,5},{5,4},{6,7},{7,6},{8,9},{9,8},{10,11... | collective-permute-start | bytes 1769480 | tf_op jit(solution)/shard_map/ppermute | solution.py:590
  223.7 26.5 %collective-permute-start.14 = (bf16[4,192,768]{2,1,0:T(8,128)(2,1)S(1)}, bf16[4,192,768]{2,1,0:T(8,128)(2,1)S(1)}, u32[]{:S(2)}, u32[]{:S(2)}) collective-permute-start(bf16[4,192,768]{2,1,0:T(8,128)(2,1)S(1)} %bitcast.203), channel_id=1, source_target_pairs={{0,4},{2,6},{4,0},{6,2},{8,12},{10,14},{12,8},{14,10},{16,20},{18,... | collective-permute-start | bytes 3538952 | tf_op jit(solution)/shard_map/ppermute | solution.py:587
  252.8 30.7 %collective-permute-start.15 = (bf16[8,192,768]{2,1,0:T(8,128)(2,1)S(1)}, bf16[8,192,768]{2,1,0:T(8,128)(2,1)}, u32[]{:S(2)}, u32[]{:S(2)}) collective-permute-start(bf16[8,192,768]{2,1,0:T(8,128)(2,1)S(1)} %bitcast.196), channel_id=1, source_target_pairs={{0,2},{2,0},{4,6},{6,4},{8,10},{10,8},{12,14},{14,12},{16,18},{18,... | collective-permute-start | bytes 7077896 | tf_op jit(solution)/shard_map/ppermute | solution.py:587
  252.8 58.5 %all-to-all-start.2 = ((bf16[2,512,768]{2,1,0:T(8,128)(2,1)}), bf16[2,512,768]{2,1,0:T(8,128)(2,1)}, u32[]{:S(2)}, u32[]{:S(2)}) async-start(bf16[2,512,768]{2,1,0:T(8,128)(2,1)} %param.16), calls=%async_computation.2 | async-start | bytes 3145728 | tf_op jit(solution)/shard_map/all_to_all | solution.py:578
  257.6 280.7 %reduce-scatter.3.cloned.1.call-start = ((), (), s32[]{:S(2)}) async-start(), calls=%async_computation.9 | async-start | bytes 11280384 | tf_op jit(solution)/shard_map/reduce_scatter | solution.py:593
  352.4 41.4 %all-to-all-start.3 = ((bf16[2,512,768]{2,1,0:T(8,128)(2,1)}), bf16[2,512,768]{2,1,0:T(8,128)(2,1)S(1)}, u32[]{:S(2)}, u32[]{:S(2)}) async-start(bf16[2,512,768]{2,1,0:T(8,128)(2,1)} %bitcast.35), calls=%async_computation.3 | async-start | bytes 3145728 | tf_op jit(solution)/shard_map/all_to_all | solution.py:766
  356.1 274.4 %reduce-scatter.5.cloned.1.call-start = ((), (), s32[]{:S(2)}) async-start(), calls=%async_computation.10 | async-start | bytes 3760128 | tf_op jit(solution)/shard_map/reduce_scatter | solution.py:593
  462.7 12.5 %collective-permute-start.17 = (bf16[8,2,48,1920]{3,2,1,0:T(8,128)(2,1)}, bf16[8,2,48,1920]{3,2,1,0:T(8,128)(2,1)}, u32[]{:S(2)}, u32[]{:S(2)}) collective-permute-start(bf16[8,2,48,1920]{3,2,1,0:T(8,128)(2,1)} %get-tuple-element.277), channel_id=1, source_target_pairs={{0,2},{2,0},{4,6},{6,4},{8,10},{10,8},{12,14},{14,12},{16,18},{18,... | collective-permute-start | bytes 8847368 | tf_op jit(solution)/shard_map/ppermute | solution.py:587
  463.4 8.7 %collective-permute-start.16 = (bf16[8,2,48,1536]{3,2,1,0:T(8,128)(2,1)}, bf16[8,2,48,1536]{3,2,1,0:T(8,128)(2,1)}, u32[]{:S(2)}, u32[]{:S(2)}) collective-permute-start(bf16[8,2,48,1536]{3,2,1,0:T(8,128)(2,1)} %get-tuple-element.272), channel_id=1, source_target_pairs={{0,2},{2,0},{4,6},{6,4},{8,10},{10,8},{12,14},{14,12},{16,18},{18,... | collective-permute-start | bytes 7077896 | tf_op jit(solution)/shard_map/ppermute | solution.py:587
  478.1 60.2 %collective-permute-start.19 = (bf16[2,2,2,48,1920]{4,3,2,1,0:T(8,128)(2,1)}, bf16[2,2,2,48,1920]{4,3,2,1,0:T(8,128)(2,1)S(1)}, u32[]{:S(2)}, u32[]{:S(2)}) collective-permute-start(bf16[2,2,2,48,1920]{4,3,2,1,0:T(8,128)(2,1)} %fusion.3), channel_id=1, source_target_pairs={{0,4},{2,6},{4,0},{6,2},{8,12},{10,14},{12,8},{14,10},{16,20},{18,... | collective-permute-start | bytes 4423688 | tf_op jit(solution)/shard_map/ppermute | solution.py:587
  478.5 59.7 %collective-permute-start.18 = (bf16[2,2,2,48,1536]{4,3,2,1,0:T(8,128)(2,1)}, bf16[2,2,2,48,1536]{4,3,2,1,0:T(8,128)(2,1)}, u32[]{:S(2)}, u32[]{:S(2)}) collective-permute-start(bf16[2,2,2,48,1536]{4,3,2,1,0:T(8,128)(2,1)} %fusion.5), channel_id=1, source_target_pairs={{0,4},{2,6},{4,0},{6,2},{8,12},{10,14},{12,8},{14,10},{16,20},{18,... | collective-permute-start | bytes 3538952 | tf_op jit(solution)/shard_map/ppermute | solution.py:587
  543.7 18.2 %collective-permute-start.21 = (bf16[8,2,48,1152]{3,2,1,0:T(8,128)(2,1)}, bf16[8,2,48,1152]{3,2,1,0:T(8,128)(2,1)}, u32[]{:S(2)}, u32[]{:S(2)}) collective-permute-start(bf16[8,2,48,1152]{3,2,1,0:T(8,128)(2,1)} %get-tuple-element.298), channel_id=1, source_target_pairs={{0,2},{2,0},{4,6},{6,4},{8,10},{10,8},{12,14},{14,12},{16,18},{18,... | collective-permute-start | bytes 5308424 | tf_op jit(solution)/shard_map/ppermute | solution.py:587
  543.7 16.1 %collective-permute-start.20 = (bf16[2,2,48,1536]{3,2,1,0:T(8,128)(2,1)}, bf16[2,2,48,1536]{3,2,1,0:T(8,128)(2,1)}, u32[]{:S(2)}, u32[]{:S(2)}) collective-permute-start(bf16[2,2,48,1536]{3,2,1,0:T(8,128)(2,1)} %fusion.6), channel_id=1, source_target_pairs={{0,8},{2,10},{4,12},{6,14},{8,0},{10,2},{12,4},{14,6},{16,24},{18,... | collective-permute-start | bytes 1769480 | tf_op jit(solution)/shard_map/ppermute | solution.py:587
  564.2 37.7 %collective-permute-start.24 = (bf16[2,2,2,48,1152]{4,3,2,1,0:T(8,128)(2,1)}, bf16[2,2,2,48,1152]{4,3,2,1,0:T(8,128)(2,1)}, u32[]{:S(2)}, u32[]{:S(2)}) collective-permute-start(bf16[2,2,2,48,1152]{4,3,2,1,0:T(8,128)(2,1)} %fusion.7), channel_id=1, source_target_pairs={{0,4},{2,6},{4,0},{6,2},{8,12},{10,14},{12,8},{14,10},{16,20},{18,... | collective-permute-start | bytes 2654216 | tf_op jit(solution)/shard_map/ppermute | solution.py:587
  564.7 37.2 %collective-permute-start.23 = (bf16[2,2,48,1920]{3,2,1,0:T(8,128)(2,1)}, bf16[2,2,48,1920]{3,2,1,0:T(8,128)(2,1)}, u32[]{:S(2)}, u32[]{:S(2)}) collective-permute-start(bf16[2,2,48,1920]{3,2,1,0:T(8,128)(2,1)} %fusion.4), channel_id=1, source_target_pairs={{0,8},{2,10},{4,12},{6,14},{8,0},{10,2},{12,4},{14,6},{16,24},{18,... | collective-permute-start | bytes 2211848 | tf_op jit(solution)/shard_map/ppermute | solution.py:587
  568.2 16.3 %collective-permute-start.25 = (bf16[48,6912]{1,0:T(8,128)(2,1)}, bf16[48,6912]{1,0:T(8,128)(2,1)S(1)}, u32[]{:S(2)}, u32[]{:S(2)}) collective-permute-start(bf16[48,6912]{1,0:T(8,128)(2,1)} %reduce-scatter.3.cloned.1.call-done), channel_id=1, source_target_pairs={{0,1},{1,0},{2,3},{3,2},{4,5},{5,4},{6,7},{7,6},{8,9},{9,8},{10,11... | collective-permute-start | bytes 1990664 | tf_op jit(solution)/shard_map/ppermute | solution.py:590
  569.9 32.1 %collective-permute-start.22 = (bf16[2,48,1536]{2,1,0:T(8,128)(2,1)}, bf16[2,48,1536]{2,1,0:T(8,128)(2,1)S(1)}, u32[]{:S(2)}, u32[]{:S(2)}) collective-permute-start(bf16[2,48,1536]{2,1,0:T(8,128)(2,1)} %fusion.15), channel_id=1, source_target_pairs={{0,16},{2,18},{4,20},{6,22},{8,24},{10,26},{12,28},{14,30},{16,0},... | collective-permute-start | bytes 884744 | tf_op jit(solution)/shard_map/ppermute | solution.py:587
  608.4 20.8 %all-to-all-start.4 = ((bf16[2,512,768]{2,1,0:T(8,128)(2,1)}), bf16[2,512,768]{2,1,0:T(8,128)(2,1)S(1)}, u32[]{:S(2)}, u32[]{:S(2)}) async-start(bf16[2,512,768]{2,1,0:T(8,128)(2,1)} %bitcast.231), calls=%async_computation.5 | async-start | bytes 3145728 | tf_op jit(solution)/shard_map/all_to_all | solution.py:766
  612.2 21.8 %collective-permute-start.28 = (bf16[2,2,48,1152]{3,2,1,0:T(8,128)(2,1)}, bf16[2,2,48,1152]{3,2,1,0:T(8,128)(2,1)}, u32[]{:S(2)}, u32[]{:S(2)}) collective-permute-start(bf16[2,2,48,1152]{3,2,1,0:T(8,128)(2,1)} %fusion.8), channel_id=1, source_target_pairs={{0,8},{2,10},{4,12},{6,14},{8,0},{10,2},{12,4},{14,6},{16,24},{18,... | collective-permute-start | bytes 1327112 | tf_op jit(solution)/shard_map/ppermute | solution.py:587
  612.3 20.1 %collective-permute-start.27 = (bf16[2,48,1920]{2,1,0:T(8,128)(2,1)}, bf16[2,48,1920]{2,1,0:T(8,128)(2,1)}, u32[]{:S(2)}, u32[]{:S(2)}) collective-permute-start(bf16[2,48,1920]{2,1,0:T(8,128)(2,1)} %fusion.11), channel_id=1, source_target_pairs={{0,16},{2,18},{4,20},{6,22},{8,24},{10,26},{12,28},{14,30},{16,0},... | collective-permute-start | bytes 1105928 | tf_op jit(solution)/shard_map/ppermute | solution.py:587
  613.8 18.7 %collective-permute-start.26 = (bf16[2,48,1536]{2,1,0:T(8,128)(2,1)S(1)}, bf16[2,48,1536]{2,1,0:T(8,128)(2,1)}, u32[]{:S(2)}, u32[]{:S(2)}) collective-permute-start(bf16[2,48,1536]{2,1,0:T(8,128)(2,1)S(1)} %copy-done.16), channel_id=1, source_target_pairs={{0,1},{1,0},{2,3},{3,2},{4,5},{5,4},{6,7},{7,6},{8,9},{9,8},{10,11... | collective-permute-start | bytes 884744 | tf_op jit(solution)/shard_map/ppermute | solution.py:590
  629.2 4.8 collective-permute-start.29
  638.0 13.6 %collective-permute-start.31 = (bf16[2,48,1920]{2,1,0:T(8,128)(2,1)S(1)}, bf16[2,48,1920]{2,1,0:T(8,128)(2,1)S(1)}, u32[]{:S(2)}, u32[]{:S(2)}) collective-permute-start(bf16[2,48,1920]{2,1,0:T(8,128)(2,1)S(1)} %fusion.10), channel_id=1, source_target_pairs={{0,1},{1,0},{2,3},{3,2},{4,5},{5,4},{6,7},{7,6},{8,9},{9,8},{10,11... | collective-permute-start | bytes 1105928 | tf_op jit(solution)/shard_map/ppermute | solution.py:590
  639.8 11.8 %collective-permute-start.30 = (bf16[48,2304]{1,0:T(8,128)(2,1)S(1)}, bf16[48,2304]{1,0:T(8,128)(2,1)S(1)}, u32[]{:S(2)}, u32[]{:S(2)}) collective-permute-start(bf16[48,2304]{1,0:T(8,128)(2,1)S(1)} %copy-done.23), channel_id=1, source_target_pairs={{0,1},{1,0},{2,3},{3,2},{4,5},{5,4},{6,7},{7,6},{8,9},{9,8},{10,11... | collective-permute-start | bytes 663560 | tf_op jit(solution)/shard_map/ppermute | solution.py:590
  640.1 11.5 %collective-permute-start.32 = (bf16[2,48,1152]{2,1,0:T(8,128)(2,1)S(1)}, bf16[2,48,1152]{2,1,0:T(8,128)(2,1)S(1)}, u32[]{:S(2)}, u32[]{:S(2)}) collective-permute-start(bf16[2,48,1152]{2,1,0:T(8,128)(2,1)S(1)} %fusion.18), channel_id=1, source_target_pairs={{0,16},{2,18},{4,20},{6,22},{8,24},{10,26},{12,28},{14,30},{16,0},... | collective-permute-start | bytes 663560 | tf_op jit(solution)/shard_map/ppermute | solution.py:587
  641.9 4.0 collective-permute-start.33
  653.9 6.0 collective-permute-start.34
  655.5 3.7 collective-permute-start.35
  659.9 4.6 collective-permute-start.36
  664.5 3.7 collective-permute-start.37
  (33 other events, 185.0 us)
Sparse Core Ops, SparseCore 0:
  12.7 65.5 all-gather.2
  80.6 89.8 all-gather.4
  352.5 119.6 reduce-scatter.2
  544.8 85.6 reduce-scatter.4

commit v7 on v6

--- a/solution.py
+++ b/solution.py
@@ -717,7 +717,7 @@
         begin(gather_columns(up_weight[0]), functools.partial(ups.__setitem__, 0)),
         begin(gather_rows(down_weight[0]), functools.partial(downs.__setitem__, 0)),
     ]
-    for _ in chip_bits:
+    for _ in chip_bits[1:]:
         time_embed = advance(time_embed, *fetches)
     my_time = lax.dynamic_index_in_dim(time_embed, place, 0, keepdims=True)
     hidden = my_tokens.astype(single) + my_time
@@ -839,9 +839,6 @@
         gains = all_gains[layer]
         hidden, normed, packed, totals, attended, middle, second, activated, slope = saved[layer]
         steps = scatter_group if layer else reduce_group
-        if not layer:
-            first = begin_group(steps, layer, [(3, (activated, gradient.astype(half)))])
-            gradient = launch(gradient, [first])
         branch, upper, middle_grad, attention_grad, upstream, sums, unit_sums = feed_grad(
             gradient, slope, middle, gains, whole, up, down
         )
@@ -850,29 +847,37 @@
             held.append(begin_group(steps, layer, [(3, (activated, branch))] + named))
             upstream = launch(upstream, held[-1:])
         else:
+            upstream = advance(upstream, first_group)
+            upper, upstream = lax.optimization_barrier((upper, upstream))
+            named = [(2, (second, upper)), (1, (attended, attention_grad))]
             second_group = begin_group(steps, layer, named)
             upstream = launch(upstream, [second_group])
-            upstream = advance(upstream, first)
             upstream = advance(upstream, second_group)
         packed_grad = attend_backward(packed, bias, upstream, totals, attended)
         if layer == layers - 1:
             packed_grad, output = lax.optimization_barrier((packed_grad, output))
             output = output.astype(single)
         named = [(0, (normed, packed_grad))]
-        if layer:
-            held.append(begin_group(steps, layer, named))
-            packed_grad = launch(packed_grad, held[-1:])
-        else:
-            packed_grad = advance(packed_grad, first, second_group, *held[:1])
+        if not layer:
+            packed_grad = advance(packed_grad, first_group, second_group, *held[:1])
             last_group = begin_group(steps, layer, named)
             packed_grad = launch(packed_grad, [last_group])
-            packed_grad = advance(packed_grad, first)
             packed_grad = advance(packed_grad, last_group)
         gradient, more_sums = project_grad(
             packed_grad, hidden, middle_grad, gains, whole, single if layer else half
         )
+        if layer == 1:
+            below = (saved[0][7], gradient.astype(half))
+            first_group = begin_group(reduce_group, 0, [(3, below)])
+            gradient = launch(gradient, [first_group])
+        if layer:
+            held.append(begin_group(steps, layer, named))
+            gradient = launch(gradient, held[-1:])
+        if layer == 1:
+            gradient = advance(gradient, first_group)
         if not layer:
-            gradient = advance(gradient, first, second_group, last_group, *held[:1])
+            gradient = advance(gradient, first_group, second_group, *held)
+            gradient = advance(gradient, last_group)
         small_grads[layer] = (
             jnp.stack([more_sums[0], sums[1]]),
             jnp.stack([more_sums[1], more_sums[2], more_sums[3], sums[3], sums[2], sums[0]]),

time: 690 us -> 686 us (level)
  starting transfers between devices: 71 us -> 59.2 us
  waiting for transfers between devices: 172 us -> 179 us
    ppermute x29, starting transfers between devices: 39.1 us -> 27.3 us  [across(): return lambda part: lax.ppermute(part, 'wide', pairs)]
    ppermute x29, waiting for transfers between devices: 131 us -> 141 us  [across(): return lambda part: lax.ppermute(part, 'wide', pairs)]
  transfers between devices with their start and end apart: 46 -> 47, of which waited for: 24 -> 23; matrix products, arithmetic and copies ran while one was open for 8% -> 9% of each run, Pallas kernels for 42% -> 42%
where the time goes in v7:
time: 686 us; the launch traced here: 674 us
  Pallas kernels  328 us (48%)
  waiting for transfers between devices  179 us (26%)
  starting transfers between devices  59.2 us (9%)
  other arithmetic  54.4 us (8%)
  local copies, waits for them, and re-layouts  39.2 us (6%)
  between operations  15 us (2%)
    ppermute x29, waiting for transfers between devices, across(): return lambda part: lax.ppermute(part, 'wide', pairs)  141 us
    pallas_call x8, Pallas kernels, row_tiled(): pl.pallas_call(kernel, grid=(length // ROW_TILE,), in_specs=in_specs, out...  130 us
    pallas_call x2, Pallas kernels, attend_backward(): pl.pallas_call(functools.partial(attend_grad_kernel, rows=BACKWARD_ROWS),...  75 us
    pallas_call x5, Pallas kernels, term_blocks(): pl.pallas_call(kernel, in_specs=[pl.BlockSpec(memory_space=pltpu.SMEM)] +...  62.9 us
    pallas_call x2, Pallas kernels, attend_forward(): pl.pallas_call(functools.partial(attend_kernel, rows=FORWARD_ROWS), grid=...  50.4 us
    ppermute x29, starting transfers between devices, across(): return lambda part: lax.ppermute(part, 'wide', pairs)  27.3 us
    ppermute x9, waiting for transfers between devices, beside_seq(): return lax.ppermute(part, 'seq', swap)  23.4 us
    convert_element_type x9, other arithmetic, reduce_group(): total_of([side_of(part, 1 - mine, axis) for part in addends]).astype(half)  21.3 us
  transfers between devices with their start and end apart: 47, of which 23 were waited for; matrix products, arithmetic and copies ran while one was open for 9% of the time, Pallas kernels for 42%

profile of v7, /device:TPU:0, one launch (start us, length us, event | category | flops | bytes accessed | tf_op | source)
XLA Modules:
  0.0 674.3 jit_solution(2397533698630934322)
XLA Ops:
  14.2 4.2 all-to-all-start
  18.5 3.8 all-to-all-done
  22.3 4.6 all-to-all-start.1
  27.6 3.1 collective-permute-start
  30.8 16.4 %collective-permute-done.refs_1_ = bf16[1,48,1536]{2,1,0:T(8,128)(2,1)S(1)} collective-permute-done((bf16[1,48,1536]{2,1,0:T(8,128)(2,1)S(1)}, bf16[1,48,1536]{2,1,0:T(8,128)(2,1)S(1)}, u32[]{:S(2)}, u32[]{:S(2)}) %collective-permute-start) | collective-permute-done | bytes 147488 | tf_op jit(solution)/shard_map/ppermute | solution.py:587
  47.2 2.8 collective-permute-done.1.refs_1_
  52.9 20.2 %collective-permute-done.2.refs_1_ = bf16[2,48,1536]{2,1,0:T(8,128)(2,1)S(1)} collective-permute-done((bf16[2,48,1536]{2,1,0:T(8,128)(2,1)S(1)}, bf16[2,48,1536]{2,1,0:T(8,128)(2,1)S(1)}, u32[]{:S(2)}, u32[]{:S(2)}) %collective-permute-start.2) | collective-permute-done | bytes 294944 | tf_op jit(solution)/shard_map/ppermute | solution.py:587
  73.1 12.4 %collective-permute-done.3.refs_1_ = bf16[2,96,768]{2,1,0:T(8,128)(2,1)S(1)} collective-permute-done((bf16[2,96,768]{2,1,0:T(8,128)(2,1)S(1)}, bf16[2,96,768]{2,1,0:T(8,128)(2,1)S(1)}, u32[]{:S(2)}, u32[]{:S(2)}) %collective-permute-start.3) | collective-permute-done | bytes 294944 | tf_op jit(solution)/shard_map/ppermute | solution.py:587
  88.9 3.3 convert_add_fusion.hidden_ref
  96.3 9.1 %project.2 = (bf16[1024,768]{1,0:T(8,128)(2,1)}, bf16[1024,2304]{1,0:T(8,128)(2,1)}) custom-call(f32[1024,768]{1,0:T(8,128)} %convert_add_fusion.hidden_ref, f32[2,768]{1,0:T(2,128)} %squeeze.136.gains_ref, f32[6,768]{1,0:T(8,128)} %squeeze.137.offsets_ref, bf16[768,3200]{1,0:T(8,128)(2,1)} %all-gather.3.cloned.1.call-done.weight_ref.out_weight_ref), custom_call_target="tpu_custom_call" | custom-call | flops 226492416 | bytes 898560 | tf_op jit(solution)/shard_map/project/pallas_call | solution.py:231
  107.8 2.8 fusion.2.bias_ref
  110.6 25.2 %attend_forward.2 = (bf16[1024,768]{1,0:T(8,128)(2,1)}, f32[6,2,1024]{2,1,0:T(2,128)}) custom-call(bf16[1024,2304]{1,0:T(8,128)(2,1)} %get-tuple-element.207.query_ref.key_ref.value_ref, bf16[1024,2304]{1,0:T(8,128)(2,1)} %get-tuple-element.207.query_ref.key_ref.value_ref, bf16[1024,2304]{1,0:T(8,128)(2,1)} %get-tuple-element.207.query_ref.key_ref.value_ref, ...), custom_call_target="tpu_custom_call" | custom-call | flops 805306368 | bytes 393216 | tf_op jit(solution)/shard_map/attend_forward/pallas_call | solution.py:68
  135.8 6.0 collective-permute-done.7.refs_1_
  146.3 3.9 collective-permute-done.8.refs_2_
  161.4 24.2 %feed.2 = (f32[1024,768]{1,0:T(8,128)}, bf16[1024,768]{1,0:T(8,128)(2,1)}, bf16[1024,3072]{1,0:T(8,128)(2,1)}, bf16[1024,3072]{1,0:T(8,128)(2,1)}, f32[1024,768]{1,0:T(8,128)}) custom-call(bf16[1024,768]{1,0:T(8,128)(2,1)} %get-tuple-element.220.attended_ref.refs_2_, f32[1024,768]{1,0:T(8,128)} %convert_add_fusion.hidden_ref, f32[2,768]{1,0:T(2,128)} %squeeze.136.gains_ref, ...), custom_call_target="tpu_custom_call" | custom-call | flops 679477248 | bytes 2472192 | tf_op jit(solution)/shard_map/feed/pallas_call | solution.py:231
  186.8 9.0 %collective-permute-done.12.refs_1_ = bf16[2,96,768]{2,1,0:T(8,128)(2,1)S(1)} collective-permute-done((bf16[2,96,768]{2,1,0:T(8,128)(2,1)S(1)}, bf16[2,96,768]{2,1,0:T(8,128)(2,1)S(1)}, u32[]{:S(2)}, u32[]{:S(2)}) %collective-permute-start.12) | collective-permute-done | bytes 294944 | tf_op jit(solution)/shard_map/ppermute | solution.py:587
  197.5 13.0 %collective-permute-done.13.refs_1_ = bf16[4,96,768]{2,1,0:T(8,128)(2,1)S(1)} collective-permute-done((bf16[4,96,768]{2,1,0:T(8,128)(2,1)S(1)}, bf16[4,96,768]{2,1,0:T(8,128)(2,1)S(1)}, u32[]{:S(2)}, u32[]{:S(2)}) %collective-permute-start.13) | collective-permute-done | bytes 589856 | tf_op jit(solution)/shard_map/ppermute | solution.py:590
  210.6 2.7 collective-permute-start.14
  214.7 9.1 %project.3 = (bf16[1024,768]{1,0:T(8,128)(2,1)}, bf16[1024,2304]{1,0:T(8,128)(2,1)}) custom-call(f32[1024,768]{1,0:T(8,128)} %get-tuple-element.236.hidden_ref, f32[2,768]{1,0:T(2,128)} %squeeze.138.gains_ref, f32[6,768]{1,0:T(8,128)} %squeeze.139.offsets_ref, bf16[768,6144]{1,0:T(8,128)(2,1)} %all-gather.5.cloned.1.call-done.weight_ref.out_weight_ref.up_ref), custom_call_target="tpu_custom_call" | custom-call | flops 226492416 | bytes 1181184 | tf_op jit(solution)/shard_map/project/pallas_call | solution.py:231
  223.8 14.0 %collective-permute-done.14.refs_1_ = bf16[4,192,768]{2,1,0:T(8,128)(2,1)S(1)} collective-permute-done((bf16[4,192,768]{2,1,0:T(8,128)(2,1)S(1)}, bf16[4,192,768]{2,1,0:T(8,128)(2,1)S(1)}, u32[]{:S(2)}, u32[]{:S(2)}) %collective-permute-start.14) | collective-permute-done | bytes 1179680 | tf_op jit(solution)/shard_map/ppermute | solution.py:587
  240.5 4.7 all-to-all-start.2
  245.9 25.2 %attend_forward.3 = (bf16[1024,768]{1,0:T(8,128)(2,1)}, f32[6,2,1024]{2,1,0:T(2,128)}) custom-call(bf16[1024,2304]{1,0:T(8,128)(2,1)} %get-tuple-element.242.query_ref.key_ref.value_ref, bf16[1024,2304]{1,0:T(8,128)(2,1)} %get-tuple-element.242.query_ref.key_ref.value_ref, bf16[1024,2304]{1,0:T(8,128)(2,1)} %get-tuple-element.242.query_ref.key_ref.value_ref, ...), custom_call_target="tpu_custom_call" | custom-call | flops 805306368 | bytes 393216 | tf_op jit(solution)/shard_map/attend_forward/pallas_call | solution.py:68
  275.0 23.9 %feed.3 = (f32[1024,768]{1,0:T(8,128)}, bf16[1024,768]{1,0:T(8,128)(2,1)}, bf16[1024,3072]{1,0:T(8,128)(2,1)}, bf16[1024,3072]{1,0:T(8,128)(2,1)}, bf16[1024,768]{1,0:T(8,128)(2,1)}) custom-call(bf16[1024,768]{1,0:T(8,128)(2,1)} %get-tuple-element.246.attended_ref.refs_4_, f32[1024,768]{1,0:T(8,128)} %get-tuple-element.236.hidden_ref, ...), custom_call_target="tpu_custom_call" | custom-call | flops 679477248 | bytes 2951424 | tf_op jit(solution)/shard_map/feed/pallas_call | solution.py:231
  299.0 21.4 %feed_grad.2 = (bf16[1024,768]{1,0:T(8,128)(2,1)}, bf16[1024,3072]{1,0:T(8,128)(2,1)}, f32[1024,768]{1,0:T(8,128)}, bf16[1024,768]{1,0:T(8,128)(2,1)}, bf16[1024...) custom-call(bf16[1024,768]{1,0:T(8,128)(2,1)} %bitcast.32.gradient_ref, ...), custom_call_target="tpu_custom_call" | custom-call | flops 679477248 | bytes 3050112 | tf_op jit(solution)/shard_map/feed_grad/pallas_call | solution.py:231
  320.4 19.6 %term_blocks.5 = bf16[16,48,6912]{2,1,0:T(8,128)(2,1)} custom-call(s32[1]{0:T(128)} %bitcast.21.core_ref, bf16[1024,3072]{1,0:T(8,128)(2,1)} %get-tuple-element.251.refs_0_, bf16[1024,768]{1,0:T(8,128)(2,1)} %get-tuple-element.252.refs_1_, bf16[1024,768]{1,0:T(8,128)(2,1)} %get-tuple-element.253.refs_2_, bf16[1024,3072]{1,0:T(8,128)(2,1)} %get-tuple-element.254.refs_3_, ...), custom_call_target="tpu_custom_call" | custom-call | flops 679477248 | bytes 1843200 | tf_op jit(solution)/shard_map/term_blocks/pallas_call | solution.py:545
  340.0 3.7 all-to-all-start.3
  343.8 37.6 %attend_backward.2.packed_grad_ref.refs_1_ = bf16[1024,2304]{1,0:T(8,128)(2,1)} custom-call(bf16[1024,2304]{1,0:T(8,128)(2,1)} %get-tuple-element.242.query_ref.key_ref.value_ref, bf16[1024,2304]{1,0:T(8,128)(2,1)} %get-tuple-element.242.query_ref.key_ref.value_ref, bf16[1024,2304]{1,0:T(8,128)(2,1)} %get-tuple-element.242.query_ref.key_ref.value_ref, ...), custom_call_target="tpu_custom_call" | custom-call | flops 2013265920 | bytes 786432 | tf_op jit(solution)/shard_map/attend_backward/pallas_call | solution.py:151
  381.4 10.6 %project_grad.2 = (f32[1024,768]{1,0:T(8,128)}, f32[8,768]{1,0:T(8,128)}) custom-call(bf16[1024,2304]{1,0:T(8,128)(2,1)} %attend_backward.2.packed_grad_ref.refs_1_, f32[1024,768]{1,0:T(8,128)} %get-tuple-element.236.hidden_ref, f32[1024,768]{1,0:T(8,128)} %get-tuple-element.261.middle_grad_ref, f32[2,768]{1,0:T(2,128)} %squeeze.138.gains_ref, ...), custom_call_target="tpu_custom_call" | custom-call | flops 226492416 | bytes 1476480 | tf_op jit(solution)/shard_map/project_grad/pallas_call | solution.py:231
  392.0 3.2 convert_element_type.337.refs_1_
  395.3 12.2 %term_blocks.6 = (bf16[8,2,48,1536]{3,2,1,0:T(8,128)(2,1)}, bf16[8,2,48,1536]{3,2,1,0:T(8,128)(2,1)}) custom-call(s32[1]{0:T(128)} %bitcast.21.core_ref, bf16[1024,3072]{1,0:T(8,128)(2,1)} %get-tuple-element.263.refs_0_, bf16[1024,768]{1,0:T(8,128)(2,1)} %convert_element_type.337.refs_1_), custom_call_target="tpu_custom_call" | custom-call | flops 301989888 | bytes 786432 | tf_op jit(solution)/shard_map/term_blocks/pallas_call | solution.py:545
  407.9 8.6 %term_blocks.7 = bf16[16,48,2304]{2,1,0:T(8,128)(2,1)} custom-call(s32[1]{0:T(128)} %bitcast.21.core_ref, bf16[1024,768]{1,0:T(8,128)(2,1)} %get-tuple-element.266.refs_0_, bf16[1024,2304]{1,0:T(8,128)(2,1)} %attend_backward.2.packed_grad_ref.refs_1_), custom_call_target="tpu_custom_call" | custom-call | flops 226492416 | bytes 614400 | tf_op jit(solution)/shard_map/term_blocks/pallas_call | solution.py:545
  416.5 3.0 fusion.5
  421.3 21.3 %feed_grad.3 = (bf16[1024,768]{1,0:T(8,128)(2,1)}, bf16[1024,3072]{1,0:T(8,128)(2,1)}, f32[1024,768]{1,0:T(8,128)}, bf16[1024,768]{1,0:T(8,128)(2,1)}, bf16[1024...) custom-call(f32[1024,768]{1,0:T(8,128)} %get-tuple-element.272.gradient_ref, ...), custom_call_target="tpu_custom_call" | custom-call | flops 679477248 | bytes 2570880 | tf_op jit(solution)/shard_map/feed_grad/pallas_call | solution.py:231
  442.6 15.9 %collective-permute-done.17 = bf16[2,2,2,48,1536]{4,3,2,1,0:T(8,128)(2,1)S(1)} collective-permute-done((bf16[2,2,2,48,1536]{4,3,2,1,0:T(8,128)(2,1)}, bf16[2,2,2,48,1536]{4,3,2,1,0:T(8,128)(2,1)S(1)}, u32[]{:S(2)}, u32[]{:S(2)}) %collective-permute-start.17) | collective-permute-done | bytes 1179680 | tf_op jit(solution)/shard_map/ppermute | solution.py:587
  458.5 2.8 fusion.6
  461.3 12.8 %term_blocks.8 = (bf16[8,2,48,1920]{3,2,1,0:T(8,128)(2,1)}, bf16[8,2,48,1920]{3,2,1,0:T(8,128)(2,1)}) custom-call(s32[1]{0:T(128)} %bitcast.21.core_ref, bf16[1024,768]{1,0:T(8,128)(2,1)} %get-tuple-element.282.refs_0_, bf16[1024,3072]{1,0:T(8,128)(2,1)} %get-tuple-element.283.refs_1_, bf16[1024,768]{1,0:T(8,128)(2,1)} %get-tuple-element.220.attended_ref.refs_2_, ...), custom_call_target="tpu_custom_call" | custom-call | flops 377487360 | bytes 1056768 | tf_op jit(solution)/shard_map/term_blocks/pallas_call | solution.py:545
  474.2 5.7 collective-permute-done.18
  479.9 3.4 fusion.3
  483.8 37.4 %attend_backward.3.refs_1_.packed_grad_ref = bf16[1024,2304]{1,0:T(8,128)(2,1)} custom-call(bf16[1024,2304]{1,0:T(8,128)(2,1)} %get-tuple-element.207.query_ref.key_ref.value_ref, bf16[1024,2304]{1,0:T(8,128)(2,1)} %get-tuple-element.207.query_ref.key_ref.value_ref, bf16[1024,2304]{1,0:T(8,128)(2,1)} %get-tuple-element.207.query_ref.key_ref.value_ref, ...), custom_call_target="tpu_custom_call" | custom-call | flops 2013265920 | bytes 786432 | tf_op jit(solution)/shard_map/attend_backward/pallas_call | solution.py:151
  521.1 9.7 %term_blocks.9 = (bf16[8,2,48,1152]{3,2,1,0:T(8,128)(2,1)}, bf16[8,2,48,1152]{3,2,1,0:T(8,128)(2,1)}) custom-call(s32[1]{0:T(128)} %bitcast.21.core_ref, bf16[1024,768]{1,0:T(8,128)(2,1)} %get-tuple-element.301.refs_0_, bf16[1024,2304]{1,0:T(8,128)(2,1)} %attend_backward.3.refs_1_.packed_grad_ref), custom_call_target="tpu_custom_call" | custom-call | flops 226492416 | bytes 614400 | tf_op jit(solution)/shard_map/term_blocks/pallas_call | solution.py:545
  546.1 10.3 %project_grad.3 = (bf16[1024,768]{1,0:T(8,128)(2,1)}, f32[8,768]{1,0:T(8,128)}) custom-call(bf16[1024,2304]{1,0:T(8,128)(2,1)} %attend_backward.3.refs_1_.packed_grad_ref, f32[1024,768]{1,0:T(8,128)} %convert_add_fusion.hidden_ref, f32[1024,768]{1,0:T(8,128)} %get-tuple-element.309.middle_grad_ref, f32[2,768]{1,0:T(2,128)} %squeeze.136.gains_ref, ...), custom_call_target="tpu_custom_call" | custom-call | flops 226492416 | bytes 1095552 | tf_op jit(solution)/shard_map/project_grad/pallas_call | solution.py:231
  559.2 9.0 %collective-permute-done.22 = bf16[2,48,1536]{2,1,0:T(8,128)(2,1)} collective-permute-done((bf16[2,48,1536]{2,1,0:T(8,128)(2,1)}, bf16[2,48,1536]{2,1,0:T(8,128)(2,1)}, u32[]{:S(2)}, u32[]{:S(2)}) %collective-permute-start.22) | collective-permute-done | bytes 294944 | tf_op jit(solution)/shard_map/ppermute | solution.py:587
  576.9 14.1 %collective-permute-done.25 = bf16[2,2,2,48,1152]{4,3,2,1,0:T(8,128)(2,1)S(1)} collective-permute-done((bf16[2,2,2,48,1152]{4,3,2,1,0:T(8,128)(2,1)S(1)}, bf16[2,2,2,48,1152]{4,3,2,1,0:T(8,128)(2,1)S(1)}, u32[]{:S(2)}, u32[]{:S(2)}) %collective-permute-start.25) | collective-permute-done | bytes 884768 | tf_op jit(solution)/shard_map/ppermute | solution.py:587
  594.0 3.8 all-to-all-start.4
  607.5 11.0 %all-to-all-done.4 = bf16[2,512,768]{2,1,0:T(8,128)(2,1)S(1)} async-done(((bf16[2,512,768]{2,1,0:T(8,128)(2,1)}), bf16[2,512,768]{2,1,0:T(8,128)(2,1)S(1)}, u32[]{:S(2)}, u32[]{:S(2)}) %all-to-all-start.4) | async-done | bytes 1572896 | tf_op jit(solution)/shard_map/all_to_all | solution.py:766
  619.7 8.0 %collective-permute-done.27 = bf16[48,2304]{1,0:T(8,128)(2,1)} collective-permute-done((bf16[48,2304]{1,0:T(8,128)(2,1)}, bf16[48,2304]{1,0:T(8,128)(2,1)}, u32[]{:S(2)}, u32[]{:S(2)}) %collective-permute-start.27) | collective-permute-done | bytes 221216 | tf_op jit(solution)/shard_map/ppermute | solution.py:590
  640.1 5.1 collective-permute-done.32
  656.2 3.7 collective-permute-done.36
  (283 shorter events, 122.0 us)
Async XLA Ops:
  7.2 81.7 %copy-start = (f32[2,768]{1,0:T(2,128)S(1)}, f32[2,768]{1,0:T(2,128)}, u32[]{:S(2)}) copy-start(f32[2,768]{1,0:T(2,128)} %param.13) | copy-start | bytes 18436
  7.2 85.0 %all-gather.3.cloned.1.call-start = ((), (), s32[]{:S(2)}) async-start(), calls=%async_computation.7 | async-start | bytes 5222400 | tf_op jit(solution)/shard_map/all_gather | solution.py:694
  12.6 202.1 %all-gather.5.cloned.1.call-start = ((), (), s32[]{:S(2)}) async-start(), calls=%async_computation.8 | async-start | bytes 10027008 | tf_op jit(solution)/shard_map/all_gather | solution.py:694
  14.2 8.1 %all-to-all-start = ((s32[2,512,2]{1,2,0:T(2,128)}), s32[2,512,2]{1,2,0:T(2,128)S(1)}, u32[]{:S(2)}, u32[]{:S(2)}) async-start(s32[2,512,2]{1,2,0:T(2,128)} %pad_add_fusion), calls=%async_computation | async-start | bytes 16384 | tf_op jit(solution)/shard_map/all_to_all | solution.py:578
  22.3 66.6 %all-to-all-start.1 = ((bf16[2,512,768]{2,1,0:T(8,128)(2,1)}), bf16[2,512,768]{2,1,0:T(8,128)(2,1)}, u32[]{:S(2)}, u32[]{:S(2)}) async-start(bf16[2,512,768]{2,1,0:T(8,128)(2,1)} %param.12), calls=%async_computation.1 | async-start | bytes 3145728 | tf_op jit(solution)/shard_map/all_to_all | solution.py:578
  27.6 19.6 %collective-permute-start = (bf16[1,48,1536]{2,1,0:T(8,128)(2,1)S(1)}, bf16[1,48,1536]{2,1,0:T(8,128)(2,1)S(1)}, u32[]{:S(2)}, u32[]{:S(2)}) collective-permute-start(bf16[1,48,1536]{2,1,0:T(8,128)(2,1)S(1)} %constant_dynamic-slice_fusion.11.refs_0_), channel_id=1, source_target_pairs={{0,16},{2,18},{4,20},{6,22},{8,24},{10,26},{12,28},{14,30},{16,0},... | collective-permute-start | bytes 442376 | tf_op jit(solution)/shard_map/ppermute | solution.py:587
  30.7 19.3 %collective-permute-start.1 = (bf16[1,96,768]{2,1,0:T(8,128)(2,1)S(1)}, bf16[1,96,768]{2,1,0:T(8,128)(2,1)S(1)}, u32[]{:S(2)}, u32[]{:S(2)}) collective-permute-start(bf16[1,96,768]{2,1,0:T(8,128)(2,1)S(1)} %get-tuple-element.190.refs_0_), channel_id=1, source_target_pairs={{0,16},{2,18},{4,20},{6,22},{8,24},{10,26},{12,28},{14,30},{16,0},... | collective-permute-start | bytes 442376 | tf_op jit(solution)/shard_map/ppermute | solution.py:587
  50.8 22.3 %collective-permute-start.2 = (bf16[2,48,1536]{2,1,0:T(8,128)(2,1)S(1)}, bf16[2,48,1536]{2,1,0:T(8,128)(2,1)S(1)}, u32[]{:S(2)}, u32[]{:S(2)}) collective-permute-start(bf16[2,48,1536]{2,1,0:T(8,128)(2,1)S(1)} %bitcast.211), channel_id=1, source_target_pairs={{0,8},{2,10},{4,12},{6,14},{8,0},{10,2},{12,4},{14,6},{16,24},{18,... | collective-permute-start | bytes 884744 | tf_op jit(solution)/shard_map/ppermute | solution.py:587
  50.8 34.6 %collective-permute-start.3 = (bf16[2,96,768]{2,1,0:T(8,128)(2,1)S(1)}, bf16[2,96,768]{2,1,0:T(8,128)(2,1)S(1)}, u32[]{:S(2)}, u32[]{:S(2)}) collective-permute-start(bf16[2,96,768]{2,1,0:T(8,128)(2,1)S(1)} %bitcast.213), channel_id=1, source_target_pairs={{0,8},{2,10},{4,12},{6,14},{8,0},{10,2},{12,4},{14,6},{16,24},{18,... | collective-permute-start | bytes 884744 | tf_op jit(solution)/shard_map/ppermute | solution.py:587
  85.7 19.7 %collective-permute-start.4 = (bf16[4,48,1536]{2,1,0:T(8,128)(2,1)S(1)}, bf16[4,48,1536]{2,1,0:T(8,128)(2,1)S(1)}, u32[]{:S(2)}, u32[]{:S(2)}) collective-permute-start(bf16[4,48,1536]{2,1,0:T(8,128)(2,1)S(1)} %bitcast.207), channel_id=1, source_target_pairs={{0,4},{2,6},{4,0},{6,2},{8,12},{10,14},{12,8},{14,10},{16,20},{18,... | collective-permute-start | bytes 1769480 | tf_op jit(solution)/shard_map/ppermute | solution.py:587
  87.4 18.1 %collective-permute-start.5 = (bf16[4,96,768]{2,1,0:T(8,128)(2,1)S(1)}, bf16[4,96,768]{2,1,0:T(8,128)(2,1)S(1)}, u32[]{:S(2)}, u32[]{:S(2)}) collective-permute-start(bf16[4,96,768]{2,1,0:T(8,128)(2,1)S(1)} %bitcast.205), channel_id=1, source_target_pairs={{0,1},{1,0},{2,3},{3,2},{4,5},{5,4},{6,7},{7,6},{8,9},{9,8},{10,11... | collective-permute-start | bytes 1769480 | tf_op jit(solution)/shard_map/ppermute | solution.py:590
  105.8 30.1 %collective-permute-start.6 = (bf16[8,48,1536]{2,1,0:T(8,128)(2,1)S(1)}, bf16[8,48,1536]{2,1,0:T(8,128)(2,1)}, u32[]{:S(2)}, u32[]{:S(2)}) collective-permute-start(bf16[8,48,1536]{2,1,0:T(8,128)(2,1)S(1)} %bitcast.198), channel_id=1, source_target_pairs={{0,1},{1,0},{2,3},{3,2},{4,5},{5,4},{6,7},{7,6},{8,9},{9,8},{10,11... | collective-permute-start | bytes 3538952 | tf_op jit(solution)/shard_map/ppermute | solution.py:590
  106.4 35.4 %collective-permute-start.7 = (bf16[4,192,768]{2,1,0:T(8,128)(2,1)S(1)}, bf16[4,192,768]{2,1,0:T(8,128)(2,1)S(1)}, u32[]{:S(2)}, u32[]{:S(2)}) collective-permute-start(bf16[4,192,768]{2,1,0:T(8,128)(2,1)S(1)} %bitcast.201), channel_id=1, source_target_pairs={{0,4},{2,6},{4,0},{6,2},{8,12},{10,14},{12,8},{14,10},{16,20},{18,... | collective-permute-start | bytes 3538952 | tf_op jit(solution)/shard_map/ppermute | solution.py:587
  142.1 8.3 %collective-permute-start.10 = (bf16[8,192,768]{2,1,0:T(8,128)(2,1)S(1)}, bf16[8,192,768]{2,1,0:T(8,128)(2,1)}, u32[]{:S(2)}, u32[]{:S(2)}) collective-permute-start(bf16[8,192,768]{2,1,0:T(8,128)(2,1)S(1)} %bitcast.194), channel_id=1, source_target_pairs={{0,2},{2,0},{4,6},{6,4},{8,10},{10,8},{12,14},{14,12},{16,18},{18,... | collective-permute-start | bytes 7077896 | tf_op jit(solution)/shard_map/ppermute | solution.py:587
  142.1 8.0 %collective-permute-start.8 = (bf16[8,48,1536]{2,1,0:T(8,128)(2,1)S(1)}, bf16[8,48,1536]{2,1,0:T(8,128)(2,1)}, u32[]{:S(2)}, u32[]{:S(2)}) collective-permute-start(bf16[8,48,1536]{2,1,0:T(8,128)(2,1)S(1)} %bitcast.199), channel_id=1, source_target_pairs={{0,2},{2,0},{4,6},{6,4},{8,10},{10,8},{12,14},{14,12},{16,18},{18,... | collective-permute-start | bytes 3538952 | tf_op jit(solution)/shard_map/ppermute | solution.py:587
  142.6 7.7 %collective-permute-start.9 = (bf16[8,48,1536]{2,1,0:T(8,128)(2,1)}, bf16[8,48,1536]{2,1,0:T(8,128)(2,1)}, u32[]{:S(2)}, u32[]{:S(2)}) collective-permute-start(bf16[8,48,1536]{2,1,0:T(8,128)(2,1)} %collective-permute-done.6.refs_1_), channel_id=1, source_target_pairs={{0,2},{2,0},{4,6},{6,4},{8,10},{10,8},{12,14},{14,12},{16,18},{18,... | collective-permute-start | bytes 3538952 | tf_op jit(solution)/shard_map/ppermute | solution.py:587
  150.4 35.1 %collective-permute-start.11 = (bf16[1,96,768]{2,1,0:T(8,128)(2,1)}, bf16[1,96,768]{2,1,0:T(8,128)(2,1)}, u32[]{:S(2)}, u32[]{:S(2)}) collective-permute-start(bf16[1,96,768]{2,1,0:T(8,128)(2,1)} %get-tuple-element.225.refs_0_), channel_id=1, source_target_pairs={{0,16},{2,18},{4,20},{6,22},{8,24},{10,26},{12,28},{14,30},{16,0},... | collective-permute-start | bytes 442376 | tf_op jit(solution)/shard_map/ppermute | solution.py:587
  186.7 9.1 %collective-permute-start.12 = (bf16[2,96,768]{2,1,0:T(8,128)(2,1)S(1)}, bf16[2,96,768]{2,1,0:T(8,128)(2,1)S(1)}, u32[]{:S(2)}, u32[]{:S(2)}) collective-permute-start(bf16[2,96,768]{2,1,0:T(8,128)(2,1)S(1)} %bitcast.215), channel_id=1, source_target_pairs={{0,8},{2,10},{4,12},{6,14},{8,0},{10,2},{12,4},{14,6},{16,24},{18,... | collective-permute-start | bytes 884744 | tf_op jit(solution)/shard_map/ppermute | solution.py:587
  195.9 14.6 %collective-permute-start.13 = (bf16[4,96,768]{2,1,0:T(8,128)(2,1)S(1)}, bf16[4,96,768]{2,1,0:T(8,128)(2,1)S(1)}, u32[]{:S(2)}, u32[]{:S(2)}) collective-permute-start(bf16[4,96,768]{2,1,0:T(8,128)(2,1)S(1)} %bitcast.209), channel_id=1, source_target_pairs={{0,1},{1,0},{2,3},{3,2},{4,5},{5,4},{6,7},{7,6},{8,9},{9,8},{10,11... | collective-permute-start | bytes 1769480 | tf_op jit(solution)/shard_map/ppermute | solution.py:590
  210.6 27.3 %collective-permute-start.14 = (bf16[4,192,768]{2,1,0:T(8,128)(2,1)S(1)}, bf16[4,192,768]{2,1,0:T(8,128)(2,1)S(1)}, u32[]{:S(2)}, u32[]{:S(2)}) collective-permute-start(bf16[4,192,768]{2,1,0:T(8,128)(2,1)S(1)} %bitcast.203), channel_id=1, source_target_pairs={{0,4},{2,6},{4,0},{6,2},{8,12},{10,14},{12,8},{14,10},{16,20},{18,... | collective-permute-start | bytes 3538952 | tf_op jit(solution)/shard_map/ppermute | solution.py:587
  240.4 30.7 %collective-permute-start.15 = (bf16[8,192,768]{2,1,0:T(8,128)(2,1)S(1)}, bf16[8,192,768]{2,1,0:T(8,128)(2,1)}, u32[]{:S(2)}, u32[]{:S(2)}) collective-permute-start(bf16[8,192,768]{2,1,0:T(8,128)(2,1)S(1)} %bitcast.196), channel_id=1, source_target_pairs={{0,2},{2,0},{4,6},{6,4},{8,10},{10,8},{12,14},{14,12},{16,18},{18,... | collective-permute-start | bytes 7077896 | tf_op jit(solution)/shard_map/ppermute | solution.py:587
  240.5 58.5 %all-to-all-start.2 = ((bf16[2,512,768]{2,1,0:T(8,128)(2,1)}), bf16[2,512,768]{2,1,0:T(8,128)(2,1)}, u32[]{:S(2)}, u32[]{:S(2)}) async-start(bf16[2,512,768]{2,1,0:T(8,128)(2,1)} %param.16), calls=%async_computation.2 | async-start | bytes 3145728 | tf_op jit(solution)/shard_map/all_to_all | solution.py:578
  245.2 285.7 %reduce-scatter.3.cloned.1.call-start = ((), (), s32[]{:S(2)}) async-start(), calls=%async_computation.9 | async-start | bytes 11280384 | tf_op jit(solution)/shard_map/reduce_scatter | solution.py:593
  340.0 41.4 %all-to-all-start.3 = ((bf16[2,512,768]{2,1,0:T(8,128)(2,1)}), bf16[2,512,768]{2,1,0:T(8,128)(2,1)S(1)}, u32[]{:S(2)}, u32[]{:S(2)}) async-start(bf16[2,512,768]{2,1,0:T(8,128)(2,1)} %bitcast.35), calls=%async_computation.3 | async-start | bytes 3145728 | tf_op jit(solution)/shard_map/all_to_all | solution.py:766
  343.7 215.5 %reduce-scatter.5.cloned.1.call-start = ((), (), s32[]{:S(2)}) async-start(), calls=%async_computation.10 | async-start | bytes 3760128 | tf_op jit(solution)/shard_map/reduce_scatter | solution.py:593
  407.5 9.0 %collective-permute-start.16 = (bf16[8,2,48,1536]{3,2,1,0:T(8,128)(2,1)}, bf16[8,2,48,1536]{3,2,1,0:T(8,128)(2,1)}, u32[]{:S(2)}, u32[]{:S(2)}) collective-permute-start(bf16[8,2,48,1536]{3,2,1,0:T(8,128)(2,1)} %get-tuple-element.268), channel_id=1, source_target_pairs={{0,2},{2,0},{4,6},{6,4},{8,10},{10,8},{12,14},{14,12},{16,18},{18,... | collective-permute-start | bytes 7077896 | tf_op jit(solution)/shard_map/ppermute | solution.py:587
  419.5 39.0 %collective-permute-start.17 = (bf16[2,2,2,48,1536]{4,3,2,1,0:T(8,128)(2,1)}, bf16[2,2,2,48,1536]{4,3,2,1,0:T(8,128)(2,1)S(1)}, u32[]{:S(2)}, u32[]{:S(2)}) collective-permute-start(bf16[2,2,2,48,1536]{4,3,2,1,0:T(8,128)(2,1)} %fusion.5), channel_id=1, source_target_pairs={{0,4},{2,6},{4,0},{6,2},{8,12},{10,14},{12,8},{14,10},{16,20},{18,... | collective-permute-start | bytes 3538952 | tf_op jit(solution)/shard_map/ppermute | solution.py:587
  474.1 5.8 collective-permute-start.18
  483.3 47.5 %collective-permute-start.20 = (bf16[2,2,2,48,1920]{4,3,2,1,0:T(8,128)(2,1)}, bf16[2,2,2,48,1920]{4,3,2,1,0:T(8,128)(2,1)S(1)}, u32[]{:S(2)}, u32[]{:S(2)}) collective-permute-start(bf16[2,2,2,48,1920]{4,3,2,1,0:T(8,128)(2,1)} %fusion.3), channel_id=1, source_target_pairs={{0,4},{2,6},{4,0},{6,2},{8,12},{10,14},{12,8},{14,10},{16,20},{18,... | collective-permute-start | bytes 4423688 | tf_op jit(solution)/shard_map/ppermute | solution.py:587
  483.8 47.0 %collective-permute-start.19 = (bf16[2,2,48,1536]{3,2,1,0:T(8,128)(2,1)}, bf16[2,2,48,1536]{3,2,1,0:T(8,128)(2,1)}, u32[]{:S(2)}, u32[]{:S(2)}) collective-permute-start(bf16[2,2,48,1536]{3,2,1,0:T(8,128)(2,1)} %fusion.6), channel_id=1, source_target_pairs={{0,8},{2,10},{4,12},{6,14},{8,0},{10,2},{12,4},{14,6},{16,24},{18,... | collective-permute-start | bytes 1769480 | tf_op jit(solution)/shard_map/ppermute | solution.py:587
  535.9 8.8 %collective-permute-start.21 = (bf16[8,2,48,1152]{3,2,1,0:T(8,128)(2,1)}, bf16[8,2,48,1152]{3,2,1,0:T(8,128)(2,1)}, u32[]{:S(2)}, u32[]{:S(2)}) collective-permute-start(bf16[8,2,48,1152]{3,2,1,0:T(8,128)(2,1)} %get-tuple-element.304), channel_id=1, source_target_pairs={{0,2},{2,0},{4,6},{6,4},{8,10},{10,8},{12,14},{14,12},{16,18},{18,... | collective-permute-start | bytes 5308424 | tf_op jit(solution)/shard_map/ppermute | solution.py:587
  538.8 30.7 %collective-permute-start.23 = (bf16[2,2,48,1920]{3,2,1,0:T(8,128)(2,1)}, bf16[2,2,48,1920]{3,2,1,0:T(8,128)(2,1)}, u32[]{:S(2)}, u32[]{:S(2)}) collective-permute-start(bf16[2,2,48,1920]{3,2,1,0:T(8,128)(2,1)} %fusion.4), channel_id=1, source_target_pairs={{0,8},{2,10},{4,12},{6,14},{8,0},{10,2},{12,4},{14,6},{16,24},{18,... | collective-permute-start | bytes 2211848 | tf_op jit(solution)/shard_map/ppermute | solution.py:587
  540.9 27.4 %collective-permute-start.24 = (bf16[48,6912]{1,0:T(8,128)(2,1)}, bf16[48,6912]{1,0:T(8,128)(2,1)S(1)}, u32[]{:S(2)}, u32[]{:S(2)}) collective-permute-start(bf16[48,6912]{1,0:T(8,128)(2,1)} %reduce-scatter.3.cloned.1.call-done), channel_id=1, source_target_pairs={{0,1},{1,0},{2,3},{3,2},{4,5},{5,4},{6,7},{7,6},{8,9},{9,8},{10,11... | collective-permute-start | bytes 1990664 | tf_op jit(solution)/shard_map/ppermute | solution.py:590
  543.2 25.0 %collective-permute-start.22 = (bf16[2,48,1536]{2,1,0:T(8,128)(2,1)}, bf16[2,48,1536]{2,1,0:T(8,128)(2,1)}, u32[]{:S(2)}, u32[]{:S(2)}) collective-permute-start(bf16[2,48,1536]{2,1,0:T(8,128)(2,1)} %fusion.15), channel_id=1, source_target_pairs={{0,16},{2,18},{4,20},{6,22},{8,24},{10,26},{12,28},{14,30},{16,0},... | collective-permute-start | bytes 884744 | tf_op jit(solution)/shard_map/ppermute | solution.py:587
  569.6 21.5 %collective-permute-start.25 = (bf16[2,2,2,48,1152]{4,3,2,1,0:T(8,128)(2,1)S(1)}, bf16[2,2,2,48,1152]{4,3,2,1,0:T(8,128)(2,1)S(1)}, u32[]{:S(2)}, u32[]{:S(2)}) collective-permute-start(bf16[2,2,2,48,1152]{4,3,2,1,0:T(8,128)(2,1)S(1)} %fusion.7), channel_id=1, source_target_pairs={{0,4},{2,6},{4,0},{6,2},{8,12},{10,14},{12,8},{14,10},{16,20},{18,... | collective-permute-start | bytes 2654216 | tf_op jit(solution)/shard_map/ppermute | solution.py:587
  594.0 24.5 %all-to-all-start.4 = ((bf16[2,512,768]{2,1,0:T(8,128)(2,1)}), bf16[2,512,768]{2,1,0:T(8,128)(2,1)S(1)}, u32[]{:S(2)}, u32[]{:S(2)}) async-start(bf16[2,512,768]{2,1,0:T(8,128)(2,1)} %bitcast.231), calls=%async_computation.6 | async-start | bytes 3145728 | tf_op jit(solution)/shard_map/all_to_all | solution.py:766
  598.0 29.7 %collective-permute-start.28 = (bf16[2,48,1920]{2,1,0:T(8,128)(2,1)}, bf16[2,48,1920]{2,1,0:T(8,128)(2,1)}, u32[]{:S(2)}, u32[]{:S(2)}) collective-permute-start(bf16[2,48,1920]{2,1,0:T(8,128)(2,1)} %fusion.11), channel_id=1, source_target_pairs={{0,16},{2,18},{4,20},{6,22},{8,24},{10,26},{12,28},{14,30},{16,0},... | collective-permute-start | bytes 1105928 | tf_op jit(solution)/shard_map/ppermute | solution.py:587
  602.5 25.2 %collective-permute-start.29 = (bf16[2,2,48,1152]{3,2,1,0:T(8,128)(2,1)}, bf16[2,2,48,1152]{3,2,1,0:T(8,128)(2,1)S(1)}, u32[]{:S(2)}, u32[]{:S(2)}) collective-permute-start(bf16[2,2,48,1152]{3,2,1,0:T(8,128)(2,1)} %fusion.8), channel_id=1, source_target_pairs={{0,8},{2,10},{4,12},{6,14},{8,0},{10,2},{12,4},{14,6},{16,24},{18,... | collective-permute-start | bytes 1327112 | tf_op jit(solution)/shard_map/ppermute | solution.py:587
  604.5 23.2 %collective-permute-start.26 = (bf16[2,48,1536]{2,1,0:T(8,128)(2,1)}, bf16[2,48,1536]{2,1,0:T(8,128)(2,1)S(1)}, u32[]{:S(2)}, u32[]{:S(2)}) collective-permute-start(bf16[2,48,1536]{2,1,0:T(8,128)(2,1)} %fusion.14), channel_id=1, source_target_pairs={{0,1},{1,0},{2,3},{3,2},{4,5},{5,4},{6,7},{7,6},{8,9},{9,8},{10,11... | collective-permute-start | bytes 884744 | tf_op jit(solution)/shard_map/ppermute | solution.py:590
  606.6 21.1 %collective-permute-start.27 = (bf16[48,2304]{1,0:T(8,128)(2,1)}, bf16[48,2304]{1,0:T(8,128)(2,1)}, u32[]{:S(2)}, u32[]{:S(2)}) collective-permute-start(bf16[48,2304]{1,0:T(8,128)(2,1)} %reduce-scatter.5.cloned.1.call-done), channel_id=1, source_target_pairs={{0,1},{1,0},{2,3},{3,2},{4,5},{5,4},{6,7},{7,6},{8,9},{9,8},{10,11... | collective-permute-start | bytes 663560 | tf_op jit(solution)/shard_map/ppermute | solution.py:590
  618.5 9.2 %collective-permute-start.30 = (f32[8,1152]{1,0:T(8,128)S(1)}, f32[8,1152]{1,0:T(8,128)S(1)}, u32[]{:S(2)}, u32[]{:S(2)}) collective-permute-start(f32[8,1152]{1,0:T(8,128)S(1)} %bitcast.239), channel_id=1, source_target_pairs={{0,2},{2,0},{4,6},{6,4},{8,10},{10,8},{12,14},{14,12},{16,18},{18,... | collective-permute-start | bytes 110600 | tf_op jit(solution)/shard_map/ppermute | solution.py:587
  633.7 11.5 %collective-permute-start.31 = (bf16[2,48,1920]{2,1,0:T(8,128)(2,1)S(1)}, bf16[2,48,1920]{2,1,0:T(8,128)(2,1)S(1)}, u32[]{:S(2)}, u32[]{:S(2)}) collective-permute-start(bf16[2,48,1920]{2,1,0:T(8,128)(2,1)S(1)} %fusion.10), channel_id=1, source_target_pairs={{0,1},{1,0},{2,3},{3,2},{4,5},{5,4},{6,7},{7,6},{8,9},{9,8},{10,11... | collective-permute-start | bytes 1105928 | tf_op jit(solution)/shard_map/ppermute | solution.py:590
  634.1 11.1 %collective-permute-start.32 = (bf16[2,48,1152]{2,1,0:T(8,128)(2,1)S(1)}, bf16[2,48,1152]{2,1,0:T(8,128)(2,1)S(1)}, u32[]{:S(2)}, u32[]{:S(2)}) collective-permute-start(bf16[2,48,1152]{2,1,0:T(8,128)(2,1)S(1)} %fusion.18), channel_id=1, source_target_pairs={{0,16},{2,18},{4,20},{6,22},{8,24},{10,26},{12,28},{14,30},{16,0},... | collective-permute-start | bytes 663560 | tf_op jit(solution)/shard_map/ppermute | solution.py:587
  636.3 3.8 collective-permute-start.33
  648.8 6.4 collective-permute-start.34
  650.3 3.7 collective-permute-start.35
  655.3 4.6 collective-permute-start.36
  659.9 3.7 collective-permute-start.37
  (34 other events, 213.8 us)
Sparse Core Ops, SparseCore 0:
  12.7 72.6 all-gather.2
  88.2 87.3 all-gather.4
  340.2 129.0 reduce-scatter.2
  474.3 83.4 reduce-scatter.4

commit v8 on v7

--- a/solution.py
+++ b/solution.py
@@ -435,8 +435,9 @@
 
 
 def project_grad_kernel(
-    packed_grad_ref, hidden_ref, middle_grad_ref, gains_ref, weight_ref, result_ref, sums_ref
+    packed_grad_ref, hidden_ref, middle_grad_ref, gains_ref, weight_ref, *out_refs
 ):
+    sums_ref = out_refs[-1]
     features = hidden_ref.shape[1]
 
     @pl.when(pl.program_id(0) == 0)
@@ -447,14 +448,15 @@
     normed_grad = contract(packed_grad, weight_ref[...], 1, 1)
     normal, inverse = normal_of(hidden_ref[...])
     result = middle_grad_ref[...] + norm_pull(normal, inverse, gains_ref[0:1], normed_grad)
-    result_ref[...] = result.astype(result_ref.dtype)
+    for result_ref in out_refs[:-1]:
+        result_ref[...] = result.astype(result_ref.dtype)
     sums_ref[0:1] += column_sum(normed_grad * normal)
     sums_ref[1:2] += column_sum(normed_grad)
     sums_ref[2:3] += column_sum(packed_grad[:, :features].astype(single))
     sums_ref[3:4] += column_sum(packed_grad[:, 2 * features :].astype(single))
 
 
-def project_grad(packed_grad, hidden, middle_grad, gains, joined, result_type):
+def project_grad(packed_grad, hidden, middle_grad, gains, joined, result_types):
     length, features = hidden.shape
     shape = jax.ShapeDtypeStruct
     return row_tiled(
@@ -468,8 +470,9 @@
             resident(gains.shape),
             resident((features, 3 * features)),
         ],
-        [tile_of(features), resident((8, features))],
-        [shape((length, features), result_type), shape((8, features), single)],
+        [tile_of(features) for _ in result_types] + [resident((8, features))],
+        [shape((length, features), result_type) for result_type in result_types]
+        + [shape((8, features), single)],
         (packed_grad, hidden, middle_grad, gains, joined),
         6 * length * features * features,
     )
@@ -692,6 +695,10 @@
         parts = [qkv_weight[layer], out_weight[layer], up_weight[layer]]
         joined_parts.append(jnp.concatenate(parts, axis=1))
     joined = [lax.all_gather(part, "wide", axis=0, tiled=True) for part in joined_parts]
+    downs = {
+        layer: lax.all_gather(down_weight[layer], "wide", axis=0, tiled=True)
+        for layer in range(1, layers)
+    }
     small_whole = joined[0][:, -side.shape[1] :][:, :side_width].reshape(groups, -1)
     cut_gains = norm_gains.size
     cut_rows = cut_gains + bias_rows.size
@@ -712,7 +719,7 @@
     bias = jnp.where(allowed, 0.0, masked_bias)
 
     matrices = [None] * layers
-    ups, downs = {}, {}
+    ups = {}
     fetches = [
         begin(gather_columns(up_weight[0]), functools.partial(ups.__setitem__, 0)),
         begin(gather_rows(down_weight[0]), functools.partial(downs.__setitem__, 0)),
@@ -738,14 +745,6 @@
         up = (whole, 4 * features // up_bias.shape[1] // groups) if layer else (ups[0], 0)
         matrices[layer] = (whole, up, downs[layer])
         fetches = []
-        if layer < layers - 1:
-            fetches = [
-                begin(
-                    gather_rows(down_weight[layer + 1]),
-                    functools.partial(downs.__setitem__, layer + 1),
-                )
-            ]
-            attended = launch(attended, fetches)
         middle, second, activated, slope, hidden = feed(
             attended,
             hidden,
@@ -757,8 +756,6 @@
             downs[layer],
             single if layer < layers - 1 else half,
         )
-        for _ in chip_bits:
-            hidden = advance(hidden, *fetches)
         saved.append((before, normed, packed, totals, attended, middle, second, activated, slope))
 
     def split_back(result):
@@ -798,16 +795,17 @@
         (received,) = yield [(other, across(1))]
         shape = (2,) * len(chip_bits) + (2, row_unit, own.shape[-1])
         addends = [part.reshape(shape) for part in (own, received)]
-        axis = len(chip_bits) - 1
-        for bit in chip_bits[::-1]:
-            mine = bit_of(bit)
+        axis = len(chip_bits)
+        for bit in [0] + chip_bits[::-1]:
+            mine, pass_on = (bit_of(bit), across(bit)) if bit else (place, beside_seq)
             sent = total_of([side_of(part, 1 - mine, axis) for part in addends]).astype(half)
-            (received,) = yield [(sent, across(bit))]
+            (received,) = yield [(sent, pass_on)]
             addends = [side_of(part, mine, axis) for part in addends] + [received]
             axis -= 1
         current = total_of(addends).astype(half)
         (received,) = yield [(current, beside_seq)]
-        low, high = current.astype(single) + received.astype(single)
+        low = jnp.where(place == 0, current, received).astype(single)
+        high = jnp.where(place == 0, received, current).astype(single)
         return shares_of(terms, low, high)
 
     def reduce_small(array):
@@ -848,7 +846,9 @@
             upstream = launch(upstream, held[-1:])
         else:
             upstream = advance(upstream, first_group)
-            upper, upstream = lax.optimization_barrier((upper, upstream))
+            upper, attention_grad, upstream = lax.optimization_barrier(
+                (upper, attention_grad, upstream)
+            )
             named = [(2, (second, upper)), (1, (attended, attention_grad))]
             second_group = begin_group(steps, layer, named)
             upstream = launch(upstream, [second_group])
@@ -862,12 +862,13 @@
             packed_grad = advance(packed_grad, first_group, second_group, *held[:1])
             last_group = begin_group(steps, layer, named)
             packed_grad = launch(packed_grad, [last_group])
+            packed_grad = advance(packed_grad, first_group)
             packed_grad = advance(packed_grad, last_group)
-        gradient, more_sums = project_grad(
-            packed_grad, hidden, middle_grad, gains, whole, single if layer else half
+        gradient, *rounded, more_sums = project_grad(
+            packed_grad, hidden, middle_grad, gains, whole, (single, half) if layer else (half,)
         )
         if layer == 1:
-            below = (saved[0][7], gradient.astype(half))
+            below = (saved[0][7], rounded[0])
             first_group = begin_group(reduce_group, 0, [(3, below)])
             gradient = launch(gradient, [first_group])
         if layer:
@@ -876,8 +877,8 @@
         if layer == 1:
             gradient = advance(gradient, first_group)
         if not layer:
+            gradient = advance(gradient, last_group)
             gradient = advance(gradient, first_group, second_group, *held)
-            gradient = advance(gradient, last_group)
         small_grads[layer] = (
             jnp.stack([more_sums[0], sums[1]]),
             jnp.stack([more_sums[1], more_sums[2], more_sums[3], sums[3], sums[2], sums[0]]),
@@ -894,10 +895,12 @@
         axis=1,
     )
     small_result = []
-    begin(reduce_small(owned), small_result.append)
+    rest = begin(reduce_small(owned), small_result.append)
+    gradient = launch(gradient, [rest])
     input_grad = split_back(gradient)
     while running:
-        input_grad = advance(input_grad)
+        input_grad = advance(input_grad, last_group)
+        input_grad = advance(input_grad, *[entry for entry in running if entry is not last_group])
     input_grad = input_grad.astype(single)
     owned = small_result[0]
     stacked = [

time: 686 us -> 632 us (0.921)
  waiting for transfers between devices: 179 us -> 132 us
  Pallas kernels: 328 us -> 335 us
    ppermute x29 -> x25, waiting for transfers between devices: 141 us -> 88.5 us  [across(): return lambda part: lax.ppermute(part, 'wide', pairs)]
    pallas_call x8, Pallas kernels: 130 us -> 141 us  [row_tiled(): pl.pallas_call(kernel, grid=(length // ROW_TILE,), in_specs=in_specs, out...]
    ppermute x29 -> x25, starting transfers between devices: 27.3 us -> 21.3 us  [across(): return lambda part: lax.ppermute(part, 'wide', pairs)]
    convert_element_type x9 -> x12, other arithmetic: 21.3 us -> 27.1 us  [reduce_group(): total_of([side_of(part, 1 - mine, axis) for part in addends]).astype(half)]
    ppermute x9 -> x11, waiting for transfers between devices: 23.4 us -> 26.2 us  [beside_seq(): return lax.ppermute(part, 'seq', swap)]
  transfers between devices with their start and end apart: 47 -> 46, of which waited for: 23 -> 20; matrix products, arithmetic and copies ran while one was open for 9% -> 10% of each run, Pallas kernels for 42% -> 45%
where the time goes in v8:
time: 632 us; the launch traced here: 626 us
  Pallas kernels  335 us (53%)
  waiting for transfers between devices  132 us (21%)
  other arithmetic  56.3 us (9%)
  starting transfers between devices  54.1 us (9%)
  local copies, waits for them, and re-layouts  34.5 us (5%)
  between operations  14.9 us (2%)
    pallas_call x8, Pallas kernels, row_tiled(): pl.pallas_call(kernel, grid=(length // ROW_TILE,), in_specs=in_specs, out...  141 us
    ppermute x25, waiting for transfers between devices, across(): return lambda part: lax.ppermute(part, 'wide', pairs)  88.5 us
    pallas_call x2, Pallas kernels, attend_backward(): pl.pallas_call(functools.partial(attend_grad_kernel, rows=BACKWARD_ROWS),...  74.4 us
    pallas_call x5, Pallas kernels, term_blocks(): pl.pallas_call(kernel, in_specs=[pl.BlockSpec(memory_space=pltpu.SMEM)] +...  63 us
    pallas_call x2, Pallas kernels, attend_forward(): pl.pallas_call(functools.partial(attend_kernel, rows=FORWARD_ROWS), grid=...  50.4 us
    convert_element_type x12, other arithmetic, reduce_group(): total_of([side_of(part, 1 - mine, axis) for part in addends]).astype(half)  27.1 us
    ppermute x11, waiting for transfers between devices, beside_seq(): return lax.ppermute(part, 'seq', swap)  26.2 us
    ppermute x25, starting transfers between devices, across(): return lambda part: lax.ppermute(part, 'wide', pairs)  21.3 us
  transfers between devices with their start and end apart: 46, of which 20 were waited for; matrix products, arithmetic and copies ran while one was open for 10% of the time, Pallas kernels for 45%

profile of v8, /device:TPU:0, one launch (start us, length us, event | category | flops | bytes accessed | tf_op | source)
XLA Modules:
  0.0 626.4 jit_solution(11195935647991139898)
XLA Ops:
  15.1 4.2 all-to-all-start
  19.3 3.8 all-to-all-done
  23.1 4.6 all-to-all-start.1
  27.8 3.1 collective-permute-start
  31.0 16.2 %collective-permute-done.refs_1_ = bf16[1,48,1536]{2,1,0:T(8,128)(2,1)S(1)} collective-permute-done((bf16[1,48,1536]{2,1,0:T(8,128)(2,1)S(1)}, bf16[1,48,1536]{2,1,0:T(8,128)(2,1)S(1)}, u32[]{:S(2)}, u32[]{:S(2)}) %collective-permute-start) | collective-permute-done | bytes 147488 | tf_op jit(solution)/shard_map/ppermute | solution.py:590
  47.2 2.9 collective-permute-done.1.refs_1_
  53.0 20.3 %collective-permute-done.2.refs_1_ = bf16[2,48,1536]{2,1,0:T(8,128)(2,1)S(1)} collective-permute-done((bf16[2,48,1536]{2,1,0:T(8,128)(2,1)S(1)}, bf16[2,48,1536]{2,1,0:T(8,128)(2,1)S(1)}, u32[]{:S(2)}, u32[]{:S(2)}) %collective-permute-start.2) | collective-permute-done | bytes 294944 | tf_op jit(solution)/shard_map/ppermute | solution.py:590
  73.2 12.4 %collective-permute-done.3.refs_1_ = bf16[2,96,768]{2,1,0:T(8,128)(2,1)S(1)} collective-permute-done((bf16[2,96,768]{2,1,0:T(8,128)(2,1)S(1)}, bf16[2,96,768]{2,1,0:T(8,128)(2,1)S(1)}, u32[]{:S(2)}, u32[]{:S(2)}) %collective-permute-start.3) | collective-permute-done | bytes 294944 | tf_op jit(solution)/shard_map/ppermute | solution.py:590
  89.0 3.3 convert_add_fusion.hidden_ref
  96.3 9.2 %project.2 = (bf16[1024,768]{1,0:T(8,128)(2,1)}, bf16[1024,2304]{1,0:T(8,128)(2,1)}) custom-call(f32[1024,768]{1,0:T(8,128)} %convert_add_fusion.hidden_ref, f32[2,768]{1,0:T(2,128)} %squeeze.171.gains_ref, f32[6,768]{1,0:T(8,128)} %squeeze.172.offsets_ref, bf16[768,3200]{1,0:T(8,128)(2,1)} %all-gather.5.cloned.1.call-done.weight_ref.out_weight_ref), custom_call_target="tpu_custom_call" | custom-call | flops 226492416 | bytes 898560 | tf_op jit(solution)/shard_map/project/pallas_call | solution.py:231
  107.9 2.8 fusion.2.bias_ref
  110.6 25.2 %attend_forward.2 = (bf16[1024,768]{1,0:T(8,128)(2,1)}, f32[6,2,1024]{2,1,0:T(2,128)}) custom-call(bf16[1024,2304]{1,0:T(8,128)(2,1)} %get-tuple-element.204.query_ref.key_ref.value_ref, bf16[1024,2304]{1,0:T(8,128)(2,1)} %get-tuple-element.204.query_ref.key_ref.value_ref, bf16[1024,2304]{1,0:T(8,128)(2,1)} %get-tuple-element.204.query_ref.key_ref.value_ref, ...), custom_call_target="tpu_custom_call" | custom-call | flops 805306368 | bytes 393216 | tf_op jit(solution)/shard_map/attend_forward/pallas_call | solution.py:68
  135.9 6.3 %collective-permute-done.7.refs_1_ = bf16[4,192,768]{2,1,0:T(8,128)(2,1)S(1)} collective-permute-done((bf16[4,192,768]{2,1,0:T(8,128)(2,1)S(1)}, bf16[4,192,768]{2,1,0:T(8,128)(2,1)S(1)}, u32[]{:S(2)}, u32[]{:S(2)}) %collective-permute-start.7) | collective-permute-done | bytes 1179680 | tf_op jit(solution)/shard_map/ppermute | solution.py:590
  157.1 2.7 place_pieces.16
  159.8 2.2 copy-done.3
  162.0 24.2 %feed.2 = (f32[1024,768]{1,0:T(8,128)}, bf16[1024,768]{1,0:T(8,128)(2,1)}, bf16[1024,3072]{1,0:T(8,128)(2,1)}, bf16[1024,3072]{1,0:T(8,128)(2,1)}, f32[1024,768]{1,0:T(8,128)}) custom-call(bf16[1024,768]{1,0:T(8,128)(2,1)} %get-tuple-element.216.attended_ref.refs_2_, f32[1024,768]{1,0:T(8,128)} %convert_add_fusion.hidden_ref, f32[2,768]{1,0:T(2,128)} %squeeze.171.gains_ref, ...), custom_call_target="tpu_custom_call" | custom-call | flops 679477248 | bytes 2472192 | tf_op jit(solution)/shard_map/feed/pallas_call | solution.py:231
  186.3 9.2 %project.3 = (bf16[1024,768]{1,0:T(8,128)(2,1)}, bf16[1024,2304]{1,0:T(8,128)(2,1)}) custom-call(f32[1024,768]{1,0:T(8,128)} %get-tuple-element.220.hidden_ref, f32[2,768]{1,0:T(2,128)} %squeeze.173.gains_ref, f32[6,768]{1,0:T(8,128)} %squeeze.174.offsets_ref, bf16[768,6144]{1,0:T(8,128)(2,1)} %all-gather.7.cloned.1.call-done.weight_ref.out_weight_ref.up_ref), custom_call_target="tpu_custom_call" | custom-call | flops 226492416 | bytes 1181184 | tf_op jit(solution)/shard_map/project/pallas_call | solution.py:231
  195.5 3.8 all-to-all-start.2
  200.0 25.2 %attend_forward.3 = (bf16[1024,768]{1,0:T(8,128)(2,1)}, f32[6,2,1024]{2,1,0:T(2,128)}) custom-call(bf16[1024,2304]{1,0:T(8,128)(2,1)} %get-tuple-element.222.query_ref.key_ref.value_ref, bf16[1024,2304]{1,0:T(8,128)(2,1)} %get-tuple-element.222.query_ref.key_ref.value_ref, bf16[1024,2304]{1,0:T(8,128)(2,1)} %get-tuple-element.222.query_ref.key_ref.value_ref, ...), custom_call_target="tpu_custom_call" | custom-call | flops 805306368 | bytes 393216 | tf_op jit(solution)/shard_map/attend_forward/pallas_call | solution.py:68
  225.2 4.4 all-gather.9.cloned.1.call-done
  229.6 23.9 %feed.3 = (f32[1024,768]{1,0:T(8,128)}, bf16[1024,768]{1,0:T(8,128)(2,1)}, bf16[1024,3072]{1,0:T(8,128)(2,1)}, bf16[1024,3072]{1,0:T(8,128)(2,1)}, bf16[1024,768]{1,0:T(8,128)(2,1)}) custom-call(bf16[1024,768]{1,0:T(8,128)(2,1)} %get-tuple-element.224.attended_ref.refs_4_, f32[1024,768]{1,0:T(8,128)} %get-tuple-element.220.hidden_ref, ...), custom_call_target="tpu_custom_call" | custom-call | flops 679477248 | bytes 2951424 | tf_op jit(solution)/shard_map/feed/pallas_call | solution.py:231
  254.7 31.8 %feed_grad.2 = (bf16[1024,768]{1,0:T(8,128)(2,1)}, bf16[1024,3072]{1,0:T(8,128)(2,1)}, f32[1024,768]{1,0:T(8,128)}, bf16[1024,768]{1,0:T(8,128)(2,1)}, bf16[1024...) custom-call(bf16[1024,768]{1,0:T(8,128)(2,1)} %bitcast.239, ...), custom_call_target="tpu_custom_call" | custom-call | flops 679477248 | bytes 3050112 | tf_op jit(solution)/shard_map/feed_grad/pallas_call | solution.py:231
  286.5 19.6 %term_blocks.5 = bf16[16,48,6912]{2,1,0:T(8,128)(2,1)} custom-call(s32[1]{0:T(128)} %bitcast.20.core_ref, bf16[1024,3072]{1,0:T(8,128)(2,1)} %get-tuple-element.228.refs_0_, bf16[1024,768]{1,0:T(8,128)(2,1)} %get-tuple-element.229.refs_1_, bf16[1024,768]{1,0:T(8,128)(2,1)} %get-tuple-element.230.refs_2_, bf16[1024,3072]{1,0:T(8,128)(2,1)} %get-tuple-element.231.refs_3_, ...), custom_call_target="tpu_custom_call" | custom-call | flops 679477248 | bytes 1843200 | tf_op jit(solution)/shard_map/term_blocks/pallas_call | solution.py:548
  306.2 3.7 all-to-all-start.3
  309.9 37.3 %attend_backward.2.packed_grad_ref.refs_1_ = bf16[1024,2304]{1,0:T(8,128)(2,1)} custom-call(bf16[1024,2304]{1,0:T(8,128)(2,1)} %get-tuple-element.222.query_ref.key_ref.value_ref, bf16[1024,2304]{1,0:T(8,128)(2,1)} %get-tuple-element.222.query_ref.key_ref.value_ref, bf16[1024,2304]{1,0:T(8,128)(2,1)} %get-tuple-element.222.query_ref.key_ref.value_ref, ...), custom_call_target="tpu_custom_call" | custom-call | flops 2013265920 | bytes 786432 | tf_op jit(solution)/shard_map/attend_backward/pallas_call | solution.py:151
  347.2 11.1 %project_grad.2 = (f32[1024,768]{1,0:T(8,128)}, bf16[1024,768]{1,0:T(8,128)(2,1)}, f32[8,768]{1,0:T(8,128)}) custom-call(bf16[1024,2304]{1,0:T(8,128)(2,1)} %attend_backward.2.packed_grad_ref.refs_1_, f32[1024,768]{1,0:T(8,128)} %get-tuple-element.220.hidden_ref, f32[1024,768]{1,0:T(8,128)} %get-tuple-element.238.middle_grad_ref, ...), custom_call_target="tpu_custom_call" | custom-call | flops 226492416 | bytes 1574784 | tf_op jit(solution)/shard_map/project_grad/pallas_call | solution.py:231
  358.3 12.2 %term_blocks.6 = (bf16[8,2,48,1536]{3,2,1,0:T(8,128)(2,1)}, bf16[8,2,48,1536]{3,2,1,0:T(8,128)(2,1)}) custom-call(s32[1]{0:T(128)} %bitcast.20.core_ref, bf16[1024,3072]{1,0:T(8,128)(2,1)} %get-tuple-element.240.refs_0_, bf16[1024,768]{1,0:T(8,128)(2,1)} %get-tuple-element.241.refs_1_), custom_call_target="tpu_custom_call" | custom-call | flops 301989888 | bytes 786432 | tf_op jit(solution)/shard_map/term_blocks/pallas_call | solution.py:548
  370.9 8.5 %term_blocks.7 = bf16[16,48,2304]{2,1,0:T(8,128)(2,1)} custom-call(s32[1]{0:T(128)} %bitcast.20.core_ref, bf16[1024,768]{1,0:T(8,128)(2,1)} %get-tuple-element.244.refs_0_, bf16[1024,2304]{1,0:T(8,128)(2,1)} %attend_backward.2.packed_grad_ref.refs_1_), custom_call_target="tpu_custom_call" | custom-call | flops 226492416 | bytes 614400 | tf_op jit(solution)/shard_map/term_blocks/pallas_call | solution.py:548
  379.5 3.0 fusion.5
  384.1 21.2 %feed_grad.3 = (bf16[1024,768]{1,0:T(8,128)(2,1)}, bf16[1024,3072]{1,0:T(8,128)(2,1)}, f32[1024,768]{1,0:T(8,128)}, bf16[1024,768]{1,0:T(8,128)(2,1)}, bf16[1024...) custom-call(f32[1024,768]{1,0:T(8,128)} %get-tuple-element.250.gradient_ref, ...), custom_call_target="tpu_custom_call" | custom-call | flops 679477248 | bytes 2570880 | tf_op jit(solution)/shard_map/feed_grad/pallas_call | solution.py:231
  405.3 5.6 collective-permute-done.12
  410.9 2.8 fusion.6
  413.7 12.9 %term_blocks.8 = (bf16[8,2,48,1920]{3,2,1,0:T(8,128)(2,1)}, bf16[8,2,48,1920]{3,2,1,0:T(8,128)(2,1)}) custom-call(s32[1]{0:T(128)} %bitcast.20.core_ref, bf16[1024,768]{1,0:T(8,128)(2,1)} %get-tuple-element.261.refs_0_, bf16[1024,3072]{1,0:T(8,128)(2,1)} %get-tuple-element.262.refs_1_, bf16[1024,768]{1,0:T(8,128)(2,1)} %get-tuple-element.216.attended_ref.refs_2_, ...), custom_call_target="tpu_custom_call" | custom-call | flops 377487360 | bytes 1056768 | tf_op jit(solution)/shard_map/term_blocks/pallas_call | solution.py:548
  426.7 5.6 collective-permute-done.13
  432.2 3.9 fusion.3
  438.7 37.2 %attend_backward.3.refs_1_.packed_grad_ref = bf16[1024,2304]{1,0:T(8,128)(2,1)} custom-call(bf16[1024,2304]{1,0:T(8,128)(2,1)} %get-tuple-element.204.query_ref.key_ref.value_ref, bf16[1024,2304]{1,0:T(8,128)(2,1)} %get-tuple-element.204.query_ref.key_ref.value_ref, bf16[1024,2304]{1,0:T(8,128)(2,1)} %get-tuple-element.204.query_ref.key_ref.value_ref, ...), custom_call_target="tpu_custom_call" | custom-call | flops 2013265920 | bytes 786432 | tf_op jit(solution)/shard_map/attend_backward/pallas_call | solution.py:151
  475.8 9.8 %term_blocks.9 = (bf16[8,2,48,1152]{3,2,1,0:T(8,128)(2,1)}, bf16[8,2,48,1152]{3,2,1,0:T(8,128)(2,1)}) custom-call(s32[1]{0:T(128)} %bitcast.20.core_ref, bf16[1024,768]{1,0:T(8,128)(2,1)} %get-tuple-element.280.refs_0_, bf16[1024,2304]{1,0:T(8,128)(2,1)} %attend_backward.3.refs_1_.packed_grad_ref), custom_call_target="tpu_custom_call" | custom-call | flops 226492416 | bytes 614400 | tf_op jit(solution)/shard_map/term_blocks/pallas_call | solution.py:548
  485.7 2.6 fusion.11
  488.3 2.5 fusion.4
  495.8 11.8 %collective-permute-done.16 = bf16[2,48,1536]{2,1,0:T(8,128)(2,1)S(1)} collective-permute-done((bf16[2,48,1536]{2,1,0:T(8,128)(2,1)}, bf16[2,48,1536]{2,1,0:T(8,128)(2,1)S(1)}, u32[]{:S(2)}, u32[]{:S(2)}) %collective-permute-start.16) | collective-permute-done | bytes 294944 | tf_op jit(solution)/shard_map/ppermute | solution.py:590
  515.6 10.0 %project_grad.3 = (bf16[1024,768]{1,0:T(8,128)(2,1)}, f32[8,768]{1,0:T(8,128)}) custom-call(bf16[1024,2304]{1,0:T(8,128)(2,1)} %attend_backward.3.refs_1_.packed_grad_ref, f32[1024,768]{1,0:T(8,128)} %convert_add_fusion.hidden_ref, f32[1024,768]{1,0:T(8,128)} %get-tuple-element.292.middle_grad_ref, f32[2,768]{1,0:T(2,128)} %squeeze.171.gains_ref, ...), custom_call_target="tpu_custom_call" | custom-call | flops 226492416 | bytes 1095552 | tf_op jit(solution)/shard_map/project_grad/pallas_call | solution.py:231
  531.3 2.4 collective-permute-done.18
  535.8 11.2 %collective-permute-done.21 = bf16[48,6912]{1,0:T(8,128)(2,1)} collective-permute-done((bf16[48,6912]{1,0:T(8,128)(2,1)S(1)}, bf16[48,6912]{1,0:T(8,128)(2,1)}, u32[]{:S(2)}, u32[]{:S(2)}) %collective-permute-start.21) | collective-permute-done | bytes 663584 | tf_op jit(solution)/shard_map/ppermute | solution.py:593
  551.2 3.7 all-to-all-start.4
  560.8 5.7 collective-permute-done.22
  566.6 9.0 %all-to-all-done.4 = bf16[2,512,768]{2,1,0:T(8,128)(2,1)S(1)} async-done(((bf16[2,512,768]{2,1,0:T(8,128)(2,1)}), bf16[2,512,768]{2,1,0:T(8,128)(2,1)S(1)}, u32[]{:S(2)}, u32[]{:S(2)}) %all-to-all-start.4) | async-done | bytes 1572896 | tf_op jit(solution)/shard_map/all_to_all | solution.py:763
  577.6 4.1 collective-permute-done.23
  600.7 4.4 collective-permute-done.30
  (258 shorter events, 108.1 us)
Async XLA Ops:
  7.2 81.7 %copy-start = (f32[2,768]{1,0:T(2,128)S(1)}, f32[2,768]{1,0:T(2,128)}, u32[]{:S(2)}) copy-start(f32[2,768]{1,0:T(2,128)} %param.13) | copy-start | bytes 18436
  7.2 85.0 %all-gather.5.cloned.1.call-start = ((), (), s32[]{:S(2)}) async-start(), calls=%async_computation.7 | async-start | bytes 5222400 | tf_op jit(solution)/shard_map/all_gather | solution.py:697
  12.6 173.7 %all-gather.7.cloned.1.call-start = ((), (), s32[]{:S(2)}) async-start(), calls=%async_computation.8 | async-start | bytes 10027008 | tf_op jit(solution)/shard_map/all_gather | solution.py:697
  13.6 216.0 %all-gather.9.cloned.1.call-start = ((), (), s32[]{:S(2)}) async-start(), calls=%async_computation.11 | async-start | bytes 5013504 | tf_op jit(solution)/shard_map/all_gather | solution.py:699
  15.1 8.1 %all-to-all-start = ((s32[2,512,2]{1,2,0:T(2,128)}), s32[2,512,2]{1,2,0:T(2,128)S(1)}, u32[]{:S(2)}, u32[]{:S(2)}) async-start(s32[2,512,2]{1,2,0:T(2,128)} %pad_add_fusion), calls=%async_computation | async-start | bytes 16384 | tf_op jit(solution)/shard_map/all_to_all | solution.py:581
  23.1 65.8 %all-to-all-start.1 = ((bf16[2,512,768]{2,1,0:T(8,128)(2,1)}), bf16[2,512,768]{2,1,0:T(8,128)(2,1)}, u32[]{:S(2)}, u32[]{:S(2)}) async-start(bf16[2,512,768]{2,1,0:T(8,128)(2,1)} %param.12), calls=%async_computation.1 | async-start | bytes 3145728 | tf_op jit(solution)/shard_map/all_to_all | solution.py:581
  27.8 19.4 %collective-permute-start = (bf16[1,48,1536]{2,1,0:T(8,128)(2,1)S(1)}, bf16[1,48,1536]{2,1,0:T(8,128)(2,1)S(1)}, u32[]{:S(2)}, u32[]{:S(2)}) collective-permute-start(bf16[1,48,1536]{2,1,0:T(8,128)(2,1)S(1)} %constant_dynamic-slice_fusion.10.refs_0_), channel_id=1, source_target_pairs={{0,16},{2,18},{4,20},{6,22},{8,24},{10,26},{12,28},{14,30},{16,0},... | collective-permute-start | bytes 442376 | tf_op jit(solution)/shard_map/ppermute | solution.py:590
  30.9 19.2 %collective-permute-start.1 = (bf16[1,96,768]{2,1,0:T(8,128)(2,1)S(1)}, bf16[1,96,768]{2,1,0:T(8,128)(2,1)S(1)}, u32[]{:S(2)}, u32[]{:S(2)}) collective-permute-start(bf16[1,96,768]{2,1,0:T(8,128)(2,1)S(1)} %constant_dynamic-slice_fusion.9.refs_0_), channel_id=1, source_target_pairs={{0,16},{2,18},{4,20},{6,22},{8,24},{10,26},{12,28},{14,30},{16,0},... | collective-permute-start | bytes 442376 | tf_op jit(solution)/shard_map/ppermute | solution.py:590
  50.9 22.4 %collective-permute-start.2 = (bf16[2,48,1536]{2,1,0:T(8,128)(2,1)S(1)}, bf16[2,48,1536]{2,1,0:T(8,128)(2,1)S(1)}, u32[]{:S(2)}, u32[]{:S(2)}) collective-permute-start(bf16[2,48,1536]{2,1,0:T(8,128)(2,1)S(1)} %bitcast.231), channel_id=1, source_target_pairs={{0,8},{2,10},{4,12},{6,14},{8,0},{10,2},{12,4},{14,6},{16,24},{18,... | collective-permute-start | bytes 884744 | tf_op jit(solution)/shard_map/ppermute | solution.py:590
  50.9 34.7 %collective-permute-start.3 = (bf16[2,96,768]{2,1,0:T(8,128)(2,1)S(1)}, bf16[2,96,768]{2,1,0:T(8,128)(2,1)S(1)}, u32[]{:S(2)}, u32[]{:S(2)}) collective-permute-start(bf16[2,96,768]{2,1,0:T(8,128)(2,1)S(1)} %bitcast.233), channel_id=1, source_target_pairs={{0,8},{2,10},{4,12},{6,14},{8,0},{10,2},{12,4},{14,6},{16,24},{18,... | collective-permute-start | bytes 884744 | tf_op jit(solution)/shard_map/ppermute | solution.py:590
  85.9 19.6 %collective-permute-start.4 = (bf16[4,48,1536]{2,1,0:T(8,128)(2,1)S(1)}, bf16[4,48,1536]{2,1,0:T(8,128)(2,1)S(1)}, u32[]{:S(2)}, u32[]{:S(2)}) collective-permute-start(bf16[4,48,1536]{2,1,0:T(8,128)(2,1)S(1)} %bitcast.229), channel_id=1, source_target_pairs={{0,4},{2,6},{4,0},{6,2},{8,12},{10,14},{12,8},{14,10},{16,20},{18,... | collective-permute-start | bytes 1769480 | tf_op jit(solution)/shard_map/ppermute | solution.py:590
  87.5 18.0 %collective-permute-start.5 = (bf16[4,96,768]{2,1,0:T(8,128)(2,1)S(1)}, bf16[4,96,768]{2,1,0:T(8,128)(2,1)S(1)}, u32[]{:S(2)}, u32[]{:S(2)}) collective-permute-start(bf16[4,96,768]{2,1,0:T(8,128)(2,1)S(1)} %bitcast.227), channel_id=1, source_target_pairs={{0,1},{1,0},{2,3},{3,2},{4,5},{5,4},{6,7},{7,6},{8,9},{9,8},{10,11... | collective-permute-start | bytes 1769480 | tf_op jit(solution)/shard_map/ppermute | solution.py:593
  105.8 30.1 %collective-permute-start.6 = (bf16[8,48,1536]{2,1,0:T(8,128)(2,1)S(1)}, bf16[8,48,1536]{2,1,0:T(8,128)(2,1)}, u32[]{:S(2)}, u32[]{:S(2)}) collective-permute-start(bf16[8,48,1536]{2,1,0:T(8,128)(2,1)S(1)} %bitcast.222), channel_id=1, source_target_pairs={{0,1},{1,0},{2,3},{3,2},{4,5},{5,4},{6,7},{7,6},{8,9},{9,8},{10,11... | collective-permute-start | bytes 3538952 | tf_op jit(solution)/shard_map/ppermute | solution.py:593
  106.6 35.6 %collective-permute-start.7 = (bf16[4,192,768]{2,1,0:T(8,128)(2,1)S(1)}, bf16[4,192,768]{2,1,0:T(8,128)(2,1)S(1)}, u32[]{:S(2)}, u32[]{:S(2)}) collective-permute-start(bf16[4,192,768]{2,1,0:T(8,128)(2,1)S(1)} %bitcast.225), channel_id=1, source_target_pairs={{0,4},{2,6},{4,0},{6,2},{8,12},{10,14},{12,8},{14,10},{16,20},{18,... | collective-permute-start | bytes 3538952 | tf_op jit(solution)/shard_map/ppermute | solution.py:590
  142.4 10.6 %collective-permute-start.10 = (bf16[8,192,768]{2,1,0:T(8,128)(2,1)S(1)}, bf16[8,192,768]{2,1,0:T(8,128)(2,1)}, u32[]{:S(2)}, u32[]{:S(2)}) collective-permute-start(bf16[8,192,768]{2,1,0:T(8,128)(2,1)S(1)} %bitcast.220), channel_id=1, source_target_pairs={{0,2},{2,0},{4,6},{6,4},{8,10},{10,8},{12,14},{14,12},{16,18},{18,... | collective-permute-start | bytes 7077896 | tf_op jit(solution)/shard_map/ppermute | solution.py:590
  142.5 10.5 %collective-permute-start.8 = (bf16[8,48,1536]{2,1,0:T(8,128)(2,1)S(1)}, bf16[8,48,1536]{2,1,0:T(8,128)(2,1)}, u32[]{:S(2)}, u32[]{:S(2)}) collective-permute-start(bf16[8,48,1536]{2,1,0:T(8,128)(2,1)S(1)} %bitcast.223), channel_id=1, source_target_pairs={{0,2},{2,0},{4,6},{6,4},{8,10},{10,8},{12,14},{14,12},{16,18},{18,... | collective-permute-start | bytes 3538952 | tf_op jit(solution)/shard_map/ppermute | solution.py:590
  143.0 10.0 %collective-permute-start.9 = (bf16[8,48,1536]{2,1,0:T(8,128)(2,1)}, bf16[8,48,1536]{2,1,0:T(8,128)(2,1)}, u32[]{:S(2)}, u32[]{:S(2)}) collective-permute-start(bf16[8,48,1536]{2,1,0:T(8,128)(2,1)} %collective-permute-done.6.refs_1_), channel_id=1, source_target_pairs={{0,2},{2,0},{4,6},{6,4},{8,10},{10,8},{12,14},{14,12},{16,18},{18,... | collective-permute-start | bytes 3538952 | tf_op jit(solution)/shard_map/ppermute | solution.py:590
  195.5 58.1 %all-to-all-start.2 = ((bf16[2,512,768]{2,1,0:T(8,128)(2,1)}), bf16[2,512,768]{2,1,0:T(8,128)(2,1)S(1)}, u32[]{:S(2)}, u32[]{:S(2)}) async-start(bf16[2,512,768]{2,1,0:T(8,128)(2,1)} %param.16), calls=%async_computation.2 | async-start | bytes 3145728 | tf_op jit(solution)/shard_map/all_to_all | solution.py:581
  199.3 286.4 %reduce-scatter.3.cloned.1.call-start = ((), (), s32[]{:S(2)}) async-start(), calls=%async_computation.9 | async-start | bytes 11280384 | tf_op jit(solution)/shard_map/reduce_scatter | solution.py:596
  306.2 41.0 %all-to-all-start.3 = ((bf16[2,512,768]{2,1,0:T(8,128)(2,1)}), bf16[2,512,768]{2,1,0:T(8,128)(2,1)S(1)}, u32[]{:S(2)}, u32[]{:S(2)}) async-start(bf16[2,512,768]{2,1,0:T(8,128)(2,1)} %bitcast.30), calls=%async_computation.3 | async-start | bytes 3145728 | tf_op jit(solution)/shard_map/all_to_all | solution.py:763
  309.9 225.9 %reduce-scatter.5.cloned.1.call-start = ((), (), s32[]{:S(2)}) async-start(), calls=%async_computation.10 | async-start | bytes 3760128 | tf_op jit(solution)/shard_map/reduce_scatter | solution.py:596
  370.4 9.0 %collective-permute-start.11 = (bf16[8,2,48,1536]{3,2,1,0:T(8,128)(2,1)}, bf16[8,2,48,1536]{3,2,1,0:T(8,128)(2,1)}, u32[]{:S(2)}, u32[]{:S(2)}) collective-permute-start(bf16[8,2,48,1536]{3,2,1,0:T(8,128)(2,1)} %get-tuple-element.246), channel_id=1, source_target_pairs={{0,2},{2,0},{4,6},{6,4},{8,10},{10,8},{12,14},{14,12},{16,18},{18,... | collective-permute-start | bytes 7077896 | tf_op jit(solution)/shard_map/ppermute | solution.py:590
  382.4 28.5 %collective-permute-start.12 = (bf16[2,2,2,48,1536]{4,3,2,1,0:T(8,128)(2,1)}, bf16[2,2,2,48,1536]{4,3,2,1,0:T(8,128)(2,1)S(1)}, u32[]{:S(2)}, u32[]{:S(2)}) collective-permute-start(bf16[2,2,2,48,1536]{4,3,2,1,0:T(8,128)(2,1)} %fusion.5), channel_id=1, source_target_pairs={{0,1},{1,0},{2,3},{3,2},{4,5},{5,4},{6,7},{7,6},{8,9},{9,8},{10,11... | collective-permute-start | bytes 3538952 | tf_op jit(solution)/shard_map/ppermute | solution.py:593
  426.6 5.7 collective-permute-start.13
  436.2 49.5 %collective-permute-start.15 = (bf16[2,2,2,48,1920]{4,3,2,1,0:T(8,128)(2,1)}, bf16[2,2,2,48,1920]{4,3,2,1,0:T(8,128)(2,1)S(1)}, u32[]{:S(2)}, u32[]{:S(2)}) collective-permute-start(bf16[2,2,2,48,1920]{4,3,2,1,0:T(8,128)(2,1)} %fusion.3), channel_id=1, source_target_pairs={{0,1},{1,0},{2,3},{3,2},{4,5},{5,4},{6,7},{7,6},{8,9},{9,8},{10,11... | collective-permute-start | bytes 4423688 | tf_op jit(solution)/shard_map/ppermute | solution.py:593
  437.9 47.7 %collective-permute-start.14 = (bf16[2,2,48,1536]{3,2,1,0:T(8,128)(2,1)}, bf16[2,2,48,1536]{3,2,1,0:T(8,128)(2,1)}, u32[]{:S(2)}, u32[]{:S(2)}) collective-permute-start(bf16[2,2,48,1536]{3,2,1,0:T(8,128)(2,1)} %fusion.6), channel_id=1, source_target_pairs={{0,4},{2,6},{4,0},{6,2},{8,12},{10,14},{12,8},{14,10},{16,20},{18,... | collective-permute-start | bytes 1769480 | tf_op jit(solution)/shard_map/ppermute | solution.py:590
  490.8 18.7 %collective-permute-start.17 = (bf16[8,2,48,1152]{3,2,1,0:T(8,128)(2,1)}, bf16[8,2,48,1152]{3,2,1,0:T(8,128)(2,1)}, u32[]{:S(2)}, u32[]{:S(2)}) collective-permute-start(bf16[8,2,48,1152]{3,2,1,0:T(8,128)(2,1)} %get-tuple-element.287), channel_id=1, source_target_pairs={{0,2},{2,0},{4,6},{6,4},{8,10},{10,8},{12,14},{14,12},{16,18},{18,... | collective-permute-start | bytes 5308424 | tf_op jit(solution)/shard_map/ppermute | solution.py:590
  491.8 17.8 %copy-start.7 = (bf16[8,2,48,1152]{3,2,1,0:T(8,128)(2,1)S(1)}, bf16[8,2,48,1152]{3,2,1,0:T(8,128)(2,1)}, u32[]{:S(2)}) copy-start(bf16[8,2,48,1152]{3,2,1,0:T(8,128)(2,1)} %get-tuple-element.289) | copy-start | bytes 5308420
  493.7 13.9 %collective-permute-start.16 = (bf16[2,48,1536]{2,1,0:T(8,128)(2,1)}, bf16[2,48,1536]{2,1,0:T(8,128)(2,1)S(1)}, u32[]{:S(2)}, u32[]{:S(2)}) collective-permute-start(bf16[2,48,1536]{2,1,0:T(8,128)(2,1)} %fusion.11), channel_id=1, source_target_pairs={{0,8},{2,10},{4,12},{6,14},{8,0},{10,2},{12,4},{14,6},{16,24},{18,... | collective-permute-start | bytes 884744 | tf_op jit(solution)/shard_map/ppermute | solution.py:590
  511.0 22.7 %collective-permute-start.18 = (bf16[2,2,2,48,1152]{4,3,2,1,0:T(8,128)(2,1)S(1)}, bf16[2,2,2,48,1152]{4,3,2,1,0:T(8,128)(2,1)}, u32[]{:S(2)}, u32[]{:S(2)}) collective-permute-start(bf16[2,2,2,48,1152]{4,3,2,1,0:T(8,128)(2,1)S(1)} %fusion.7), channel_id=1, source_target_pairs={{0,1},{1,0},{2,3},{3,2},{4,5},{5,4},{6,7},{7,6},{8,9},{9,8},{10,11... | collective-permute-start | bytes 2654216 | tf_op jit(solution)/shard_map/ppermute | solution.py:593
  511.9 35.1 %collective-permute-start.20 = (bf16[2,2,48,1920]{3,2,1,0:T(8,128)(2,1)}, bf16[2,2,48,1920]{3,2,1,0:T(8,128)(2,1)}, u32[]{:S(2)}, u32[]{:S(2)}) collective-permute-start(bf16[2,2,48,1920]{3,2,1,0:T(8,128)(2,1)} %fusion.4), channel_id=1, source_target_pairs={{0,4},{2,6},{4,0},{6,2},{8,12},{10,14},{12,8},{14,10},{16,20},{18,... | collective-permute-start | bytes 2211848 | tf_op jit(solution)/shard_map/ppermute | solution.py:590
  513.2 33.8 %collective-permute-start.21 = (bf16[48,6912]{1,0:T(8,128)(2,1)S(1)}, bf16[48,6912]{1,0:T(8,128)(2,1)}, u32[]{:S(2)}, u32[]{:S(2)}) collective-permute-start(bf16[48,6912]{1,0:T(8,128)(2,1)S(1)} %copy-done.10), channel_id=1, source_target_pairs={{0,1},{1,0},{2,3},{3,2},{4,5},{5,4},{6,7},{7,6},{8,9},{9,8},{10,11... | collective-permute-start | bytes 1990664 | tf_op jit(solution)/shard_map/ppermute | solution.py:593
  514.6 21.2 %collective-permute-start.19 = (bf16[48,1536]{1,0:T(8,128)(2,1)}, bf16[48,1536]{1,0:T(8,128)(2,1)}, u32[]{:S(2)}, u32[]{:S(2)}) collective-permute-start(bf16[48,1536]{1,0:T(8,128)(2,1)} %fusion.19), channel_id=1, source_target_pairs={{0,16},{2,18},{4,20},{6,22},{8,24},{10,26},{12,28},{14,30},{16,0},... | collective-permute-start | bytes 442376 | tf_op jit(solution)/shard_map/ppermute | solution.py:590
  551.2 24.3 %all-to-all-start.4 = ((bf16[2,512,768]{2,1,0:T(8,128)(2,1)}), bf16[2,512,768]{2,1,0:T(8,128)(2,1)S(1)}, u32[]{:S(2)}, u32[]{:S(2)}) async-start(bf16[2,512,768]{2,1,0:T(8,128)(2,1)} %bitcast.64), calls=%async_computation.6 | async-start | bytes 3145728 | tf_op jit(solution)/shard_map/all_to_all | solution.py:763
  554.9 11.7 %collective-permute-start.22 = (bf16[2,2,48,1152]{3,2,1,0:T(8,128)(2,1)}, bf16[2,2,48,1152]{3,2,1,0:T(8,128)(2,1)}, u32[]{:S(2)}, u32[]{:S(2)}) collective-permute-start(bf16[2,2,48,1152]{3,2,1,0:T(8,128)(2,1)} %fusion.8), channel_id=1, source_target_pairs={{0,4},{2,6},{4,0},{6,2},{8,12},{10,14},{12,8},{14,10},{16,20},{18,... | collective-permute-start | bytes 1327112 | tf_op jit(solution)/shard_map/ppermute | solution.py:590
  556.4 21.2 %collective-permute-start.26 = (f32[8,1152]{1,0:T(8,128)}, f32[8,1152]{1,0:T(8,128)S(1)}, u32[]{:S(2)}, u32[]{:S(2)}) collective-permute-start(f32[8,1152]{1,0:T(8,128)} %bitcast.210), channel_id=1, source_target_pairs={{0,2},{2,0},{4,6},{6,4},{8,10},{10,8},{12,14},{14,12},{16,18},{18,... | collective-permute-start | bytes 110600 | tf_op jit(solution)/shard_map/ppermute | solution.py:590
  556.4 25.4 %collective-permute-start.25 = (bf16[2,48,1920]{2,1,0:T(8,128)(2,1)}, bf16[2,48,1920]{2,1,0:T(8,128)(2,1)}, u32[]{:S(2)}, u32[]{:S(2)}) collective-permute-start(bf16[2,48,1920]{2,1,0:T(8,128)(2,1)} %fusion.9), channel_id=1, source_target_pairs={{0,8},{2,10},{4,12},{6,14},{8,0},{10,2},{12,4},{14,6},{16,24},{18,... | collective-permute-start | bytes 1105928 | tf_op jit(solution)/shard_map/ppermute | solution.py:590
  556.6 25.1 %collective-permute-start.24 = (bf16[48,2304]{1,0:T(8,128)(2,1)}, bf16[48,2304]{1,0:T(8,128)(2,1)}, u32[]{:S(2)}, u32[]{:S(2)}) collective-permute-start(bf16[48,2304]{1,0:T(8,128)(2,1)} %reduce-scatter.5.cloned.1.call-done), channel_id=1, source_target_pairs={{0,1},{1,0},{2,3},{3,2},{4,5},{5,4},{6,7},{7,6},{8,9},{9,8},{10,11... | collective-permute-start | bytes 663560 | tf_op jit(solution)/shard_map/ppermute | solution.py:593
  558.6 23.2 %collective-permute-start.23 = (bf16[48,1536]{1,0:T(8,128)(2,1)}, bf16[48,1536]{1,0:T(8,128)(2,1)}, u32[]{:S(2)}, u32[]{:S(2)}) collective-permute-start(bf16[48,1536]{1,0:T(8,128)(2,1)} %fusion.18), channel_id=1, source_target_pairs={{0,1},{1,0},{2,3},{3,2},{4,5},{5,4},{6,7},{7,6},{8,9},{9,8},{10,11... | collective-permute-start | bytes 442376 | tf_op jit(solution)/shard_map/ppermute | solution.py:593
  585.5 9.8 %collective-permute-start.27 = (bf16[2,48,1152]{2,1,0:T(8,128)(2,1)}, bf16[2,48,1152]{2,1,0:T(8,128)(2,1)S(1)}, u32[]{:S(2)}, u32[]{:S(2)}) collective-permute-start(bf16[2,48,1152]{2,1,0:T(8,128)(2,1)} %fusion.12), channel_id=1, source_target_pairs={{0,8},{2,10},{4,12},{6,14},{8,0},{10,2},{12,4},{14,6},{16,24},{18,... | collective-permute-start | bytes 663560 | tf_op jit(solution)/shard_map/ppermute | solution.py:590
  585.6 11.6 %collective-permute-start.28 = (bf16[48,1920]{1,0:T(8,128)(2,1)S(1)}, bf16[48,1920]{1,0:T(8,128)(2,1)}, u32[]{:S(2)}, u32[]{:S(2)}) collective-permute-start(bf16[48,1920]{1,0:T(8,128)(2,1)S(1)} %fusion.15), channel_id=1, source_target_pairs={{0,16},{2,18},{4,20},{6,22},{8,24},{10,26},{12,28},{14,30},{16,0},... | collective-permute-start | bytes 552968 | tf_op jit(solution)/shard_map/ppermute | solution.py:590
  587.3 9.9 %collective-permute-start.29 = (f32[4,1152]{1,0:T(4,128)S(1)}, f32[4,1152]{1,0:T(4,128)S(1)}, u32[]{:S(2)}, u32[]{:S(2)}) collective-permute-start(f32[4,1152]{1,0:T(4,128)S(1)} %bitcast.268), channel_id=1, source_target_pairs={{0,4},{2,6},{4,0},{6,2},{8,12},{10,14},{12,8},{14,10},{16,20},{18,... | collective-permute-start | bytes 55304 | tf_op jit(solution)/shard_map/ppermute | solution.py:590
  598.7 6.4 %collective-permute-start.30 = (bf16[48,1152]{1,0:T(8,128)(2,1)S(1)}, bf16[48,1152]{1,0:T(8,128)(2,1)S(1)}, u32[]{:S(2)}, u32[]{:S(2)}) collective-permute-start(bf16[48,1152]{1,0:T(8,128)(2,1)S(1)} %fusion.23), channel_id=1, source_target_pairs={{0,16},{2,18},{4,20},{6,22},{8,24},{10,26},{12,28},{14,30},{16,0},... | collective-permute-start | bytes 331784 | tf_op jit(solution)/shard_map/ppermute | solution.py:590
  598.8 8.4 %collective-permute-start.31 = (bf16[48,1920]{1,0:T(8,128)(2,1)S(1)}, bf16[48,1920]{1,0:T(8,128)(2,1)S(1)}, u32[]{:S(2)}, u32[]{:S(2)}) collective-permute-start(bf16[48,1920]{1,0:T(8,128)(2,1)S(1)} %fusion.14), channel_id=1, source_target_pairs={{0,1},{1,0},{2,3},{3,2},{4,5},{5,4},{6,7},{7,6},{8,9},{9,8},{10,11... | collective-permute-start | bytes 552968 | tf_op jit(solution)/shard_map/ppermute | solution.py:593
  599.4 7.7 %collective-permute-start.32 = (f32[2,1152]{1,0:T(2,128)S(1)}, f32[2,1152]{1,0:T(2,128)S(1)}, u32[]{:S(2)}, u32[]{:S(2)}) collective-permute-start(f32[2,1152]{1,0:T(2,128)S(1)} %bitcast.269), channel_id=1, source_target_pairs={{0,8},{2,10},{4,12},{6,14},{8,0},{10,2},{12,4},{14,6},{16,24},{18,... | collective-permute-start | bytes 27656 | tf_op jit(solution)/shard_map/ppermute | solution.py:590
  606.3 4.8 collective-permute-start.33
  607.4 4.6 collective-permute-start.34
  612.0 3.7 collective-permute-start.35
  (25 other events, 134.2 us)
Sparse Core Ops, SparseCore 0:
  12.7 72.6 all-gather.4
  88.3 86.4 all-gather.6
  177.6 51.9 all-gather.8
  306.3 118.7 reduce-scatter.2
  438.1 68.4 reduce-scatter.4

commit v9 on v8

--- a/solution.py
+++ b/solution.py
@@ -796,29 +796,28 @@
         shape = (2,) * len(chip_bits) + (2, row_unit, own.shape[-1])
         addends = [part.reshape(shape) for part in (own, received)]
         axis = len(chip_bits)
-        for bit in [0] + chip_bits[::-1]:
+        for bit in [0] + chip_bits[:1:-1]:
             mine, pass_on = (bit_of(bit), across(bit)) if bit else (place, beside_seq)
             sent = total_of([side_of(part, 1 - mine, axis) for part in addends]).astype(half)
             (received,) = yield [(sent, pass_on)]
             addends = [side_of(part, mine, axis) for part in addends] + [received]
             axis -= 1
+        far, near = chip_bits[:2]
+
+        def corner(part, bits):
+            part = side_of(part, bit_of(far) ^ (1 if bits & far else 0), 0)
+            return side_of(part, bit_of(near) ^ (1 if bits & near else 0), 0)
+
+        received = yield [
+            (total_of([corner(part, bits) for part in addends]).astype(half), across(bits))
+            for bits in (near, far, near | far)
+        ]
+        addends = [corner(part, 0) for part in addends] + received
         current = total_of(addends).astype(half)
         (received,) = yield [(current, beside_seq)]
         low = jnp.where(place == 0, current, received).astype(single)
         high = jnp.where(place == 0, received, current).astype(single)
         return shares_of(terms, low, high)
-
-    def reduce_small(array):
-        bit = 1
-        while bit < groups:
-            view = array.reshape(-1, 2, array.shape[-1])
-            mine = bit_of(bit)
-            sent = side_of(view, 1 - mine, 1)
-            (received,) = yield [(sent, across(bit))]
-            array = side_of(view, mine, 1) + received
-            bit *= 2
-        (received,) = yield [(array, beside_seq)]
-        return (array + received)[0]
 
     weight_grads = [[None] * 4 for _ in range(layers)]
 
@@ -853,6 +852,7 @@
             second_group = begin_group(steps, layer, named)
             upstream = launch(upstream, [second_group])
             upstream = advance(upstream, second_group)
+            upstream = advance(upstream, *held[:1])
         packed_grad = attend_backward(packed, bias, upstream, totals, attended)
         if layer == layers - 1:
             packed_grad, output = lax.optimization_barrier((packed_grad, output))
@@ -862,7 +862,6 @@
             packed_grad = advance(packed_grad, first_group, second_group, *held[:1])
             last_group = begin_group(steps, layer, named)
             packed_grad = launch(packed_grad, [last_group])
-            packed_grad = advance(packed_grad, first_group)
             packed_grad = advance(packed_grad, last_group)
         gradient, *rounded, more_sums = project_grad(
             packed_grad, hidden, middle_grad, gains, whole, (single, half) if layer else (half,)
@@ -894,15 +893,15 @@
         [by_owner([small_grads[layer][part] for layer in range(layers)]) for part in range(3)],
         axis=1,
     )
-    small_result = []
-    rest = begin(reduce_small(owned), small_result.append)
-    gradient = launch(gradient, [rest])
-    input_grad = split_back(gradient)
+    owned, result = lax.optimization_barrier((owned, gradient))
+    totals = lax.psum(owned, ("wide", "seq"))
+    input_grad = split_back(result)
     while running:
-        input_grad = advance(input_grad, last_group)
-        input_grad = advance(input_grad, *[entry for entry in running if entry is not last_group])
+        output = advance(output, last_group)
+        output = advance(output, *[entry for entry in running if entry is not last_group])
+    output, totals = lax.optimization_barrier((output, totals))
+    owned = lax.dynamic_index_in_dim(totals, lax.axis_index("wide"), 0, keepdims=False)
     input_grad = input_grad.astype(single)
-    owned = small_result[0]
     stacked = [
         jnp.stack([weight_grads[layer][part] for layer in range(layers)]) for part in range(4)
     ]

time: 632 us -> 690 us (1.092)
  waiting for transfers between devices: 132 us -> 192 us
    psum x0 -> x1, waiting for transfers between devices: none -> 90.5 us  [per_device(): totals = lax.psum(owned, ('wide', 'seq'))]
    ppermute x25 -> x24, waiting for transfers between devices: 88.5 us -> 64.6 us  [across(): return lambda part: lax.ppermute(part, 'wide', pairs)]
    convert_element_type x12 -> x6, other arithmetic: 27.1 us -> 17.4 us  [reduce_group(): total_of([side_of(part, 1 - mine, axis) for part in addends]).astype(half)]
    all_to_all x2, waiting for transfers between devices: 9.01 us -> 0.01 us  [split_back(): return lax.all_to_all(parts, 'seq', split_axis=0, concat_axis=0, tiled=True)]
    ppermute x25 -> x24, starting transfers between devices: 21.3 us -> 25.5 us  [across(): return lambda part: lax.ppermute(part, 'wide', pairs)]
    ppermute x11 -> x10, waiting for transfers between devices: 26.2 us -> 27.7 us  [beside_seq(): return lax.ppermute(part, 'seq', swap)]
  transfers between devices with their start and end apart: 46 -> 45, of which waited for: 20 -> 14; matrix products, arithmetic and copies ran while one was open for 10% -> 10% of each run, Pallas kernels for 45% -> 41%
where the time goes in v9:
time: 690 us; the launch traced here: 683 us
  Pallas kernels  335 us (49%)
  waiting for transfers between devices  192 us (28%)
  starting transfers between devices  58.3 us (8%)
  other arithmetic  50.1 us (7%)
  local copies, waits for them, and re-layouts  33.1 us (5%)
  between operations  15.3 us (2%)
    pallas_call x8, Pallas kernels, row_tiled(): pl.pallas_call(kernel, grid=(length // ROW_TILE,), in_specs=in_specs, out...  141 us
    psum x1, waiting for transfers between devices, per_device(): totals = lax.psum(owned, ('wide', 'seq'))  90.5 us
    pallas_call x2, Pallas kernels, attend_backward(): pl.pallas_call(functools.partial(attend_grad_kernel, rows=BACKWARD_ROWS),...  74.4 us
    ppermute x24, waiting for transfers between devices, across(): return lambda part: lax.ppermute(part, 'wide', pairs)  64.6 us
    pallas_call x5, Pallas kernels, term_blocks(): pl.pallas_call(kernel, in_specs=[pl.BlockSpec(memory_space=pltpu.SMEM)] +...  62.9 us
    pallas_call x2, Pallas kernels, attend_forward(): pl.pallas_call(functools.partial(attend_kernel, rows=FORWARD_ROWS), grid=...  50.4 us
    ppermute x10, waiting for transfers between devices, beside_seq(): return lax.ppermute(part, 'seq', swap)  27.7 us
    ppermute x24, starting transfers between devices, across(): return lambda part: lax.ppermute(part, 'wide', pairs)  25.5 us
  transfers between devices with their start and end apart: 45, of which 14 were waited for; matrix products, arithmetic and copies ran while one was open for 10% of the time, Pallas kernels for 41%

profile of v9, /device:TPU:0, one launch (start us, length us, event | category | flops | bytes accessed | tf_op | source)
XLA Modules:
  0.0 682.9 jit_solution(9028325098763585788)
XLA Ops:
  15.1 4.2 all-to-all-start
  19.3 3.8 all-to-all-done
  23.1 4.6 all-to-all-start.1
  27.8 3.1 collective-permute-start
  31.0 16.2 %collective-permute-done.refs_1_ = bf16[1,48,1536]{2,1,0:T(8,128)(2,1)S(1)} collective-permute-done((bf16[1,48,1536]{2,1,0:T(8,128)(2,1)S(1)}, bf16[1,48,1536]{2,1,0:T(8,128)(2,1)S(1)}, u32[]{:S(2)}, u32[]{:S(2)}) %collective-permute-start) | collective-permute-done | bytes 147488 | tf_op jit(solution)/shard_map/ppermute | solution.py:590
  47.2 2.8 collective-permute-done.1.refs_1_
  52.9 20.3 %collective-permute-done.2.refs_1_ = bf16[2,48,1536]{2,1,0:T(8,128)(2,1)S(1)} collective-permute-done((bf16[2,48,1536]{2,1,0:T(8,128)(2,1)S(1)}, bf16[2,48,1536]{2,1,0:T(8,128)(2,1)S(1)}, u32[]{:S(2)}, u32[]{:S(2)}) %collective-permute-start.2) | collective-permute-done | bytes 294944 | tf_op jit(solution)/shard_map/ppermute | solution.py:590
  73.2 12.5 %collective-permute-done.3.refs_1_ = bf16[2,96,768]{2,1,0:T(8,128)(2,1)S(1)} collective-permute-done((bf16[2,96,768]{2,1,0:T(8,128)(2,1)S(1)}, bf16[2,96,768]{2,1,0:T(8,128)(2,1)S(1)}, u32[]{:S(2)}, u32[]{:S(2)}) %collective-permute-start.3) | collective-permute-done | bytes 294944 | tf_op jit(solution)/shard_map/ppermute | solution.py:590
  89.0 3.3 convert_add_fusion.hidden_ref
  96.3 9.1 %project.2 = (bf16[1024,768]{1,0:T(8,128)(2,1)}, bf16[1024,2304]{1,0:T(8,128)(2,1)}) custom-call(f32[1024,768]{1,0:T(8,128)} %convert_add_fusion.hidden_ref, f32[2,768]{1,0:T(2,128)} %squeeze.186.gains_ref, f32[6,768]{1,0:T(8,128)} %squeeze.187.offsets_ref, bf16[768,3200]{1,0:T(8,128)(2,1)} %all-gather.5.cloned.1.call-done.weight_ref.out_weight_ref), custom_call_target="tpu_custom_call" | custom-call | flops 226492416 | bytes 898560 | tf_op jit(solution)/shard_map/project/pallas_call | solution.py:231
  107.9 2.8 fusion.2.bias_ref
  110.7 25.2 %attend_forward.2 = (bf16[1024,768]{1,0:T(8,128)(2,1)}, f32[6,2,1024]{2,1,0:T(2,128)}) custom-call(bf16[1024,2304]{1,0:T(8,128)(2,1)} %get-tuple-element.194.query_ref.key_ref.value_ref, bf16[1024,2304]{1,0:T(8,128)(2,1)} %get-tuple-element.194.query_ref.key_ref.value_ref, bf16[1024,2304]{1,0:T(8,128)(2,1)} %get-tuple-element.194.query_ref.key_ref.value_ref, ...), custom_call_target="tpu_custom_call" | custom-call | flops 805306368 | bytes 393216 | tf_op jit(solution)/shard_map/attend_forward/pallas_call | solution.py:68
  135.9 6.2 collective-permute-done.7.refs_1_
  157.1 2.7 place_pieces.16
  159.7 2.2 copy-done.3
  162.0 24.2 %feed.2 = (f32[1024,768]{1,0:T(8,128)}, bf16[1024,768]{1,0:T(8,128)(2,1)}, bf16[1024,3072]{1,0:T(8,128)(2,1)}, bf16[1024,3072]{1,0:T(8,128)(2,1)}, f32[1024,768]{1,0:T(8,128)}) custom-call(bf16[1024,768]{1,0:T(8,128)(2,1)} %get-tuple-element.206.attended_ref.refs_2_, f32[1024,768]{1,0:T(8,128)} %convert_add_fusion.hidden_ref, f32[2,768]{1,0:T(2,128)} %squeeze.186.gains_ref, ...), custom_call_target="tpu_custom_call" | custom-call | flops 679477248 | bytes 2472192 | tf_op jit(solution)/shard_map/feed/pallas_call | solution.py:231
  186.2 9.2 %project.3 = (bf16[1024,768]{1,0:T(8,128)(2,1)}, bf16[1024,2304]{1,0:T(8,128)(2,1)}) custom-call(f32[1024,768]{1,0:T(8,128)} %get-tuple-element.210.hidden_ref, f32[2,768]{1,0:T(2,128)} %squeeze.188.gains_ref, f32[6,768]{1,0:T(8,128)} %squeeze.189.offsets_ref, bf16[768,6144]{1,0:T(8,128)(2,1)} %all-gather.7.cloned.1.call-done.weight_ref.out_weight_ref.up_ref), custom_call_target="tpu_custom_call" | custom-call | flops 226492416 | bytes 1181184 | tf_op jit(solution)/shard_map/project/pallas_call | solution.py:231
  195.4 3.8 all-to-all-start.2
  200.0 25.2 %attend_forward.3 = (bf16[1024,768]{1,0:T(8,128)(2,1)}, f32[6,2,1024]{2,1,0:T(2,128)}) custom-call(bf16[1024,2304]{1,0:T(8,128)(2,1)} %get-tuple-element.212.query_ref.key_ref.value_ref, bf16[1024,2304]{1,0:T(8,128)(2,1)} %get-tuple-element.212.query_ref.key_ref.value_ref, bf16[1024,2304]{1,0:T(8,128)(2,1)} %get-tuple-element.212.query_ref.key_ref.value_ref, ...), custom_call_target="tpu_custom_call" | custom-call | flops 805306368 | bytes 393216 | tf_op jit(solution)/shard_map/attend_forward/pallas_call | solution.py:68
  225.2 4.4 all-gather.9.cloned.1.call-done
  229.6 23.9 %feed.3 = (f32[1024,768]{1,0:T(8,128)}, bf16[1024,768]{1,0:T(8,128)(2,1)}, bf16[1024,3072]{1,0:T(8,128)(2,1)}, bf16[1024,3072]{1,0:T(8,128)(2,1)}, bf16[1024,768]{1,0:T(8,128)(2,1)}) custom-call(bf16[1024,768]{1,0:T(8,128)(2,1)} %get-tuple-element.214.attended_ref.refs_4_, f32[1024,768]{1,0:T(8,128)} %get-tuple-element.210.hidden_ref, ...), custom_call_target="tpu_custom_call" | custom-call | flops 679477248 | bytes 2951424 | tf_op jit(solution)/shard_map/feed/pallas_call | solution.py:231
  254.7 31.8 %feed_grad.2 = (bf16[1024,768]{1,0:T(8,128)(2,1)}, bf16[1024,3072]{1,0:T(8,128)(2,1)}, f32[1024,768]{1,0:T(8,128)}, bf16[1024,768]{1,0:T(8,128)(2,1)}, bf16[1024...) custom-call(bf16[1024,768]{1,0:T(8,128)(2,1)} %bitcast.230, ...), custom_call_target="tpu_custom_call" | custom-call | flops 679477248 | bytes 3050112 | tf_op jit(solution)/shard_map/feed_grad/pallas_call | solution.py:231
  286.5 19.7 %term_blocks.5 = bf16[16,48,6912]{2,1,0:T(8,128)(2,1)} custom-call(s32[1]{0:T(128)} %bitcast.20.core_ref, bf16[1024,3072]{1,0:T(8,128)(2,1)} %get-tuple-element.218.refs_0_, bf16[1024,768]{1,0:T(8,128)(2,1)} %get-tuple-element.219.refs_1_, bf16[1024,768]{1,0:T(8,128)(2,1)} %get-tuple-element.220.refs_2_, bf16[1024,3072]{1,0:T(8,128)(2,1)} %get-tuple-element.221.refs_3_, ...), custom_call_target="tpu_custom_call" | custom-call | flops 679477248 | bytes 1843200 | tf_op jit(solution)/shard_map/term_blocks/pallas_call | solution.py:548
  306.2 3.7 all-to-all-start.3
  310.0 37.3 %attend_backward.2.packed_grad_ref.refs_1_ = bf16[1024,2304]{1,0:T(8,128)(2,1)} custom-call(bf16[1024,2304]{1,0:T(8,128)(2,1)} %get-tuple-element.212.query_ref.key_ref.value_ref, bf16[1024,2304]{1,0:T(8,128)(2,1)} %get-tuple-element.212.query_ref.key_ref.value_ref, bf16[1024,2304]{1,0:T(8,128)(2,1)} %get-tuple-element.212.query_ref.key_ref.value_ref, ...), custom_call_target="tpu_custom_call" | custom-call | flops 2013265920 | bytes 786432 | tf_op jit(solution)/shard_map/attend_backward/pallas_call | solution.py:151
  347.3 11.1 %project_grad.2 = (f32[1024,768]{1,0:T(8,128)}, bf16[1024,768]{1,0:T(8,128)(2,1)}, f32[8,768]{1,0:T(8,128)}) custom-call(bf16[1024,2304]{1,0:T(8,128)(2,1)} %attend_backward.2.packed_grad_ref.refs_1_, f32[1024,768]{1,0:T(8,128)} %get-tuple-element.210.hidden_ref, f32[1024,768]{1,0:T(8,128)} %get-tuple-element.228.middle_grad_ref, ...), custom_call_target="tpu_custom_call" | custom-call | flops 226492416 | bytes 1574784 | tf_op jit(solution)/shard_map/project_grad/pallas_call | solution.py:231
  358.4 12.2 %term_blocks.6 = (bf16[8,2,48,1536]{3,2,1,0:T(8,128)(2,1)}, bf16[8,2,48,1536]{3,2,1,0:T(8,128)(2,1)}) custom-call(s32[1]{0:T(128)} %bitcast.20.core_ref, bf16[1024,3072]{1,0:T(8,128)(2,1)} %get-tuple-element.230.refs_0_, bf16[1024,768]{1,0:T(8,128)(2,1)} %get-tuple-element.231.refs_1_), custom_call_target="tpu_custom_call" | custom-call | flops 301989888 | bytes 786432 | tf_op jit(solution)/shard_map/term_blocks/pallas_call | solution.py:548
  371.0 8.5 %term_blocks.7 = bf16[16,48,2304]{2,1,0:T(8,128)(2,1)} custom-call(s32[1]{0:T(128)} %bitcast.20.core_ref, bf16[1024,768]{1,0:T(8,128)(2,1)} %get-tuple-element.234.refs_0_, bf16[1024,2304]{1,0:T(8,128)(2,1)} %attend_backward.2.packed_grad_ref.refs_1_), custom_call_target="tpu_custom_call" | custom-call | flops 226492416 | bytes 614400 | tf_op jit(solution)/shard_map/term_blocks/pallas_call | solution.py:548
  379.5 3.0 fusion.5
  384.2 21.2 %feed_grad.3 = (bf16[1024,768]{1,0:T(8,128)(2,1)}, bf16[1024,3072]{1,0:T(8,128)(2,1)}, f32[1024,768]{1,0:T(8,128)}, bf16[1024,768]{1,0:T(8,128)(2,1)}, bf16[1024...) custom-call(f32[1024,768]{1,0:T(8,128)} %get-tuple-element.240.gradient_ref, ...), custom_call_target="tpu_custom_call" | custom-call | flops 679477248 | bytes 2570880 | tf_op jit(solution)/shard_map/feed_grad/pallas_call | solution.py:231
  405.4 5.6 collective-permute-done.12
  411.0 2.8 fusion.6
  413.8 12.9 %term_blocks.8 = (bf16[8,2,48,1920]{3,2,1,0:T(8,128)(2,1)}, bf16[8,2,48,1920]{3,2,1,0:T(8,128)(2,1)}) custom-call(s32[1]{0:T(128)} %bitcast.20.core_ref, bf16[1024,768]{1,0:T(8,128)(2,1)} %get-tuple-element.251.refs_0_, bf16[1024,3072]{1,0:T(8,128)(2,1)} %get-tuple-element.252.refs_1_, bf16[1024,768]{1,0:T(8,128)(2,1)} %get-tuple-element.206.attended_ref.refs_2_, ...), custom_call_target="tpu_custom_call" | custom-call | flops 377487360 | bytes 1056768 | tf_op jit(solution)/shard_map/term_blocks/pallas_call | solution.py:548
  426.7 5.6 collective-permute-done.13
  432.3 3.9 fusion.3
  439.0 37.2 %attend_backward.3.refs_1_.packed_grad_ref = bf16[1024,2304]{1,0:T(8,128)(2,1)} custom-call(bf16[1024,2304]{1,0:T(8,128)(2,1)} %get-tuple-element.194.query_ref.key_ref.value_ref, bf16[1024,2304]{1,0:T(8,128)(2,1)} %get-tuple-element.194.query_ref.key_ref.value_ref, bf16[1024,2304]{1,0:T(8,128)(2,1)} %get-tuple-element.194.query_ref.key_ref.value_ref, ...), custom_call_target="tpu_custom_call" | custom-call | flops 2013265920 | bytes 786432 | tf_op jit(solution)/shard_map/attend_backward/pallas_call | solution.py:151
  476.1 9.7 %term_blocks.9 = (bf16[8,2,48,1152]{3,2,1,0:T(8,128)(2,1)}, bf16[8,2,48,1152]{3,2,1,0:T(8,128)(2,1)}) custom-call(s32[1]{0:T(128)} %bitcast.20.core_ref, bf16[1024,768]{1,0:T(8,128)(2,1)} %get-tuple-element.271.refs_0_, bf16[1024,2304]{1,0:T(8,128)(2,1)} %attend_backward.3.refs_1_.packed_grad_ref), custom_call_target="tpu_custom_call" | custom-call | flops 226492416 | bytes 614400 | tf_op jit(solution)/shard_map/term_blocks/pallas_call | solution.py:548
  485.9 3.0 fusion.4
  489.0 2.5 fusion.22
  500.5 2.3 fusion.7
  506.7 10.1 %project_grad.3 = (bf16[1024,768]{1,0:T(8,128)(2,1)}, f32[8,768]{1,0:T(8,128)}) custom-call(bf16[1024,2304]{1,0:T(8,128)(2,1)} %attend_backward.3.refs_1_.packed_grad_ref, f32[1024,768]{1,0:T(8,128)} %convert_add_fusion.hidden_ref, f32[1024,768]{1,0:T(8,128)} %get-tuple-element.279.middle_grad_ref, f32[2,768]{1,0:T(2,128)} %squeeze.186.gains_ref, ...), custom_call_target="tpu_custom_call" | custom-call | flops 226492416 | bytes 1095552 | tf_op jit(solution)/shard_map/project_grad/pallas_call | solution.py:231
  519.5 4.4 collective-permute-done.18
  523.9 2.4 fusion.8
  526.3 2.7 fusion.14
  538.0 3.7 all-to-all-start.4
  545.9 15.9 %collective-permute-done.24 = bf16[48,1536]{1,0:T(8,128)(2,1)S(1)} collective-permute-done((bf16[48,1536]{1,0:T(8,128)(2,1)}, bf16[48,1536]{1,0:T(8,128)(2,1)S(1)}, u32[]{:S(2)}, u32[]{:S(2)}) %collective-permute-start.24) | collective-permute-done | bytes 147488 | tf_op jit(solution)/shard_map/ppermute | solution.py:593
  565.4 2.3 collective-permute-start.31
  578.1 90.5 %all-reduce.3.cloned.1.call-done = f32[16,1152]{1,0:T(8,128)} async-done(((f32[16,1152]{1,0:T(8,128)}), f32[16,1152]{1,0:T(8,128)}) %all-reduce.3.cloned.1.call-update) | async-done | bytes 73744 | tf_op jit(solution)/shard_map/psum | solution.py:897
  (236 shorter events, 91.9 us)
Async XLA Ops:
  7.2 81.8 %copy-start = (f32[2,768]{1,0:T(2,128)S(1)}, f32[2,768]{1,0:T(2,128)}, u32[]{:S(2)}) copy-start(f32[2,768]{1,0:T(2,128)} %param.13) | copy-start | bytes 18436
  7.2 85.0 %all-gather.5.cloned.1.call-start = ((), (), s32[]{:S(2)}) async-start(), calls=%async_computation.7 | async-start | bytes 5222400 | tf_op jit(solution)/shard_map/all_gather | solution.py:697
  12.6 173.6 %all-gather.7.cloned.1.call-start = ((), (), s32[]{:S(2)}) async-start(), calls=%async_computation.8 | async-start | bytes 10027008 | tf_op jit(solution)/shard_map/all_gather | solution.py:697
  13.6 216.0 %all-gather.9.cloned.1.call-start = ((), (), s32[]{:S(2)}) async-start(), calls=%async_computation.12 | async-start | bytes 5013504 | tf_op jit(solution)/shard_map/all_gather | solution.py:699
  15.1 8.1 %all-to-all-start = ((s32[2,512,2]{1,2,0:T(2,128)}), s32[2,512,2]{1,2,0:T(2,128)S(1)}, u32[]{:S(2)}, u32[]{:S(2)}) async-start(s32[2,512,2]{1,2,0:T(2,128)} %pad_add_fusion), calls=%async_computation | async-start | bytes 16384 | tf_op jit(solution)/shard_map/all_to_all | solution.py:581
  23.1 65.8 %all-to-all-start.1 = ((bf16[2,512,768]{2,1,0:T(8,128)(2,1)}), bf16[2,512,768]{2,1,0:T(8,128)(2,1)}, u32[]{:S(2)}, u32[]{:S(2)}) async-start(bf16[2,512,768]{2,1,0:T(8,128)(2,1)} %param.12), calls=%async_computation.1 | async-start | bytes 3145728 | tf_op jit(solution)/shard_map/all_to_all | solution.py:581
  27.8 19.4 %collective-permute-start = (bf16[1,48,1536]{2,1,0:T(8,128)(2,1)S(1)}, bf16[1,48,1536]{2,1,0:T(8,128)(2,1)S(1)}, u32[]{:S(2)}, u32[]{:S(2)}) collective-permute-start(bf16[1,48,1536]{2,1,0:T(8,128)(2,1)S(1)} %constant_dynamic-slice_fusion.3.refs_0_), channel_id=1, source_target_pairs={{0,16},{2,18},{4,20},{6,22},{8,24},{10,26},{12,28},{14,30},{16,0},... | collective-permute-start | bytes 442376 | tf_op jit(solution)/shard_map/ppermute | solution.py:590
  30.9 19.2 %collective-permute-start.1 = (bf16[1,96,768]{2,1,0:T(8,128)(2,1)S(1)}, bf16[1,96,768]{2,1,0:T(8,128)(2,1)S(1)}, u32[]{:S(2)}, u32[]{:S(2)}) collective-permute-start(bf16[1,96,768]{2,1,0:T(8,128)(2,1)S(1)} %constant_dynamic-slice_fusion.2.refs_0_), channel_id=1, source_target_pairs={{0,16},{2,18},{4,20},{6,22},{8,24},{10,26},{12,28},{14,30},{16,0},... | collective-permute-start | bytes 442376 | tf_op jit(solution)/shard_map/ppermute | solution.py:590
  50.9 22.3 %collective-permute-start.2 = (bf16[2,48,1536]{2,1,0:T(8,128)(2,1)S(1)}, bf16[2,48,1536]{2,1,0:T(8,128)(2,1)S(1)}, u32[]{:S(2)}, u32[]{:S(2)}) collective-permute-start(bf16[2,48,1536]{2,1,0:T(8,128)(2,1)S(1)} %bitcast.222), channel_id=1, source_target_pairs={{0,8},{2,10},{4,12},{6,14},{8,0},{10,2},{12,4},{14,6},{16,24},{18,... | collective-permute-start | bytes 884744 | tf_op jit(solution)/shard_map/ppermute | solution.py:590
  50.9 34.7 %collective-permute-start.3 = (bf16[2,96,768]{2,1,0:T(8,128)(2,1)S(1)}, bf16[2,96,768]{2,1,0:T(8,128)(2,1)S(1)}, u32[]{:S(2)}, u32[]{:S(2)}) collective-permute-start(bf16[2,96,768]{2,1,0:T(8,128)(2,1)S(1)} %bitcast.224), channel_id=1, source_target_pairs={{0,8},{2,10},{4,12},{6,14},{8,0},{10,2},{12,4},{14,6},{16,24},{18,... | collective-permute-start | bytes 884744 | tf_op jit(solution)/shard_map/ppermute | solution.py:590
  85.9 19.6 %collective-permute-start.4 = (bf16[4,48,1536]{2,1,0:T(8,128)(2,1)S(1)}, bf16[4,48,1536]{2,1,0:T(8,128)(2,1)S(1)}, u32[]{:S(2)}, u32[]{:S(2)}) collective-permute-start(bf16[4,48,1536]{2,1,0:T(8,128)(2,1)S(1)} %bitcast.220), channel_id=1, source_target_pairs={{0,4},{2,6},{4,0},{6,2},{8,12},{10,14},{12,8},{14,10},{16,20},{18,... | collective-permute-start | bytes 1769480 | tf_op jit(solution)/shard_map/ppermute | solution.py:590
  87.5 18.0 %collective-permute-start.5 = (bf16[4,96,768]{2,1,0:T(8,128)(2,1)S(1)}, bf16[4,96,768]{2,1,0:T(8,128)(2,1)S(1)}, u32[]{:S(2)}, u32[]{:S(2)}) collective-permute-start(bf16[4,96,768]{2,1,0:T(8,128)(2,1)S(1)} %bitcast.218), channel_id=1, source_target_pairs={{0,1},{1,0},{2,3},{3,2},{4,5},{5,4},{6,7},{7,6},{8,9},{9,8},{10,11... | collective-permute-start | bytes 1769480 | tf_op jit(solution)/shard_map/ppermute | solution.py:593
  105.8 30.1 %collective-permute-start.6 = (bf16[8,48,1536]{2,1,0:T(8,128)(2,1)S(1)}, bf16[8,48,1536]{2,1,0:T(8,128)(2,1)}, u32[]{:S(2)}, u32[]{:S(2)}) collective-permute-start(bf16[8,48,1536]{2,1,0:T(8,128)(2,1)S(1)} %bitcast.213), channel_id=1, source_target_pairs={{0,1},{1,0},{2,3},{3,2},{4,5},{5,4},{6,7},{7,6},{8,9},{9,8},{10,11... | collective-permute-start | bytes 3538952 | tf_op jit(solution)/shard_map/ppermute | solution.py:593
  106.5 35.6 %collective-permute-start.7 = (bf16[4,192,768]{2,1,0:T(8,128)(2,1)S(1)}, bf16[4,192,768]{2,1,0:T(8,128)(2,1)S(1)}, u32[]{:S(2)}, u32[]{:S(2)}) collective-permute-start(bf16[4,192,768]{2,1,0:T(8,128)(2,1)S(1)} %bitcast.216), channel_id=1, source_target_pairs={{0,4},{2,6},{4,0},{6,2},{8,12},{10,14},{12,8},{14,10},{16,20},{18,... | collective-permute-start | bytes 3538952 | tf_op jit(solution)/shard_map/ppermute | solution.py:590
  142.4 10.6 %collective-permute-start.10 = (bf16[8,192,768]{2,1,0:T(8,128)(2,1)S(1)}, bf16[8,192,768]{2,1,0:T(8,128)(2,1)}, u32[]{:S(2)}, u32[]{:S(2)}) collective-permute-start(bf16[8,192,768]{2,1,0:T(8,128)(2,1)S(1)} %bitcast.211), channel_id=1, source_target_pairs={{0,2},{2,0},{4,6},{6,4},{8,10},{10,8},{12,14},{14,12},{16,18},{18,... | collective-permute-start | bytes 7077896 | tf_op jit(solution)/shard_map/ppermute | solution.py:590
  142.5 10.5 %collective-permute-start.8 = (bf16[8,48,1536]{2,1,0:T(8,128)(2,1)S(1)}, bf16[8,48,1536]{2,1,0:T(8,128)(2,1)}, u32[]{:S(2)}, u32[]{:S(2)}) collective-permute-start(bf16[8,48,1536]{2,1,0:T(8,128)(2,1)S(1)} %bitcast.214), channel_id=1, source_target_pairs={{0,2},{2,0},{4,6},{6,4},{8,10},{10,8},{12,14},{14,12},{16,18},{18,... | collective-permute-start | bytes 3538952 | tf_op jit(solution)/shard_map/ppermute | solution.py:590
  142.9 10.0 %collective-permute-start.9 = (bf16[8,48,1536]{2,1,0:T(8,128)(2,1)}, bf16[8,48,1536]{2,1,0:T(8,128)(2,1)}, u32[]{:S(2)}, u32[]{:S(2)}) collective-permute-start(bf16[8,48,1536]{2,1,0:T(8,128)(2,1)} %collective-permute-done.6.refs_1_), channel_id=1, source_target_pairs={{0,2},{2,0},{4,6},{6,4},{8,10},{10,8},{12,14},{14,12},{16,18},{18,... | collective-permute-start | bytes 3538952 | tf_op jit(solution)/shard_map/ppermute | solution.py:590
  195.4 58.1 %all-to-all-start.2 = ((bf16[2,512,768]{2,1,0:T(8,128)(2,1)}), bf16[2,512,768]{2,1,0:T(8,128)(2,1)S(1)}, u32[]{:S(2)}, u32[]{:S(2)}) async-start(bf16[2,512,768]{2,1,0:T(8,128)(2,1)} %param.16), calls=%async_computation.2 | async-start | bytes 3145728 | tf_op jit(solution)/shard_map/all_to_all | solution.py:581
  199.3 238.7 %reduce-scatter.3.cloned.1.call-start = ((), (), s32[]{:S(2)}) async-start(), calls=%async_computation.9 | async-start | bytes 11280384 | tf_op jit(solution)/shard_map/reduce_scatter | solution.py:596
  306.2 41.0 %all-to-all-start.3 = ((bf16[2,512,768]{2,1,0:T(8,128)(2,1)}), bf16[2,512,768]{2,1,0:T(8,128)(2,1)S(1)}, u32[]{:S(2)}, u32[]{:S(2)}) async-start(bf16[2,512,768]{2,1,0:T(8,128)(2,1)} %bitcast.30), calls=%async_computation.3 | async-start | bytes 3145728 | tf_op jit(solution)/shard_map/all_to_all | solution.py:763
  309.9 216.4 %reduce-scatter.5.cloned.1.call-start = ((), (), s32[]{:S(2)}) async-start(), calls=%async_computation.10 | async-start | bytes 3760128 | tf_op jit(solution)/shard_map/reduce_scatter | solution.py:596
  370.5 9.0 %collective-permute-start.11 = (bf16[8,2,48,1536]{3,2,1,0:T(8,128)(2,1)}, bf16[8,2,48,1536]{3,2,1,0:T(8,128)(2,1)}, u32[]{:S(2)}, u32[]{:S(2)}) collective-permute-start(bf16[8,2,48,1536]{3,2,1,0:T(8,128)(2,1)} %get-tuple-element.236), channel_id=1, source_target_pairs={{0,2},{2,0},{4,6},{6,4},{8,10},{10,8},{12,14},{14,12},{16,18},{18,... | collective-permute-start | bytes 7077896 | tf_op jit(solution)/shard_map/ppermute | solution.py:590
  382.5 28.5 %collective-permute-start.12 = (bf16[2,2,2,48,1536]{4,3,2,1,0:T(8,128)(2,1)}, bf16[2,2,2,48,1536]{4,3,2,1,0:T(8,128)(2,1)S(1)}, u32[]{:S(2)}, u32[]{:S(2)}) collective-permute-start(bf16[2,2,2,48,1536]{4,3,2,1,0:T(8,128)(2,1)} %fusion.5), channel_id=1, source_target_pairs={{0,1},{1,0},{2,3},{3,2},{4,5},{5,4},{6,7},{7,6},{8,9},{9,8},{10,11... | collective-permute-start | bytes 3538952 | tf_op jit(solution)/shard_map/ppermute | solution.py:593
  426.7 5.7 collective-permute-start.13
  436.2 49.7 %collective-permute-start.15 = (bf16[2,2,2,48,1920]{4,3,2,1,0:T(8,128)(2,1)}, bf16[2,2,2,48,1920]{4,3,2,1,0:T(8,128)(2,1)S(1)}, u32[]{:S(2)}, u32[]{:S(2)}) collective-permute-start(bf16[2,2,2,48,1920]{4,3,2,1,0:T(8,128)(2,1)} %fusion.3), channel_id=1, source_target_pairs={{0,1},{1,0},{2,3},{3,2},{4,5},{5,4},{6,7},{7,6},{8,9},{9,8},{10,11... | collective-permute-start | bytes 4423688 | tf_op jit(solution)/shard_map/ppermute | solution.py:593
  438.0 48.0 %collective-permute-start.16 = (bf16[48,6912]{1,0:T(8,128)(2,1)}, bf16[48,6912]{1,0:T(8,128)(2,1)}, u32[]{:S(2)}, u32[]{:S(2)}) collective-permute-start(bf16[48,6912]{1,0:T(8,128)(2,1)} %reduce-scatter.3.cloned.1.call-done), channel_id=1, source_target_pairs={{0,1},{1,0},{2,3},{3,2},{4,5},{5,4},{6,7},{7,6},{8,9},{9,8},{10,11... | collective-permute-start | bytes 1990664 | tf_op jit(solution)/shard_map/ppermute | solution.py:593
  438.3 47.6 %collective-permute-start.14 = (bf16[2,2,48,1536]{3,2,1,0:T(8,128)(2,1)}, bf16[2,2,48,1536]{3,2,1,0:T(8,128)(2,1)}, u32[]{:S(2)}, u32[]{:S(2)}) collective-permute-start(bf16[2,2,48,1536]{3,2,1,0:T(8,128)(2,1)} %fusion.6), channel_id=1, source_target_pairs={{0,4},{2,6},{4,0},{6,2},{8,12},{10,14},{12,8},{14,10},{16,20},{18,... | collective-permute-start | bytes 1769480 | tf_op jit(solution)/shard_map/ppermute | solution.py:590
  491.4 9.0 %collective-permute-start.17 = (bf16[8,2,48,1152]{3,2,1,0:T(8,128)(2,1)}, bf16[8,2,48,1152]{3,2,1,0:T(8,128)(2,1)}, u32[]{:S(2)}, u32[]{:S(2)}) collective-permute-start(bf16[8,2,48,1152]{3,2,1,0:T(8,128)(2,1)} %get-tuple-element.274), channel_id=1, source_target_pairs={{0,2},{2,0},{4,6},{6,4},{8,10},{10,8},{12,14},{14,12},{16,18},{18,... | collective-permute-start | bytes 5308424 | tf_op jit(solution)/shard_map/ppermute | solution.py:590
  494.7 31.7 %collective-permute-start.23 = (bf16[2,2,48,1920]{3,2,1,0:T(8,128)(2,1)}, bf16[2,2,48,1920]{3,2,1,0:T(8,128)(2,1)}, u32[]{:S(2)}, u32[]{:S(2)}) collective-permute-start(bf16[2,2,48,1920]{3,2,1,0:T(8,128)(2,1)} %fusion.4), channel_id=1, source_target_pairs={{0,4},{2,6},{4,0},{6,2},{8,12},{10,14},{12,8},{14,10},{16,20},{18,... | collective-permute-start | bytes 2211848 | tf_op jit(solution)/shard_map/ppermute | solution.py:590
  496.1 30.3 %collective-permute-start.20 = (bf16[48,1536]{1,0:T(8,128)(2,1)}, bf16[48,1536]{1,0:T(8,128)(2,1)}, u32[]{:S(2)}, u32[]{:S(2)}) collective-permute-start(bf16[48,1536]{1,0:T(8,128)(2,1)} %get-tuple-element.289), channel_id=1, source_target_pairs={{0,8},{2,10},{4,12},{6,14},{8,0},{10,2},{12,4},{14,6},{16,24},{18,... | collective-permute-start | bytes 442376 | tf_op jit(solution)/shard_map/ppermute | solution.py:590
  497.8 28.6 %collective-permute-start.21 = (bf16[48,1536]{1,0:T(8,128)(2,1)}, bf16[48,1536]{1,0:T(8,128)(2,1)}, u32[]{:S(2)}, u32[]{:S(2)}) collective-permute-start(bf16[48,1536]{1,0:T(8,128)(2,1)} %get-tuple-element.290), channel_id=1, source_target_pairs={{0,16},{2,18},{4,20},{6,22},{8,24},{10,26},{12,28},{14,30},{16,0},... | collective-permute-start | bytes 442376 | tf_op jit(solution)/shard_map/ppermute | solution.py:590
  498.5 27.8 %collective-permute-start.22 = (bf16[48,1536]{1,0:T(8,128)(2,1)}, bf16[48,1536]{1,0:T(8,128)(2,1)}, u32[]{:S(2)}, u32[]{:S(2)}) collective-permute-start(bf16[48,1536]{1,0:T(8,128)(2,1)} %get-tuple-element.291), channel_id=1, source_target_pairs={{0,24},{2,26},{4,28},{6,30},{8,16},{10,18},{12,20},{14,22},{16,8},... | collective-permute-start | bytes 442376 | tf_op jit(solution)/shard_map/ppermute | solution.py:590
  502.8 21.1 %collective-permute-start.18 = (bf16[2,2,2,48,1152]{4,3,2,1,0:T(8,128)(2,1)}, bf16[2,2,2,48,1152]{4,3,2,1,0:T(8,128)(2,1)S(1)}, u32[]{:S(2)}, u32[]{:S(2)}) collective-permute-start(bf16[2,2,2,48,1152]{4,3,2,1,0:T(8,128)(2,1)} %fusion.7), channel_id=1, source_target_pairs={{0,1},{1,0},{2,3},{3,2},{4,5},{5,4},{6,7},{7,6},{8,9},{9,8},{10,11... | collective-permute-start | bytes 2654216 | tf_op jit(solution)/shard_map/ppermute | solution.py:593
  529.0 13.2 %collective-permute-start.19 = (bf16[2,2,48,1152]{3,2,1,0:T(8,128)(2,1)}, bf16[2,2,48,1152]{3,2,1,0:T(8,128)(2,1)}, u32[]{:S(2)}, u32[]{:S(2)}) collective-permute-start(bf16[2,2,48,1152]{3,2,1,0:T(8,128)(2,1)} %fusion.8), channel_id=1, source_target_pairs={{0,4},{2,6},{4,0},{6,2},{8,12},{10,14},{12,8},{14,10},{16,20},{18,... | collective-permute-start | bytes 1327112 | tf_op jit(solution)/shard_map/ppermute | solution.py:590
  531.9 29.9 %collective-permute-start.25 = (bf16[48,2304]{1,0:T(8,128)(2,1)}, bf16[48,2304]{1,0:T(8,128)(2,1)}, u32[]{:S(2)}, u32[]{:S(2)}) collective-permute-start(bf16[48,2304]{1,0:T(8,128)(2,1)} %reduce-scatter.5.cloned.1.call-done), channel_id=1, source_target_pairs={{0,1},{1,0},{2,3},{3,2},{4,5},{5,4},{6,7},{7,6},{8,9},{9,8},{10,11... | collective-permute-start | bytes 663560 | tf_op jit(solution)/shard_map/ppermute | solution.py:593
  533.6 28.2 %collective-permute-start.26 = (bf16[48,1920]{1,0:T(8,128)(2,1)}, bf16[48,1920]{1,0:T(8,128)(2,1)}, u32[]{:S(2)}, u32[]{:S(2)}) collective-permute-start(bf16[48,1920]{1,0:T(8,128)(2,1)} %get-tuple-element.302), channel_id=1, source_target_pairs={{0,8},{2,10},{4,12},{6,14},{8,0},{10,2},{12,4},{14,6},{16,24},{18,... | collective-permute-start | bytes 552968 | tf_op jit(solution)/shard_map/ppermute | solution.py:590
  534.4 27.3 %collective-permute-start.27 = (bf16[48,1920]{1,0:T(8,128)(2,1)}, bf16[48,1920]{1,0:T(8,128)(2,1)}, u32[]{:S(2)}, u32[]{:S(2)}) collective-permute-start(bf16[48,1920]{1,0:T(8,128)(2,1)} %get-tuple-element.303), channel_id=1, source_target_pairs={{0,16},{2,18},{4,20},{6,22},{8,24},{10,26},{12,28},{14,30},{16,0},... | collective-permute-start | bytes 552968 | tf_op jit(solution)/shard_map/ppermute | solution.py:590
  535.7 26.0 %collective-permute-start.28 = (bf16[48,1920]{1,0:T(8,128)(2,1)}, bf16[48,1920]{1,0:T(8,128)(2,1)}, u32[]{:S(2)}, u32[]{:S(2)}) collective-permute-start(bf16[48,1920]{1,0:T(8,128)(2,1)} %get-tuple-element.304), channel_id=1, source_target_pairs={{0,24},{2,26},{4,28},{6,30},{8,16},{10,18},{12,20},{14,22},{16,8},... | collective-permute-start | bytes 552968 | tf_op jit(solution)/shard_map/ppermute | solution.py:590
  538.0 136.0 %all-to-all-start.4 = ((bf16[2,512,768]{2,1,0:T(8,128)(2,1)}), bf16[2,512,768]{2,1,0:T(8,128)(2,1)S(1)}, u32[]{:S(2)}, u32[]{:S(2)}) async-start(bf16[2,512,768]{2,1,0:T(8,128)(2,1)} %bitcast.247), calls=%async_computation.6 | async-start | bytes 3145728 | tf_op jit(solution)/shard_map/all_to_all | solution.py:763
  541.7 126.9 %all-reduce.3.cloned.1.call-start = ((), (), s32[]{:S(2)}) async-start(), calls=%async_computation.11 | async-start | bytes 147456 | tf_op jit(solution)/shard_map/psum | solution.py:897
  542.2 27.7 %copy-start.12 = (bf16[48,1536]{1,0:T(8,128)(2,1)S(1)}, bf16[48,1536]{1,0:T(8,128)(2,1)}, u32[]{:S(2)}) copy-start(bf16[48,1536]{1,0:T(8,128)(2,1)} %fusion.21) | copy-start | bytes 442372
  542.3 19.5 %collective-permute-start.24 = (bf16[48,1536]{1,0:T(8,128)(2,1)}, bf16[48,1536]{1,0:T(8,128)(2,1)S(1)}, u32[]{:S(2)}, u32[]{:S(2)}) collective-permute-start(bf16[48,1536]{1,0:T(8,128)(2,1)} %fusion.21), channel_id=1, source_target_pairs={{0,1},{1,0},{2,3},{3,2},{4,5},{5,4},{6,7},{7,6},{8,9},{9,8},{10,11... | collective-permute-start | bytes 442376 | tf_op jit(solution)/shard_map/ppermute | solution.py:593
  563.3 7.8 %collective-permute-start.29 = (bf16[48,1152]{1,0:T(8,128)(2,1)S(1)}, bf16[48,1152]{1,0:T(8,128)(2,1)S(1)}, u32[]{:S(2)}, u32[]{:S(2)}) collective-permute-start(bf16[48,1152]{1,0:T(8,128)(2,1)S(1)} %get-tuple-element.310), channel_id=1, source_target_pairs={{0,8},{2,10},{4,12},{6,14},{8,0},{10,2},{12,4},{14,6},{16,24},{18,... | collective-permute-start | bytes 331784 | tf_op jit(solution)/shard_map/ppermute | solution.py:590
  563.4 7.8 %collective-permute-start.30 = (bf16[48,1152]{1,0:T(8,128)(2,1)S(1)}, bf16[48,1152]{1,0:T(8,128)(2,1)S(1)}, u32[]{:S(2)}, u32[]{:S(2)}) collective-permute-start(bf16[48,1152]{1,0:T(8,128)(2,1)S(1)} %get-tuple-element.311), channel_id=1, source_target_pairs={{0,16},{2,18},{4,20},{6,22},{8,24},{10,26},{12,28},{14,30},{16,0},... | collective-permute-start | bytes 331784 | tf_op jit(solution)/shard_map/ppermute | solution.py:590
  565.4 6.6 collective-permute-start.31
  567.8 6.4 collective-permute-start.32
  573.2 4.8 collective-permute-start.33
  574.4 98.6 %copy-start.6 = (f32[1,48,2304]{2,1,0:T(8,128)S(1)}, f32[1,48,2304]{2,1,0:T(8,128)}, u32[]{:S(2)}) copy-start(f32[1,48,2304]{2,1,0:T(8,128)} %add_bitcast_fusion) | copy-start | bytes 1327108
  (22 other events, 98.9 us)
Sparse Core Ops, SparseCore 0:
  12.7 72.6 all-gather.4
  88.3 86.4 all-gather.6
  177.6 51.9 all-gather.8
  306.3 118.7 reduce-scatter.2
  439.1 76.6 reduce-scatter.4
  547.8 120.7 all-reduce.2

commit v10 on v9

--- a/solution.py
+++ b/solution.py
@@ -680,8 +680,6 @@
             current = join(current, received, bit_of(bit))
         return current.reshape(-1, columns)
 
-    marks = whole_sequence(jnp.stack([segment_ids, pad_mask], axis=2))
-    tokens, marks = lax.optimization_barrier((tokens, marks))
     my_tokens = whole_sequence(tokens)
 
     small = jnp.concatenate(
@@ -711,21 +709,23 @@
     all_offsets = whole_rows(small_whole[:, cut_gains:cut_rows], bias_rows.shape[1])
     all_up_bias = whole_rows(small_whole[:, cut_rows:], 1)[:, 0]
 
-    doc, pad = marks[:, 0], marks[:, 1]
-    positions = jnp.arange(doc.shape[0])
-    allowed = (doc[:, None] == doc[None, :]) & (
-        (pad[:, None] == 1) | (positions[:, None] == positions[None, :])
-    )
-    bias = jnp.where(allowed, 0.0, masked_bias)
-
     matrices = [None] * layers
     ups = {}
     fetches = [
         begin(gather_columns(up_weight[0]), functools.partial(ups.__setitem__, 0)),
         begin(gather_rows(down_weight[0]), functools.partial(downs.__setitem__, 0)),
     ]
+    marks = jnp.stack([segment_ids, pad_mask], axis=2)
     for _ in chip_bits[1:]:
-        time_embed = advance(time_embed, *fetches)
+        time_embed, marks = advance((time_embed, marks), *fetches)
+    marks = whole_sequence(marks)
+    doc, pad = marks[:, 0], marks[:, 1]
+    positions = jnp.arange(doc.shape[0])
+    allowed = (doc[:, None] == doc[None, :]) & (
+        (pad[:, None] == 1) | (positions[:, None] == positions[None, :])
+    )
+    bias = jnp.where(allowed, 0.0, masked_bias)
+
     my_time = lax.dynamic_index_in_dim(time_embed, place, 0, keepdims=True)
     hidden = my_tokens.astype(single) + my_time
     saved = []
@@ -818,6 +818,28 @@
         low = jnp.where(place == 0, current, received).astype(single)
         high = jnp.where(place == 0, received, current).astype(single)
         return shares_of(terms, low, high)
+
+    def reduce_small(array):
+        parts = [array.reshape((2,) * (len(chip_bits) + 1) + array.shape[1:])]
+        pairs = [(2, 1, len(chip_bits) - 1)]
+        pairs += [(bit, None, chip_bits.index(bit)) for bit in chip_bits[-2:1:-1]]
+        pairs += [(chip_bits[0], chip_bits[1], 0)]
+        for high, low, axis in pairs:
+
+            def chosen(bits):
+                def pick(part):
+                    if low is not None:
+                        part = side_of(part, bit_of(low) ^ (1 if bits & low else 0), axis + 1)
+                    return side_of(part, bit_of(high) ^ (1 if bits & high else 0), axis)
+
+                return total_of([pick(part) for part in parts])
+
+            masks = [high] if low is None else [low, high, low | high]
+            received = yield [(chosen(bits), across(bits)) for bits in masks]
+            parts = [chosen(0)] + received
+        current = total_of(parts)
+        (received,) = yield [(current, beside_seq)]
+        return current + received
 
     weight_grads = [[None] * 4 for _ in range(layers)]
 
@@ -877,7 +899,6 @@
             gradient = advance(gradient, first_group)
         if not layer:
             gradient = advance(gradient, last_group)
-            gradient = advance(gradient, first_group, second_group, *held)
         small_grads[layer] = (
             jnp.stack([more_sums[0], sums[1]]),
             jnp.stack([more_sums[1], more_sums[2], more_sums[3], sums[3], sums[2], sums[0]]),
@@ -893,14 +914,15 @@
         [by_owner([small_grads[layer][part] for layer in range(layers)]) for part in range(3)],
         axis=1,
     )
-    owned, result = lax.optimization_barrier((owned, gradient))
-    totals = lax.psum(owned, ("wide", "seq"))
-    input_grad = split_back(result)
+    small_result = []
+    begin(reduce_small(owned), small_result.append)
+    output = launch(output, running[-1:])
+    output = advance(output, first_group, second_group, *held)
+    input_grad = split_back(gradient)
     while running:
         output = advance(output, last_group)
         output = advance(output, *[entry for entry in running if entry is not last_group])
-    output, totals = lax.optimization_barrier((output, totals))
-    owned = lax.dynamic_index_in_dim(totals, lax.axis_index("wide"), 0, keepdims=False)
+    owned = small_result[0]
     input_grad = input_grad.astype(single)
     stacked = [
         jnp.stack([weight_grads[layer][part] for layer in range(layers)]) for part in range(4)

time: 690 us -> 601 us (0.87)
  waiting for transfers between devices: 192 us -> 86.1 us
  blocking collectives: 0 us -> 25.1 us
  Pallas kernels: 335 us -> 323 us
    psum x1 -> x0, waiting for transfers between devices: 90.5 us -> none  [per_device(): totals = lax.psum(owned, ('wide', 'seq'))]
    all_to_all x0 -> x1, blocking collectives: none -> 25.1 us  [whole_sequence(): lax.all_to_all(part, 'seq', split_axis=0, concat_axis=1, tiled=True)[0]]
    ppermute x24 -> x30, starting transfers between devices: 25.5 us -> 38.2 us  [across(): return lambda part: lax.ppermute(part, 'wide', pairs)]
    pallas_call x8, Pallas kernels: 141 us -> 130 us  [row_tiled(): pl.pallas_call(kernel, grid=(length // ROW_TILE,), in_specs=in_specs, out...]
    ppermute x10 -> x11, waiting for transfers between devices: 27.7 us -> 20 us  [beside_seq(): return lax.ppermute(part, 'seq', swap)]
    ppermute x24 -> x30, waiting for transfers between devices: 64.6 us -> 65.9 us  [across(): return lambda part: lax.ppermute(part, 'wide', pairs)]
  transfers between devices with their start and end apart: 45 -> 50, of which waited for: 14 -> 13; matrix products, arithmetic and copies ran while one was open for 10% -> 11% of each run, Pallas kernels for 41% -> 47%
where the time goes in v10:
time: 601 us; the launch traced here: 595 us
  Pallas kernels  323 us (54%)
  waiting for transfers between devices  86.1 us (14%)
  starting transfers between devices  63.7 us (11%)
  other arithmetic  47.2 us (8%)
  local copies, waits for them, and re-layouts  34.7 us (6%)
  blocking collectives  25.1 us (4%)
  between operations  15 us (2%)
    pallas_call x8, Pallas kernels, row_tiled(): pl.pallas_call(kernel, grid=(length // ROW_TILE,), in_specs=in_specs, out...  130 us
    pallas_call x2, Pallas kernels, attend_backward(): pl.pallas_call(functools.partial(attend_grad_kernel, rows=BACKWARD_ROWS),...  74.2 us
    ppermute x30, waiting for transfers between devices, across(): return lambda part: lax.ppermute(part, 'wide', pairs)  65.9 us
    pallas_call x5, Pallas kernels, term_blocks(): pl.pallas_call(kernel, in_specs=[pl.BlockSpec(memory_space=pltpu.SMEM)] +...  63.2 us
    pallas_call x2, Pallas kernels, attend_forward(): pl.pallas_call(functools.partial(attend_kernel, rows=FORWARD_ROWS), grid=...  50.4 us
    ppermute x30, starting transfers between devices, across(): return lambda part: lax.ppermute(part, 'wide', pairs)  38.2 us
    all_to_all x1, blocking collectives, whole_sequence(): lax.all_to_all(part, 'seq', split_axis=0, concat_axis=1, tiled=True)[0]  25.1 us
    ppermute x11, waiting for transfers between devices, beside_seq(): return lax.ppermute(part, 'seq', swap)  20 us
  transfers between devices with their start and end apart: 50, of which 13 were waited for; matrix products, arithmetic and copies ran while one was open for 11% of the time, Pallas kernels for 47%

profile of v10, /device:TPU:0, one launch (start us, length us, event | category | flops | bytes accessed | tf_op | source)
XLA Modules:
  0.0 595.2 jit_solution(10164496637210265019)
XLA Ops:
  14.4 4.7 all-to-all-start
  19.2 4.1 collective-permute-start
  23.4 16.7 %collective-permute-done.refs_1_ = bf16[1,48,1536]{2,1,0:T(8,128)(2,1)S(1)} collective-permute-done((bf16[1,48,1536]{2,1,0:T(8,128)(2,1)S(1)}, bf16[1,48,1536]{2,1,0:T(8,128)(2,1)S(1)}, u32[]{:S(2)}, u32[]{:S(2)}) %collective-permute-start) | collective-permute-done | bytes 147488 | tf_op jit(solution)/shard_map/ppermute | solution.py:590
  40.1 6.5 %collective-permute-done.1.refs_1_ = bf16[1,96,768]{2,1,0:T(8,128)(2,1)S(1)} collective-permute-done((bf16[1,96,768]{2,1,0:T(8,128)(2,1)S(1)}, bf16[1,96,768]{2,1,0:T(8,128)(2,1)S(1)}, u32[]{:S(2)}, u32[]{:S(2)}) %collective-permute-start.1) | collective-permute-done | bytes 147488 | tf_op jit(solution)/shard_map/ppermute | solution.py:590
  49.5 14.9 %collective-permute-done.2.refs_1_ = bf16[2,48,1536]{2,1,0:T(8,128)(2,1)S(1)} collective-permute-done((bf16[2,48,1536]{2,1,0:T(8,128)(2,1)S(1)}, bf16[2,48,1536]{2,1,0:T(8,128)(2,1)S(1)}, u32[]{:S(2)}, u32[]{:S(2)}) %collective-permute-start.2) | collective-permute-done | bytes 294944 | tf_op jit(solution)/shard_map/ppermute | solution.py:590
  64.3 13.5 %collective-permute-done.3.refs_1_ = bf16[2,96,768]{2,1,0:T(8,128)(2,1)S(1)} collective-permute-done((bf16[2,96,768]{2,1,0:T(8,128)(2,1)S(1)}, bf16[2,96,768]{2,1,0:T(8,128)(2,1)S(1)}, u32[]{:S(2)}, u32[]{:S(2)}) %collective-permute-start.3) | collective-permute-done | bytes 294944 | tf_op jit(solution)/shard_map/ppermute | solution.py:590
  81.6 3.4 convert_add_fusion.hidden_ref
  89.0 8.9 %project.2 = (bf16[1024,768]{1,0:T(8,128)(2,1)}, bf16[1024,2304]{1,0:T(8,128)(2,1)}) custom-call(f32[1024,768]{1,0:T(8,128)} %convert_add_fusion.hidden_ref, f32[2,768]{1,0:T(2,128)} %squeeze.265.gains_ref, f32[6,768]{1,0:T(8,128)} %squeeze.266.offsets_ref, bf16[768,3200]{1,0:T(8,128)(2,1)} %all-gather.5.cloned.1.call-done.weight_ref.out_weight_ref), custom_call_target="tpu_custom_call" | custom-call | flops 226492416 | bytes 898560 | tf_op jit(solution)/shard_map/project/pallas_call | solution.py:231
  99.8 25.1 %all_to_all.37 = s32[2,512,2]{1,2,0:T(2,128)S(1)} all-to-all(s32[2,512,2]{1,2,0:T(2,128)S(1)} %pad_add_fusion), channel_id=1, replica_groups=mesh['wide'=16,'seq'=2] {'seq'}, dimensions={0} | all-to-all | bytes 16384 | tf_op jit(solution)/shard_map/all_to_all | solution.py:581
  124.9 2.8 fusion.2.bias_ref
  127.7 25.2 %attend_forward.2 = (bf16[1024,768]{1,0:T(8,128)(2,1)}, f32[6,2,1024]{2,1,0:T(2,128)}) custom-call(bf16[1024,2304]{1,0:T(8,128)(2,1)} %get-tuple-element.213.query_ref.key_ref.value_ref, bf16[1024,2304]{1,0:T(8,128)(2,1)} %get-tuple-element.213.query_ref.key_ref.value_ref, bf16[1024,2304]{1,0:T(8,128)(2,1)} %get-tuple-element.213.query_ref.key_ref.value_ref, ...), custom_call_target="tpu_custom_call" | custom-call | flops 805306368 | bytes 393216 | tf_op jit(solution)/shard_map/attend_forward/pallas_call | solution.py:68
  167.8 2.7 place_pieces.16
  170.5 2.2 copy-done.3
  172.7 24.2 %feed.2 = (f32[1024,768]{1,0:T(8,128)}, bf16[1024,768]{1,0:T(8,128)(2,1)}, bf16[1024,3072]{1,0:T(8,128)(2,1)}, bf16[1024,3072]{1,0:T(8,128)(2,1)}, f32[1024,768]{1,0:T(8,128)}) custom-call(bf16[1024,768]{1,0:T(8,128)(2,1)} %get-tuple-element.225.attended_ref.refs_2_, f32[1024,768]{1,0:T(8,128)} %convert_add_fusion.hidden_ref, f32[2,768]{1,0:T(2,128)} %squeeze.265.gains_ref, ...), custom_call_target="tpu_custom_call" | custom-call | flops 679477248 | bytes 2472192 | tf_op jit(solution)/shard_map/feed/pallas_call | solution.py:231
  197.0 9.0 %project.3 = (bf16[1024,768]{1,0:T(8,128)(2,1)}, bf16[1024,2304]{1,0:T(8,128)(2,1)}) custom-call(f32[1024,768]{1,0:T(8,128)} %get-tuple-element.229.hidden_ref, f32[2,768]{1,0:T(2,128)} %squeeze.268.gains_ref, f32[6,768]{1,0:T(8,128)} %squeeze.269.offsets_ref, bf16[768,6144]{1,0:T(8,128)(2,1)} %all-gather.7.cloned.1.call-done.weight_ref.out_weight_ref.up_ref), custom_call_target="tpu_custom_call" | custom-call | flops 226492416 | bytes 1181184 | tf_op jit(solution)/shard_map/project/pallas_call | solution.py:231
  206.0 3.8 all-to-all-start.2
  211.0 25.2 %attend_forward.3 = (bf16[1024,768]{1,0:T(8,128)(2,1)}, f32[6,2,1024]{2,1,0:T(2,128)}) custom-call(bf16[1024,2304]{1,0:T(8,128)(2,1)} %get-tuple-element.231.query_ref.key_ref.value_ref, bf16[1024,2304]{1,0:T(8,128)(2,1)} %get-tuple-element.231.query_ref.key_ref.value_ref, bf16[1024,2304]{1,0:T(8,128)(2,1)} %get-tuple-element.231.query_ref.key_ref.value_ref, ...), custom_call_target="tpu_custom_call" | custom-call | flops 805306368 | bytes 393216 | tf_op jit(solution)/shard_map/attend_forward/pallas_call | solution.py:68
  236.2 23.9 %feed.3 = (f32[1024,768]{1,0:T(8,128)}, bf16[1024,768]{1,0:T(8,128)(2,1)}, bf16[1024,3072]{1,0:T(8,128)(2,1)}, bf16[1024,3072]{1,0:T(8,128)(2,1)}, bf16[1024,768]{1,0:T(8,128)(2,1)}) custom-call(bf16[1024,768]{1,0:T(8,128)(2,1)} %get-tuple-element.233.attended_ref.refs_4_, f32[1024,768]{1,0:T(8,128)} %get-tuple-element.229.hidden_ref, ...), custom_call_target="tpu_custom_call" | custom-call | flops 679477248 | bytes 2951424 | tf_op jit(solution)/shard_map/feed/pallas_call | solution.py:231
  261.3 21.1 %feed_grad.2 = (bf16[1024,768]{1,0:T(8,128)(2,1)}, bf16[1024,3072]{1,0:T(8,128)(2,1)}, f32[1024,768]{1,0:T(8,128)}, bf16[1024,768]{1,0:T(8,128)(2,1)}, bf16[1024...) custom-call(bf16[1024,768]{1,0:T(8,128)(2,1)} %bitcast.239, ...), custom_call_target="tpu_custom_call" | custom-call | flops 679477248 | bytes 3050112 | tf_op jit(solution)/shard_map/feed_grad/pallas_call | solution.py:231
  282.4 19.7 %term_blocks.5 = bf16[16,48,6912]{2,1,0:T(8,128)(2,1)} custom-call(s32[1]{0:T(128)} %bitcast.20.core_ref, bf16[1024,3072]{1,0:T(8,128)(2,1)} %get-tuple-element.237.refs_0_, bf16[1024,768]{1,0:T(8,128)(2,1)} %get-tuple-element.238.refs_1_, bf16[1024,768]{1,0:T(8,128)(2,1)} %get-tuple-element.239.refs_2_, bf16[1024,3072]{1,0:T(8,128)(2,1)} %get-tuple-element.240.refs_3_, ...), custom_call_target="tpu_custom_call" | custom-call | flops 679477248 | bytes 1843200 | tf_op jit(solution)/shard_map/term_blocks/pallas_call | solution.py:548
  302.2 3.7 all-to-all-start.3
  305.9 36.9 %attend_backward.2.packed_grad_ref.refs_1_ = bf16[1024,2304]{1,0:T(8,128)(2,1)} custom-call(bf16[1024,2304]{1,0:T(8,128)(2,1)} %get-tuple-element.231.query_ref.key_ref.value_ref, bf16[1024,2304]{1,0:T(8,128)(2,1)} %get-tuple-element.231.query_ref.key_ref.value_ref, bf16[1024,2304]{1,0:T(8,128)(2,1)} %get-tuple-element.231.query_ref.key_ref.value_ref, ...), custom_call_target="tpu_custom_call" | custom-call | flops 2013265920 | bytes 786432 | tf_op jit(solution)/shard_map/attend_backward/pallas_call | solution.py:151
  342.8 11.0 %project_grad.2 = (f32[1024,768]{1,0:T(8,128)}, bf16[1024,768]{1,0:T(8,128)(2,1)}, f32[8,768]{1,0:T(8,128)}) custom-call(bf16[1024,2304]{1,0:T(8,128)(2,1)} %attend_backward.2.packed_grad_ref.refs_1_, f32[1024,768]{1,0:T(8,128)} %get-tuple-element.229.hidden_ref, f32[1024,768]{1,0:T(8,128)} %get-tuple-element.247.middle_grad_ref, ...), custom_call_target="tpu_custom_call" | custom-call | flops 226492416 | bytes 1574784 | tf_op jit(solution)/shard_map/project_grad/pallas_call | solution.py:231
  353.9 12.2 %term_blocks.6 = (bf16[8,2,48,1536]{3,2,1,0:T(8,128)(2,1)}, bf16[8,2,48,1536]{3,2,1,0:T(8,128)(2,1)}) custom-call(s32[1]{0:T(128)} %bitcast.20.core_ref, bf16[1024,3072]{1,0:T(8,128)(2,1)} %get-tuple-element.249.refs_0_, bf16[1024,768]{1,0:T(8,128)(2,1)} %get-tuple-element.250.refs_1_), custom_call_target="tpu_custom_call" | custom-call | flops 301989888 | bytes 786432 | tf_op jit(solution)/shard_map/term_blocks/pallas_call | solution.py:548
  366.5 8.6 %term_blocks.7 = bf16[16,48,2304]{2,1,0:T(8,128)(2,1)} custom-call(s32[1]{0:T(128)} %bitcast.20.core_ref, bf16[1024,768]{1,0:T(8,128)(2,1)} %get-tuple-element.253.refs_0_, bf16[1024,2304]{1,0:T(8,128)(2,1)} %attend_backward.2.packed_grad_ref.refs_1_), custom_call_target="tpu_custom_call" | custom-call | flops 226492416 | bytes 614400 | tf_op jit(solution)/shard_map/term_blocks/pallas_call | solution.py:548
  375.2 3.1 fusion.5
  380.0 21.2 %feed_grad.3 = (bf16[1024,768]{1,0:T(8,128)(2,1)}, bf16[1024,3072]{1,0:T(8,128)(2,1)}, f32[1024,768]{1,0:T(8,128)}, bf16[1024,768]{1,0:T(8,128)(2,1)}, bf16[1024...) custom-call(f32[1024,768]{1,0:T(8,128)} %get-tuple-element.259.gradient_ref, ...), custom_call_target="tpu_custom_call" | custom-call | flops 679477248 | bytes 2570880 | tf_op jit(solution)/shard_map/feed_grad/pallas_call | solution.py:231
  401.2 5.4 collective-permute-done.12
  406.6 2.8 fusion.6
  409.4 12.8 %term_blocks.8 = (bf16[8,2,48,1920]{3,2,1,0:T(8,128)(2,1)}, bf16[8,2,48,1920]{3,2,1,0:T(8,128)(2,1)}) custom-call(s32[1]{0:T(128)} %bitcast.20.core_ref, bf16[1024,768]{1,0:T(8,128)(2,1)} %get-tuple-element.270.refs_0_, bf16[1024,3072]{1,0:T(8,128)(2,1)} %get-tuple-element.271.refs_1_, bf16[1024,768]{1,0:T(8,128)(2,1)} %get-tuple-element.225.attended_ref.refs_2_, ...), custom_call_target="tpu_custom_call" | custom-call | flops 377487360 | bytes 1056768 | tf_op jit(solution)/shard_map/term_blocks/pallas_call | solution.py:548
  422.3 5.6 collective-permute-done.13
  427.8 3.9 fusion.3
  439.1 37.3 %attend_backward.3.refs_1_.packed_grad_ref = bf16[1024,2304]{1,0:T(8,128)(2,1)} custom-call(bf16[1024,2304]{1,0:T(8,128)(2,1)} %get-tuple-element.213.query_ref.key_ref.value_ref, bf16[1024,2304]{1,0:T(8,128)(2,1)} %get-tuple-element.213.query_ref.key_ref.value_ref, bf16[1024,2304]{1,0:T(8,128)(2,1)} %get-tuple-element.213.query_ref.key_ref.value_ref, ...), custom_call_target="tpu_custom_call" | custom-call | flops 2013265920 | bytes 786432 | tf_op jit(solution)/shard_map/attend_backward/pallas_call | solution.py:151
  476.4 9.9 %term_blocks.9 = (bf16[8,2,48,1152]{3,2,1,0:T(8,128)(2,1)}, bf16[8,2,48,1152]{3,2,1,0:T(8,128)(2,1)}) custom-call(s32[1]{0:T(128)} %bitcast.20.core_ref, bf16[1024,768]{1,0:T(8,128)(2,1)} %get-tuple-element.290.refs_0_, bf16[1024,2304]{1,0:T(8,128)(2,1)} %attend_backward.3.refs_1_.packed_grad_ref), custom_call_target="tpu_custom_call" | custom-call | flops 226492416 | bytes 614400 | tf_op jit(solution)/shard_map/term_blocks/pallas_call | solution.py:548
  486.3 2.9 fusion.22
  489.2 2.7 fusion.4
  493.4 2.3 collective-permute-done.17
  499.8 3.0 collective-permute-start.18
  502.8 4.7 collective-permute-start.19
  507.6 10.0 %project_grad.3 = (bf16[1024,768]{1,0:T(8,128)(2,1)}, f32[8,768]{1,0:T(8,128)}) custom-call(bf16[1024,2304]{1,0:T(8,128)(2,1)} %attend_backward.3.refs_1_.packed_grad_ref, f32[1024,768]{1,0:T(8,128)} %convert_add_fusion.hidden_ref, f32[1024,768]{1,0:T(8,128)} %get-tuple-element.298.middle_grad_ref, f32[2,768]{1,0:T(2,128)} %squeeze.265.gains_ref, ...), custom_call_target="tpu_custom_call" | custom-call | flops 226492416 | bytes 1095552 | tf_op jit(solution)/shard_map/project_grad/pallas_call | solution.py:231
  528.2 2.5 fusion.14
  531.0 3.7 all-to-all-start.4
  534.7 3.9 collective-permute-done.23
  539.1 3.8 collective-permute-start.27
  544.8 13.5 %collective-permute-done.24 = bf16[48,1536]{1,0:T(8,128)(2,1)S(1)} collective-permute-done((bf16[48,1536]{1,0:T(8,128)(2,1)}, bf16[48,1536]{1,0:T(8,128)(2,1)S(1)}, u32[]{:S(2)}, u32[]{:S(2)}) %collective-permute-start.24) | collective-permute-done | bytes 147488 | tf_op jit(solution)/shard_map/ppermute | solution.py:593
  562.9 3.0 collective-permute-start.33
  569.1 3.8 collective-permute-start.37
  574.1 2.7 collective-permute-start.38
  (263 shorter events, 85.6 us)
Async XLA Ops:
  7.2 77.7 %all-gather.5.cloned.1.call-start = ((), (), s32[]{:S(2)}) async-start(), calls=%async_computation.7 | async-start | bytes 5222400 | tf_op jit(solution)/shard_map/all_gather | solution.py:695
  12.6 184.4 %all-gather.7.cloned.1.call-start = ((), (), s32[]{:S(2)}) async-start(), calls=%async_computation.8 | async-start | bytes 10027008 | tf_op jit(solution)/shard_map/all_gather | solution.py:695
  13.6 222.6 %all-gather.9.cloned.1.call-start = ((), (), s32[]{:S(2)}) async-start(), calls=%async_computation.11 | async-start | bytes 5013504 | tf_op jit(solution)/shard_map/all_gather | solution.py:697
  14.4 67.1 %all-to-all-start = ((bf16[2,512,768]{2,1,0:T(8,128)(2,1)}), bf16[2,512,768]{2,1,0:T(8,128)(2,1)}, u32[]{:S(2)}, u32[]{:S(2)}) async-start(bf16[2,512,768]{2,1,0:T(8,128)(2,1)} %param.12), calls=%async_computation | async-start | bytes 3145728 | tf_op jit(solution)/shard_map/all_to_all | solution.py:581
  19.2 20.9 %collective-permute-start = (bf16[1,48,1536]{2,1,0:T(8,128)(2,1)S(1)}, bf16[1,48,1536]{2,1,0:T(8,128)(2,1)S(1)}, u32[]{:S(2)}, u32[]{:S(2)}) collective-permute-start(bf16[1,48,1536]{2,1,0:T(8,128)(2,1)S(1)} %constant_dynamic-slice_fusion.21.refs_0_), channel_id=1, source_target_pairs={{0,16},{2,18},{4,20},{6,22},{8,24},{10,26},{12,28},{14,30},{16,0},... | collective-permute-start | bytes 442376 | tf_op jit(solution)/shard_map/ppermute | solution.py:590
  23.3 23.2 %collective-permute-start.1 = (bf16[1,96,768]{2,1,0:T(8,128)(2,1)S(1)}, bf16[1,96,768]{2,1,0:T(8,128)(2,1)S(1)}, u32[]{:S(2)}, u32[]{:S(2)}) collective-permute-start(bf16[1,96,768]{2,1,0:T(8,128)(2,1)S(1)} %constant_dynamic-slice_fusion.20.refs_0_), channel_id=1, source_target_pairs={{0,16},{2,18},{4,20},{6,22},{8,24},{10,26},{12,28},{14,30},{16,0},... | collective-permute-start | bytes 442376 | tf_op jit(solution)/shard_map/ppermute | solution.py:590
  47.4 16.9 %collective-permute-start.2 = (bf16[2,48,1536]{2,1,0:T(8,128)(2,1)S(1)}, bf16[2,48,1536]{2,1,0:T(8,128)(2,1)S(1)}, u32[]{:S(2)}, u32[]{:S(2)}) collective-permute-start(bf16[2,48,1536]{2,1,0:T(8,128)(2,1)S(1)} %bitcast.231), channel_id=1, source_target_pairs={{0,8},{2,10},{4,12},{6,14},{8,0},{10,2},{12,4},{14,6},{16,24},{18,... | collective-permute-start | bytes 884744 | tf_op jit(solution)/shard_map/ppermute | solution.py:590
  48.1 29.7 %collective-permute-start.3 = (bf16[2,96,768]{2,1,0:T(8,128)(2,1)S(1)}, bf16[2,96,768]{2,1,0:T(8,128)(2,1)S(1)}, u32[]{:S(2)}, u32[]{:S(2)}) collective-permute-start(bf16[2,96,768]{2,1,0:T(8,128)(2,1)S(1)} %bitcast.233), channel_id=1, source_target_pairs={{0,8},{2,10},{4,12},{6,14},{8,0},{10,2},{12,4},{14,6},{16,24},{18,... | collective-permute-start | bytes 884744 | tf_op jit(solution)/shard_map/ppermute | solution.py:590
  78.1 19.9 %collective-permute-start.4 = (bf16[4,48,1536]{2,1,0:T(8,128)(2,1)S(1)}, bf16[4,48,1536]{2,1,0:T(8,128)(2,1)S(1)}, u32[]{:S(2)}, u32[]{:S(2)}) collective-permute-start(bf16[4,48,1536]{2,1,0:T(8,128)(2,1)S(1)} %bitcast.229), channel_id=1, source_target_pairs={{0,4},{2,6},{4,0},{6,2},{8,12},{10,14},{12,8},{14,10},{16,20},{18,... | collective-permute-start | bytes 1769480 | tf_op jit(solution)/shard_map/ppermute | solution.py:590
  79.6 18.4 %collective-permute-start.5 = (bf16[4,96,768]{2,1,0:T(8,128)(2,1)S(1)}, bf16[4,96,768]{2,1,0:T(8,128)(2,1)S(1)}, u32[]{:S(2)}, u32[]{:S(2)}) collective-permute-start(bf16[4,96,768]{2,1,0:T(8,128)(2,1)S(1)} %bitcast.227), channel_id=1, source_target_pairs={{0,1},{1,0},{2,3},{3,2},{4,5},{5,4},{6,7},{7,6},{8,9},{9,8},{10,11... | collective-permute-start | bytes 1769480 | tf_op jit(solution)/shard_map/ppermute | solution.py:593
  98.3 54.6 %collective-permute-start.6 = (bf16[8,48,1536]{2,1,0:T(8,128)(2,1)S(1)}, bf16[8,48,1536]{2,1,0:T(8,128)(2,1)}, u32[]{:S(2)}, u32[]{:S(2)}) collective-permute-start(bf16[8,48,1536]{2,1,0:T(8,128)(2,1)S(1)} %bitcast.222), channel_id=1, source_target_pairs={{0,1},{1,0},{2,3},{3,2},{4,5},{5,4},{6,7},{7,6},{8,9},{9,8},{10,11... | collective-permute-start | bytes 3538952 | tf_op jit(solution)/shard_map/ppermute | solution.py:593
  98.5 54.4 %collective-permute-start.7 = (bf16[4,192,768]{2,1,0:T(8,128)(2,1)S(1)}, bf16[4,192,768]{2,1,0:T(8,128)(2,1)S(1)}, u32[]{:S(2)}, u32[]{:S(2)}) collective-permute-start(bf16[4,192,768]{2,1,0:T(8,128)(2,1)S(1)} %bitcast.225), channel_id=1, source_target_pairs={{0,4},{2,6},{4,0},{6,2},{8,12},{10,14},{12,8},{14,10},{16,20},{18,... | collective-permute-start | bytes 3538952 | tf_op jit(solution)/shard_map/ppermute | solution.py:590
  153.2 10.6 %collective-permute-start.10 = (bf16[8,192,768]{2,1,0:T(8,128)(2,1)S(1)}, bf16[8,192,768]{2,1,0:T(8,128)(2,1)}, u32[]{:S(2)}, u32[]{:S(2)}) collective-permute-start(bf16[8,192,768]{2,1,0:T(8,128)(2,1)S(1)} %bitcast.220), channel_id=1, source_target_pairs={{0,2},{2,0},{4,6},{6,4},{8,10},{10,8},{12,14},{14,12},{16,18},{18,... | collective-permute-start | bytes 7077896 | tf_op jit(solution)/shard_map/ppermute | solution.py:590
  153.3 10.5 %collective-permute-start.8 = (bf16[8,48,1536]{2,1,0:T(8,128)(2,1)S(1)}, bf16[8,48,1536]{2,1,0:T(8,128)(2,1)}, u32[]{:S(2)}, u32[]{:S(2)}) collective-permute-start(bf16[8,48,1536]{2,1,0:T(8,128)(2,1)S(1)} %bitcast.223), channel_id=1, source_target_pairs={{0,2},{2,0},{4,6},{6,4},{8,10},{10,8},{12,14},{14,12},{16,18},{18,... | collective-permute-start | bytes 3538952 | tf_op jit(solution)/shard_map/ppermute | solution.py:590
  153.8 10.0 %collective-permute-start.9 = (bf16[8,48,1536]{2,1,0:T(8,128)(2,1)}, bf16[8,48,1536]{2,1,0:T(8,128)(2,1)}, u32[]{:S(2)}, u32[]{:S(2)}) collective-permute-start(bf16[8,48,1536]{2,1,0:T(8,128)(2,1)} %collective-permute-done.6.refs_1_), channel_id=1, source_target_pairs={{0,2},{2,0},{4,6},{6,4},{8,10},{10,8},{12,14},{14,12},{16,18},{18,... | collective-permute-start | bytes 3538952 | tf_op jit(solution)/shard_map/ppermute | solution.py:590
  206.0 54.1 %all-to-all-start.2 = ((bf16[2,512,768]{2,1,0:T(8,128)(2,1)}), bf16[2,512,768]{2,1,0:T(8,128)(2,1)S(1)}, u32[]{:S(2)}, u32[]{:S(2)}) async-start(bf16[2,512,768]{2,1,0:T(8,128)(2,1)} %param.16), calls=%async_computation.2 | async-start | bytes 3145728 | tf_op jit(solution)/shard_map/all_to_all | solution.py:581
  209.8 228.7 %reduce-scatter.3.cloned.1.call-start = ((), (), s32[]{:S(2)}) async-start(), calls=%async_computation.9 | async-start | bytes 11280384 | tf_op jit(solution)/shard_map/reduce_scatter | solution.py:596
  302.2 40.7 %all-to-all-start.3 = ((bf16[2,512,768]{2,1,0:T(8,128)(2,1)}), bf16[2,512,768]{2,1,0:T(8,128)(2,1)S(1)}, u32[]{:S(2)}, u32[]{:S(2)}) async-start(bf16[2,512,768]{2,1,0:T(8,128)(2,1)} %bitcast.30), calls=%async_computation.3 | async-start | bytes 3145728 | tf_op jit(solution)/shard_map/all_to_all | solution.py:763
  305.9 215.8 %reduce-scatter.5.cloned.1.call-start = ((), (), s32[]{:S(2)}) async-start(), calls=%async_computation.10 | async-start | bytes 3760128 | tf_op jit(solution)/shard_map/reduce_scatter | solution.py:596
  366.1 9.1 %collective-permute-start.11 = (bf16[8,2,48,1536]{3,2,1,0:T(8,128)(2,1)}, bf16[8,2,48,1536]{3,2,1,0:T(8,128)(2,1)}, u32[]{:S(2)}, u32[]{:S(2)}) collective-permute-start(bf16[8,2,48,1536]{3,2,1,0:T(8,128)(2,1)} %get-tuple-element.255), channel_id=1, source_target_pairs={{0,2},{2,0},{4,6},{6,4},{8,10},{10,8},{12,14},{14,12},{16,18},{18,... | collective-permute-start | bytes 7077896 | tf_op jit(solution)/shard_map/ppermute | solution.py:590
  378.3 28.4 %collective-permute-start.12 = (bf16[2,2,2,48,1536]{4,3,2,1,0:T(8,128)(2,1)}, bf16[2,2,2,48,1536]{4,3,2,1,0:T(8,128)(2,1)S(1)}, u32[]{:S(2)}, u32[]{:S(2)}) collective-permute-start(bf16[2,2,2,48,1536]{4,3,2,1,0:T(8,128)(2,1)} %fusion.5), channel_id=1, source_target_pairs={{0,1},{1,0},{2,3},{3,2},{4,5},{5,4},{6,7},{7,6},{8,9},{9,8},{10,11... | collective-permute-start | bytes 3538952 | tf_op jit(solution)/shard_map/ppermute | solution.py:593
  422.2 5.7 collective-permute-start.13
  431.8 54.5 %collective-permute-start.15 = (bf16[2,2,2,48,1920]{4,3,2,1,0:T(8,128)(2,1)}, bf16[2,2,2,48,1920]{4,3,2,1,0:T(8,128)(2,1)S(1)}, u32[]{:S(2)}, u32[]{:S(2)}) collective-permute-start(bf16[2,2,2,48,1920]{4,3,2,1,0:T(8,128)(2,1)} %fusion.3), channel_id=1, source_target_pairs={{0,1},{1,0},{2,3},{3,2},{4,5},{5,4},{6,7},{7,6},{8,9},{9,8},{10,11... | collective-permute-start | bytes 4423688 | tf_op jit(solution)/shard_map/ppermute | solution.py:593
  437.1 49.2 %collective-permute-start.14 = (bf16[2,2,48,1536]{3,2,1,0:T(8,128)(2,1)}, bf16[2,2,48,1536]{3,2,1,0:T(8,128)(2,1)}, u32[]{:S(2)}, u32[]{:S(2)}) collective-permute-start(bf16[2,2,48,1536]{3,2,1,0:T(8,128)(2,1)} %fusion.6), channel_id=1, source_target_pairs={{0,4},{2,6},{4,0},{6,2},{8,12},{10,14},{12,8},{14,10},{16,20},{18,... | collective-permute-start | bytes 1769480 | tf_op jit(solution)/shard_map/ppermute | solution.py:590
  438.5 47.9 %collective-permute-start.16 = (bf16[48,6912]{1,0:T(8,128)(2,1)}, bf16[48,6912]{1,0:T(8,128)(2,1)}, u32[]{:S(2)}, u32[]{:S(2)}) collective-permute-start(bf16[48,6912]{1,0:T(8,128)(2,1)} %reduce-scatter.3.cloned.1.call-done), channel_id=1, source_target_pairs={{0,1},{1,0},{2,3},{3,2},{4,5},{5,4},{6,7},{7,6},{8,9},{9,8},{10,11... | collective-permute-start | bytes 1990664 | tf_op jit(solution)/shard_map/ppermute | solution.py:593
  497.0 26.6 %collective-permute-start.22 = (bf16[2,2,2,48,1152]{4,3,2,1,0:T(8,128)(2,1)}, bf16[2,2,2,48,1152]{4,3,2,1,0:T(8,128)(2,1)}, u32[]{:S(2)}, u32[]{:S(2)}) collective-permute-start(bf16[2,2,2,48,1152]{4,3,2,1,0:T(8,128)(2,1)} %fusion.7), channel_id=1, source_target_pairs={{0,1},{1,0},{2,3},{3,2},{4,5},{5,4},{6,7},{7,6},{8,9},{9,8},{10,11... | collective-permute-start | bytes 2654216 | tf_op jit(solution)/shard_map/ppermute | solution.py:593
  499.3 22.4 %collective-permute-start.21 = (bf16[2,2,48,1920]{3,2,1,0:T(8,128)(2,1)}, bf16[2,2,48,1920]{3,2,1,0:T(8,128)(2,1)S(1)}, u32[]{:S(2)}, u32[]{:S(2)}) collective-permute-start(bf16[2,2,48,1920]{3,2,1,0:T(8,128)(2,1)} %fusion.4), channel_id=1, source_target_pairs={{0,4},{2,6},{4,0},{6,2},{8,12},{10,14},{12,8},{14,10},{16,20},{18,... | collective-permute-start | bytes 2211848 | tf_op jit(solution)/shard_map/ppermute | solution.py:590
  499.8 21.8 %collective-permute-start.18 = (bf16[48,1536]{1,0:T(8,128)(2,1)}, bf16[48,1536]{1,0:T(8,128)(2,1)}, u32[]{:S(2)}, u32[]{:S(2)}) collective-permute-start(bf16[48,1536]{1,0:T(8,128)(2,1)} %get-tuple-element.306), channel_id=1, source_target_pairs={{0,8},{2,10},{4,12},{6,14},{8,0},{10,2},{12,4},{14,6},{16,24},{18,... | collective-permute-start | bytes 442376 | tf_op jit(solution)/shard_map/ppermute | solution.py:590
  502.8 18.9 %collective-permute-start.19 = (bf16[48,1536]{1,0:T(8,128)(2,1)}, bf16[48,1536]{1,0:T(8,128)(2,1)}, u32[]{:S(2)}, u32[]{:S(2)}) collective-permute-start(bf16[48,1536]{1,0:T(8,128)(2,1)} %get-tuple-element.307), channel_id=1, source_target_pairs={{0,16},{2,18},{4,20},{6,22},{8,24},{10,26},{12,28},{14,30},{16,0},... | collective-permute-start | bytes 442376 | tf_op jit(solution)/shard_map/ppermute | solution.py:590
  507.5 14.2 %collective-permute-start.20 = (bf16[48,1536]{1,0:T(8,128)(2,1)}, bf16[48,1536]{1,0:T(8,128)(2,1)}, u32[]{:S(2)}, u32[]{:S(2)}) collective-permute-start(bf16[48,1536]{1,0:T(8,128)(2,1)} %get-tuple-element.308), channel_id=1, source_target_pairs={{0,24},{2,26},{4,28},{6,30},{8,16},{10,18},{12,20},{14,22},{16,8},... | collective-permute-start | bytes 442376 | tf_op jit(solution)/shard_map/ppermute | solution.py:590
  521.7 17.4 %collective-permute-start.29 = (f32[2,2,1152]{2,1,0:T(2,128)}, f32[2,2,1152]{2,1,0:T(2,128)}, u32[]{:S(2)}, u32[]{:S(2)}) collective-permute-start(f32[2,2,1152]{2,1,0:T(2,128)} %bitcast.215), channel_id=1, source_target_pairs={{0,2},{2,0},{4,6},{6,4},{8,10},{10,8},{12,14},{14,12},{16,18},{18,... | collective-permute-start | bytes 55304 | tf_op jit(solution)/shard_map/ppermute | solution.py:590
  521.8 21.2 %collective-permute-start.30 = (f32[2,2,1152]{2,1,0:T(2,128)}, f32[2,2,1152]{2,1,0:T(2,128)S(1)}, u32[]{:S(2)}, u32[]{:S(2)}) collective-permute-start(f32[2,2,1152]{2,1,0:T(2,128)} %bitcast.214), channel_id=1, source_target_pairs={{0,4},{2,6},{4,0},{6,2},{8,12},{10,14},{12,8},{14,10},{16,20},{18,... | collective-permute-start | bytes 55304 | tf_op jit(solution)/shard_map/ppermute | solution.py:590
  521.9 21.1 %collective-permute-start.31 = (f32[2,2,1152]{2,1,0:T(2,128)}, f32[2,2,1152]{2,1,0:T(2,128)}, u32[]{:S(2)}, u32[]{:S(2)}) collective-permute-start(f32[2,2,1152]{2,1,0:T(2,128)} %bitcast.213), channel_id=1, source_target_pairs={{0,6},{2,4},{4,2},{6,0},{8,14},{10,12},{12,10},{14,8},{16,22},{18,... | collective-permute-start | bytes 55304 | tf_op jit(solution)/shard_map/ppermute | solution.py:590
  525.9 12.7 %collective-permute-start.23 = (bf16[2,2,48,1152]{3,2,1,0:T(8,128)(2,1)}, bf16[2,2,48,1152]{3,2,1,0:T(8,128)(2,1)}, u32[]{:S(2)}, u32[]{:S(2)}) collective-permute-start(bf16[2,2,48,1152]{3,2,1,0:T(8,128)(2,1)} %fusion.8), channel_id=1, source_target_pairs={{0,4},{2,6},{4,0},{6,2},{8,12},{10,14},{12,8},{14,10},{16,20},{18,... | collective-permute-start | bytes 1327112 | tf_op jit(solution)/shard_map/ppermute | solution.py:590
  530.7 27.6 %collective-permute-start.25 = (bf16[48,2304]{1,0:T(8,128)(2,1)}, bf16[48,2304]{1,0:T(8,128)(2,1)}, u32[]{:S(2)}, u32[]{:S(2)}) collective-permute-start(bf16[48,2304]{1,0:T(8,128)(2,1)} %reduce-scatter.5.cloned.1.call-done), channel_id=1, source_target_pairs={{0,1},{1,0},{2,3},{3,2},{4,5},{5,4},{6,7},{7,6},{8,9},{9,8},{10,11... | collective-permute-start | bytes 663560 | tf_op jit(solution)/shard_map/ppermute | solution.py:593
  531.0 55.5 %all-to-all-start.4 = ((bf16[2,512,768]{2,1,0:T(8,128)(2,1)}), bf16[2,512,768]{2,1,0:T(8,128)(2,1)S(1)}, u32[]{:S(2)}, u32[]{:S(2)}) async-start(bf16[2,512,768]{2,1,0:T(8,128)(2,1)} %bitcast.260), calls=%async_computation.6 | async-start | bytes 3145728 | tf_op jit(solution)/shard_map/all_to_all | solution.py:763
  538.6 19.7 %collective-permute-start.26 = (bf16[48,1920]{1,0:T(8,128)(2,1)}, bf16[48,1920]{1,0:T(8,128)(2,1)S(1)}, u32[]{:S(2)}, u32[]{:S(2)}) collective-permute-start(bf16[48,1920]{1,0:T(8,128)(2,1)} %get-tuple-element.328), channel_id=1, source_target_pairs={{0,8},{2,10},{4,12},{6,14},{8,0},{10,2},{12,4},{14,6},{16,24},{18,... | collective-permute-start | bytes 552968 | tf_op jit(solution)/shard_map/ppermute | solution.py:590
  539.1 19.2 %collective-permute-start.27 = (bf16[48,1920]{1,0:T(8,128)(2,1)}, bf16[48,1920]{1,0:T(8,128)(2,1)S(1)}, u32[]{:S(2)}, u32[]{:S(2)}) collective-permute-start(bf16[48,1920]{1,0:T(8,128)(2,1)} %get-tuple-element.329), channel_id=1, source_target_pairs={{0,16},{2,18},{4,20},{6,22},{8,24},{10,26},{12,28},{14,30},{16,0},... | collective-permute-start | bytes 552968 | tf_op jit(solution)/shard_map/ppermute | solution.py:590
  543.0 15.3 %collective-permute-start.28 = (bf16[48,1920]{1,0:T(8,128)(2,1)}, bf16[48,1920]{1,0:T(8,128)(2,1)S(1)}, u32[]{:S(2)}, u32[]{:S(2)}) collective-permute-start(bf16[48,1920]{1,0:T(8,128)(2,1)} %get-tuple-element.330), channel_id=1, source_target_pairs={{0,24},{2,26},{4,28},{6,30},{8,16},{10,18},{12,20},{14,22},{16,8},... | collective-permute-start | bytes 552968 | tf_op jit(solution)/shard_map/ppermute | solution.py:590
  543.0 15.3 %collective-permute-start.24 = (bf16[48,1536]{1,0:T(8,128)(2,1)}, bf16[48,1536]{1,0:T(8,128)(2,1)S(1)}, u32[]{:S(2)}, u32[]{:S(2)}) collective-permute-start(bf16[48,1536]{1,0:T(8,128)(2,1)} %fusion.21), channel_id=1, source_target_pairs={{0,1},{1,0},{2,3},{3,2},{4,5},{5,4},{6,7},{7,6},{8,9},{9,8},{10,11... | collective-permute-start | bytes 442376 | tf_op jit(solution)/shard_map/ppermute | solution.py:593
  561.4 7.7 %collective-permute-start.32 = (bf16[48,1152]{1,0:T(8,128)(2,1)S(1)}, bf16[48,1152]{1,0:T(8,128)(2,1)S(1)}, u32[]{:S(2)}, u32[]{:S(2)}) collective-permute-start(bf16[48,1152]{1,0:T(8,128)(2,1)S(1)} %get-tuple-element.342), channel_id=1, source_target_pairs={{0,8},{2,10},{4,12},{6,14},{8,0},{10,2},{12,4},{14,6},{16,24},{18,... | collective-permute-start | bytes 331784 | tf_op jit(solution)/shard_map/ppermute | solution.py:590
  562.9 11.2 %collective-permute-start.33 = (bf16[48,1152]{1,0:T(8,128)(2,1)S(1)}, bf16[48,1152]{1,0:T(8,128)(2,1)S(1)}, u32[]{:S(2)}, u32[]{:S(2)}) collective-permute-start(bf16[48,1152]{1,0:T(8,128)(2,1)S(1)} %get-tuple-element.343), channel_id=1, source_target_pairs={{0,16},{2,18},{4,20},{6,22},{8,24},{10,26},{12,28},{14,30},{16,0},... | collective-permute-start | bytes 331784 | tf_op jit(solution)/shard_map/ppermute | solution.py:590
  565.9 10.9 %collective-permute-start.34 = (bf16[48,1152]{1,0:T(8,128)(2,1)S(1)}, bf16[48,1152]{1,0:T(8,128)(2,1)S(1)}, u32[]{:S(2)}, u32[]{:S(2)}) collective-permute-start(bf16[48,1152]{1,0:T(8,128)(2,1)S(1)} %get-tuple-element.344), channel_id=1, source_target_pairs={{0,24},{2,26},{4,28},{6,30},{8,16},{10,18},{12,20},{14,22},{16,8},... | collective-permute-start | bytes 331784 | tf_op jit(solution)/shard_map/ppermute | solution.py:590
  565.9 13.6 %collective-permute-start.35 = (bf16[48,1920]{1,0:T(8,128)(2,1)S(1)}, bf16[48,1920]{1,0:T(8,128)(2,1)S(1)}, u32[]{:S(2)}, u32[]{:S(2)}) collective-permute-start(bf16[48,1920]{1,0:T(8,128)(2,1)S(1)} %fusion.13), channel_id=1, source_target_pairs={{0,1},{1,0},{2,3},{3,2},{4,5},{5,4},{6,7},{7,6},{8,9},{9,8},{10,11... | collective-permute-start | bytes 552968 | tf_op jit(solution)/shard_map/ppermute | solution.py:593
  566.2 12.0 %collective-permute-start.36 = (f32[1152]{0:T(1024)S(1)}, f32[1152]{0:T(1024)S(1)}, u32[]{:S(2)}, u32[]{:S(2)}) collective-permute-start(f32[1152]{0:T(1024)S(1)} %add_add_fusion.3), channel_id=1, source_target_pairs={{0,8},{2,10},{4,12},{6,14},{8,0},{10,2},{12,4},{14,6},{16,24},{18,... | collective-permute-start | bytes 13832 | tf_op jit(solution)/shard_map/ppermute | solution.py:590
  569.1 9.1 %collective-permute-start.37 = (f32[1152]{0:T(1024)S(1)}, f32[1152]{0:T(1024)S(1)}, u32[]{:S(2)}, u32[]{:S(2)}) collective-permute-start(f32[1152]{0:T(1024)S(1)} %add_add_fusion.2), channel_id=1, source_target_pairs={{0,16},{2,18},{4,20},{6,22},{8,24},{10,26},{12,28},{14,30},{16,0},... | collective-permute-start | bytes 13832 | tf_op jit(solution)/shard_map/ppermute | solution.py:590
  574.1 5.4 collective-permute-start.38
  577.9 4.8 collective-permute-start.39
  (29 other events, 234.7 us)
Sparse Core Ops, SparseCore 0:
  12.7 70.4 all-gather.4
  86.0 88.2 all-gather.6
  177.2 51.4 all-gather.8
  302.3 123.8 reduce-scatter.2
  433.6 70.6 reduce-scatter.4

commit v11 on v10

--- a/solution.py
+++ b/solution.py
@@ -240,30 +240,29 @@
     )(*operands)
 
 
-def project_kernel(hidden_ref, gains_ref, offsets_ref, weight_ref, normed_ref, packed_ref):
+def project_kernel(hidden_ref, rows_ref, weight_ref, normed_ref, packed_ref, *, gain, shift):
     features = hidden_ref.shape[1]
     normal, _ = normal_of(hidden_ref[...])
-    normed = (normal * gains_ref[0:1] + offsets_ref[0:1]).astype(half)
+    normed = (normal * rows_ref[gain : gain + 1] + rows_ref[shift : shift + 1]).astype(half)
     normed_ref[...] = normed
     for part in range(3):
         window = slice(part * features, (part + 1) * features)
         product = contract(normed, weight_ref[:, window], 1, 0)
         if part != 1:
-            row = 1 if part == 0 else 2
-            product = product + offsets_ref[row : row + 1]
+            row = shift + (1 if part == 0 else 2)
+            product = product + rows_ref[row : row + 1]
         packed_ref[:, window] = product.astype(half)
 
 
-def project(hidden, gains, offsets, joined):
+def project(hidden, rows, gain, shift, joined):
     length, features = hidden.shape
     return row_tiled(
-        project_kernel,
+        functools.partial(project_kernel, gain=gain, shift=shift),
         "project",
         length,
         [
             tile_of(features),
-            resident(gains.shape),
-            resident(offsets.shape),
+            resident(rows.shape),
             resident((features, 3 * features)),
         ],
         [tile_of(features), tile_of(3 * features)],
@@ -271,7 +270,7 @@
             jax.ShapeDtypeStruct((length, features), half),
             jax.ShapeDtypeStruct((length, 3 * features), half),
         ],
-        (hidden, gains, offsets, joined),
+        (hidden, rows, joined),
         6 * length * features * features,
     )
 
@@ -279,8 +278,7 @@
 def feed_kernel(
     attended_ref,
     hidden_ref,
-    gains_ref,
-    offsets_ref,
+    rows_ref,
     up_bias_ref,
     out_weight_ref,
     up_ref,
@@ -290,16 +288,20 @@
     activated_ref,
     slope_ref,
     result_ref,
+    *,
+    gain,
+    shift,
 ):
     hidden_units = up_ref.shape[1]
     middle = hidden_ref[...] + (
-        contract(attended_ref[...], out_weight_ref[...], 1, 0) + offsets_ref[3:4]
+        contract(attended_ref[...], out_weight_ref[...], 1, 0) + rows_ref[shift + 3 : shift + 4]
     )
     middle_ref[...] = middle
     normal, _ = normal_of(middle)
-    second = (normal * gains_ref[1:2] + offsets_ref[4:5]).astype(half)
+    second = normal * rows_ref[gain + 1 : gain + 2] + rows_ref[shift + 4 : shift + 5]
+    second = second.astype(half)
     second_ref[...] = second
-    result = middle + offsets_ref[5:6]
+    result = middle + rows_ref[shift + 5 : shift + 6]
     rate = 0.7978845608028654
     for start in range(0, hidden_units, FF_CHUNK):
         window = slice(start, start + FF_CHUNK)
@@ -315,20 +317,19 @@
     result_ref[...] = result.astype(result_ref.dtype)
 
 
-def feed(attended, hidden, gains, offsets, up_bias, joined, up, down, result_type):
+def feed(attended, hidden, rows, gain, shift, up_bias, joined, up, down, result_type):
     length, features = hidden.shape
     units = down.shape[0]
     up_array, up_place = up
     shape = jax.ShapeDtypeStruct
     return row_tiled(
-        feed_kernel,
+        functools.partial(feed_kernel, gain=gain, shift=shift),
         "feed",
         length,
         [
             tile_of(features),
             tile_of(features),
-            resident(gains.shape),
-            resident(offsets.shape),
+            resident(rows.shape),
             resident(up_bias.shape),
             resident((features, features), 0, 3),
             resident((features, units), 0, up_place),
@@ -342,7 +343,7 @@
             shape((length, units), half),
             shape((length, features), result_type),
         ],
-        (attended, hidden, gains, offsets, up_bias, joined, up_array, down),
+        (attended, hidden, rows, up_bias, joined, up_array, down),
         2 * length * features * (features + 2 * units),
     )
 
@@ -351,7 +352,7 @@
     gradient_ref,
     slope_ref,
     middle_ref,
-    gains_ref,
+    rows_ref,
     out_weight_ref,
     up_ref,
     down_ref,
@@ -362,6 +363,8 @@
     upstream_ref,
     sums_ref,
     unit_sums_ref,
+    *,
+    gain,
 ):
     units = up_ref.shape[1]
 
@@ -383,7 +386,9 @@
         unit_sums_ref[:, window] += column_sum(upper.astype(single))
         second_grad = second_grad + contract(upper, up_ref[:, window], 1, 1)
     normal, inverse = normal_of(middle_ref[...])
-    middle_grad = gradient + norm_pull(normal, inverse, gains_ref[1:2], second_grad)
+    middle_grad = gradient + norm_pull(
+        normal, inverse, rows_ref[gain + 1 : gain + 2], second_grad
+    )
     sums_ref[1:2] += column_sum(second_grad * normal)
     sums_ref[2:3] += column_sum(second_grad)
     middle_grad_ref[...] = middle_grad
@@ -393,20 +398,20 @@
     upstream_ref[...] = contract(attention_grad, out_weight_ref[...], 1, 1).astype(half)
 
 
-def feed_grad(gradient, slope, middle, gains, joined, up, down):
+def feed_grad(gradient, slope, middle, rows, gain, joined, up, down):
     up_array, up_place = up
     length, features = middle.shape
     units = down.shape[0]
     shape = jax.ShapeDtypeStruct
     return row_tiled(
-        feed_grad_kernel,
+        functools.partial(feed_grad_kernel, gain=gain),
         "feed_grad",
         length,
         [
             tile_of(features),
             tile_of(units),
             tile_of(features),
-            resident(gains.shape),
+            resident(rows.shape),
             resident((features, features), 0, 3),
             resident((features, units), 0, up_place),
             resident(down.shape),
@@ -429,13 +434,13 @@
             shape((8, features), single),
             shape((1, units), single),
         ],
-        (gradient, slope, middle, gains, joined, up_array, down),
+        (gradient, slope, middle, rows, joined, up_array, down),
         2 * length * features * (features + 2 * units),
     )
 
 
 def project_grad_kernel(
-    packed_grad_ref, hidden_ref, middle_grad_ref, gains_ref, weight_ref, *out_refs
+    packed_grad_ref, hidden_ref, middle_grad_ref, rows_ref, weight_ref, *out_refs, gain
 ):
     sums_ref = out_refs[-1]
     features = hidden_ref.shape[1]
@@ -447,7 +452,9 @@
     packed_grad = packed_grad_ref[...]
     normed_grad = contract(packed_grad, weight_ref[...], 1, 1)
     normal, inverse = normal_of(hidden_ref[...])
-    result = middle_grad_ref[...] + norm_pull(normal, inverse, gains_ref[0:1], normed_grad)
+    result = middle_grad_ref[...] + norm_pull(
+        normal, inverse, rows_ref[gain : gain + 1], normed_grad
+    )
     for result_ref in out_refs[:-1]:
         result_ref[...] = result.astype(result_ref.dtype)
     sums_ref[0:1] += column_sum(normed_grad * normal)
@@ -456,24 +463,24 @@
     sums_ref[3:4] += column_sum(packed_grad[:, 2 * features :].astype(single))
 
 
-def project_grad(packed_grad, hidden, middle_grad, gains, joined, result_types):
+def project_grad(packed_grad, hidden, middle_grad, rows, gain, joined, result_types):
     length, features = hidden.shape
     shape = jax.ShapeDtypeStruct
     return row_tiled(
-        project_grad_kernel,
+        functools.partial(project_grad_kernel, gain=gain),
         "project_grad",
         length,
         [
             tile_of(3 * features),
             tile_of(features),
             tile_of(features),
-            resident(gains.shape),
+            resident(rows.shape),
             resident((features, 3 * features)),
         ],
         [tile_of(features) for _ in result_types] + [resident((8, features))],
         [shape((length, features), result_type) for result_type in result_types]
         + [shape((8, features), single)],
-        (packed_grad, hidden, middle_grad, gains, joined),
+        (packed_grad, hidden, middle_grad, rows, joined),
         6 * length * features * features,
     )
 
@@ -682,12 +689,17 @@
 
     my_tokens = whole_sequence(tokens)
 
+    gain_count = layers * norm_gains.shape[1]
+    row_count = gain_count + layers * bias_rows.shape[1]
+    up_pieces = up_bias.shape[1] // row_unit
     small = jnp.concatenate(
-        [norm_gains.reshape(-1), bias_rows.reshape(-1), up_bias.reshape(-1)]
-    )
-    side = small.reshape(row_unit, -1)
-    side_width = side.shape[1]
-    side = jnp.pad(side, ((0, 0), (0, -side_width % PAIR)))
+        [
+            norm_gains.reshape(gain_count, row_unit),
+            bias_rows.reshape(row_count - gain_count, row_unit),
+            up_bias.reshape(layers * up_pieces, row_unit),
+        ]
+    )
+    side = jnp.pad(small.T, ((0, 0), (0, -small.shape[0] % PAIR)))
     joined_parts = [jnp.concatenate([qkv_weight[0], out_weight[0], side], axis=1)]
     for layer in range(1, layers):
         parts = [qkv_weight[layer], out_weight[layer], up_weight[layer]]
@@ -697,18 +709,14 @@
         layer: lax.all_gather(down_weight[layer], "wide", axis=0, tiled=True)
         for layer in range(1, layers)
     }
-    small_whole = joined[0][:, -side.shape[1] :][:, :side_width].reshape(groups, -1)
+    rows = joined[0][:, -side.shape[1] :].T.astype(single)
+    spread_bias = rows[row_count : row_count + layers * up_pieces]
+    spread_bias = spread_bias.reshape(layers, up_pieces, groups, row_unit).swapaxes(1, 2)
+    all_up_bias = spread_bias.reshape(layers, 1, -1)
     cut_gains = norm_gains.size
     cut_rows = cut_gains + bias_rows.size
-
-    def whole_rows(part, count):
-        parts = part.reshape(groups, layers, count, -1)
-        return parts.transpose(1, 2, 0, 3).reshape(layers, count, -1).astype(single)
-
-    all_gains = whole_rows(small_whole[:, :cut_gains], norm_gains.shape[1])
-    all_offsets = whole_rows(small_whole[:, cut_gains:cut_rows], bias_rows.shape[1])
-    all_up_bias = whole_rows(small_whole[:, cut_rows:], 1)[:, 0]
-
+    gain_row = lambda layer: layer * norm_gains.shape[1]
+    shift_row = lambda layer: gain_count + layer * bias_rows.shape[1]
     matrices = [None] * layers
     ups = {}
     fetches = [
@@ -716,9 +724,10 @@
         begin(gather_rows(down_weight[0]), functools.partial(downs.__setitem__, 0)),
     ]
     marks = jnp.stack([segment_ids, pad_mask], axis=2)
-    for _ in chip_bits[1:]:
+    time_embed, marks = advance((time_embed, marks), *fetches)
+    marks = whole_sequence(marks)
+    for _ in chip_bits[2:]:
         time_embed, marks = advance((time_embed, marks), *fetches)
-    marks = whole_sequence(marks)
     doc, pad = marks[:, 0], marks[:, 1]
     positions = jnp.arange(doc.shape[0])
     allowed = (doc[:, None] == doc[None, :]) & (
@@ -731,9 +740,8 @@
     saved = []
     for layer in range(layers):
         whole = joined[layer]
-        gains, offsets = all_gains[layer], all_offsets[layer]
         before = hidden
-        normed, packed = project(hidden, gains, offsets, whole)
+        normed, packed = project(hidden, rows, gain_row(layer), shift_row(layer), whole)
         if layer == layers - 1:
             packed, out_grad = lax.optimization_barrier((packed, out_grad))
             my_upstream = whole_sequence(out_grad)
@@ -748,9 +756,10 @@
         middle, second, activated, slope, hidden = feed(
             attended,
             hidden,
-            gains,
-            offsets,
-            all_up_bias[layer][None],
+            rows,
+            gain_row(layer),
+            shift_row(layer),
+            all_up_bias[layer],
             whole,
             up,
             downs[layer],
@@ -855,11 +864,10 @@
     held = []
     for layer in range(layers - 1, -1, -1):
         whole, up, down = matrices[layer]
-        gains = all_gains[layer]
         hidden, normed, packed, totals, attended, middle, second, activated, slope = saved[layer]
         steps = scatter_group if layer else reduce_group
         branch, upper, middle_grad, attention_grad, upstream, sums, unit_sums = feed_grad(
-            gradient, slope, middle, gains, whole, up, down
+            gradient, slope, middle, rows, gain_row(layer), whole, up, down
         )
         named = [(2, (second, upper)), (1, (attended, attention_grad))]
         if layer:
@@ -886,7 +894,13 @@
             packed_grad = launch(packed_grad, [last_group])
             packed_grad = advance(packed_grad, last_group)
         gradient, *rounded, more_sums = project_grad(
-            packed_grad, hidden, middle_grad, gains, whole, (single, half) if layer else (half,)
+            packed_grad,
+            hidden,
+            middle_grad,
+            rows,
+            gain_row(layer),
+            whole,
+            (single, half) if layer else (half,),
         )
         if layer == 1:
             below = (saved[0][7], rounded[0])

time: 601 us -> 605 us (level)
  blocking collectives: 25.1 us -> 6.45 us
  waiting for transfers between devices: 86.1 us -> 102 us
  Pallas kernels: 323 us -> 336 us
  starting transfers between devices: 63.7 us -> 56.5 us
    all_to_all x1, blocking collectives: 25.1 us -> 6.45 us  [whole_sequence(): lax.all_to_all(part, 'seq', split_axis=0, concat_axis=1, tiled=True)[0]]
    pallas_call x8, Pallas kernels: 130 us -> 141 us  [row_tiled(): pl.pallas_call(kernel, grid=(length // ROW_TILE,), in_specs=in_specs, out...]
    all_gather x1, waiting for transfers between devices: 0.01 us -> 10.8 us  [per_device(): lax.all_gather(down_weight[layer], 'wide', axis=0, tiled=True)]
    ppermute x30, starting transfers between devices: 38.2 us -> 31.4 us  [across(): return lambda part: lax.ppermute(part, 'wide', pairs)]
  transfers between devices with their start and end apart: 50 -> 50, of which waited for: 13 -> 14; matrix products, arithmetic and copies ran while one was open for 11% -> 11% of each run, Pallas kernels for 47% -> 48%
where the time goes in v11:
time: 605 us; the launch traced here: 594 us
  Pallas kernels  336 us (56%)
  waiting for transfers between devices  102 us (17%)
  starting transfers between devices  56.5 us (9%)
  other arithmetic  46.6 us (8%)
  local copies, waits for them, and re-layouts  31.6 us (5%)
  between operations  15.1 us (2%)
  blocking collectives  6.45 us (1%)
    pallas_call x8, Pallas kernels, row_tiled(): pl.pallas_call(kernel, grid=(length // ROW_TILE,), in_specs=in_specs, out...  141 us
    pallas_call x2, Pallas kernels, attend_backward(): pl.pallas_call(functools.partial(attend_grad_kernel, rows=BACKWARD_ROWS),...  74.7 us
    ppermute x30, waiting for transfers between devices, across(): return lambda part: lax.ppermute(part, 'wide', pairs)  70.6 us
    pallas_call x5, Pallas kernels, term_blocks(): pl.pallas_call(kernel, in_specs=[pl.BlockSpec(memory_space=pltpu.SMEM)] +...  63 us
    pallas_call x2, Pallas kernels, attend_forward(): pl.pallas_call(functools.partial(attend_kernel, rows=FORWARD_ROWS), grid=...  50.4 us
    ppermute x30, starting transfers between devices, across(): return lambda part: lax.ppermute(part, 'wide', pairs)  31.4 us
    ppermute x11, waiting for transfers between devices, beside_seq(): return lax.ppermute(part, 'seq', swap)  21 us
    convert_element_type x6, other arithmetic, reduce_group(): total_of([side_of(part, 1 - mine, axis) for part in addends]).astype(half)  15.8 us
  transfers between devices with their start and end apart: 50, of which 14 were waited for; matrix products, arithmetic and copies ran while one was open for 11% of the time, Pallas kernels for 48%

profile of v11, /device:TPU:0, one launch (start us, length us, event | category | flops | bytes accessed | tf_op | source)
XLA Modules:
  0.0 594.3 jit_solution(16520520798723993464)
XLA Ops:
  14.6 4.1 collective-permute-start
  18.8 15.7 %collective-permute-done.refs_1_ = bf16[1,48,1536]{2,1,0:T(8,128)(2,1)S(1)} collective-permute-done((bf16[1,48,1536]{2,1,0:T(8,128)(2,1)S(1)}, bf16[1,48,1536]{2,1,0:T(8,128)(2,1)S(1)}, u32[]{:S(2)}, u32[]{:S(2)}) %collective-permute-start) | collective-permute-done | bytes 147488 | tf_op jit(solution)/shard_map/ppermute | solution.py:597
  34.5 7.5 %collective-permute-done.1.refs_1_ = bf16[1,96,768]{2,1,0:T(8,128)(2,1)S(1)} collective-permute-done((bf16[1,96,768]{2,1,0:T(8,128)(2,1)S(1)}, bf16[1,96,768]{2,1,0:T(8,128)(2,1)S(1)}, u32[]{:S(2)}, u32[]{:S(2)}) %collective-permute-start.1) | collective-permute-done | bytes 147488 | tf_op jit(solution)/shard_map/ppermute | solution.py:597
  42.8 6.4 %all_to_all.37 = s32[2,512,2]{1,2,0:T(2,128)S(1)} all-to-all(s32[2,512,2]{1,2,0:T(2,128)S(1)} %pad_add_fusion), channel_id=1, replica_groups=mesh['wide'=16,'seq'=2] {'seq'}, dimensions={0} | all-to-all | bytes 16384 | tf_op jit(solution)/shard_map/all_to_all | solution.py:588
  49.2 4.7 all-to-all-start
  56.0 20.2 %collective-permute-done.2.refs_1_ = bf16[2,48,1536]{2,1,0:T(8,128)(2,1)S(1)} collective-permute-done((bf16[2,48,1536]{2,1,0:T(8,128)(2,1)S(1)}, bf16[2,48,1536]{2,1,0:T(8,128)(2,1)S(1)}, u32[]{:S(2)}, u32[]{:S(2)}) %collective-permute-start.2) | collective-permute-done | bytes 294944 | tf_op jit(solution)/shard_map/ppermute | solution.py:597
  76.1 5.9 collective-permute-done.3.refs_1_
  85.3 3.3 convert_add_fusion.hidden_ref
  90.5 9.1 %project.2 = (bf16[1024,768]{1,0:T(8,128)(2,1)}, bf16[1024,2304]{1,0:T(8,128)(2,1)}) custom-call(f32[1024,768]{1,0:T(8,128)} %convert_add_fusion.hidden_ref, f32[128,768]{1,0:T(8,128)} %copy.88.rows_ref, bf16[768,3200]{1,0:T(8,128)(2,1)} %all-gather.5.cloned.1.call-done.weight_ref.out_weight_ref), custom_call_target="tpu_custom_call" | custom-call | flops 226492416 | bytes 921600 | tf_op jit(solution)/shard_map/project/pallas_call | solution.py:231
  101.3 2.8 fusion.2.bias_ref
  104.1 25.2 %attend_forward.2 = (bf16[1024,768]{1,0:T(8,128)(2,1)}, f32[6,2,1024]{2,1,0:T(2,128)}) custom-call(bf16[1024,2304]{1,0:T(8,128)(2,1)} %get-tuple-element.213.query_ref.key_ref.value_ref, bf16[1024,2304]{1,0:T(8,128)(2,1)} %get-tuple-element.213.query_ref.key_ref.value_ref, bf16[1024,2304]{1,0:T(8,128)(2,1)} %get-tuple-element.213.query_ref.key_ref.value_ref, ...), custom_call_target="tpu_custom_call" | custom-call | flops 805306368 | bytes 393216 | tf_op jit(solution)/shard_map/attend_forward/pallas_call | solution.py:68
  129.3 4.9 collective-permute-done.7.refs_1_
  147.8 2.8 place_pieces.16
  150.5 2.3 copy-done.3
  152.8 24.6 %feed.2 = (f32[1024,768]{1,0:T(8,128)}, bf16[1024,768]{1,0:T(8,128)(2,1)}, bf16[1024,3072]{1,0:T(8,128)(2,1)}, bf16[1024,3072]{1,0:T(8,128)(2,1)}, f32[1024,768]{1,0:T(8,128)}) custom-call(bf16[1024,768]{1,0:T(8,128)(2,1)} %get-tuple-element.225.attended_ref.refs_2_, f32[1024,768]{1,0:T(8,128)} %convert_add_fusion.hidden_ref, f32[128,768]{1,0:T(8,128)} %copy.88.rows_ref, ...), custom_call_target="tpu_custom_call" | custom-call | flops 679477248 | bytes 2495232 | tf_op jit(solution)/shard_map/feed/pallas_call | solution.py:231
  177.4 9.3 %project.3 = (bf16[1024,768]{1,0:T(8,128)(2,1)}, bf16[1024,2304]{1,0:T(8,128)(2,1)}) custom-call(f32[1024,768]{1,0:T(8,128)} %get-tuple-element.229.hidden_ref, f32[128,768]{1,0:T(8,128)} %copy.88.rows_ref, bf16[768,6144]{1,0:T(8,128)(2,1)} %all-gather.7.cloned.1.call-done.weight_ref.out_weight_ref.up_ref), custom_call_target="tpu_custom_call" | custom-call | flops 226492416 | bytes 1204224 | tf_op jit(solution)/shard_map/project/pallas_call | solution.py:231
  186.7 3.8 all-to-all-start.2
  191.3 25.2 %attend_forward.3 = (bf16[1024,768]{1,0:T(8,128)(2,1)}, f32[6,2,1024]{2,1,0:T(2,128)}) custom-call(bf16[1024,2304]{1,0:T(8,128)(2,1)} %get-tuple-element.231.query_ref.key_ref.value_ref, bf16[1024,2304]{1,0:T(8,128)(2,1)} %get-tuple-element.231.query_ref.key_ref.value_ref, bf16[1024,2304]{1,0:T(8,128)(2,1)} %get-tuple-element.231.query_ref.key_ref.value_ref, ...), custom_call_target="tpu_custom_call" | custom-call | flops 805306368 | bytes 393216 | tf_op jit(solution)/shard_map/attend_forward/pallas_call | solution.py:68
  216.5 10.8 %all-gather.9.cloned.1.call-done = bf16[1,3072,768]{2,1,0:T(8,128)(2,1)} async-done(((bf16[1,192,768]{2,1,0:T(8,128)(2,1)}), bf16[1,3072,768]{2,1,0:T(8,128)(2,1)}) %all-gather.9.cloned.1.call-update) | async-done | bytes 4718608 | tf_op jit(solution)/shard_map/all_gather | solution.py:709
  227.3 24.1 %feed.3 = (f32[1024,768]{1,0:T(8,128)}, bf16[1024,768]{1,0:T(8,128)(2,1)}, bf16[1024,3072]{1,0:T(8,128)(2,1)}, bf16[1024,3072]{1,0:T(8,128)(2,1)}, bf16[1024,768]{1,0:T(8,128)(2,1)}) custom-call(bf16[1024,768]{1,0:T(8,128)(2,1)} %get-tuple-element.233.attended_ref.refs_4_, f32[1024,768]{1,0:T(8,128)} %get-tuple-element.229.hidden_ref, ...), custom_call_target="tpu_custom_call" | custom-call | flops 679477248 | bytes 2974464 | tf_op jit(solution)/shard_map/feed/pallas_call | solution.py:231
  252.5 31.8 %feed_grad.2 = (bf16[1024,768]{1,0:T(8,128)(2,1)}, bf16[1024,3072]{1,0:T(8,128)(2,1)}, f32[1024,768]{1,0:T(8,128)}, bf16[1024,768]{1,0:T(8,128)(2,1)}, bf16[1024...) custom-call(bf16[1024,768]{1,0:T(8,128)(2,1)} %bitcast.226, ...), custom_call_target="tpu_custom_call" | custom-call | flops 679477248 | bytes 3074304 | tf_op jit(solution)/shard_map/feed_grad/pallas_call | solution.py:231
  284.4 19.7 %term_blocks.5 = bf16[16,48,6912]{2,1,0:T(8,128)(2,1)} custom-call(s32[1]{0:T(128)} %bitcast.21.core_ref, bf16[1024,3072]{1,0:T(8,128)(2,1)} %get-tuple-element.237.refs_0_, bf16[1024,768]{1,0:T(8,128)(2,1)} %get-tuple-element.238.refs_1_, bf16[1024,768]{1,0:T(8,128)(2,1)} %get-tuple-element.239.refs_2_, bf16[1024,3072]{1,0:T(8,128)(2,1)} %get-tuple-element.240.refs_3_, ...), custom_call_target="tpu_custom_call" | custom-call | flops 679477248 | bytes 1843200 | tf_op jit(solution)/shard_map/term_blocks/pallas_call | solution.py:555
  304.1 3.7 all-to-all-start.3
  307.9 37.3 %attend_backward.2.packed_grad_ref.refs_1_ = bf16[1024,2304]{1,0:T(8,128)(2,1)} custom-call(bf16[1024,2304]{1,0:T(8,128)(2,1)} %get-tuple-element.231.query_ref.key_ref.value_ref, bf16[1024,2304]{1,0:T(8,128)(2,1)} %get-tuple-element.231.query_ref.key_ref.value_ref, bf16[1024,2304]{1,0:T(8,128)(2,1)} %get-tuple-element.231.query_ref.key_ref.value_ref, ...), custom_call_target="tpu_custom_call" | custom-call | flops 2013265920 | bytes 786432 | tf_op jit(solution)/shard_map/attend_backward/pallas_call | solution.py:151
  345.2 11.1 %project_grad.2 = (f32[1024,768]{1,0:T(8,128)}, bf16[1024,768]{1,0:T(8,128)(2,1)}, f32[8,768]{1,0:T(8,128)}) custom-call(bf16[1024,2304]{1,0:T(8,128)(2,1)} %attend_backward.2.packed_grad_ref.refs_1_, f32[1024,768]{1,0:T(8,128)} %get-tuple-element.229.hidden_ref, f32[1024,768]{1,0:T(8,128)} %get-tuple-element.247.middle_grad_ref, f32[128,768]{1,0:T(8,128)} %copy.88.rows_ref, ...), custom_call_target="tpu_custom_call" | custom-call | flops 226492416 | bytes 1598976 | tf_op jit(solution)/shard_map/project_grad/pallas_call | solution.py:231
  356.2 12.2 %term_blocks.6 = (bf16[8,2,48,1536]{3,2,1,0:T(8,128)(2,1)}, bf16[8,2,48,1536]{3,2,1,0:T(8,128)(2,1)}) custom-call(s32[1]{0:T(128)} %bitcast.21.core_ref, bf16[1024,3072]{1,0:T(8,128)(2,1)} %get-tuple-element.249.refs_0_, bf16[1024,768]{1,0:T(8,128)(2,1)} %get-tuple-element.250.refs_1_), custom_call_target="tpu_custom_call" | custom-call | flops 301989888 | bytes 786432 | tf_op jit(solution)/shard_map/term_blocks/pallas_call | solution.py:555
  368.9 8.6 %term_blocks.7 = bf16[16,48,2304]{2,1,0:T(8,128)(2,1)} custom-call(s32[1]{0:T(128)} %bitcast.21.core_ref, bf16[1024,768]{1,0:T(8,128)(2,1)} %get-tuple-element.253.refs_0_, bf16[1024,2304]{1,0:T(8,128)(2,1)} %attend_backward.2.packed_grad_ref.refs_1_), custom_call_target="tpu_custom_call" | custom-call | flops 226492416 | bytes 614400 | tf_op jit(solution)/shard_map/term_blocks/pallas_call | solution.py:555
  377.4 3.0 fusion.5
  382.1 21.3 %feed_grad.3 = (bf16[1024,768]{1,0:T(8,128)(2,1)}, bf16[1024,3072]{1,0:T(8,128)(2,1)}, f32[1024,768]{1,0:T(8,128)}, bf16[1024,768]{1,0:T(8,128)(2,1)}, bf16[1024...) custom-call(f32[1024,768]{1,0:T(8,128)} %get-tuple-element.259.gradient_ref, ...), custom_call_target="tpu_custom_call" | custom-call | flops 679477248 | bytes 2595072 | tf_op jit(solution)/shard_map/feed_grad/pallas_call | solution.py:231
  403.4 5.5 collective-permute-done.12
  408.9 2.8 fusion.6
  411.7 12.8 %term_blocks.8 = (bf16[8,2,48,1920]{3,2,1,0:T(8,128)(2,1)}, bf16[8,2,48,1920]{3,2,1,0:T(8,128)(2,1)}) custom-call(s32[1]{0:T(128)} %bitcast.21.core_ref, bf16[1024,768]{1,0:T(8,128)(2,1)} %get-tuple-element.270.refs_0_, bf16[1024,3072]{1,0:T(8,128)(2,1)} %get-tuple-element.271.refs_1_, bf16[1024,768]{1,0:T(8,128)(2,1)} %get-tuple-element.225.attended_ref.refs_2_, ...), custom_call_target="tpu_custom_call" | custom-call | flops 377487360 | bytes 1056768 | tf_op jit(solution)/shard_map/term_blocks/pallas_call | solution.py:555
  424.6 5.6 collective-permute-done.13
  430.2 3.9 fusion.3
  440.7 37.4 %attend_backward.3.refs_1_.packed_grad_ref = bf16[1024,2304]{1,0:T(8,128)(2,1)} custom-call(bf16[1024,2304]{1,0:T(8,128)(2,1)} %get-tuple-element.213.query_ref.key_ref.value_ref, bf16[1024,2304]{1,0:T(8,128)(2,1)} %get-tuple-element.213.query_ref.key_ref.value_ref, bf16[1024,2304]{1,0:T(8,128)(2,1)} %get-tuple-element.213.query_ref.key_ref.value_ref, ...), custom_call_target="tpu_custom_call" | custom-call | flops 2013265920 | bytes 786432 | tf_op jit(solution)/shard_map/attend_backward/pallas_call | solution.py:151
  478.2 9.8 %term_blocks.9 = (bf16[8,2,48,1152]{3,2,1,0:T(8,128)(2,1)}, bf16[8,2,48,1152]{3,2,1,0:T(8,128)(2,1)}) custom-call(s32[1]{0:T(128)} %bitcast.21.core_ref, bf16[1024,768]{1,0:T(8,128)(2,1)} %get-tuple-element.290.refs_0_, bf16[1024,2304]{1,0:T(8,128)(2,1)} %attend_backward.3.refs_1_.packed_grad_ref), custom_call_target="tpu_custom_call" | custom-call | flops 226492416 | bytes 614400 | tf_op jit(solution)/shard_map/term_blocks/pallas_call | solution.py:555
  488.0 2.8 fusion.22
  490.8 2.6 fusion.4
  495.0 2.3 collective-permute-done.17
  506.7 10.1 %project_grad.3 = (bf16[1024,768]{1,0:T(8,128)(2,1)}, f32[8,768]{1,0:T(8,128)}) custom-call(bf16[1024,2304]{1,0:T(8,128)(2,1)} %attend_backward.3.refs_1_.packed_grad_ref, f32[1024,768]{1,0:T(8,128)} %convert_add_fusion.hidden_ref, f32[1024,768]{1,0:T(8,128)} %get-tuple-element.298.middle_grad_ref, f32[128,768]{1,0:T(8,128)} %copy.88.rows_ref, ...), custom_call_target="tpu_custom_call" | custom-call | flops 226492416 | bytes 1119744 | tf_op jit(solution)/shard_map/project_grad/pallas_call | solution.py:231
  522.9 2.2 fusion.8
  527.8 2.5 fusion.14
  530.7 3.7 all-to-all-start.4
  534.4 3.4 collective-permute-done.23
  544.1 13.9 %collective-permute-done.24 = bf16[48,1536]{1,0:T(8,128)(2,1)S(1)} collective-permute-done((bf16[48,1536]{1,0:T(8,128)(2,1)}, bf16[48,1536]{1,0:T(8,128)(2,1)S(1)}, u32[]{:S(2)}, u32[]{:S(2)}) %collective-permute-start.24) | collective-permute-done | bytes 147488 | tf_op jit(solution)/shard_map/ppermute | solution.py:600
  563.3 2.2 collective-permute-start.34
  570.3 2.7 collective-permute-done.33
  576.0 2.4 collective-permute-done.38
  (253 shorter events, 89.4 us)
Async XLA Ops:
  7.2 81.4 %all-gather.5.cloned.1.call-start = ((), (), s32[]{:S(2)}) async-start(), calls=%async_computation.7 | async-start | bytes 5222400 | tf_op jit(solution)/shard_map/all_gather | solution.py:707
  12.6 164.8 %all-gather.7.cloned.1.call-start = ((), (), s32[]{:S(2)}) async-start(), calls=%async_computation.8 | async-start | bytes 10027008 | tf_op jit(solution)/shard_map/all_gather | solution.py:707
  13.6 213.7 %all-gather.9.cloned.1.call-start = ((), (), s32[]{:S(2)}) async-start(), calls=%async_computation.11 | async-start | bytes 5013504 | tf_op jit(solution)/shard_map/all_gather | solution.py:709
  14.6 19.9 %collective-permute-start = (bf16[1,48,1536]{2,1,0:T(8,128)(2,1)S(1)}, bf16[1,48,1536]{2,1,0:T(8,128)(2,1)S(1)}, u32[]{:S(2)}, u32[]{:S(2)}) collective-permute-start(bf16[1,48,1536]{2,1,0:T(8,128)(2,1)S(1)} %constant_dynamic-slice_fusion.21.refs_0_), channel_id=1, source_target_pairs={{0,16},{2,18},{4,20},{6,22},{8,24},{10,26},{12,28},{14,30},{16,0},... | collective-permute-start | bytes 442376 | tf_op jit(solution)/shard_map/ppermute | solution.py:597
  18.7 23.3 %collective-permute-start.1 = (bf16[1,96,768]{2,1,0:T(8,128)(2,1)S(1)}, bf16[1,96,768]{2,1,0:T(8,128)(2,1)S(1)}, u32[]{:S(2)}, u32[]{:S(2)}) collective-permute-start(bf16[1,96,768]{2,1,0:T(8,128)(2,1)S(1)} %constant_dynamic-slice_fusion.20.refs_0_), channel_id=1, source_target_pairs={{0,16},{2,18},{4,20},{6,22},{8,24},{10,26},{12,28},{14,30},{16,0},... | collective-permute-start | bytes 442376 | tf_op jit(solution)/shard_map/ppermute | solution.py:597
  49.2 36.1 %all-to-all-start = ((bf16[2,512,768]{2,1,0:T(8,128)(2,1)}), bf16[2,512,768]{2,1,0:T(8,128)(2,1)}, u32[]{:S(2)}, u32[]{:S(2)}) async-start(bf16[2,512,768]{2,1,0:T(8,128)(2,1)} %param.12), calls=%async_computation | async-start | bytes 3145728 | tf_op jit(solution)/shard_map/all_to_all | solution.py:588
  53.9 22.3 %collective-permute-start.2 = (bf16[2,48,1536]{2,1,0:T(8,128)(2,1)S(1)}, bf16[2,48,1536]{2,1,0:T(8,128)(2,1)S(1)}, u32[]{:S(2)}, u32[]{:S(2)}) collective-permute-start(bf16[2,48,1536]{2,1,0:T(8,128)(2,1)S(1)} %bitcast.218), channel_id=1, source_target_pairs={{0,8},{2,10},{4,12},{6,14},{8,0},{10,2},{12,4},{14,6},{16,24},{18,... | collective-permute-start | bytes 884744 | tf_op jit(solution)/shard_map/ppermute | solution.py:597
  54.5 27.5 %collective-permute-start.3 = (bf16[2,96,768]{2,1,0:T(8,128)(2,1)S(1)}, bf16[2,96,768]{2,1,0:T(8,128)(2,1)S(1)}, u32[]{:S(2)}, u32[]{:S(2)}) collective-permute-start(bf16[2,96,768]{2,1,0:T(8,128)(2,1)S(1)} %bitcast.220), channel_id=1, source_target_pairs={{0,8},{2,10},{4,12},{6,14},{8,0},{10,2},{12,4},{14,6},{16,24},{18,... | collective-permute-start | bytes 884744 | tf_op jit(solution)/shard_map/ppermute | solution.py:597
  82.2 17.3 %collective-permute-start.4 = (bf16[4,48,1536]{2,1,0:T(8,128)(2,1)S(1)}, bf16[4,48,1536]{2,1,0:T(8,128)(2,1)S(1)}, u32[]{:S(2)}, u32[]{:S(2)}) collective-permute-start(bf16[4,48,1536]{2,1,0:T(8,128)(2,1)S(1)} %bitcast.216), channel_id=1, source_target_pairs={{0,4},{2,6},{4,0},{6,2},{8,12},{10,14},{12,8},{14,10},{16,20},{18,... | collective-permute-start | bytes 1769480 | tf_op jit(solution)/shard_map/ppermute | solution.py:597
  83.8 15.7 %collective-permute-start.5 = (bf16[4,96,768]{2,1,0:T(8,128)(2,1)S(1)}, bf16[4,96,768]{2,1,0:T(8,128)(2,1)S(1)}, u32[]{:S(2)}, u32[]{:S(2)}) collective-permute-start(bf16[4,96,768]{2,1,0:T(8,128)(2,1)S(1)} %bitcast.214), channel_id=1, source_target_pairs={{0,1},{1,0},{2,3},{3,2},{4,5},{5,4},{6,7},{7,6},{8,9},{9,8},{10,11... | collective-permute-start | bytes 1769480 | tf_op jit(solution)/shard_map/ppermute | solution.py:600
  99.8 29.5 %collective-permute-start.6 = (bf16[8,48,1536]{2,1,0:T(8,128)(2,1)S(1)}, bf16[8,48,1536]{2,1,0:T(8,128)(2,1)}, u32[]{:S(2)}, u32[]{:S(2)}) collective-permute-start(bf16[8,48,1536]{2,1,0:T(8,128)(2,1)S(1)} %bitcast.209), channel_id=1, source_target_pairs={{0,1},{1,0},{2,3},{3,2},{4,5},{5,4},{6,7},{7,6},{8,9},{9,8},{10,11... | collective-permute-start | bytes 3538952 | tf_op jit(solution)/shard_map/ppermute | solution.py:600
  100.4 33.8 %collective-permute-start.7 = (bf16[4,192,768]{2,1,0:T(8,128)(2,1)S(1)}, bf16[4,192,768]{2,1,0:T(8,128)(2,1)S(1)}, u32[]{:S(2)}, u32[]{:S(2)}) collective-permute-start(bf16[4,192,768]{2,1,0:T(8,128)(2,1)S(1)} %bitcast.212), channel_id=1, source_target_pairs={{0,4},{2,6},{4,0},{6,2},{8,12},{10,14},{12,8},{14,10},{16,20},{18,... | collective-permute-start | bytes 3538952 | tf_op jit(solution)/shard_map/ppermute | solution.py:597
  134.5 9.3 %collective-permute-start.10 = (bf16[8,192,768]{2,1,0:T(8,128)(2,1)S(1)}, bf16[8,192,768]{2,1,0:T(8,128)(2,1)}, u32[]{:S(2)}, u32[]{:S(2)}) collective-permute-start(bf16[8,192,768]{2,1,0:T(8,128)(2,1)S(1)} %bitcast.207), channel_id=1, source_target_pairs={{0,2},{2,0},{4,6},{6,4},{8,10},{10,8},{12,14},{14,12},{16,18},{18,... | collective-permute-start | bytes 7077896 | tf_op jit(solution)/shard_map/ppermute | solution.py:597
  134.6 9.2 %collective-permute-start.8 = (bf16[8,48,1536]{2,1,0:T(8,128)(2,1)S(1)}, bf16[8,48,1536]{2,1,0:T(8,128)(2,1)}, u32[]{:S(2)}, u32[]{:S(2)}) collective-permute-start(bf16[8,48,1536]{2,1,0:T(8,128)(2,1)S(1)} %bitcast.210), channel_id=1, source_target_pairs={{0,2},{2,0},{4,6},{6,4},{8,10},{10,8},{12,14},{14,12},{16,18},{18,... | collective-permute-start | bytes 3538952 | tf_op jit(solution)/shard_map/ppermute | solution.py:597
  135.0 8.7 %collective-permute-start.9 = (bf16[8,48,1536]{2,1,0:T(8,128)(2,1)}, bf16[8,48,1536]{2,1,0:T(8,128)(2,1)}, u32[]{:S(2)}, u32[]{:S(2)}) collective-permute-start(bf16[8,48,1536]{2,1,0:T(8,128)(2,1)} %collective-permute-done.6.refs_1_), channel_id=1, source_target_pairs={{0,2},{2,0},{4,6},{6,4},{8,10},{10,8},{12,14},{14,12},{16,18},{18,... | collective-permute-start | bytes 3538952 | tf_op jit(solution)/shard_map/ppermute | solution.py:597
  186.7 64.7 %all-to-all-start.2 = ((bf16[2,512,768]{2,1,0:T(8,128)(2,1)}), bf16[2,512,768]{2,1,0:T(8,128)(2,1)S(1)}, u32[]{:S(2)}, u32[]{:S(2)}) async-start(bf16[2,512,768]{2,1,0:T(8,128)(2,1)} %param.16), calls=%async_computation.2 | async-start | bytes 3145728 | tf_op jit(solution)/shard_map/all_to_all | solution.py:588
  190.5 249.6 %reduce-scatter.3.cloned.1.call-start = ((), (), s32[]{:S(2)}) async-start(), calls=%async_computation.9 | async-start | bytes 11280384 | tf_op jit(solution)/shard_map/reduce_scatter | solution.py:603
  304.1 41.0 %all-to-all-start.3 = ((bf16[2,512,768]{2,1,0:T(8,128)(2,1)}), bf16[2,512,768]{2,1,0:T(8,128)(2,1)S(1)}, u32[]{:S(2)}, u32[]{:S(2)}) async-start(bf16[2,512,768]{2,1,0:T(8,128)(2,1)} %bitcast.31), calls=%async_computation.3 | async-start | bytes 3145728 | tf_op jit(solution)/shard_map/all_to_all | solution.py:772
  307.8 213.1 %reduce-scatter.5.cloned.1.call-start = ((), (), s32[]{:S(2)}) async-start(), calls=%async_computation.10 | async-start | bytes 3760128 | tf_op jit(solution)/shard_map/reduce_scatter | solution.py:603
  368.4 9.0 %collective-permute-start.11 = (bf16[8,2,48,1536]{3,2,1,0:T(8,128)(2,1)}, bf16[8,2,48,1536]{3,2,1,0:T(8,128)(2,1)}, u32[]{:S(2)}, u32[]{:S(2)}) collective-permute-start(bf16[8,2,48,1536]{3,2,1,0:T(8,128)(2,1)} %get-tuple-element.255), channel_id=1, source_target_pairs={{0,2},{2,0},{4,6},{6,4},{8,10},{10,8},{12,14},{14,12},{16,18},{18,... | collective-permute-start | bytes 7077896 | tf_op jit(solution)/shard_map/ppermute | solution.py:597
  380.4 28.5 %collective-permute-start.12 = (bf16[2,2,2,48,1536]{4,3,2,1,0:T(8,128)(2,1)}, bf16[2,2,2,48,1536]{4,3,2,1,0:T(8,128)(2,1)S(1)}, u32[]{:S(2)}, u32[]{:S(2)}) collective-permute-start(bf16[2,2,2,48,1536]{4,3,2,1,0:T(8,128)(2,1)} %fusion.5), channel_id=1, source_target_pairs={{0,1},{1,0},{2,3},{3,2},{4,5},{5,4},{6,7},{7,6},{8,9},{9,8},{10,11... | collective-permute-start | bytes 3538952 | tf_op jit(solution)/shard_map/ppermute | solution.py:600
  424.5 5.7 collective-permute-start.13
  434.1 53.8 %collective-permute-start.15 = (bf16[2,2,2,48,1920]{4,3,2,1,0:T(8,128)(2,1)}, bf16[2,2,2,48,1920]{4,3,2,1,0:T(8,128)(2,1)S(1)}, u32[]{:S(2)}, u32[]{:S(2)}) collective-permute-start(bf16[2,2,2,48,1920]{4,3,2,1,0:T(8,128)(2,1)} %fusion.3), channel_id=1, source_target_pairs={{0,1},{1,0},{2,3},{3,2},{4,5},{5,4},{6,7},{7,6},{8,9},{9,8},{10,11... | collective-permute-start | bytes 4423688 | tf_op jit(solution)/shard_map/ppermute | solution.py:600
  439.4 48.5 %collective-permute-start.14 = (bf16[2,2,48,1536]{3,2,1,0:T(8,128)(2,1)}, bf16[2,2,48,1536]{3,2,1,0:T(8,128)(2,1)}, u32[]{:S(2)}, u32[]{:S(2)}) collective-permute-start(bf16[2,2,48,1536]{3,2,1,0:T(8,128)(2,1)} %fusion.6), channel_id=1, source_target_pairs={{0,4},{2,6},{4,0},{6,2},{8,12},{10,14},{12,8},{14,10},{16,20},{18,... | collective-permute-start | bytes 1769480 | tf_op jit(solution)/shard_map/ppermute | solution.py:597
  440.1 47.9 %collective-permute-start.16 = (bf16[48,6912]{1,0:T(8,128)(2,1)}, bf16[48,6912]{1,0:T(8,128)(2,1)}, u32[]{:S(2)}, u32[]{:S(2)}) collective-permute-start(bf16[48,6912]{1,0:T(8,128)(2,1)} %reduce-scatter.3.cloned.1.call-done), channel_id=1, source_target_pairs={{0,1},{1,0},{2,3},{3,2},{4,5},{5,4},{6,7},{7,6},{8,9},{9,8},{10,11... | collective-permute-start | bytes 1990664 | tf_op jit(solution)/shard_map/ppermute | solution.py:600
  498.5 24.3 %collective-permute-start.22 = (bf16[2,2,2,48,1152]{4,3,2,1,0:T(8,128)(2,1)}, bf16[2,2,2,48,1152]{4,3,2,1,0:T(8,128)(2,1)}, u32[]{:S(2)}, u32[]{:S(2)}) collective-permute-start(bf16[2,2,2,48,1152]{4,3,2,1,0:T(8,128)(2,1)} %fusion.7), channel_id=1, source_target_pairs={{0,1},{1,0},{2,3},{3,2},{4,5},{5,4},{6,7},{7,6},{8,9},{9,8},{10,11... | collective-permute-start | bytes 2654216 | tf_op jit(solution)/shard_map/ppermute | solution.py:600
  501.0 20.0 %collective-permute-start.21 = (bf16[2,2,48,1920]{3,2,1,0:T(8,128)(2,1)}, bf16[2,2,48,1920]{3,2,1,0:T(8,128)(2,1)S(1)}, u32[]{:S(2)}, u32[]{:S(2)}) collective-permute-start(bf16[2,2,48,1920]{3,2,1,0:T(8,128)(2,1)} %fusion.4), channel_id=1, source_target_pairs={{0,4},{2,6},{4,0},{6,2},{8,12},{10,14},{12,8},{14,10},{16,20},{18,... | collective-permute-start | bytes 2211848 | tf_op jit(solution)/shard_map/ppermute | solution.py:597
  502.3 18.6 %collective-permute-start.18 = (bf16[48,1536]{1,0:T(8,128)(2,1)}, bf16[48,1536]{1,0:T(8,128)(2,1)}, u32[]{:S(2)}, u32[]{:S(2)}) collective-permute-start(bf16[48,1536]{1,0:T(8,128)(2,1)} %get-tuple-element.306), channel_id=1, source_target_pairs={{0,8},{2,10},{4,12},{6,14},{8,0},{10,2},{12,4},{14,6},{16,24},{18,... | collective-permute-start | bytes 442376 | tf_op jit(solution)/shard_map/ppermute | solution.py:597
  504.0 16.9 %collective-permute-start.19 = (bf16[48,1536]{1,0:T(8,128)(2,1)}, bf16[48,1536]{1,0:T(8,128)(2,1)}, u32[]{:S(2)}, u32[]{:S(2)}) collective-permute-start(bf16[48,1536]{1,0:T(8,128)(2,1)} %get-tuple-element.307), channel_id=1, source_target_pairs={{0,16},{2,18},{4,20},{6,22},{8,24},{10,26},{12,28},{14,30},{16,0},... | collective-permute-start | bytes 442376 | tf_op jit(solution)/shard_map/ppermute | solution.py:597
  504.7 16.2 %collective-permute-start.20 = (bf16[48,1536]{1,0:T(8,128)(2,1)}, bf16[48,1536]{1,0:T(8,128)(2,1)}, u32[]{:S(2)}, u32[]{:S(2)}) collective-permute-start(bf16[48,1536]{1,0:T(8,128)(2,1)} %get-tuple-element.308), channel_id=1, source_target_pairs={{0,24},{2,26},{4,28},{6,30},{8,16},{10,18},{12,20},{14,22},{16,8},... | collective-permute-start | bytes 442376 | tf_op jit(solution)/shard_map/ppermute | solution.py:597
  520.9 17.7 %collective-permute-start.29 = (f32[2,2,1152]{2,1,0:T(2,128)}, f32[2,2,1152]{2,1,0:T(2,128)}, u32[]{:S(2)}, u32[]{:S(2)}) collective-permute-start(f32[2,2,1152]{2,1,0:T(2,128)} %bitcast.202), channel_id=1, source_target_pairs={{0,2},{2,0},{4,6},{6,4},{8,10},{10,8},{12,14},{14,12},{16,18},{18,... | collective-permute-start | bytes 55304 | tf_op jit(solution)/shard_map/ppermute | solution.py:597
  521.0 19.2 %collective-permute-start.30 = (f32[2,2,1152]{2,1,0:T(2,128)}, f32[2,2,1152]{2,1,0:T(2,128)S(1)}, u32[]{:S(2)}, u32[]{:S(2)}) collective-permute-start(f32[2,2,1152]{2,1,0:T(2,128)} %bitcast.201), channel_id=1, source_target_pairs={{0,4},{2,6},{4,0},{6,2},{8,12},{10,14},{12,8},{14,10},{16,20},{18,... | collective-permute-start | bytes 55304 | tf_op jit(solution)/shard_map/ppermute | solution.py:597
  521.8 20.4 %collective-permute-start.31 = (f32[2,2,1152]{2,1,0:T(2,128)}, f32[2,2,1152]{2,1,0:T(2,128)}, u32[]{:S(2)}, u32[]{:S(2)}) collective-permute-start(f32[2,2,1152]{2,1,0:T(2,128)} %bitcast.200), channel_id=1, source_target_pairs={{0,6},{2,4},{4,2},{6,0},{8,14},{10,12},{12,10},{14,8},{16,22},{18,... | collective-permute-start | bytes 55304 | tf_op jit(solution)/shard_map/ppermute | solution.py:597
  525.1 12.7 %collective-permute-start.23 = (bf16[2,2,48,1152]{3,2,1,0:T(8,128)(2,1)}, bf16[2,2,48,1152]{3,2,1,0:T(8,128)(2,1)}, u32[]{:S(2)}, u32[]{:S(2)}) collective-permute-start(bf16[2,2,48,1152]{3,2,1,0:T(8,128)(2,1)} %fusion.8), channel_id=1, source_target_pairs={{0,4},{2,6},{4,0},{6,2},{8,12},{10,14},{12,8},{14,10},{16,20},{18,... | collective-permute-start | bytes 1327112 | tf_op jit(solution)/shard_map/ppermute | solution.py:597
  530.3 27.6 %collective-permute-start.25 = (bf16[48,2304]{1,0:T(8,128)(2,1)}, bf16[48,2304]{1,0:T(8,128)(2,1)}, u32[]{:S(2)}, u32[]{:S(2)}) collective-permute-start(bf16[48,2304]{1,0:T(8,128)(2,1)} %reduce-scatter.5.cloned.1.call-done), channel_id=1, source_target_pairs={{0,1},{1,0},{2,3},{3,2},{4,5},{5,4},{6,7},{7,6},{8,9},{9,8},{10,11... | collective-permute-start | bytes 663560 | tf_op jit(solution)/shard_map/ppermute | solution.py:600
  530.7 54.8 %all-to-all-start.4 = ((bf16[2,512,768]{2,1,0:T(8,128)(2,1)}), bf16[2,512,768]{2,1,0:T(8,128)(2,1)S(1)}, u32[]{:S(2)}, u32[]{:S(2)}) async-start(bf16[2,512,768]{2,1,0:T(8,128)(2,1)} %bitcast.247), calls=%async_computation.6 | async-start | bytes 3145728 | tf_op jit(solution)/shard_map/all_to_all | solution.py:772
  537.8 20.1 %collective-permute-start.26 = (bf16[48,1920]{1,0:T(8,128)(2,1)}, bf16[48,1920]{1,0:T(8,128)(2,1)S(1)}, u32[]{:S(2)}, u32[]{:S(2)}) collective-permute-start(bf16[48,1920]{1,0:T(8,128)(2,1)} %get-tuple-element.328), channel_id=1, source_target_pairs={{0,8},{2,10},{4,12},{6,14},{8,0},{10,2},{12,4},{14,6},{16,24},{18,... | collective-permute-start | bytes 552968 | tf_op jit(solution)/shard_map/ppermute | solution.py:597
  538.7 19.3 %collective-permute-start.27 = (bf16[48,1920]{1,0:T(8,128)(2,1)}, bf16[48,1920]{1,0:T(8,128)(2,1)S(1)}, u32[]{:S(2)}, u32[]{:S(2)}) collective-permute-start(bf16[48,1920]{1,0:T(8,128)(2,1)} %get-tuple-element.329), channel_id=1, source_target_pairs={{0,16},{2,18},{4,20},{6,22},{8,24},{10,26},{12,28},{14,30},{16,0},... | collective-permute-start | bytes 552968 | tf_op jit(solution)/shard_map/ppermute | solution.py:597
  540.2 17.7 %collective-permute-start.28 = (bf16[48,1920]{1,0:T(8,128)(2,1)}, bf16[48,1920]{1,0:T(8,128)(2,1)S(1)}, u32[]{:S(2)}, u32[]{:S(2)}) collective-permute-start(bf16[48,1920]{1,0:T(8,128)(2,1)} %get-tuple-element.330), channel_id=1, source_target_pairs={{0,24},{2,26},{4,28},{6,30},{8,16},{10,18},{12,20},{14,22},{16,8},... | collective-permute-start | bytes 552968 | tf_op jit(solution)/shard_map/ppermute | solution.py:597
  542.2 15.7 %collective-permute-start.24 = (bf16[48,1536]{1,0:T(8,128)(2,1)}, bf16[48,1536]{1,0:T(8,128)(2,1)S(1)}, u32[]{:S(2)}, u32[]{:S(2)}) collective-permute-start(bf16[48,1536]{1,0:T(8,128)(2,1)} %fusion.21), channel_id=1, source_target_pairs={{0,1},{1,0},{2,3},{3,2},{4,5},{5,4},{6,7},{7,6},{8,9},{9,8},{10,11... | collective-permute-start | bytes 442376 | tf_op jit(solution)/shard_map/ppermute | solution.py:600
  561.1 7.1 %collective-permute-start.32 = (bf16[48,1152]{1,0:T(8,128)(2,1)S(1)}, bf16[48,1152]{1,0:T(8,128)(2,1)S(1)}, u32[]{:S(2)}, u32[]{:S(2)}) collective-permute-start(bf16[48,1152]{1,0:T(8,128)(2,1)S(1)} %get-tuple-element.342), channel_id=1, source_target_pairs={{0,8},{2,10},{4,12},{6,14},{8,0},{10,2},{12,4},{14,6},{16,24},{18,... | collective-permute-start | bytes 331784 | tf_op jit(solution)/shard_map/ppermute | solution.py:597
  562.1 10.9 %collective-permute-start.33 = (bf16[48,1152]{1,0:T(8,128)(2,1)S(1)}, bf16[48,1152]{1,0:T(8,128)(2,1)S(1)}, u32[]{:S(2)}, u32[]{:S(2)}) collective-permute-start(bf16[48,1152]{1,0:T(8,128)(2,1)S(1)} %get-tuple-element.343), channel_id=1, source_target_pairs={{0,16},{2,18},{4,20},{6,22},{8,24},{10,26},{12,28},{14,30},{16,0},... | collective-permute-start | bytes 331784 | tf_op jit(solution)/shard_map/ppermute | solution.py:597
  563.3 11.2 %collective-permute-start.34 = (bf16[48,1152]{1,0:T(8,128)(2,1)S(1)}, bf16[48,1152]{1,0:T(8,128)(2,1)S(1)}, u32[]{:S(2)}, u32[]{:S(2)}) collective-permute-start(bf16[48,1152]{1,0:T(8,128)(2,1)S(1)} %get-tuple-element.344), channel_id=1, source_target_pairs={{0,24},{2,26},{4,28},{6,30},{8,16},{10,18},{12,20},{14,22},{16,8},... | collective-permute-start | bytes 331784 | tf_op jit(solution)/shard_map/ppermute | solution.py:597
  565.5 12.9 %collective-permute-start.35 = (bf16[48,1920]{1,0:T(8,128)(2,1)S(1)}, bf16[48,1920]{1,0:T(8,128)(2,1)S(1)}, u32[]{:S(2)}, u32[]{:S(2)}) collective-permute-start(bf16[48,1920]{1,0:T(8,128)(2,1)S(1)} %fusion.13), channel_id=1, source_target_pairs={{0,1},{1,0},{2,3},{3,2},{4,5},{5,4},{6,7},{7,6},{8,9},{9,8},{10,11... | collective-permute-start | bytes 552968 | tf_op jit(solution)/shard_map/ppermute | solution.py:600
  565.8 10.2 %collective-permute-start.36 = (f32[1152]{0:T(1024)S(1)}, f32[1152]{0:T(1024)S(1)}, u32[]{:S(2)}, u32[]{:S(2)}) collective-permute-start(f32[1152]{0:T(1024)S(1)} %add_add_fusion.3), channel_id=1, source_target_pairs={{0,8},{2,10},{4,12},{6,14},{8,0},{10,2},{12,4},{14,6},{16,24},{18,... | collective-permute-start | bytes 13832 | tf_op jit(solution)/shard_map/ppermute | solution.py:597
  568.2 7.8 %collective-permute-start.37 = (f32[1152]{0:T(1024)S(1)}, f32[1152]{0:T(1024)S(1)}, u32[]{:S(2)}, u32[]{:S(2)}) collective-permute-start(f32[1152]{0:T(1024)S(1)} %add_add_fusion.2), channel_id=1, source_target_pairs={{0,16},{2,18},{4,20},{6,22},{8,24},{10,26},{12,28},{14,30},{16,0},... | collective-permute-start | bytes 13832 | tf_op jit(solution)/shard_map/ppermute | solution.py:597
  573.0 5.4 collective-permute-start.38
  575.7 5.1 collective-permute-start.39
  (29 other events, 227.0 us)
Sparse Core Ops, SparseCore 0:
  12.8 67.0 all-gather.4
  82.7 90.0 all-gather.6
  175.7 51.5 all-gather.8
  304.2 118.7 reduce-scatter.2
  436.0 65.9 reduce-scatter.4

commit v12 on v11

--- a/solution.py
+++ b/solution.py
@@ -9,7 +9,7 @@
 
 HEAD_SIZE = 64
 PAIR = 2 * HEAD_SIZE
-FORWARD_ROWS = 512
+FORWARD_ROWS = 1024
 BACKWARD_ROWS = 256
 ROW_TILE = 256
 FF_CHUNK = 1024
@@ -589,7 +589,6 @@
 
     core = lax.axis_index("wide") & 1
     place = lax.axis_index("seq")
-    indices = jnp.stack([core, place]).astype(jnp.int32)
     row_unit = qkv_weight.shape[1]
 
     def across(bit):
@@ -649,31 +648,6 @@
         )
         return joined.reshape((2 * lead,) + current.shape[1:])
 
-    def gather_columns(shard):
-        rows, columns = shard.shape[0], shard.shape[1] // 2
-        current = lax.dynamic_slice_in_dim(shard, place * columns, columns, axis=1)[None]
-        for bit in chip_bits:
-            (received,) = yield [(current, across(bit))]
-            current = join(current, received, bit_of(bit))
-        (aside,) = yield [(current, beside_seq)]
-        passed = yield [(part, across(1)) for part in (current, aside)]
-
-        def target(own_core, own_place):
-            def where(ref):
-                which_core = ref[0] if own_core else 1 - ref[0]
-                which_place = ref[1] if own_place else 1 - ref[1]
-                start = pl.multiple_of(which_place * columns, columns)
-                return (slice(None), which_core, slice(None), pl.ds(start, columns))
-
-            return where
-
-        return place_pieces(
-            [current, aside, *passed],
-            (current.shape[0], 2, rows, 2 * columns),
-            [target(True, True), target(True, False), target(False, True), target(False, False)],
-            indices,
-        ).reshape(-1, 2 * columns)
-
     def gather_rows(shard):
         rows, columns = shard.shape[0] // 2, shard.shape[1]
         current = side_of(shard.reshape(2, rows, columns), place, 0)[None]
@@ -700,15 +674,25 @@
         ]
     )
     side = jnp.pad(small.T, ((0, 0), (0, -small.shape[0] % PAIR)))
-    joined_parts = [jnp.concatenate([qkv_weight[0], out_weight[0], side], axis=1)]
+    joined_parts = [
+        jnp.concatenate([qkv_weight[0], out_weight[0], up_weight[0], side], axis=1)
+    ]
     for layer in range(1, layers):
-        parts = [qkv_weight[layer], out_weight[layer], up_weight[layer]]
-        joined_parts.append(jnp.concatenate(parts, axis=1))
-    joined = [lax.all_gather(part, "wide", axis=0, tiled=True) for part in joined_parts]
-    downs = {
-        layer: lax.all_gather(down_weight[layer], "wide", axis=0, tiled=True)
-        for layer in range(1, layers)
-    }
+        joined_parts.append(jnp.concatenate([qkv_weight[layer], out_weight[layer]], axis=1))
+
+    def whole_matrix(part):
+        return lax.all_gather(part, "wide", axis=0, tiled=True)
+
+    joined = [whole_matrix(part) for part in joined_parts]
+    ups = [(joined[0], 4 * features // (up_bias.shape[1] * groups))]
+    ups += [(whole_matrix(up_weight[layer]), 0) for layer in range(1, layers)]
+    downs = {}
+
+    def fetch_down(layer):
+        return begin(
+            gather_rows(down_weight[layer]), functools.partial(downs.__setitem__, layer)
+        )
+
     rows = joined[0][:, -side.shape[1] :].T.astype(single)
     spread_bias = rows[row_count : row_count + layers * up_pieces]
     spread_bias = spread_bias.reshape(layers, up_pieces, groups, row_unit).swapaxes(1, 2)
@@ -718,16 +702,12 @@
     gain_row = lambda layer: layer * norm_gains.shape[1]
     shift_row = lambda layer: gain_count + layer * bias_rows.shape[1]
     matrices = [None] * layers
-    ups = {}
-    fetches = [
-        begin(gather_columns(up_weight[0]), functools.partial(ups.__setitem__, 0)),
-        begin(gather_rows(down_weight[0]), functools.partial(downs.__setitem__, 0)),
-    ]
+    fetch = fetch_down(0)
     marks = jnp.stack([segment_ids, pad_mask], axis=2)
-    time_embed, marks = advance((time_embed, marks), *fetches)
+    time_embed, marks = advance((time_embed, marks), fetch)
     marks = whole_sequence(marks)
-    for _ in chip_bits[2:]:
-        time_embed, marks = advance((time_embed, marks), *fetches)
+    for _ in chip_bits[1:]:
+        time_embed, marks = advance((time_embed, marks), fetch)
     doc, pad = marks[:, 0], marks[:, 1]
     positions = jnp.arange(doc.shape[0])
     allowed = (doc[:, None] == doc[None, :]) & (
@@ -745,14 +725,19 @@
         if layer == layers - 1:
             packed, out_grad = lax.optimization_barrier((packed, out_grad))
             my_upstream = whole_sequence(out_grad)
-        packed = advance(packed, *fetches)
+        packed = advance(packed, fetch)
+        later = None
+        if layer < layers - 1:
+            later = fetch_down(layer + 1)
+            packed = launch(packed, [later])
         attended, totals = attend_forward(packed, bias)
-        attended = advance(attended, *fetches)
-        while running:
-            attended = advance(attended, *fetches)
-        up = (whole, 4 * features // up_bias.shape[1] // groups) if layer else (ups[0], 0)
+        while layer not in downs:
+            attended = advance(attended, fetch)
+        if later is not None:
+            attended = advance(attended, later)
+            fetch = later
+        up = ups[layer]
         matrices[layer] = (whole, up, downs[layer])
-        fetches = []
         middle, second, activated, slope, hidden = feed(
             attended,
             hidden,
@@ -765,6 +750,8 @@
             downs[layer],
             single if layer < layers - 1 else half,
         )
+        if later is not None:
+            hidden = advance(hidden, later)
         saved.append((before, normed, packed, totals, attended, middle, second, activated, slope))
 
     def split_back(result):

time: 605 us -> 641 us (1.060)
  waiting for transfers between devices: 102 us -> 145 us
  starting transfers between devices: 56.5 us -> 63.1 us
  blocking collectives: 6.45 us -> 0 us
    all_gather x3, waiting for transfers between devices: 10.8 us -> 41.2 us  [whole_matrix(): return lax.all_gather(part, 'wide', axis=0, tiled=True)]
    ppermute x30 -> x29, waiting for transfers between devices: 70.6 us -> 52.1 us  [across(): return lambda part: lax.ppermute(part, 'wide', pairs)]
    all_to_all x2 -> x3, waiting for transfers between devices: 0.01 us -> 16.9 us  [whole_sequence(): lax.all_to_all(part, 'seq', split_axis=0, concat_axis=1, tiled=True)[0]]
    ppermute x11, waiting for transfers between devices: 21 us -> 34.7 us  [beside_seq(): return lax.ppermute(part, 'seq', swap)]
    all_to_all x1 -> x0, blocking collectives: 6.45 us -> none  [whole_sequence(): lax.all_to_all(part, 'seq', split_axis=0, concat_axis=1, tiled=True)[0]]
    ppermute x30 -> x29, starting transfers between devices: 31.4 us -> 33 us  [across(): return lambda part: lax.ppermute(part, 'wide', pairs)]
  transfers between devices with their start and end apart: 50 -> 50, of which waited for: 14 -> 17; matrix products, arithmetic and copies ran while one was open for 11% -> 9% of each run, Pallas kernels for 48% -> 44%
where the time goes in v12:
time: 641 us; the launch traced here: 630 us
  Pallas kernels  331 us (52%)
  waiting for transfers between devices  145 us (23%)
  starting transfers between devices  63.1 us (10%)
  other arithmetic  47.3 us (7%)
  local copies, waits for them, and re-layouts  28.5 us (4%)
  between operations  15.2 us (2%)
    pallas_call x8, Pallas kernels, row_tiled(): pl.pallas_call(kernel, grid=(length // ROW_TILE,), in_specs=in_specs, out...  141 us
    pallas_call x2, Pallas kernels, attend_backward(): pl.pallas_call(functools.partial(attend_grad_kernel, rows=BACKWARD_ROWS),...  75 us
    pallas_call x5, Pallas kernels, term_blocks(): pl.pallas_call(kernel, in_specs=[pl.BlockSpec(memory_space=pltpu.SMEM)] +...  63.1 us
    ppermute x29, waiting for transfers between devices, across(): return lambda part: lax.ppermute(part, 'wide', pairs)  52.1 us
    pallas_call x2, Pallas kernels, attend_forward(): pl.pallas_call(functools.partial(attend_kernel, rows=FORWARD_ROWS), grid=...  48 us
    all_gather x3, waiting for transfers between devices, whole_matrix(): return lax.all_gather(part, 'wide', axis=0, tiled=True)  41.2 us
    ppermute x11, waiting for transfers between devices, beside_seq(): return lax.ppermute(part, 'seq', swap)  34.7 us
    ppermute x29, starting transfers between devices, across(): return lambda part: lax.ppermute(part, 'wide', pairs)  33 us
  transfers between devices with their start and end apart: 50, of which 17 were waited for; matrix products, arithmetic and copies ran while one was open for 9% of the time, Pallas kernels for 44%

profile of v12, /device:TPU:0, one launch (start us, length us, event | category | flops | bytes accessed | tf_op | source)
XLA Modules:
  0.0 630.0 jit_solution(8708912792650934620)
XLA Ops:
  13.9 4.0 collective-permute-start
  18.0 7.0 %collective-permute-done.refs_1_ = bf16[1,96,768]{2,1,0:T(8,128)(2,1)S(1)} collective-permute-done((bf16[1,96,768]{2,1,0:T(8,128)(2,1)S(1)}, bf16[1,96,768]{2,1,0:T(8,128)(2,1)S(1)}, u32[]{:S(2)}, u32[]{:S(2)}) %collective-permute-start) | collective-permute-done | bytes 147488 | tf_op jit(solution)/shard_map/ppermute | solution.py:596
  27.4 3.2 all-to-all-start.1
  30.7 3.8 all-to-all-done.1
  34.5 14.5 %collective-permute-done.1.refs_1_ = bf16[2,96,768]{2,1,0:T(8,128)(2,1)S(1)} collective-permute-done((bf16[2,96,768]{2,1,0:T(8,128)(2,1)S(1)}, bf16[2,96,768]{2,1,0:T(8,128)(2,1)S(1)}, u32[]{:S(2)}, u32[]{:S(2)}) %collective-permute-start.1) | collective-permute-done | bytes 294944 | tf_op jit(solution)/shard_map/ppermute | solution.py:596
  50.6 4.7 all-to-all-start
  55.3 10.1 %collective-permute-done.2.refs_1_ = bf16[4,96,768]{2,1,0:T(8,128)(2,1)S(1)} collective-permute-done((bf16[4,96,768]{2,1,0:T(8,128)(2,1)S(1)}, bf16[4,96,768]{2,1,0:T(8,128)(2,1)S(1)}, u32[]{:S(2)}, u32[]{:S(2)}) %collective-permute-start.2) | collective-permute-done | bytes 589856 | tf_op jit(solution)/shard_map/ppermute | solution.py:599
  67.0 13.1 %all-to-all-done = bf16[2,512,768]{2,1,0:T(8,128)(2,1)} async-done(((bf16[2,512,768]{2,1,0:T(8,128)(2,1)}), bf16[2,512,768]{2,1,0:T(8,128)(2,1)}, u32[]{:S(2)}, u32[]{:S(2)}) %all-to-all-start) | async-done | bytes 1572896 | tf_op jit(solution)/shard_map/all_to_all | solution.py:588
  80.2 3.3 convert_add_fusion.hidden_ref
  83.4 41.1 %all-gather.5.cloned.1.call-done.weight_ref.out_weight_ref.up_ref = bf16[768,6272]{1,0:T(8,128)(2,1)} async-done(((bf16[48,6272]{1,0:T(8,128)(2,1)}), bf16[768,6272]{1,0:T(8,128)(2,1)}) %all-gather.5.cloned.1.call-update) | async-done | bytes 9633808 | tf_op jit(solution)/shard_map/all_gather | solution.py:684
  126.5 9.0 %project.2 = (bf16[1024,768]{1,0:T(8,128)(2,1)}, bf16[1024,2304]{1,0:T(8,128)(2,1)}) custom-call(f32[1024,768]{1,0:T(8,128)} %convert_add_fusion.hidden_ref, f32[128,768]{1,0:T(8,128)} %copy.88.rows_ref, bf16[768,6272]{1,0:T(8,128)(2,1)} %all-gather.5.cloned.1.call-done.weight_ref.out_weight_ref.up_ref), custom_call_target="tpu_custom_call" | custom-call | flops 226492416 | bytes 1216512 | tf_op jit(solution)/shard_map/project/pallas_call | solution.py:231
  138.7 2.8 fusion.2.bias_ref
  141.5 23.9 %attend_forward.2 = (bf16[1024,768]{1,0:T(8,128)(2,1)}, f32[6,2,1024]{2,1,0:T(2,128)}) custom-call(bf16[1024,2304]{1,0:T(8,128)(2,1)} %get-tuple-element.224.query_ref.key_ref.value_ref, bf16[1024,2304]{1,0:T(8,128)(2,1)} %get-tuple-element.224.query_ref.key_ref.value_ref, bf16[1024,2304]{1,0:T(8,128)(2,1)} %get-tuple-element.224.query_ref.key_ref.value_ref, ...), custom_call_target="tpu_custom_call" | custom-call | flops 805306368 | bytes 393216 | tf_op jit(solution)/shard_map/attend_forward/pallas_call | solution.py:68
  176.6 24.3 %feed.2 = (f32[1024,768]{1,0:T(8,128)}, bf16[1024,768]{1,0:T(8,128)(2,1)}, bf16[1024,3072]{1,0:T(8,128)(2,1)}, bf16[1024,3072]{1,0:T(8,128)(2,1)}, f32[1024,768]{1,0:T(8,128)}) custom-call(bf16[1024,768]{1,0:T(8,128)(2,1)} %get-tuple-element.232.attended_ref.refs_2_, f32[1024,768]{1,0:T(8,128)} %convert_add_fusion.hidden_ref, f32[128,768]{1,0:T(8,128)} %copy.88.rows_ref, ...), custom_call_target="tpu_custom_call" | custom-call | flops 679477248 | bytes 3097344 | tf_op jit(solution)/shard_map/feed/pallas_call | solution.py:231
  202.6 9.1 %project.3 = (bf16[1024,768]{1,0:T(8,128)(2,1)}, bf16[1024,2304]{1,0:T(8,128)(2,1)}) custom-call(f32[1024,768]{1,0:T(8,128)} %get-tuple-element.238.hidden_ref, f32[128,768]{1,0:T(8,128)} %copy.88.rows_ref, bf16[768,3072]{1,0:T(8,128)(2,1)} %all-gather.7.cloned.1.call-done.weight_ref.out_weight_ref), custom_call_target="tpu_custom_call" | custom-call | flops 226492416 | bytes 909312 | tf_op jit(solution)/shard_map/project/pallas_call | solution.py:231
  211.7 4.3 collective-permute-done.7.refs_1_
  216.3 24.1 %attend_forward.3 = (bf16[1024,768]{1,0:T(8,128)(2,1)}, f32[6,2,1024]{2,1,0:T(2,128)}) custom-call(bf16[1024,2304]{1,0:T(8,128)(2,1)} %get-tuple-element.244.query_ref.key_ref.value_ref, bf16[1024,2304]{1,0:T(8,128)(2,1)} %get-tuple-element.244.query_ref.key_ref.value_ref, bf16[1024,2304]{1,0:T(8,128)(2,1)} %get-tuple-element.244.query_ref.key_ref.value_ref, ...), custom_call_target="tpu_custom_call" | custom-call | flops 805306368 | bytes 393216 | tf_op jit(solution)/shard_map/attend_forward/pallas_call | solution.py:68
  240.4 15.1 %collective-permute-done.8.refs_1_ = bf16[4,192,768]{2,1,0:T(8,128)(2,1)S(1)} collective-permute-done((bf16[4,192,768]{2,1,0:T(8,128)(2,1)S(1)}, bf16[4,192,768]{2,1,0:T(8,128)(2,1)S(1)}, u32[]{:S(2)}, u32[]{:S(2)}) %collective-permute-start.8) | collective-permute-done | bytes 1179680 | tf_op jit(solution)/shard_map/ppermute | solution.py:596
  255.8 4.7 all-to-all-start.2
  265.3 24.1 %feed.3 = (f32[1024,768]{1,0:T(8,128)}, bf16[1024,768]{1,0:T(8,128)(2,1)}, bf16[1024,3072]{1,0:T(8,128)(2,1)}, bf16[1024,3072]{1,0:T(8,128)(2,1)}, bf16[1024,768]{1,0:T(8,128)(2,1)}) custom-call(bf16[1024,768]{1,0:T(8,128)(2,1)} %get-tuple-element.252.attended_ref.refs_4_, f32[1024,768]{1,0:T(8,128)} %get-tuple-element.238.hidden_ref, ...), custom_call_target="tpu_custom_call" | custom-call | flops 679477248 | bytes 2384640 | tf_op jit(solution)/shard_map/feed/pallas_call | solution.py:231
  289.3 31.9 %feed_grad.2 = (bf16[1024,768]{1,0:T(8,128)(2,1)}, bf16[1024,3072]{1,0:T(8,128)(2,1)}, f32[1024,768]{1,0:T(8,128)}, bf16[1024,768]{1,0:T(8,128)(2,1)}, bf16[1024...) custom-call(bf16[1024,768]{1,0:T(8,128)(2,1)} %bitcast.27.gradient_ref, ...), custom_call_target="tpu_custom_call" | custom-call | flops 679477248 | bytes 2484480 | tf_op jit(solution)/shard_map/feed_grad/pallas_call | solution.py:231
  321.2 19.7 %term_blocks.5 = bf16[16,48,6912]{2,1,0:T(8,128)(2,1)} custom-call(s32[1]{0:T(128)} %bitcast.31.core_ref, bf16[1024,3072]{1,0:T(8,128)(2,1)} %get-tuple-element.257.refs_0_, bf16[1024,768]{1,0:T(8,128)(2,1)} %get-tuple-element.258.refs_1_, bf16[1024,768]{1,0:T(8,128)(2,1)} %get-tuple-element.259.refs_2_, bf16[1024,3072]{1,0:T(8,128)(2,1)} %get-tuple-element.260.refs_3_, ...), custom_call_target="tpu_custom_call" | custom-call | flops 679477248 | bytes 1843200 | tf_op jit(solution)/shard_map/term_blocks/pallas_call | solution.py:555
  340.9 3.7 all-to-all-start.3
  344.7 37.6 %attend_backward.2.packed_grad_ref.refs_1_ = bf16[1024,2304]{1,0:T(8,128)(2,1)} custom-call(bf16[1024,2304]{1,0:T(8,128)(2,1)} %get-tuple-element.244.query_ref.key_ref.value_ref, bf16[1024,2304]{1,0:T(8,128)(2,1)} %get-tuple-element.244.query_ref.key_ref.value_ref, bf16[1024,2304]{1,0:T(8,128)(2,1)} %get-tuple-element.244.query_ref.key_ref.value_ref, ...), custom_call_target="tpu_custom_call" | custom-call | flops 2013265920 | bytes 786432 | tf_op jit(solution)/shard_map/attend_backward/pallas_call | solution.py:151
  382.2 11.1 %project_grad.2 = (f32[1024,768]{1,0:T(8,128)}, bf16[1024,768]{1,0:T(8,128)(2,1)}, f32[8,768]{1,0:T(8,128)}) custom-call(bf16[1024,2304]{1,0:T(8,128)(2,1)} %attend_backward.2.packed_grad_ref.refs_1_, f32[1024,768]{1,0:T(8,128)} %get-tuple-element.238.hidden_ref, f32[1024,768]{1,0:T(8,128)} %get-tuple-element.267.middle_grad_ref, f32[128,768]{1,0:T(8,128)} %copy.88.rows_ref, ...), custom_call_target="tpu_custom_call" | custom-call | flops 226492416 | bytes 1304064 | tf_op jit(solution)/shard_map/project_grad/pallas_call | solution.py:231
  393.4 12.2 %term_blocks.6 = (bf16[8,2,48,1536]{3,2,1,0:T(8,128)(2,1)}, bf16[8,2,48,1536]{3,2,1,0:T(8,128)(2,1)}) custom-call(s32[1]{0:T(128)} %bitcast.31.core_ref, bf16[1024,3072]{1,0:T(8,128)(2,1)} %get-tuple-element.269.refs_0_, bf16[1024,768]{1,0:T(8,128)(2,1)} %get-tuple-element.270.refs_1_), custom_call_target="tpu_custom_call" | custom-call | flops 301989888 | bytes 786432 | tf_op jit(solution)/shard_map/term_blocks/pallas_call | solution.py:555
  406.2 8.5 %term_blocks.7 = bf16[16,48,2304]{2,1,0:T(8,128)(2,1)} custom-call(s32[1]{0:T(128)} %bitcast.31.core_ref, bf16[1024,768]{1,0:T(8,128)(2,1)} %get-tuple-element.273.refs_0_, bf16[1024,2304]{1,0:T(8,128)(2,1)} %attend_backward.2.packed_grad_ref.refs_1_), custom_call_target="tpu_custom_call" | custom-call | flops 226492416 | bytes 614400 | tf_op jit(solution)/shard_map/term_blocks/pallas_call | solution.py:555
  414.7 3.0 fusion.6
  419.3 21.3 %feed_grad.3 = (bf16[1024,768]{1,0:T(8,128)(2,1)}, bf16[1024,3072]{1,0:T(8,128)(2,1)}, f32[1024,768]{1,0:T(8,128)}, bf16[1024,768]{1,0:T(8,128)(2,1)}, bf16[1024...) custom-call(f32[1024,768]{1,0:T(8,128)} %get-tuple-element.279.gradient_ref, ...), custom_call_target="tpu_custom_call" | custom-call | flops 679477248 | bytes 3197184 | tf_op jit(solution)/shard_map/feed_grad/pallas_call | solution.py:231
  440.7 5.3 collective-permute-done.11
  445.9 2.8 fusion.7
  448.7 12.9 %term_blocks.8 = (bf16[8,2,48,1920]{3,2,1,0:T(8,128)(2,1)}, bf16[8,2,48,1920]{3,2,1,0:T(8,128)(2,1)}) custom-call(s32[1]{0:T(128)} %bitcast.31.core_ref, bf16[1024,768]{1,0:T(8,128)(2,1)} %get-tuple-element.290.refs_0_, bf16[1024,3072]{1,0:T(8,128)(2,1)} %get-tuple-element.291.refs_1_, bf16[1024,768]{1,0:T(8,128)(2,1)} %get-tuple-element.232.attended_ref.refs_2_, ...), custom_call_target="tpu_custom_call" | custom-call | flops 377487360 | bytes 1056768 | tf_op jit(solution)/shard_map/term_blocks/pallas_call | solution.py:555
  461.7 5.6 collective-permute-done.12
  467.3 4.1 fusion.3
  476.7 37.4 %attend_backward.3.refs_1_.packed_grad_ref = bf16[1024,2304]{1,0:T(8,128)(2,1)} custom-call(bf16[1024,2304]{1,0:T(8,128)(2,1)} %get-tuple-element.224.query_ref.key_ref.value_ref, bf16[1024,2304]{1,0:T(8,128)(2,1)} %get-tuple-element.224.query_ref.key_ref.value_ref, bf16[1024,2304]{1,0:T(8,128)(2,1)} %get-tuple-element.224.query_ref.key_ref.value_ref, ...), custom_call_target="tpu_custom_call" | custom-call | flops 2013265920 | bytes 786432 | tf_op jit(solution)/shard_map/attend_backward/pallas_call | solution.py:151
  514.1 9.8 %term_blocks.9 = (bf16[8,2,48,1152]{3,2,1,0:T(8,128)(2,1)}, bf16[8,2,48,1152]{3,2,1,0:T(8,128)(2,1)}) custom-call(s32[1]{0:T(128)} %bitcast.31.core_ref, bf16[1024,768]{1,0:T(8,128)(2,1)} %get-tuple-element.310.refs_0_, bf16[1024,2304]{1,0:T(8,128)(2,1)} %attend_backward.3.refs_1_.packed_grad_ref), custom_call_target="tpu_custom_call" | custom-call | flops 226492416 | bytes 614400 | tf_op jit(solution)/shard_map/term_blocks/pallas_call | solution.py:555
  524.0 2.9 fusion.22
  526.9 2.6 fusion.4
  531.0 2.3 collective-permute-done.16
  539.0 2.4 collective-permute-start.18
  543.3 10.1 %project_grad.3 = (bf16[1024,768]{1,0:T(8,128)(2,1)}, f32[8,768]{1,0:T(8,128)}) custom-call(bf16[1024,2304]{1,0:T(8,128)(2,1)} %attend_backward.3.refs_1_.packed_grad_ref, f32[1024,768]{1,0:T(8,128)} %convert_add_fusion.hidden_ref, f32[1024,768]{1,0:T(8,128)} %get-tuple-element.318.middle_grad_ref, f32[128,768]{1,0:T(8,128)} %copy.88.rows_ref, ...), custom_call_target="tpu_custom_call" | custom-call | flops 226492416 | bytes 1414656 | tf_op jit(solution)/shard_map/project_grad/pallas_call | solution.py:231
  564.1 2.5 fusion.15
  567.0 3.7 all-to-all-start.4
  570.7 3.8 collective-permute-done.22
  574.5 2.5 collective-permute-start.26
  580.7 13.5 %collective-permute-done.23 = bf16[48,1536]{1,0:T(8,128)(2,1)S(1)} collective-permute-done((bf16[48,1536]{1,0:T(8,128)(2,1)}, bf16[48,1536]{1,0:T(8,128)(2,1)S(1)}, u32[]{:S(2)}, u32[]{:S(2)}) %collective-permute-start.23) | collective-permute-done | bytes 147488 | tf_op jit(solution)/shard_map/ppermute | solution.py:599
  597.4 2.5 collective-permute-start.32
  604.4 2.5 collective-permute-start.36
  (267 shorter events, 90.8 us)
Async XLA Ops:
  7.2 117.4 %all-gather.5.cloned.1.call-start = ((), (), s32[]{:S(2)}) async-start(), calls=%async_computation.7 | async-start | bytes 10235904 | tf_op jit(solution)/shard_map/all_gather | solution.py:684
  11.7 190.9 %all-gather.7.cloned.1.call-start = ((), (), s32[]{:S(2)}) async-start(), calls=%async_computation.8 | async-start | bytes 5013504 | tf_op jit(solution)/shard_map/all_gather | solution.py:684
  12.5 252.7 %all-gather.9.cloned.1.call-start = ((), (), s32[]{:S(2)}) async-start(), calls=%async_computation.11 | async-start | bytes 5013504 | tf_op jit(solution)/shard_map/all_gather | solution.py:684
  13.9 11.0 %collective-permute-start = (bf16[1,96,768]{2,1,0:T(8,128)(2,1)S(1)}, bf16[1,96,768]{2,1,0:T(8,128)(2,1)S(1)}, u32[]{:S(2)}, u32[]{:S(2)}) collective-permute-start(bf16[1,96,768]{2,1,0:T(8,128)(2,1)S(1)} %get-tuple-element.202.refs_0_), channel_id=1, source_target_pairs={{0,16},{2,18},{4,20},{6,22},{8,24},{10,26},{12,28},{14,30},{16,0},... | collective-permute-start | bytes 442376 | tf_op jit(solution)/shard_map/ppermute | solution.py:596
  25.4 23.6 %collective-permute-start.1 = (bf16[2,96,768]{2,1,0:T(8,128)(2,1)S(1)}, bf16[2,96,768]{2,1,0:T(8,128)(2,1)S(1)}, u32[]{:S(2)}, u32[]{:S(2)}) collective-permute-start(bf16[2,96,768]{2,1,0:T(8,128)(2,1)S(1)} %bitcast.223), channel_id=1, source_target_pairs={{0,8},{2,10},{4,12},{6,14},{8,0},{10,2},{12,4},{14,6},{16,24},{18,... | collective-permute-start | bytes 884744 | tf_op jit(solution)/shard_map/ppermute | solution.py:596
  27.4 7.0 %all-to-all-start.1 = ((s32[2,512,2]{1,2,0:T(2,128)}), s32[2,512,2]{1,2,0:T(2,128)S(1)}, u32[]{:S(2)}, u32[]{:S(2)}) async-start(s32[2,512,2]{1,2,0:T(2,128)} %pad_add_fusion), calls=%async_computation.1 | async-start | bytes 16384 | tf_op jit(solution)/shard_map/all_to_all | solution.py:588
  49.1 16.3 %collective-permute-start.2 = (bf16[4,96,768]{2,1,0:T(8,128)(2,1)S(1)}, bf16[4,96,768]{2,1,0:T(8,128)(2,1)S(1)}, u32[]{:S(2)}, u32[]{:S(2)}) collective-permute-start(bf16[4,96,768]{2,1,0:T(8,128)(2,1)S(1)} %bitcast.219), channel_id=1, source_target_pairs={{0,1},{1,0},{2,3},{3,2},{4,5},{5,4},{6,7},{7,6},{8,9},{9,8},{10,11... | collective-permute-start | bytes 1769480 | tf_op jit(solution)/shard_map/ppermute | solution.py:599
  50.6 29.5 %all-to-all-start = ((bf16[2,512,768]{2,1,0:T(8,128)(2,1)}), bf16[2,512,768]{2,1,0:T(8,128)(2,1)}, u32[]{:S(2)}, u32[]{:S(2)}) async-start(bf16[2,512,768]{2,1,0:T(8,128)(2,1)} %param.12), calls=%async_computation | async-start | bytes 3145728 | tf_op jit(solution)/shard_map/all_to_all | solution.py:588
  65.6 70.0 %collective-permute-start.3 = (bf16[4,192,768]{2,1,0:T(8,128)(2,1)S(1)}, bf16[4,192,768]{2,1,0:T(8,128)(2,1)S(1)}, u32[]{:S(2)}, u32[]{:S(2)}) collective-permute-start(bf16[4,192,768]{2,1,0:T(8,128)(2,1)S(1)} %bitcast.213), channel_id=1, source_target_pairs={{0,4},{2,6},{4,0},{6,2},{8,12},{10,14},{12,8},{14,10},{16,20},{18,... | collective-permute-start | bytes 3538952 | tf_op jit(solution)/shard_map/ppermute | solution.py:596
  138.1 27.3 %collective-permute-start.4 = (bf16[8,192,768]{2,1,0:T(8,128)(2,1)S(1)}, bf16[8,192,768]{2,1,0:T(8,128)(2,1)S(1)}, u32[]{:S(2)}, u32[]{:S(2)}) collective-permute-start(bf16[8,192,768]{2,1,0:T(8,128)(2,1)S(1)} %bitcast.209), channel_id=1, source_target_pairs={{0,2},{2,0},{4,6},{6,4},{8,10},{10,8},{12,14},{14,12},{16,18},{18,... | collective-permute-start | bytes 7077896 | tf_op jit(solution)/shard_map/ppermute | solution.py:596
  138.7 28.1 %collective-permute-start.5 = (bf16[1,96,768]{2,1,0:T(8,128)(2,1)S(1)}, bf16[1,96,768]{2,1,0:T(8,128)(2,1)S(1)}, u32[]{:S(2)}, u32[]{:S(2)}) collective-permute-start(bf16[1,96,768]{2,1,0:T(8,128)(2,1)S(1)} %copy-done.8), channel_id=1, source_target_pairs={{0,16},{2,18},{4,20},{6,22},{8,24},{10,26},{12,28},{14,30},{16,0},... | collective-permute-start | bytes 442376 | tf_op jit(solution)/shard_map/ppermute | solution.py:596
  167.2 33.7 %collective-permute-start.6 = (bf16[2,96,768]{2,1,0:T(8,128)(2,1)S(1)}, bf16[2,96,768]{2,1,0:T(8,128)(2,1)S(1)}, u32[]{:S(2)}, u32[]{:S(2)}) collective-permute-start(bf16[2,96,768]{2,1,0:T(8,128)(2,1)S(1)} %bitcast.221), channel_id=1, source_target_pairs={{0,8},{2,10},{4,12},{6,14},{8,0},{10,2},{12,4},{14,6},{16,24},{18,... | collective-permute-start | bytes 884744 | tf_op jit(solution)/shard_map/ppermute | solution.py:596
  201.0 15.0 %collective-permute-start.7 = (bf16[4,96,768]{2,1,0:T(8,128)(2,1)S(1)}, bf16[4,96,768]{2,1,0:T(8,128)(2,1)S(1)}, u32[]{:S(2)}, u32[]{:S(2)}) collective-permute-start(bf16[4,96,768]{2,1,0:T(8,128)(2,1)S(1)} %bitcast.217), channel_id=1, source_target_pairs={{0,1},{1,0},{2,3},{3,2},{4,5},{5,4},{6,7},{7,6},{8,9},{9,8},{10,11... | collective-permute-start | bytes 1769480 | tf_op jit(solution)/shard_map/ppermute | solution.py:599
  216.1 39.3 %collective-permute-start.8 = (bf16[4,192,768]{2,1,0:T(8,128)(2,1)S(1)}, bf16[4,192,768]{2,1,0:T(8,128)(2,1)S(1)}, u32[]{:S(2)}, u32[]{:S(2)}) collective-permute-start(bf16[4,192,768]{2,1,0:T(8,128)(2,1)S(1)} %bitcast.215), channel_id=1, source_target_pairs={{0,4},{2,6},{4,0},{6,2},{8,12},{10,14},{12,8},{14,10},{16,20},{18,... | collective-permute-start | bytes 3538952 | tf_op jit(solution)/shard_map/ppermute | solution.py:596
  255.7 5.5 collective-permute-start.9
  255.8 33.5 %all-to-all-start.2 = ((bf16[2,512,768]{2,1,0:T(8,128)(2,1)}), bf16[2,512,768]{2,1,0:T(8,128)(2,1)}, u32[]{:S(2)}, u32[]{:S(2)}) async-start(bf16[2,512,768]{2,1,0:T(8,128)(2,1)} %param.16), calls=%async_computation.2 | async-start | bytes 3145728 | tf_op jit(solution)/shard_map/all_to_all | solution.py:588
  260.5 215.6 %reduce-scatter.3.cloned.1.call-start = ((), (), s32[]{:S(2)}) async-start(), calls=%async_computation.9 | async-start | bytes 11280384 | tf_op jit(solution)/shard_map/reduce_scatter | solution.py:602
  340.9 41.3 %all-to-all-start.3 = ((bf16[2,512,768]{2,1,0:T(8,128)(2,1)}), bf16[2,512,768]{2,1,0:T(8,128)(2,1)S(1)}, u32[]{:S(2)}, u32[]{:S(2)}) async-start(bf16[2,512,768]{2,1,0:T(8,128)(2,1)} %bitcast.33), calls=%async_computation.3 | async-start | bytes 3145728 | tf_op jit(solution)/shard_map/all_to_all | solution.py:759
  344.6 212.9 %reduce-scatter.5.cloned.1.call-start = ((), (), s32[]{:S(2)}) async-start(), calls=%async_computation.10 | async-start | bytes 3760128 | tf_op jit(solution)/shard_map/reduce_scatter | solution.py:602
  405.5 9.2 %collective-permute-start.10 = (bf16[8,2,48,1536]{3,2,1,0:T(8,128)(2,1)}, bf16[8,2,48,1536]{3,2,1,0:T(8,128)(2,1)}, u32[]{:S(2)}, u32[]{:S(2)}) collective-permute-start(bf16[8,2,48,1536]{3,2,1,0:T(8,128)(2,1)} %get-tuple-element.275), channel_id=1, source_target_pairs={{0,2},{2,0},{4,6},{6,4},{8,10},{10,8},{12,14},{14,12},{16,18},{18,... | collective-permute-start | bytes 7077896 | tf_op jit(solution)/shard_map/ppermute | solution.py:596
  417.7 28.2 %collective-permute-start.11 = (bf16[2,2,2,48,1536]{4,3,2,1,0:T(8,128)(2,1)}, bf16[2,2,2,48,1536]{4,3,2,1,0:T(8,128)(2,1)S(1)}, u32[]{:S(2)}, u32[]{:S(2)}) collective-permute-start(bf16[2,2,2,48,1536]{4,3,2,1,0:T(8,128)(2,1)} %fusion.6), channel_id=1, source_target_pairs={{0,1},{1,0},{2,3},{3,2},{4,5},{5,4},{6,7},{7,6},{8,9},{9,8},{10,11... | collective-permute-start | bytes 3538952 | tf_op jit(solution)/shard_map/ppermute | solution.py:599
  461.6 5.7 collective-permute-start.12
  471.4 52.6 %collective-permute-start.14 = (bf16[2,2,2,48,1920]{4,3,2,1,0:T(8,128)(2,1)}, bf16[2,2,2,48,1920]{4,3,2,1,0:T(8,128)(2,1)S(1)}, u32[]{:S(2)}, u32[]{:S(2)}) collective-permute-start(bf16[2,2,2,48,1920]{4,3,2,1,0:T(8,128)(2,1)} %fusion.3), channel_id=1, source_target_pairs={{0,1},{1,0},{2,3},{3,2},{4,5},{5,4},{6,7},{7,6},{8,9},{9,8},{10,11... | collective-permute-start | bytes 4423688 | tf_op jit(solution)/shard_map/ppermute | solution.py:599
  475.9 48.1 %collective-permute-start.13 = (bf16[2,2,48,1536]{3,2,1,0:T(8,128)(2,1)}, bf16[2,2,48,1536]{3,2,1,0:T(8,128)(2,1)}, u32[]{:S(2)}, u32[]{:S(2)}) collective-permute-start(bf16[2,2,48,1536]{3,2,1,0:T(8,128)(2,1)} %fusion.7), channel_id=1, source_target_pairs={{0,4},{2,6},{4,0},{6,2},{8,12},{10,14},{12,8},{14,10},{16,20},{18,... | collective-permute-start | bytes 1769480 | tf_op jit(solution)/shard_map/ppermute | solution.py:596
  476.1 47.9 %collective-permute-start.15 = (bf16[48,6912]{1,0:T(8,128)(2,1)}, bf16[48,6912]{1,0:T(8,128)(2,1)}, u32[]{:S(2)}, u32[]{:S(2)}) collective-permute-start(bf16[48,6912]{1,0:T(8,128)(2,1)} %reduce-scatter.3.cloned.1.call-done), channel_id=1, source_target_pairs={{0,1},{1,0},{2,3},{3,2},{4,5},{5,4},{6,7},{7,6},{8,9},{9,8},{10,11... | collective-permute-start | bytes 1990664 | tf_op jit(solution)/shard_map/ppermute | solution.py:599
  534.6 24.9 %collective-permute-start.21 = (bf16[2,2,2,48,1152]{4,3,2,1,0:T(8,128)(2,1)}, bf16[2,2,2,48,1152]{4,3,2,1,0:T(8,128)(2,1)}, u32[]{:S(2)}, u32[]{:S(2)}) collective-permute-start(bf16[2,2,2,48,1152]{4,3,2,1,0:T(8,128)(2,1)} %fusion.8), channel_id=1, source_target_pairs={{0,1},{1,0},{2,3},{3,2},{4,5},{5,4},{6,7},{7,6},{8,9},{9,8},{10,11... | collective-permute-start | bytes 2654216 | tf_op jit(solution)/shard_map/ppermute | solution.py:599
  537.1 20.5 %collective-permute-start.20 = (bf16[2,2,48,1920]{3,2,1,0:T(8,128)(2,1)}, bf16[2,2,48,1920]{3,2,1,0:T(8,128)(2,1)S(1)}, u32[]{:S(2)}, u32[]{:S(2)}) collective-permute-start(bf16[2,2,48,1920]{3,2,1,0:T(8,128)(2,1)} %fusion.4), channel_id=1, source_target_pairs={{0,4},{2,6},{4,0},{6,2},{8,12},{10,14},{12,8},{14,10},{16,20},{18,... | collective-permute-start | bytes 2211848 | tf_op jit(solution)/shard_map/ppermute | solution.py:596
  538.9 18.6 %collective-permute-start.17 = (bf16[48,1536]{1,0:T(8,128)(2,1)}, bf16[48,1536]{1,0:T(8,128)(2,1)}, u32[]{:S(2)}, u32[]{:S(2)}) collective-permute-start(bf16[48,1536]{1,0:T(8,128)(2,1)} %get-tuple-element.326), channel_id=1, source_target_pairs={{0,8},{2,10},{4,12},{6,14},{8,0},{10,2},{12,4},{14,6},{16,24},{18,... | collective-permute-start | bytes 442376 | tf_op jit(solution)/shard_map/ppermute | solution.py:596
  539.0 18.5 %collective-permute-start.18 = (bf16[48,1536]{1,0:T(8,128)(2,1)}, bf16[48,1536]{1,0:T(8,128)(2,1)}, u32[]{:S(2)}, u32[]{:S(2)}) collective-permute-start(bf16[48,1536]{1,0:T(8,128)(2,1)} %get-tuple-element.327), channel_id=1, source_target_pairs={{0,16},{2,18},{4,20},{6,22},{8,24},{10,26},{12,28},{14,30},{16,0},... | collective-permute-start | bytes 442376 | tf_op jit(solution)/shard_map/ppermute | solution.py:596
  541.4 16.2 %collective-permute-start.19 = (bf16[48,1536]{1,0:T(8,128)(2,1)}, bf16[48,1536]{1,0:T(8,128)(2,1)}, u32[]{:S(2)}, u32[]{:S(2)}) collective-permute-start(bf16[48,1536]{1,0:T(8,128)(2,1)} %get-tuple-element.328), channel_id=1, source_target_pairs={{0,24},{2,26},{4,28},{6,30},{8,16},{10,18},{12,20},{14,22},{16,8},... | collective-permute-start | bytes 442376 | tf_op jit(solution)/shard_map/ppermute | solution.py:596
  557.6 16.9 %collective-permute-start.28 = (f32[2,2,1152]{2,1,0:T(2,128)}, f32[2,2,1152]{2,1,0:T(2,128)}, u32[]{:S(2)}, u32[]{:S(2)}) collective-permute-start(f32[2,2,1152]{2,1,0:T(2,128)} %bitcast.204), channel_id=1, source_target_pairs={{0,2},{2,0},{4,6},{6,4},{8,10},{10,8},{12,14},{14,12},{16,18},{18,... | collective-permute-start | bytes 55304 | tf_op jit(solution)/shard_map/ppermute | solution.py:596
  557.7 19.3 %collective-permute-start.29 = (f32[2,2,1152]{2,1,0:T(2,128)}, f32[2,2,1152]{2,1,0:T(2,128)}, u32[]{:S(2)}, u32[]{:S(2)}) collective-permute-start(f32[2,2,1152]{2,1,0:T(2,128)} %bitcast.203), channel_id=1, source_target_pairs={{0,4},{2,6},{4,0},{6,2},{8,12},{10,14},{12,8},{14,10},{16,20},{18,... | collective-permute-start | bytes 55304 | tf_op jit(solution)/shard_map/ppermute | solution.py:596
  557.9 20.9 %collective-permute-start.30 = (f32[2,2,1152]{2,1,0:T(2,128)}, f32[2,2,1152]{2,1,0:T(2,128)S(1)}, u32[]{:S(2)}, u32[]{:S(2)}) collective-permute-start(f32[2,2,1152]{2,1,0:T(2,128)} %bitcast.202), channel_id=1, source_target_pairs={{0,6},{2,4},{4,2},{6,0},{8,14},{10,12},{12,10},{14,8},{16,22},{18,... | collective-permute-start | bytes 55304 | tf_op jit(solution)/shard_map/ppermute | solution.py:596
  561.7 12.7 %collective-permute-start.22 = (bf16[2,2,48,1152]{3,2,1,0:T(8,128)(2,1)}, bf16[2,2,48,1152]{3,2,1,0:T(8,128)(2,1)}, u32[]{:S(2)}, u32[]{:S(2)}) collective-permute-start(bf16[2,2,48,1152]{3,2,1,0:T(8,128)(2,1)} %fusion.9), channel_id=1, source_target_pairs={{0,4},{2,6},{4,0},{6,2},{8,12},{10,14},{12,8},{14,10},{16,20},{18,... | collective-permute-start | bytes 1327112 | tf_op jit(solution)/shard_map/ppermute | solution.py:596
  566.6 27.6 %collective-permute-start.24 = (bf16[48,2304]{1,0:T(8,128)(2,1)}, bf16[48,2304]{1,0:T(8,128)(2,1)}, u32[]{:S(2)}, u32[]{:S(2)}) collective-permute-start(bf16[48,2304]{1,0:T(8,128)(2,1)} %reduce-scatter.5.cloned.1.call-done), channel_id=1, source_target_pairs={{0,1},{1,0},{2,3},{3,2},{4,5},{5,4},{6,7},{7,6},{8,9},{9,8},{10,11... | collective-permute-start | bytes 663560 | tf_op jit(solution)/shard_map/ppermute | solution.py:599
  567.0 54.2 %all-to-all-start.4 = ((bf16[2,512,768]{2,1,0:T(8,128)(2,1)}), bf16[2,512,768]{2,1,0:T(8,128)(2,1)S(1)}, u32[]{:S(2)}, u32[]{:S(2)}) async-start(bf16[2,512,768]{2,1,0:T(8,128)(2,1)} %bitcast.249), calls=%async_computation.6 | async-start | bytes 3145728 | tf_op jit(solution)/shard_map/all_to_all | solution.py:759
  574.5 19.7 %collective-permute-start.25 = (bf16[48,1920]{1,0:T(8,128)(2,1)}, bf16[48,1920]{1,0:T(8,128)(2,1)S(1)}, u32[]{:S(2)}, u32[]{:S(2)}) collective-permute-start(bf16[48,1920]{1,0:T(8,128)(2,1)} %get-tuple-element.348), channel_id=1, source_target_pairs={{0,8},{2,10},{4,12},{6,14},{8,0},{10,2},{12,4},{14,6},{16,24},{18,... | collective-permute-start | bytes 552968 | tf_op jit(solution)/shard_map/ppermute | solution.py:596
  574.5 19.7 %collective-permute-start.26 = (bf16[48,1920]{1,0:T(8,128)(2,1)}, bf16[48,1920]{1,0:T(8,128)(2,1)S(1)}, u32[]{:S(2)}, u32[]{:S(2)}) collective-permute-start(bf16[48,1920]{1,0:T(8,128)(2,1)} %get-tuple-element.349), channel_id=1, source_target_pairs={{0,16},{2,18},{4,20},{6,22},{8,24},{10,26},{12,28},{14,30},{16,0},... | collective-permute-start | bytes 552968 | tf_op jit(solution)/shard_map/ppermute | solution.py:596
  576.9 17.2 %collective-permute-start.27 = (bf16[48,1920]{1,0:T(8,128)(2,1)}, bf16[48,1920]{1,0:T(8,128)(2,1)S(1)}, u32[]{:S(2)}, u32[]{:S(2)}) collective-permute-start(bf16[48,1920]{1,0:T(8,128)(2,1)} %get-tuple-element.350), channel_id=1, source_target_pairs={{0,24},{2,26},{4,28},{6,30},{8,16},{10,18},{12,20},{14,22},{16,8},... | collective-permute-start | bytes 552968 | tf_op jit(solution)/shard_map/ppermute | solution.py:596
  578.9 15.3 %collective-permute-start.23 = (bf16[48,1536]{1,0:T(8,128)(2,1)}, bf16[48,1536]{1,0:T(8,128)(2,1)S(1)}, u32[]{:S(2)}, u32[]{:S(2)}) collective-permute-start(bf16[48,1536]{1,0:T(8,128)(2,1)} %fusion.21), channel_id=1, source_target_pairs={{0,1},{1,0},{2,3},{3,2},{4,5},{5,4},{6,7},{7,6},{8,9},{9,8},{10,11... | collective-permute-start | bytes 442376 | tf_op jit(solution)/shard_map/ppermute | solution.py:599
  597.3 7.1 %collective-permute-start.31 = (bf16[48,1152]{1,0:T(8,128)(2,1)S(1)}, bf16[48,1152]{1,0:T(8,128)(2,1)S(1)}, u32[]{:S(2)}, u32[]{:S(2)}) collective-permute-start(bf16[48,1152]{1,0:T(8,128)(2,1)S(1)} %get-tuple-element.362), channel_id=1, source_target_pairs={{0,8},{2,10},{4,12},{6,14},{8,0},{10,2},{12,4},{14,6},{16,24},{18,... | collective-permute-start | bytes 331784 | tf_op jit(solution)/shard_map/ppermute | solution.py:596
  597.4 11.4 %collective-permute-start.32 = (bf16[48,1152]{1,0:T(8,128)(2,1)S(1)}, bf16[48,1152]{1,0:T(8,128)(2,1)S(1)}, u32[]{:S(2)}, u32[]{:S(2)}) collective-permute-start(bf16[48,1152]{1,0:T(8,128)(2,1)S(1)} %get-tuple-element.363), channel_id=1, source_target_pairs={{0,16},{2,18},{4,20},{6,22},{8,24},{10,26},{12,28},{14,30},{16,0},... | collective-permute-start | bytes 331784 | tf_op jit(solution)/shard_map/ppermute | solution.py:596
  599.9 10.8 %collective-permute-start.33 = (bf16[48,1152]{1,0:T(8,128)(2,1)S(1)}, bf16[48,1152]{1,0:T(8,128)(2,1)S(1)}, u32[]{:S(2)}, u32[]{:S(2)}) collective-permute-start(bf16[48,1152]{1,0:T(8,128)(2,1)S(1)} %get-tuple-element.364), channel_id=1, source_target_pairs={{0,24},{2,26},{4,28},{6,30},{8,16},{10,18},{12,20},{14,22},{16,8},... | collective-permute-start | bytes 331784 | tf_op jit(solution)/shard_map/ppermute | solution.py:596
  601.8 12.4 %collective-permute-start.34 = (bf16[48,1920]{1,0:T(8,128)(2,1)S(1)}, bf16[48,1920]{1,0:T(8,128)(2,1)S(1)}, u32[]{:S(2)}, u32[]{:S(2)}) collective-permute-start(bf16[48,1920]{1,0:T(8,128)(2,1)S(1)} %fusion.14), channel_id=1, source_target_pairs={{0,1},{1,0},{2,3},{3,2},{4,5},{5,4},{6,7},{7,6},{8,9},{9,8},{10,11... | collective-permute-start | bytes 552968 | tf_op jit(solution)/shard_map/ppermute | solution.py:599
  602.1 10.0 %collective-permute-start.35 = (f32[1152]{0:T(1024)S(1)}, f32[1152]{0:T(1024)S(1)}, u32[]{:S(2)}, u32[]{:S(2)}) collective-permute-start(f32[1152]{0:T(1024)S(1)} %add_add_fusion.3), channel_id=1, source_target_pairs={{0,8},{2,10},{4,12},{6,14},{8,0},{10,2},{12,4},{14,6},{16,24},{18,... | collective-permute-start | bytes 13832 | tf_op jit(solution)/shard_map/ppermute | solution.py:596
  604.4 7.7 %collective-permute-start.36 = (f32[1152]{0:T(1024)S(1)}, f32[1152]{0:T(1024)S(1)}, u32[]{:S(2)}, u32[]{:S(2)}) collective-permute-start(f32[1152]{0:T(1024)S(1)} %add_add_fusion.2), channel_id=1, source_target_pairs={{0,16},{2,18},{4,20},{6,22},{8,24},{10,26},{12,28},{14,30},{16,0},... | collective-permute-start | bytes 13832 | tf_op jit(solution)/shard_map/ppermute | solution.py:596
  608.8 5.4 collective-permute-start.37
  611.8 4.8 collective-permute-start.38
  (36 other events, 250.8 us)
Sparse Core Ops, SparseCore 0:
  11.8 112.7 all-gather.4
  126.9 59.3 all-gather.6
  189.1 66.1 all-gather.8
  341.0 119.4 reduce-scatter.2
  473.2 65.8 reduce-scatter.4

commit v13 on v11

--- a/solution.py
+++ b/solution.py
@@ -9,7 +9,7 @@
 
 HEAD_SIZE = 64
 PAIR = 2 * HEAD_SIZE
-FORWARD_ROWS = 512
+FORWARD_ROWS = 1024
 BACKWARD_ROWS = 256
 ROW_TILE = 256
 FF_CHUNK = 1024
@@ -171,17 +171,18 @@
 
 def place_pieces(pieces, out_shape, targets, indices):
     def kernel(index_ref, *refs):
-        sources, out_ref, semaphores = refs[: len(pieces)], refs[-2], refs[-1]
+        sources, out_ref, held, semaphores = refs[: len(pieces)], *refs[-3:]
         copies = [
-            pltpu.make_async_copy(
-                source, out_ref.at[target(index_ref)], semaphores.at[number]
-            )
+            pltpu.make_async_copy(source, held.at[target(index_ref)], semaphores.at[number])
             for number, (source, target) in enumerate(zip(sources, targets))
         ]
         for copy in copies:
             copy.start()
         for copy in copies:
             copy.wait()
+        last = pltpu.make_async_copy(held, out_ref, semaphores.at[len(pieces)])
+        last.start()
+        last.wait()
 
     size = 2 * 2
     for extent in out_shape:
@@ -190,10 +191,13 @@
     return pl.pallas_call(
         kernel,
         in_specs=[pl.BlockSpec(memory_space=pltpu.SMEM)] + [anywhere] * len(pieces),
-        out_specs=pl.BlockSpec(memory_space=pltpu.VMEM),
+        out_specs=anywhere,
         out_shape=jax.ShapeDtypeStruct(out_shape, pieces[0].dtype),
-        scratch_shapes=[pltpu.SemaphoreType.DMA((len(pieces),))],
-        compiler_params=pltpu.CompilerParams(vmem_limit_bytes=32 << 20),
+        scratch_shapes=[
+            pltpu.VMEM(out_shape, pieces[0].dtype),
+            pltpu.SemaphoreType.DMA((len(pieces) + 1,)),
+        ],
+        compiler_params=pltpu.CompilerParams(vmem_limit_bytes=60 << 20),
         cost_estimate=estimate(0, size),
         name="place_pieces",
     )(indices, *pieces)
@@ -711,6 +715,7 @@
     }
     rows = joined[0][:, -side.shape[1] :].T.astype(single)
     spread_bias = rows[row_count : row_count + layers * up_pieces]
+    rows = rows[:row_count]
     spread_bias = spread_bias.reshape(layers, up_pieces, groups, row_unit).swapaxes(1, 2)
     all_up_bias = spread_bias.reshape(layers, 1, -1)
     cut_gains = norm_gains.size

time: 605 us -> 624 us (1.031)
  Pallas kernels: 336 us -> 351 us
  waiting for transfers between devices: 102 us -> 113 us
  local copies, waits for them, and re-layouts: 31.6 us -> 22.3 us
    ppermute x30, waiting for transfers between devices: 70.6 us -> 91.2 us  [across(): return lambda part: lax.ppermute(part, 'wide', pairs)]
    pallas_call x9, Pallas kernels: 6.1 us -> 25.1 us  [place_pieces(): pl.pallas_call(kernel, in_specs=[pl.BlockSpec(memory_space=pltpu.SMEM)] +...]
    all_gather x1, waiting for transfers between devices: 10.8 us -> 0.01 us  [per_device(): lax.all_gather(down_weight[layer], 'wide', axis=0, tiled=True)]
  transfers between devices with their start and end apart: 50 -> 50, of which waited for: 14 -> 16; matrix products, arithmetic and copies ran while one was open for 11% -> 9% of each run, Pallas kernels for 48% -> 49%
where the time goes in v13:
time: 624 us; the launch traced here: 613 us
  Pallas kernels  351 us (56%)
  waiting for transfers between devices  113 us (18%)
  starting transfers between devices  57.9 us (9%)
  other arithmetic  45.9 us (7%)
  local copies, waits for them, and re-layouts  22.3 us (4%)
  between operations  15.2 us (2%)
  blocking collectives  6.59 us (1%)
    pallas_call x8, Pallas kernels, row_tiled(): pl.pallas_call(kernel, grid=(length // ROW_TILE,), in_specs=in_specs, out...  140 us
    ppermute x30, waiting for transfers between devices, across(): return lambda part: lax.ppermute(part, 'wide', pairs)  91.2 us
    pallas_call x2, Pallas kernels, attend_backward(): pl.pallas_call(functools.partial(attend_grad_kernel, rows=BACKWARD_ROWS),...  74.8 us
    pallas_call x5, Pallas kernels, term_blocks(): pl.pallas_call(kernel, in_specs=[pl.BlockSpec(memory_space=pltpu.SMEM)] +...  63.1 us
    pallas_call x2, Pallas kernels, attend_forward(): pl.pallas_call(functools.partial(attend_kernel, rows=FORWARD_ROWS), grid=...  48 us
    ppermute x30, starting transfers between devices, across(): return lambda part: lax.ppermute(part, 'wide', pairs)  32.6 us
    pallas_call x9, Pallas kernels, place_pieces(): pl.pallas_call(kernel, in_specs=[pl.BlockSpec(memory_space=pltpu.SMEM)] +...  25.1 us
    ppermute x11, waiting for transfers between devices, beside_seq(): return lax.ppermute(part, 'seq', swap)  22.1 us
  transfers between devices with their start and end apart: 50, of which 16 were waited for; matrix products, arithmetic and copies ran while one was open for 9% of the time, Pallas kernels for 49%

profile of v13, /device:TPU:0, one launch (start us, length us, event | category | flops | bytes accessed | tf_op | source)
XLA Modules:
  0.0 612.6 jit_solution(9249596300394604825)
XLA Ops:
  14.7 4.1 collective-permute-start
  18.9 15.8 %collective-permute-done.refs_1_ = bf16[1,48,1536]{2,1,0:T(8,128)(2,1)S(1)} collective-permute-done((bf16[1,48,1536]{2,1,0:T(8,128)(2,1)S(1)}, bf16[1,48,1536]{2,1,0:T(8,128)(2,1)S(1)}, u32[]{:S(2)}, u32[]{:S(2)}) %collective-permute-start) | collective-permute-done | bytes 147488 | tf_op jit(solution)/shard_map/ppermute | solution.py:601
  34.6 7.4 %collective-permute-done.1.refs_1_ = bf16[1,96,768]{2,1,0:T(8,128)(2,1)S(1)} collective-permute-done((bf16[1,96,768]{2,1,0:T(8,128)(2,1)S(1)}, bf16[1,96,768]{2,1,0:T(8,128)(2,1)S(1)}, u32[]{:S(2)}, u32[]{:S(2)}) %collective-permute-start.1) | collective-permute-done | bytes 147488 | tf_op jit(solution)/shard_map/ppermute | solution.py:601
  45.6 6.6 %all_to_all.37 = s32[2,512,2]{1,2,0:T(2,128)S(1)} all-to-all(s32[2,512,2]{1,2,0:T(2,128)S(1)} %pad_add_fusion), channel_id=1, replica_groups=mesh['wide'=16,'seq'=2] {'seq'}, dimensions={0} | all-to-all | bytes 16384 | tf_op jit(solution)/shard_map/all_to_all | solution.py:592
  52.2 3.7 all-to-all-start
  58.0 18.3 %collective-permute-done.2.refs_1_ = bf16[2,48,1536]{2,1,0:T(8,128)(2,1)S(1)} collective-permute-done((bf16[2,48,1536]{2,1,0:T(8,128)(2,1)S(1)}, bf16[2,48,1536]{2,1,0:T(8,128)(2,1)S(1)}, u32[]{:S(2)}, u32[]{:S(2)}) %collective-permute-start.2) | collective-permute-done | bytes 294944 | tf_op jit(solution)/shard_map/ppermute | solution.py:601
  76.3 5.8 collective-permute-done.3.refs_1_
  93.4 9.1 %project.2 = (bf16[1024,768]{1,0:T(8,128)(2,1)}, bf16[1024,2304]{1,0:T(8,128)(2,1)}) custom-call(f32[1024,768]{1,0:T(8,128)} %convert_add_fusion.hidden_ref, f32[16,768]{1,0:T(8,128)} %copy.88.rows_ref, bf16[768,3200]{1,0:T(8,128)(2,1)} %all-gather.5.cloned.1.call-done.weight_ref.out_weight_ref), custom_call_target="tpu_custom_call" | custom-call | flops 226492416 | bytes 900096 | tf_op jit(solution)/shard_map/project/pallas_call | solution.py:235
  102.5 5.6 collective-permute-done.4.refs_1_
  116.6 2.8 fusion.2.bias_ref
  119.4 23.9 %attend_forward.2 = (bf16[1024,768]{1,0:T(8,128)(2,1)}, f32[6,2,1024]{2,1,0:T(2,128)}) custom-call(bf16[1024,2304]{1,0:T(8,128)(2,1)} %get-tuple-element.213.query_ref.key_ref.value_ref, bf16[1024,2304]{1,0:T(8,128)(2,1)} %get-tuple-element.213.query_ref.key_ref.value_ref, bf16[1024,2304]{1,0:T(8,128)(2,1)} %get-tuple-element.213.query_ref.key_ref.value_ref, ...), custom_call_target="tpu_custom_call" | custom-call | flops 805306368 | bytes 393216 | tf_op jit(solution)/shard_map/attend_forward/pallas_call | solution.py:68
  143.3 15.8 %collective-permute-done.7.refs_1_ = bf16[4,192,768]{2,1,0:T(8,128)(2,1)S(1)} collective-permute-done((bf16[4,192,768]{2,1,0:T(8,128)(2,1)S(1)}, bf16[4,192,768]{2,1,0:T(8,128)(2,1)S(1)}, u32[]{:S(2)}, u32[]{:S(2)}) %collective-permute-start.7) | collective-permute-done | bytes 1179680 | tf_op jit(solution)/shard_map/ppermute | solution.py:601
  160.1 3.2 place_pieces.15
  165.7 4.6 collective-permute-done.8.refs_2_
  172.4 4.7 place_pieces.17
  177.1 5.3 place_pieces.16
  182.3 24.2 %feed.2 = (f32[1024,768]{1,0:T(8,128)}, bf16[1024,768]{1,0:T(8,128)(2,1)}, bf16[1024,3072]{1,0:T(8,128)(2,1)}, bf16[1024,3072]{1,0:T(8,128)(2,1)}, f32[1024,768]{1,0:T(8,128)}) custom-call(bf16[1024,768]{1,0:T(8,128)(2,1)} %get-tuple-element.225.attended_ref.refs_2_, f32[1024,768]{1,0:T(8,128)} %convert_add_fusion.hidden_ref, f32[16,768]{1,0:T(8,128)} %copy.88.rows_ref, ...), custom_call_target="tpu_custom_call" | custom-call | flops 679477248 | bytes 2473728 | tf_op jit(solution)/shard_map/feed/pallas_call | solution.py:235
  206.5 9.0 %project.3 = (bf16[1024,768]{1,0:T(8,128)(2,1)}, bf16[1024,2304]{1,0:T(8,128)(2,1)}) custom-call(f32[1024,768]{1,0:T(8,128)} %get-tuple-element.229.hidden_ref, f32[16,768]{1,0:T(8,128)} %copy.88.rows_ref, bf16[768,6144]{1,0:T(8,128)(2,1)} %all-gather.7.cloned.1.call-done.weight_ref.out_weight_ref.up_ref), custom_call_target="tpu_custom_call" | custom-call | flops 226492416 | bytes 1182720 | tf_op jit(solution)/shard_map/project/pallas_call | solution.py:235
  215.5 3.7 all-to-all-start.2
  220.0 24.1 %attend_forward.3 = (bf16[1024,768]{1,0:T(8,128)(2,1)}, f32[6,2,1024]{2,1,0:T(2,128)}) custom-call(bf16[1024,2304]{1,0:T(8,128)(2,1)} %get-tuple-element.231.query_ref.key_ref.value_ref, bf16[1024,2304]{1,0:T(8,128)(2,1)} %get-tuple-element.231.query_ref.key_ref.value_ref, bf16[1024,2304]{1,0:T(8,128)(2,1)} %get-tuple-element.231.query_ref.key_ref.value_ref, ...), custom_call_target="tpu_custom_call" | custom-call | flops 805306368 | bytes 393216 | tf_op jit(solution)/shard_map/attend_forward/pallas_call | solution.py:68
  244.1 24.0 %feed.3 = (f32[1024,768]{1,0:T(8,128)}, bf16[1024,768]{1,0:T(8,128)(2,1)}, bf16[1024,3072]{1,0:T(8,128)(2,1)}, bf16[1024,3072]{1,0:T(8,128)(2,1)}, bf16[1024,768]{1,0:T(8,128)(2,1)}) custom-call(bf16[1024,768]{1,0:T(8,128)(2,1)} %get-tuple-element.233.attended_ref.refs_4_, f32[1024,768]{1,0:T(8,128)} %get-tuple-element.229.hidden_ref, ...), custom_call_target="tpu_custom_call" | custom-call | flops 679477248 | bytes 2952960 | tf_op jit(solution)/shard_map/feed/pallas_call | solution.py:235
  269.3 31.7 %feed_grad.2 = (bf16[1024,768]{1,0:T(8,128)(2,1)}, bf16[1024,3072]{1,0:T(8,128)(2,1)}, f32[1024,768]{1,0:T(8,128)}, bf16[1024,768]{1,0:T(8,128)(2,1)}, bf16[1024...) custom-call(bf16[1024,768]{1,0:T(8,128)(2,1)} %bitcast.214, ...), custom_call_target="tpu_custom_call" | custom-call | flops 679477248 | bytes 3052800 | tf_op jit(solution)/shard_map/feed_grad/pallas_call | solution.py:235
  301.0 19.7 %term_blocks.5 = bf16[16,48,6912]{2,1,0:T(8,128)(2,1)} custom-call(s32[1]{0:T(128)} %bitcast.21.core_ref, bf16[1024,3072]{1,0:T(8,128)(2,1)} %get-tuple-element.237.refs_0_, bf16[1024,768]{1,0:T(8,128)(2,1)} %get-tuple-element.238.refs_1_, bf16[1024,768]{1,0:T(8,128)(2,1)} %get-tuple-element.239.refs_2_, bf16[1024,3072]{1,0:T(8,128)(2,1)} %get-tuple-element.240.refs_3_, ...), custom_call_target="tpu_custom_call" | custom-call | flops 679477248 | bytes 1843200 | tf_op jit(solution)/shard_map/term_blocks/pallas_call | solution.py:559
  320.8 3.7 all-to-all-start.3
  324.5 37.4 %attend_backward.2.packed_grad_ref.refs_1_ = bf16[1024,2304]{1,0:T(8,128)(2,1)} custom-call(bf16[1024,2304]{1,0:T(8,128)(2,1)} %get-tuple-element.231.query_ref.key_ref.value_ref, bf16[1024,2304]{1,0:T(8,128)(2,1)} %get-tuple-element.231.query_ref.key_ref.value_ref, bf16[1024,2304]{1,0:T(8,128)(2,1)} %get-tuple-element.231.query_ref.key_ref.value_ref, ...), custom_call_target="tpu_custom_call" | custom-call | flops 2013265920 | bytes 786432 | tf_op jit(solution)/shard_map/attend_backward/pallas_call | solution.py:151
  361.9 11.1 %project_grad.2 = (f32[1024,768]{1,0:T(8,128)}, bf16[1024,768]{1,0:T(8,128)(2,1)}, f32[8,768]{1,0:T(8,128)}) custom-call(bf16[1024,2304]{1,0:T(8,128)(2,1)} %attend_backward.2.packed_grad_ref.refs_1_, f32[1024,768]{1,0:T(8,128)} %get-tuple-element.229.hidden_ref, f32[1024,768]{1,0:T(8,128)} %get-tuple-element.247.middle_grad_ref, f32[16,768]{1,0:T(8,128)} %copy.88.rows_ref, ...), custom_call_target="tpu_custom_call" | custom-call | flops 226492416 | bytes 1577472 | tf_op jit(solution)/shard_map/project_grad/pallas_call | solution.py:235
  373.0 12.2 %term_blocks.6 = (bf16[8,2,48,1536]{3,2,1,0:T(8,128)(2,1)}, bf16[8,2,48,1536]{3,2,1,0:T(8,128)(2,1)}) custom-call(s32[1]{0:T(128)} %bitcast.21.core_ref, bf16[1024,3072]{1,0:T(8,128)(2,1)} %get-tuple-element.249.refs_0_, bf16[1024,768]{1,0:T(8,128)(2,1)} %get-tuple-element.250.refs_1_), custom_call_target="tpu_custom_call" | custom-call | flops 301989888 | bytes 786432 | tf_op jit(solution)/shard_map/term_blocks/pallas_call | solution.py:559
  385.2 8.6 %term_blocks.7 = bf16[16,48,2304]{2,1,0:T(8,128)(2,1)} custom-call(s32[1]{0:T(128)} %bitcast.21.core_ref, bf16[1024,768]{1,0:T(8,128)(2,1)} %get-tuple-element.253.refs_0_, bf16[1024,2304]{1,0:T(8,128)(2,1)} %attend_backward.2.packed_grad_ref.refs_1_), custom_call_target="tpu_custom_call" | custom-call | flops 226492416 | bytes 614400 | tf_op jit(solution)/shard_map/term_blocks/pallas_call | solution.py:559
  393.8 3.0 fusion.5
  398.9 21.2 %feed_grad.3 = (bf16[1024,768]{1,0:T(8,128)(2,1)}, bf16[1024,3072]{1,0:T(8,128)(2,1)}, f32[1024,768]{1,0:T(8,128)}, bf16[1024,768]{1,0:T(8,128)(2,1)}, bf16[1024...) custom-call(f32[1024,768]{1,0:T(8,128)} %get-tuple-element.259.gradient_ref, ...), custom_call_target="tpu_custom_call" | custom-call | flops 679477248 | bytes 2573568 | tf_op jit(solution)/shard_map/feed_grad/pallas_call | solution.py:235
  420.1 5.5 collective-permute-done.12
  425.6 2.8 fusion.6
  428.4 12.8 %term_blocks.8 = (bf16[8,2,48,1920]{3,2,1,0:T(8,128)(2,1)}, bf16[8,2,48,1920]{3,2,1,0:T(8,128)(2,1)}) custom-call(s32[1]{0:T(128)} %bitcast.21.core_ref, bf16[1024,768]{1,0:T(8,128)(2,1)} %get-tuple-element.270.refs_0_, bf16[1024,3072]{1,0:T(8,128)(2,1)} %get-tuple-element.271.refs_1_, bf16[1024,768]{1,0:T(8,128)(2,1)} %get-tuple-element.225.attended_ref.refs_2_, ...), custom_call_target="tpu_custom_call" | custom-call | flops 377487360 | bytes 1056768 | tf_op jit(solution)/shard_map/term_blocks/pallas_call | solution.py:559
  441.3 5.6 collective-permute-done.13
  446.9 3.9 fusion.3
  456.2 2.6 collective-permute-start.14
  459.4 37.4 %attend_backward.3.refs_1_.packed_grad_ref = bf16[1024,2304]{1,0:T(8,128)(2,1)} custom-call(bf16[1024,2304]{1,0:T(8,128)(2,1)} %get-tuple-element.213.query_ref.key_ref.value_ref, bf16[1024,2304]{1,0:T(8,128)(2,1)} %get-tuple-element.213.query_ref.key_ref.value_ref, bf16[1024,2304]{1,0:T(8,128)(2,1)} %get-tuple-element.213.query_ref.key_ref.value_ref, ...), custom_call_target="tpu_custom_call" | custom-call | flops 2013265920 | bytes 786432 | tf_op jit(solution)/shard_map/attend_backward/pallas_call | solution.py:151
  496.8 9.8 %term_blocks.9 = (bf16[8,2,48,1152]{3,2,1,0:T(8,128)(2,1)}, bf16[8,2,48,1152]{3,2,1,0:T(8,128)(2,1)}) custom-call(s32[1]{0:T(128)} %bitcast.21.core_ref, bf16[1024,768]{1,0:T(8,128)(2,1)} %get-tuple-element.290.refs_0_, bf16[1024,2304]{1,0:T(8,128)(2,1)} %attend_backward.3.refs_1_.packed_grad_ref), custom_call_target="tpu_custom_call" | custom-call | flops 226492416 | bytes 614400 | tf_op jit(solution)/shard_map/term_blocks/pallas_call | solution.py:559
  506.7 2.8 fusion.22
  509.5 2.6 fusion.4
  521.1 3.0 collective-permute-start.20
  524.2 10.1 %project_grad.3 = (bf16[1024,768]{1,0:T(8,128)(2,1)}, f32[8,768]{1,0:T(8,128)}) custom-call(bf16[1024,2304]{1,0:T(8,128)(2,1)} %attend_backward.3.refs_1_.packed_grad_ref, f32[1024,768]{1,0:T(8,128)} %convert_add_fusion.hidden_ref, f32[1024,768]{1,0:T(8,128)} %get-tuple-element.298.middle_grad_ref, f32[16,768]{1,0:T(8,128)} %copy.88.rows_ref, ...), custom_call_target="tpu_custom_call" | custom-call | flops 226492416 | bytes 1098240 | tf_op jit(solution)/shard_map/project_grad/pallas_call | solution.py:235
  549.4 3.7 all-to-all-start.4
  556.8 3.0 collective-permute-start.28
  561.7 14.9 %collective-permute-done.24 = bf16[48,1536]{1,0:T(8,128)(2,1)S(1)} collective-permute-done((bf16[48,1536]{1,0:T(8,128)(2,1)}, bf16[48,1536]{1,0:T(8,128)(2,1)S(1)}, u32[]{:S(2)}, u32[]{:S(2)}) %collective-permute-start.24) | collective-permute-done | bytes 147488 | tf_op jit(solution)/shard_map/ppermute | solution.py:604
  581.2 3.0 collective-permute-start.34
  588.2 3.1 collective-permute-done.33
  594.2 2.5 collective-permute-done.38
  (273 shorter events, 98.1 us)
Async XLA Ops:
  7.2 84.5 %all-gather.5.cloned.1.call-start = ((), (), s32[]{:S(2)}) async-start(), calls=%async_computation.7 | async-start | bytes 5222400 | tf_op jit(solution)/shard_map/all_gather | solution.py:711
  12.6 193.9 %all-gather.7.cloned.1.call-start = ((), (), s32[]{:S(2)}) async-start(), calls=%async_computation.8 | async-start | bytes 10027008 | tf_op jit(solution)/shard_map/all_gather | solution.py:711
  13.7 230.4 %all-gather.9.cloned.1.call-start = ((), (), s32[]{:S(2)}) async-start(), calls=%async_computation.11 | async-start | bytes 5013504 | tf_op jit(solution)/shard_map/all_gather | solution.py:713
  14.7 20.0 %collective-permute-start = (bf16[1,48,1536]{2,1,0:T(8,128)(2,1)S(1)}, bf16[1,48,1536]{2,1,0:T(8,128)(2,1)S(1)}, u32[]{:S(2)}, u32[]{:S(2)}) collective-permute-start(bf16[1,48,1536]{2,1,0:T(8,128)(2,1)S(1)} %constant_dynamic-slice_fusion.21.refs_0_), channel_id=1, source_target_pairs={{0,16},{2,18},{4,20},{6,22},{8,24},{10,26},{12,28},{14,30},{16,0},... | collective-permute-start | bytes 442376 | tf_op jit(solution)/shard_map/ppermute | solution.py:601
  18.8 23.2 %collective-permute-start.1 = (bf16[1,96,768]{2,1,0:T(8,128)(2,1)S(1)}, bf16[1,96,768]{2,1,0:T(8,128)(2,1)S(1)}, u32[]{:S(2)}, u32[]{:S(2)}) collective-permute-start(bf16[1,96,768]{2,1,0:T(8,128)(2,1)S(1)} %constant_dynamic-slice_fusion.20.refs_0_), channel_id=1, source_target_pairs={{0,16},{2,18},{4,20},{6,22},{8,24},{10,26},{12,28},{14,30},{16,0},... | collective-permute-start | bytes 442376 | tf_op jit(solution)/shard_map/ppermute | solution.py:601
  52.2 37.4 %all-to-all-start = ((bf16[2,512,768]{2,1,0:T(8,128)(2,1)}), bf16[2,512,768]{2,1,0:T(8,128)(2,1)S(1)}, u32[]{:S(2)}, u32[]{:S(2)}) async-start(bf16[2,512,768]{2,1,0:T(8,128)(2,1)} %param.12), calls=%async_computation | async-start | bytes 3145728 | tf_op jit(solution)/shard_map/all_to_all | solution.py:592
  55.9 20.4 %collective-permute-start.2 = (bf16[2,48,1536]{2,1,0:T(8,128)(2,1)S(1)}, bf16[2,48,1536]{2,1,0:T(8,128)(2,1)S(1)}, u32[]{:S(2)}, u32[]{:S(2)}) collective-permute-start(bf16[2,48,1536]{2,1,0:T(8,128)(2,1)S(1)} %bitcast.247), channel_id=1, source_target_pairs={{0,8},{2,10},{4,12},{6,14},{8,0},{10,2},{12,4},{14,6},{16,24},{18,... | collective-permute-start | bytes 884744 | tf_op jit(solution)/shard_map/ppermute | solution.py:601
  56.6 25.5 %collective-permute-start.3 = (bf16[2,96,768]{2,1,0:T(8,128)(2,1)S(1)}, bf16[2,96,768]{2,1,0:T(8,128)(2,1)S(1)}, u32[]{:S(2)}, u32[]{:S(2)}) collective-permute-start(bf16[2,96,768]{2,1,0:T(8,128)(2,1)S(1)} %bitcast.249), channel_id=1, source_target_pairs={{0,8},{2,10},{4,12},{6,14},{8,0},{10,2},{12,4},{14,6},{16,24},{18,... | collective-permute-start | bytes 884744 | tf_op jit(solution)/shard_map/ppermute | solution.py:601
  86.6 21.4 %collective-permute-start.4 = (bf16[4,48,1536]{2,1,0:T(8,128)(2,1)}, bf16[4,48,1536]{2,1,0:T(8,128)(2,1)S(1)}, u32[]{:S(2)}, u32[]{:S(2)}) collective-permute-start(bf16[4,48,1536]{2,1,0:T(8,128)(2,1)} %bitcast.231), channel_id=1, source_target_pairs={{0,4},{2,6},{4,0},{6,2},{8,12},{10,14},{12,8},{14,10},{16,20},{18,... | collective-permute-start | bytes 1769480 | tf_op jit(solution)/shard_map/ppermute | solution.py:601
  88.1 19.9 %collective-permute-start.5 = (bf16[4,96,768]{2,1,0:T(8,128)(2,1)}, bf16[4,96,768]{2,1,0:T(8,128)(2,1)S(1)}, u32[]{:S(2)}, u32[]{:S(2)}) collective-permute-start(bf16[4,96,768]{2,1,0:T(8,128)(2,1)} %bitcast.229), channel_id=1, source_target_pairs={{0,1},{1,0},{2,3},{3,2},{4,5},{5,4},{6,7},{7,6},{8,9},{9,8},{10,11... | collective-permute-start | bytes 1769480 | tf_op jit(solution)/shard_map/ppermute | solution.py:604
  113.6 29.7 %collective-permute-start.6 = (bf16[8,48,1536]{2,1,0:T(8,128)(2,1)}, bf16[8,48,1536]{2,1,0:T(8,128)(2,1)S(1)}, u32[]{:S(2)}, u32[]{:S(2)}) collective-permute-start(bf16[8,48,1536]{2,1,0:T(8,128)(2,1)} %bitcast.215), channel_id=1, source_target_pairs={{0,1},{1,0},{2,3},{3,2},{4,5},{5,4},{6,7},{7,6},{8,9},{9,8},{10,11... | collective-permute-start | bytes 3538952 | tf_op jit(solution)/shard_map/ppermute | solution.py:604
  115.1 44.0 %collective-permute-start.7 = (bf16[4,192,768]{2,1,0:T(8,128)(2,1)S(1)}, bf16[4,192,768]{2,1,0:T(8,128)(2,1)S(1)}, u32[]{:S(2)}, u32[]{:S(2)}) collective-permute-start(bf16[4,192,768]{2,1,0:T(8,128)(2,1)S(1)} %bitcast.219), channel_id=1, source_target_pairs={{0,4},{2,6},{4,0},{6,2},{8,12},{10,14},{12,8},{14,10},{16,20},{18,... | collective-permute-start | bytes 3538952 | tf_op jit(solution)/shard_map/ppermute | solution.py:601
  163.3 9.1 %collective-permute-start.10 = (bf16[8,192,768]{2,1,0:T(8,128)(2,1)}, bf16[8,192,768]{2,1,0:T(8,128)(2,1)}, u32[]{:S(2)}, u32[]{:S(2)}) collective-permute-start(bf16[8,192,768]{2,1,0:T(8,128)(2,1)} %bitcast.212), channel_id=1, source_target_pairs={{0,2},{2,0},{4,6},{6,4},{8,10},{10,8},{12,14},{14,12},{16,18},{18,... | collective-permute-start | bytes 7077896 | tf_op jit(solution)/shard_map/ppermute | solution.py:601
  163.4 6.9 %collective-permute-start.8 = (bf16[8,48,1536]{2,1,0:T(8,128)(2,1)S(1)}, bf16[8,48,1536]{2,1,0:T(8,128)(2,1)}, u32[]{:S(2)}, u32[]{:S(2)}) collective-permute-start(bf16[8,48,1536]{2,1,0:T(8,128)(2,1)S(1)} %bitcast.217), channel_id=1, source_target_pairs={{0,2},{2,0},{4,6},{6,4},{8,10},{10,8},{12,14},{14,12},{16,18},{18,... | collective-permute-start | bytes 3538952 | tf_op jit(solution)/shard_map/ppermute | solution.py:601
  163.9 8.5 %collective-permute-start.9 = (bf16[8,48,1536]{2,1,0:T(8,128)(2,1)S(1)}, bf16[8,48,1536]{2,1,0:T(8,128)(2,1)}, u32[]{:S(2)}, u32[]{:S(2)}) collective-permute-start(bf16[8,48,1536]{2,1,0:T(8,128)(2,1)S(1)} %collective-permute-done.6.refs_1_), channel_id=1, source_target_pairs={{0,2},{2,0},{4,6},{6,4},{8,10},{10,8},{12,14},{14,12},{16,18},{18,... | collective-permute-start | bytes 3538952 | tf_op jit(solution)/shard_map/ppermute | solution.py:601
  215.5 52.6 %all-to-all-start.2 = ((bf16[2,512,768]{2,1,0:T(8,128)(2,1)}), bf16[2,512,768]{2,1,0:T(8,128)(2,1)S(1)}, u32[]{:S(2)}, u32[]{:S(2)}) async-start(bf16[2,512,768]{2,1,0:T(8,128)(2,1)} %param.16), calls=%async_computation.2 | async-start | bytes 3145728 | tf_op jit(solution)/shard_map/all_to_all | solution.py:592
  219.2 239.6 %reduce-scatter.3.cloned.1.call-start = ((), (), s32[]{:S(2)}) async-start(), calls=%async_computation.9 | async-start | bytes 11280384 | tf_op jit(solution)/shard_map/reduce_scatter | solution.py:607
  320.8 41.1 %all-to-all-start.3 = ((bf16[2,512,768]{2,1,0:T(8,128)(2,1)}), bf16[2,512,768]{2,1,0:T(8,128)(2,1)S(1)}, u32[]{:S(2)}, u32[]{:S(2)}) async-start(bf16[2,512,768]{2,1,0:T(8,128)(2,1)} %bitcast.31), calls=%async_computation.3 | async-start | bytes 3145728 | tf_op jit(solution)/shard_map/all_to_all | solution.py:777
  324.5 213.9 %reduce-scatter.5.cloned.1.call-start = ((), (), s32[]{:S(2)}) async-start(), calls=%async_computation.10 | async-start | bytes 3760128 | tf_op jit(solution)/shard_map/reduce_scatter | solution.py:607
  385.2 8.7 %collective-permute-start.11 = (bf16[8,2,48,1536]{3,2,1,0:T(8,128)(2,1)}, bf16[8,2,48,1536]{3,2,1,0:T(8,128)(2,1)}, u32[]{:S(2)}, u32[]{:S(2)}) collective-permute-start(bf16[8,2,48,1536]{3,2,1,0:T(8,128)(2,1)} %get-tuple-element.255), channel_id=1, source_target_pairs={{0,2},{2,0},{4,6},{6,4},{8,10},{10,8},{12,14},{14,12},{16,18},{18,... | collective-permute-start | bytes 7077896 | tf_op jit(solution)/shard_map/ppermute | solution.py:601
  396.8 28.8 %collective-permute-start.12 = (bf16[2,2,2,48,1536]{4,3,2,1,0:T(8,128)(2,1)}, bf16[2,2,2,48,1536]{4,3,2,1,0:T(8,128)(2,1)S(1)}, u32[]{:S(2)}, u32[]{:S(2)}) collective-permute-start(bf16[2,2,2,48,1536]{4,3,2,1,0:T(8,128)(2,1)} %fusion.5), channel_id=1, source_target_pairs={{0,1},{1,0},{2,3},{3,2},{4,5},{5,4},{6,7},{7,6},{8,9},{9,8},{10,11... | collective-permute-start | bytes 3538952 | tf_op jit(solution)/shard_map/ppermute | solution.py:604
  441.3 5.7 collective-permute-start.13
  450.9 55.8 %collective-permute-start.15 = (bf16[2,2,2,48,1920]{4,3,2,1,0:T(8,128)(2,1)}, bf16[2,2,2,48,1920]{4,3,2,1,0:T(8,128)(2,1)S(1)}, u32[]{:S(2)}, u32[]{:S(2)}) collective-permute-start(bf16[2,2,2,48,1920]{4,3,2,1,0:T(8,128)(2,1)} %fusion.3), channel_id=1, source_target_pairs={{0,1},{1,0},{2,3},{3,2},{4,5},{5,4},{6,7},{7,6},{8,9},{9,8},{10,11... | collective-permute-start | bytes 4423688 | tf_op jit(solution)/shard_map/ppermute | solution.py:604
  456.2 50.5 %collective-permute-start.14 = (bf16[2,2,48,1536]{3,2,1,0:T(8,128)(2,1)}, bf16[2,2,48,1536]{3,2,1,0:T(8,128)(2,1)}, u32[]{:S(2)}, u32[]{:S(2)}) collective-permute-start(bf16[2,2,48,1536]{3,2,1,0:T(8,128)(2,1)} %fusion.6), channel_id=1, source_target_pairs={{0,4},{2,6},{4,0},{6,2},{8,12},{10,14},{12,8},{14,10},{16,20},{18,... | collective-permute-start | bytes 1769480 | tf_op jit(solution)/shard_map/ppermute | solution.py:601
  458.8 47.9 %collective-permute-start.16 = (bf16[48,6912]{1,0:T(8,128)(2,1)}, bf16[48,6912]{1,0:T(8,128)(2,1)}, u32[]{:S(2)}, u32[]{:S(2)}) collective-permute-start(bf16[48,6912]{1,0:T(8,128)(2,1)} %reduce-scatter.3.cloned.1.call-done), channel_id=1, source_target_pairs={{0,1},{1,0},{2,3},{3,2},{4,5},{5,4},{6,7},{7,6},{8,9},{9,8},{10,11... | collective-permute-start | bytes 1990664 | tf_op jit(solution)/shard_map/ppermute | solution.py:604
  517.2 23.3 %collective-permute-start.22 = (bf16[2,2,2,48,1152]{4,3,2,1,0:T(8,128)(2,1)}, bf16[2,2,2,48,1152]{4,3,2,1,0:T(8,128)(2,1)}, u32[]{:S(2)}, u32[]{:S(2)}) collective-permute-start(bf16[2,2,2,48,1152]{4,3,2,1,0:T(8,128)(2,1)} %fusion.7), channel_id=1, source_target_pairs={{0,1},{1,0},{2,3},{3,2},{4,5},{5,4},{6,7},{7,6},{8,9},{9,8},{10,11... | collective-permute-start | bytes 2654216 | tf_op jit(solution)/shard_map/ppermute | solution.py:604
  519.7 18.7 %collective-permute-start.21 = (bf16[2,2,48,1920]{3,2,1,0:T(8,128)(2,1)}, bf16[2,2,48,1920]{3,2,1,0:T(8,128)(2,1)S(1)}, u32[]{:S(2)}, u32[]{:S(2)}) collective-permute-start(bf16[2,2,48,1920]{3,2,1,0:T(8,128)(2,1)} %fusion.4), channel_id=1, source_target_pairs={{0,4},{2,6},{4,0},{6,2},{8,12},{10,14},{12,8},{14,10},{16,20},{18,... | collective-permute-start | bytes 2211848 | tf_op jit(solution)/shard_map/ppermute | solution.py:601
  519.7 18.6 %collective-permute-start.18 = (bf16[48,1536]{1,0:T(8,128)(2,1)}, bf16[48,1536]{1,0:T(8,128)(2,1)}, u32[]{:S(2)}, u32[]{:S(2)}) collective-permute-start(bf16[48,1536]{1,0:T(8,128)(2,1)} %get-tuple-element.306), channel_id=1, source_target_pairs={{0,8},{2,10},{4,12},{6,14},{8,0},{10,2},{12,4},{14,6},{16,24},{18,... | collective-permute-start | bytes 442376 | tf_op jit(solution)/shard_map/ppermute | solution.py:601
  519.7 18.6 %collective-permute-start.19 = (bf16[48,1536]{1,0:T(8,128)(2,1)}, bf16[48,1536]{1,0:T(8,128)(2,1)}, u32[]{:S(2)}, u32[]{:S(2)}) collective-permute-start(bf16[48,1536]{1,0:T(8,128)(2,1)} %get-tuple-element.307), channel_id=1, source_target_pairs={{0,16},{2,18},{4,20},{6,22},{8,24},{10,26},{12,28},{14,30},{16,0},... | collective-permute-start | bytes 442376 | tf_op jit(solution)/shard_map/ppermute | solution.py:601
  521.1 17.2 %collective-permute-start.20 = (bf16[48,1536]{1,0:T(8,128)(2,1)}, bf16[48,1536]{1,0:T(8,128)(2,1)}, u32[]{:S(2)}, u32[]{:S(2)}) collective-permute-start(bf16[48,1536]{1,0:T(8,128)(2,1)} %get-tuple-element.308), channel_id=1, source_target_pairs={{0,24},{2,26},{4,28},{6,30},{8,16},{10,18},{12,20},{14,22},{16,8},... | collective-permute-start | bytes 442376 | tf_op jit(solution)/shard_map/ppermute | solution.py:601
  538.3 17.1 %collective-permute-start.29 = (f32[2,2,1152]{2,1,0:T(2,128)}, f32[2,2,1152]{2,1,0:T(2,128)}, u32[]{:S(2)}, u32[]{:S(2)}) collective-permute-start(f32[2,2,1152]{2,1,0:T(2,128)} %bitcast.202), channel_id=1, source_target_pairs={{0,2},{2,0},{4,6},{6,4},{8,10},{10,8},{12,14},{14,12},{16,18},{18,... | collective-permute-start | bytes 55304 | tf_op jit(solution)/shard_map/ppermute | solution.py:601
  538.4 18.4 %collective-permute-start.30 = (f32[2,2,1152]{2,1,0:T(2,128)}, f32[2,2,1152]{2,1,0:T(2,128)S(1)}, u32[]{:S(2)}, u32[]{:S(2)}) collective-permute-start(f32[2,2,1152]{2,1,0:T(2,128)} %bitcast.201), channel_id=1, source_target_pairs={{0,4},{2,6},{4,0},{6,2},{8,12},{10,14},{12,8},{14,10},{16,20},{18,... | collective-permute-start | bytes 55304 | tf_op jit(solution)/shard_map/ppermute | solution.py:601
  540.5 19.4 %collective-permute-start.31 = (f32[2,2,1152]{2,1,0:T(2,128)}, f32[2,2,1152]{2,1,0:T(2,128)}, u32[]{:S(2)}, u32[]{:S(2)}) collective-permute-start(f32[2,2,1152]{2,1,0:T(2,128)} %bitcast.200), channel_id=1, source_target_pairs={{0,6},{2,4},{4,2},{6,0},{8,14},{10,12},{12,10},{14,8},{16,22},{18,... | collective-permute-start | bytes 55304 | tf_op jit(solution)/shard_map/ppermute | solution.py:601
  542.8 12.7 %collective-permute-start.23 = (bf16[2,2,48,1152]{3,2,1,0:T(8,128)(2,1)}, bf16[2,2,48,1152]{3,2,1,0:T(8,128)(2,1)}, u32[]{:S(2)}, u32[]{:S(2)}) collective-permute-start(bf16[2,2,48,1152]{3,2,1,0:T(8,128)(2,1)} %fusion.8), channel_id=1, source_target_pairs={{0,4},{2,6},{4,0},{6,2},{8,12},{10,14},{12,8},{14,10},{16,20},{18,... | collective-permute-start | bytes 1327112 | tf_op jit(solution)/shard_map/ppermute | solution.py:601
  549.0 27.6 %collective-permute-start.25 = (bf16[48,2304]{1,0:T(8,128)(2,1)}, bf16[48,2304]{1,0:T(8,128)(2,1)}, u32[]{:S(2)}, u32[]{:S(2)}) collective-permute-start(bf16[48,2304]{1,0:T(8,128)(2,1)} %reduce-scatter.5.cloned.1.call-done), channel_id=1, source_target_pairs={{0,1},{1,0},{2,3},{3,2},{4,5},{5,4},{6,7},{7,6},{8,9},{9,8},{10,11... | collective-permute-start | bytes 663560 | tf_op jit(solution)/shard_map/ppermute | solution.py:604
  549.4 54.4 %all-to-all-start.4 = ((bf16[2,512,768]{2,1,0:T(8,128)(2,1)}), bf16[2,512,768]{2,1,0:T(8,128)(2,1)S(1)}, u32[]{:S(2)}, u32[]{:S(2)}) async-start(bf16[2,512,768]{2,1,0:T(8,128)(2,1)} %bitcast.245), calls=%async_computation.6 | async-start | bytes 3145728 | tf_op jit(solution)/shard_map/all_to_all | solution.py:777
  555.5 21.2 %collective-permute-start.26 = (bf16[48,1920]{1,0:T(8,128)(2,1)}, bf16[48,1920]{1,0:T(8,128)(2,1)S(1)}, u32[]{:S(2)}, u32[]{:S(2)}) collective-permute-start(bf16[48,1920]{1,0:T(8,128)(2,1)} %get-tuple-element.328), channel_id=1, source_target_pairs={{0,8},{2,10},{4,12},{6,14},{8,0},{10,2},{12,4},{14,6},{16,24},{18,... | collective-permute-start | bytes 552968 | tf_op jit(solution)/shard_map/ppermute | solution.py:601
  555.5 21.2 %collective-permute-start.27 = (bf16[48,1920]{1,0:T(8,128)(2,1)}, bf16[48,1920]{1,0:T(8,128)(2,1)S(1)}, u32[]{:S(2)}, u32[]{:S(2)}) collective-permute-start(bf16[48,1920]{1,0:T(8,128)(2,1)} %get-tuple-element.329), channel_id=1, source_target_pairs={{0,16},{2,18},{4,20},{6,22},{8,24},{10,26},{12,28},{14,30},{16,0},... | collective-permute-start | bytes 552968 | tf_op jit(solution)/shard_map/ppermute | solution.py:601
  556.8 19.8 %collective-permute-start.28 = (bf16[48,1920]{1,0:T(8,128)(2,1)}, bf16[48,1920]{1,0:T(8,128)(2,1)S(1)}, u32[]{:S(2)}, u32[]{:S(2)}) collective-permute-start(bf16[48,1920]{1,0:T(8,128)(2,1)} %get-tuple-element.330), channel_id=1, source_target_pairs={{0,24},{2,26},{4,28},{6,30},{8,16},{10,18},{12,20},{14,22},{16,8},... | collective-permute-start | bytes 552968 | tf_op jit(solution)/shard_map/ppermute | solution.py:601
  559.9 16.8 %collective-permute-start.24 = (bf16[48,1536]{1,0:T(8,128)(2,1)}, bf16[48,1536]{1,0:T(8,128)(2,1)S(1)}, u32[]{:S(2)}, u32[]{:S(2)}) collective-permute-start(bf16[48,1536]{1,0:T(8,128)(2,1)} %fusion.21), channel_id=1, source_target_pairs={{0,1},{1,0},{2,3},{3,2},{4,5},{5,4},{6,7},{7,6},{8,9},{9,8},{10,11... | collective-permute-start | bytes 442376 | tf_op jit(solution)/shard_map/ppermute | solution.py:604
  579.8 7.1 %collective-permute-start.32 = (bf16[48,1152]{1,0:T(8,128)(2,1)S(1)}, bf16[48,1152]{1,0:T(8,128)(2,1)S(1)}, u32[]{:S(2)}, u32[]{:S(2)}) collective-permute-start(bf16[48,1152]{1,0:T(8,128)(2,1)S(1)} %get-tuple-element.342), channel_id=1, source_target_pairs={{0,8},{2,10},{4,12},{6,14},{8,0},{10,2},{12,4},{14,6},{16,24},{18,... | collective-permute-start | bytes 331784 | tf_op jit(solution)/shard_map/ppermute | solution.py:601
  579.8 11.5 %collective-permute-start.33 = (bf16[48,1152]{1,0:T(8,128)(2,1)S(1)}, bf16[48,1152]{1,0:T(8,128)(2,1)S(1)}, u32[]{:S(2)}, u32[]{:S(2)}) collective-permute-start(bf16[48,1152]{1,0:T(8,128)(2,1)S(1)} %get-tuple-element.343), channel_id=1, source_target_pairs={{0,16},{2,18},{4,20},{6,22},{8,24},{10,26},{12,28},{14,30},{16,0},... | collective-permute-start | bytes 331784 | tf_op jit(solution)/shard_map/ppermute | solution.py:601
  581.2 11.5 %collective-permute-start.34 = (bf16[48,1152]{1,0:T(8,128)(2,1)S(1)}, bf16[48,1152]{1,0:T(8,128)(2,1)S(1)}, u32[]{:S(2)}, u32[]{:S(2)}) collective-permute-start(bf16[48,1152]{1,0:T(8,128)(2,1)S(1)} %get-tuple-element.344), channel_id=1, source_target_pairs={{0,24},{2,26},{4,28},{6,30},{8,16},{10,18},{12,20},{14,22},{16,8},... | collective-permute-start | bytes 331784 | tf_op jit(solution)/shard_map/ppermute | solution.py:601
  584.2 12.6 %collective-permute-start.35 = (bf16[48,1920]{1,0:T(8,128)(2,1)S(1)}, bf16[48,1920]{1,0:T(8,128)(2,1)S(1)}, u32[]{:S(2)}, u32[]{:S(2)}) collective-permute-start(bf16[48,1920]{1,0:T(8,128)(2,1)S(1)} %fusion.13), channel_id=1, source_target_pairs={{0,1},{1,0},{2,3},{3,2},{4,5},{5,4},{6,7},{7,6},{8,9},{9,8},{10,11... | collective-permute-start | bytes 552968 | tf_op jit(solution)/shard_map/ppermute | solution.py:604
  584.5 9.7 %collective-permute-start.36 = (f32[1152]{0:T(1024)S(1)}, f32[1152]{0:T(1024)S(1)}, u32[]{:S(2)}, u32[]{:S(2)}) collective-permute-start(f32[1152]{0:T(1024)S(1)} %add_add_fusion.3), channel_id=1, source_target_pairs={{0,8},{2,10},{4,12},{6,14},{8,0},{10,2},{12,4},{14,6},{16,24},{18,... | collective-permute-start | bytes 13832 | tf_op jit(solution)/shard_map/ppermute | solution.py:601
  586.9 7.4 %collective-permute-start.37 = (f32[1152]{0:T(1024)S(1)}, f32[1152]{0:T(1024)S(1)}, u32[]{:S(2)}, u32[]{:S(2)}) collective-permute-start(f32[1152]{0:T(1024)S(1)} %add_add_fusion.2), channel_id=1, source_target_pairs={{0,16},{2,18},{4,20},{6,22},{8,24},{10,26},{12,28},{14,30},{16,0},... | collective-permute-start | bytes 13832 | tf_op jit(solution)/shard_map/ppermute | solution.py:601
  591.3 5.4 collective-permute-start.38
  593.8 5.2 collective-permute-start.39
  (39 other events, 349.5 us)
Sparse Core Ops, SparseCore 0:
  12.8 65.5 all-gather.4
  80.7 102.7 all-gather.6
  185.8 51.5 all-gather.8
  320.9 120.7 reduce-scatter.2
  452.8 67.0 reduce-scatter.4

commit v14 on v10

--- a/solution.py
+++ b/solution.py
@@ -9,7 +9,7 @@
 
 HEAD_SIZE = 64
 PAIR = 2 * HEAD_SIZE
-FORWARD_ROWS = 512
+FORWARD_ROWS = 1024
 BACKWARD_ROWS = 256
 ROW_TILE = 256
 FF_CHUNK = 1024
@@ -716,9 +716,10 @@
         begin(gather_rows(down_weight[0]), functools.partial(downs.__setitem__, 0)),
     ]
     marks = jnp.stack([segment_ids, pad_mask], axis=2)
-    for _ in chip_bits[1:]:
+    time_embed, marks = advance((time_embed, marks), *fetches)
+    marks = whole_sequence(marks)
+    for _ in chip_bits[2:]:
         time_embed, marks = advance((time_embed, marks), *fetches)
-    marks = whole_sequence(marks)
     doc, pad = marks[:, 0], marks[:, 1]
     positions = jnp.arange(doc.shape[0])
     allowed = (doc[:, None] == doc[None, :]) & (

time: 601 us -> 605 us (level)
  blocking collectives: 25.1 us -> 6.45 us
  waiting for transfers between devices: 86.1 us -> 102 us
  Pallas kernels: 323 us -> 332 us
  starting transfers between devices: 63.7 us -> 56.1 us
    all_to_all x1, blocking collectives: 25.1 us -> 6.45 us  [whole_sequence(): lax.all_to_all(part, 'seq', split_axis=0, concat_axis=1, tiled=True)[0]]
    pallas_call x8, Pallas kernels: 130 us -> 141 us  [row_tiled(): pl.pallas_call(kernel, grid=(length // ROW_TILE,), in_specs=in_specs, out...]
    all_gather x1, waiting for transfers between devices: 0.01 us -> 9.7 us  [per_device(): lax.all_gather(down_weight[layer], 'wide', axis=0, tiled=True)]
    ppermute x30, starting transfers between devices: 38.2 us -> 31.2 us  [across(): return lambda part: lax.ppermute(part, 'wide', pairs)]
  transfers between devices with their start and end apart: 50 -> 50, of which waited for: 13 -> 14; matrix products, arithmetic and copies ran while one was open for 11% -> 11% of each run, Pallas kernels for 47% -> 47%
where the time goes in v14:
time: 605 us; the launch traced here: 594 us
  Pallas kernels  332 us (55%)
  waiting for transfers between devices  102 us (17%)
  starting transfers between devices  56.1 us (9%)
  other arithmetic  46.9 us (8%)
  local copies, waits for them, and re-layouts  34.6 us (6%)
  between operations  15.1 us (2%)
  blocking collectives  6.45 us (1%)
    pallas_call x8, Pallas kernels, row_tiled(): pl.pallas_call(kernel, grid=(length // ROW_TILE,), in_specs=in_specs, out...  141 us
    pallas_call x2, Pallas kernels, attend_backward(): pl.pallas_call(functools.partial(attend_grad_kernel, rows=BACKWARD_ROWS),...  74.7 us
    ppermute x30, waiting for transfers between devices, across(): return lambda part: lax.ppermute(part, 'wide', pairs)  71.7 us
    pallas_call x5, Pallas kernels, term_blocks(): pl.pallas_call(kernel, in_specs=[pl.BlockSpec(memory_space=pltpu.SMEM)] +...  63 us
    pallas_call x2, Pallas kernels, attend_forward(): pl.pallas_call(functools.partial(attend_kernel, rows=FORWARD_ROWS), grid=...  47.7 us
    ppermute x30, starting transfers between devices, across(): return lambda part: lax.ppermute(part, 'wide', pairs)  31.2 us
    ppermute x11, waiting for transfers between devices, beside_seq(): return lax.ppermute(part, 'seq', swap)  20.9 us
    convert_element_type x6, other arithmetic, reduce_group(): total_of([side_of(part, 1 - mine, axis) for part in addends]).astype(half)  15.8 us
  transfers between devices with their start and end apart: 50, of which 14 were waited for; matrix products, arithmetic and copies ran while one was open for 11% of the time, Pallas kernels for 47%

profile of v14, /device:TPU:0, one launch (start us, length us, event | category | flops | bytes accessed | tf_op | source)
XLA Modules:
  0.0 593.9 jit_solution(9820597303958997529)
XLA Ops:
  14.6 4.1 collective-permute-start
  18.7 15.7 %collective-permute-done.refs_1_ = bf16[1,48,1536]{2,1,0:T(8,128)(2,1)S(1)} collective-permute-done((bf16[1,48,1536]{2,1,0:T(8,128)(2,1)S(1)}, bf16[1,48,1536]{2,1,0:T(8,128)(2,1)S(1)}, u32[]{:S(2)}, u32[]{:S(2)}) %collective-permute-start) | collective-permute-done | bytes 147488 | tf_op jit(solution)/shard_map/ppermute | solution.py:590
  34.5 7.5 %collective-permute-done.1.refs_1_ = bf16[1,96,768]{2,1,0:T(8,128)(2,1)S(1)} collective-permute-done((bf16[1,96,768]{2,1,0:T(8,128)(2,1)S(1)}, bf16[1,96,768]{2,1,0:T(8,128)(2,1)S(1)}, u32[]{:S(2)}, u32[]{:S(2)}) %collective-permute-start.1) | collective-permute-done | bytes 147488 | tf_op jit(solution)/shard_map/ppermute | solution.py:590
  42.7 6.4 %all_to_all.37 = s32[2,512,2]{1,2,0:T(2,128)S(1)} all-to-all(s32[2,512,2]{1,2,0:T(2,128)S(1)} %pad_add_fusion), channel_id=1, replica_groups=mesh['wide'=16,'seq'=2] {'seq'}, dimensions={0} | all-to-all | bytes 16384 | tf_op jit(solution)/shard_map/all_to_all | solution.py:581
  49.2 4.6 all-to-all-start
  55.9 20.2 %collective-permute-done.2.refs_1_ = bf16[2,48,1536]{2,1,0:T(8,128)(2,1)S(1)} collective-permute-done((bf16[2,48,1536]{2,1,0:T(8,128)(2,1)S(1)}, bf16[2,48,1536]{2,1,0:T(8,128)(2,1)S(1)}, u32[]{:S(2)}, u32[]{:S(2)}) %collective-permute-start.2) | collective-permute-done | bytes 294944 | tf_op jit(solution)/shard_map/ppermute | solution.py:590
  76.1 5.9 collective-permute-done.3.refs_1_
  85.2 3.3 convert_add_fusion.hidden_ref
  92.6 9.3 %project.2 = (bf16[1024,768]{1,0:T(8,128)(2,1)}, bf16[1024,2304]{1,0:T(8,128)(2,1)}) custom-call(f32[1024,768]{1,0:T(8,128)} %convert_add_fusion.hidden_ref, f32[2,768]{1,0:T(2,128)} %squeeze.266.gains_ref, f32[6,768]{1,0:T(8,128)} %squeeze.267.offsets_ref, bf16[768,3200]{1,0:T(8,128)(2,1)} %all-gather.5.cloned.1.call-done.weight_ref.out_weight_ref), custom_call_target="tpu_custom_call" | custom-call | flops 226492416 | bytes 898560 | tf_op jit(solution)/shard_map/project/pallas_call | solution.py:231
  103.1 2.8 fusion.2.bias_ref
  105.9 23.9 %attend_forward.2 = (bf16[1024,768]{1,0:T(8,128)(2,1)}, f32[6,2,1024]{2,1,0:T(2,128)}) custom-call(bf16[1024,2304]{1,0:T(8,128)(2,1)} %get-tuple-element.213.query_ref.key_ref.value_ref, bf16[1024,2304]{1,0:T(8,128)(2,1)} %get-tuple-element.213.query_ref.key_ref.value_ref, bf16[1024,2304]{1,0:T(8,128)(2,1)} %get-tuple-element.213.query_ref.key_ref.value_ref, ...), custom_call_target="tpu_custom_call" | custom-call | flops 805306368 | bytes 393216 | tf_op jit(solution)/shard_map/attend_forward/pallas_call | solution.py:68
  129.8 6.1 %collective-permute-done.7.refs_1_ = bf16[4,192,768]{2,1,0:T(8,128)(2,1)S(1)} collective-permute-done((bf16[4,192,768]{2,1,0:T(8,128)(2,1)S(1)}, bf16[4,192,768]{2,1,0:T(8,128)(2,1)S(1)}, u32[]{:S(2)}, u32[]{:S(2)}) %collective-permute-start.7) | collective-permute-done | bytes 1179680 | tf_op jit(solution)/shard_map/ppermute | solution.py:590
  150.7 2.7 place_pieces.16
  153.4 2.2 copy-done.3
  155.6 24.1 %feed.2 = (f32[1024,768]{1,0:T(8,128)}, bf16[1024,768]{1,0:T(8,128)(2,1)}, bf16[1024,3072]{1,0:T(8,128)(2,1)}, bf16[1024,3072]{1,0:T(8,128)(2,1)}, f32[1024,768]{1,0:T(8,128)}) custom-call(bf16[1024,768]{1,0:T(8,128)(2,1)} %get-tuple-element.225.attended_ref.refs_2_, f32[1024,768]{1,0:T(8,128)} %convert_add_fusion.hidden_ref, f32[2,768]{1,0:T(2,128)} %squeeze.266.gains_ref, ...), custom_call_target="tpu_custom_call" | custom-call | flops 679477248 | bytes 2472192 | tf_op jit(solution)/shard_map/feed/pallas_call | solution.py:231
  179.8 9.4 %project.3 = (bf16[1024,768]{1,0:T(8,128)(2,1)}, bf16[1024,2304]{1,0:T(8,128)(2,1)}) custom-call(f32[1024,768]{1,0:T(8,128)} %get-tuple-element.229.hidden_ref, f32[2,768]{1,0:T(2,128)} %squeeze.268.gains_ref, f32[6,768]{1,0:T(8,128)} %squeeze.269.offsets_ref, bf16[768,6144]{1,0:T(8,128)(2,1)} %all-gather.7.cloned.1.call-done.weight_ref.out_weight_ref.up_ref), custom_call_target="tpu_custom_call" | custom-call | flops 226492416 | bytes 1181184 | tf_op jit(solution)/shard_map/project/pallas_call | solution.py:231
  189.2 3.8 all-to-all-start.2
  193.7 23.8 %attend_forward.3 = (bf16[1024,768]{1,0:T(8,128)(2,1)}, f32[6,2,1024]{2,1,0:T(2,128)}) custom-call(bf16[1024,2304]{1,0:T(8,128)(2,1)} %get-tuple-element.231.query_ref.key_ref.value_ref, bf16[1024,2304]{1,0:T(8,128)(2,1)} %get-tuple-element.231.query_ref.key_ref.value_ref, bf16[1024,2304]{1,0:T(8,128)(2,1)} %get-tuple-element.231.query_ref.key_ref.value_ref, ...), custom_call_target="tpu_custom_call" | custom-call | flops 805306368 | bytes 393216 | tf_op jit(solution)/shard_map/attend_forward/pallas_call | solution.py:68
  217.6 9.7 %all-gather.9.cloned.1.call-done = bf16[1,3072,768]{2,1,0:T(8,128)(2,1)} async-done(((bf16[1,192,768]{2,1,0:T(8,128)(2,1)}), bf16[1,3072,768]{2,1,0:T(8,128)(2,1)}) %all-gather.9.cloned.1.call-update) | async-done | bytes 4718608 | tf_op jit(solution)/shard_map/all_gather | solution.py:697
  227.3 23.9 %feed.3 = (f32[1024,768]{1,0:T(8,128)}, bf16[1024,768]{1,0:T(8,128)(2,1)}, bf16[1024,3072]{1,0:T(8,128)(2,1)}, bf16[1024,3072]{1,0:T(8,128)(2,1)}, bf16[1024,768]{1,0:T(8,128)(2,1)}) custom-call(bf16[1024,768]{1,0:T(8,128)(2,1)} %get-tuple-element.233.attended_ref.refs_4_, f32[1024,768]{1,0:T(8,128)} %get-tuple-element.229.hidden_ref, ...), custom_call_target="tpu_custom_call" | custom-call | flops 679477248 | bytes 2951424 | tf_op jit(solution)/shard_map/feed/pallas_call | solution.py:231
  252.4 31.8 %feed_grad.2 = (bf16[1024,768]{1,0:T(8,128)(2,1)}, bf16[1024,3072]{1,0:T(8,128)(2,1)}, f32[1024,768]{1,0:T(8,128)}, bf16[1024,768]{1,0:T(8,128)(2,1)}, bf16[1024...) custom-call(bf16[1024,768]{1,0:T(8,128)(2,1)} %bitcast.239, ...), custom_call_target="tpu_custom_call" | custom-call | flops 679477248 | bytes 3050112 | tf_op jit(solution)/shard_map/feed_grad/pallas_call | solution.py:231
  284.2 19.7 %term_blocks.5 = bf16[16,48,6912]{2,1,0:T(8,128)(2,1)} custom-call(s32[1]{0:T(128)} %bitcast.20.core_ref, bf16[1024,3072]{1,0:T(8,128)(2,1)} %get-tuple-element.237.refs_0_, bf16[1024,768]{1,0:T(8,128)(2,1)} %get-tuple-element.238.refs_1_, bf16[1024,768]{1,0:T(8,128)(2,1)} %get-tuple-element.239.refs_2_, bf16[1024,3072]{1,0:T(8,128)(2,1)} %get-tuple-element.240.refs_3_, ...), custom_call_target="tpu_custom_call" | custom-call | flops 679477248 | bytes 1843200 | tf_op jit(solution)/shard_map/term_blocks/pallas_call | solution.py:548
  303.9 3.7 all-to-all-start.3
  307.6 37.3 %attend_backward.2.packed_grad_ref.refs_1_ = bf16[1024,2304]{1,0:T(8,128)(2,1)} custom-call(bf16[1024,2304]{1,0:T(8,128)(2,1)} %get-tuple-element.231.query_ref.key_ref.value_ref, bf16[1024,2304]{1,0:T(8,128)(2,1)} %get-tuple-element.231.query_ref.key_ref.value_ref, bf16[1024,2304]{1,0:T(8,128)(2,1)} %get-tuple-element.231.query_ref.key_ref.value_ref, ...), custom_call_target="tpu_custom_call" | custom-call | flops 2013265920 | bytes 786432 | tf_op jit(solution)/shard_map/attend_backward/pallas_call | solution.py:151
  344.9 11.1 %project_grad.2 = (f32[1024,768]{1,0:T(8,128)}, bf16[1024,768]{1,0:T(8,128)(2,1)}, f32[8,768]{1,0:T(8,128)}) custom-call(bf16[1024,2304]{1,0:T(8,128)(2,1)} %attend_backward.2.packed_grad_ref.refs_1_, f32[1024,768]{1,0:T(8,128)} %get-tuple-element.229.hidden_ref, f32[1024,768]{1,0:T(8,128)} %get-tuple-element.247.middle_grad_ref, ...), custom_call_target="tpu_custom_call" | custom-call | flops 226492416 | bytes 1574784 | tf_op jit(solution)/shard_map/project_grad/pallas_call | solution.py:231
  356.0 12.2 %term_blocks.6 = (bf16[8,2,48,1536]{3,2,1,0:T(8,128)(2,1)}, bf16[8,2,48,1536]{3,2,1,0:T(8,128)(2,1)}) custom-call(s32[1]{0:T(128)} %bitcast.20.core_ref, bf16[1024,3072]{1,0:T(8,128)(2,1)} %get-tuple-element.249.refs_0_, bf16[1024,768]{1,0:T(8,128)(2,1)} %get-tuple-element.250.refs_1_), custom_call_target="tpu_custom_call" | custom-call | flops 301989888 | bytes 786432 | tf_op jit(solution)/shard_map/term_blocks/pallas_call | solution.py:548
  368.6 8.6 %term_blocks.7 = bf16[16,48,2304]{2,1,0:T(8,128)(2,1)} custom-call(s32[1]{0:T(128)} %bitcast.20.core_ref, bf16[1024,768]{1,0:T(8,128)(2,1)} %get-tuple-element.253.refs_0_, bf16[1024,2304]{1,0:T(8,128)(2,1)} %attend_backward.2.packed_grad_ref.refs_1_), custom_call_target="tpu_custom_call" | custom-call | flops 226492416 | bytes 614400 | tf_op jit(solution)/shard_map/term_blocks/pallas_call | solution.py:548
  377.2 3.0 fusion.5
  381.8 21.2 %feed_grad.3 = (bf16[1024,768]{1,0:T(8,128)(2,1)}, bf16[1024,3072]{1,0:T(8,128)(2,1)}, f32[1024,768]{1,0:T(8,128)}, bf16[1024,768]{1,0:T(8,128)(2,1)}, bf16[1024...) custom-call(f32[1024,768]{1,0:T(8,128)} %get-tuple-element.259.gradient_ref, ...), custom_call_target="tpu_custom_call" | custom-call | flops 679477248 | bytes 2570880 | tf_op jit(solution)/shard_map/feed_grad/pallas_call | solution.py:231
  403.1 5.6 collective-permute-done.12
  408.6 2.8 fusion.6
  411.4 12.8 %term_blocks.8 = (bf16[8,2,48,1920]{3,2,1,0:T(8,128)(2,1)}, bf16[8,2,48,1920]{3,2,1,0:T(8,128)(2,1)}) custom-call(s32[1]{0:T(128)} %bitcast.20.core_ref, bf16[1024,768]{1,0:T(8,128)(2,1)} %get-tuple-element.270.refs_0_, bf16[1024,3072]{1,0:T(8,128)(2,1)} %get-tuple-element.271.refs_1_, bf16[1024,768]{1,0:T(8,128)(2,1)} %get-tuple-element.225.attended_ref.refs_2_, ...), custom_call_target="tpu_custom_call" | custom-call | flops 377487360 | bytes 1056768 | tf_op jit(solution)/shard_map/term_blocks/pallas_call | solution.py:548
  424.3 5.6 collective-permute-done.13
  429.9 3.9 fusion.3
  440.4 37.4 %attend_backward.3.refs_1_.packed_grad_ref = bf16[1024,2304]{1,0:T(8,128)(2,1)} custom-call(bf16[1024,2304]{1,0:T(8,128)(2,1)} %get-tuple-element.213.query_ref.key_ref.value_ref, bf16[1024,2304]{1,0:T(8,128)(2,1)} %get-tuple-element.213.query_ref.key_ref.value_ref, bf16[1024,2304]{1,0:T(8,128)(2,1)} %get-tuple-element.213.query_ref.key_ref.value_ref, ...), custom_call_target="tpu_custom_call" | custom-call | flops 2013265920 | bytes 786432 | tf_op jit(solution)/shard_map/attend_backward/pallas_call | solution.py:151
  477.9 9.8 %term_blocks.9 = (bf16[8,2,48,1152]{3,2,1,0:T(8,128)(2,1)}, bf16[8,2,48,1152]{3,2,1,0:T(8,128)(2,1)}) custom-call(s32[1]{0:T(128)} %bitcast.20.core_ref, bf16[1024,768]{1,0:T(8,128)(2,1)} %get-tuple-element.290.refs_0_, bf16[1024,2304]{1,0:T(8,128)(2,1)} %attend_backward.3.refs_1_.packed_grad_ref), custom_call_target="tpu_custom_call" | custom-call | flops 226492416 | bytes 614400 | tf_op jit(solution)/shard_map/term_blocks/pallas_call | solution.py:548
  487.7 2.9 fusion.22
  490.6 2.6 fusion.4
  494.7 2.3 collective-permute-done.17
  506.5 10.0 %project_grad.3 = (bf16[1024,768]{1,0:T(8,128)(2,1)}, f32[8,768]{1,0:T(8,128)}) custom-call(bf16[1024,2304]{1,0:T(8,128)(2,1)} %attend_backward.3.refs_1_.packed_grad_ref, f32[1024,768]{1,0:T(8,128)} %convert_add_fusion.hidden_ref, f32[1024,768]{1,0:T(8,128)} %get-tuple-element.298.middle_grad_ref, f32[2,768]{1,0:T(2,128)} %squeeze.266.gains_ref, ...), custom_call_target="tpu_custom_call" | custom-call | flops 226492416 | bytes 1095552 | tf_op jit(solution)/shard_map/project_grad/pallas_call | solution.py:231
  522.6 2.2 fusion.8
  527.5 2.5 fusion.14
  530.4 3.7 all-to-all-start.4
  534.1 3.4 collective-permute-done.23
  543.8 13.8 %collective-permute-done.24 = bf16[48,1536]{1,0:T(8,128)(2,1)S(1)} collective-permute-done((bf16[48,1536]{1,0:T(8,128)(2,1)}, bf16[48,1536]{1,0:T(8,128)(2,1)S(1)}, u32[]{:S(2)}, u32[]{:S(2)}) %collective-permute-start.24) | collective-permute-done | bytes 147488 | tf_op jit(solution)/shard_map/ppermute | solution.py:593
  567.9 2.2 collective-permute-start.37
  570.1 2.6 collective-permute-done.33
  575.7 2.4 collective-permute-done.38
  (263 shorter events, 92.4 us)
Async XLA Ops:
  7.2 81.3 %all-gather.5.cloned.1.call-start = ((), (), s32[]{:S(2)}) async-start(), calls=%async_computation.7 | async-start | bytes 5222400 | tf_op jit(solution)/shard_map/all_gather | solution.py:695
  12.6 167.2 %all-gather.7.cloned.1.call-start = ((), (), s32[]{:S(2)}) async-start(), calls=%async_computation.8 | async-start | bytes 10027008 | tf_op jit(solution)/shard_map/all_gather | solution.py:695
  13.6 213.7 %all-gather.9.cloned.1.call-start = ((), (), s32[]{:S(2)}) async-start(), calls=%async_computation.11 | async-start | bytes 5013504 | tf_op jit(solution)/shard_map/all_gather | solution.py:697
  14.6 19.9 %collective-permute-start = (bf16[1,48,1536]{2,1,0:T(8,128)(2,1)S(1)}, bf16[1,48,1536]{2,1,0:T(8,128)(2,1)S(1)}, u32[]{:S(2)}, u32[]{:S(2)}) collective-permute-start(bf16[1,48,1536]{2,1,0:T(8,128)(2,1)S(1)} %constant_dynamic-slice_fusion.21.refs_0_), channel_id=1, source_target_pairs={{0,16},{2,18},{4,20},{6,22},{8,24},{10,26},{12,28},{14,30},{16,0},... | collective-permute-start | bytes 442376 | tf_op jit(solution)/shard_map/ppermute | solution.py:590
  18.7 23.3 %collective-permute-start.1 = (bf16[1,96,768]{2,1,0:T(8,128)(2,1)S(1)}, bf16[1,96,768]{2,1,0:T(8,128)(2,1)S(1)}, u32[]{:S(2)}, u32[]{:S(2)}) collective-permute-start(bf16[1,96,768]{2,1,0:T(8,128)(2,1)S(1)} %constant_dynamic-slice_fusion.20.refs_0_), channel_id=1, source_target_pairs={{0,16},{2,18},{4,20},{6,22},{8,24},{10,26},{12,28},{14,30},{16,0},... | collective-permute-start | bytes 442376 | tf_op jit(solution)/shard_map/ppermute | solution.py:590
  49.2 36.1 %all-to-all-start = ((bf16[2,512,768]{2,1,0:T(8,128)(2,1)}), bf16[2,512,768]{2,1,0:T(8,128)(2,1)}, u32[]{:S(2)}, u32[]{:S(2)}) async-start(bf16[2,512,768]{2,1,0:T(8,128)(2,1)} %param.12), calls=%async_computation | async-start | bytes 3145728 | tf_op jit(solution)/shard_map/all_to_all | solution.py:581
  53.8 22.3 %collective-permute-start.2 = (bf16[2,48,1536]{2,1,0:T(8,128)(2,1)S(1)}, bf16[2,48,1536]{2,1,0:T(8,128)(2,1)S(1)}, u32[]{:S(2)}, u32[]{:S(2)}) collective-permute-start(bf16[2,48,1536]{2,1,0:T(8,128)(2,1)S(1)} %bitcast.231), channel_id=1, source_target_pairs={{0,8},{2,10},{4,12},{6,14},{8,0},{10,2},{12,4},{14,6},{16,24},{18,... | collective-permute-start | bytes 884744 | tf_op jit(solution)/shard_map/ppermute | solution.py:590
  54.5 27.5 %collective-permute-start.3 = (bf16[2,96,768]{2,1,0:T(8,128)(2,1)S(1)}, bf16[2,96,768]{2,1,0:T(8,128)(2,1)S(1)}, u32[]{:S(2)}, u32[]{:S(2)}) collective-permute-start(bf16[2,96,768]{2,1,0:T(8,128)(2,1)S(1)} %bitcast.233), channel_id=1, source_target_pairs={{0,8},{2,10},{4,12},{6,14},{8,0},{10,2},{12,4},{14,6},{16,24},{18,... | collective-permute-start | bytes 884744 | tf_op jit(solution)/shard_map/ppermute | solution.py:590
  82.2 19.7 %collective-permute-start.4 = (bf16[4,48,1536]{2,1,0:T(8,128)(2,1)S(1)}, bf16[4,48,1536]{2,1,0:T(8,128)(2,1)S(1)}, u32[]{:S(2)}, u32[]{:S(2)}) collective-permute-start(bf16[4,48,1536]{2,1,0:T(8,128)(2,1)S(1)} %bitcast.229), channel_id=1, source_target_pairs={{0,4},{2,6},{4,0},{6,2},{8,12},{10,14},{12,8},{14,10},{16,20},{18,... | collective-permute-start | bytes 1769480 | tf_op jit(solution)/shard_map/ppermute | solution.py:590
  83.7 18.2 %collective-permute-start.5 = (bf16[4,96,768]{2,1,0:T(8,128)(2,1)S(1)}, bf16[4,96,768]{2,1,0:T(8,128)(2,1)S(1)}, u32[]{:S(2)}, u32[]{:S(2)}) collective-permute-start(bf16[4,96,768]{2,1,0:T(8,128)(2,1)S(1)} %bitcast.227), channel_id=1, source_target_pairs={{0,1},{1,0},{2,3},{3,2},{4,5},{5,4},{6,7},{7,6},{8,9},{9,8},{10,11... | collective-permute-start | bytes 1769480 | tf_op jit(solution)/shard_map/ppermute | solution.py:593
  102.2 27.5 %collective-permute-start.6 = (bf16[8,48,1536]{2,1,0:T(8,128)(2,1)S(1)}, bf16[8,48,1536]{2,1,0:T(8,128)(2,1)}, u32[]{:S(2)}, u32[]{:S(2)}) collective-permute-start(bf16[8,48,1536]{2,1,0:T(8,128)(2,1)S(1)} %bitcast.222), channel_id=1, source_target_pairs={{0,1},{1,0},{2,3},{3,2},{4,5},{5,4},{6,7},{7,6},{8,9},{9,8},{10,11... | collective-permute-start | bytes 3538952 | tf_op jit(solution)/shard_map/ppermute | solution.py:593
  102.5 33.4 %collective-permute-start.7 = (bf16[4,192,768]{2,1,0:T(8,128)(2,1)S(1)}, bf16[4,192,768]{2,1,0:T(8,128)(2,1)S(1)}, u32[]{:S(2)}, u32[]{:S(2)}) collective-permute-start(bf16[4,192,768]{2,1,0:T(8,128)(2,1)S(1)} %bitcast.225), channel_id=1, source_target_pairs={{0,4},{2,6},{4,0},{6,2},{8,12},{10,14},{12,8},{14,10},{16,20},{18,... | collective-permute-start | bytes 3538952 | tf_op jit(solution)/shard_map/ppermute | solution.py:590
  136.1 10.6 %collective-permute-start.10 = (bf16[8,192,768]{2,1,0:T(8,128)(2,1)S(1)}, bf16[8,192,768]{2,1,0:T(8,128)(2,1)}, u32[]{:S(2)}, u32[]{:S(2)}) collective-permute-start(bf16[8,192,768]{2,1,0:T(8,128)(2,1)S(1)} %bitcast.220), channel_id=1, source_target_pairs={{0,2},{2,0},{4,6},{6,4},{8,10},{10,8},{12,14},{14,12},{16,18},{18,... | collective-permute-start | bytes 7077896 | tf_op jit(solution)/shard_map/ppermute | solution.py:590
  136.2 10.5 %collective-permute-start.8 = (bf16[8,48,1536]{2,1,0:T(8,128)(2,1)S(1)}, bf16[8,48,1536]{2,1,0:T(8,128)(2,1)}, u32[]{:S(2)}, u32[]{:S(2)}) collective-permute-start(bf16[8,48,1536]{2,1,0:T(8,128)(2,1)S(1)} %bitcast.223), channel_id=1, source_target_pairs={{0,2},{2,0},{4,6},{6,4},{8,10},{10,8},{12,14},{14,12},{16,18},{18,... | collective-permute-start | bytes 3538952 | tf_op jit(solution)/shard_map/ppermute | solution.py:590
  136.7 10.0 %collective-permute-start.9 = (bf16[8,48,1536]{2,1,0:T(8,128)(2,1)}, bf16[8,48,1536]{2,1,0:T(8,128)(2,1)}, u32[]{:S(2)}, u32[]{:S(2)}) collective-permute-start(bf16[8,48,1536]{2,1,0:T(8,128)(2,1)} %collective-permute-done.6.refs_1_), channel_id=1, source_target_pairs={{0,2},{2,0},{4,6},{6,4},{8,10},{10,8},{12,14},{14,12},{16,18},{18,... | collective-permute-start | bytes 3538952 | tf_op jit(solution)/shard_map/ppermute | solution.py:590
  189.2 62.0 %all-to-all-start.2 = ((bf16[2,512,768]{2,1,0:T(8,128)(2,1)}), bf16[2,512,768]{2,1,0:T(8,128)(2,1)S(1)}, u32[]{:S(2)}, u32[]{:S(2)}) async-start(bf16[2,512,768]{2,1,0:T(8,128)(2,1)} %param.16), calls=%async_computation.2 | async-start | bytes 3145728 | tf_op jit(solution)/shard_map/all_to_all | solution.py:581
  193.0 246.8 %reduce-scatter.3.cloned.1.call-start = ((), (), s32[]{:S(2)}) async-start(), calls=%async_computation.9 | async-start | bytes 11280384 | tf_op jit(solution)/shard_map/reduce_scatter | solution.py:596
  303.9 41.0 %all-to-all-start.3 = ((bf16[2,512,768]{2,1,0:T(8,128)(2,1)}), bf16[2,512,768]{2,1,0:T(8,128)(2,1)S(1)}, u32[]{:S(2)}, u32[]{:S(2)}) async-start(bf16[2,512,768]{2,1,0:T(8,128)(2,1)} %bitcast.30), calls=%async_computation.3 | async-start | bytes 3145728 | tf_op jit(solution)/shard_map/all_to_all | solution.py:764
  307.6 213.0 %reduce-scatter.5.cloned.1.call-start = ((), (), s32[]{:S(2)}) async-start(), calls=%async_computation.10 | async-start | bytes 3760128 | tf_op jit(solution)/shard_map/reduce_scatter | solution.py:596
  368.2 9.0 %collective-permute-start.11 = (bf16[8,2,48,1536]{3,2,1,0:T(8,128)(2,1)}, bf16[8,2,48,1536]{3,2,1,0:T(8,128)(2,1)}, u32[]{:S(2)}, u32[]{:S(2)}) collective-permute-start(bf16[8,2,48,1536]{3,2,1,0:T(8,128)(2,1)} %get-tuple-element.255), channel_id=1, source_target_pairs={{0,2},{2,0},{4,6},{6,4},{8,10},{10,8},{12,14},{14,12},{16,18},{18,... | collective-permute-start | bytes 7077896 | tf_op jit(solution)/shard_map/ppermute | solution.py:590
  380.1 28.5 %collective-permute-start.12 = (bf16[2,2,2,48,1536]{4,3,2,1,0:T(8,128)(2,1)}, bf16[2,2,2,48,1536]{4,3,2,1,0:T(8,128)(2,1)S(1)}, u32[]{:S(2)}, u32[]{:S(2)}) collective-permute-start(bf16[2,2,2,48,1536]{4,3,2,1,0:T(8,128)(2,1)} %fusion.5), channel_id=1, source_target_pairs={{0,1},{1,0},{2,3},{3,2},{4,5},{5,4},{6,7},{7,6},{8,9},{9,8},{10,11... | collective-permute-start | bytes 3538952 | tf_op jit(solution)/shard_map/ppermute | solution.py:593
  424.2 5.7 collective-permute-start.13
  433.8 53.8 %collective-permute-start.15 = (bf16[2,2,2,48,1920]{4,3,2,1,0:T(8,128)(2,1)}, bf16[2,2,2,48,1920]{4,3,2,1,0:T(8,128)(2,1)S(1)}, u32[]{:S(2)}, u32[]{:S(2)}) collective-permute-start(bf16[2,2,2,48,1920]{4,3,2,1,0:T(8,128)(2,1)} %fusion.3), channel_id=1, source_target_pairs={{0,1},{1,0},{2,3},{3,2},{4,5},{5,4},{6,7},{7,6},{8,9},{9,8},{10,11... | collective-permute-start | bytes 4423688 | tf_op jit(solution)/shard_map/ppermute | solution.py:593
  439.1 48.5 %collective-permute-start.14 = (bf16[2,2,48,1536]{3,2,1,0:T(8,128)(2,1)}, bf16[2,2,48,1536]{3,2,1,0:T(8,128)(2,1)}, u32[]{:S(2)}, u32[]{:S(2)}) collective-permute-start(bf16[2,2,48,1536]{3,2,1,0:T(8,128)(2,1)} %fusion.6), channel_id=1, source_target_pairs={{0,4},{2,6},{4,0},{6,2},{8,12},{10,14},{12,8},{14,10},{16,20},{18,... | collective-permute-start | bytes 1769480 | tf_op jit(solution)/shard_map/ppermute | solution.py:590
  439.8 47.9 %collective-permute-start.16 = (bf16[48,6912]{1,0:T(8,128)(2,1)}, bf16[48,6912]{1,0:T(8,128)(2,1)}, u32[]{:S(2)}, u32[]{:S(2)}) collective-permute-start(bf16[48,6912]{1,0:T(8,128)(2,1)} %reduce-scatter.3.cloned.1.call-done), channel_id=1, source_target_pairs={{0,1},{1,0},{2,3},{3,2},{4,5},{5,4},{6,7},{7,6},{8,9},{9,8},{10,11... | collective-permute-start | bytes 1990664 | tf_op jit(solution)/shard_map/ppermute | solution.py:593
  498.3 24.3 %collective-permute-start.22 = (bf16[2,2,2,48,1152]{4,3,2,1,0:T(8,128)(2,1)}, bf16[2,2,2,48,1152]{4,3,2,1,0:T(8,128)(2,1)}, u32[]{:S(2)}, u32[]{:S(2)}) collective-permute-start(bf16[2,2,2,48,1152]{4,3,2,1,0:T(8,128)(2,1)} %fusion.7), channel_id=1, source_target_pairs={{0,1},{1,0},{2,3},{3,2},{4,5},{5,4},{6,7},{7,6},{8,9},{9,8},{10,11... | collective-permute-start | bytes 2654216 | tf_op jit(solution)/shard_map/ppermute | solution.py:593
  500.7 19.9 %collective-permute-start.21 = (bf16[2,2,48,1920]{3,2,1,0:T(8,128)(2,1)}, bf16[2,2,48,1920]{3,2,1,0:T(8,128)(2,1)S(1)}, u32[]{:S(2)}, u32[]{:S(2)}) collective-permute-start(bf16[2,2,48,1920]{3,2,1,0:T(8,128)(2,1)} %fusion.4), channel_id=1, source_target_pairs={{0,4},{2,6},{4,0},{6,2},{8,12},{10,14},{12,8},{14,10},{16,20},{18,... | collective-permute-start | bytes 2211848 | tf_op jit(solution)/shard_map/ppermute | solution.py:590
  502.0 18.6 %collective-permute-start.18 = (bf16[48,1536]{1,0:T(8,128)(2,1)}, bf16[48,1536]{1,0:T(8,128)(2,1)}, u32[]{:S(2)}, u32[]{:S(2)}) collective-permute-start(bf16[48,1536]{1,0:T(8,128)(2,1)} %get-tuple-element.306), channel_id=1, source_target_pairs={{0,8},{2,10},{4,12},{6,14},{8,0},{10,2},{12,4},{14,6},{16,24},{18,... | collective-permute-start | bytes 442376 | tf_op jit(solution)/shard_map/ppermute | solution.py:590
  503.8 16.8 %collective-permute-start.19 = (bf16[48,1536]{1,0:T(8,128)(2,1)}, bf16[48,1536]{1,0:T(8,128)(2,1)}, u32[]{:S(2)}, u32[]{:S(2)}) collective-permute-start(bf16[48,1536]{1,0:T(8,128)(2,1)} %get-tuple-element.307), channel_id=1, source_target_pairs={{0,16},{2,18},{4,20},{6,22},{8,24},{10,26},{12,28},{14,30},{16,0},... | collective-permute-start | bytes 442376 | tf_op jit(solution)/shard_map/ppermute | solution.py:590
  504.5 16.1 %collective-permute-start.20 = (bf16[48,1536]{1,0:T(8,128)(2,1)}, bf16[48,1536]{1,0:T(8,128)(2,1)}, u32[]{:S(2)}, u32[]{:S(2)}) collective-permute-start(bf16[48,1536]{1,0:T(8,128)(2,1)} %get-tuple-element.308), channel_id=1, source_target_pairs={{0,24},{2,26},{4,28},{6,30},{8,16},{10,18},{12,20},{14,22},{16,8},... | collective-permute-start | bytes 442376 | tf_op jit(solution)/shard_map/ppermute | solution.py:590
  520.6 17.7 %collective-permute-start.29 = (f32[2,2,1152]{2,1,0:T(2,128)}, f32[2,2,1152]{2,1,0:T(2,128)}, u32[]{:S(2)}, u32[]{:S(2)}) collective-permute-start(f32[2,2,1152]{2,1,0:T(2,128)} %bitcast.215), channel_id=1, source_target_pairs={{0,2},{2,0},{4,6},{6,4},{8,10},{10,8},{12,14},{14,12},{16,18},{18,... | collective-permute-start | bytes 55304 | tf_op jit(solution)/shard_map/ppermute | solution.py:590
  520.7 19.3 %collective-permute-start.30 = (f32[2,2,1152]{2,1,0:T(2,128)}, f32[2,2,1152]{2,1,0:T(2,128)S(1)}, u32[]{:S(2)}, u32[]{:S(2)}) collective-permute-start(f32[2,2,1152]{2,1,0:T(2,128)} %bitcast.214), channel_id=1, source_target_pairs={{0,4},{2,6},{4,0},{6,2},{8,12},{10,14},{12,8},{14,10},{16,20},{18,... | collective-permute-start | bytes 55304 | tf_op jit(solution)/shard_map/ppermute | solution.py:590
  521.4 20.5 %collective-permute-start.31 = (f32[2,2,1152]{2,1,0:T(2,128)}, f32[2,2,1152]{2,1,0:T(2,128)}, u32[]{:S(2)}, u32[]{:S(2)}) collective-permute-start(f32[2,2,1152]{2,1,0:T(2,128)} %bitcast.213), channel_id=1, source_target_pairs={{0,6},{2,4},{4,2},{6,0},{8,14},{10,12},{12,10},{14,8},{16,22},{18,... | collective-permute-start | bytes 55304 | tf_op jit(solution)/shard_map/ppermute | solution.py:590
  524.8 12.7 %collective-permute-start.23 = (bf16[2,2,48,1152]{3,2,1,0:T(8,128)(2,1)}, bf16[2,2,48,1152]{3,2,1,0:T(8,128)(2,1)}, u32[]{:S(2)}, u32[]{:S(2)}) collective-permute-start(bf16[2,2,48,1152]{3,2,1,0:T(8,128)(2,1)} %fusion.8), channel_id=1, source_target_pairs={{0,4},{2,6},{4,0},{6,2},{8,12},{10,14},{12,8},{14,10},{16,20},{18,... | collective-permute-start | bytes 1327112 | tf_op jit(solution)/shard_map/ppermute | solution.py:590
  530.0 27.6 %collective-permute-start.25 = (bf16[48,2304]{1,0:T(8,128)(2,1)}, bf16[48,2304]{1,0:T(8,128)(2,1)}, u32[]{:S(2)}, u32[]{:S(2)}) collective-permute-start(bf16[48,2304]{1,0:T(8,128)(2,1)} %reduce-scatter.5.cloned.1.call-done), channel_id=1, source_target_pairs={{0,1},{1,0},{2,3},{3,2},{4,5},{5,4},{6,7},{7,6},{8,9},{9,8},{10,11... | collective-permute-start | bytes 663560 | tf_op jit(solution)/shard_map/ppermute | solution.py:593
  530.4 54.7 %all-to-all-start.4 = ((bf16[2,512,768]{2,1,0:T(8,128)(2,1)}), bf16[2,512,768]{2,1,0:T(8,128)(2,1)S(1)}, u32[]{:S(2)}, u32[]{:S(2)}) async-start(bf16[2,512,768]{2,1,0:T(8,128)(2,1)} %bitcast.260), calls=%async_computation.6 | async-start | bytes 3145728 | tf_op jit(solution)/shard_map/all_to_all | solution.py:764
  537.5 20.1 %collective-permute-start.26 = (bf16[48,1920]{1,0:T(8,128)(2,1)}, bf16[48,1920]{1,0:T(8,128)(2,1)S(1)}, u32[]{:S(2)}, u32[]{:S(2)}) collective-permute-start(bf16[48,1920]{1,0:T(8,128)(2,1)} %get-tuple-element.328), channel_id=1, source_target_pairs={{0,8},{2,10},{4,12},{6,14},{8,0},{10,2},{12,4},{14,6},{16,24},{18,... | collective-permute-start | bytes 552968 | tf_op jit(solution)/shard_map/ppermute | solution.py:590
  538.3 19.3 %collective-permute-start.27 = (bf16[48,1920]{1,0:T(8,128)(2,1)}, bf16[48,1920]{1,0:T(8,128)(2,1)S(1)}, u32[]{:S(2)}, u32[]{:S(2)}) collective-permute-start(bf16[48,1920]{1,0:T(8,128)(2,1)} %get-tuple-element.329), channel_id=1, source_target_pairs={{0,16},{2,18},{4,20},{6,22},{8,24},{10,26},{12,28},{14,30},{16,0},... | collective-permute-start | bytes 552968 | tf_op jit(solution)/shard_map/ppermute | solution.py:590
  540.0 17.6 %collective-permute-start.28 = (bf16[48,1920]{1,0:T(8,128)(2,1)}, bf16[48,1920]{1,0:T(8,128)(2,1)S(1)}, u32[]{:S(2)}, u32[]{:S(2)}) collective-permute-start(bf16[48,1920]{1,0:T(8,128)(2,1)} %get-tuple-element.330), channel_id=1, source_target_pairs={{0,24},{2,26},{4,28},{6,30},{8,16},{10,18},{12,20},{14,22},{16,8},... | collective-permute-start | bytes 552968 | tf_op jit(solution)/shard_map/ppermute | solution.py:590
  541.9 15.7 %collective-permute-start.24 = (bf16[48,1536]{1,0:T(8,128)(2,1)}, bf16[48,1536]{1,0:T(8,128)(2,1)S(1)}, u32[]{:S(2)}, u32[]{:S(2)}) collective-permute-start(bf16[48,1536]{1,0:T(8,128)(2,1)} %fusion.21), channel_id=1, source_target_pairs={{0,1},{1,0},{2,3},{3,2},{4,5},{5,4},{6,7},{7,6},{8,9},{9,8},{10,11... | collective-permute-start | bytes 442376 | tf_op jit(solution)/shard_map/ppermute | solution.py:593
  560.7 7.2 %collective-permute-start.32 = (bf16[48,1152]{1,0:T(8,128)(2,1)S(1)}, bf16[48,1152]{1,0:T(8,128)(2,1)S(1)}, u32[]{:S(2)}, u32[]{:S(2)}) collective-permute-start(bf16[48,1152]{1,0:T(8,128)(2,1)S(1)} %get-tuple-element.342), channel_id=1, source_target_pairs={{0,8},{2,10},{4,12},{6,14},{8,0},{10,2},{12,4},{14,6},{16,24},{18,... | collective-permute-start | bytes 331784 | tf_op jit(solution)/shard_map/ppermute | solution.py:590
  561.7 10.9 %collective-permute-start.33 = (bf16[48,1152]{1,0:T(8,128)(2,1)S(1)}, bf16[48,1152]{1,0:T(8,128)(2,1)S(1)}, u32[]{:S(2)}, u32[]{:S(2)}) collective-permute-start(bf16[48,1152]{1,0:T(8,128)(2,1)S(1)} %get-tuple-element.343), channel_id=1, source_target_pairs={{0,16},{2,18},{4,20},{6,22},{8,24},{10,26},{12,28},{14,30},{16,0},... | collective-permute-start | bytes 331784 | tf_op jit(solution)/shard_map/ppermute | solution.py:590
  563.0 11.2 %collective-permute-start.34 = (bf16[48,1152]{1,0:T(8,128)(2,1)S(1)}, bf16[48,1152]{1,0:T(8,128)(2,1)S(1)}, u32[]{:S(2)}, u32[]{:S(2)}) collective-permute-start(bf16[48,1152]{1,0:T(8,128)(2,1)S(1)} %get-tuple-element.344), channel_id=1, source_target_pairs={{0,24},{2,26},{4,28},{6,30},{8,16},{10,18},{12,20},{14,22},{16,8},... | collective-permute-start | bytes 331784 | tf_op jit(solution)/shard_map/ppermute | solution.py:590
  565.2 12.9 %collective-permute-start.35 = (bf16[48,1920]{1,0:T(8,128)(2,1)S(1)}, bf16[48,1920]{1,0:T(8,128)(2,1)S(1)}, u32[]{:S(2)}, u32[]{:S(2)}) collective-permute-start(bf16[48,1920]{1,0:T(8,128)(2,1)S(1)} %fusion.13), channel_id=1, source_target_pairs={{0,1},{1,0},{2,3},{3,2},{4,5},{5,4},{6,7},{7,6},{8,9},{9,8},{10,11... | collective-permute-start | bytes 552968 | tf_op jit(solution)/shard_map/ppermute | solution.py:593
  565.5 10.2 %collective-permute-start.36 = (f32[1152]{0:T(1024)S(1)}, f32[1152]{0:T(1024)S(1)}, u32[]{:S(2)}, u32[]{:S(2)}) collective-permute-start(f32[1152]{0:T(1024)S(1)} %add_add_fusion.3), channel_id=1, source_target_pairs={{0,8},{2,10},{4,12},{6,14},{8,0},{10,2},{12,4},{14,6},{16,24},{18,... | collective-permute-start | bytes 13832 | tf_op jit(solution)/shard_map/ppermute | solution.py:590
  567.9 7.8 %collective-permute-start.37 = (f32[1152]{0:T(1024)S(1)}, f32[1152]{0:T(1024)S(1)}, u32[]{:S(2)}, u32[]{:S(2)}) collective-permute-start(f32[1152]{0:T(1024)S(1)} %add_add_fusion.2), channel_id=1, source_target_pairs={{0,16},{2,18},{4,20},{6,22},{8,24},{10,26},{12,28},{14,30},{16,0},... | collective-permute-start | bytes 13832 | tf_op jit(solution)/shard_map/ppermute | solution.py:590
  572.6 5.4 collective-permute-start.38
  575.4 5.1 collective-permute-start.39
  (29 other events, 228.9 us)
Sparse Core Ops, SparseCore 0:
  12.7 67.1 all-gather.4
  82.7 90.0 all-gather.6
  175.7 51.5 all-gather.8
  304.0 118.7 reduce-scatter.2
  435.7 65.9 reduce-scatter.4

commit v15 on v10

--- a/solution.py
+++ b/solution.py
@@ -9,7 +9,7 @@
 
 HEAD_SIZE = 64
 PAIR = 2 * HEAD_SIZE
-FORWARD_ROWS = 512
+FORWARD_ROWS = 1024
 BACKWARD_ROWS = 256
 ROW_TILE = 256
 FF_CHUNK = 1024
@@ -680,6 +680,8 @@
             current = join(current, received, bit_of(bit))
         return current.reshape(-1, columns)
 
+    marks = whole_sequence(jnp.stack([segment_ids, pad_mask], axis=2))
+    tokens, marks = lax.optimization_barrier((tokens, marks))
     my_tokens = whole_sequence(tokens)
 
     small = jnp.concatenate(
@@ -715,10 +717,8 @@
         begin(gather_columns(up_weight[0]), functools.partial(ups.__setitem__, 0)),
         begin(gather_rows(down_weight[0]), functools.partial(downs.__setitem__, 0)),
     ]
-    marks = jnp.stack([segment_ids, pad_mask], axis=2)
     for _ in chip_bits[1:]:
-        time_embed, marks = advance((time_embed, marks), *fetches)
-    marks = whole_sequence(marks)
+        time_embed = advance(time_embed, *fetches)
     doc, pad = marks[:, 0], marks[:, 1]
     positions = jnp.arange(doc.shape[0])
     allowed = (doc[:, None] == doc[None, :]) & (

time: 601 us -> 607 us (level)
  blocking collectives: 25.1 us -> 0 us
  waiting for transfers between devices: 86.1 us -> 106 us
  Pallas kernels: 323 us -> 332 us
    all_to_all x1 -> x0, blocking collectives: 25.1 us -> none  [whole_sequence(): lax.all_to_all(part, 'seq', split_axis=0, concat_axis=1, tiled=True)[0]]
    pallas_call x8, Pallas kernels: 130 us -> 141 us  [row_tiled(): pl.pallas_call(kernel, grid=(length // ROW_TILE,), in_specs=in_specs, out...]
    ppermute x30, waiting for transfers between devices: 65.9 us -> 75.8 us  [across(): return lambda part: lax.ppermute(part, 'wide', pairs)]
    ppermute x30, starting transfers between devices: 38.2 us -> 31 us  [across(): return lambda part: lax.ppermute(part, 'wide', pairs)]
    all_to_all x2 -> x3, starting transfers between devices: 8.46 us -> 12.7 us  [whole_sequence(): lax.all_to_all(part, 'seq', split_axis=0, concat_axis=1, tiled=True)[0]]
  transfers between devices with their start and end apart: 50 -> 51, of which waited for: 13 -> 15; matrix products, arithmetic and copies ran while one was open for 11% -> 12% of each run, Pallas kernels for 47% -> 47%
where the time goes in v15:
time: 607 us; the launch traced here: 596 us
  Pallas kernels  332 us (55%)
  waiting for transfers between devices  106 us (17%)
  starting transfers between devices  60.4 us (10%)
  other arithmetic  47.5 us (8%)
  local copies, waits for them, and re-layouts  34.7 us (6%)
  between operations  15.1 us (2%)
    pallas_call x8, Pallas kernels, row_tiled(): pl.pallas_call(kernel, grid=(length // ROW_TILE,), in_specs=in_specs, out...  141 us
    ppermute x30, waiting for transfers between devices, across(): return lambda part: lax.ppermute(part, 'wide', pairs)  75.8 us
    pallas_call x2, Pallas kernels, attend_backward(): pl.pallas_call(functools.partial(attend_grad_kernel, rows=BACKWARD_ROWS),...  74.7 us
    pallas_call x5, Pallas kernels, term_blocks(): pl.pallas_call(kernel, in_specs=[pl.BlockSpec(memory_space=pltpu.SMEM)] +...  63 us
    pallas_call x2, Pallas kernels, attend_forward(): pl.pallas_call(functools.partial(attend_kernel, rows=FORWARD_ROWS), grid=...  47.7 us
    ppermute x30, starting transfers between devices, across(): return lambda part: lax.ppermute(part, 'wide', pairs)  31 us
    ppermute x11, waiting for transfers between devices, beside_seq(): return lax.ppermute(part, 'seq', swap)  21 us
    convert_element_type x6, other arithmetic, reduce_group(): total_of([side_of(part, 1 - mine, axis) for part in addends]).astype(half)  15.8 us
  transfers between devices with their start and end apart: 51, of which 15 were waited for; matrix products, arithmetic and copies ran while one was open for 12% of the time, Pallas kernels for 47%

profile of v15, /device:TPU:0, one launch (start us, length us, event | category | flops | bytes accessed | tf_op | source)
XLA Modules:
  0.0 596.3 jit_solution(11928190008139563451)
XLA Ops:
  15.1 4.2 all-to-all-start
  19.3 3.8 all-to-all-done
  23.1 4.6 all-to-all-start.1
  27.8 3.1 collective-permute-start
  31.0 16.2 %collective-permute-done.refs_1_ = bf16[1,48,1536]{2,1,0:T(8,128)(2,1)S(1)} collective-permute-done((bf16[1,48,1536]{2,1,0:T(8,128)(2,1)S(1)}, bf16[1,48,1536]{2,1,0:T(8,128)(2,1)S(1)}, u32[]{:S(2)}, u32[]{:S(2)}) %collective-permute-start) | collective-permute-done | bytes 147488 | tf_op jit(solution)/shard_map/ppermute | solution.py:590
  47.2 2.9 collective-permute-done.1.refs_1_
  53.0 20.3 %collective-permute-done.2.refs_1_ = bf16[2,48,1536]{2,1,0:T(8,128)(2,1)S(1)} collective-permute-done((bf16[2,48,1536]{2,1,0:T(8,128)(2,1)S(1)}, bf16[2,48,1536]{2,1,0:T(8,128)(2,1)S(1)}, u32[]{:S(2)}, u32[]{:S(2)}) %collective-permute-start.2) | collective-permute-done | bytes 294944 | tf_op jit(solution)/shard_map/ppermute | solution.py:590
  73.2 12.5 %collective-permute-done.3.refs_1_ = bf16[2,96,768]{2,1,0:T(8,128)(2,1)S(1)} collective-permute-done((bf16[2,96,768]{2,1,0:T(8,128)(2,1)S(1)}, bf16[2,96,768]{2,1,0:T(8,128)(2,1)S(1)}, u32[]{:S(2)}, u32[]{:S(2)}) %collective-permute-start.3) | collective-permute-done | bytes 294944 | tf_op jit(solution)/shard_map/ppermute | solution.py:590
  89.0 3.3 convert_add_fusion.hidden_ref
  96.3 9.2 %project.2 = (bf16[1024,768]{1,0:T(8,128)(2,1)}, bf16[1024,2304]{1,0:T(8,128)(2,1)}) custom-call(f32[1024,768]{1,0:T(8,128)} %convert_add_fusion.hidden_ref, f32[2,768]{1,0:T(2,128)} %squeeze.266.gains_ref, f32[6,768]{1,0:T(8,128)} %squeeze.267.offsets_ref, bf16[768,3200]{1,0:T(8,128)(2,1)} %all-gather.5.cloned.1.call-done.weight_ref.out_weight_ref), custom_call_target="tpu_custom_call" | custom-call | flops 226492416 | bytes 898560 | tf_op jit(solution)/shard_map/project/pallas_call | solution.py:231
  107.9 2.8 fusion.2.bias_ref
  110.7 23.9 %attend_forward.2 = (bf16[1024,768]{1,0:T(8,128)(2,1)}, f32[6,2,1024]{2,1,0:T(2,128)}) custom-call(bf16[1024,2304]{1,0:T(8,128)(2,1)} %get-tuple-element.207.query_ref.key_ref.value_ref, bf16[1024,2304]{1,0:T(8,128)(2,1)} %get-tuple-element.207.query_ref.key_ref.value_ref, bf16[1024,2304]{1,0:T(8,128)(2,1)} %get-tuple-element.207.query_ref.key_ref.value_ref, ...), custom_call_target="tpu_custom_call" | custom-call | flops 805306368 | bytes 393216 | tf_op jit(solution)/shard_map/attend_forward/pallas_call | solution.py:68
  134.5 7.7 %collective-permute-done.7.refs_1_ = bf16[4,192,768]{2,1,0:T(8,128)(2,1)S(1)} collective-permute-done((bf16[4,192,768]{2,1,0:T(8,128)(2,1)S(1)}, bf16[4,192,768]{2,1,0:T(8,128)(2,1)S(1)}, u32[]{:S(2)}, u32[]{:S(2)}) %collective-permute-start.7) | collective-permute-done | bytes 1179680 | tf_op jit(solution)/shard_map/ppermute | solution.py:590
  157.1 2.7 place_pieces.16
  159.8 2.2 copy-done.3
  162.0 24.2 %feed.2 = (f32[1024,768]{1,0:T(8,128)}, bf16[1024,768]{1,0:T(8,128)(2,1)}, bf16[1024,3072]{1,0:T(8,128)(2,1)}, bf16[1024,3072]{1,0:T(8,128)(2,1)}, f32[1024,768]{1,0:T(8,128)}) custom-call(bf16[1024,768]{1,0:T(8,128)(2,1)} %get-tuple-element.219.attended_ref.refs_2_, f32[1024,768]{1,0:T(8,128)} %convert_add_fusion.hidden_ref, f32[2,768]{1,0:T(2,128)} %squeeze.266.gains_ref, ...), custom_call_target="tpu_custom_call" | custom-call | flops 679477248 | bytes 2472192 | tf_op jit(solution)/shard_map/feed/pallas_call | solution.py:231
  186.3 9.2 %project.3 = (bf16[1024,768]{1,0:T(8,128)(2,1)}, bf16[1024,2304]{1,0:T(8,128)(2,1)}) custom-call(f32[1024,768]{1,0:T(8,128)} %get-tuple-element.223.hidden_ref, f32[2,768]{1,0:T(2,128)} %squeeze.268.gains_ref, f32[6,768]{1,0:T(8,128)} %squeeze.269.offsets_ref, bf16[768,6144]{1,0:T(8,128)(2,1)} %all-gather.7.cloned.1.call-done.weight_ref.out_weight_ref.up_ref), custom_call_target="tpu_custom_call" | custom-call | flops 226492416 | bytes 1181184 | tf_op jit(solution)/shard_map/project/pallas_call | solution.py:231
  195.5 3.8 all-to-all-start.2
  200.1 23.8 %attend_forward.3 = (bf16[1024,768]{1,0:T(8,128)(2,1)}, f32[6,2,1024]{2,1,0:T(2,128)}) custom-call(bf16[1024,2304]{1,0:T(8,128)(2,1)} %get-tuple-element.225.query_ref.key_ref.value_ref, bf16[1024,2304]{1,0:T(8,128)(2,1)} %get-tuple-element.225.query_ref.key_ref.value_ref, bf16[1024,2304]{1,0:T(8,128)(2,1)} %get-tuple-element.225.query_ref.key_ref.value_ref, ...), custom_call_target="tpu_custom_call" | custom-call | flops 805306368 | bytes 393216 | tf_op jit(solution)/shard_map/attend_forward/pallas_call | solution.py:68
  223.9 5.7 all-gather.9.cloned.1.call-done
  229.6 23.9 %feed.3 = (f32[1024,768]{1,0:T(8,128)}, bf16[1024,768]{1,0:T(8,128)(2,1)}, bf16[1024,3072]{1,0:T(8,128)(2,1)}, bf16[1024,3072]{1,0:T(8,128)(2,1)}, bf16[1024,768]{1,0:T(8,128)(2,1)}) custom-call(bf16[1024,768]{1,0:T(8,128)(2,1)} %get-tuple-element.227.attended_ref.refs_4_, f32[1024,768]{1,0:T(8,128)} %get-tuple-element.223.hidden_ref, ...), custom_call_target="tpu_custom_call" | custom-call | flops 679477248 | bytes 2951424 | tf_op jit(solution)/shard_map/feed/pallas_call | solution.py:231
  254.7 31.8 %feed_grad.2 = (bf16[1024,768]{1,0:T(8,128)(2,1)}, bf16[1024,3072]{1,0:T(8,128)(2,1)}, f32[1024,768]{1,0:T(8,128)}, bf16[1024,768]{1,0:T(8,128)(2,1)}, bf16[1024...) custom-call(bf16[1024,768]{1,0:T(8,128)(2,1)} %bitcast.239, ...), custom_call_target="tpu_custom_call" | custom-call | flops 679477248 | bytes 3050112 | tf_op jit(solution)/shard_map/feed_grad/pallas_call | solution.py:231
  286.5 19.7 %term_blocks.5 = bf16[16,48,6912]{2,1,0:T(8,128)(2,1)} custom-call(s32[1]{0:T(128)} %bitcast.20.core_ref, bf16[1024,3072]{1,0:T(8,128)(2,1)} %get-tuple-element.231.refs_0_, bf16[1024,768]{1,0:T(8,128)(2,1)} %get-tuple-element.232.refs_1_, bf16[1024,768]{1,0:T(8,128)(2,1)} %get-tuple-element.233.refs_2_, bf16[1024,3072]{1,0:T(8,128)(2,1)} %get-tuple-element.234.refs_3_, ...), custom_call_target="tpu_custom_call" | custom-call | flops 679477248 | bytes 1843200 | tf_op jit(solution)/shard_map/term_blocks/pallas_call | solution.py:548
  306.2 3.7 all-to-all-start.3
  309.9 37.3 %attend_backward.2.packed_grad_ref.refs_1_ = bf16[1024,2304]{1,0:T(8,128)(2,1)} custom-call(bf16[1024,2304]{1,0:T(8,128)(2,1)} %get-tuple-element.225.query_ref.key_ref.value_ref, bf16[1024,2304]{1,0:T(8,128)(2,1)} %get-tuple-element.225.query_ref.key_ref.value_ref, bf16[1024,2304]{1,0:T(8,128)(2,1)} %get-tuple-element.225.query_ref.key_ref.value_ref, ...), custom_call_target="tpu_custom_call" | custom-call | flops 2013265920 | bytes 786432 | tf_op jit(solution)/shard_map/attend_backward/pallas_call | solution.py:151
  347.2 11.1 %project_grad.2 = (f32[1024,768]{1,0:T(8,128)}, bf16[1024,768]{1,0:T(8,128)(2,1)}, f32[8,768]{1,0:T(8,128)}) custom-call(bf16[1024,2304]{1,0:T(8,128)(2,1)} %attend_backward.2.packed_grad_ref.refs_1_, f32[1024,768]{1,0:T(8,128)} %get-tuple-element.223.hidden_ref, f32[1024,768]{1,0:T(8,128)} %get-tuple-element.241.middle_grad_ref, ...), custom_call_target="tpu_custom_call" | custom-call | flops 226492416 | bytes 1574784 | tf_op jit(solution)/shard_map/project_grad/pallas_call | solution.py:231
  358.3 12.2 %term_blocks.6 = (bf16[8,2,48,1536]{3,2,1,0:T(8,128)(2,1)}, bf16[8,2,48,1536]{3,2,1,0:T(8,128)(2,1)}) custom-call(s32[1]{0:T(128)} %bitcast.20.core_ref, bf16[1024,3072]{1,0:T(8,128)(2,1)} %get-tuple-element.243.refs_0_, bf16[1024,768]{1,0:T(8,128)(2,1)} %get-tuple-element.244.refs_1_), custom_call_target="tpu_custom_call" | custom-call | flops 301989888 | bytes 786432 | tf_op jit(solution)/shard_map/term_blocks/pallas_call | solution.py:548
  370.9 8.6 %term_blocks.7 = bf16[16,48,2304]{2,1,0:T(8,128)(2,1)} custom-call(s32[1]{0:T(128)} %bitcast.20.core_ref, bf16[1024,768]{1,0:T(8,128)(2,1)} %get-tuple-element.247.refs_0_, bf16[1024,2304]{1,0:T(8,128)(2,1)} %attend_backward.2.packed_grad_ref.refs_1_), custom_call_target="tpu_custom_call" | custom-call | flops 226492416 | bytes 614400 | tf_op jit(solution)/shard_map/term_blocks/pallas_call | solution.py:548
  379.5 3.0 fusion.5
  384.1 21.2 %feed_grad.3 = (bf16[1024,768]{1,0:T(8,128)(2,1)}, bf16[1024,3072]{1,0:T(8,128)(2,1)}, f32[1024,768]{1,0:T(8,128)}, bf16[1024,768]{1,0:T(8,128)(2,1)}, bf16[1024...) custom-call(f32[1024,768]{1,0:T(8,128)} %get-tuple-element.253.gradient_ref, ...), custom_call_target="tpu_custom_call" | custom-call | flops 679477248 | bytes 2570880 | tf_op jit(solution)/shard_map/feed_grad/pallas_call | solution.py:231
  405.4 5.6 collective-permute-done.12
  411.0 2.8 fusion.6
  413.7 12.8 %term_blocks.8 = (bf16[8,2,48,1920]{3,2,1,0:T(8,128)(2,1)}, bf16[8,2,48,1920]{3,2,1,0:T(8,128)(2,1)}) custom-call(s32[1]{0:T(128)} %bitcast.20.core_ref, bf16[1024,768]{1,0:T(8,128)(2,1)} %get-tuple-element.264.refs_0_, bf16[1024,3072]{1,0:T(8,128)(2,1)} %get-tuple-element.265.refs_1_, bf16[1024,768]{1,0:T(8,128)(2,1)} %get-tuple-element.219.attended_ref.refs_2_, ...), custom_call_target="tpu_custom_call" | custom-call | flops 377487360 | bytes 1056768 | tf_op jit(solution)/shard_map/term_blocks/pallas_call | solution.py:548
  426.6 5.6 collective-permute-done.13
  432.2 3.9 fusion.3
  442.8 37.5 %attend_backward.3.refs_1_.packed_grad_ref = bf16[1024,2304]{1,0:T(8,128)(2,1)} custom-call(bf16[1024,2304]{1,0:T(8,128)(2,1)} %get-tuple-element.207.query_ref.key_ref.value_ref, bf16[1024,2304]{1,0:T(8,128)(2,1)} %get-tuple-element.207.query_ref.key_ref.value_ref, bf16[1024,2304]{1,0:T(8,128)(2,1)} %get-tuple-element.207.query_ref.key_ref.value_ref, ...), custom_call_target="tpu_custom_call" | custom-call | flops 2013265920 | bytes 786432 | tf_op jit(solution)/shard_map/attend_backward/pallas_call | solution.py:151
  480.3 9.8 %term_blocks.9 = (bf16[8,2,48,1152]{3,2,1,0:T(8,128)(2,1)}, bf16[8,2,48,1152]{3,2,1,0:T(8,128)(2,1)}) custom-call(s32[1]{0:T(128)} %bitcast.20.core_ref, bf16[1024,768]{1,0:T(8,128)(2,1)} %get-tuple-element.284.refs_0_, bf16[1024,2304]{1,0:T(8,128)(2,1)} %attend_backward.3.refs_1_.packed_grad_ref), custom_call_target="tpu_custom_call" | custom-call | flops 226492416 | bytes 614400 | tf_op jit(solution)/shard_map/term_blocks/pallas_call | solution.py:548
  490.1 2.9 fusion.22
  493.0 2.6 fusion.4
  497.1 2.3 collective-permute-done.17
  508.9 10.0 %project_grad.3 = (bf16[1024,768]{1,0:T(8,128)(2,1)}, f32[8,768]{1,0:T(8,128)}) custom-call(bf16[1024,2304]{1,0:T(8,128)(2,1)} %attend_backward.3.refs_1_.packed_grad_ref, f32[1024,768]{1,0:T(8,128)} %convert_add_fusion.hidden_ref, f32[1024,768]{1,0:T(8,128)} %get-tuple-element.292.middle_grad_ref, f32[2,768]{1,0:T(2,128)} %squeeze.266.gains_ref, ...), custom_call_target="tpu_custom_call" | custom-call | flops 226492416 | bytes 1095552 | tf_op jit(solution)/shard_map/project_grad/pallas_call | solution.py:231
  525.0 2.2 fusion.8
  529.9 2.5 fusion.14
  532.8 3.7 all-to-all-start.4
  536.5 3.4 collective-permute-done.23
  546.2 13.9 %collective-permute-done.24 = bf16[48,1536]{1,0:T(8,128)(2,1)S(1)} collective-permute-done((bf16[48,1536]{1,0:T(8,128)(2,1)}, bf16[48,1536]{1,0:T(8,128)(2,1)S(1)}, u32[]{:S(2)}, u32[]{:S(2)}) %collective-permute-start.24) | collective-permute-done | bytes 147488 | tf_op jit(solution)/shard_map/ppermute | solution.py:593
  572.4 2.6 collective-permute-done.33
  578.1 2.4 collective-permute-done.38
  (264 shorter events, 96.4 us)
Async XLA Ops:
  7.2 85.0 %all-gather.5.cloned.1.call-start = ((), (), s32[]{:S(2)}) async-start(), calls=%async_computation.7 | async-start | bytes 5222400 | tf_op jit(solution)/shard_map/all_gather | solution.py:697
  12.6 173.7 %all-gather.7.cloned.1.call-start = ((), (), s32[]{:S(2)}) async-start(), calls=%async_computation.8 | async-start | bytes 10027008 | tf_op jit(solution)/shard_map/all_gather | solution.py:697
  13.6 216.0 %all-gather.9.cloned.1.call-start = ((), (), s32[]{:S(2)}) async-start(), calls=%async_computation.11 | async-start | bytes 5013504 | tf_op jit(solution)/shard_map/all_gather | solution.py:699
  15.1 8.1 %all-to-all-start = ((s32[2,512,2]{1,2,0:T(2,128)}), s32[2,512,2]{1,2,0:T(2,128)S(1)}, u32[]{:S(2)}, u32[]{:S(2)}) async-start(s32[2,512,2]{1,2,0:T(2,128)} %pad_add_fusion), calls=%async_computation | async-start | bytes 16384 | tf_op jit(solution)/shard_map/all_to_all | solution.py:581
  23.1 65.8 %all-to-all-start.1 = ((bf16[2,512,768]{2,1,0:T(8,128)(2,1)}), bf16[2,512,768]{2,1,0:T(8,128)(2,1)}, u32[]{:S(2)}, u32[]{:S(2)}) async-start(bf16[2,512,768]{2,1,0:T(8,128)(2,1)} %param.12), calls=%async_computation.1 | async-start | bytes 3145728 | tf_op jit(solution)/shard_map/all_to_all | solution.py:581
  27.8 19.4 %collective-permute-start = (bf16[1,48,1536]{2,1,0:T(8,128)(2,1)S(1)}, bf16[1,48,1536]{2,1,0:T(8,128)(2,1)S(1)}, u32[]{:S(2)}, u32[]{:S(2)}) collective-permute-start(bf16[1,48,1536]{2,1,0:T(8,128)(2,1)S(1)} %constant_dynamic-slice_fusion.21.refs_0_), channel_id=1, source_target_pairs={{0,16},{2,18},{4,20},{6,22},{8,24},{10,26},{12,28},{14,30},{16,0},... | collective-permute-start | bytes 442376 | tf_op jit(solution)/shard_map/ppermute | solution.py:590
  30.9 19.2 %collective-permute-start.1 = (bf16[1,96,768]{2,1,0:T(8,128)(2,1)S(1)}, bf16[1,96,768]{2,1,0:T(8,128)(2,1)S(1)}, u32[]{:S(2)}, u32[]{:S(2)}) collective-permute-start(bf16[1,96,768]{2,1,0:T(8,128)(2,1)S(1)} %constant_dynamic-slice_fusion.20.refs_0_), channel_id=1, source_target_pairs={{0,16},{2,18},{4,20},{6,22},{8,24},{10,26},{12,28},{14,30},{16,0},... | collective-permute-start | bytes 442376 | tf_op jit(solution)/shard_map/ppermute | solution.py:590
  50.9 22.4 %collective-permute-start.2 = (bf16[2,48,1536]{2,1,0:T(8,128)(2,1)S(1)}, bf16[2,48,1536]{2,1,0:T(8,128)(2,1)S(1)}, u32[]{:S(2)}, u32[]{:S(2)}) collective-permute-start(bf16[2,48,1536]{2,1,0:T(8,128)(2,1)S(1)} %bitcast.231), channel_id=1, source_target_pairs={{0,8},{2,10},{4,12},{6,14},{8,0},{10,2},{12,4},{14,6},{16,24},{18,... | collective-permute-start | bytes 884744 | tf_op jit(solution)/shard_map/ppermute | solution.py:590
  50.9 34.7 %collective-permute-start.3 = (bf16[2,96,768]{2,1,0:T(8,128)(2,1)S(1)}, bf16[2,96,768]{2,1,0:T(8,128)(2,1)S(1)}, u32[]{:S(2)}, u32[]{:S(2)}) collective-permute-start(bf16[2,96,768]{2,1,0:T(8,128)(2,1)S(1)} %bitcast.233), channel_id=1, source_target_pairs={{0,8},{2,10},{4,12},{6,14},{8,0},{10,2},{12,4},{14,6},{16,24},{18,... | collective-permute-start | bytes 884744 | tf_op jit(solution)/shard_map/ppermute | solution.py:590
  85.9 19.6 %collective-permute-start.4 = (bf16[4,48,1536]{2,1,0:T(8,128)(2,1)S(1)}, bf16[4,48,1536]{2,1,0:T(8,128)(2,1)S(1)}, u32[]{:S(2)}, u32[]{:S(2)}) collective-permute-start(bf16[4,48,1536]{2,1,0:T(8,128)(2,1)S(1)} %bitcast.229), channel_id=1, source_target_pairs={{0,4},{2,6},{4,0},{6,2},{8,12},{10,14},{12,8},{14,10},{16,20},{18,... | collective-permute-start | bytes 1769480 | tf_op jit(solution)/shard_map/ppermute | solution.py:590
  87.5 18.0 %collective-permute-start.5 = (bf16[4,96,768]{2,1,0:T(8,128)(2,1)S(1)}, bf16[4,96,768]{2,1,0:T(8,128)(2,1)S(1)}, u32[]{:S(2)}, u32[]{:S(2)}) collective-permute-start(bf16[4,96,768]{2,1,0:T(8,128)(2,1)S(1)} %bitcast.227), channel_id=1, source_target_pairs={{0,1},{1,0},{2,3},{3,2},{4,5},{5,4},{6,7},{7,6},{8,9},{9,8},{10,11... | collective-permute-start | bytes 1769480 | tf_op jit(solution)/shard_map/ppermute | solution.py:593
  105.8 28.7 %collective-permute-start.6 = (bf16[8,48,1536]{2,1,0:T(8,128)(2,1)S(1)}, bf16[8,48,1536]{2,1,0:T(8,128)(2,1)}, u32[]{:S(2)}, u32[]{:S(2)}) collective-permute-start(bf16[8,48,1536]{2,1,0:T(8,128)(2,1)S(1)} %bitcast.222), channel_id=1, source_target_pairs={{0,1},{1,0},{2,3},{3,2},{4,5},{5,4},{6,7},{7,6},{8,9},{9,8},{10,11... | collective-permute-start | bytes 3538952 | tf_op jit(solution)/shard_map/ppermute | solution.py:593
  106.6 35.7 %collective-permute-start.7 = (bf16[4,192,768]{2,1,0:T(8,128)(2,1)S(1)}, bf16[4,192,768]{2,1,0:T(8,128)(2,1)S(1)}, u32[]{:S(2)}, u32[]{:S(2)}) collective-permute-start(bf16[4,192,768]{2,1,0:T(8,128)(2,1)S(1)} %bitcast.225), channel_id=1, source_target_pairs={{0,4},{2,6},{4,0},{6,2},{8,12},{10,14},{12,8},{14,10},{16,20},{18,... | collective-permute-start | bytes 3538952 | tf_op jit(solution)/shard_map/ppermute | solution.py:590
  142.5 10.6 %collective-permute-start.10 = (bf16[8,192,768]{2,1,0:T(8,128)(2,1)S(1)}, bf16[8,192,768]{2,1,0:T(8,128)(2,1)}, u32[]{:S(2)}, u32[]{:S(2)}) collective-permute-start(bf16[8,192,768]{2,1,0:T(8,128)(2,1)S(1)} %bitcast.220), channel_id=1, source_target_pairs={{0,2},{2,0},{4,6},{6,4},{8,10},{10,8},{12,14},{14,12},{16,18},{18,... | collective-permute-start | bytes 7077896 | tf_op jit(solution)/shard_map/ppermute | solution.py:590
  142.6 10.5 %collective-permute-start.8 = (bf16[8,48,1536]{2,1,0:T(8,128)(2,1)S(1)}, bf16[8,48,1536]{2,1,0:T(8,128)(2,1)}, u32[]{:S(2)}, u32[]{:S(2)}) collective-permute-start(bf16[8,48,1536]{2,1,0:T(8,128)(2,1)S(1)} %bitcast.223), channel_id=1, source_target_pairs={{0,2},{2,0},{4,6},{6,4},{8,10},{10,8},{12,14},{14,12},{16,18},{18,... | collective-permute-start | bytes 3538952 | tf_op jit(solution)/shard_map/ppermute | solution.py:590
  143.1 10.0 %collective-permute-start.9 = (bf16[8,48,1536]{2,1,0:T(8,128)(2,1)}, bf16[8,48,1536]{2,1,0:T(8,128)(2,1)}, u32[]{:S(2)}, u32[]{:S(2)}) collective-permute-start(bf16[8,48,1536]{2,1,0:T(8,128)(2,1)} %collective-permute-done.6.refs_1_), channel_id=1, source_target_pairs={{0,2},{2,0},{4,6},{6,4},{8,10},{10,8},{12,14},{14,12},{16,18},{18,... | collective-permute-start | bytes 3538952 | tf_op jit(solution)/shard_map/ppermute | solution.py:590
  195.5 58.0 %all-to-all-start.2 = ((bf16[2,512,768]{2,1,0:T(8,128)(2,1)}), bf16[2,512,768]{2,1,0:T(8,128)(2,1)S(1)}, u32[]{:S(2)}, u32[]{:S(2)}) async-start(bf16[2,512,768]{2,1,0:T(8,128)(2,1)} %param.16), calls=%async_computation.2 | async-start | bytes 3145728 | tf_op jit(solution)/shard_map/all_to_all | solution.py:581
  199.3 242.8 %reduce-scatter.3.cloned.1.call-start = ((), (), s32[]{:S(2)}) async-start(), calls=%async_computation.9 | async-start | bytes 11280384 | tf_op jit(solution)/shard_map/reduce_scatter | solution.py:596
  306.2 41.0 %all-to-all-start.3 = ((bf16[2,512,768]{2,1,0:T(8,128)(2,1)}), bf16[2,512,768]{2,1,0:T(8,128)(2,1)S(1)}, u32[]{:S(2)}, u32[]{:S(2)}) async-start(bf16[2,512,768]{2,1,0:T(8,128)(2,1)} %bitcast.30), calls=%async_computation.3 | async-start | bytes 3145728 | tf_op jit(solution)/shard_map/all_to_all | solution.py:763
  309.9 213.1 %reduce-scatter.5.cloned.1.call-start = ((), (), s32[]{:S(2)}) async-start(), calls=%async_computation.10 | async-start | bytes 3760128 | tf_op jit(solution)/shard_map/reduce_scatter | solution.py:596
  370.5 9.1 %collective-permute-start.11 = (bf16[8,2,48,1536]{3,2,1,0:T(8,128)(2,1)}, bf16[8,2,48,1536]{3,2,1,0:T(8,128)(2,1)}, u32[]{:S(2)}, u32[]{:S(2)}) collective-permute-start(bf16[8,2,48,1536]{3,2,1,0:T(8,128)(2,1)} %get-tuple-element.249), channel_id=1, source_target_pairs={{0,2},{2,0},{4,6},{6,4},{8,10},{10,8},{12,14},{14,12},{16,18},{18,... | collective-permute-start | bytes 7077896 | tf_op jit(solution)/shard_map/ppermute | solution.py:590
  382.5 28.5 %collective-permute-start.12 = (bf16[2,2,2,48,1536]{4,3,2,1,0:T(8,128)(2,1)}, bf16[2,2,2,48,1536]{4,3,2,1,0:T(8,128)(2,1)S(1)}, u32[]{:S(2)}, u32[]{:S(2)}) collective-permute-start(bf16[2,2,2,48,1536]{4,3,2,1,0:T(8,128)(2,1)} %fusion.5), channel_id=1, source_target_pairs={{0,1},{1,0},{2,3},{3,2},{4,5},{5,4},{6,7},{7,6},{8,9},{9,8},{10,11... | collective-permute-start | bytes 3538952 | tf_op jit(solution)/shard_map/ppermute | solution.py:593
  426.6 5.7 collective-permute-start.13
  436.2 53.9 %collective-permute-start.15 = (bf16[2,2,2,48,1920]{4,3,2,1,0:T(8,128)(2,1)}, bf16[2,2,2,48,1920]{4,3,2,1,0:T(8,128)(2,1)S(1)}, u32[]{:S(2)}, u32[]{:S(2)}) collective-permute-start(bf16[2,2,2,48,1920]{4,3,2,1,0:T(8,128)(2,1)} %fusion.3), channel_id=1, source_target_pairs={{0,1},{1,0},{2,3},{3,2},{4,5},{5,4},{6,7},{7,6},{8,9},{9,8},{10,11... | collective-permute-start | bytes 4423688 | tf_op jit(solution)/shard_map/ppermute | solution.py:593
  441.4 48.6 %collective-permute-start.14 = (bf16[2,2,48,1536]{3,2,1,0:T(8,128)(2,1)}, bf16[2,2,48,1536]{3,2,1,0:T(8,128)(2,1)}, u32[]{:S(2)}, u32[]{:S(2)}) collective-permute-start(bf16[2,2,48,1536]{3,2,1,0:T(8,128)(2,1)} %fusion.6), channel_id=1, source_target_pairs={{0,4},{2,6},{4,0},{6,2},{8,12},{10,14},{12,8},{14,10},{16,20},{18,... | collective-permute-start | bytes 1769480 | tf_op jit(solution)/shard_map/ppermute | solution.py:590
  442.2 47.9 %collective-permute-start.16 = (bf16[48,6912]{1,0:T(8,128)(2,1)}, bf16[48,6912]{1,0:T(8,128)(2,1)}, u32[]{:S(2)}, u32[]{:S(2)}) collective-permute-start(bf16[48,6912]{1,0:T(8,128)(2,1)} %reduce-scatter.3.cloned.1.call-done), channel_id=1, source_target_pairs={{0,1},{1,0},{2,3},{3,2},{4,5},{5,4},{6,7},{7,6},{8,9},{9,8},{10,11... | collective-permute-start | bytes 1990664 | tf_op jit(solution)/shard_map/ppermute | solution.py:593
  500.7 24.3 %collective-permute-start.22 = (bf16[2,2,2,48,1152]{4,3,2,1,0:T(8,128)(2,1)}, bf16[2,2,2,48,1152]{4,3,2,1,0:T(8,128)(2,1)}, u32[]{:S(2)}, u32[]{:S(2)}) collective-permute-start(bf16[2,2,2,48,1152]{4,3,2,1,0:T(8,128)(2,1)} %fusion.7), channel_id=1, source_target_pairs={{0,1},{1,0},{2,3},{3,2},{4,5},{5,4},{6,7},{7,6},{8,9},{9,8},{10,11... | collective-permute-start | bytes 2654216 | tf_op jit(solution)/shard_map/ppermute | solution.py:593
  503.1 19.9 %collective-permute-start.21 = (bf16[2,2,48,1920]{3,2,1,0:T(8,128)(2,1)}, bf16[2,2,48,1920]{3,2,1,0:T(8,128)(2,1)S(1)}, u32[]{:S(2)}, u32[]{:S(2)}) collective-permute-start(bf16[2,2,48,1920]{3,2,1,0:T(8,128)(2,1)} %fusion.4), channel_id=1, source_target_pairs={{0,4},{2,6},{4,0},{6,2},{8,12},{10,14},{12,8},{14,10},{16,20},{18,... | collective-permute-start | bytes 2211848 | tf_op jit(solution)/shard_map/ppermute | solution.py:590
  504.4 18.6 %collective-permute-start.18 = (bf16[48,1536]{1,0:T(8,128)(2,1)}, bf16[48,1536]{1,0:T(8,128)(2,1)}, u32[]{:S(2)}, u32[]{:S(2)}) collective-permute-start(bf16[48,1536]{1,0:T(8,128)(2,1)} %get-tuple-element.300), channel_id=1, source_target_pairs={{0,8},{2,10},{4,12},{6,14},{8,0},{10,2},{12,4},{14,6},{16,24},{18,... | collective-permute-start | bytes 442376 | tf_op jit(solution)/shard_map/ppermute | solution.py:590
  506.2 16.8 %collective-permute-start.19 = (bf16[48,1536]{1,0:T(8,128)(2,1)}, bf16[48,1536]{1,0:T(8,128)(2,1)}, u32[]{:S(2)}, u32[]{:S(2)}) collective-permute-start(bf16[48,1536]{1,0:T(8,128)(2,1)} %get-tuple-element.301), channel_id=1, source_target_pairs={{0,16},{2,18},{4,20},{6,22},{8,24},{10,26},{12,28},{14,30},{16,0},... | collective-permute-start | bytes 442376 | tf_op jit(solution)/shard_map/ppermute | solution.py:590
  506.9 16.1 %collective-permute-start.20 = (bf16[48,1536]{1,0:T(8,128)(2,1)}, bf16[48,1536]{1,0:T(8,128)(2,1)}, u32[]{:S(2)}, u32[]{:S(2)}) collective-permute-start(bf16[48,1536]{1,0:T(8,128)(2,1)} %get-tuple-element.302), channel_id=1, source_target_pairs={{0,24},{2,26},{4,28},{6,30},{8,16},{10,18},{12,20},{14,22},{16,8},... | collective-permute-start | bytes 442376 | tf_op jit(solution)/shard_map/ppermute | solution.py:590
  523.0 17.7 %collective-permute-start.29 = (f32[2,2,1152]{2,1,0:T(2,128)}, f32[2,2,1152]{2,1,0:T(2,128)}, u32[]{:S(2)}, u32[]{:S(2)}) collective-permute-start(f32[2,2,1152]{2,1,0:T(2,128)} %bitcast.215), channel_id=1, source_target_pairs={{0,2},{2,0},{4,6},{6,4},{8,10},{10,8},{12,14},{14,12},{16,18},{18,... | collective-permute-start | bytes 55304 | tf_op jit(solution)/shard_map/ppermute | solution.py:590
  523.1 19.3 %collective-permute-start.30 = (f32[2,2,1152]{2,1,0:T(2,128)}, f32[2,2,1152]{2,1,0:T(2,128)S(1)}, u32[]{:S(2)}, u32[]{:S(2)}) collective-permute-start(f32[2,2,1152]{2,1,0:T(2,128)} %bitcast.214), channel_id=1, source_target_pairs={{0,4},{2,6},{4,0},{6,2},{8,12},{10,14},{12,8},{14,10},{16,20},{18,... | collective-permute-start | bytes 55304 | tf_op jit(solution)/shard_map/ppermute | solution.py:590
  523.9 20.4 %collective-permute-start.31 = (f32[2,2,1152]{2,1,0:T(2,128)}, f32[2,2,1152]{2,1,0:T(2,128)}, u32[]{:S(2)}, u32[]{:S(2)}) collective-permute-start(f32[2,2,1152]{2,1,0:T(2,128)} %bitcast.213), channel_id=1, source_target_pairs={{0,6},{2,4},{4,2},{6,0},{8,14},{10,12},{12,10},{14,8},{16,22},{18,... | collective-permute-start | bytes 55304 | tf_op jit(solution)/shard_map/ppermute | solution.py:590
  527.2 12.7 %collective-permute-start.23 = (bf16[2,2,48,1152]{3,2,1,0:T(8,128)(2,1)}, bf16[2,2,48,1152]{3,2,1,0:T(8,128)(2,1)}, u32[]{:S(2)}, u32[]{:S(2)}) collective-permute-start(bf16[2,2,48,1152]{3,2,1,0:T(8,128)(2,1)} %fusion.8), channel_id=1, source_target_pairs={{0,4},{2,6},{4,0},{6,2},{8,12},{10,14},{12,8},{14,10},{16,20},{18,... | collective-permute-start | bytes 1327112 | tf_op jit(solution)/shard_map/ppermute | solution.py:590
  532.4 27.6 %collective-permute-start.25 = (bf16[48,2304]{1,0:T(8,128)(2,1)}, bf16[48,2304]{1,0:T(8,128)(2,1)}, u32[]{:S(2)}, u32[]{:S(2)}) collective-permute-start(bf16[48,2304]{1,0:T(8,128)(2,1)} %reduce-scatter.5.cloned.1.call-done), channel_id=1, source_target_pairs={{0,1},{1,0},{2,3},{3,2},{4,5},{5,4},{6,7},{7,6},{8,9},{9,8},{10,11... | collective-permute-start | bytes 663560 | tf_op jit(solution)/shard_map/ppermute | solution.py:593
  532.8 54.7 %all-to-all-start.4 = ((bf16[2,512,768]{2,1,0:T(8,128)(2,1)}), bf16[2,512,768]{2,1,0:T(8,128)(2,1)S(1)}, u32[]{:S(2)}, u32[]{:S(2)}) async-start(bf16[2,512,768]{2,1,0:T(8,128)(2,1)} %bitcast.260), calls=%async_computation.6 | async-start | bytes 3145728 | tf_op jit(solution)/shard_map/all_to_all | solution.py:763
  539.9 20.1 %collective-permute-start.26 = (bf16[48,1920]{1,0:T(8,128)(2,1)}, bf16[48,1920]{1,0:T(8,128)(2,1)S(1)}, u32[]{:S(2)}, u32[]{:S(2)}) collective-permute-start(bf16[48,1920]{1,0:T(8,128)(2,1)} %get-tuple-element.322), channel_id=1, source_target_pairs={{0,8},{2,10},{4,12},{6,14},{8,0},{10,2},{12,4},{14,6},{16,24},{18,... | collective-permute-start | bytes 552968 | tf_op jit(solution)/shard_map/ppermute | solution.py:590
  540.7 19.3 %collective-permute-start.27 = (bf16[48,1920]{1,0:T(8,128)(2,1)}, bf16[48,1920]{1,0:T(8,128)(2,1)S(1)}, u32[]{:S(2)}, u32[]{:S(2)}) collective-permute-start(bf16[48,1920]{1,0:T(8,128)(2,1)} %get-tuple-element.323), channel_id=1, source_target_pairs={{0,16},{2,18},{4,20},{6,22},{8,24},{10,26},{12,28},{14,30},{16,0},... | collective-permute-start | bytes 552968 | tf_op jit(solution)/shard_map/ppermute | solution.py:590
  542.4 17.7 %collective-permute-start.28 = (bf16[48,1920]{1,0:T(8,128)(2,1)}, bf16[48,1920]{1,0:T(8,128)(2,1)S(1)}, u32[]{:S(2)}, u32[]{:S(2)}) collective-permute-start(bf16[48,1920]{1,0:T(8,128)(2,1)} %get-tuple-element.324), channel_id=1, source_target_pairs={{0,24},{2,26},{4,28},{6,30},{8,16},{10,18},{12,20},{14,22},{16,8},... | collective-permute-start | bytes 552968 | tf_op jit(solution)/shard_map/ppermute | solution.py:590
  544.3 15.7 %collective-permute-start.24 = (bf16[48,1536]{1,0:T(8,128)(2,1)}, bf16[48,1536]{1,0:T(8,128)(2,1)S(1)}, u32[]{:S(2)}, u32[]{:S(2)}) collective-permute-start(bf16[48,1536]{1,0:T(8,128)(2,1)} %fusion.21), channel_id=1, source_target_pairs={{0,1},{1,0},{2,3},{3,2},{4,5},{5,4},{6,7},{7,6},{8,9},{9,8},{10,11... | collective-permute-start | bytes 442376 | tf_op jit(solution)/shard_map/ppermute | solution.py:593
  563.2 7.2 %collective-permute-start.32 = (bf16[48,1152]{1,0:T(8,128)(2,1)S(1)}, bf16[48,1152]{1,0:T(8,128)(2,1)S(1)}, u32[]{:S(2)}, u32[]{:S(2)}) collective-permute-start(bf16[48,1152]{1,0:T(8,128)(2,1)S(1)} %get-tuple-element.336), channel_id=1, source_target_pairs={{0,8},{2,10},{4,12},{6,14},{8,0},{10,2},{12,4},{14,6},{16,24},{18,... | collective-permute-start | bytes 331784 | tf_op jit(solution)/shard_map/ppermute | solution.py:590
  564.2 10.9 %collective-permute-start.33 = (bf16[48,1152]{1,0:T(8,128)(2,1)S(1)}, bf16[48,1152]{1,0:T(8,128)(2,1)S(1)}, u32[]{:S(2)}, u32[]{:S(2)}) collective-permute-start(bf16[48,1152]{1,0:T(8,128)(2,1)S(1)} %get-tuple-element.337), channel_id=1, source_target_pairs={{0,16},{2,18},{4,20},{6,22},{8,24},{10,26},{12,28},{14,30},{16,0},... | collective-permute-start | bytes 331784 | tf_op jit(solution)/shard_map/ppermute | solution.py:590
  565.4 11.2 %collective-permute-start.34 = (bf16[48,1152]{1,0:T(8,128)(2,1)S(1)}, bf16[48,1152]{1,0:T(8,128)(2,1)S(1)}, u32[]{:S(2)}, u32[]{:S(2)}) collective-permute-start(bf16[48,1152]{1,0:T(8,128)(2,1)S(1)} %get-tuple-element.338), channel_id=1, source_target_pairs={{0,24},{2,26},{4,28},{6,30},{8,16},{10,18},{12,20},{14,22},{16,8},... | collective-permute-start | bytes 331784 | tf_op jit(solution)/shard_map/ppermute | solution.py:590
  567.6 12.9 %collective-permute-start.35 = (bf16[48,1920]{1,0:T(8,128)(2,1)S(1)}, bf16[48,1920]{1,0:T(8,128)(2,1)S(1)}, u32[]{:S(2)}, u32[]{:S(2)}) collective-permute-start(bf16[48,1920]{1,0:T(8,128)(2,1)S(1)} %fusion.13), channel_id=1, source_target_pairs={{0,1},{1,0},{2,3},{3,2},{4,5},{5,4},{6,7},{7,6},{8,9},{9,8},{10,11... | collective-permute-start | bytes 552968 | tf_op jit(solution)/shard_map/ppermute | solution.py:593
  567.9 10.2 %collective-permute-start.36 = (f32[1152]{0:T(1024)S(1)}, f32[1152]{0:T(1024)S(1)}, u32[]{:S(2)}, u32[]{:S(2)}) collective-permute-start(f32[1152]{0:T(1024)S(1)} %add_add_fusion.3), channel_id=1, source_target_pairs={{0,8},{2,10},{4,12},{6,14},{8,0},{10,2},{12,4},{14,6},{16,24},{18,... | collective-permute-start | bytes 13832 | tf_op jit(solution)/shard_map/ppermute | solution.py:590
  570.3 7.8 %collective-permute-start.37 = (f32[1152]{0:T(1024)S(1)}, f32[1152]{0:T(1024)S(1)}, u32[]{:S(2)}, u32[]{:S(2)}) collective-permute-start(f32[1152]{0:T(1024)S(1)} %add_add_fusion.2), channel_id=1, source_target_pairs={{0,16},{2,18},{4,20},{6,22},{8,24},{10,26},{12,28},{14,30},{16,0},... | collective-permute-start | bytes 13832 | tf_op jit(solution)/shard_map/ppermute | solution.py:590
  575.1 5.4 collective-permute-start.38
  (30 other events, 237.8 us)
Sparse Core Ops, SparseCore 0:
  12.7 72.6 all-gather.4
  88.3 86.4 all-gather.6
  177.6 51.9 all-gather.8
  306.3 118.7 reduce-scatter.2
  438.0 65.9 reduce-scatter.4

commit v16 on v15

--- a/solution.py
+++ b/solution.py
@@ -9,7 +9,7 @@
 
 HEAD_SIZE = 64
 PAIR = 2 * HEAD_SIZE
-FORWARD_ROWS = 1024
+FORWARD_ROWS = 512
 BACKWARD_ROWS = 256
 ROW_TILE = 256
 FF_CHUNK = 1024

time: 607 us -> 607 us (level)
  transfers between devices with their start and end apart: 51 -> 51, of which waited for: 15 -> 15; matrix products, arithmetic and copies ran while one was open for 12% -> 12% of each run, Pallas kernels for 47% -> 48%
where the time goes in v16:
time: 607 us; the launch traced here: 596 us
  Pallas kernels  335 us (55%)
  waiting for transfers between devices  104 us (17%)
  starting transfers between devices  60.5 us (10%)
  other arithmetic  47.5 us (8%)
  local copies, waits for them, and re-layouts  34.7 us (6%)
  between operations  15.1 us (2%)
    pallas_call x8, Pallas kernels, row_tiled(): pl.pallas_call(kernel, grid=(length // ROW_TILE,), in_specs=in_specs, out...  141 us
    pallas_call x2, Pallas kernels, attend_backward(): pl.pallas_call(functools.partial(attend_grad_kernel, rows=BACKWARD_ROWS),...  74.7 us
    ppermute x30, waiting for transfers between devices, across(): return lambda part: lax.ppermute(part, 'wide', pairs)  74.4 us
    pallas_call x5, Pallas kernels, term_blocks(): pl.pallas_call(kernel, in_specs=[pl.BlockSpec(memory_space=pltpu.SMEM)] +...  63 us
    pallas_call x2, Pallas kernels, attend_forward(): pl.pallas_call(functools.partial(attend_kernel, rows=FORWARD_ROWS), grid=...  50.4 us
    ppermute x30, starting transfers between devices, across(): return lambda part: lax.ppermute(part, 'wide', pairs)  31 us
    ppermute x11, waiting for transfers between devices, beside_seq(): return lax.ppermute(part, 'seq', swap)  20.9 us
    convert_element_type x6, other arithmetic, reduce_group(): total_of([side_of(part, 1 - mine, axis) for part in addends]).astype(half)  15.8 us
  transfers between devices with their start and end apart: 51, of which 15 were waited for; matrix products, arithmetic and copies ran while one was open for 12% of the time, Pallas kernels for 48%

profile of v16, /device:TPU:0, one launch (start us, length us, event | category | flops | bytes accessed | tf_op | source)
XLA Modules:
  0.0 596.3 jit_solution(15600666573160291864)
XLA Ops:
  15.1 4.2 all-to-all-start
  19.3 3.8 all-to-all-done
  23.1 4.6 all-to-all-start.1
  27.8 3.1 collective-permute-start
  31.0 16.2 %collective-permute-done.refs_1_ = bf16[1,48,1536]{2,1,0:T(8,128)(2,1)S(1)} collective-permute-done((bf16[1,48,1536]{2,1,0:T(8,128)(2,1)S(1)}, bf16[1,48,1536]{2,1,0:T(8,128)(2,1)S(1)}, u32[]{:S(2)}, u32[]{:S(2)}) %collective-permute-start) | collective-permute-done | bytes 147488 | tf_op jit(solution)/shard_map/ppermute | solution.py:590
  47.2 2.9 collective-permute-done.1.refs_1_
  53.0 20.3 %collective-permute-done.2.refs_1_ = bf16[2,48,1536]{2,1,0:T(8,128)(2,1)S(1)} collective-permute-done((bf16[2,48,1536]{2,1,0:T(8,128)(2,1)S(1)}, bf16[2,48,1536]{2,1,0:T(8,128)(2,1)S(1)}, u32[]{:S(2)}, u32[]{:S(2)}) %collective-permute-start.2) | collective-permute-done | bytes 294944 | tf_op jit(solution)/shard_map/ppermute | solution.py:590
  73.2 12.5 %collective-permute-done.3.refs_1_ = bf16[2,96,768]{2,1,0:T(8,128)(2,1)S(1)} collective-permute-done((bf16[2,96,768]{2,1,0:T(8,128)(2,1)S(1)}, bf16[2,96,768]{2,1,0:T(8,128)(2,1)S(1)}, u32[]{:S(2)}, u32[]{:S(2)}) %collective-permute-start.3) | collective-permute-done | bytes 294944 | tf_op jit(solution)/shard_map/ppermute | solution.py:590
  89.0 3.3 convert_add_fusion.hidden_ref
  96.3 9.2 %project.2 = (bf16[1024,768]{1,0:T(8,128)(2,1)}, bf16[1024,2304]{1,0:T(8,128)(2,1)}) custom-call(f32[1024,768]{1,0:T(8,128)} %convert_add_fusion.hidden_ref, f32[2,768]{1,0:T(2,128)} %squeeze.266.gains_ref, f32[6,768]{1,0:T(8,128)} %squeeze.267.offsets_ref, bf16[768,3200]{1,0:T(8,128)(2,1)} %all-gather.5.cloned.1.call-done.weight_ref.out_weight_ref), custom_call_target="tpu_custom_call" | custom-call | flops 226492416 | bytes 898560 | tf_op jit(solution)/shard_map/project/pallas_call | solution.py:231
  107.9 2.8 fusion.2.bias_ref
  110.7 25.2 %attend_forward.2 = (bf16[1024,768]{1,0:T(8,128)(2,1)}, f32[6,2,1024]{2,1,0:T(2,128)}) custom-call(bf16[1024,2304]{1,0:T(8,128)(2,1)} %get-tuple-element.207.query_ref.key_ref.value_ref, bf16[1024,2304]{1,0:T(8,128)(2,1)} %get-tuple-element.207.query_ref.key_ref.value_ref, bf16[1024,2304]{1,0:T(8,128)(2,1)} %get-tuple-element.207.query_ref.key_ref.value_ref, ...), custom_call_target="tpu_custom_call" | custom-call | flops 805306368 | bytes 393216 | tf_op jit(solution)/shard_map/attend_forward/pallas_call | solution.py:68
  135.9 6.4 %collective-permute-done.7.refs_1_ = bf16[4,192,768]{2,1,0:T(8,128)(2,1)S(1)} collective-permute-done((bf16[4,192,768]{2,1,0:T(8,128)(2,1)S(1)}, bf16[4,192,768]{2,1,0:T(8,128)(2,1)S(1)}, u32[]{:S(2)}, u32[]{:S(2)}) %collective-permute-start.7) | collective-permute-done | bytes 1179680 | tf_op jit(solution)/shard_map/ppermute | solution.py:590
  157.1 2.7 place_pieces.16
  159.8 2.2 copy-done.3
  162.0 24.2 %feed.2 = (f32[1024,768]{1,0:T(8,128)}, bf16[1024,768]{1,0:T(8,128)(2,1)}, bf16[1024,3072]{1,0:T(8,128)(2,1)}, bf16[1024,3072]{1,0:T(8,128)(2,1)}, f32[1024,768]{1,0:T(8,128)}) custom-call(bf16[1024,768]{1,0:T(8,128)(2,1)} %get-tuple-element.219.attended_ref.refs_2_, f32[1024,768]{1,0:T(8,128)} %convert_add_fusion.hidden_ref, f32[2,768]{1,0:T(2,128)} %squeeze.266.gains_ref, ...), custom_call_target="tpu_custom_call" | custom-call | flops 679477248 | bytes 2472192 | tf_op jit(solution)/shard_map/feed/pallas_call | solution.py:231
  186.3 9.2 %project.3 = (bf16[1024,768]{1,0:T(8,128)(2,1)}, bf16[1024,2304]{1,0:T(8,128)(2,1)}) custom-call(f32[1024,768]{1,0:T(8,128)} %get-tuple-element.223.hidden_ref, f32[2,768]{1,0:T(2,128)} %squeeze.268.gains_ref, f32[6,768]{1,0:T(8,128)} %squeeze.269.offsets_ref, bf16[768,6144]{1,0:T(8,128)(2,1)} %all-gather.7.cloned.1.call-done.weight_ref.out_weight_ref.up_ref), custom_call_target="tpu_custom_call" | custom-call | flops 226492416 | bytes 1181184 | tf_op jit(solution)/shard_map/project/pallas_call | solution.py:231
  195.5 3.8 all-to-all-start.2
  200.1 25.2 %attend_forward.3 = (bf16[1024,768]{1,0:T(8,128)(2,1)}, f32[6,2,1024]{2,1,0:T(2,128)}) custom-call(bf16[1024,2304]{1,0:T(8,128)(2,1)} %get-tuple-element.225.query_ref.key_ref.value_ref, bf16[1024,2304]{1,0:T(8,128)(2,1)} %get-tuple-element.225.query_ref.key_ref.value_ref, bf16[1024,2304]{1,0:T(8,128)(2,1)} %get-tuple-element.225.query_ref.key_ref.value_ref, ...), custom_call_target="tpu_custom_call" | custom-call | flops 805306368 | bytes 393216 | tf_op jit(solution)/shard_map/attend_forward/pallas_call | solution.py:68
  225.2 4.4 all-gather.9.cloned.1.call-done
  229.6 23.9 %feed.3 = (f32[1024,768]{1,0:T(8,128)}, bf16[1024,768]{1,0:T(8,128)(2,1)}, bf16[1024,3072]{1,0:T(8,128)(2,1)}, bf16[1024,3072]{1,0:T(8,128)(2,1)}, bf16[1024,768]{1,0:T(8,128)(2,1)}) custom-call(bf16[1024,768]{1,0:T(8,128)(2,1)} %get-tuple-element.227.attended_ref.refs_4_, f32[1024,768]{1,0:T(8,128)} %get-tuple-element.223.hidden_ref, ...), custom_call_target="tpu_custom_call" | custom-call | flops 679477248 | bytes 2951424 | tf_op jit(solution)/shard_map/feed/pallas_call | solution.py:231
  254.7 31.8 %feed_grad.2 = (bf16[1024,768]{1,0:T(8,128)(2,1)}, bf16[1024,3072]{1,0:T(8,128)(2,1)}, f32[1024,768]{1,0:T(8,128)}, bf16[1024,768]{1,0:T(8,128)(2,1)}, bf16[1024...) custom-call(bf16[1024,768]{1,0:T(8,128)(2,1)} %bitcast.239, ...), custom_call_target="tpu_custom_call" | custom-call | flops 679477248 | bytes 3050112 | tf_op jit(solution)/shard_map/feed_grad/pallas_call | solution.py:231
  286.5 19.7 %term_blocks.5 = bf16[16,48,6912]{2,1,0:T(8,128)(2,1)} custom-call(s32[1]{0:T(128)} %bitcast.20.core_ref, bf16[1024,3072]{1,0:T(8,128)(2,1)} %get-tuple-element.231.refs_0_, bf16[1024,768]{1,0:T(8,128)(2,1)} %get-tuple-element.232.refs_1_, bf16[1024,768]{1,0:T(8,128)(2,1)} %get-tuple-element.233.refs_2_, bf16[1024,3072]{1,0:T(8,128)(2,1)} %get-tuple-element.234.refs_3_, ...), custom_call_target="tpu_custom_call" | custom-call | flops 679477248 | bytes 1843200 | tf_op jit(solution)/shard_map/term_blocks/pallas_call | solution.py:548
  306.2 3.7 all-to-all-start.3
  309.9 37.3 %attend_backward.2.packed_grad_ref.refs_1_ = bf16[1024,2304]{1,0:T(8,128)(2,1)} custom-call(bf16[1024,2304]{1,0:T(8,128)(2,1)} %get-tuple-element.225.query_ref.key_ref.value_ref, bf16[1024,2304]{1,0:T(8,128)(2,1)} %get-tuple-element.225.query_ref.key_ref.value_ref, bf16[1024,2304]{1,0:T(8,128)(2,1)} %get-tuple-element.225.query_ref.key_ref.value_ref, ...), custom_call_target="tpu_custom_call" | custom-call | flops 2013265920 | bytes 786432 | tf_op jit(solution)/shard_map/attend_backward/pallas_call | solution.py:151
  347.2 11.1 %project_grad.2 = (f32[1024,768]{1,0:T(8,128)}, bf16[1024,768]{1,0:T(8,128)(2,1)}, f32[8,768]{1,0:T(8,128)}) custom-call(bf16[1024,2304]{1,0:T(8,128)(2,1)} %attend_backward.2.packed_grad_ref.refs_1_, f32[1024,768]{1,0:T(8,128)} %get-tuple-element.223.hidden_ref, f32[1024,768]{1,0:T(8,128)} %get-tuple-element.241.middle_grad_ref, ...), custom_call_target="tpu_custom_call" | custom-call | flops 226492416 | bytes 1574784 | tf_op jit(solution)/shard_map/project_grad/pallas_call | solution.py:231
  358.3 12.2 %term_blocks.6 = (bf16[8,2,48,1536]{3,2,1,0:T(8,128)(2,1)}, bf16[8,2,48,1536]{3,2,1,0:T(8,128)(2,1)}) custom-call(s32[1]{0:T(128)} %bitcast.20.core_ref, bf16[1024,3072]{1,0:T(8,128)(2,1)} %get-tuple-element.243.refs_0_, bf16[1024,768]{1,0:T(8,128)(2,1)} %get-tuple-element.244.refs_1_), custom_call_target="tpu_custom_call" | custom-call | flops 301989888 | bytes 786432 | tf_op jit(solution)/shard_map/term_blocks/pallas_call | solution.py:548
  370.9 8.6 %term_blocks.7 = bf16[16,48,2304]{2,1,0:T(8,128)(2,1)} custom-call(s32[1]{0:T(128)} %bitcast.20.core_ref, bf16[1024,768]{1,0:T(8,128)(2,1)} %get-tuple-element.247.refs_0_, bf16[1024,2304]{1,0:T(8,128)(2,1)} %attend_backward.2.packed_grad_ref.refs_1_), custom_call_target="tpu_custom_call" | custom-call | flops 226492416 | bytes 614400 | tf_op jit(solution)/shard_map/term_blocks/pallas_call | solution.py:548
  379.5 3.0 fusion.5
  384.1 21.2 %feed_grad.3 = (bf16[1024,768]{1,0:T(8,128)(2,1)}, bf16[1024,3072]{1,0:T(8,128)(2,1)}, f32[1024,768]{1,0:T(8,128)}, bf16[1024,768]{1,0:T(8,128)(2,1)}, bf16[1024...) custom-call(f32[1024,768]{1,0:T(8,128)} %get-tuple-element.253.gradient_ref, ...), custom_call_target="tpu_custom_call" | custom-call | flops 679477248 | bytes 2570880 | tf_op jit(solution)/shard_map/feed_grad/pallas_call | solution.py:231
  405.4 5.6 collective-permute-done.12
  411.0 2.8 fusion.6
  413.7 12.8 %term_blocks.8 = (bf16[8,2,48,1920]{3,2,1,0:T(8,128)(2,1)}, bf16[8,2,48,1920]{3,2,1,0:T(8,128)(2,1)}) custom-call(s32[1]{0:T(128)} %bitcast.20.core_ref, bf16[1024,768]{1,0:T(8,128)(2,1)} %get-tuple-element.264.refs_0_, bf16[1024,3072]{1,0:T(8,128)(2,1)} %get-tuple-element.265.refs_1_, bf16[1024,768]{1,0:T(8,128)(2,1)} %get-tuple-element.219.attended_ref.refs_2_, ...), custom_call_target="tpu_custom_call" | custom-call | flops 377487360 | bytes 1056768 | tf_op jit(solution)/shard_map/term_blocks/pallas_call | solution.py:548
  426.6 5.6 collective-permute-done.13
  432.2 3.9 fusion.3
  442.7 37.5 %attend_backward.3.refs_1_.packed_grad_ref = bf16[1024,2304]{1,0:T(8,128)(2,1)} custom-call(bf16[1024,2304]{1,0:T(8,128)(2,1)} %get-tuple-element.207.query_ref.key_ref.value_ref, bf16[1024,2304]{1,0:T(8,128)(2,1)} %get-tuple-element.207.query_ref.key_ref.value_ref, bf16[1024,2304]{1,0:T(8,128)(2,1)} %get-tuple-element.207.query_ref.key_ref.value_ref, ...), custom_call_target="tpu_custom_call" | custom-call | flops 2013265920 | bytes 786432 | tf_op jit(solution)/shard_map/attend_backward/pallas_call | solution.py:151
  480.2 9.8 %term_blocks.9 = (bf16[8,2,48,1152]{3,2,1,0:T(8,128)(2,1)}, bf16[8,2,48,1152]{3,2,1,0:T(8,128)(2,1)}) custom-call(s32[1]{0:T(128)} %bitcast.20.core_ref, bf16[1024,768]{1,0:T(8,128)(2,1)} %get-tuple-element.284.refs_0_, bf16[1024,2304]{1,0:T(8,128)(2,1)} %attend_backward.3.refs_1_.packed_grad_ref), custom_call_target="tpu_custom_call" | custom-call | flops 226492416 | bytes 614400 | tf_op jit(solution)/shard_map/term_blocks/pallas_call | solution.py:548
  490.1 2.9 fusion.22
  492.9 2.6 fusion.4
  497.1 2.3 collective-permute-done.17
  508.9 10.0 %project_grad.3 = (bf16[1024,768]{1,0:T(8,128)(2,1)}, f32[8,768]{1,0:T(8,128)}) custom-call(bf16[1024,2304]{1,0:T(8,128)(2,1)} %attend_backward.3.refs_1_.packed_grad_ref, f32[1024,768]{1,0:T(8,128)} %convert_add_fusion.hidden_ref, f32[1024,768]{1,0:T(8,128)} %get-tuple-element.292.middle_grad_ref, f32[2,768]{1,0:T(2,128)} %squeeze.266.gains_ref, ...), custom_call_target="tpu_custom_call" | custom-call | flops 226492416 | bytes 1095552 | tf_op jit(solution)/shard_map/project_grad/pallas_call | solution.py:231
  525.0 2.2 fusion.8
  529.9 2.5 fusion.14
  532.8 3.7 all-to-all-start.4
  536.5 3.5 collective-permute-done.23
  546.2 13.8 %collective-permute-done.24 = bf16[48,1536]{1,0:T(8,128)(2,1)S(1)} collective-permute-done((bf16[48,1536]{1,0:T(8,128)(2,1)}, bf16[48,1536]{1,0:T(8,128)(2,1)S(1)}, u32[]{:S(2)}, u32[]{:S(2)}) %collective-permute-start.24) | collective-permute-done | bytes 147488 | tf_op jit(solution)/shard_map/ppermute | solution.py:593
  572.4 2.6 collective-permute-done.33
  578.2 2.3 collective-permute-done.38
  (264 shorter events, 96.4 us)
Async XLA Ops:
  7.2 85.0 %all-gather.5.cloned.1.call-start = ((), (), s32[]{:S(2)}) async-start(), calls=%async_computation.7 | async-start | bytes 5222400 | tf_op jit(solution)/shard_map/all_gather | solution.py:697
  12.6 173.7 %all-gather.7.cloned.1.call-start = ((), (), s32[]{:S(2)}) async-start(), calls=%async_computation.8 | async-start | bytes 10027008 | tf_op jit(solution)/shard_map/all_gather | solution.py:697
  13.6 216.0 %all-gather.9.cloned.1.call-start = ((), (), s32[]{:S(2)}) async-start(), calls=%async_computation.11 | async-start | bytes 5013504 | tf_op jit(solution)/shard_map/all_gather | solution.py:699
  15.1 8.1 %all-to-all-start = ((s32[2,512,2]{1,2,0:T(2,128)}), s32[2,512,2]{1,2,0:T(2,128)S(1)}, u32[]{:S(2)}, u32[]{:S(2)}) async-start(s32[2,512,2]{1,2,0:T(2,128)} %pad_add_fusion), calls=%async_computation | async-start | bytes 16384 | tf_op jit(solution)/shard_map/all_to_all | solution.py:581
  23.1 65.8 %all-to-all-start.1 = ((bf16[2,512,768]{2,1,0:T(8,128)(2,1)}), bf16[2,512,768]{2,1,0:T(8,128)(2,1)}, u32[]{:S(2)}, u32[]{:S(2)}) async-start(bf16[2,512,768]{2,1,0:T(8,128)(2,1)} %param.12), calls=%async_computation.1 | async-start | bytes 3145728 | tf_op jit(solution)/shard_map/all_to_all | solution.py:581
  27.8 19.4 %collective-permute-start = (bf16[1,48,1536]{2,1,0:T(8,128)(2,1)S(1)}, bf16[1,48,1536]{2,1,0:T(8,128)(2,1)S(1)}, u32[]{:S(2)}, u32[]{:S(2)}) collective-permute-start(bf16[1,48,1536]{2,1,0:T(8,128)(2,1)S(1)} %constant_dynamic-slice_fusion.21.refs_0_), channel_id=1, source_target_pairs={{0,16},{2,18},{4,20},{6,22},{8,24},{10,26},{12,28},{14,30},{16,0},... | collective-permute-start | bytes 442376 | tf_op jit(solution)/shard_map/ppermute | solution.py:590
  30.9 19.2 %collective-permute-start.1 = (bf16[1,96,768]{2,1,0:T(8,128)(2,1)S(1)}, bf16[1,96,768]{2,1,0:T(8,128)(2,1)S(1)}, u32[]{:S(2)}, u32[]{:S(2)}) collective-permute-start(bf16[1,96,768]{2,1,0:T(8,128)(2,1)S(1)} %constant_dynamic-slice_fusion.20.refs_0_), channel_id=1, source_target_pairs={{0,16},{2,18},{4,20},{6,22},{8,24},{10,26},{12,28},{14,30},{16,0},... | collective-permute-start | bytes 442376 | tf_op jit(solution)/shard_map/ppermute | solution.py:590
  50.9 22.4 %collective-permute-start.2 = (bf16[2,48,1536]{2,1,0:T(8,128)(2,1)S(1)}, bf16[2,48,1536]{2,1,0:T(8,128)(2,1)S(1)}, u32[]{:S(2)}, u32[]{:S(2)}) collective-permute-start(bf16[2,48,1536]{2,1,0:T(8,128)(2,1)S(1)} %bitcast.231), channel_id=1, source_target_pairs={{0,8},{2,10},{4,12},{6,14},{8,0},{10,2},{12,4},{14,6},{16,24},{18,... | collective-permute-start | bytes 884744 | tf_op jit(solution)/shard_map/ppermute | solution.py:590
  50.9 34.7 %collective-permute-start.3 = (bf16[2,96,768]{2,1,0:T(8,128)(2,1)S(1)}, bf16[2,96,768]{2,1,0:T(8,128)(2,1)S(1)}, u32[]{:S(2)}, u32[]{:S(2)}) collective-permute-start(bf16[2,96,768]{2,1,0:T(8,128)(2,1)S(1)} %bitcast.233), channel_id=1, source_target_pairs={{0,8},{2,10},{4,12},{6,14},{8,0},{10,2},{12,4},{14,6},{16,24},{18,... | collective-permute-start | bytes 884744 | tf_op jit(solution)/shard_map/ppermute | solution.py:590
  85.9 19.6 %collective-permute-start.4 = (bf16[4,48,1536]{2,1,0:T(8,128)(2,1)S(1)}, bf16[4,48,1536]{2,1,0:T(8,128)(2,1)S(1)}, u32[]{:S(2)}, u32[]{:S(2)}) collective-permute-start(bf16[4,48,1536]{2,1,0:T(8,128)(2,1)S(1)} %bitcast.229), channel_id=1, source_target_pairs={{0,4},{2,6},{4,0},{6,2},{8,12},{10,14},{12,8},{14,10},{16,20},{18,... | collective-permute-start | bytes 1769480 | tf_op jit(solution)/shard_map/ppermute | solution.py:590
  87.5 18.0 %collective-permute-start.5 = (bf16[4,96,768]{2,1,0:T(8,128)(2,1)S(1)}, bf16[4,96,768]{2,1,0:T(8,128)(2,1)S(1)}, u32[]{:S(2)}, u32[]{:S(2)}) collective-permute-start(bf16[4,96,768]{2,1,0:T(8,128)(2,1)S(1)} %bitcast.227), channel_id=1, source_target_pairs={{0,1},{1,0},{2,3},{3,2},{4,5},{5,4},{6,7},{7,6},{8,9},{9,8},{10,11... | collective-permute-start | bytes 1769480 | tf_op jit(solution)/shard_map/ppermute | solution.py:593
  105.8 30.1 %collective-permute-start.6 = (bf16[8,48,1536]{2,1,0:T(8,128)(2,1)S(1)}, bf16[8,48,1536]{2,1,0:T(8,128)(2,1)}, u32[]{:S(2)}, u32[]{:S(2)}) collective-permute-start(bf16[8,48,1536]{2,1,0:T(8,128)(2,1)S(1)} %bitcast.222), channel_id=1, source_target_pairs={{0,1},{1,0},{2,3},{3,2},{4,5},{5,4},{6,7},{7,6},{8,9},{9,8},{10,11... | collective-permute-start | bytes 3538952 | tf_op jit(solution)/shard_map/ppermute | solution.py:593
  106.6 35.7 %collective-permute-start.7 = (bf16[4,192,768]{2,1,0:T(8,128)(2,1)S(1)}, bf16[4,192,768]{2,1,0:T(8,128)(2,1)S(1)}, u32[]{:S(2)}, u32[]{:S(2)}) collective-permute-start(bf16[4,192,768]{2,1,0:T(8,128)(2,1)S(1)} %bitcast.225), channel_id=1, source_target_pairs={{0,4},{2,6},{4,0},{6,2},{8,12},{10,14},{12,8},{14,10},{16,20},{18,... | collective-permute-start | bytes 3538952 | tf_op jit(solution)/shard_map/ppermute | solution.py:590
  142.5 10.6 %collective-permute-start.10 = (bf16[8,192,768]{2,1,0:T(8,128)(2,1)S(1)}, bf16[8,192,768]{2,1,0:T(8,128)(2,1)}, u32[]{:S(2)}, u32[]{:S(2)}) collective-permute-start(bf16[8,192,768]{2,1,0:T(8,128)(2,1)S(1)} %bitcast.220), channel_id=1, source_target_pairs={{0,2},{2,0},{4,6},{6,4},{8,10},{10,8},{12,14},{14,12},{16,18},{18,... | collective-permute-start | bytes 7077896 | tf_op jit(solution)/shard_map/ppermute | solution.py:590
  142.6 10.5 %collective-permute-start.8 = (bf16[8,48,1536]{2,1,0:T(8,128)(2,1)S(1)}, bf16[8,48,1536]{2,1,0:T(8,128)(2,1)}, u32[]{:S(2)}, u32[]{:S(2)}) collective-permute-start(bf16[8,48,1536]{2,1,0:T(8,128)(2,1)S(1)} %bitcast.223), channel_id=1, source_target_pairs={{0,2},{2,0},{4,6},{6,4},{8,10},{10,8},{12,14},{14,12},{16,18},{18,... | collective-permute-start | bytes 3538952 | tf_op jit(solution)/shard_map/ppermute | solution.py:590
  143.1 10.0 %collective-permute-start.9 = (bf16[8,48,1536]{2,1,0:T(8,128)(2,1)}, bf16[8,48,1536]{2,1,0:T(8,128)(2,1)}, u32[]{:S(2)}, u32[]{:S(2)}) collective-permute-start(bf16[8,48,1536]{2,1,0:T(8,128)(2,1)} %collective-permute-done.6.refs_1_), channel_id=1, source_target_pairs={{0,2},{2,0},{4,6},{6,4},{8,10},{10,8},{12,14},{14,12},{16,18},{18,... | collective-permute-start | bytes 3538952 | tf_op jit(solution)/shard_map/ppermute | solution.py:590
  195.5 58.0 %all-to-all-start.2 = ((bf16[2,512,768]{2,1,0:T(8,128)(2,1)}), bf16[2,512,768]{2,1,0:T(8,128)(2,1)S(1)}, u32[]{:S(2)}, u32[]{:S(2)}) async-start(bf16[2,512,768]{2,1,0:T(8,128)(2,1)} %param.16), calls=%async_computation.2 | async-start | bytes 3145728 | tf_op jit(solution)/shard_map/all_to_all | solution.py:581
  199.3 242.8 %reduce-scatter.3.cloned.1.call-start = ((), (), s32[]{:S(2)}) async-start(), calls=%async_computation.9 | async-start | bytes 11280384 | tf_op jit(solution)/shard_map/reduce_scatter | solution.py:596
  306.2 41.0 %all-to-all-start.3 = ((bf16[2,512,768]{2,1,0:T(8,128)(2,1)}), bf16[2,512,768]{2,1,0:T(8,128)(2,1)S(1)}, u32[]{:S(2)}, u32[]{:S(2)}) async-start(bf16[2,512,768]{2,1,0:T(8,128)(2,1)} %bitcast.30), calls=%async_computation.3 | async-start | bytes 3145728 | tf_op jit(solution)/shard_map/all_to_all | solution.py:763
  309.9 213.1 %reduce-scatter.5.cloned.1.call-start = ((), (), s32[]{:S(2)}) async-start(), calls=%async_computation.10 | async-start | bytes 3760128 | tf_op jit(solution)/shard_map/reduce_scatter | solution.py:596
  370.5 9.1 %collective-permute-start.11 = (bf16[8,2,48,1536]{3,2,1,0:T(8,128)(2,1)}, bf16[8,2,48,1536]{3,2,1,0:T(8,128)(2,1)}, u32[]{:S(2)}, u32[]{:S(2)}) collective-permute-start(bf16[8,2,48,1536]{3,2,1,0:T(8,128)(2,1)} %get-tuple-element.249), channel_id=1, source_target_pairs={{0,2},{2,0},{4,6},{6,4},{8,10},{10,8},{12,14},{14,12},{16,18},{18,... | collective-permute-start | bytes 7077896 | tf_op jit(solution)/shard_map/ppermute | solution.py:590
  382.5 28.5 %collective-permute-start.12 = (bf16[2,2,2,48,1536]{4,3,2,1,0:T(8,128)(2,1)}, bf16[2,2,2,48,1536]{4,3,2,1,0:T(8,128)(2,1)S(1)}, u32[]{:S(2)}, u32[]{:S(2)}) collective-permute-start(bf16[2,2,2,48,1536]{4,3,2,1,0:T(8,128)(2,1)} %fusion.5), channel_id=1, source_target_pairs={{0,1},{1,0},{2,3},{3,2},{4,5},{5,4},{6,7},{7,6},{8,9},{9,8},{10,11... | collective-permute-start | bytes 3538952 | tf_op jit(solution)/shard_map/ppermute | solution.py:593
  426.6 5.7 collective-permute-start.13
  436.2 53.9 %collective-permute-start.15 = (bf16[2,2,2,48,1920]{4,3,2,1,0:T(8,128)(2,1)}, bf16[2,2,2,48,1920]{4,3,2,1,0:T(8,128)(2,1)S(1)}, u32[]{:S(2)}, u32[]{:S(2)}) collective-permute-start(bf16[2,2,2,48,1920]{4,3,2,1,0:T(8,128)(2,1)} %fusion.3), channel_id=1, source_target_pairs={{0,1},{1,0},{2,3},{3,2},{4,5},{5,4},{6,7},{7,6},{8,9},{9,8},{10,11... | collective-permute-start | bytes 4423688 | tf_op jit(solution)/shard_map/ppermute | solution.py:593
  441.4 48.6 %collective-permute-start.14 = (bf16[2,2,48,1536]{3,2,1,0:T(8,128)(2,1)}, bf16[2,2,48,1536]{3,2,1,0:T(8,128)(2,1)}, u32[]{:S(2)}, u32[]{:S(2)}) collective-permute-start(bf16[2,2,48,1536]{3,2,1,0:T(8,128)(2,1)} %fusion.6), channel_id=1, source_target_pairs={{0,4},{2,6},{4,0},{6,2},{8,12},{10,14},{12,8},{14,10},{16,20},{18,... | collective-permute-start | bytes 1769480 | tf_op jit(solution)/shard_map/ppermute | solution.py:590
  442.1 47.9 %collective-permute-start.16 = (bf16[48,6912]{1,0:T(8,128)(2,1)}, bf16[48,6912]{1,0:T(8,128)(2,1)}, u32[]{:S(2)}, u32[]{:S(2)}) collective-permute-start(bf16[48,6912]{1,0:T(8,128)(2,1)} %reduce-scatter.3.cloned.1.call-done), channel_id=1, source_target_pairs={{0,1},{1,0},{2,3},{3,2},{4,5},{5,4},{6,7},{7,6},{8,9},{9,8},{10,11... | collective-permute-start | bytes 1990664 | tf_op jit(solution)/shard_map/ppermute | solution.py:593
  500.6 24.3 %collective-permute-start.22 = (bf16[2,2,2,48,1152]{4,3,2,1,0:T(8,128)(2,1)}, bf16[2,2,2,48,1152]{4,3,2,1,0:T(8,128)(2,1)}, u32[]{:S(2)}, u32[]{:S(2)}) collective-permute-start(bf16[2,2,2,48,1152]{4,3,2,1,0:T(8,128)(2,1)} %fusion.7), channel_id=1, source_target_pairs={{0,1},{1,0},{2,3},{3,2},{4,5},{5,4},{6,7},{7,6},{8,9},{9,8},{10,11... | collective-permute-start | bytes 2654216 | tf_op jit(solution)/shard_map/ppermute | solution.py:593
  503.1 20.0 %collective-permute-start.21 = (bf16[2,2,48,1920]{3,2,1,0:T(8,128)(2,1)}, bf16[2,2,48,1920]{3,2,1,0:T(8,128)(2,1)S(1)}, u32[]{:S(2)}, u32[]{:S(2)}) collective-permute-start(bf16[2,2,48,1920]{3,2,1,0:T(8,128)(2,1)} %fusion.4), channel_id=1, source_target_pairs={{0,4},{2,6},{4,0},{6,2},{8,12},{10,14},{12,8},{14,10},{16,20},{18,... | collective-permute-start | bytes 2211848 | tf_op jit(solution)/shard_map/ppermute | solution.py:590
  504.4 18.6 %collective-permute-start.18 = (bf16[48,1536]{1,0:T(8,128)(2,1)}, bf16[48,1536]{1,0:T(8,128)(2,1)}, u32[]{:S(2)}, u32[]{:S(2)}) collective-permute-start(bf16[48,1536]{1,0:T(8,128)(2,1)} %get-tuple-element.300), channel_id=1, source_target_pairs={{0,8},{2,10},{4,12},{6,14},{8,0},{10,2},{12,4},{14,6},{16,24},{18,... | collective-permute-start | bytes 442376 | tf_op jit(solution)/shard_map/ppermute | solution.py:590
  506.1 16.9 %collective-permute-start.19 = (bf16[48,1536]{1,0:T(8,128)(2,1)}, bf16[48,1536]{1,0:T(8,128)(2,1)}, u32[]{:S(2)}, u32[]{:S(2)}) collective-permute-start(bf16[48,1536]{1,0:T(8,128)(2,1)} %get-tuple-element.301), channel_id=1, source_target_pairs={{0,16},{2,18},{4,20},{6,22},{8,24},{10,26},{12,28},{14,30},{16,0},... | collective-permute-start | bytes 442376 | tf_op jit(solution)/shard_map/ppermute | solution.py:590
  506.9 16.1 %collective-permute-start.20 = (bf16[48,1536]{1,0:T(8,128)(2,1)}, bf16[48,1536]{1,0:T(8,128)(2,1)}, u32[]{:S(2)}, u32[]{:S(2)}) collective-permute-start(bf16[48,1536]{1,0:T(8,128)(2,1)} %get-tuple-element.302), channel_id=1, source_target_pairs={{0,24},{2,26},{4,28},{6,30},{8,16},{10,18},{12,20},{14,22},{16,8},... | collective-permute-start | bytes 442376 | tf_op jit(solution)/shard_map/ppermute | solution.py:590
  523.0 17.7 %collective-permute-start.29 = (f32[2,2,1152]{2,1,0:T(2,128)}, f32[2,2,1152]{2,1,0:T(2,128)}, u32[]{:S(2)}, u32[]{:S(2)}) collective-permute-start(f32[2,2,1152]{2,1,0:T(2,128)} %bitcast.215), channel_id=1, source_target_pairs={{0,2},{2,0},{4,6},{6,4},{8,10},{10,8},{12,14},{14,12},{16,18},{18,... | collective-permute-start | bytes 55304 | tf_op jit(solution)/shard_map/ppermute | solution.py:590
  523.1 19.3 %collective-permute-start.30 = (f32[2,2,1152]{2,1,0:T(2,128)}, f32[2,2,1152]{2,1,0:T(2,128)S(1)}, u32[]{:S(2)}, u32[]{:S(2)}) collective-permute-start(f32[2,2,1152]{2,1,0:T(2,128)} %bitcast.214), channel_id=1, source_target_pairs={{0,4},{2,6},{4,0},{6,2},{8,12},{10,14},{12,8},{14,10},{16,20},{18,... | collective-permute-start | bytes 55304 | tf_op jit(solution)/shard_map/ppermute | solution.py:590
  523.9 20.5 %collective-permute-start.31 = (f32[2,2,1152]{2,1,0:T(2,128)}, f32[2,2,1152]{2,1,0:T(2,128)}, u32[]{:S(2)}, u32[]{:S(2)}) collective-permute-start(f32[2,2,1152]{2,1,0:T(2,128)} %bitcast.213), channel_id=1, source_target_pairs={{0,6},{2,4},{4,2},{6,0},{8,14},{10,12},{12,10},{14,8},{16,22},{18,... | collective-permute-start | bytes 55304 | tf_op jit(solution)/shard_map/ppermute | solution.py:590
  527.2 12.7 %collective-permute-start.23 = (bf16[2,2,48,1152]{3,2,1,0:T(8,128)(2,1)}, bf16[2,2,48,1152]{3,2,1,0:T(8,128)(2,1)}, u32[]{:S(2)}, u32[]{:S(2)}) collective-permute-start(bf16[2,2,48,1152]{3,2,1,0:T(8,128)(2,1)} %fusion.8), channel_id=1, source_target_pairs={{0,4},{2,6},{4,0},{6,2},{8,12},{10,14},{12,8},{14,10},{16,20},{18,... | collective-permute-start | bytes 1327112 | tf_op jit(solution)/shard_map/ppermute | solution.py:590
  532.4 27.6 %collective-permute-start.25 = (bf16[48,2304]{1,0:T(8,128)(2,1)}, bf16[48,2304]{1,0:T(8,128)(2,1)}, u32[]{:S(2)}, u32[]{:S(2)}) collective-permute-start(bf16[48,2304]{1,0:T(8,128)(2,1)} %reduce-scatter.5.cloned.1.call-done), channel_id=1, source_target_pairs={{0,1},{1,0},{2,3},{3,2},{4,5},{5,4},{6,7},{7,6},{8,9},{9,8},{10,11... | collective-permute-start | bytes 663560 | tf_op jit(solution)/shard_map/ppermute | solution.py:593
  532.8 54.7 %all-to-all-start.4 = ((bf16[2,512,768]{2,1,0:T(8,128)(2,1)}), bf16[2,512,768]{2,1,0:T(8,128)(2,1)S(1)}, u32[]{:S(2)}, u32[]{:S(2)}) async-start(bf16[2,512,768]{2,1,0:T(8,128)(2,1)} %bitcast.260), calls=%async_computation.6 | async-start | bytes 3145728 | tf_op jit(solution)/shard_map/all_to_all | solution.py:763
  539.9 20.1 %collective-permute-start.26 = (bf16[48,1920]{1,0:T(8,128)(2,1)}, bf16[48,1920]{1,0:T(8,128)(2,1)S(1)}, u32[]{:S(2)}, u32[]{:S(2)}) collective-permute-start(bf16[48,1920]{1,0:T(8,128)(2,1)} %get-tuple-element.322), channel_id=1, source_target_pairs={{0,8},{2,10},{4,12},{6,14},{8,0},{10,2},{12,4},{14,6},{16,24},{18,... | collective-permute-start | bytes 552968 | tf_op jit(solution)/shard_map/ppermute | solution.py:590
  540.7 19.3 %collective-permute-start.27 = (bf16[48,1920]{1,0:T(8,128)(2,1)}, bf16[48,1920]{1,0:T(8,128)(2,1)S(1)}, u32[]{:S(2)}, u32[]{:S(2)}) collective-permute-start(bf16[48,1920]{1,0:T(8,128)(2,1)} %get-tuple-element.323), channel_id=1, source_target_pairs={{0,16},{2,18},{4,20},{6,22},{8,24},{10,26},{12,28},{14,30},{16,0},... | collective-permute-start | bytes 552968 | tf_op jit(solution)/shard_map/ppermute | solution.py:590
  542.4 17.6 %collective-permute-start.28 = (bf16[48,1920]{1,0:T(8,128)(2,1)}, bf16[48,1920]{1,0:T(8,128)(2,1)S(1)}, u32[]{:S(2)}, u32[]{:S(2)}) collective-permute-start(bf16[48,1920]{1,0:T(8,128)(2,1)} %get-tuple-element.324), channel_id=1, source_target_pairs={{0,24},{2,26},{4,28},{6,30},{8,16},{10,18},{12,20},{14,22},{16,8},... | collective-permute-start | bytes 552968 | tf_op jit(solution)/shard_map/ppermute | solution.py:590
  544.3 15.7 %collective-permute-start.24 = (bf16[48,1536]{1,0:T(8,128)(2,1)}, bf16[48,1536]{1,0:T(8,128)(2,1)S(1)}, u32[]{:S(2)}, u32[]{:S(2)}) collective-permute-start(bf16[48,1536]{1,0:T(8,128)(2,1)} %fusion.21), channel_id=1, source_target_pairs={{0,1},{1,0},{2,3},{3,2},{4,5},{5,4},{6,7},{7,6},{8,9},{9,8},{10,11... | collective-permute-start | bytes 442376 | tf_op jit(solution)/shard_map/ppermute | solution.py:593
  563.1 7.2 %collective-permute-start.32 = (bf16[48,1152]{1,0:T(8,128)(2,1)S(1)}, bf16[48,1152]{1,0:T(8,128)(2,1)S(1)}, u32[]{:S(2)}, u32[]{:S(2)}) collective-permute-start(bf16[48,1152]{1,0:T(8,128)(2,1)S(1)} %get-tuple-element.336), channel_id=1, source_target_pairs={{0,8},{2,10},{4,12},{6,14},{8,0},{10,2},{12,4},{14,6},{16,24},{18,... | collective-permute-start | bytes 331784 | tf_op jit(solution)/shard_map/ppermute | solution.py:590
  564.2 10.9 %collective-permute-start.33 = (bf16[48,1152]{1,0:T(8,128)(2,1)S(1)}, bf16[48,1152]{1,0:T(8,128)(2,1)S(1)}, u32[]{:S(2)}, u32[]{:S(2)}) collective-permute-start(bf16[48,1152]{1,0:T(8,128)(2,1)S(1)} %get-tuple-element.337), channel_id=1, source_target_pairs={{0,16},{2,18},{4,20},{6,22},{8,24},{10,26},{12,28},{14,30},{16,0},... | collective-permute-start | bytes 331784 | tf_op jit(solution)/shard_map/ppermute | solution.py:590
  565.4 11.2 %collective-permute-start.34 = (bf16[48,1152]{1,0:T(8,128)(2,1)S(1)}, bf16[48,1152]{1,0:T(8,128)(2,1)S(1)}, u32[]{:S(2)}, u32[]{:S(2)}) collective-permute-start(bf16[48,1152]{1,0:T(8,128)(2,1)S(1)} %get-tuple-element.338), channel_id=1, source_target_pairs={{0,24},{2,26},{4,28},{6,30},{8,16},{10,18},{12,20},{14,22},{16,8},... | collective-permute-start | bytes 331784 | tf_op jit(solution)/shard_map/ppermute | solution.py:590
  567.6 12.9 %collective-permute-start.35 = (bf16[48,1920]{1,0:T(8,128)(2,1)S(1)}, bf16[48,1920]{1,0:T(8,128)(2,1)S(1)}, u32[]{:S(2)}, u32[]{:S(2)}) collective-permute-start(bf16[48,1920]{1,0:T(8,128)(2,1)S(1)} %fusion.13), channel_id=1, source_target_pairs={{0,1},{1,0},{2,3},{3,2},{4,5},{5,4},{6,7},{7,6},{8,9},{9,8},{10,11... | collective-permute-start | bytes 552968 | tf_op jit(solution)/shard_map/ppermute | solution.py:593
  567.9 10.3 %collective-permute-start.36 = (f32[1152]{0:T(1024)S(1)}, f32[1152]{0:T(1024)S(1)}, u32[]{:S(2)}, u32[]{:S(2)}) collective-permute-start(f32[1152]{0:T(1024)S(1)} %add_add_fusion.3), channel_id=1, source_target_pairs={{0,8},{2,10},{4,12},{6,14},{8,0},{10,2},{12,4},{14,6},{16,24},{18,... | collective-permute-start | bytes 13832 | tf_op jit(solution)/shard_map/ppermute | solution.py:590
  570.3 7.8 %collective-permute-start.37 = (f32[1152]{0:T(1024)S(1)}, f32[1152]{0:T(1024)S(1)}, u32[]{:S(2)}, u32[]{:S(2)}) collective-permute-start(f32[1152]{0:T(1024)S(1)} %add_add_fusion.2), channel_id=1, source_target_pairs={{0,16},{2,18},{4,20},{6,22},{8,24},{10,26},{12,28},{14,30},{16,0},... | collective-permute-start | bytes 13832 | tf_op jit(solution)/shard_map/ppermute | solution.py:590
  575.0 5.4 collective-permute-start.38
  (30 other events, 237.8 us)
Sparse Core Ops, SparseCore 0:
  12.7 72.6 all-gather.4
  88.3 86.4 all-gather.6
  177.6 51.9 all-gather.8
  306.3 118.7 reduce-scatter.2
  438.0 65.9 reduce-scatter.4

commit v17 on v14

--- a/solution.py
+++ b/solution.py
@@ -12,7 +12,7 @@
 FORWARD_ROWS = 1024
 BACKWARD_ROWS = 256
 ROW_TILE = 256
-FF_CHUNK = 1024
+FF_CHUNK = 768
 
 epsilon = 1e-05
 masked_bias = -1e30

time: 605 us -> 593 us (0.980)
  Pallas kernels: 332 us -> 320 us
    pallas_call x8, Pallas kernels: 141 us -> 128 us  [row_tiled(): pl.pallas_call(kernel, grid=(length // ROW_TILE,), in_specs=in_specs, out...]
  transfers between devices with their start and end apart: 50 -> 50, of which waited for: 14 -> 14; matrix products, arithmetic and copies ran while one was open for 11% -> 12% of each run, Pallas kernels for 47% -> 48%
where the time goes in v17:
time: 593 us; the launch traced here: 582 us
  Pallas kernels  320 us (54%)
  waiting for transfers between devices  104 us (18%)
  starting transfers between devices  55.9 us (9%)
  other arithmetic  46.9 us (8%)
  local copies, waits for them, and re-layouts  34.6 us (6%)
  between operations  15 us (3%)
  blocking collectives  6.45 us (1%)
    pallas_call x8, Pallas kernels, row_tiled(): pl.pallas_call(kernel, grid=(length // ROW_TILE,), in_specs=in_specs, out...  128 us
    pallas_call x2, Pallas kernels, attend_backward(): pl.pallas_call(functools.partial(attend_grad_kernel, rows=BACKWARD_ROWS),...  74.9 us
    ppermute x30, waiting for transfers between devices, across(): return lambda part: lax.ppermute(part, 'wide', pairs)  72 us
    pallas_call x5, Pallas kernels, term_blocks(): pl.pallas_call(kernel, in_specs=[pl.BlockSpec(memory_space=pltpu.SMEM)] +...  63.1 us
    pallas_call x2, Pallas kernels, attend_forward(): pl.pallas_call(functools.partial(attend_kernel, rows=FORWARD_ROWS), grid=...  47.7 us
    ppermute x30, starting transfers between devices, across(): return lambda part: lax.ppermute(part, 'wide', pairs)  31 us
    ppermute x11, waiting for transfers between devices, beside_seq(): return lax.ppermute(part, 'seq', swap)  20.6 us
    convert_element_type x6, other arithmetic, reduce_group(): total_of([side_of(part, 1 - mine, axis) for part in addends]).astype(half)  15.8 us
  transfers between devices with their start and end apart: 50, of which 14 were waited for; matrix products, arithmetic and copies ran while one was open for 12% of the time, Pallas kernels for 48%

profile of v17, /device:TPU:0, one launch (start us, length us, event | category | flops | bytes accessed | tf_op | source)
XLA Modules:
  0.0 582.3 jit_solution(11542488474081676980)
XLA Ops:
  14.6 4.1 collective-permute-start
  18.7 15.7 %collective-permute-done.refs_1_ = bf16[1,48,1536]{2,1,0:T(8,128)(2,1)S(1)} collective-permute-done((bf16[1,48,1536]{2,1,0:T(8,128)(2,1)S(1)}, bf16[1,48,1536]{2,1,0:T(8,128)(2,1)S(1)}, u32[]{:S(2)}, u32[]{:S(2)}) %collective-permute-start) | collective-permute-done | bytes 147488 | tf_op jit(solution)/shard_map/ppermute | solution.py:590
  34.5 7.5 %collective-permute-done.1.refs_1_ = bf16[1,96,768]{2,1,0:T(8,128)(2,1)S(1)} collective-permute-done((bf16[1,96,768]{2,1,0:T(8,128)(2,1)S(1)}, bf16[1,96,768]{2,1,0:T(8,128)(2,1)S(1)}, u32[]{:S(2)}, u32[]{:S(2)}) %collective-permute-start.1) | collective-permute-done | bytes 147488 | tf_op jit(solution)/shard_map/ppermute | solution.py:590
  42.7 6.4 %all_to_all.37 = s32[2,512,2]{1,2,0:T(2,128)S(1)} all-to-all(s32[2,512,2]{1,2,0:T(2,128)S(1)} %pad_add_fusion), channel_id=1, replica_groups=mesh['wide'=16,'seq'=2] {'seq'}, dimensions={0} | all-to-all | bytes 16384 | tf_op jit(solution)/shard_map/all_to_all | solution.py:581
  49.2 4.6 all-to-all-start
  55.9 20.2 %collective-permute-done.2.refs_1_ = bf16[2,48,1536]{2,1,0:T(8,128)(2,1)S(1)} collective-permute-done((bf16[2,48,1536]{2,1,0:T(8,128)(2,1)S(1)}, bf16[2,48,1536]{2,1,0:T(8,128)(2,1)S(1)}, u32[]{:S(2)}, u32[]{:S(2)}) %collective-permute-start.2) | collective-permute-done | bytes 294944 | tf_op jit(solution)/shard_map/ppermute | solution.py:590
  76.1 5.9 %collective-permute-done.3.refs_1_ = bf16[2,96,768]{2,1,0:T(8,128)(2,1)S(1)} collective-permute-done((bf16[2,96,768]{2,1,0:T(8,128)(2,1)S(1)}, bf16[2,96,768]{2,1,0:T(8,128)(2,1)S(1)}, u32[]{:S(2)}, u32[]{:S(2)}) %collective-permute-start.3) | collective-permute-done | bytes 294944 | tf_op jit(solution)/shard_map/ppermute | solution.py:590
  85.2 3.3 convert_add_fusion.hidden_ref
  92.6 9.3 %project.2 = (bf16[1024,768]{1,0:T(8,128)(2,1)}, bf16[1024,2304]{1,0:T(8,128)(2,1)}) custom-call(f32[1024,768]{1,0:T(8,128)} %convert_add_fusion.hidden_ref, f32[2,768]{1,0:T(2,128)} %squeeze.266.gains_ref, f32[6,768]{1,0:T(8,128)} %squeeze.267.offsets_ref, bf16[768,3200]{1,0:T(8,128)(2,1)} %all-gather.5.cloned.1.call-done.weight_ref.out_weight_ref), custom_call_target="tpu_custom_call" | custom-call | flops 226492416 | bytes 898560 | tf_op jit(solution)/shard_map/project/pallas_call | solution.py:231
  103.1 2.8 fusion.2.bias_ref
  105.9 23.9 %attend_forward.2 = (bf16[1024,768]{1,0:T(8,128)(2,1)}, f32[6,2,1024]{2,1,0:T(2,128)}) custom-call(bf16[1024,2304]{1,0:T(8,128)(2,1)} %get-tuple-element.213.query_ref.key_ref.value_ref, bf16[1024,2304]{1,0:T(8,128)(2,1)} %get-tuple-element.213.query_ref.key_ref.value_ref, bf16[1024,2304]{1,0:T(8,128)(2,1)} %get-tuple-element.213.query_ref.key_ref.value_ref, ...), custom_call_target="tpu_custom_call" | custom-call | flops 805306368 | bytes 393216 | tf_op jit(solution)/shard_map/attend_forward/pallas_call | solution.py:68
  129.8 6.1 %collective-permute-done.7.refs_1_ = bf16[4,192,768]{2,1,0:T(8,128)(2,1)S(1)} collective-permute-done((bf16[4,192,768]{2,1,0:T(8,128)(2,1)S(1)}, bf16[4,192,768]{2,1,0:T(8,128)(2,1)S(1)}, u32[]{:S(2)}, u32[]{:S(2)}) %collective-permute-start.7) | collective-permute-done | bytes 1179680 | tf_op jit(solution)/shard_map/ppermute | solution.py:590
  150.7 2.7 place_pieces.16
  153.4 2.2 copy-done.3
  155.6 23.0 %feed.2 = (f32[1024,768]{1,0:T(8,128)}, bf16[1024,768]{1,0:T(8,128)(2,1)}, bf16[1024,3072]{1,0:T(8,128)(2,1)}, bf16[1024,3072]{1,0:T(8,128)(2,1)}, f32[1024,768]{1,0:T(8,128)}) custom-call(bf16[1024,768]{1,0:T(8,128)(2,1)} %get-tuple-element.225.attended_ref.refs_2_, f32[1024,768]{1,0:T(8,128)} %convert_add_fusion.hidden_ref, f32[2,768]{1,0:T(2,128)} %squeeze.266.gains_ref, ...), custom_call_target="tpu_custom_call" | custom-call | flops 679477248 | bytes 2472192 | tf_op jit(solution)/shard_map/feed/pallas_call | solution.py:231
  178.7 9.2 %project.3 = (bf16[1024,768]{1,0:T(8,128)(2,1)}, bf16[1024,2304]{1,0:T(8,128)(2,1)}) custom-call(f32[1024,768]{1,0:T(8,128)} %get-tuple-element.229.hidden_ref, f32[2,768]{1,0:T(2,128)} %squeeze.268.gains_ref, f32[6,768]{1,0:T(8,128)} %squeeze.269.offsets_ref, bf16[768,6144]{1,0:T(8,128)(2,1)} %all-gather.7.cloned.1.call-done.weight_ref.out_weight_ref.up_ref), custom_call_target="tpu_custom_call" | custom-call | flops 226492416 | bytes 1181184 | tf_op jit(solution)/shard_map/project/pallas_call | solution.py:231
  187.9 3.8 all-to-all-start.2
  192.4 23.8 %attend_forward.3 = (bf16[1024,768]{1,0:T(8,128)(2,1)}, f32[6,2,1024]{2,1,0:T(2,128)}) custom-call(bf16[1024,2304]{1,0:T(8,128)(2,1)} %get-tuple-element.231.query_ref.key_ref.value_ref, bf16[1024,2304]{1,0:T(8,128)(2,1)} %get-tuple-element.231.query_ref.key_ref.value_ref, bf16[1024,2304]{1,0:T(8,128)(2,1)} %get-tuple-element.231.query_ref.key_ref.value_ref, ...), custom_call_target="tpu_custom_call" | custom-call | flops 805306368 | bytes 393216 | tf_op jit(solution)/shard_map/attend_forward/pallas_call | solution.py:68
  216.3 10.9 %all-gather.9.cloned.1.call-done = bf16[1,3072,768]{2,1,0:T(8,128)(2,1)} async-done(((bf16[1,192,768]{2,1,0:T(8,128)(2,1)}), bf16[1,3072,768]{2,1,0:T(8,128)(2,1)}) %all-gather.9.cloned.1.call-update) | async-done | bytes 4718608 | tf_op jit(solution)/shard_map/all_gather | solution.py:697
  227.1 22.8 %feed.3 = (f32[1024,768]{1,0:T(8,128)}, bf16[1024,768]{1,0:T(8,128)(2,1)}, bf16[1024,3072]{1,0:T(8,128)(2,1)}, bf16[1024,3072]{1,0:T(8,128)(2,1)}, bf16[1024,768]{1,0:T(8,128)(2,1)}) custom-call(bf16[1024,768]{1,0:T(8,128)(2,1)} %get-tuple-element.233.attended_ref.refs_4_, f32[1024,768]{1,0:T(8,128)} %get-tuple-element.229.hidden_ref, ...), custom_call_target="tpu_custom_call" | custom-call | flops 679477248 | bytes 2951424 | tf_op jit(solution)/shard_map/feed/pallas_call | solution.py:231
  251.1 21.2 %feed_grad.2 = (bf16[1024,768]{1,0:T(8,128)(2,1)}, bf16[1024,3072]{1,0:T(8,128)(2,1)}, f32[1024,768]{1,0:T(8,128)}, bf16[1024,768]{1,0:T(8,128)(2,1)}, bf16[1024...) custom-call(bf16[1024,768]{1,0:T(8,128)(2,1)} %bitcast.239, ...), custom_call_target="tpu_custom_call" | custom-call | flops 679477248 | bytes 3050112 | tf_op jit(solution)/shard_map/feed_grad/pallas_call | solution.py:231
  272.4 19.7 %term_blocks.5 = bf16[16,48,6912]{2,1,0:T(8,128)(2,1)} custom-call(s32[1]{0:T(128)} %bitcast.20.core_ref, bf16[1024,3072]{1,0:T(8,128)(2,1)} %get-tuple-element.237.refs_0_, bf16[1024,768]{1,0:T(8,128)(2,1)} %get-tuple-element.238.refs_1_, bf16[1024,768]{1,0:T(8,128)(2,1)} %get-tuple-element.239.refs_2_, bf16[1024,3072]{1,0:T(8,128)(2,1)} %get-tuple-element.240.refs_3_, ...), custom_call_target="tpu_custom_call" | custom-call | flops 679477248 | bytes 1843200 | tf_op jit(solution)/shard_map/term_blocks/pallas_call | solution.py:548
  292.1 3.7 all-to-all-start.3
  295.9 37.5 %attend_backward.2.packed_grad_ref.refs_1_ = bf16[1024,2304]{1,0:T(8,128)(2,1)} custom-call(bf16[1024,2304]{1,0:T(8,128)(2,1)} %get-tuple-element.231.query_ref.key_ref.value_ref, bf16[1024,2304]{1,0:T(8,128)(2,1)} %get-tuple-element.231.query_ref.key_ref.value_ref, bf16[1024,2304]{1,0:T(8,128)(2,1)} %get-tuple-element.231.query_ref.key_ref.value_ref, ...), custom_call_target="tpu_custom_call" | custom-call | flops 2013265920 | bytes 786432 | tf_op jit(solution)/shard_map/attend_backward/pallas_call | solution.py:151
  333.4 10.9 %project_grad.2 = (f32[1024,768]{1,0:T(8,128)}, bf16[1024,768]{1,0:T(8,128)(2,1)}, f32[8,768]{1,0:T(8,128)}) custom-call(bf16[1024,2304]{1,0:T(8,128)(2,1)} %attend_backward.2.packed_grad_ref.refs_1_, f32[1024,768]{1,0:T(8,128)} %get-tuple-element.229.hidden_ref, f32[1024,768]{1,0:T(8,128)} %get-tuple-element.247.middle_grad_ref, ...), custom_call_target="tpu_custom_call" | custom-call | flops 226492416 | bytes 1574784 | tf_op jit(solution)/shard_map/project_grad/pallas_call | solution.py:231
  344.2 12.2 %term_blocks.6 = (bf16[8,2,48,1536]{3,2,1,0:T(8,128)(2,1)}, bf16[8,2,48,1536]{3,2,1,0:T(8,128)(2,1)}) custom-call(s32[1]{0:T(128)} %bitcast.20.core_ref, bf16[1024,3072]{1,0:T(8,128)(2,1)} %get-tuple-element.249.refs_0_, bf16[1024,768]{1,0:T(8,128)(2,1)} %get-tuple-element.250.refs_1_), custom_call_target="tpu_custom_call" | custom-call | flops 301989888 | bytes 786432 | tf_op jit(solution)/shard_map/term_blocks/pallas_call | solution.py:548
  356.8 8.6 %term_blocks.7 = bf16[16,48,2304]{2,1,0:T(8,128)(2,1)} custom-call(s32[1]{0:T(128)} %bitcast.20.core_ref, bf16[1024,768]{1,0:T(8,128)(2,1)} %get-tuple-element.253.refs_0_, bf16[1024,2304]{1,0:T(8,128)(2,1)} %attend_backward.2.packed_grad_ref.refs_1_), custom_call_target="tpu_custom_call" | custom-call | flops 226492416 | bytes 614400 | tf_op jit(solution)/shard_map/term_blocks/pallas_call | solution.py:548
  365.4 3.0 fusion.5
  370.1 21.5 %feed_grad.3 = (bf16[1024,768]{1,0:T(8,128)(2,1)}, bf16[1024,3072]{1,0:T(8,128)(2,1)}, f32[1024,768]{1,0:T(8,128)}, bf16[1024,768]{1,0:T(8,128)(2,1)}, bf16[1024...) custom-call(f32[1024,768]{1,0:T(8,128)} %get-tuple-element.259.gradient_ref, ...), custom_call_target="tpu_custom_call" | custom-call | flops 679477248 | bytes 2570880 | tf_op jit(solution)/shard_map/feed_grad/pallas_call | solution.py:231
  391.5 5.4 collective-permute-done.12
  396.9 2.8 fusion.6
  399.7 12.8 %term_blocks.8 = (bf16[8,2,48,1920]{3,2,1,0:T(8,128)(2,1)}, bf16[8,2,48,1920]{3,2,1,0:T(8,128)(2,1)}) custom-call(s32[1]{0:T(128)} %bitcast.20.core_ref, bf16[1024,768]{1,0:T(8,128)(2,1)} %get-tuple-element.270.refs_0_, bf16[1024,3072]{1,0:T(8,128)(2,1)} %get-tuple-element.271.refs_1_, bf16[1024,768]{1,0:T(8,128)(2,1)} %get-tuple-element.225.attended_ref.refs_2_, ...), custom_call_target="tpu_custom_call" | custom-call | flops 377487360 | bytes 1056768 | tf_op jit(solution)/shard_map/term_blocks/pallas_call | solution.py:548
  412.6 5.6 collective-permute-done.13
  418.1 3.9 fusion.3
  428.7 37.4 %attend_backward.3.refs_1_.packed_grad_ref = bf16[1024,2304]{1,0:T(8,128)(2,1)} custom-call(bf16[1024,2304]{1,0:T(8,128)(2,1)} %get-tuple-element.213.query_ref.key_ref.value_ref, bf16[1024,2304]{1,0:T(8,128)(2,1)} %get-tuple-element.213.query_ref.key_ref.value_ref, bf16[1024,2304]{1,0:T(8,128)(2,1)} %get-tuple-element.213.query_ref.key_ref.value_ref, ...), custom_call_target="tpu_custom_call" | custom-call | flops 2013265920 | bytes 786432 | tf_op jit(solution)/shard_map/attend_backward/pallas_call | solution.py:151
  466.1 9.8 %term_blocks.9 = (bf16[8,2,48,1152]{3,2,1,0:T(8,128)(2,1)}, bf16[8,2,48,1152]{3,2,1,0:T(8,128)(2,1)}) custom-call(s32[1]{0:T(128)} %bitcast.20.core_ref, bf16[1024,768]{1,0:T(8,128)(2,1)} %get-tuple-element.290.refs_0_, bf16[1024,2304]{1,0:T(8,128)(2,1)} %attend_backward.3.refs_1_.packed_grad_ref), custom_call_target="tpu_custom_call" | custom-call | flops 226492416 | bytes 614400 | tf_op jit(solution)/shard_map/term_blocks/pallas_call | solution.py:548
  475.9 2.9 fusion.22
  478.8 2.6 fusion.4
  482.9 2.3 collective-permute-done.17
  494.7 10.2 %project_grad.3 = (bf16[1024,768]{1,0:T(8,128)(2,1)}, f32[8,768]{1,0:T(8,128)}) custom-call(bf16[1024,2304]{1,0:T(8,128)(2,1)} %attend_backward.3.refs_1_.packed_grad_ref, f32[1024,768]{1,0:T(8,128)} %convert_add_fusion.hidden_ref, f32[1024,768]{1,0:T(8,128)} %get-tuple-element.298.middle_grad_ref, f32[2,768]{1,0:T(2,128)} %squeeze.266.gains_ref, ...), custom_call_target="tpu_custom_call" | custom-call | flops 226492416 | bytes 1095552 | tf_op jit(solution)/shard_map/project_grad/pallas_call | solution.py:231
  511.0 2.2 fusion.8
  515.9 2.5 fusion.14
  518.8 3.7 all-to-all-start.4
  522.5 3.4 collective-permute-done.23
  532.2 13.8 %collective-permute-done.24 = bf16[48,1536]{1,0:T(8,128)(2,1)S(1)} collective-permute-done((bf16[48,1536]{1,0:T(8,128)(2,1)}, bf16[48,1536]{1,0:T(8,128)(2,1)S(1)}, u32[]{:S(2)}, u32[]{:S(2)}) %collective-permute-start.24) | collective-permute-done | bytes 147488 | tf_op jit(solution)/shard_map/ppermute | solution.py:593
  556.4 2.3 collective-permute-start.37
  558.6 2.6 collective-permute-done.33
  563.9 2.8 collective-permute-done.38
  (263 shorter events, 92.1 us)
Async XLA Ops:
  7.2 81.3 %all-gather.5.cloned.1.call-start = ((), (), s32[]{:S(2)}) async-start(), calls=%async_computation.7 | async-start | bytes 5222400 | tf_op jit(solution)/shard_map/all_gather | solution.py:695
  12.6 166.1 %all-gather.7.cloned.1.call-start = ((), (), s32[]{:S(2)}) async-start(), calls=%async_computation.8 | async-start | bytes 10027008 | tf_op jit(solution)/shard_map/all_gather | solution.py:695
  13.6 213.5 %all-gather.9.cloned.1.call-start = ((), (), s32[]{:S(2)}) async-start(), calls=%async_computation.11 | async-start | bytes 5013504 | tf_op jit(solution)/shard_map/all_gather | solution.py:697
  14.6 19.9 %collective-permute-start = (bf16[1,48,1536]{2,1,0:T(8,128)(2,1)S(1)}, bf16[1,48,1536]{2,1,0:T(8,128)(2,1)S(1)}, u32[]{:S(2)}, u32[]{:S(2)}) collective-permute-start(bf16[1,48,1536]{2,1,0:T(8,128)(2,1)S(1)} %constant_dynamic-slice_fusion.21.refs_0_), channel_id=1, source_target_pairs={{0,16},{2,18},{4,20},{6,22},{8,24},{10,26},{12,28},{14,30},{16,0},... | collective-permute-start | bytes 442376 | tf_op jit(solution)/shard_map/ppermute | solution.py:590
  18.7 23.3 %collective-permute-start.1 = (bf16[1,96,768]{2,1,0:T(8,128)(2,1)S(1)}, bf16[1,96,768]{2,1,0:T(8,128)(2,1)S(1)}, u32[]{:S(2)}, u32[]{:S(2)}) collective-permute-start(bf16[1,96,768]{2,1,0:T(8,128)(2,1)S(1)} %constant_dynamic-slice_fusion.20.refs_0_), channel_id=1, source_target_pairs={{0,16},{2,18},{4,20},{6,22},{8,24},{10,26},{12,28},{14,30},{16,0},... | collective-permute-start | bytes 442376 | tf_op jit(solution)/shard_map/ppermute | solution.py:590
  49.2 36.1 %all-to-all-start = ((bf16[2,512,768]{2,1,0:T(8,128)(2,1)}), bf16[2,512,768]{2,1,0:T(8,128)(2,1)}, u32[]{:S(2)}, u32[]{:S(2)}) async-start(bf16[2,512,768]{2,1,0:T(8,128)(2,1)} %param.12), calls=%async_computation | async-start | bytes 3145728 | tf_op jit(solution)/shard_map/all_to_all | solution.py:581
  53.8 22.3 %collective-permute-start.2 = (bf16[2,48,1536]{2,1,0:T(8,128)(2,1)S(1)}, bf16[2,48,1536]{2,1,0:T(8,128)(2,1)S(1)}, u32[]{:S(2)}, u32[]{:S(2)}) collective-permute-start(bf16[2,48,1536]{2,1,0:T(8,128)(2,1)S(1)} %bitcast.231), channel_id=1, source_target_pairs={{0,8},{2,10},{4,12},{6,14},{8,0},{10,2},{12,4},{14,6},{16,24},{18,... | collective-permute-start | bytes 884744 | tf_op jit(solution)/shard_map/ppermute | solution.py:590
  54.5 27.5 %collective-permute-start.3 = (bf16[2,96,768]{2,1,0:T(8,128)(2,1)S(1)}, bf16[2,96,768]{2,1,0:T(8,128)(2,1)S(1)}, u32[]{:S(2)}, u32[]{:S(2)}) collective-permute-start(bf16[2,96,768]{2,1,0:T(8,128)(2,1)S(1)} %bitcast.233), channel_id=1, source_target_pairs={{0,8},{2,10},{4,12},{6,14},{8,0},{10,2},{12,4},{14,6},{16,24},{18,... | collective-permute-start | bytes 884744 | tf_op jit(solution)/shard_map/ppermute | solution.py:590
  82.2 19.7 %collective-permute-start.4 = (bf16[4,48,1536]{2,1,0:T(8,128)(2,1)S(1)}, bf16[4,48,1536]{2,1,0:T(8,128)(2,1)S(1)}, u32[]{:S(2)}, u32[]{:S(2)}) collective-permute-start(bf16[4,48,1536]{2,1,0:T(8,128)(2,1)S(1)} %bitcast.229), channel_id=1, source_target_pairs={{0,4},{2,6},{4,0},{6,2},{8,12},{10,14},{12,8},{14,10},{16,20},{18,... | collective-permute-start | bytes 1769480 | tf_op jit(solution)/shard_map/ppermute | solution.py:590
  83.7 18.2 %collective-permute-start.5 = (bf16[4,96,768]{2,1,0:T(8,128)(2,1)S(1)}, bf16[4,96,768]{2,1,0:T(8,128)(2,1)S(1)}, u32[]{:S(2)}, u32[]{:S(2)}) collective-permute-start(bf16[4,96,768]{2,1,0:T(8,128)(2,1)S(1)} %bitcast.227), channel_id=1, source_target_pairs={{0,1},{1,0},{2,3},{3,2},{4,5},{5,4},{6,7},{7,6},{8,9},{9,8},{10,11... | collective-permute-start | bytes 1769480 | tf_op jit(solution)/shard_map/ppermute | solution.py:593
  102.2 27.5 %collective-permute-start.6 = (bf16[8,48,1536]{2,1,0:T(8,128)(2,1)S(1)}, bf16[8,48,1536]{2,1,0:T(8,128)(2,1)}, u32[]{:S(2)}, u32[]{:S(2)}) collective-permute-start(bf16[8,48,1536]{2,1,0:T(8,128)(2,1)S(1)} %bitcast.222), channel_id=1, source_target_pairs={{0,1},{1,0},{2,3},{3,2},{4,5},{5,4},{6,7},{7,6},{8,9},{9,8},{10,11... | collective-permute-start | bytes 3538952 | tf_op jit(solution)/shard_map/ppermute | solution.py:593
  102.5 33.4 %collective-permute-start.7 = (bf16[4,192,768]{2,1,0:T(8,128)(2,1)S(1)}, bf16[4,192,768]{2,1,0:T(8,128)(2,1)S(1)}, u32[]{:S(2)}, u32[]{:S(2)}) collective-permute-start(bf16[4,192,768]{2,1,0:T(8,128)(2,1)S(1)} %bitcast.225), channel_id=1, source_target_pairs={{0,4},{2,6},{4,0},{6,2},{8,12},{10,14},{12,8},{14,10},{16,20},{18,... | collective-permute-start | bytes 3538952 | tf_op jit(solution)/shard_map/ppermute | solution.py:590
  136.1 10.6 %collective-permute-start.10 = (bf16[8,192,768]{2,1,0:T(8,128)(2,1)S(1)}, bf16[8,192,768]{2,1,0:T(8,128)(2,1)}, u32[]{:S(2)}, u32[]{:S(2)}) collective-permute-start(bf16[8,192,768]{2,1,0:T(8,128)(2,1)S(1)} %bitcast.220), channel_id=1, source_target_pairs={{0,2},{2,0},{4,6},{6,4},{8,10},{10,8},{12,14},{14,12},{16,18},{18,... | collective-permute-start | bytes 7077896 | tf_op jit(solution)/shard_map/ppermute | solution.py:590
  136.2 10.5 %collective-permute-start.8 = (bf16[8,48,1536]{2,1,0:T(8,128)(2,1)S(1)}, bf16[8,48,1536]{2,1,0:T(8,128)(2,1)}, u32[]{:S(2)}, u32[]{:S(2)}) collective-permute-start(bf16[8,48,1536]{2,1,0:T(8,128)(2,1)S(1)} %bitcast.223), channel_id=1, source_target_pairs={{0,2},{2,0},{4,6},{6,4},{8,10},{10,8},{12,14},{14,12},{16,18},{18,... | collective-permute-start | bytes 3538952 | tf_op jit(solution)/shard_map/ppermute | solution.py:590
  136.7 10.0 %collective-permute-start.9 = (bf16[8,48,1536]{2,1,0:T(8,128)(2,1)}, bf16[8,48,1536]{2,1,0:T(8,128)(2,1)}, u32[]{:S(2)}, u32[]{:S(2)}) collective-permute-start(bf16[8,48,1536]{2,1,0:T(8,128)(2,1)} %collective-permute-done.6.refs_1_), channel_id=1, source_target_pairs={{0,2},{2,0},{4,6},{6,4},{8,10},{10,8},{12,14},{14,12},{16,18},{18,... | collective-permute-start | bytes 3538952 | tf_op jit(solution)/shard_map/ppermute | solution.py:590
  187.9 62.1 %all-to-all-start.2 = ((bf16[2,512,768]{2,1,0:T(8,128)(2,1)}), bf16[2,512,768]{2,1,0:T(8,128)(2,1)S(1)}, u32[]{:S(2)}, u32[]{:S(2)}) async-start(bf16[2,512,768]{2,1,0:T(8,128)(2,1)} %param.16), calls=%async_computation.2 | async-start | bytes 3145728 | tf_op jit(solution)/shard_map/all_to_all | solution.py:581
  191.7 236.3 %reduce-scatter.3.cloned.1.call-start = ((), (), s32[]{:S(2)}) async-start(), calls=%async_computation.9 | async-start | bytes 11280384 | tf_op jit(solution)/shard_map/reduce_scatter | solution.py:596
  292.1 41.2 %all-to-all-start.3 = ((bf16[2,512,768]{2,1,0:T(8,128)(2,1)}), bf16[2,512,768]{2,1,0:T(8,128)(2,1)S(1)}, u32[]{:S(2)}, u32[]{:S(2)}) async-start(bf16[2,512,768]{2,1,0:T(8,128)(2,1)} %bitcast.30), calls=%async_computation.3 | async-start | bytes 3145728 | tf_op jit(solution)/shard_map/all_to_all | solution.py:764
  295.8 213.2 %reduce-scatter.5.cloned.1.call-start = ((), (), s32[]{:S(2)}) async-start(), calls=%async_computation.10 | async-start | bytes 3760128 | tf_op jit(solution)/shard_map/reduce_scatter | solution.py:596
  356.4 9.0 %collective-permute-start.11 = (bf16[8,2,48,1536]{3,2,1,0:T(8,128)(2,1)}, bf16[8,2,48,1536]{3,2,1,0:T(8,128)(2,1)}, u32[]{:S(2)}, u32[]{:S(2)}) collective-permute-start(bf16[8,2,48,1536]{3,2,1,0:T(8,128)(2,1)} %get-tuple-element.255), channel_id=1, source_target_pairs={{0,2},{2,0},{4,6},{6,4},{8,10},{10,8},{12,14},{14,12},{16,18},{18,... | collective-permute-start | bytes 7077896 | tf_op jit(solution)/shard_map/ppermute | solution.py:590
  368.4 28.5 %collective-permute-start.12 = (bf16[2,2,2,48,1536]{4,3,2,1,0:T(8,128)(2,1)}, bf16[2,2,2,48,1536]{4,3,2,1,0:T(8,128)(2,1)S(1)}, u32[]{:S(2)}, u32[]{:S(2)}) collective-permute-start(bf16[2,2,2,48,1536]{4,3,2,1,0:T(8,128)(2,1)} %fusion.5), channel_id=1, source_target_pairs={{0,1},{1,0},{2,3},{3,2},{4,5},{5,4},{6,7},{7,6},{8,9},{9,8},{10,11... | collective-permute-start | bytes 3538952 | tf_op jit(solution)/shard_map/ppermute | solution.py:593
  412.5 5.7 collective-permute-start.13
  422.1 53.8 %collective-permute-start.15 = (bf16[2,2,2,48,1920]{4,3,2,1,0:T(8,128)(2,1)}, bf16[2,2,2,48,1920]{4,3,2,1,0:T(8,128)(2,1)S(1)}, u32[]{:S(2)}, u32[]{:S(2)}) collective-permute-start(bf16[2,2,2,48,1920]{4,3,2,1,0:T(8,128)(2,1)} %fusion.3), channel_id=1, source_target_pairs={{0,1},{1,0},{2,3},{3,2},{4,5},{5,4},{6,7},{7,6},{8,9},{9,8},{10,11... | collective-permute-start | bytes 4423688 | tf_op jit(solution)/shard_map/ppermute | solution.py:593
  427.4 48.5 %collective-permute-start.14 = (bf16[2,2,48,1536]{3,2,1,0:T(8,128)(2,1)}, bf16[2,2,48,1536]{3,2,1,0:T(8,128)(2,1)}, u32[]{:S(2)}, u32[]{:S(2)}) collective-permute-start(bf16[2,2,48,1536]{3,2,1,0:T(8,128)(2,1)} %fusion.6), channel_id=1, source_target_pairs={{0,4},{2,6},{4,0},{6,2},{8,12},{10,14},{12,8},{14,10},{16,20},{18,... | collective-permute-start | bytes 1769480 | tf_op jit(solution)/shard_map/ppermute | solution.py:590
  428.0 47.9 %collective-permute-start.16 = (bf16[48,6912]{1,0:T(8,128)(2,1)}, bf16[48,6912]{1,0:T(8,128)(2,1)}, u32[]{:S(2)}, u32[]{:S(2)}) collective-permute-start(bf16[48,6912]{1,0:T(8,128)(2,1)} %reduce-scatter.3.cloned.1.call-done), channel_id=1, source_target_pairs={{0,1},{1,0},{2,3},{3,2},{4,5},{5,4},{6,7},{7,6},{8,9},{9,8},{10,11... | collective-permute-start | bytes 1990664 | tf_op jit(solution)/shard_map/ppermute | solution.py:593
  486.5 24.5 %collective-permute-start.22 = (bf16[2,2,2,48,1152]{4,3,2,1,0:T(8,128)(2,1)}, bf16[2,2,2,48,1152]{4,3,2,1,0:T(8,128)(2,1)}, u32[]{:S(2)}, u32[]{:S(2)}) collective-permute-start(bf16[2,2,2,48,1152]{4,3,2,1,0:T(8,128)(2,1)} %fusion.7), channel_id=1, source_target_pairs={{0,1},{1,0},{2,3},{3,2},{4,5},{5,4},{6,7},{7,6},{8,9},{9,8},{10,11... | collective-permute-start | bytes 2654216 | tf_op jit(solution)/shard_map/ppermute | solution.py:593
  488.9 20.2 %collective-permute-start.21 = (bf16[2,2,48,1920]{3,2,1,0:T(8,128)(2,1)}, bf16[2,2,48,1920]{3,2,1,0:T(8,128)(2,1)S(1)}, u32[]{:S(2)}, u32[]{:S(2)}) collective-permute-start(bf16[2,2,48,1920]{3,2,1,0:T(8,128)(2,1)} %fusion.4), channel_id=1, source_target_pairs={{0,4},{2,6},{4,0},{6,2},{8,12},{10,14},{12,8},{14,10},{16,20},{18,... | collective-permute-start | bytes 2211848 | tf_op jit(solution)/shard_map/ppermute | solution.py:590
  490.3 18.8 %collective-permute-start.18 = (bf16[48,1536]{1,0:T(8,128)(2,1)}, bf16[48,1536]{1,0:T(8,128)(2,1)}, u32[]{:S(2)}, u32[]{:S(2)}) collective-permute-start(bf16[48,1536]{1,0:T(8,128)(2,1)} %get-tuple-element.306), channel_id=1, source_target_pairs={{0,8},{2,10},{4,12},{6,14},{8,0},{10,2},{12,4},{14,6},{16,24},{18,... | collective-permute-start | bytes 442376 | tf_op jit(solution)/shard_map/ppermute | solution.py:590
  492.0 17.0 %collective-permute-start.19 = (bf16[48,1536]{1,0:T(8,128)(2,1)}, bf16[48,1536]{1,0:T(8,128)(2,1)}, u32[]{:S(2)}, u32[]{:S(2)}) collective-permute-start(bf16[48,1536]{1,0:T(8,128)(2,1)} %get-tuple-element.307), channel_id=1, source_target_pairs={{0,16},{2,18},{4,20},{6,22},{8,24},{10,26},{12,28},{14,30},{16,0},... | collective-permute-start | bytes 442376 | tf_op jit(solution)/shard_map/ppermute | solution.py:590
  492.7 16.3 %collective-permute-start.20 = (bf16[48,1536]{1,0:T(8,128)(2,1)}, bf16[48,1536]{1,0:T(8,128)(2,1)}, u32[]{:S(2)}, u32[]{:S(2)}) collective-permute-start(bf16[48,1536]{1,0:T(8,128)(2,1)} %get-tuple-element.308), channel_id=1, source_target_pairs={{0,24},{2,26},{4,28},{6,30},{8,16},{10,18},{12,20},{14,22},{16,8},... | collective-permute-start | bytes 442376 | tf_op jit(solution)/shard_map/ppermute | solution.py:590
  509.0 17.7 %collective-permute-start.29 = (f32[2,2,1152]{2,1,0:T(2,128)}, f32[2,2,1152]{2,1,0:T(2,128)}, u32[]{:S(2)}, u32[]{:S(2)}) collective-permute-start(f32[2,2,1152]{2,1,0:T(2,128)} %bitcast.215), channel_id=1, source_target_pairs={{0,2},{2,0},{4,6},{6,4},{8,10},{10,8},{12,14},{14,12},{16,18},{18,... | collective-permute-start | bytes 55304 | tf_op jit(solution)/shard_map/ppermute | solution.py:590
  509.1 19.3 %collective-permute-start.30 = (f32[2,2,1152]{2,1,0:T(2,128)}, f32[2,2,1152]{2,1,0:T(2,128)S(1)}, u32[]{:S(2)}, u32[]{:S(2)}) collective-permute-start(f32[2,2,1152]{2,1,0:T(2,128)} %bitcast.214), channel_id=1, source_target_pairs={{0,4},{2,6},{4,0},{6,2},{8,12},{10,14},{12,8},{14,10},{16,20},{18,... | collective-permute-start | bytes 55304 | tf_op jit(solution)/shard_map/ppermute | solution.py:590
  509.8 20.5 %collective-permute-start.31 = (f32[2,2,1152]{2,1,0:T(2,128)}, f32[2,2,1152]{2,1,0:T(2,128)}, u32[]{:S(2)}, u32[]{:S(2)}) collective-permute-start(f32[2,2,1152]{2,1,0:T(2,128)} %bitcast.213), channel_id=1, source_target_pairs={{0,6},{2,4},{4,2},{6,0},{8,14},{10,12},{12,10},{14,8},{16,22},{18,... | collective-permute-start | bytes 55304 | tf_op jit(solution)/shard_map/ppermute | solution.py:590
  513.2 12.7 %collective-permute-start.23 = (bf16[2,2,48,1152]{3,2,1,0:T(8,128)(2,1)}, bf16[2,2,48,1152]{3,2,1,0:T(8,128)(2,1)}, u32[]{:S(2)}, u32[]{:S(2)}) collective-permute-start(bf16[2,2,48,1152]{3,2,1,0:T(8,128)(2,1)} %fusion.8), channel_id=1, source_target_pairs={{0,4},{2,6},{4,0},{6,2},{8,12},{10,14},{12,8},{14,10},{16,20},{18,... | collective-permute-start | bytes 1327112 | tf_op jit(solution)/shard_map/ppermute | solution.py:590
  518.4 27.6 %collective-permute-start.25 = (bf16[48,2304]{1,0:T(8,128)(2,1)}, bf16[48,2304]{1,0:T(8,128)(2,1)}, u32[]{:S(2)}, u32[]{:S(2)}) collective-permute-start(bf16[48,2304]{1,0:T(8,128)(2,1)} %reduce-scatter.5.cloned.1.call-done), channel_id=1, source_target_pairs={{0,1},{1,0},{2,3},{3,2},{4,5},{5,4},{6,7},{7,6},{8,9},{9,8},{10,11... | collective-permute-start | bytes 663560 | tf_op jit(solution)/shard_map/ppermute | solution.py:593
  518.8 54.9 %all-to-all-start.4 = ((bf16[2,512,768]{2,1,0:T(8,128)(2,1)}), bf16[2,512,768]{2,1,0:T(8,128)(2,1)S(1)}, u32[]{:S(2)}, u32[]{:S(2)}) async-start(bf16[2,512,768]{2,1,0:T(8,128)(2,1)} %bitcast.260), calls=%async_computation.6 | async-start | bytes 3145728 | tf_op jit(solution)/shard_map/all_to_all | solution.py:764
  525.9 20.1 %collective-permute-start.26 = (bf16[48,1920]{1,0:T(8,128)(2,1)}, bf16[48,1920]{1,0:T(8,128)(2,1)S(1)}, u32[]{:S(2)}, u32[]{:S(2)}) collective-permute-start(bf16[48,1920]{1,0:T(8,128)(2,1)} %get-tuple-element.328), channel_id=1, source_target_pairs={{0,8},{2,10},{4,12},{6,14},{8,0},{10,2},{12,4},{14,6},{16,24},{18,... | collective-permute-start | bytes 552968 | tf_op jit(solution)/shard_map/ppermute | solution.py:590
  526.8 19.2 %collective-permute-start.27 = (bf16[48,1920]{1,0:T(8,128)(2,1)}, bf16[48,1920]{1,0:T(8,128)(2,1)S(1)}, u32[]{:S(2)}, u32[]{:S(2)}) collective-permute-start(bf16[48,1920]{1,0:T(8,128)(2,1)} %get-tuple-element.329), channel_id=1, source_target_pairs={{0,16},{2,18},{4,20},{6,22},{8,24},{10,26},{12,28},{14,30},{16,0},... | collective-permute-start | bytes 552968 | tf_op jit(solution)/shard_map/ppermute | solution.py:590
  528.4 17.6 %collective-permute-start.28 = (bf16[48,1920]{1,0:T(8,128)(2,1)}, bf16[48,1920]{1,0:T(8,128)(2,1)S(1)}, u32[]{:S(2)}, u32[]{:S(2)}) collective-permute-start(bf16[48,1920]{1,0:T(8,128)(2,1)} %get-tuple-element.330), channel_id=1, source_target_pairs={{0,24},{2,26},{4,28},{6,30},{8,16},{10,18},{12,20},{14,22},{16,8},... | collective-permute-start | bytes 552968 | tf_op jit(solution)/shard_map/ppermute | solution.py:590
  530.3 15.7 %collective-permute-start.24 = (bf16[48,1536]{1,0:T(8,128)(2,1)}, bf16[48,1536]{1,0:T(8,128)(2,1)S(1)}, u32[]{:S(2)}, u32[]{:S(2)}) collective-permute-start(bf16[48,1536]{1,0:T(8,128)(2,1)} %fusion.21), channel_id=1, source_target_pairs={{0,1},{1,0},{2,3},{3,2},{4,5},{5,4},{6,7},{7,6},{8,9},{9,8},{10,11... | collective-permute-start | bytes 442376 | tf_op jit(solution)/shard_map/ppermute | solution.py:593
  549.1 7.3 %collective-permute-start.32 = (bf16[48,1152]{1,0:T(8,128)(2,1)S(1)}, bf16[48,1152]{1,0:T(8,128)(2,1)S(1)}, u32[]{:S(2)}, u32[]{:S(2)}) collective-permute-start(bf16[48,1152]{1,0:T(8,128)(2,1)S(1)} %get-tuple-element.342), channel_id=1, source_target_pairs={{0,8},{2,10},{4,12},{6,14},{8,0},{10,2},{12,4},{14,6},{16,24},{18,... | collective-permute-start | bytes 331784 | tf_op jit(solution)/shard_map/ppermute | solution.py:590
  550.2 11.0 %collective-permute-start.33 = (bf16[48,1152]{1,0:T(8,128)(2,1)S(1)}, bf16[48,1152]{1,0:T(8,128)(2,1)S(1)}, u32[]{:S(2)}, u32[]{:S(2)}) collective-permute-start(bf16[48,1152]{1,0:T(8,128)(2,1)S(1)} %get-tuple-element.343), channel_id=1, source_target_pairs={{0,16},{2,18},{4,20},{6,22},{8,24},{10,26},{12,28},{14,30},{16,0},... | collective-permute-start | bytes 331784 | tf_op jit(solution)/shard_map/ppermute | solution.py:590
  551.6 10.8 %collective-permute-start.34 = (bf16[48,1152]{1,0:T(8,128)(2,1)S(1)}, bf16[48,1152]{1,0:T(8,128)(2,1)S(1)}, u32[]{:S(2)}, u32[]{:S(2)}) collective-permute-start(bf16[48,1152]{1,0:T(8,128)(2,1)S(1)} %get-tuple-element.344), channel_id=1, source_target_pairs={{0,24},{2,26},{4,28},{6,30},{8,16},{10,18},{12,20},{14,22},{16,8},... | collective-permute-start | bytes 331784 | tf_op jit(solution)/shard_map/ppermute | solution.py:590
  553.5 13.1 %collective-permute-start.35 = (bf16[48,1920]{1,0:T(8,128)(2,1)S(1)}, bf16[48,1920]{1,0:T(8,128)(2,1)S(1)}, u32[]{:S(2)}, u32[]{:S(2)}) collective-permute-start(bf16[48,1920]{1,0:T(8,128)(2,1)S(1)} %fusion.13), channel_id=1, source_target_pairs={{0,1},{1,0},{2,3},{3,2},{4,5},{5,4},{6,7},{7,6},{8,9},{9,8},{10,11... | collective-permute-start | bytes 552968 | tf_op jit(solution)/shard_map/ppermute | solution.py:593
  553.9 10.0 %collective-permute-start.36 = (f32[1152]{0:T(1024)S(1)}, f32[1152]{0:T(1024)S(1)}, u32[]{:S(2)}, u32[]{:S(2)}) collective-permute-start(f32[1152]{0:T(1024)S(1)} %add_add_fusion.3), channel_id=1, source_target_pairs={{0,8},{2,10},{4,12},{6,14},{8,0},{10,2},{12,4},{14,6},{16,24},{18,... | collective-permute-start | bytes 13832 | tf_op jit(solution)/shard_map/ppermute | solution.py:590
  556.4 7.5 %collective-permute-start.37 = (f32[1152]{0:T(1024)S(1)}, f32[1152]{0:T(1024)S(1)}, u32[]{:S(2)}, u32[]{:S(2)}) collective-permute-start(f32[1152]{0:T(1024)S(1)} %add_add_fusion.2), channel_id=1, source_target_pairs={{0,16},{2,18},{4,20},{6,22},{8,24},{10,26},{12,28},{14,30},{16,0},... | collective-permute-start | bytes 13832 | tf_op jit(solution)/shard_map/ppermute | solution.py:590
  561.2 5.4 collective-permute-start.38
  563.6 5.5 collective-permute-start.39
  (29 other events, 229.2 us)
Sparse Core Ops, SparseCore 0:
  12.7 67.1 all-gather.4
  82.7 90.0 all-gather.6
  175.7 51.4 all-gather.8
  292.2 118.7 reduce-scatter.2
  423.9 65.7 reduce-scatter.4

commit v18 on v17

--- a/solution.py
+++ b/solution.py
@@ -517,27 +517,33 @@
             copies[2 * index + 1].wait()
             left, right = buffers[2 * index], buffers[2 * index + 1]
             rows = groups * row_unit
-            step = max(size for size in (768, 640, 512, 384, 256, 128) if width % size == 0)
+            columns = right.shape[1]
+            step = max(size for size in (768, 640, 512, 384, 256, 128) if columns % size == 0)
             held = chips // count
             for turn in range(count):
                 turned = left[:, turn * rows : (turn + 1) * rows].T
                 some = slice(turn * held, (turn + 1) * held)
-                for low in range(0, right.shape[1], step):
+                for low in range(0, columns, step):
                     product = contract(turned, right[:, low : low + step], 1, 0).astype(half)
                     product = product.reshape(held, 2, count, row_unit, step)
-                    side, inside = divmod(low, width)
-                    for piece in range(count):
-                        lanes = start + piece * width + inside
-                        lanes = slice(lanes, lanes + step)
-                        even, odd = product[:, 0, piece], product[:, 1, piece]
-                        if by_core:
-                            outs[0][some, side, :, lanes] = jnp.where(first_core, odd, even)
-                            outs[1][some, side, :, lanes] = jnp.where(first_core, even, odd)
-                        else:
-                            for chip in range(held):
-                                owner = 2 * (turn * held + chip)
-                                outs[0][owner, :, lanes] = even[chip]
-                                outs[0][owner + 1, :, lanes] = odd[chip]
+                    for side in range(columns // width):
+                        first = max(low, side * width)
+                        last = min(low + step, (side + 1) * width)
+                        if first >= last:
+                            continue
+                        for piece in range(count):
+                            lanes = start + piece * width + first - side * width
+                            lanes = slice(lanes, lanes + last - first)
+                            even = product[:, 0, piece, :, first - low : last - low]
+                            odd = product[:, 1, piece, :, first - low : last - low]
+                            if by_core:
+                                outs[0][some, side, :, lanes] = jnp.where(first_core, odd, even)
+                                outs[1][some, side, :, lanes] = jnp.where(first_core, even, odd)
+                            else:
+                                for chip in range(held):
+                                    owner = 2 * (turn * held + chip)
+                                    outs[0][owner, :, lanes] = even[chip]
+                                    outs[0][owner + 1, :, lanes] = odd[chip]
             start += count * width
 
     anywhere = pl.BlockSpec(memory_space=pl.ANY)

time: 593 us -> 596 us (level)
  Pallas kernels: 320 us -> 327 us
    pallas_call x8, Pallas kernels: 128 us -> 138 us  [row_tiled(): pl.pallas_call(kernel, grid=(length // ROW_TILE,), in_specs=in_specs, out...]
  transfers between devices with their start and end apart: 50 -> 50, of which waited for: 14 -> 14; matrix products, arithmetic and copies ran while one was open for 12% -> 12% of each run, Pallas kernels for 48% -> 47%
where the time goes in v18:
time: 596 us; the launch traced here: 590 us
  Pallas kernels  327 us (55%)
  waiting for transfers between devices  103 us (17%)
  starting transfers between devices  56.4 us (9%)
  other arithmetic  47.1 us (8%)
  local copies, waits for them, and re-layouts  34.6 us (6%)
  between operations  15 us (3%)
  blocking collectives  6.45 us (1%)
    pallas_call x8, Pallas kernels, row_tiled(): pl.pallas_call(kernel, grid=(length // ROW_TILE,), in_specs=in_specs, out...  138 us
    pallas_call x2, Pallas kernels, attend_backward(): pl.pallas_call(functools.partial(attend_grad_kernel, rows=BACKWARD_ROWS),...  74.7 us
    ppermute x30, waiting for transfers between devices, across(): return lambda part: lax.ppermute(part, 'wide', pairs)  71.1 us
    pallas_call x5, Pallas kernels, term_blocks(): pl.pallas_call(kernel, in_specs=[pl.BlockSpec(memory_space=pltpu.SMEM)] +...  60.7 us
    pallas_call x2, Pallas kernels, attend_forward(): pl.pallas_call(functools.partial(attend_kernel, rows=FORWARD_ROWS), grid=...  47.7 us
    ppermute x30, starting transfers between devices, across(): return lambda part: lax.ppermute(part, 'wide', pairs)  31.5 us
    ppermute x11, waiting for transfers between devices, beside_seq(): return lax.ppermute(part, 'seq', swap)  20.8 us
    convert_element_type x6, other arithmetic, reduce_group(): total_of([side_of(part, 1 - mine, axis) for part in addends]).astype(half)  15.9 us
  transfers between devices with their start and end apart: 50, of which 14 were waited for; matrix products, arithmetic and copies ran while one was open for 12% of the time, Pallas kernels for 47%

profile of v18, /device:TPU:0, one launch (start us, length us, event | category | flops | bytes accessed | tf_op | source)
XLA Modules:
  0.0 590.1 jit_solution(5908865117079968203)
XLA Ops:
  14.6 4.1 collective-permute-start
  18.7 15.7 %collective-permute-done.refs_1_ = bf16[1,48,1536]{2,1,0:T(8,128)(2,1)S(1)} collective-permute-done((bf16[1,48,1536]{2,1,0:T(8,128)(2,1)S(1)}, bf16[1,48,1536]{2,1,0:T(8,128)(2,1)S(1)}, u32[]{:S(2)}, u32[]{:S(2)}) %collective-permute-start) | collective-permute-done | bytes 147488 | tf_op jit(solution)/shard_map/ppermute | solution.py:596
  34.5 7.5 %collective-permute-done.1.refs_1_ = bf16[1,96,768]{2,1,0:T(8,128)(2,1)S(1)} collective-permute-done((bf16[1,96,768]{2,1,0:T(8,128)(2,1)S(1)}, bf16[1,96,768]{2,1,0:T(8,128)(2,1)S(1)}, u32[]{:S(2)}, u32[]{:S(2)}) %collective-permute-start.1) | collective-permute-done | bytes 147488 | tf_op jit(solution)/shard_map/ppermute | solution.py:596
  42.7 6.4 %all_to_all.37 = s32[2,512,2]{1,2,0:T(2,128)S(1)} all-to-all(s32[2,512,2]{1,2,0:T(2,128)S(1)} %pad_add_fusion), channel_id=1, replica_groups=mesh['wide'=16,'seq'=2] {'seq'}, dimensions={0} | all-to-all | bytes 16384 | tf_op jit(solution)/shard_map/all_to_all | solution.py:587
  49.2 4.6 all-to-all-start
  55.9 20.2 %collective-permute-done.2.refs_1_ = bf16[2,48,1536]{2,1,0:T(8,128)(2,1)S(1)} collective-permute-done((bf16[2,48,1536]{2,1,0:T(8,128)(2,1)S(1)}, bf16[2,48,1536]{2,1,0:T(8,128)(2,1)S(1)}, u32[]{:S(2)}, u32[]{:S(2)}) %collective-permute-start.2) | collective-permute-done | bytes 294944 | tf_op jit(solution)/shard_map/ppermute | solution.py:596
  76.1 5.9 %collective-permute-done.3.refs_1_ = bf16[2,96,768]{2,1,0:T(8,128)(2,1)S(1)} collective-permute-done((bf16[2,96,768]{2,1,0:T(8,128)(2,1)S(1)}, bf16[2,96,768]{2,1,0:T(8,128)(2,1)S(1)}, u32[]{:S(2)}, u32[]{:S(2)}) %collective-permute-start.3) | collective-permute-done | bytes 294944 | tf_op jit(solution)/shard_map/ppermute | solution.py:596
  85.2 3.3 convert_add_fusion.hidden_ref
  92.6 9.3 %project.2 = (bf16[1024,768]{1,0:T(8,128)(2,1)}, bf16[1024,2304]{1,0:T(8,128)(2,1)}) custom-call(f32[1024,768]{1,0:T(8,128)} %convert_add_fusion.hidden_ref, f32[2,768]{1,0:T(2,128)} %squeeze.266.gains_ref, f32[6,768]{1,0:T(8,128)} %squeeze.267.offsets_ref, bf16[768,3200]{1,0:T(8,128)(2,1)} %all-gather.5.cloned.1.call-done.weight_ref.out_weight_ref), custom_call_target="tpu_custom_call" | custom-call | flops 226492416 | bytes 898560 | tf_op jit(solution)/shard_map/project/pallas_call | solution.py:231
  103.1 2.8 fusion.2.bias_ref
  105.9 23.9 %attend_forward.2 = (bf16[1024,768]{1,0:T(8,128)(2,1)}, f32[6,2,1024]{2,1,0:T(2,128)}) custom-call(bf16[1024,2304]{1,0:T(8,128)(2,1)} %get-tuple-element.213.query_ref.key_ref.value_ref, bf16[1024,2304]{1,0:T(8,128)(2,1)} %get-tuple-element.213.query_ref.key_ref.value_ref, bf16[1024,2304]{1,0:T(8,128)(2,1)} %get-tuple-element.213.query_ref.key_ref.value_ref, ...), custom_call_target="tpu_custom_call" | custom-call | flops 805306368 | bytes 393216 | tf_op jit(solution)/shard_map/attend_forward/pallas_call | solution.py:68
  129.8 6.1 %collective-permute-done.7.refs_1_ = bf16[4,192,768]{2,1,0:T(8,128)(2,1)S(1)} collective-permute-done((bf16[4,192,768]{2,1,0:T(8,128)(2,1)S(1)}, bf16[4,192,768]{2,1,0:T(8,128)(2,1)S(1)}, u32[]{:S(2)}, u32[]{:S(2)}) %collective-permute-start.7) | collective-permute-done | bytes 1179680 | tf_op jit(solution)/shard_map/ppermute | solution.py:596
  150.7 2.7 place_pieces.16
  153.4 2.2 copy-done.3
  155.6 23.0 %feed.2 = (f32[1024,768]{1,0:T(8,128)}, bf16[1024,768]{1,0:T(8,128)(2,1)}, bf16[1024,3072]{1,0:T(8,128)(2,1)}, bf16[1024,3072]{1,0:T(8,128)(2,1)}, f32[1024,768]{1,0:T(8,128)}) custom-call(bf16[1024,768]{1,0:T(8,128)(2,1)} %get-tuple-element.225.attended_ref.refs_2_, f32[1024,768]{1,0:T(8,128)} %convert_add_fusion.hidden_ref, f32[2,768]{1,0:T(2,128)} %squeeze.266.gains_ref, ...), custom_call_target="tpu_custom_call" | custom-call | flops 679477248 | bytes 2472192 | tf_op jit(solution)/shard_map/feed/pallas_call | solution.py:231
  178.7 9.3 %project.3 = (bf16[1024,768]{1,0:T(8,128)(2,1)}, bf16[1024,2304]{1,0:T(8,128)(2,1)}) custom-call(f32[1024,768]{1,0:T(8,128)} %get-tuple-element.229.hidden_ref, f32[2,768]{1,0:T(2,128)} %squeeze.268.gains_ref, f32[6,768]{1,0:T(8,128)} %squeeze.269.offsets_ref, bf16[768,6144]{1,0:T(8,128)(2,1)} %all-gather.7.cloned.1.call-done.weight_ref.out_weight_ref.up_ref), custom_call_target="tpu_custom_call" | custom-call | flops 226492416 | bytes 1181184 | tf_op jit(solution)/shard_map/project/pallas_call | solution.py:231
  187.9 3.8 all-to-all-start.2
  192.5 23.8 %attend_forward.3 = (bf16[1024,768]{1,0:T(8,128)(2,1)}, f32[6,2,1024]{2,1,0:T(2,128)}) custom-call(bf16[1024,2304]{1,0:T(8,128)(2,1)} %get-tuple-element.231.query_ref.key_ref.value_ref, bf16[1024,2304]{1,0:T(8,128)(2,1)} %get-tuple-element.231.query_ref.key_ref.value_ref, bf16[1024,2304]{1,0:T(8,128)(2,1)} %get-tuple-element.231.query_ref.key_ref.value_ref, ...), custom_call_target="tpu_custom_call" | custom-call | flops 805306368 | bytes 393216 | tf_op jit(solution)/shard_map/attend_forward/pallas_call | solution.py:68
  216.3 11.0 %all-gather.9.cloned.1.call-done = bf16[1,3072,768]{2,1,0:T(8,128)(2,1)} async-done(((bf16[1,192,768]{2,1,0:T(8,128)(2,1)}), bf16[1,3072,768]{2,1,0:T(8,128)(2,1)}) %all-gather.9.cloned.1.call-update) | async-done | bytes 4718608 | tf_op jit(solution)/shard_map/all_gather | solution.py:703
  227.3 22.8 %feed.3 = (f32[1024,768]{1,0:T(8,128)}, bf16[1024,768]{1,0:T(8,128)(2,1)}, bf16[1024,3072]{1,0:T(8,128)(2,1)}, bf16[1024,3072]{1,0:T(8,128)(2,1)}, bf16[1024,768]{1,0:T(8,128)(2,1)}) custom-call(bf16[1024,768]{1,0:T(8,128)(2,1)} %get-tuple-element.233.attended_ref.refs_4_, f32[1024,768]{1,0:T(8,128)} %get-tuple-element.229.hidden_ref, ...), custom_call_target="tpu_custom_call" | custom-call | flops 679477248 | bytes 2951424 | tf_op jit(solution)/shard_map/feed/pallas_call | solution.py:231
  251.3 31.7 %feed_grad.2 = (bf16[1024,768]{1,0:T(8,128)(2,1)}, bf16[1024,3072]{1,0:T(8,128)(2,1)}, f32[1024,768]{1,0:T(8,128)}, bf16[1024,768]{1,0:T(8,128)(2,1)}, bf16[1024...) custom-call(bf16[1024,768]{1,0:T(8,128)(2,1)} %bitcast.239, ...), custom_call_target="tpu_custom_call" | custom-call | flops 679477248 | bytes 3050112 | tf_op jit(solution)/shard_map/feed_grad/pallas_call | solution.py:231
  282.9 19.7 %term_blocks.5 = bf16[16,48,6912]{2,1,0:T(8,128)(2,1)} custom-call(s32[1]{0:T(128)} %bitcast.20.core_ref, bf16[1024,3072]{1,0:T(8,128)(2,1)} %get-tuple-element.237.refs_0_, bf16[1024,768]{1,0:T(8,128)(2,1)} %get-tuple-element.238.refs_1_, bf16[1024,768]{1,0:T(8,128)(2,1)} %get-tuple-element.239.refs_2_, bf16[1024,3072]{1,0:T(8,128)(2,1)} %get-tuple-element.240.refs_3_, ...), custom_call_target="tpu_custom_call" | custom-call | flops 679477248 | bytes 1843200 | tf_op jit(solution)/shard_map/term_blocks/pallas_call | solution.py:554
  302.7 3.7 all-to-all-start.3
  306.4 37.3 %attend_backward.2.packed_grad_ref.refs_1_ = bf16[1024,2304]{1,0:T(8,128)(2,1)} custom-call(bf16[1024,2304]{1,0:T(8,128)(2,1)} %get-tuple-element.231.query_ref.key_ref.value_ref, bf16[1024,2304]{1,0:T(8,128)(2,1)} %get-tuple-element.231.query_ref.key_ref.value_ref, bf16[1024,2304]{1,0:T(8,128)(2,1)} %get-tuple-element.231.query_ref.key_ref.value_ref, ...), custom_call_target="tpu_custom_call" | custom-call | flops 2013265920 | bytes 786432 | tf_op jit(solution)/shard_map/attend_backward/pallas_call | solution.py:151
  343.7 11.1 %project_grad.2 = (f32[1024,768]{1,0:T(8,128)}, bf16[1024,768]{1,0:T(8,128)(2,1)}, f32[8,768]{1,0:T(8,128)}) custom-call(bf16[1024,2304]{1,0:T(8,128)(2,1)} %attend_backward.2.packed_grad_ref.refs_1_, f32[1024,768]{1,0:T(8,128)} %get-tuple-element.229.hidden_ref, f32[1024,768]{1,0:T(8,128)} %get-tuple-element.247.middle_grad_ref, ...), custom_call_target="tpu_custom_call" | custom-call | flops 226492416 | bytes 1574784 | tf_op jit(solution)/shard_map/project_grad/pallas_call | solution.py:231
  354.8 10.6 %term_blocks.6 = (bf16[8,2,48,1536]{3,2,1,0:T(8,128)(2,1)}, bf16[8,2,48,1536]{3,2,1,0:T(8,128)(2,1)}) custom-call(s32[1]{0:T(128)} %bitcast.20.core_ref, bf16[1024,3072]{1,0:T(8,128)(2,1)} %get-tuple-element.249.refs_0_, bf16[1024,768]{1,0:T(8,128)(2,1)} %get-tuple-element.250.refs_1_), custom_call_target="tpu_custom_call" | custom-call | flops 301989888 | bytes 786432 | tf_op jit(solution)/shard_map/term_blocks/pallas_call | solution.py:554
  365.8 8.6 %term_blocks.7 = bf16[16,48,2304]{2,1,0:T(8,128)(2,1)} custom-call(s32[1]{0:T(128)} %bitcast.20.core_ref, bf16[1024,768]{1,0:T(8,128)(2,1)} %get-tuple-element.253.refs_0_, bf16[1024,2304]{1,0:T(8,128)(2,1)} %attend_backward.2.packed_grad_ref.refs_1_), custom_call_target="tpu_custom_call" | custom-call | flops 226492416 | bytes 614400 | tf_op jit(solution)/shard_map/term_blocks/pallas_call | solution.py:554
  374.4 3.1 fusion.5
  379.2 21.2 %feed_grad.3 = (bf16[1024,768]{1,0:T(8,128)(2,1)}, bf16[1024,3072]{1,0:T(8,128)(2,1)}, f32[1024,768]{1,0:T(8,128)}, bf16[1024,768]{1,0:T(8,128)(2,1)}, bf16[1024...) custom-call(f32[1024,768]{1,0:T(8,128)} %get-tuple-element.259.gradient_ref, ...), custom_call_target="tpu_custom_call" | custom-call | flops 679477248 | bytes 2570880 | tf_op jit(solution)/shard_map/feed_grad/pallas_call | solution.py:231
  400.5 5.5 collective-permute-done.12
  405.9 2.8 fusion.6
  408.7 13.2 %term_blocks.8 = (bf16[8,2,48,1920]{3,2,1,0:T(8,128)(2,1)}, bf16[8,2,48,1920]{3,2,1,0:T(8,128)(2,1)}) custom-call(s32[1]{0:T(128)} %bitcast.20.core_ref, bf16[1024,768]{1,0:T(8,128)(2,1)} %get-tuple-element.270.refs_0_, bf16[1024,3072]{1,0:T(8,128)(2,1)} %get-tuple-element.271.refs_1_, bf16[1024,768]{1,0:T(8,128)(2,1)} %get-tuple-element.225.attended_ref.refs_2_, ...), custom_call_target="tpu_custom_call" | custom-call | flops 377487360 | bytes 1056768 | tf_op jit(solution)/shard_map/term_blocks/pallas_call | solution.py:554
  422.0 5.6 collective-permute-done.13
  427.6 3.9 fusion.3
  438.2 37.4 %attend_backward.3.refs_1_.packed_grad_ref = bf16[1024,2304]{1,0:T(8,128)(2,1)} custom-call(bf16[1024,2304]{1,0:T(8,128)(2,1)} %get-tuple-element.213.query_ref.key_ref.value_ref, bf16[1024,2304]{1,0:T(8,128)(2,1)} %get-tuple-element.213.query_ref.key_ref.value_ref, bf16[1024,2304]{1,0:T(8,128)(2,1)} %get-tuple-element.213.query_ref.key_ref.value_ref, ...), custom_call_target="tpu_custom_call" | custom-call | flops 2013265920 | bytes 786432 | tf_op jit(solution)/shard_map/attend_backward/pallas_call | solution.py:151
  475.7 8.6 %term_blocks.9 = (bf16[8,2,48,1152]{3,2,1,0:T(8,128)(2,1)}, bf16[8,2,48,1152]{3,2,1,0:T(8,128)(2,1)}) custom-call(s32[1]{0:T(128)} %bitcast.20.core_ref, bf16[1024,768]{1,0:T(8,128)(2,1)} %get-tuple-element.290.refs_0_, bf16[1024,2304]{1,0:T(8,128)(2,1)} %attend_backward.3.refs_1_.packed_grad_ref), custom_call_target="tpu_custom_call" | custom-call | flops 226492416 | bytes 614400 | tf_op jit(solution)/shard_map/term_blocks/pallas_call | solution.py:554
  484.3 2.9 fusion.22
  487.2 2.6 fusion.4
  491.3 2.3 collective-permute-done.17
  503.1 10.0 %project_grad.3 = (bf16[1024,768]{1,0:T(8,128)(2,1)}, f32[8,768]{1,0:T(8,128)}) custom-call(bf16[1024,2304]{1,0:T(8,128)(2,1)} %attend_backward.3.refs_1_.packed_grad_ref, f32[1024,768]{1,0:T(8,128)} %convert_add_fusion.hidden_ref, f32[1024,768]{1,0:T(8,128)} %get-tuple-element.298.middle_grad_ref, f32[2,768]{1,0:T(2,128)} %squeeze.266.gains_ref, ...), custom_call_target="tpu_custom_call" | custom-call | flops 226492416 | bytes 1095552 | tf_op jit(solution)/shard_map/project_grad/pallas_call | solution.py:231
  519.2 2.2 fusion.8
  524.1 2.5 fusion.14
  527.0 3.7 all-to-all-start.4
  530.7 3.4 collective-permute-done.23
  540.4 13.8 %collective-permute-done.24 = bf16[48,1536]{1,0:T(8,128)(2,1)S(1)} collective-permute-done((bf16[48,1536]{1,0:T(8,128)(2,1)}, bf16[48,1536]{1,0:T(8,128)(2,1)S(1)}, u32[]{:S(2)}, u32[]{:S(2)}) %collective-permute-start.24) | collective-permute-done | bytes 147488 | tf_op jit(solution)/shard_map/ppermute | solution.py:599
  559.6 2.2 collective-permute-start.34
  564.5 2.2 collective-permute-start.37
  566.7 2.3 collective-permute-done.33
  (263 shorter events, 92.7 us)
Async XLA Ops:
  7.2 81.3 %all-gather.5.cloned.1.call-start = ((), (), s32[]{:S(2)}) async-start(), calls=%async_computation.7 | async-start | bytes 5222400 | tf_op jit(solution)/shard_map/all_gather | solution.py:701
  12.6 166.1 %all-gather.7.cloned.1.call-start = ((), (), s32[]{:S(2)}) async-start(), calls=%async_computation.8 | async-start | bytes 10027008 | tf_op jit(solution)/shard_map/all_gather | solution.py:701
  13.6 213.7 %all-gather.9.cloned.1.call-start = ((), (), s32[]{:S(2)}) async-start(), calls=%async_computation.11 | async-start | bytes 5013504 | tf_op jit(solution)/shard_map/all_gather | solution.py:703
  14.6 19.9 %collective-permute-start = (bf16[1,48,1536]{2,1,0:T(8,128)(2,1)S(1)}, bf16[1,48,1536]{2,1,0:T(8,128)(2,1)S(1)}, u32[]{:S(2)}, u32[]{:S(2)}) collective-permute-start(bf16[1,48,1536]{2,1,0:T(8,128)(2,1)S(1)} %constant_dynamic-slice_fusion.21.refs_0_), channel_id=1, source_target_pairs={{0,16},{2,18},{4,20},{6,22},{8,24},{10,26},{12,28},{14,30},{16,0},... | collective-permute-start | bytes 442376 | tf_op jit(solution)/shard_map/ppermute | solution.py:596
  18.7 23.3 %collective-permute-start.1 = (bf16[1,96,768]{2,1,0:T(8,128)(2,1)S(1)}, bf16[1,96,768]{2,1,0:T(8,128)(2,1)S(1)}, u32[]{:S(2)}, u32[]{:S(2)}) collective-permute-start(bf16[1,96,768]{2,1,0:T(8,128)(2,1)S(1)} %constant_dynamic-slice_fusion.20.refs_0_), channel_id=1, source_target_pairs={{0,16},{2,18},{4,20},{6,22},{8,24},{10,26},{12,28},{14,30},{16,0},... | collective-permute-start | bytes 442376 | tf_op jit(solution)/shard_map/ppermute | solution.py:596
  49.2 36.1 %all-to-all-start = ((bf16[2,512,768]{2,1,0:T(8,128)(2,1)}), bf16[2,512,768]{2,1,0:T(8,128)(2,1)}, u32[]{:S(2)}, u32[]{:S(2)}) async-start(bf16[2,512,768]{2,1,0:T(8,128)(2,1)} %param.12), calls=%async_computation | async-start | bytes 3145728 | tf_op jit(solution)/shard_map/all_to_all | solution.py:587
  53.8 22.3 %collective-permute-start.2 = (bf16[2,48,1536]{2,1,0:T(8,128)(2,1)S(1)}, bf16[2,48,1536]{2,1,0:T(8,128)(2,1)S(1)}, u32[]{:S(2)}, u32[]{:S(2)}) collective-permute-start(bf16[2,48,1536]{2,1,0:T(8,128)(2,1)S(1)} %bitcast.231), channel_id=1, source_target_pairs={{0,8},{2,10},{4,12},{6,14},{8,0},{10,2},{12,4},{14,6},{16,24},{18,... | collective-permute-start | bytes 884744 | tf_op jit(solution)/shard_map/ppermute | solution.py:596
  54.5 27.5 %collective-permute-start.3 = (bf16[2,96,768]{2,1,0:T(8,128)(2,1)S(1)}, bf16[2,96,768]{2,1,0:T(8,128)(2,1)S(1)}, u32[]{:S(2)}, u32[]{:S(2)}) collective-permute-start(bf16[2,96,768]{2,1,0:T(8,128)(2,1)S(1)} %bitcast.233), channel_id=1, source_target_pairs={{0,8},{2,10},{4,12},{6,14},{8,0},{10,2},{12,4},{14,6},{16,24},{18,... | collective-permute-start | bytes 884744 | tf_op jit(solution)/shard_map/ppermute | solution.py:596
  82.2 19.7 %collective-permute-start.4 = (bf16[4,48,1536]{2,1,0:T(8,128)(2,1)S(1)}, bf16[4,48,1536]{2,1,0:T(8,128)(2,1)S(1)}, u32[]{:S(2)}, u32[]{:S(2)}) collective-permute-start(bf16[4,48,1536]{2,1,0:T(8,128)(2,1)S(1)} %bitcast.229), channel_id=1, source_target_pairs={{0,4},{2,6},{4,0},{6,2},{8,12},{10,14},{12,8},{14,10},{16,20},{18,... | collective-permute-start | bytes 1769480 | tf_op jit(solution)/shard_map/ppermute | solution.py:596
  83.7 18.2 %collective-permute-start.5 = (bf16[4,96,768]{2,1,0:T(8,128)(2,1)S(1)}, bf16[4,96,768]{2,1,0:T(8,128)(2,1)S(1)}, u32[]{:S(2)}, u32[]{:S(2)}) collective-permute-start(bf16[4,96,768]{2,1,0:T(8,128)(2,1)S(1)} %bitcast.227), channel_id=1, source_target_pairs={{0,1},{1,0},{2,3},{3,2},{4,5},{5,4},{6,7},{7,6},{8,9},{9,8},{10,11... | collective-permute-start | bytes 1769480 | tf_op jit(solution)/shard_map/ppermute | solution.py:599
  102.2 27.5 %collective-permute-start.6 = (bf16[8,48,1536]{2,1,0:T(8,128)(2,1)S(1)}, bf16[8,48,1536]{2,1,0:T(8,128)(2,1)}, u32[]{:S(2)}, u32[]{:S(2)}) collective-permute-start(bf16[8,48,1536]{2,1,0:T(8,128)(2,1)S(1)} %bitcast.222), channel_id=1, source_target_pairs={{0,1},{1,0},{2,3},{3,2},{4,5},{5,4},{6,7},{7,6},{8,9},{9,8},{10,11... | collective-permute-start | bytes 3538952 | tf_op jit(solution)/shard_map/ppermute | solution.py:599
  102.5 33.4 %collective-permute-start.7 = (bf16[4,192,768]{2,1,0:T(8,128)(2,1)S(1)}, bf16[4,192,768]{2,1,0:T(8,128)(2,1)S(1)}, u32[]{:S(2)}, u32[]{:S(2)}) collective-permute-start(bf16[4,192,768]{2,1,0:T(8,128)(2,1)S(1)} %bitcast.225), channel_id=1, source_target_pairs={{0,4},{2,6},{4,0},{6,2},{8,12},{10,14},{12,8},{14,10},{16,20},{18,... | collective-permute-start | bytes 3538952 | tf_op jit(solution)/shard_map/ppermute | solution.py:596
  136.1 10.6 %collective-permute-start.10 = (bf16[8,192,768]{2,1,0:T(8,128)(2,1)S(1)}, bf16[8,192,768]{2,1,0:T(8,128)(2,1)}, u32[]{:S(2)}, u32[]{:S(2)}) collective-permute-start(bf16[8,192,768]{2,1,0:T(8,128)(2,1)S(1)} %bitcast.220), channel_id=1, source_target_pairs={{0,2},{2,0},{4,6},{6,4},{8,10},{10,8},{12,14},{14,12},{16,18},{18,... | collective-permute-start | bytes 7077896 | tf_op jit(solution)/shard_map/ppermute | solution.py:596
  136.2 10.5 %collective-permute-start.8 = (bf16[8,48,1536]{2,1,0:T(8,128)(2,1)S(1)}, bf16[8,48,1536]{2,1,0:T(8,128)(2,1)}, u32[]{:S(2)}, u32[]{:S(2)}) collective-permute-start(bf16[8,48,1536]{2,1,0:T(8,128)(2,1)S(1)} %bitcast.223), channel_id=1, source_target_pairs={{0,2},{2,0},{4,6},{6,4},{8,10},{10,8},{12,14},{14,12},{16,18},{18,... | collective-permute-start | bytes 3538952 | tf_op jit(solution)/shard_map/ppermute | solution.py:596
  136.7 10.0 %collective-permute-start.9 = (bf16[8,48,1536]{2,1,0:T(8,128)(2,1)}, bf16[8,48,1536]{2,1,0:T(8,128)(2,1)}, u32[]{:S(2)}, u32[]{:S(2)}) collective-permute-start(bf16[8,48,1536]{2,1,0:T(8,128)(2,1)} %collective-permute-done.6.refs_1_), channel_id=1, source_target_pairs={{0,2},{2,0},{4,6},{6,4},{8,10},{10,8},{12,14},{14,12},{16,18},{18,... | collective-permute-start | bytes 3538952 | tf_op jit(solution)/shard_map/ppermute | solution.py:596
  187.9 62.2 %all-to-all-start.2 = ((bf16[2,512,768]{2,1,0:T(8,128)(2,1)}), bf16[2,512,768]{2,1,0:T(8,128)(2,1)S(1)}, u32[]{:S(2)}, u32[]{:S(2)}) async-start(bf16[2,512,768]{2,1,0:T(8,128)(2,1)} %param.16), calls=%async_computation.2 | async-start | bytes 3145728 | tf_op jit(solution)/shard_map/all_to_all | solution.py:587
  191.7 245.9 %reduce-scatter.3.cloned.1.call-start = ((), (), s32[]{:S(2)}) async-start(), calls=%async_computation.9 | async-start | bytes 11280384 | tf_op jit(solution)/shard_map/reduce_scatter | solution.py:602
  302.7 41.0 %all-to-all-start.3 = ((bf16[2,512,768]{2,1,0:T(8,128)(2,1)}), bf16[2,512,768]{2,1,0:T(8,128)(2,1)S(1)}, u32[]{:S(2)}, u32[]{:S(2)}) async-start(bf16[2,512,768]{2,1,0:T(8,128)(2,1)} %bitcast.30), calls=%async_computation.3 | async-start | bytes 3145728 | tf_op jit(solution)/shard_map/all_to_all | solution.py:770
  306.4 210.8 %reduce-scatter.5.cloned.1.call-start = ((), (), s32[]{:S(2)}) async-start(), calls=%async_computation.10 | async-start | bytes 3760128 | tf_op jit(solution)/shard_map/reduce_scatter | solution.py:602
  365.4 9.0 %collective-permute-start.11 = (bf16[8,2,48,1536]{3,2,1,0:T(8,128)(2,1)}, bf16[8,2,48,1536]{3,2,1,0:T(8,128)(2,1)}, u32[]{:S(2)}, u32[]{:S(2)}) collective-permute-start(bf16[8,2,48,1536]{3,2,1,0:T(8,128)(2,1)} %get-tuple-element.255), channel_id=1, source_target_pairs={{0,2},{2,0},{4,6},{6,4},{8,10},{10,8},{12,14},{14,12},{16,18},{18,... | collective-permute-start | bytes 7077896 | tf_op jit(solution)/shard_map/ppermute | solution.py:596
  377.5 28.4 %collective-permute-start.12 = (bf16[2,2,2,48,1536]{4,3,2,1,0:T(8,128)(2,1)}, bf16[2,2,2,48,1536]{4,3,2,1,0:T(8,128)(2,1)S(1)}, u32[]{:S(2)}, u32[]{:S(2)}) collective-permute-start(bf16[2,2,2,48,1536]{4,3,2,1,0:T(8,128)(2,1)} %fusion.5), channel_id=1, source_target_pairs={{0,1},{1,0},{2,3},{3,2},{4,5},{5,4},{6,7},{7,6},{8,9},{9,8},{10,11... | collective-permute-start | bytes 3538952 | tf_op jit(solution)/shard_map/ppermute | solution.py:599
  422.0 5.7 collective-permute-start.13
  431.6 52.7 %collective-permute-start.15 = (bf16[2,2,2,48,1920]{4,3,2,1,0:T(8,128)(2,1)}, bf16[2,2,2,48,1920]{4,3,2,1,0:T(8,128)(2,1)S(1)}, u32[]{:S(2)}, u32[]{:S(2)}) collective-permute-start(bf16[2,2,2,48,1920]{4,3,2,1,0:T(8,128)(2,1)} %fusion.3), channel_id=1, source_target_pairs={{0,1},{1,0},{2,3},{3,2},{4,5},{5,4},{6,7},{7,6},{8,9},{9,8},{10,11... | collective-permute-start | bytes 4423688 | tf_op jit(solution)/shard_map/ppermute | solution.py:599
  436.8 47.4 %collective-permute-start.14 = (bf16[2,2,48,1536]{3,2,1,0:T(8,128)(2,1)}, bf16[2,2,48,1536]{3,2,1,0:T(8,128)(2,1)}, u32[]{:S(2)}, u32[]{:S(2)}) collective-permute-start(bf16[2,2,48,1536]{3,2,1,0:T(8,128)(2,1)} %fusion.6), channel_id=1, source_target_pairs={{0,4},{2,6},{4,0},{6,2},{8,12},{10,14},{12,8},{14,10},{16,20},{18,... | collective-permute-start | bytes 1769480 | tf_op jit(solution)/shard_map/ppermute | solution.py:596
  437.6 46.7 %collective-permute-start.16 = (bf16[48,6912]{1,0:T(8,128)(2,1)}, bf16[48,6912]{1,0:T(8,128)(2,1)}, u32[]{:S(2)}, u32[]{:S(2)}) collective-permute-start(bf16[48,6912]{1,0:T(8,128)(2,1)} %reduce-scatter.3.cloned.1.call-done), channel_id=1, source_target_pairs={{0,1},{1,0},{2,3},{3,2},{4,5},{5,4},{6,7},{7,6},{8,9},{9,8},{10,11... | collective-permute-start | bytes 1990664 | tf_op jit(solution)/shard_map/ppermute | solution.py:599
  494.9 24.2 %collective-permute-start.22 = (bf16[2,2,2,48,1152]{4,3,2,1,0:T(8,128)(2,1)}, bf16[2,2,2,48,1152]{4,3,2,1,0:T(8,128)(2,1)}, u32[]{:S(2)}, u32[]{:S(2)}) collective-permute-start(bf16[2,2,2,48,1152]{4,3,2,1,0:T(8,128)(2,1)} %fusion.7), channel_id=1, source_target_pairs={{0,1},{1,0},{2,3},{3,2},{4,5},{5,4},{6,7},{7,6},{8,9},{9,8},{10,11... | collective-permute-start | bytes 2654216 | tf_op jit(solution)/shard_map/ppermute | solution.py:599
  497.3 19.9 %collective-permute-start.21 = (bf16[2,2,48,1920]{3,2,1,0:T(8,128)(2,1)}, bf16[2,2,48,1920]{3,2,1,0:T(8,128)(2,1)S(1)}, u32[]{:S(2)}, u32[]{:S(2)}) collective-permute-start(bf16[2,2,48,1920]{3,2,1,0:T(8,128)(2,1)} %fusion.4), channel_id=1, source_target_pairs={{0,4},{2,6},{4,0},{6,2},{8,12},{10,14},{12,8},{14,10},{16,20},{18,... | collective-permute-start | bytes 2211848 | tf_op jit(solution)/shard_map/ppermute | solution.py:596
  498.6 18.6 %collective-permute-start.18 = (bf16[48,1536]{1,0:T(8,128)(2,1)}, bf16[48,1536]{1,0:T(8,128)(2,1)}, u32[]{:S(2)}, u32[]{:S(2)}) collective-permute-start(bf16[48,1536]{1,0:T(8,128)(2,1)} %get-tuple-element.306), channel_id=1, source_target_pairs={{0,8},{2,10},{4,12},{6,14},{8,0},{10,2},{12,4},{14,6},{16,24},{18,... | collective-permute-start | bytes 442376 | tf_op jit(solution)/shard_map/ppermute | solution.py:596
  500.1 17.1 %collective-permute-start.19 = (bf16[48,1536]{1,0:T(8,128)(2,1)}, bf16[48,1536]{1,0:T(8,128)(2,1)}, u32[]{:S(2)}, u32[]{:S(2)}) collective-permute-start(bf16[48,1536]{1,0:T(8,128)(2,1)} %get-tuple-element.307), channel_id=1, source_target_pairs={{0,16},{2,18},{4,20},{6,22},{8,24},{10,26},{12,28},{14,30},{16,0},... | collective-permute-start | bytes 442376 | tf_op jit(solution)/shard_map/ppermute | solution.py:596
  500.9 16.3 %collective-permute-start.20 = (bf16[48,1536]{1,0:T(8,128)(2,1)}, bf16[48,1536]{1,0:T(8,128)(2,1)}, u32[]{:S(2)}, u32[]{:S(2)}) collective-permute-start(bf16[48,1536]{1,0:T(8,128)(2,1)} %get-tuple-element.308), channel_id=1, source_target_pairs={{0,24},{2,26},{4,28},{6,30},{8,16},{10,18},{12,20},{14,22},{16,8},... | collective-permute-start | bytes 442376 | tf_op jit(solution)/shard_map/ppermute | solution.py:596
  517.2 17.4 %collective-permute-start.29 = (f32[2,2,1152]{2,1,0:T(2,128)}, f32[2,2,1152]{2,1,0:T(2,128)}, u32[]{:S(2)}, u32[]{:S(2)}) collective-permute-start(f32[2,2,1152]{2,1,0:T(2,128)} %bitcast.215), channel_id=1, source_target_pairs={{0,2},{2,0},{4,6},{6,4},{8,10},{10,8},{12,14},{14,12},{16,18},{18,... | collective-permute-start | bytes 55304 | tf_op jit(solution)/shard_map/ppermute | solution.py:596
  517.3 19.1 %collective-permute-start.30 = (f32[2,2,1152]{2,1,0:T(2,128)}, f32[2,2,1152]{2,1,0:T(2,128)S(1)}, u32[]{:S(2)}, u32[]{:S(2)}) collective-permute-start(f32[2,2,1152]{2,1,0:T(2,128)} %bitcast.214), channel_id=1, source_target_pairs={{0,4},{2,6},{4,0},{6,2},{8,12},{10,14},{12,8},{14,10},{16,20},{18,... | collective-permute-start | bytes 55304 | tf_op jit(solution)/shard_map/ppermute | solution.py:596
  518.1 20.4 %collective-permute-start.31 = (f32[2,2,1152]{2,1,0:T(2,128)}, f32[2,2,1152]{2,1,0:T(2,128)}, u32[]{:S(2)}, u32[]{:S(2)}) collective-permute-start(f32[2,2,1152]{2,1,0:T(2,128)} %bitcast.213), channel_id=1, source_target_pairs={{0,6},{2,4},{4,2},{6,0},{8,14},{10,12},{12,10},{14,8},{16,22},{18,... | collective-permute-start | bytes 55304 | tf_op jit(solution)/shard_map/ppermute | solution.py:596
  521.4 12.7 %collective-permute-start.23 = (bf16[2,2,48,1152]{3,2,1,0:T(8,128)(2,1)}, bf16[2,2,48,1152]{3,2,1,0:T(8,128)(2,1)}, u32[]{:S(2)}, u32[]{:S(2)}) collective-permute-start(bf16[2,2,48,1152]{3,2,1,0:T(8,128)(2,1)} %fusion.8), channel_id=1, source_target_pairs={{0,4},{2,6},{4,0},{6,2},{8,12},{10,14},{12,8},{14,10},{16,20},{18,... | collective-permute-start | bytes 1327112 | tf_op jit(solution)/shard_map/ppermute | solution.py:596
  526.6 27.6 %collective-permute-start.25 = (bf16[48,2304]{1,0:T(8,128)(2,1)}, bf16[48,2304]{1,0:T(8,128)(2,1)}, u32[]{:S(2)}, u32[]{:S(2)}) collective-permute-start(bf16[48,2304]{1,0:T(8,128)(2,1)} %reduce-scatter.5.cloned.1.call-done), channel_id=1, source_target_pairs={{0,1},{1,0},{2,3},{3,2},{4,5},{5,4},{6,7},{7,6},{8,9},{9,8},{10,11... | collective-permute-start | bytes 663560 | tf_op jit(solution)/shard_map/ppermute | solution.py:599
  527.0 54.4 %all-to-all-start.4 = ((bf16[2,512,768]{2,1,0:T(8,128)(2,1)}), bf16[2,512,768]{2,1,0:T(8,128)(2,1)S(1)}, u32[]{:S(2)}, u32[]{:S(2)}) async-start(bf16[2,512,768]{2,1,0:T(8,128)(2,1)} %bitcast.260), calls=%async_computation.6 | async-start | bytes 3145728 | tf_op jit(solution)/shard_map/all_to_all | solution.py:770
  534.1 20.1 %collective-permute-start.26 = (bf16[48,1920]{1,0:T(8,128)(2,1)}, bf16[48,1920]{1,0:T(8,128)(2,1)S(1)}, u32[]{:S(2)}, u32[]{:S(2)}) collective-permute-start(bf16[48,1920]{1,0:T(8,128)(2,1)} %get-tuple-element.328), channel_id=1, source_target_pairs={{0,8},{2,10},{4,12},{6,14},{8,0},{10,2},{12,4},{14,6},{16,24},{18,... | collective-permute-start | bytes 552968 | tf_op jit(solution)/shard_map/ppermute | solution.py:596
  534.7 19.6 %collective-permute-start.27 = (bf16[48,1920]{1,0:T(8,128)(2,1)}, bf16[48,1920]{1,0:T(8,128)(2,1)S(1)}, u32[]{:S(2)}, u32[]{:S(2)}) collective-permute-start(bf16[48,1920]{1,0:T(8,128)(2,1)} %get-tuple-element.329), channel_id=1, source_target_pairs={{0,16},{2,18},{4,20},{6,22},{8,24},{10,26},{12,28},{14,30},{16,0},... | collective-permute-start | bytes 552968 | tf_op jit(solution)/shard_map/ppermute | solution.py:596
  536.4 17.9 %collective-permute-start.28 = (bf16[48,1920]{1,0:T(8,128)(2,1)}, bf16[48,1920]{1,0:T(8,128)(2,1)S(1)}, u32[]{:S(2)}, u32[]{:S(2)}) collective-permute-start(bf16[48,1920]{1,0:T(8,128)(2,1)} %get-tuple-element.330), channel_id=1, source_target_pairs={{0,24},{2,26},{4,28},{6,30},{8,16},{10,18},{12,20},{14,22},{16,8},... | collective-permute-start | bytes 552968 | tf_op jit(solution)/shard_map/ppermute | solution.py:596
  538.5 15.7 %collective-permute-start.24 = (bf16[48,1536]{1,0:T(8,128)(2,1)}, bf16[48,1536]{1,0:T(8,128)(2,1)S(1)}, u32[]{:S(2)}, u32[]{:S(2)}) collective-permute-start(bf16[48,1536]{1,0:T(8,128)(2,1)} %fusion.21), channel_id=1, source_target_pairs={{0,1},{1,0},{2,3},{3,2},{4,5},{5,4},{6,7},{7,6},{8,9},{9,8},{10,11... | collective-permute-start | bytes 442376 | tf_op jit(solution)/shard_map/ppermute | solution.py:599
  557.3 7.1 %collective-permute-start.32 = (bf16[48,1152]{1,0:T(8,128)(2,1)S(1)}, bf16[48,1152]{1,0:T(8,128)(2,1)S(1)}, u32[]{:S(2)}, u32[]{:S(2)}) collective-permute-start(bf16[48,1152]{1,0:T(8,128)(2,1)S(1)} %get-tuple-element.342), channel_id=1, source_target_pairs={{0,8},{2,10},{4,12},{6,14},{8,0},{10,2},{12,4},{14,6},{16,24},{18,... | collective-permute-start | bytes 331784 | tf_op jit(solution)/shard_map/ppermute | solution.py:596
  557.9 11.1 %collective-permute-start.33 = (bf16[48,1152]{1,0:T(8,128)(2,1)S(1)}, bf16[48,1152]{1,0:T(8,128)(2,1)S(1)}, u32[]{:S(2)}, u32[]{:S(2)}) collective-permute-start(bf16[48,1152]{1,0:T(8,128)(2,1)S(1)} %get-tuple-element.343), channel_id=1, source_target_pairs={{0,16},{2,18},{4,20},{6,22},{8,24},{10,26},{12,28},{14,30},{16,0},... | collective-permute-start | bytes 331784 | tf_op jit(solution)/shard_map/ppermute | solution.py:596
  559.6 11.2 %collective-permute-start.34 = (bf16[48,1152]{1,0:T(8,128)(2,1)S(1)}, bf16[48,1152]{1,0:T(8,128)(2,1)S(1)}, u32[]{:S(2)}, u32[]{:S(2)}) collective-permute-start(bf16[48,1152]{1,0:T(8,128)(2,1)S(1)} %get-tuple-element.344), channel_id=1, source_target_pairs={{0,24},{2,26},{4,28},{6,30},{8,16},{10,18},{12,20},{14,22},{16,8},... | collective-permute-start | bytes 331784 | tf_op jit(solution)/shard_map/ppermute | solution.py:596
  561.8 12.6 %collective-permute-start.35 = (bf16[48,1920]{1,0:T(8,128)(2,1)S(1)}, bf16[48,1920]{1,0:T(8,128)(2,1)S(1)}, u32[]{:S(2)}, u32[]{:S(2)}) collective-permute-start(bf16[48,1920]{1,0:T(8,128)(2,1)S(1)} %fusion.13), channel_id=1, source_target_pairs={{0,1},{1,0},{2,3},{3,2},{4,5},{5,4},{6,7},{7,6},{8,9},{9,8},{10,11... | collective-permute-start | bytes 552968 | tf_op jit(solution)/shard_map/ppermute | solution.py:599
  562.1 10.2 %collective-permute-start.36 = (f32[1152]{0:T(1024)S(1)}, f32[1152]{0:T(1024)S(1)}, u32[]{:S(2)}, u32[]{:S(2)}) collective-permute-start(f32[1152]{0:T(1024)S(1)} %add_add_fusion.3), channel_id=1, source_target_pairs={{0,8},{2,10},{4,12},{6,14},{8,0},{10,2},{12,4},{14,6},{16,24},{18,... | collective-permute-start | bytes 13832 | tf_op jit(solution)/shard_map/ppermute | solution.py:596
  564.5 7.8 %collective-permute-start.37 = (f32[1152]{0:T(1024)S(1)}, f32[1152]{0:T(1024)S(1)}, u32[]{:S(2)}, u32[]{:S(2)}) collective-permute-start(f32[1152]{0:T(1024)S(1)} %add_add_fusion.2), channel_id=1, source_target_pairs={{0,16},{2,18},{4,20},{6,22},{8,24},{10,26},{12,28},{14,30},{16,0},... | collective-permute-start | bytes 13832 | tf_op jit(solution)/shard_map/ppermute | solution.py:596
  569.0 5.4 collective-permute-start.38
  571.9 4.9 collective-permute-start.39
  (29 other events, 228.4 us)
Sparse Core Ops, SparseCore 0:
  12.7 67.1 all-gather.4
  82.7 90.0 all-gather.6
  175.7 51.5 all-gather.8
  302.8 118.7 reduce-scatter.2
  433.4 65.7 reduce-scatter.4
